TPU v7x, 32 devices: a whole 2x2x4 slice. The times are simulated.
32 devices in a mesh: dp: 4 (over y, core), seq: 8 (over z, x).
Axes of the slice: x: 2, y: 2, z: 4, core: 2. Of those that a mesh axis runs over, the one named last changes fastest.
Arguments:
- tokens: bfloat16 [8, 1024, 2048], P('dp', 'seq'), may hold values from -6 to 6
- lengths: int32 [8], P('dp'), may hold values from 256 to 1024, as said below
- norm_gain: float32 [2048], replicated, may hold values from 0.5 to 1.5
- in_weight: bfloat16 [2048, 6144], P('seq'), may hold values from -0.125 to 0.125
- conv_taps: float32 [3, 6144], replicated, may hold values from -3 to 3
- filter_residue: float32 [2048, 16], replicated, may hold values from -0.0625 to 0.0625
- filter_decay: float32 [2048, 16], replicated, may hold values from 0.00048828125 to 0.03125
- out_weight: bfloat16 [2048, 2048], P('seq'), may hold values from -0.125 to 0.125
- feed_gain: float32 [2048], replicated, may hold values from 0.5 to 1.5
- gate_weight: bfloat16 [2048, 5632], P('seq'), may hold values from -0.125 to 0.125
- up_weight: bfloat16 [2048, 5632], P('seq'), may hold values from -0.125 to 0.125
- down_weight: bfloat16 [5632, 2048], P('seq'), may hold values from -0.078125 to 0.078125
- cotangent: bfloat16 [8, 1024, 2048], P('dp', 'seq'), may hold values from -6 to 6
Outputs:
- output: bfloat16 [8, 1024, 2048], P('dp', 'seq')
- grad_tokens: bfloat16 [8, 1024, 2048], P('dp', 'seq')
- grad_norm_gain: float32 [2048], replicated
- grad_in_weight: float32 [2048, 6144], P('seq')
- grad_conv_taps: float32 [3, 6144], replicated
- grad_filter_residue: float32 [2048, 16], replicated
- grad_filter_decay: float32 [2048, 16], replicated
- grad_out_weight: float32 [2048, 2048], P('seq')
- grad_feed_gain: float32 [2048], replicated
- grad_gate_weight: float32 [2048, 5632], P('seq')
- grad_up_weight: float32 [2048, 5632], P('seq')
- grad_down_weight: float32 [5632, 2048], P('seq')
Inputs may be any that keep to these rules, and one draw needn't show every extreme that they name: `lengths`: in each aligned block of 2 sequences (those of one index of dp) one sequence is valid to the full 1024 positions.
All inputs are finite; a program needn't handle non-finite values.
Results may differ from a plain program's by a relative error of at most 0.019.
Values may be sent and summed in bfloat16 or wider, within the bound.
No kernel may reach another device: no remote copies, remote signals or barrier semaphores. Data moves between devices by JAX's collectives and lax.ppermute only.
A program may use at most 640 MiB of HBM per device.

v0:
```python
import math

import jax
import jax.numpy as jnp
from jax import lax
from jax.sharding import PartitionSpec as P

epsilon = 1e-06
highest = lax.Precision.HIGHEST


def from_behind(shard, axis, by):
    length = lax.axis_size(axis)
    pairs = [(i, i + by) for i in range(length) if 0 <= i + by < length]
    return lax.ppermute(shard, axis, pairs)


def rms_scale(values):
    return lax.rsqrt(jnp.mean(values * values, axis=-1, keepdims=True) + epsilon)


def norm_back(values, scale, gain, grad_normed):
    grad_gain = jnp.sum(grad_normed * values * scale, axis=(0, 1))
    scaled = grad_normed * gain
    grad_values = scale * scaled - values * scale * scale * scale * jnp.mean(
        scaled * values, axis=-1, keepdims=True
    )
    return (grad_values, grad_gain)


def mode_response(residue, decay, length):
    steps = jnp.arange(length).astype(jnp.float32)
    terms = residue.T[:, None, :] * jnp.exp(-decay.T[:, None, :] * steps[None, :, None])
    return jnp.sum(terms, axis=0)


def split_size(total):
    first = 1
    for option in range(1, math.isqrt(total) + 1):
        if total % option == 0:
            first = option
    return (first, total // first)


def turn_table(rows, cols, modulus):
    index = jnp.arange(rows)[:, None] * jnp.arange(cols)[None, :] % modulus
    angle = index.astype(jnp.float32) * (2.0 * math.pi / modulus)
    return (jnp.cos(angle), jnp.sin(angle))


def complex_mix(spec, table, pair):
    real_table, imag_table = table
    real_part, imag_part = pair
    first = jnp.einsum(spec, real_table, real_part, precision=highest) - jnp.einsum(
        spec, imag_table, imag_part, precision=highest
    )
    second = jnp.einsum(spec, real_table, imag_part, precision=highest) + jnp.einsum(
        spec, imag_table, real_part, precision=highest
    )
    return (first, second)


def complex_times(one, two):
    return (one[0] * two[0] - one[1] * two[1], one[0] * two[1] + one[1] * two[0])


def conjugate(pair):
    return (pair[0], -pair[1])


def spectrum(signal, total):
    batch, length, width = signal.shape
    padded = jnp.pad(signal, ((0, 0), (0, total - length), (0, 0)))
    first, second = split_size(total)
    grid = padded.reshape(batch, second, first, width)
    cosine_inner, sine_inner = turn_table(second, second, second)
    section = (
        jnp.einsum("kn,bnmc->bkmc", cosine_inner, grid, precision=highest),
        -jnp.einsum("kn,bnmc->bkmc", sine_inner, grid, precision=highest),
    )
    cosine_twist, sine_twist = turn_table(second, first, total)
    section = complex_times(
        section, (cosine_twist[None, :, :, None], -sine_twist[None, :, :, None])
    )
    cosine_outer, sine_outer = turn_table(first, first, first)
    result = complex_mix("jm,bkmc->bjkc", (cosine_outer, -sine_outer), section)
    return (result[0].reshape(batch, total, width), result[1].reshape(batch, total, width))


def inverse(pair, total, keep):
    batch = pair[0].shape[0]
    width = pair[0].shape[2]
    first, second = split_size(total)
    grid = (
        pair[0].reshape(batch, first, second, width),
        pair[1].reshape(batch, first, second, width),
    )
    cosine_outer, sine_outer = turn_table(first, first, first)
    section = complex_mix("mj,bjkc->bmkc", (cosine_outer, sine_outer), grid)
    cosine_twist, sine_twist = turn_table(first, second, total)
    section = complex_times(section, (cosine_twist[None, :, :, None], sine_twist[None, :, :, None]))
    cosine_inner, sine_inner = turn_table(second, second, second)
    real = jnp.einsum("nk,bmkc->bnmc", cosine_inner, section[0], precision=highest) - jnp.einsum(
        "nk,bmkc->bnmc", sine_inner, section[1], precision=highest
    )
    return real.reshape(batch, total, width)[:, :keep] / total


def body(
    tokens,
    lengths,
    norm_gain,
    in_weight,
    conv_taps,
    filter_residue,
    filter_decay,
    out_weight,
    feed_gain,
    gate_weight,
    up_weight,
    down_weight,
    cotangent,
):
    parts = lax.axis_size("seq")
    local_len = tokens.shape[1]
    width = tokens.shape[2]
    full_len = local_len * parts
    channels = width // parts
    size = 2 * full_len
    place = lax.axis_index("seq")
    position = place * local_len + jnp.arange(local_len)
    mask = (position[None, :] < lengths[:, None]).astype(jnp.float32)[..., None]
    w_in, w_out, w_gate, w_up, w_down = (
        lax.all_gather(in_weight, "seq", axis=0, tiled=True),
        lax.all_gather(out_weight, "seq", axis=0, tiled=True),
        lax.all_gather(gate_weight, "seq", axis=0, tiled=True),
        lax.all_gather(up_weight, "seq", axis=0, tiled=True),
        lax.all_gather(down_weight, "seq", axis=0, tiled=True),
    )
    hidden = tokens.astype(jnp.float32)
    scale_one = rms_scale(hidden)
    normed = (hidden * scale_one * norm_gain).astype(jnp.bfloat16)
    mixed = jnp.dot(normed, w_in, preferred_element_type=jnp.float32).astype(jnp.bfloat16)
    carried = from_behind(mixed[:, local_len - 2 :, :], "seq", 1)
    extended = jnp.concatenate([carried, mixed], axis=1).astype(jnp.float32)
    short = (
        conv_taps[0] * extended[:, 2:]
        + conv_taps[1] * extended[:, 1:-1]
        + conv_taps[2] * extended[:, :-2]
    )
    query = short[..., :width]
    keys = short[..., width : 2 * width]
    values = short[..., 2 * width :]
    product = (keys * values).astype(jnp.bfloat16)
    product_chan = lax.all_to_all(product, "seq", split_axis=2, concat_axis=1, tiled=True)
    start = place * channels
    residue_part = lax.dynamic_slice_in_dim(filter_residue, start, channels, 0)
    decay_part = lax.dynamic_slice_in_dim(filter_decay, start, channels, 0)
    response = mode_response(residue_part, decay_part, full_len)
    product_spec = spectrum(product_chan.astype(jnp.float32), size)
    response_spec = spectrum(response[None], size)
    conv_chan = inverse(complex_times(product_spec, response_spec), size, full_len)
    convolved = lax.all_to_all(
        conv_chan.astype(jnp.bfloat16), "seq", split_axis=1, concat_axis=2, tiled=True
    ).astype(jnp.float32)
    gated = (query * convolved).astype(jnp.bfloat16)
    middle = hidden + jnp.dot(gated, w_out, preferred_element_type=jnp.float32)
    scale_two = rms_scale(middle)
    normed_two = (middle * scale_two * feed_gain).astype(jnp.bfloat16)
    gate = jnp.dot(normed_two, w_gate, preferred_element_type=jnp.float32)
    upper = jnp.dot(normed_two, w_up, preferred_element_type=jnp.float32)
    sigma = jax.nn.sigmoid(gate)
    active = (gate * sigma * upper).astype(jnp.bfloat16)
    feed = jnp.dot(active, w_down, preferred_element_type=jnp.float32)
    output = (mask * (middle + feed)).astype(jnp.bfloat16)
    grad_out = cotangent.astype(jnp.float32) * mask
    grad_feed = grad_out.astype(jnp.bfloat16)
    grad_active = jnp.einsum("btd,fd->btf", grad_feed, w_down, preferred_element_type=jnp.float32)
    grad_gate = (grad_active * upper * sigma * (1.0 + gate * (1.0 - sigma))).astype(jnp.bfloat16)
    grad_upper = (grad_active * gate * sigma).astype(jnp.bfloat16)
    grad_normed_two = jnp.einsum(
        "btf,df->btd", grad_gate, w_gate, preferred_element_type=jnp.float32
    ) + jnp.einsum("btf,df->btd", grad_upper, w_up, preferred_element_type=jnp.float32)
    term_gate = jnp.einsum("btd,btf->df", normed_two, grad_gate, preferred_element_type=jnp.float32)
    term_up = jnp.einsum("btd,btf->df", normed_two, grad_upper, preferred_element_type=jnp.float32)
    term_down = jnp.einsum("btf,btd->fd", active, grad_feed, preferred_element_type=jnp.float32)
    feed_terms = (
        lax.psum_scatter(
            term_gate.astype(jnp.bfloat16), "seq", scatter_dimension=0, tiled=True
        ).astype(jnp.float32),
        lax.psum_scatter(
            term_up.astype(jnp.bfloat16), "seq", scatter_dimension=0, tiled=True
        ).astype(jnp.float32),
        lax.psum_scatter(
            term_down.astype(jnp.bfloat16), "seq", scatter_dimension=0, tiled=True
        ).astype(jnp.float32),
    )
    grad_middle, grad_feed_gain = norm_back(middle, scale_two, feed_gain, grad_normed_two)
    grad_middle = grad_middle + grad_out
    grad_mix = grad_middle.astype(jnp.bfloat16)
    term_out = jnp.einsum("btd,bte->de", gated, grad_mix, preferred_element_type=jnp.float32)
    grad_gated = jnp.einsum("bte,de->btd", grad_mix, w_out, preferred_element_type=jnp.float32)
    grad_query = grad_gated * convolved
    grad_conv = (grad_gated * query).astype(jnp.bfloat16)
    grad_conv_chan = lax.all_to_all(
        grad_conv, "seq", split_axis=2, concat_axis=1, tiled=True
    ).astype(jnp.float32)
    grad_spec = spectrum(grad_conv_chan, size)
    grad_product_chan = inverse(complex_times(grad_spec, conjugate(response_spec)), size, full_len)
    cross = complex_times(conjugate(product_spec), grad_spec)
    cross = (jnp.sum(cross[0], axis=0, keepdims=True), jnp.sum(cross[1], axis=0, keepdims=True))
    grad_response = inverse(cross, size, full_len)[0]
    grad_product = lax.all_to_all(
        grad_product_chan.astype(jnp.bfloat16), "seq", split_axis=1, concat_axis=2, tiled=True
    ).astype(jnp.float32)
    grad_short = jnp.concatenate([grad_query, grad_product * values, grad_product * keys], axis=-1)
    following = from_behind(grad_short[:, :2, :].astype(jnp.bfloat16), "seq", -1).astype(
        jnp.float32
    )
    grad_extended = jnp.concatenate([grad_short, following], axis=1)
    grad_mixed = (
        conv_taps[0] * grad_extended[:, :local_len]
        + conv_taps[1] * grad_extended[:, 1 : local_len + 1]
        + conv_taps[2] * grad_extended[:, 2:]
    )
    grad_taps = jnp.stack(
        [
            jnp.sum(grad_short * extended[:, 2:], axis=(0, 1)),
            jnp.sum(grad_short * extended[:, 1:-1], axis=(0, 1)),
            jnp.sum(grad_short * extended[:, :-2], axis=(0, 1)),
        ]
    )
    grad_mixed_low = grad_mixed.astype(jnp.bfloat16)
    term_in = jnp.einsum("btd,bte->de", normed, grad_mixed_low, preferred_element_type=jnp.float32)
    grad_normed = jnp.einsum(
        "bte,de->btd", grad_mixed_low, w_in, preferred_element_type=jnp.float32
    )
    mixer_terms = (
        lax.psum_scatter(
            term_in.astype(jnp.bfloat16), "seq", scatter_dimension=0, tiled=True
        ).astype(jnp.float32),
        lax.psum_scatter(
            term_out.astype(jnp.bfloat16), "seq", scatter_dimension=0, tiled=True
        ).astype(jnp.float32),
    )
    grad_hidden, grad_norm_gain = norm_back(hidden, scale_one, norm_gain, grad_normed)
    grad_tokens = (grad_hidden + grad_middle).astype(jnp.bfloat16)

    def response_of(residue_in, decay_in):
        return mode_response(residue_in, decay_in, full_len)

    unused, pull = jax.vjp(response_of, residue_part, decay_part)
    grad_residue_part, grad_decay_part = pull(grad_response)
    grad_residue = lax.dynamic_update_slice_in_dim(
        jnp.zeros_like(filter_residue), grad_residue_part, start, 0
    )
    grad_decay = lax.dynamic_update_slice_in_dim(
        jnp.zeros_like(filter_decay), grad_decay_part, start, 0
    )
    small = lax.psum(
        (grad_norm_gain, grad_taps, grad_residue, grad_decay, grad_feed_gain), ("dp", "seq")
    )
    large = (
        lax.psum(mixer_terms[0].astype(jnp.bfloat16), "dp").astype(jnp.float32),
        lax.psum(mixer_terms[1].astype(jnp.bfloat16), "dp").astype(jnp.float32),
        lax.psum(feed_terms[0].astype(jnp.bfloat16), "dp").astype(jnp.float32),
        lax.psum(feed_terms[1].astype(jnp.bfloat16), "dp").astype(jnp.float32),
        lax.psum(feed_terms[2].astype(jnp.bfloat16), "dp").astype(jnp.float32),
    )
    return (
        output,
        grad_tokens,
        small[0],
        large[0],
        small[1],
        small[2],
        small[3],
        large[1],
        small[4],
        large[2],
        large[3],
        large[4],
    )


def solution(mesh):
    placed = (
        P("dp", "seq", None),
        P("dp"),
        P(),
        P("seq", None),
        P(),
        P(),
        P(),
        P("seq", None),
        P(),
        P("seq", None),
        P("seq", None),
        P("seq", None),
        P("dp", "seq", None),
    )
    return jax.shard_map(
        body,
        mesh=mesh,
        in_specs=placed,
        out_specs=(
            P("dp", "seq", None),
            P("dp", "seq", None),
            P(),
            P("seq", None),
            P(),
            P(),
            P(),
            P("seq", None),
            P(),
            P("seq", None),
            P("seq", None),
            P("seq", None),
        ),
        check_vma=False,
    )
```

profile of v0, /device:TPU:9, one launch (start us, length us, event | category | flops | bytes accessed | tf_op | source)
XLA Modules:
  0.0 4131.6 jit_solution(7491863182339162644)
XLA Ops:
  19.6 471.7 %all-gather.6.cloned.1.call-done = bf16[2048,6144]{1,0:T(8,128)(2,1)} async-done(((bf16[256,6144]{1,0:T(8,128)(2,1)}), bf16[2048,6144]{1,0:T(8,128)(2,1)}) %all-gather.6.cloned.1.call-update) | async-done | bytes 25165840 | tf_op jit(solution)/shard_map/all_gather | solution.py:134
  491.4 11.8 fusion.20
  507.2 25.8 collective-permute-done
  567.9 15.1 fusion.425
  653.5 9.0 fusion.46
  679.3 278.3 %all-gather.14.cloned.1.call-done = bf16[5632,2048]{1,0:T(8,128)(2,1)} async-done(((bf16[704,2048]{1,0:T(8,128)(2,1)}), bf16[5632,2048]{1,0:T(8,128)(2,1)}) %all-gather.14.cloned.1.call-update) | async-done | bytes 23068688 | tf_op jit(solution)/shard_map/all_gather | solution.py:138
  957.6 13.5 fusion.4
  975.8 106.3 %all-gather.8.cloned.1.call-done = bf16[2048,2048]{1,0:T(8,128)(2,1)} async-done(((bf16[256,2048]{1,0:T(8,128)(2,1)}), bf16[2048,2048]{1,0:T(8,128)(2,1)}) %all-gather.8.cloned.1.call-update) | async-done | bytes 8388624 | tf_op jit(solution)/shard_map/all_gather | solution.py:135
  1088.6 436.7 %all-gather.12.cloned.1.call-done = bf16[2048,5632]{1,0:T(8,128)(2,1)} async-done(((bf16[256,5632]{1,0:T(8,128)(2,1)}), bf16[2048,5632]{1,0:T(8,128)(2,1)}) %all-gather.12.cloned.1.call-update) | async-done | bytes 23068688 | tf_op jit(solution)/shard_map/all_gather | solution.py:137
  1525.3 13.2 fusion.10
  1538.5 429.3 %all-gather.10.cloned.1.call-done = bf16[2048,5632]{1,0:T(8,128)(2,1)} async-done(((bf16[256,5632]{1,0:T(8,128)(2,1)}), bf16[2048,5632]{1,0:T(8,128)(2,1)}) %all-gather.10.cloned.1.call-update) | async-done | bytes 23068688 | tf_op jit(solution)/shard_map/all_gather | solution.py:136
  1967.8 20.0 multiply_convert_fusion.1
  1987.8 12.8 fusion.8
  2000.6 13.7 multiply_reduce_fusion.6
  2023.5 13.1 bitcast_convert_fusion.3
  2036.7 13.2 bitcast_convert_fusion.2
  2051.1 13.0 bitcast_convert_fusion.1
  2073.7 49.4 %all_to_all.16 = bf16[2,128,2048]{1,0,2:T(2,128)(2,1)S(1)} all-to-all(bf16[2,128,2048]{1,0,2:T(2,128)(2,1)S(1)} %copy.189), channel_id=1, replica_groups=mesh['dp'=4,'seq'=8] {'seq'}, dimensions={2} | all-to-all | bytes 2097152 | tf_op jit(solution)/shard_map/all_to_all | solution.py:205
  2151.8 15.1 fusion.31
  2192.5 9.0 fusion.42
  2211.6 55.5 %all_to_all.17 = bf16[2,1024,256]{2,0,1:T(2,128)(2,1)S(1)} all-to-all(bf16[2,1024,256]{2,0,1:T(2,128)(2,1)S(1)} %copy.201), channel_id=1, replica_groups=mesh['dp'=4,'seq'=8] {'seq'}, dimensions={1} | all-to-all | bytes 2097152 | tf_op jit(solution)/shard_map/all_to_all | solution.py:213
  2284.3 18.1 multiply_reduce_fusion.5
  2302.4 14.2 bitcast_convert_fusion
  2318.2 13.1 fusion.77
  2331.2 260.6 %reduce-scatter.10.cloned.1.call-done = bf16[256,5632]{1,0:T(8,128)(2,1)} async-done(((bf16[2048,5632]{1,0:T(8,128)(2,1)}), bf16[256,5632]{1,0:T(8,128)(2,1)}) %reduce-scatter.10.cloned.1.call-update) | async-done | bytes 2883600 | tf_op jit(solution)/shard_map/reduce_scatter | solution.py:188
  2591.9 377.1 %reduce-scatter.12.cloned.1.call-done = bf16[256,5632]{1,0:T(8,128)(2,1)} async-done(((bf16[2048,5632]{1,0:T(8,128)(2,1)}), bf16[256,5632]{1,0:T(8,128)(2,1)}) %reduce-scatter.12.cloned.1.call-update) | async-done | bytes 2883600 | tf_op jit(solution)/shard_map/reduce_scatter | solution.py:191
  2969.0 377.0 %reduce-scatter.14.cloned.1.call-done = bf16[704,2048]{1,0:T(8,128)(2,1)} async-done(((bf16[5632,2048]{1,0:T(8,128)(2,1)}), bf16[704,2048]{1,0:T(8,128)(2,1)}) %reduce-scatter.14.cloned.1.call-update) | async-done | bytes 2883600 | tf_op jit(solution)/shard_map/reduce_scatter | solution.py:194
  3346.0 406.9 %reduce-scatter.6.cloned.1.call-done = bf16[256,6144]{1,0:T(8,128)(2,1)} async-done(((bf16[2048,6144]{1,0:T(8,128)(2,1)}), bf16[256,6144]{1,0:T(8,128)(2,1)}) %reduce-scatter.6.cloned.1.call-update) | async-done | bytes 3145744 | tf_op jit(solution)/shard_map/reduce_scatter | solution.py:239
  3777.7 14.1 fusion.107
  3795.9 43.2 %all-reduce.3 = (f32[2048]{0:T(1024)}, f32[2048]{0:T(1024)}) all-reduce(f32[2048]{0:T(1024)S(1)} %get-tuple-element.19, f32[2048]{0:T(1024)S(1)} %copy-done.57), channel_id=1, replica_groups=mesh['dp'=4,'seq'=8] {'dp','seq'}, use_global_device_ids=true, to_apply=%region_6.7 | all-reduce | flops 4096 | bytes 32768 | tf_op jit(solution)/shard_map/psum | solution.py:260
  3839.1 145.6 %all-reduce.11.cloned.1.call-done = (bf16[256,6144]{1,0:T(8,128)(2,1)}, bf16[256,2048]{1,0:T(8,128)(2,1)}, bf16[256,5632]{1,0:T(8,128)(2,1)}, bf16[256,5632]{1,0:T(8,128)(2,1)}, bf16[704,2048]{1,0:T(8,128)(2,1)}) async-done(((bf16[256,6144]{1,0:T(8,128)(2,1)}, bf16[256,2048]{1,0:T(8,128)(2,1)}, bf16[256,5632]{1,0:T(8,128)(2,1)}, bf16[256,5632]{1,0:T(8,128)(2,1)}, bf16[704,2048]{1,0:T(8,128)(2,1)}), ...) | async-done | bytes 12845072 | tf_op jit(solution)/shard_map/psum | solution.py:264
  4001.5 118.0 %all-reduce.9.cloned.1.call-done = (f32[3,6144]{1,0:T(4,128)}, f32[2048,16]{0,1:T(8,128)}, f32[2048,16]{0,1:T(8,128)}) async-done(((f32[3,6144]{1,0:T(4,128)}, f32[2048,16]{0,1:T(8,128)}, f32[2048,16]{0,1:T(8,128)}), (f32[3,6144]{1,0:T(4,128)}, f32[2048,16]{0,1:T(8,128)}, f32[2048,16]{0,1:T(8,128)})) %all-reduce.9.cloned.1.call-update) | async-done | bytes 335888 | tf_op jit(solution)/shard_map/psum | solution.py:260
  (257 shorter events, 302.4 us)
Async XLA Ops:
  7.2 484.2 %all-gather.6.cloned.1.call-start = ((), (), s32[]{:S(2)}) async-start(), calls=%async_computation.9 | async-start | bytes 28311552 | tf_op jit(solution)/shard_map/all_gather | solution.py:134
  7.9 949.6 %all-gather.14.cloned.1.call-start = ((), (), s32[]{:S(2)}) async-start(), calls=%async_computation.13 | async-start | bytes 25952256 | tf_op jit(solution)/shard_map/all_gather | solution.py:138
  8.7 1073.5 %all-gather.8.cloned.1.call-start = ((), (), s32[]{:S(2)}) async-start(), calls=%async_computation.10 | async-start | bytes 9437184 | tf_op jit(solution)/shard_map/all_gather | solution.py:135
  9.4 1515.9 %all-gather.12.cloned.1.call-start = ((), (), s32[]{:S(2)}) async-start(), calls=%async_computation.12 | async-start | bytes 25952256 | tf_op jit(solution)/shard_map/all_gather | solution.py:137
  10.0 1957.8 %all-gather.10.cloned.1.call-start = ((), (), s32[]{:S(2)}) async-start(), calls=%async_computation.11 | async-start | bytes 25952256 | tf_op jit(solution)/shard_map/all_gather | solution.py:136
  14.2 477.1 %copy-start.47 = (f32[2048]{0:T(1024)S(1)}, f32[2048]{0:T(1024)}, u32[]{:S(2)}) copy-start(f32[2048]{0:T(1024)} %param.15) | copy-start | bytes 24580
  14.6 630.3 %copy-start.30 = (f32[32,64]{0,1:T(8,128)}, f32[32,64]{0,1:T(8,128)S(1)}, u32[]{:S(2)}) copy-start(f32[32,64]{0,1:T(8,128)S(1)} %get-tuple-element.67) | copy-start | bytes 24580
  14.6 630.3 %copy-start.32 = (f32[32,64]{0,1:T(8,128)}, f32[32,64]{0,1:T(8,128)S(1)}, u32[]{:S(2)}) copy-start(f32[32,64]{0,1:T(8,128)S(1)} %get-tuple-element.68) | copy-start | bytes 24580
  14.9 488.2 %copy-start.50 = (f32[2,128]{1,0:T(2,128)}, f32[2,128]{1,0:T(2,128)S(1)}, u32[]{:S(2)}) copy-start(f32[2,128]{1,0:T(2,128)S(1)} %add_rsqrt_fusion.1) | copy-start | bytes 3076
  19.6 516.3 %copy-start.41 = (f32[1,6144]{1,0:T(1,128)}, f32[1,6144]{1,0:T(1,128)S(1)}, u32[]{:S(2)}) copy-start(f32[1,6144]{1,0:T(1,128)S(1)} %get-tuple-element.53) | copy-start | bytes 73732
  19.6 516.3 %copy-start.43 = (f32[1,6144]{1,0:T(1,128)}, f32[1,6144]{1,0:T(1,128)S(1)}, u32[]{:S(2)}) copy-start(f32[1,6144]{1,0:T(1,128)S(1)} %get-tuple-element.54) | copy-start | bytes 73732
  19.6 516.3 %copy-start.45 = (f32[1,6144]{1,0:T(1,128)}, f32[1,6144]{1,0:T(1,128)S(1)}, u32[]{:S(2)}) copy-start(f32[1,6144]{1,0:T(1,128)S(1)} %get-tuple-element.55) | copy-start | bytes 73732
  504.9 28.2 collective-permute-start
  507.2 91.8 %copy-start.37 = (f32[64,32]{0,1:T(8,128)}, f32[64,32]{0,1:T(8,128)S(1)}, u32[]{:S(2)}) copy-start(f32[64,32]{0,1:T(8,128)S(1)} %get-tuple-element.63) | copy-start | bytes 24580
  507.2 91.8 %copy-start.39 = (f32[64,32]{0,1:T(8,128)}, f32[64,32]{0,1:T(8,128)S(1)}, u32[]{:S(2)}) copy-start(f32[64,32]{0,1:T(8,128)S(1)} %get-tuple-element.64) | copy-start | bytes 24580
  546.2 44.1 %all-to-all-start = ((bf16[2,128,2048]{1,0,2:T(2,128)(2,1)}), bf16[2,128,2048]{1,0,2:T(2,128)(2,1)}, u32[]{:S(2)}, u32[]{:S(2)}) async-start(bf16[2,128,2048]{1,0,2:T(2,128)(2,1)} %copy.168), calls=%async_computation | async-start | bytes 2097152 | tf_op jit(solution)/shard_map/all_to_all | solution.py:155
  567.9 76.9 %copy-start = (f32[32,64,256]{2,0,1:T(8,128)}, f32[32,64,256]{2,0,1:T(8,128)S(1)}, u32[]{:S(2)}) copy-start(f32[32,64,256]{2,0,1:T(8,128)S(1)} %subtract_bitcast_fusion.3) | copy-start | bytes 6291460
  623.4 21.5 copy-start.3
  671.4 286.2 %copy-start.24 = (bf16[2,128,2048]{2,1,0:T(8,128)(2,1)S(1)}, bf16[2,128,2048]{2,1,0:T(8,128)(2,1)}, u32[]{:S(2)}) copy-start(bf16[2,128,2048]{2,1,0:T(8,128)(2,1)} %param.25) | copy-start | bytes 3145732
  673.6 297.5 %all-to-all-start.1 = ((bf16[2,1024,256]{2,0,1:T(2,128)(2,1)}), bf16[2,1024,256]{2,0,1:T(2,128)(2,1)S(1)}, u32[]{:S(2)}, u32[]{:S(2)}) async-start(bf16[2,1024,256]{2,0,1:T(2,128)(2,1)} %copy.186), calls=%async_computation.1 | async-start | bytes 2097152 | tf_op jit(solution)/shard_map/all_to_all | solution.py:163
  679.2 1652.1 %reduce-scatter.8.cloned.1.call-start = ((), (), s32[]{:S(2)}) async-start(), calls=%async_computation.15 | async-start | bytes 9437184 | tf_op jit(solution)/shard_map/reduce_scatter | solution.py:242
  975.8 112.5 %copy-start.52 = (f32[2048]{0:T(1024)S(1)}, f32[2048]{0:T(1024)}, u32[]{:S(2)}) copy-start(f32[2048]{0:T(1024)} %param.21) | copy-start | bytes 24580
  1088.3 912.2 %copy-start.21 = (f32[2,128,2048]{2,1,0:T(8,128)}, f32[2,128,2048]{2,1,0:T(8,128)S(1)}, u32[]{:S(2)}) copy-start(f32[2,128,2048]{2,1,0:T(8,128)S(1)} %get-tuple-element.57) | copy-start | bytes 6291460
  2017.7 46.5 %copy-start.11 = (f32[2,128,2048]{2,1,0:T(8,128)}, f32[2,128,2048]{2,1,0:T(8,128)S(1)}, u32[]{:S(2)}) copy-start(f32[2,128,2048]{2,1,0:T(8,128)S(1)} %subtract_add_fusion) | copy-start | bytes 6291460
  2023.5 568.4 %reduce-scatter.10.cloned.1.call-start = ((), (), s32[]{:S(2)}) async-start(), calls=%async_computation.16 | async-start | bytes 25952256 | tf_op jit(solution)/shard_map/reduce_scatter | solution.py:188
  2036.6 932.3 %reduce-scatter.12.cloned.1.call-start = ((), (), s32[]{:S(2)}) async-start(), calls=%async_computation.17 | async-start | bytes 25952256 | tf_op jit(solution)/shard_map/reduce_scatter | solution.py:191
  2049.9 1296.1 %reduce-scatter.14.cloned.1.call-start = ((), (), s32[]{:S(2)}) async-start(), calls=%async_computation.18 | async-start | bytes 25952256 | tf_op jit(solution)/shard_map/reduce_scatter | solution.py:194
  2064.1 1688.7 %reduce-scatter.6.cloned.1.call-start = ((), (), s32[]{:S(2)}) async-start(), calls=%async_computation.14 | async-start | bytes 28311552 | tf_op jit(solution)/shard_map/reduce_scatter | solution.py:239
  2210.4 57.4 %slice-start = ((s8[6291456]{0:T(1024)(128)(4,1)}), s8[4194304]{0:T(1024)(128)(4,1)S(1)}, s32[]{:S(2)}) async-start(s8[6291456]{0:T(1024)(128)(4,1)} %bitcast.429), calls=%async_computation.21 | async-start | bytes 8388608
  2270.9 10.1 collective-permute-start.1
  2316.6 1668.1 %all-reduce.11.cloned.1.call-start = ((), (), s32[]{:S(2)}) async-start(), calls=%async_computation.20 | async-start | bytes 25690112 | tf_op jit(solution)/shard_map/psum | solution.py:264
  3752.9 366.6 %all-reduce.9.cloned.1.call-start = ((), (), s32[]{:S(2)}) async-start(), calls=%async_computation.19 | async-start | bytes 720896 | tf_op jit(solution)/shard_map/psum | solution.py:260
  (47 other events, 291.0 us)
Sparse Core Ops, SparseCore 0:
  9.5 481.7 all-gather.5
  492.9 464.6 all-gather.13
  959.7 122.4 all-gather.7
  1083.5 441.7 all-gather.11
  1526.7 441.0 all-gather.9
  2023.6 167.9 reduce-scatter.7
  2195.9 395.9 reduce-scatter.9
  2596.3 372.6 reduce-scatter.11
  2973.3 372.5 reduce-scatter.13
  3350.2 402.6 reduce-scatter.5
  3756.2 228.5 all-reduce.10
  3991.9 127.5 all-reduce.8
where the time goes:
time: 4140 us; the launch traced here: 4130 us
  waiting for transfers between devices  3450 us (83%)
  matrix products  394 us (10%)
  blocking collectives  148 us (4%)
  other arithmetic  66.6 us (2%)
    all_gather x1, waiting for transfers between devices, body(): lax.all_gather(in_weight, 'seq', axis=0, tiled=True)  472 us
    all_gather x1, waiting for transfers between devices, body(): lax.all_gather(up_weight, 'seq', axis=0, tiled=True)  437 us
    all_gather x1, waiting for transfers between devices, body(): lax.all_gather(gate_weight, 'seq', axis=0, tiled=True)  429 us
    reduce_scatter x1, waiting for transfers between devices, body(): lax.psum_scatter(term_in.astype(jnp.bfloat16), 'seq', scatter_dimension=0...  407 us
    reduce_scatter x1, waiting for transfers between devices, body(): lax.psum_scatter(term_up.astype(jnp.bfloat16), 'seq', scatter_dimension=0...  377 us
    reduce_scatter x1, waiting for transfers between devices, body(): lax.psum_scatter(term_down.astype(jnp.bfloat16), 'seq', scatter_dimension...  377 us
    all_gather x1, waiting for transfers between devices, body(): lax.all_gather(down_weight, 'seq', axis=0, tiled=True)  278 us
    reduce_scatter x1, waiting for transfers between devices, body(): lax.psum_scatter(term_gate.astype(jnp.bfloat16), 'seq', scatter_dimension...  261 us
  transfers between devices with their start and end apart: 16, of which 14 were waited for; matrix products, arithmetic and copies ran while one was open for 10% of the time, Pallas kernels for 0%

commit v1 on v0

v1 whole, which is shorter than its diff:
```python
import jax
import jax.numpy as jnp
from jax import lax
from jax.experimental import pallas as pl
from jax.experimental.pallas import tpu as pltpu
from jax.sharding import Mesh, PartitionSpec as P

epsilon = 1e-06
low = jnp.bfloat16
wide = jnp.float32
tile = 8
depth = 4
cores = 2


def turned(value, axis, by):
    length = lax.axis_size(axis)
    return lax.ppermute(value, axis, [(i, (i + by) % length) for i in range(length)])


def passed(value, axis, by):
    length = lax.axis_size(axis)
    pairs = [(i, i + by) for i in range(length) if 0 <= i + by < length]
    return lax.ppermute(value, axis, pairs)


def gather_slots(value, axis):
    length = lax.axis_size(axis)
    return jnp.stack([value] + [turned(value, axis, -d) for d in range(1, length)])


def sum_slots(partial, axis):
    length = lax.axis_size(axis)
    total = partial[0]
    for d in range(1, length):
        total = total + turned(partial[d].astype(low), axis, d).astype(wide)
    return total


def sum_axis(value, axis):
    length = lax.axis_size(axis)
    total = value
    for d in range(1, length):
        total = total + turned(value, axis, d)
    return total


def in_order(slots, axis):
    length = lax.axis_size(axis)
    place = lax.axis_index(axis)
    return jnp.stack(
        [lax.dynamic_index_in_dim(slots, (j - place) % length, 0, False) for j in range(length)]
    )


def gather_tokens(value):
    half = value.shape[0] // 2
    width = value.shape[-1]
    first = gather_slots(gather_slots(value[:half], "x"), "y")
    second = gather_slots(gather_slots(value[half:], "y"), "x")
    own = jnp.stack([first, jnp.swapaxes(second, 0, 1)])
    own = own.reshape(-1, width)
    length = lax.axis_size("c")
    return [own] + [turned(own, "c", -d) for d in range(1, length)]


def scatter_tokens(near, far, batch):
    width = near.shape[-1]
    total = near
    for d, part in enumerate(far):
        total = total + turned(part, "c", d + 1).astype(wide)
    grid = total.reshape(2, lax.axis_size("y"), lax.axis_size("x"), batch // 2, -1, width)
    first = sum_slots(sum_slots(jnp.swapaxes(grid[0], 0, 1), "x"), "y")
    second = sum_slots(sum_slots(grid[1], "y"), "x")
    return jnp.concatenate([first, second], axis=0)


def segments(weight, groups, offset):
    rows = weight.shape[0]
    spread = lax.axis_size("x")
    pairs = lax.axis_size("y") * lax.axis_size("c")
    pair = lax.axis_index("y") * lax.axis_size("c") + lax.axis_index("c")
    part = weight.shape[1] // (groups * depth * spread * pairs)
    place = (lax.axis_index("x") + offset) % spread
    picked = []
    for g in range(groups):
        for k in range(depth):
            start = (((g * depth + k) * spread + place) * pairs + pair) * part
            picked.append(lax.dynamic_slice_in_dim(weight, start, part, 1))
    return jnp.concatenate(picked, axis=1)


def column_tile(weight, groups):
    spread = lax.axis_size("x")
    place = lax.axis_index("x")
    got = jnp.stack(
        [segments(weight, groups, 0)]
        + [turned(segments(weight, groups, d), "x", d) for d in range(1, spread)]
    )
    ordered = jnp.stack(
        [lax.dynamic_index_in_dim(got, (place - j) % spread, 0, False) for j in range(spread)]
    )
    return lax.all_gather(ordered.reshape(-1, got.shape[-1]), "z", axis=0, tiled=True)


def row_tile(weight):
    pairs = lax.axis_size("y") * lax.axis_size("c")
    pair = lax.axis_index("y") * lax.axis_size("c") + lax.axis_index("c")
    part = weight.shape[0] // pairs
    return lax.all_gather(
        lax.dynamic_slice_in_dim(weight, pair * part, part, 0), "z", axis=0, tiled=True
    )


def column_owner(term, groups):
    spread, ycount, ccount = lax.axis_size("x"), lax.axis_size("y"), lax.axis_size("c")
    place = lax.axis_index("x")
    mine = lax.psum_scatter(term, "z", scatter_dimension=0, tiled=True)
    rows = mine.shape[0] // spread
    parts = mine.reshape(spread, rows, -1)
    slots = jnp.stack(
        [lax.dynamic_index_in_dim(parts, place, 0, False)]
        + [
            turned(lax.dynamic_index_in_dim(parts, (place - d) % spread, 0, False), "x", -d)
            for d in range(1, spread)
        ]
    )
    whole = gather_slots(gather_slots(slots, "y"), "c")
    part = mine.shape[1] // (groups * depth)
    pieces = []
    cplace, yplace = lax.axis_index("c"), lax.axis_index("y")
    ranks = {}
    flat = whole.reshape(-1, rows, mine.shape[1])
    for j in range(spread):
        for yy in range(ycount):
            for cc in range(ccount):
                slot = ((cc - cplace) % ccount * ycount + (yy - yplace) % ycount) * spread + (
                    j - place
                ) % spread
                ranks[j, yy, cc] = lax.dynamic_index_in_dim(flat, slot, 0, False)
    for g in range(groups):
        for k in range(depth):
            for j in range(spread):
                for yy in range(ycount):
                    for cc in range(ccount):
                        at = (g * depth + k) * part
                        pieces.append(ranks[j, yy, cc][:, at : at + part])
    return jnp.concatenate(pieces, axis=1).astype(wide)


def row_owner(term):
    mine = lax.psum_scatter(term, "z", scatter_dimension=0, tiled=True)
    whole = in_order(gather_slots(mine, "y"), "y")
    whole = in_order(gather_slots(whole, "c"), "c")
    return jnp.swapaxes(whole, 0, 1).reshape(-1, term.shape[1]).astype(wide)


def rank_rows(values, axis):
    spread, pairs = lax.axis_size("x"), lax.axis_size("y") * lax.axis_size("c")
    pair = lax.axis_index("y") * lax.axis_size("c") + lax.axis_index("c")
    part = values.shape[axis] // (depth * spread * pairs)
    return jnp.concatenate(
        [
            lax.dynamic_slice_in_dim(
                values, ((k * spread + lax.axis_index("x")) * pairs + pair) * part, part, axis
            )
            for k in range(depth)
        ],
        axis=axis,
    )


def all_channels(values):
    rows = values.shape[0]
    whole = in_order(gather_slots(values, "x"), "x")
    whole = in_order(gather_slots(whole, "y"), "y")
    whole = in_order(gather_slots(whole, "c"), "c")
    spread, ycount, ccount = lax.axis_size("x"), lax.axis_size("y"), lax.axis_size("c")
    whole = whole.reshape(ccount, ycount, spread, rows, depth, -1)
    return jnp.transpose(whole, (3, 4, 2, 1, 0, 5)).reshape(rows, -1)


def fill(source, target, place):
    groups, parts, inner, length = source.shape[:4]
    for j in range(parts):
        slot = lax.rem(j + parts - place, parts)
        for g in range(groups):
            for b in range(inner):
                target[g * inner + b, j * length : (j + 1) * length, :] = source[g, slot, b].astype(
                    wide
                )


def empty(source, target, place):
    groups, parts, inner, length = target.shape[:4]
    for j in range(parts):
        slot = lax.rem(j + parts - place, parts)
        for g in range(groups):
            for b in range(inner):
                target[g, slot, b] = source[g * inner + b, j * length : (j + 1) * length, :].astype(
                    low
                )


def halves(ref):
    return [ref[k * tile : (k + 1) * tile, :] for k in range(ref.shape[0] // tile)]


def row_of(ref, seq, at):
    return ref[seq, pl.ds(at, tile, stride=0), :]


def states_kernel(place_ref, signal_ref, decay_ref, state_ref, slope_ref, held):
    fill(signal_ref, held, place_ref[0])
    seqs, length, lanes = held.shape
    keep = [jnp.exp(-d) for d in halves(decay_ref)]
    count = len(keep)
    zero = jnp.zeros((tile, lanes), wide)

    def step(i, carry):
        state, slope = [list(v) for v in carry]
        for k in range(tile):
            for n in range(seqs):
                new = row_of(held, n, i * tile + k)
                for h in range(count):
                    at = n * count + h
                    slope[at] = keep[h] * (slope[at] + state[at])
                    state[at] = keep[h] * state[at] + new
        return tuple(state), tuple(slope)

    start = tuple(zero for _ in range(seqs * count))
    state, slope = lax.fori_loop(0, length // tile, step, (start, start))
    for n in range(seqs):
        for h in range(count):
            state_ref[n, h * tile : (h + 1) * tile, :] = state[n * count + h]
            slope_ref[n, h * tile : (h + 1) * tile, :] = slope[n * count + h]


def forward_kernel(place_ref, signal_ref, decay_ref, residue_ref, start_ref, out_ref, held, terms, made):
    fill(signal_ref, held, place_ref[0])
    seqs, length, lanes = held.shape
    keep = [jnp.exp(-d) for d in halves(decay_ref)]
    weigh = halves(residue_ref)
    count = len(keep)

    def step(i, carry):
        state = list(carry)
        for k in range(tile):
            for n in range(seqs):
                new = row_of(held, n, i * tile + k)
                total = None
                for h in range(count):
                    at = n * count + h
                    state[at] = keep[h] * state[at] + new
                    term = weigh[h] * state[at]
                    total = term if total is None else total + term
                terms[n, k * tile : (k + 1) * tile, :] = total
        for n in range(seqs):
            result = terms[n, pl.ds(0, tile, stride=tile), :]
            for p in range(1, tile):
                result = result + terms[n, pl.ds(p, tile, stride=tile), :]
            made[n, pl.ds(i * tile, tile), :] = result
        return tuple(state)

    start = tuple(
        start_ref[n, h * tile : (h + 1) * tile, :] for n in range(seqs) for h in range(count)
    )
    lax.fori_loop(0, length // tile, step, start)
    empty(made, out_ref, place_ref[0])


def later_kernel(place_ref, signal_ref, decay_ref, state_ref, held):
    fill(signal_ref, held, place_ref[0])
    seqs, length, lanes = held.shape
    keep = [jnp.exp(-d) for d in halves(decay_ref)]
    count = len(keep)

    def step(i, carry):
        state = list(carry)
        base = length - tile - i * tile
        for k in range(tile - 1, -1, -1):
            for n in range(seqs):
                new = row_of(held, n, base + k)
                for h in range(count):
                    at = n * count + h
                    state[at] = keep[h] * state[at] + new
        return tuple(state)

    zero = jnp.zeros((tile, lanes), wide)
    state = lax.fori_loop(0, length // tile, step, tuple(zero for _ in range(seqs * count)))
    for n in range(seqs):
        for h in range(count):
            state_ref[n, h * tile : (h + 1) * tile, :] = state[n * count + h]


def backward_kernel(
    place_ref,
    signal_ref,
    grad_ref,
    decay_ref,
    residue_ref,
    start_ref,
    slope_ref,
    end_ref,
    out_ref,
    residue_grad_ref,
    decay_grad_ref,
    held,
    grads,
    terms,
    made,
):
    fill(signal_ref, held, place_ref[0])
    fill(grad_ref, grads, place_ref[0])
    seqs, length, lanes = held.shape
    keep = [jnp.exp(-d) for d in halves(decay_ref)]
    weigh = halves(residue_ref)
    count = len(keep)
    zero = jnp.zeros((tile, lanes), wide)

    def ahead(i, carry):
        state, slope, first, second = [list(v) for v in carry]
        for k in range(tile):
            for n in range(seqs):
                new = row_of(held, n, i * tile + k)
                back = row_of(grads, n, i * tile + k)
                for h in range(count):
                    at = n * count + h
                    slope[at] = keep[h] * (slope[at] + state[at])
                    state[at] = keep[h] * state[at] + new
                    first[at] = first[at] + back * state[at]
                    second[at] = second[at] + back * slope[at]
        return tuple(state), tuple(slope), tuple(first), tuple(second)

    def load(ref):
        return tuple(
            ref[n, h * tile : (h + 1) * tile, :] for n in range(seqs) for h in range(count)
        )

    none = tuple(zero for _ in range(seqs * count))
    _, _, first, second = lax.fori_loop(
        0, length // tile, ahead, (load(start_ref), load(slope_ref), none, none)
    )
    for h in range(count):
        sum_first, sum_second = first[h], second[h]
        for n in range(1, seqs):
            sum_first = sum_first + first[n * count + h]
            sum_second = sum_second + second[n * count + h]
        residue_grad_ref[h * tile : (h + 1) * tile, :] = sum_first
        decay_grad_ref[h * tile : (h + 1) * tile, :] = -weigh[h] * sum_second

    def back_step(i, carry):
        state = list(carry)
        base = length - tile - i * tile
        for k in range(tile - 1, -1, -1):
            for n in range(seqs):
                new = row_of(grads, n, base + k)
                total = None
                for h in range(count):
                    at = n * count + h
                    state[at] = keep[h] * state[at] + new
                    term = weigh[h] * state[at]
                    total = term if total is None else total + term
                terms[n, k * tile : (k + 1) * tile, :] = total
        for n in range(seqs):
            result = terms[n, pl.ds(0, tile, stride=tile), :]
            for p in range(1, tile):
                result = result + terms[n, pl.ds(p, tile, stride=tile), :]
            made[n, pl.ds(base, tile), :] = result
        return tuple(state)

    lax.fori_loop(0, length // tile, back_step, load(end_ref))
    empty(made, out_ref, place_ref[0])


def conv_call(kernel, place, arrays, results, scratch, flops):
    channels = arrays[0].shape[-1]
    lanes = min(channels, 128)

    def spec(shape):
        lead = len(shape) - 1
        return pl.BlockSpec(shape[:-1] + (lanes,), lambda i, *_: (0,) * lead + (i,))

    return pl.pallas_call(
        kernel,
        out_shape=results,
        grid_spec=pltpu.PrefetchScalarGridSpec(
            num_scalar_prefetch=1,
            grid=(channels // lanes,),
            in_specs=[spec(a.shape) for a in arrays],
            out_specs=[spec(r.shape) for r in results],
            scratch_shapes=[pltpu.VMEM(s + (lanes,), wide) for s in scratch],
        ),
        compiler_params=pltpu.CompilerParams(
            dimension_semantics=("arbitrary",), vmem_limit_bytes=48 << 20
        ),
        cost_estimate=pl.CostEstimate(
            flops=flops, transcendentals=0, bytes_accessed=sum(a.size * 4 for a in arrays)
        ),
    )(place, *arrays)


def sizes(signal, poles):
    groups, parts, inner, length, channels = signal.shape
    return groups * inner, parts * length, channels, signal.size * poles


def states_of(place, signal, decay):
    seqs, length, channels, work = sizes(signal, decay.shape[0])
    shape = jax.ShapeDtypeStruct((seqs, decay.shape[0], channels), wide)
    return conv_call(
        states_kernel, place, [signal, decay], [shape, shape], [(seqs, length)], 4 * work
    )


def forward_of(place, signal, decay, residue, start):
    seqs, length, channels, work = sizes(signal, decay.shape[0])
    return conv_call(
        forward_kernel,
        place,
        [signal, decay, residue, start],
        [jax.ShapeDtypeStruct(signal.shape, low)],
        [(seqs, length), (seqs, tile * tile), (seqs, length)],
        4 * work,
    )[0]


def later_of(place, signal, decay):
    seqs, length, channels, work = sizes(signal, decay.shape[0])
    shape = jax.ShapeDtypeStruct((seqs, decay.shape[0], channels), wide)
    return conv_call(later_kernel, place, [signal, decay], [shape], [(seqs, length)], 2 * work)[0]


def backward_of(place, signal, grad, decay, residue, start, slope, end):
    seqs, length, channels, work = sizes(signal, decay.shape[0])
    shape = jax.ShapeDtypeStruct(decay.shape, wide)
    return conv_call(
        backward_kernel,
        place,
        [signal, grad, decay, residue, start, slope, end],
        [jax.ShapeDtypeStruct(signal.shape, low), shape, shape],
        [(seqs, length), (seqs, length), (seqs, tile * tile), (seqs, length)],
        12 * work,
    )


def rms_scale(values):
    return lax.rsqrt(jnp.mean(values * values, axis=-1, keepdims=True) + epsilon)


def norm_back(values, scale, gain, grad_normed):
    grad_gain = jnp.sum(grad_normed * values * scale, axis=(0, 1))
    scaled = grad_normed * gain
    grad_values = scale * scaled - values * scale * scale * scale * jnp.mean(
        scaled * values, axis=-1, keepdims=True
    )
    return (grad_values, grad_gain)


def dot(a, b, kind=wide):
    return jnp.dot(a, b, preferred_element_type=wide).astype(kind)


def dot_t(a, b, kind=wide):
    return lax.dot_general(a, b, (((1,), (1,)), ((), ())), preferred_element_type=wide).astype(kind)


def dot_w(a, b):
    return lax.dot_general(a, b, (((0,), (0,)), ((), ())), preferred_element_type=wide).astype(low)


def body(
    tokens,
    lengths,
    norm_gain,
    in_weight,
    conv_taps,
    filter_residue,
    filter_decay,
    out_weight,
    feed_gain,
    gate_weight,
    up_weight,
    down_weight,
    cotangent,
):
    spread = lax.axis_size("x")
    batch, local, width = tokens.shape
    place = lax.axis_index("z") * spread + lax.axis_index("x")
    position = place * local + jnp.arange(local)
    mask = (position[None, :] < lengths[:, None]).astype(wide)[..., None]
    block = spread * local

    w_in = column_tile(in_weight, 3)
    w_out = row_tile(out_weight)
    w_gate = column_tile(gate_weight, 1)
    w_up = column_tile(up_weight, 1)
    w_down = row_tile(down_weight)

    hidden = tokens.astype(wide)
    scale_one = rms_scale(hidden)
    normed = (hidden * scale_one * norm_gain).astype(low)
    normed_all = gather_tokens(normed)
    grad_out = cotangent.astype(wide) * mask
    grad_feed_all = gather_tokens(grad_out.astype(low))

    channels = w_out.shape[0]
    ycount = lax.axis_size("y")
    grid = (2 * ycount, spread, batch // 2, local)
    taps = jnp.concatenate(
        [rank_rows(conv_taps[:, g * width : (g + 1) * width], 1) for g in range(3)], axis=1
    )
    decay = rank_rows(filter_decay, 0).T
    residue = rank_rows(filter_residue, 0).T
    mixed = [dot(v, w_in, low).reshape(grid + (3 * channels,)) for v in normed_all]
    opening = (lax.axis_index("x") + jnp.arange(spread)) % spread == 0
    opening = opening[None, :, None, None, None]
    closing = (lax.axis_index("x") + jnp.arange(spread)) % spread == spread - 1
    closing = closing[None, :, None, None, None]

    tails = jnp.stack([jnp.roll(m[:, :, :, local - 2 :], 1, axis=1) for m in mixed])
    from_z = passed(tails, "z", 1)
    extended = []
    for m, tail, behind in zip(mixed, tails, from_z):
        extended.append(jnp.concatenate([jnp.where(opening, behind, tail), m], axis=3).astype(wide))
    short = [
        taps[0] * e[:, :, :, 2:] + taps[1] * e[:, :, :, 1:-1] + taps[2] * e[:, :, :, :-2]
        for e in extended
    ]
    query = [s[..., :channels] for s in short]
    keys = [s[..., channels : 2 * channels] for s in short]
    values = [s[..., 2 * channels :] for s in short]
    product = [(k * v).astype(low) for k, v in zip(keys, values)]

    spot = lax.axis_index("x").astype(jnp.int32).reshape(1)
    ends = [states_of(spot, p, decay) for p in product]
    state_end = jnp.stack([e[0] for e in ends])
    slope_end = jnp.stack([e[1] for e in ends])
    states = [passed(state_end, "z", k) for k in range(1, depth)]
    start = states[0]
    for k in range(1, depth - 1):
        start = start + jnp.exp(-decay * (k * block)) * states[k]
    convolved = [forward_of(spot, p, decay, residue, s) for p, s in zip(product, start)]
    gated = [(q * c.astype(wide)).astype(low).reshape(-1, channels) for q, c in zip(query, convolved)]
    mixer = scatter_tokens(dot(gated[0], w_out), [dot(g, w_out, low) for g in gated[1:]], batch)
    middle = hidden + mixer

    scale_two = rms_scale(middle)
    normed_two = (middle * scale_two * feed_gain).astype(low)
    normed_two_all = gather_tokens(normed_two)
    active, grad_gate, grad_upper = [], [], []
    for v, g in zip(normed_two_all, grad_feed_all):
        gate = dot(v, w_gate)
        upper = dot(v, w_up)
        sigma = jax.nn.sigmoid(gate)
        active.append((gate * sigma * upper).astype(low))
        grad_active = dot_t(g, w_down)
        grad_gate.append((grad_active * upper * sigma * (1.0 + gate * (1.0 - sigma))).astype(low))
        grad_upper.append((grad_active * gate * sigma).astype(low))

    def back_of(k, kind):
        return (dot_t(grad_gate[k], w_gate) + dot_t(grad_upper[k], w_up)).astype(kind)

    far = [back_of(k, low) for k in range(1, len(active))]
    grad_normed_two = scatter_tokens(back_of(0, wide), far, batch)
    feed = scatter_tokens(dot(active[0], w_down), [dot(a, w_down, low) for a in active[1:]], batch)
    output = (mask * (middle + feed)).astype(low)

    def joined(parts):
        return jnp.concatenate(parts, axis=0)

    normed_two_full = joined(normed_two_all)
    grad_down = row_owner(dot_w(joined(active), joined(grad_feed_all)))
    grad_gate_weight = column_owner(dot_w(normed_two_full, joined(grad_gate)), 1)
    grad_up_weight = column_owner(dot_w(normed_two_full, joined(grad_upper)), 1)

    grad_middle, grad_feed_gain = norm_back(middle, scale_two, feed_gain, grad_normed_two)
    grad_middle = grad_middle + grad_out
    grad_mix_all = gather_tokens(grad_middle.astype(low))
    grad_out_weight = row_owner(dot_w(joined(gated), joined(grad_mix_all)))

    grad_gated = [dot_t(g, w_out).reshape(grid + (channels,)) for g in grad_mix_all]
    grad_query = [g * c.astype(wide) for g, c in zip(grad_gated, convolved)]
    grad_conv = [(g * q).astype(low) for g, q in zip(grad_gated, query)]
    slopes = [passed(slope_end, "z", k) for k in range(1, depth)]
    slope = slopes[0]
    for k in range(1, depth - 1):
        slope = slope + jnp.exp(-decay * (k * block)) * (slopes[k] + (k * block) * states[k])
    later_end = jnp.stack([later_of(spot, g, decay) for g in grad_conv])
    laters = [passed(later_end, "z", -k) for k in range(1, depth)]
    later = laters[0]
    for k in range(1, depth - 1):
        later = later + jnp.exp(-decay * (k * block)) * laters[k]
    backs = [
        backward_of(spot, product[k], grad_conv[k], decay, residue, start[k], slope[k], later[k])
        for k in range(len(product))
    ]
    grad_product = [b[0].astype(wide) for b in backs]
    grad_poles = jnp.concatenate(
        [sum(b[1] for b in backs[1:]) + backs[0][1], sum(b[2] for b in backs[1:]) + backs[0][2]],
        axis=0,
    )
    grad_short = [
        jnp.concatenate([q, p * v, p * k], axis=-1)
        for q, p, v, k in zip(grad_query, grad_product, values, keys)
    ]
    heads = jnp.stack([jnp.roll(g[:, :, :, :2].astype(low), -1, axis=1) for g in grad_short])
    from_next = passed(heads, "z", -1)
    grad_mixed, grad_taps = [], []
    for g, e, head, ahead in zip(grad_short, extended, heads, from_next):
        whole = jnp.concatenate([g, jnp.where(closing, ahead, head).astype(wide)], axis=3)
        grad_mixed.append(
            (
                taps[0] * whole[:, :, :, :-2] + taps[1] * whole[:, :, :, 1:-1] + taps[2] * whole[:, :, :, 2:]
            )
            .astype(low)
            .reshape(-1, 3 * channels)
        )
        grad_taps.append(
            jnp.stack(
                [
                    jnp.sum(g * e[:, :, :, 2:], axis=(0, 1, 2, 3)),
                    jnp.sum(g * e[:, :, :, 1:-1], axis=(0, 1, 2, 3)),
                    jnp.sum(g * e[:, :, :, :-2], axis=(0, 1, 2, 3)),
                ]
            )
        )
    grad_taps = sum(grad_taps[1:]) + grad_taps[0]
    grad_in_weight = column_owner(dot_w(joined(normed_all), joined(grad_mixed)), 3)
    grad_normed = scatter_tokens(
        dot_t(grad_mixed[0], w_in), [dot_t(g, w_in, low) for g in grad_mixed[1:]], batch
    )
    grad_hidden, grad_norm_gain = norm_back(hidden, scale_one, norm_gain, grad_normed)
    grad_tokens = (grad_hidden + grad_middle).astype(low)

    gains = jnp.stack([grad_norm_gain, grad_feed_gain])
    for axis in ("x", "y", "c", "z"):
        gains = sum_axis(gains, axis)
    small = jnp.concatenate(
        [grad_poles]
        + [grad_taps[:, g * channels : (g + 1) * channels] for g in range(3)],
        axis=0,
    )
    small = all_channels(sum_axis(small, "z"))
    poles = decay.shape[0]
    grad_residue = small[:poles].T
    grad_decay = small[poles : 2 * poles].T
    grad_conv_taps = jnp.concatenate(
        [small[2 * poles + 3 * g : 2 * poles + 3 * g + 3] for g in range(3)], axis=1
    )
    return (
        output,
        grad_tokens,
        gains[0],
        grad_in_weight,
        grad_conv_taps,
        grad_residue,
        grad_decay,
        grad_out_weight,
        gains[1],
        grad_gate_weight,
        grad_up_weight,
        grad_down,
    )


def solution(mesh):
    pairs, blocks = mesh.shape["dp"], mesh.shape["seq"]
    devices = mesh.devices.reshape(pairs // cores, cores, depth, blocks // depth)
    inner = Mesh(devices, ("y", "c", "z", "x"))
    dp, seq = ("y", "c"), ("z", "x")
    tokens, rows = P(dp, seq, None), P(seq, None)
    return jax.shard_map(
        body,
        mesh=inner,
        in_specs=(
            tokens,
            P(dp),
            P(),
            rows,
            P(),
            P(),
            P(),
            rows,
            P(),
            rows,
            rows,
            rows,
            tokens,
        ),
        out_specs=(tokens, tokens, P(), rows, P(), P(), P(), rows, P(), rows, rows, rows),
        check_vma=False,
    )
```

time: 4140 us -> 933 us (0.23)
  waiting for transfers between devices: 3450 us -> 370 us
  matrix products: 394 us -> 174 us
  blocking collectives: 148 us -> 0 us
  starting transfers between devices: 20.7 us -> 113 us
  local copies, waits for them, and re-layouts: 38.8 us -> 125 us
    all_gather x5, waiting for transfers between devices: 1720 us -> 45.7 us  [the longest x2 28.9 us: row_tile(): lax.all_gather(lax.dynamic_slice_in_dim(weight, pair * part, part, 0), 'z...]
    reduce_scatter x5, waiting for transfers between devices: 1420 us -> 31.8 us  [the longest x2 31.7 us: row_owner(): mine = lax.psum_scatter(term, 'z', scatter_dimension=0, tiled=True)]
    psum x2 -> x0, waiting for transfers between devices: 264 us -> none  [the longest x1 146 us: body(): lax.psum(mixer_terms[0].astype(jnp.bfloat16), 'dp').astype(jnp.float32)]
    ppermute x2 -> x79, waiting for transfers between devices: 29.3 us -> 293 us  [the longest x68 261 us: turned(): lax.ppermute(value, axis, [(i, (i + by) % length) for i in range(length)])]
    dot_general x51 -> x25, matrix products: 394 us -> 174 us  [the longest x10 67 us: dot(): return jnp.dot(a, b, preferred_element_type=wide).astype(kind)]
    all_to_all x2 -> x0, blocking collectives: 105 us -> none  [the longest x1 55.5 us: body(): lax.all_to_all(grad_product_chan.astype(jnp.bfloat16), 'seq', split_axis=...]
    ppermute x2 -> x79, starting transfers between devices: 8.79 us -> 113 us  [the longest x68 89 us: turned(): lax.ppermute(value, axis, [(i, (i + by) % length) for i in range(length)])]
    psum x1 -> x0, blocking collectives: 43.2 us -> none  [body(): lax.psum((grad_norm_gain, grad_taps, grad_residue, grad_decay, grad_feed_...]
  transfers between devices with their start and end apart: 16 -> 89, of which waited for: 14 -> 42; matrix products, arithmetic and copies ran while one was open for 10% -> 31% of each run, Pallas kernels for 0% -> 2%
where the time goes in v1:
time: 933 us; the launch traced here: 921 us
  waiting for transfers between devices  370 us (40%)
  matrix products  174 us (19%)
  local copies, waits for them, and re-layouts  125 us (13%)
  starting transfers between devices  113 us (12%)
  other arithmetic  87.3 us (9%)
  Pallas kernels  33.7 us (4%)
  between operations  17.5 us (2%)
    ppermute x68, waiting for transfers between devices, turned(): lax.ppermute(value, axis, [(i, (i + by) % length) for i in range(length)])  261 us
    ppermute x68, starting transfers between devices, turned(): lax.ppermute(value, axis, [(i, (i + by) % length) for i in range(length)])  89 us
    dot_general x10, matrix products, dot(): return jnp.dot(a, b, preferred_element_type=wide).astype(kind)  67 us
    dot_general x10, matrix products, dot_t(): lax.dot_general(a, b, (((1,), (1,)), ((), ())), preferred_element_type=wide)  59 us
    dot_general x5, matrix products, dot_w(): lax.dot_general(a, b, (((0,), (0,)), ((), ())), preferred_element_type=wide)  48.3 us
    unnamed x287, local copies, waits for them, and re-layouts  46.7 us
    pallas_call x8, Pallas kernels, conv_call(): pl.pallas_call(kernel, out_shape=results, grid_spec=pltpu.PrefetchScalarG...  33.7 us
    ppermute x11, waiting for transfers between devices, passed(): return lax.ppermute(value, axis, pairs)  31.8 us
  transfers between devices with their start and end apart: 89, of which 42 were waited for; matrix products, arithmetic and copies ran while one was open for 31% of the time, Pallas kernels for 2%

profile of v1, /device:TPU:9, one launch (start us, length us, event | category | flops | bytes accessed | tf_op | source)
XLA Modules:
  0.0 921.0 jit_solution(15652864833272640421)
XLA Ops:
  30.3 9.4 %collective-permute-done.2 = bf16[1,128,2048]{2,1,0:T(8,128)(2,1)S(1)} collective-permute-done((bf16[1,128,2048]{2,1,0:T(8,128)(2,1)S(1)}, bf16[1,128,2048]{2,1,0:T(8,128)(2,1)S(1)}, u32[]{:S(2)}, u32[]{:S(2)}) %collective-permute-start.2) | collective-permute-done | bytes 524320 | tf_op jit(solution)/shard_map/ppermute | solution.py:18
  42.6 20.4 %collective-permute-done.3 = bf16[2,1,128,2048]{3,2,0,1:T(8,128)(2,1)S(1)} collective-permute-done((bf16[2,1,128,2048]{3,2,0,1:T(8,128)(2,1)S(1)}, bf16[2,1,128,2048]{3,2,0,1:T(8,128)(2,1)S(1)}, u32[]{:S(2)}, u32[]{:S(2)}) %collective-permute-start.3) | collective-permute-done | bytes 1048608 | tf_op jit(solution)/shard_map/ppermute | solution.py:18
  72.7 16.9 %all-gather.6.cloned.1.call-done = bf16[2048,768]{1,0:T(8,128)(2,1)} async-done(((bf16[512,768]{1,0:T(8,128)(2,1)}), bf16[2048,768]{1,0:T(8,128)(2,1)}) %all-gather.6.cloned.1.call-update) | async-done | bytes 3145744 | tf_op jit(solution)/shard_map/all_gather | solution.py:103
  172.2 8.4 collective-permute-done.20
  201.3 18.7 %collective-permute-done.13 = bf16[2,1,128,2048]{3,2,1,0:T(8,128)(2,1)} collective-permute-done((bf16[2,1,128,2048]{3,2,1,0:T(8,128)(2,1)}, bf16[2,1,128,2048]{3,2,1,0:T(8,128)(2,1)}, u32[]{:S(2)}, u32[]{:S(2)}) %collective-permute-start.13) | collective-permute-done | bytes 1048608 | tf_op jit(solution)/shard_map/ppermute | solution.py:18
  243.0 8.8 collective-permute-done.17
  267.4 19.5 %collective-permute-done.27 = bf16[1,128,2048]{2,1,0:T(8,128)(2,1)} collective-permute-done((bf16[1,128,2048]{2,1,0:T(8,128)(2,1)}, bf16[1,128,2048]{2,1,0:T(8,128)(2,1)}, u32[]{:S(2)}, u32[]{:S(2)}) %collective-permute-start.27) | collective-permute-done | bytes 524320 | tf_op jit(solution)/shard_map/ppermute | solution.py:18
  294.0 8.9 collective-permute-start.21
  318.1 14.3 %fusion.156 = f32[1024,704]{0,1:T(8,128)S(1)} fusion(bf16[1024,2048]{1,0:T(8,128)(2,1)} %bitcast.67, bf16[2048,704]{1,0:T(8,128)(2,1)} %all-gather.12.cloned.1.call-done), kind=kOutput, calls=%fused_computation.558 | convolution fusion | flops 2952790016 | bytes 9961472 | tf_op jit(solution)/shard_map/dot_general | solution.py:461
  332.4 8.0 fusion.155
  340.4 28.9 %all-gather.14.cloned.1.call-done = bf16[704,2048]{1,0:T(8,128)(2,1)} async-done(((bf16[176,2048]{1,0:T(8,128)(2,1)}), bf16[704,2048]{1,0:T(8,128)(2,1)}) %all-gather.14.cloned.1.call-update) | async-done | bytes 2883600 | tf_op jit(solution)/shard_map/all_gather | solution.py:110
  369.3 9.8 %multiply_convert_fusion.2 = (bf16[1024,704]{0,1:T(8,128)(2,1)S(1)}, bf16[1024,704]{0,1:T(8,128)(2,1)}, bf16[1024,704]{0,1:T(8,128)(2,1)}) fusion(f32[1024,704]{0,1:T(8,128)} %fusion.155, f32[1024,704]{0,1:T(8,128)S(1)} %fusion.156, bf16[1024,2048]{1,0:T(8,128)(2,1)} %bitcast.100, bf16[704,2048]{1,0:T(8,128)(2,1)} %all-gather.14.cloned.1.call-done), kind=kOutput, calls=%fused_computation.85 | convolution fusion | flops 2964324352 | bytes 17170432 | tf_op jit(solution)/shard_map/dot_general | solution.py:465
  390.0 8.1 multiply_convert_fusion
  399.1 9.7 %fusion.17 = bf16[2048,704]{0,1:T(8,128)(2,1)} fusion(bf16[1024,2048]{1,0:T(8,128)(2,1)} %collective-permute-done.21, bf16[1024,2048]{1,0:T(8,128)(2,1)} %bitcast.67, bf16[1024,704]{0,1:T(8,128)(2,1)S(1)} %get-tuple-element.76, bf16[1024,704]{0,1:T(8,128)(2,1)S(1)} %get-tuple-element.73), kind=kOutput, calls=%fused_computation.40 | convolution fusion | flops 5929566208 | bytes 14155776 | tf_op jit(solution)/shard_map/dot_general | solution.py:469
  408.9 10.6 %fusion.18 = bf16[2048,704]{0,1:T(8,128)(2,1)} fusion(bf16[1024,2048]{1,0:T(8,128)(2,1)} %collective-permute-done.21, bf16[1024,2048]{1,0:T(8,128)(2,1)} %bitcast.67, bf16[1024,704]{0,1:T(8,128)(2,1)} %get-tuple-element.77, bf16[1024,704]{0,1:T(8,128)(2,1)} %get-tuple-element.74), kind=kOutput, calls=%fused_computation.41 | convolution fusion | flops 5929566208 | bytes 14155776 | tf_op jit(solution)/shard_map/dot_general | solution.py:469
  444.0 9.7 %fusion.19 = bf16[704,2048]{1,0:T(8,128)(2,1)} fusion(bf16[1024,2048]{1,0:T(8,128)(2,1)} %collective-permute-done.31, bf16[1024,2048]{1,0:T(8,128)(2,1)} %bitcast.100, bf16[1024,704]{0,1:T(8,128)(2,1)S(1)} %copy-done.106, bf16[1024,704]{0,1:T(8,128)(2,1)S(1)} %copy-done.104), kind=kOutput, calls=%fused_computation.42 | convolution fusion | flops 5929566208 | bytes 14155776 | tf_op jit(solution)/shard_map/dot_general | solution.py:469
  480.9 8.0 collective-permute-done.25
  491.5 10.9 %collective-permute-done.23 = bf16[2,1,128,2048]{3,2,1,0:T(8,128)(2,1)S(1)} collective-permute-done((bf16[2,1,128,2048]{3,2,1,0:T(8,128)(2,1)S(1)}, bf16[2,1,128,2048]{3,2,1,0:T(8,128)(2,1)S(1)}, u32[]{:S(2)}, u32[]{:S(2)}) %collective-permute-start.23) | collective-permute-done | bytes 1048608 | tf_op jit(solution)/shard_map/ppermute | solution.py:18
  514.0 10.8 %collective-permute-done.33 = bf16[2,1,128,2048]{3,2,1,0:T(8,128)(2,1)S(1)} collective-permute-done((bf16[2,1,128,2048]{3,2,1,0:T(8,128)(2,1)S(1)}, bf16[2,1,128,2048]{3,2,1,0:T(8,128)(2,1)S(1)}, u32[]{:S(2)}, u32[]{:S(2)}) %collective-permute-start.33) | collective-permute-done | bytes 1048608 | tf_op jit(solution)/shard_map/ppermute | solution.py:18
  538.7 8.6 collective-permute-done.36
  550.7 31.7 %reduce-scatter.14.cloned.1.call-done = bf16[176,2048]{1,0:T(8,128)(2,1)} async-done(((bf16[704,2048]{1,0:T(8,128)(2,1)}), bf16[176,2048]{1,0:T(8,128)(2,1)}) %reduce-scatter.14.cloned.1.call-update) | async-done | bytes 720912 | tf_op jit(solution)/shard_map/reduce_scatter | solution.py:152
  597.4 13.5 %collective-permute-done.39 = bf16[1,128,2048]{2,1,0:T(8,128)(2,1)S(1)} collective-permute-done((bf16[1,128,2048]{2,1,0:T(8,128)(2,1)S(1)}, bf16[1,128,2048]{2,1,0:T(8,128)(2,1)S(1)}, u32[]{:S(2)}, u32[]{:S(2)}) %collective-permute-start.39) | collective-permute-done | bytes 524320 | tf_op jit(solution)/shard_map/ppermute | solution.py:18
  630.2 11.6 %collective-permute-done.75 = bf16[2,256,704]{1,2,0:T(8,128)(2,1)S(1)} collective-permute-done((bf16[2,256,704]{1,2,0:T(8,128)(2,1)S(1)}, bf16[2,256,704]{1,2,0:T(8,128)(2,1)S(1)}, u32[]{:S(2)}, u32[]{:S(2)}) %collective-permute-start.75) | collective-permute-done | bytes 720928 | tf_op jit(solution)/shard_map/ppermute | solution.py:18
  645.8 18.4 %collective-permute-done.38 = bf16[2,1,128,2048]{3,2,0,1:T(8,128)(2,1)S(1)} collective-permute-done((bf16[2,1,128,2048]{3,2,0,1:T(8,128)(2,1)S(1)}, bf16[2,1,128,2048]{3,2,0,1:T(8,128)(2,1)S(1)}, u32[]{:S(2)}, u32[]{:S(2)}) %collective-permute-start.38) | collective-permute-done | bytes 1048608 | tf_op jit(solution)/shard_map/ppermute | solution.py:18
  700.7 8.0 collective-permute-done.45
  708.7 8.6 shard_map.226
  717.7 8.6 shard_map.227
  776.0 11.6 %fusion.14 = bf16[2048,768]{1,0:T(8,128)(2,1)} fusion(bf16[1024,2048]{1,0:T(8,128)(2,1)} %collective-permute-done.5, bf16[1024,2048]{1,0:T(8,128)(2,1)} %bitcast.14, bf16[1024,768]{1,0:T(8,128)(2,1)} %bitcast.539, bf16[1024,768]{1,0:T(8,128)(2,1)} %bitcast.536), kind=kOutput, calls=%fused_computation.37 | convolution fusion | flops 6467092480 | bytes 14680064 | tf_op jit(solution)/shard_map/dot_general | solution.py:469
  810.9 15.3 %collective-permute-done.52 = bf16[2,1,128,2048]{3,2,1,0:T(8,128)(2,1)} collective-permute-done((bf16[2,1,128,2048]{3,2,1,0:T(8,128)(2,1)}, bf16[2,1,128,2048]{3,2,1,0:T(8,128)(2,1)}, u32[]{:S(2)}, u32[]{:S(2)}) %collective-permute-start.52) | collective-permute-done | bytes 1048608 | tf_op jit(solution)/shard_map/ppermute | solution.py:18
  836.5 9.3 %collective-permute-done.53 = bf16[1,128,2048]{2,1,0:T(8,128)(2,1)S(1)} collective-permute-done((bf16[1,128,2048]{2,1,0:T(8,128)(2,1)S(1)}, bf16[1,128,2048]{2,1,0:T(8,128)(2,1)S(1)}, u32[]{:S(2)}, u32[]{:S(2)}) %collective-permute-start.53) | collective-permute-done | bytes 524320 | tf_op jit(solution)/shard_map/ppermute | solution.py:18
  862.5 13.5 %collective-permute-done.55 = f32[2,2048]{1,0:T(2,128)S(1)} collective-permute-done((f32[2,2048]{1,0:T(2,128)S(1)}, f32[2,2048]{1,0:T(2,128)S(1)}, u32[]{:S(2)}, u32[]{:S(2)}) %collective-permute-start.55) | collective-permute-done | bytes 16416 | tf_op jit(solution)/shard_map/ppermute | solution.py:18
  898.6 9.9 %concatenate.228 = bf16[256,6144]{1,0:T(8,128)(2,1)} concatenate(bf16[256,64]{1,0:T(8,128)(2,1)} %get-tuple-element.337, bf16[256,64]{1,0:T(8,128)(2,1)} %get-tuple-element.325, bf16[256,64]{1,0:T(8,128)(2,1)} %get-tuple-element.313, bf16[256,64]{1,0:T(8,128)(2,1)} %get-tuple-element.301, bf16[256,64]{1,0:T(8,128)(2,1)} %get-tuple-element.289, ...), dimensions={1} | concatenate | bytes 6291456 | tf_op jit(solution)/shard_map/concatenate | solution.py:148
  (710 shorter events, 495.2 us)
Async XLA Ops:
  7.2 82.4 %all-gather.6.cloned.1.call-start = ((), (), s32[]{:S(2)}) async-start(), calls=%async_computation.5 | async-start | bytes 3932160 | tf_op jit(solution)/shard_map/all_gather | solution.py:103
  26.3 127.8 %all-gather.8.cloned.1.call-start = ((), (), s32[]{:S(2)}) async-start(), calls=%async_computation.6 | async-start | bytes 1310720 | tf_op jit(solution)/shard_map/all_gather | solution.py:110
  71.2 246.9 %all-gather.12.cloned.1.call-start = ((), (), s32[]{:S(2)}) async-start(), calls=%async_computation.8 | async-start | bytes 3932160 | tf_op jit(solution)/shard_map/all_gather | solution.py:103
  183.1 149.3 %all-gather.10.cloned.1.call-start = ((), (), s32[]{:S(2)}) async-start(), calls=%async_computation.7 | async-start | bytes 3932160 | tf_op jit(solution)/shard_map/all_gather | solution.py:103
  227.9 141.4 %all-gather.14.cloned.1.call-start = ((), (), s32[]{:S(2)}) async-start(), calls=%async_computation.9 | async-start | bytes 3604480 | tf_op jit(solution)/shard_map/all_gather | solution.py:110
  253.3 35.1 %collective-permute-start.18 = (bf16[2,1,128,2048]{3,2,1,0:T(8,128)(2,1)}, bf16[2,1,128,2048]{3,2,1,0:T(8,128)(2,1)}, u32[]{:S(2)}, u32[]{:S(2)}) collective-permute-start(bf16[2,1,128,2048]{3,2,1,0:T(8,128)(2,1)} %get-tuple-element.204), channel_id=1, source_target_pairs={{0,1},{1,0},{2,3},{3,2},{4,5},{5,4},{6,7},{7,6},{8,9},{9,8},{10,11... | collective-permute-start | bytes 3145736 | tf_op jit(solution)/shard_map/ppermute | solution.py:18
  256.0 30.9 %collective-permute-start.27 = (bf16[1,128,2048]{2,1,0:T(8,128)(2,1)}, bf16[1,128,2048]{2,1,0:T(8,128)(2,1)}, u32[]{:S(2)}, u32[]{:S(2)}) collective-permute-start(bf16[1,128,2048]{2,1,0:T(8,128)(2,1)} %get-tuple-element.194), channel_id=1, source_target_pairs={{0,1},{1,0},{2,3},{3,2},{4,5},{5,4},{6,7},{7,6},{8,9},{9,8},{10,11... | collective-permute-start | bytes 1572872 | tf_op jit(solution)/shard_map/ppermute | solution.py:18
  261.4 265.3 %reduce-scatter.12.cloned.1.call-start = ((), (), s32[]{:S(2)}) async-start(), calls=%async_computation.13 | async-start | bytes 3604480 | tf_op jit(solution)/shard_map/reduce_scatter | solution.py:118
  266.9 42.4 %collective-permute-start.30 = (bf16[2,1,128,2048]{3,2,1,0:T(8,128)(2,1)S(1)}, bf16[2,1,128,2048]{3,2,1,0:T(8,128)(2,1)S(1)}, u32[]{:S(2)}, u32[]{:S(2)}) collective-permute-start(bf16[2,1,128,2048]{3,2,1,0:T(8,128)(2,1)S(1)} %get-tuple-element.196), channel_id=1, source_target_pairs={{0,1},{1,0},{2,3},{3,2},{4,5},{5,4},{6,7},{7,6},{8,9},{9,8},{10,11... | collective-permute-start | bytes 3145736 | tf_op jit(solution)/shard_map/ppermute | solution.py:18
  294.0 85.1 %collective-permute-start.21 = (bf16[1024,2048]{1,0:T(8,128)(2,1)}, bf16[1024,2048]{1,0:T(8,128)(2,1)}, u32[]{:S(2)}, u32[]{:S(2)}) collective-permute-start(bf16[1024,2048]{1,0:T(8,128)(2,1)} %bitcast.67), channel_id=1, source_target_pairs={{0,8},{8,0},{1,9},{9,1},{2,10},{10,2},{3,11},{11,3},{4,12},{12,4},... | collective-permute-start | bytes 12582920 | tf_op jit(solution)/shard_map/ppermute | solution.py:18
  312.5 77.5 %collective-permute-start.31 = (bf16[1024,2048]{1,0:T(8,128)(2,1)}, bf16[1024,2048]{1,0:T(8,128)(2,1)}, u32[]{:S(2)}, u32[]{:S(2)}) collective-permute-start(bf16[1024,2048]{1,0:T(8,128)(2,1)} %bitcast.100), channel_id=1, source_target_pairs={{0,8},{8,0},{1,9},{9,1},{2,10},{10,2},{3,11},{11,3},{4,12},{12,4},... | collective-permute-start | bytes 12582920 | tf_op jit(solution)/shard_map/ppermute | solution.py:18
  408.9 124.2 %reduce-scatter.10.cloned.1.call-start = ((), (), s32[]{:S(2)}) async-start(), calls=%async_computation.12 | async-start | bytes 3604480 | tf_op jit(solution)/shard_map/reduce_scatter | solution.py:118
  419.5 162.8 %reduce-scatter.14.cloned.1.call-start = ((), (), s32[]{:S(2)}) async-start(), calls=%async_computation.14 | async-start | bytes 3604480 | tf_op jit(solution)/shard_map/reduce_scatter | solution.py:152
  453.7 335.9 %reduce-scatter.8.cloned.1.call-start = ((), (), s32[]{:S(2)}) async-start(), calls=%async_computation.11 | async-start | bytes 1310720 | tf_op jit(solution)/shard_map/reduce_scatter | solution.py:152
  479.6 31.8 %collective-permute-start.35 = (bf16[2,1,128,2048]{3,2,1,0:T(8,128)(2,1)S(1)}, bf16[2,1,128,2048]{3,2,1,0:T(8,128)(2,1)S(1)}, u32[]{:S(2)}, u32[]{:S(2)}) collective-permute-start(bf16[2,1,128,2048]{3,2,1,0:T(8,128)(2,1)S(1)} %bitcast.540), channel_id=1, source_target_pairs={{0,16},{16,0},{1,17},{17,1},{2,18},{18,2},{3,19},{19,3},{4,20},{20... | collective-permute-start | bytes 3145736 | tf_op jit(solution)/shard_map/ppermute | solution.py:18
  480.6 44.2 %collective-permute-start.33 = (bf16[2,1,128,2048]{3,2,1,0:T(8,128)(2,1)S(1)}, bf16[2,1,128,2048]{3,2,1,0:T(8,128)(2,1)S(1)}, u32[]{:S(2)}, u32[]{:S(2)}) collective-permute-start(bf16[2,1,128,2048]{3,2,1,0:T(8,128)(2,1)S(1)} %fusion.68), channel_id=1, source_target_pairs={{0,1},{1,0},{2,3},{3,2},{4,5},{5,4},{6,7},{7,6},{8,9},{9,8},{10,11... | collective-permute-start | bytes 3145736 | tf_op jit(solution)/shard_map/ppermute | solution.py:18
  490.2 96.5 %collective-permute-start.26 = (bf16[1,128,2048]{2,1,0:T(8,128)(2,1)}, bf16[1,128,2048]{2,1,0:T(8,128)(2,1)}, u32[]{:S(2)}, u32[]{:S(2)}) collective-permute-start(bf16[1,128,2048]{2,1,0:T(8,128)(2,1)} %fusion.87), channel_id=1, source_target_pairs={{0,1},{1,0},{2,3},{3,2},{4,5},{5,4},{6,7},{7,6},{8,9},{9,8},{10,11... | collective-permute-start | bytes 1572872 | tf_op jit(solution)/shard_map/ppermute | solution.py:18
  503.7 86.6 %collective-permute-start.24 = (bf16[1,128,2048]{2,1,0:T(8,128)(2,1)}, bf16[1,128,2048]{2,1,0:T(8,128)(2,1)}, u32[]{:S(2)}, u32[]{:S(2)}) collective-permute-start(bf16[1,128,2048]{2,1,0:T(8,128)(2,1)} %fusion.86), channel_id=1, source_target_pairs={{0,16},{16,0},{1,17},{17,1},{2,18},{18,2},{3,19},{19,3},{4,20},{20... | collective-permute-start | bytes 1572872 | tf_op jit(solution)/shard_map/ppermute | solution.py:18
  512.7 34.6 %collective-permute-start.36 = (bf16[1,128,2048]{2,1,0:T(8,128)(2,1)}, bf16[1,128,2048]{2,1,0:T(8,128)(2,1)}, u32[]{:S(2)}, u32[]{:S(2)}) collective-permute-start(bf16[1,128,2048]{2,1,0:T(8,128)(2,1)} %fusion.89), channel_id=1, source_target_pairs={{0,1},{1,0},{2,3},{3,2},{4,5},{5,4},{6,7},{7,6},{8,9},{9,8},{10,11... | collective-permute-start | bytes 1572872 | tf_op jit(solution)/shard_map/ppermute | solution.py:18
  526.1 56.3 %collective-permute-start.34 = (bf16[1,128,2048]{2,1,0:T(8,128)(2,1)}, bf16[1,128,2048]{2,1,0:T(8,128)(2,1)S(1)}, u32[]{:S(2)}, u32[]{:S(2)}) collective-permute-start(bf16[1,128,2048]{2,1,0:T(8,128)(2,1)} %fusion.88), channel_id=1, source_target_pairs={{0,16},{16,0},{1,17},{17,1},{2,18},{18,2},{3,19},{19,3},{4,20},{20... | collective-permute-start | bytes 1572872 | tf_op jit(solution)/shard_map/ppermute | solution.py:18
  531.9 63.2 %collective-permute-start.74 = (bf16[256,704]{0,1:T(8,128)(2,1)}, bf16[256,704]{0,1:T(8,128)(2,1)}, u32[]{:S(2)}, u32[]{:S(2)}) collective-permute-start(bf16[256,704]{0,1:T(8,128)(2,1)} %bitcast.489), channel_id=1, source_target_pairs={{0,1},{1,0},{2,3},{3,2},{4,5},{5,4},{6,7},{7,6},{8,9},{9,8},{10,11... | collective-permute-start | bytes 1081352 | tf_op jit(solution)/shard_map/ppermute | solution.py:18
  547.3 46.3 %collective-permute-start.71 = (bf16[256,704]{0,1:T(8,128)(2,1)}, bf16[256,704]{0,1:T(8,128)(2,1)}, u32[]{:S(2)}, u32[]{:S(2)}) collective-permute-start(bf16[256,704]{0,1:T(8,128)(2,1)} %bitcast.490), channel_id=1, source_target_pairs={{0,1},{1,0},{2,3},{3,2},{4,5},{5,4},{6,7},{7,6},{8,9},{9,8},{10,11... | collective-permute-start | bytes 1081352 | tf_op jit(solution)/shard_map/ppermute | solution.py:18
  582.4 31.3 %collective-permute-start.77 = (bf16[176,2048]{1,0:T(8,128)(2,1)}, bf16[176,2048]{1,0:T(8,128)(2,1)S(1)}, u32[]{:S(2)}, u32[]{:S(2)}) collective-permute-start(bf16[176,2048]{1,0:T(8,128)(2,1)} %reduce-scatter.14.cloned.1.call-done), channel_id=1, source_target_pairs={{0,16},{16,0},{1,17},{17,1},{2,18},{18,2},{3,19},{19,3},{4,20},{20... | collective-permute-start | bytes 2162696 | tf_op jit(solution)/shard_map/ppermute | solution.py:18
  594.7 31.6 %collective-permute-start.72 = (bf16[2,256,704]{1,2,0:T(8,128)(2,1)S(1)}, bf16[2,256,704]{1,2,0:T(8,128)(2,1)S(1)}, u32[]{:S(2)}, u32[]{:S(2)}) collective-permute-start(bf16[2,256,704]{1,2,0:T(8,128)(2,1)S(1)} %get-tuple-element.228), channel_id=1, source_target_pairs={{0,16},{16,0},{1,17},{17,1},{2,18},{18,2},{3,19},{19,3},{4,20},{20... | collective-permute-start | bytes 2162696 | tf_op jit(solution)/shard_map/ppermute | solution.py:18
  596.3 45.5 %collective-permute-start.75 = (bf16[2,256,704]{1,2,0:T(8,128)(2,1)S(1)}, bf16[2,256,704]{1,2,0:T(8,128)(2,1)S(1)}, u32[]{:S(2)}, u32[]{:S(2)}) collective-permute-start(bf16[2,256,704]{1,2,0:T(8,128)(2,1)S(1)} %get-tuple-element.224), channel_id=1, source_target_pairs={{0,16},{16,0},{1,17},{17,1},{2,18},{18,2},{3,19},{19,3},{4,20},{20... | collective-permute-start | bytes 2162696 | tf_op jit(solution)/shard_map/ppermute | solution.py:18
  611.0 34.6 %collective-permute-start.40 = (bf16[2,1,128,2048]{3,2,1,0:T(8,128)(2,1)S(1)}, bf16[2,1,128,2048]{3,2,1,0:T(8,128)(2,1)S(1)}, u32[]{:S(2)}, u32[]{:S(2)}) collective-permute-start(bf16[2,1,128,2048]{3,2,1,0:T(8,128)(2,1)S(1)} %get-tuple-element.188), channel_id=1, source_target_pairs={{0,1},{1,0},{2,3},{3,2},{4,5},{5,4},{6,7},{7,6},{8,9},{9,8},{10,11... | collective-permute-start | bytes 3145736 | tf_op jit(solution)/shard_map/ppermute | solution.py:18
  612.5 51.8 %collective-permute-start.38 = (bf16[2,1,128,2048]{3,2,0,1:T(8,128)(2,1)S(1)}, bf16[2,1,128,2048]{3,2,0,1:T(8,128)(2,1)S(1)}, u32[]{:S(2)}, u32[]{:S(2)}) collective-permute-start(bf16[2,1,128,2048]{3,2,0,1:T(8,128)(2,1)S(1)} %get-tuple-element.182), channel_id=1, source_target_pairs={{0,16},{16,0},{1,17},{17,1},{2,18},{18,2},{3,19},{19,3},{4,20},{20... | collective-permute-start | bytes 3145736 | tf_op jit(solution)/shard_map/ppermute | solution.py:18
  615.5 57.6 %collective-permute-start.78 = (bf16[2,176,2048]{2,1,0:T(8,128)(2,1)}, bf16[2,176,2048]{2,1,0:T(8,128)(2,1)}, u32[]{:S(2)}, u32[]{:S(2)}) collective-permute-start(bf16[2,176,2048]{2,1,0:T(8,128)(2,1)} %get-tuple-element.167), channel_id=1, source_target_pairs={{0,8},{8,0},{1,9},{9,1},{2,10},{10,2},{3,11},{11,3},{4,12},{12,4},... | collective-permute-start | bytes 4325384 | tf_op jit(solution)/shard_map/ppermute | solution.py:18
  627.6 51.1 %collective-permute-start.73 = (bf16[2,2,256,704]{2,3,1,0:T(8,128)(2,1)}, bf16[2,2,256,704]{2,3,1,0:T(8,128)(2,1)}, u32[]{:S(2)}, u32[]{:S(2)}) collective-permute-start(bf16[2,2,256,704]{2,3,1,0:T(8,128)(2,1)} %get-tuple-element.174), channel_id=1, source_target_pairs={{0,8},{8,0},{1,9},{9,1},{2,10},{10,2},{3,11},{11,3},{4,12},{12,4},... | collective-permute-start | bytes 4325384 | tf_op jit(solution)/shard_map/ppermute | solution.py:18
  643.1 37.3 %collective-permute-start.76 = (bf16[2,2,256,704]{2,3,1,0:T(8,128)(2,1)}, bf16[2,2,256,704]{2,3,1,0:T(8,128)(2,1)}, u32[]{:S(2)}, u32[]{:S(2)}) collective-permute-start(bf16[2,2,256,704]{2,3,1,0:T(8,128)(2,1)} %get-tuple-element.172), channel_id=1, source_target_pairs={{0,8},{8,0},{1,9},{9,1},{2,10},{10,2},{3,11},{11,3},{4,12},{12,4},... | collective-permute-start | bytes 4325384 | tf_op jit(solution)/shard_map/ppermute | solution.py:18
  747.2 42.7 %collective-permute-start.49 = (bf16[1024,2048]{1,0:T(8,128)(2,1)}, bf16[1024,2048]{1,0:T(8,128)(2,1)}, u32[]{:S(2)}, u32[]{:S(2)}) collective-permute-start(bf16[1024,2048]{1,0:T(8,128)(2,1)} %convolution_convert_fusion.2), channel_id=1, source_target_pairs={{0,8},{8,0},{1,9},{9,1},{2,10},{10,2},{3,11},{11,3},{4,12},{12,4},... | collective-permute-start | bytes 12582920 | tf_op jit(solution)/shard_map/ppermute | solution.py:18
  757.6 90.9 %reduce-scatter.6.cloned.1.call-start = ((), (), s32[]{:S(2)}) async-start(), calls=%async_computation.10 | async-start | bytes 3932160 | tf_op jit(solution)/shard_map/reduce_scatter | solution.py:118
  (172 other events, 2405.5 us)
Sparse Core Ops, SparseCore 0:
  26.4 63.0 all-gather.5
  91.7 28.7 all-gather.7
  183.2 62.3 all-gather.11
  247.6 62.1 all-gather.9
  311.2 57.9 all-gather.13
  409.0 56.5 reduce-scatter.11
  467.9 56.0 reduce-scatter.9
  526.3 56.0 reduce-scatter.13
  757.7 27.3 reduce-scatter.7
  787.7 60.7 reduce-scatter.5

commit v2 on v1

--- a/solution.py
+++ b/solution.py
@@ -13,6 +13,10 @@
 cores = 2
 
 
+def after(value, *earlier):
+    return lax.optimization_barrier((value, earlier))[0]
+
+
 def turned(value, axis, by):
     length = lax.axis_size(axis)
     return lax.ppermute(value, axis, [(i, (i + by) % length) for i in range(length)])
@@ -31,7 +35,7 @@
 
 def sum_slots(partial, axis):
     length = lax.axis_size(axis)
-    total = partial[0]
+    total = partial[0].astype(wide)
     for d in range(1, length):
         total = total + turned(partial[d].astype(low), axis, d).astype(wide)
     return total
@@ -45,6 +49,206 @@
     return total
 
 
+def swap_slots(slots):
+    ycount, spread = lax.axis_size("y"), lax.axis_size("x")
+    result = []
+    for dy in range(ycount):
+        line = []
+        for dx in range(spread):
+            sy, sx = (ycount - dy) % ycount, (spread - dx) % spread
+            if sy == 0 and sx == 0:
+                line.append(slots[0][0])
+                continue
+            pairs = [
+                (i * spread + j, (i + sy) % ycount * spread + (j + sx) % spread)
+                for i in range(ycount)
+                for j in range(spread)
+            ]
+            line.append(lax.ppermute(slots[sy][sx], ("y", "x"), pairs))
+        result.append(line)
+    return result
+
+
+def gather_tokens(value):
+    half = value.shape[0] // 2
+    width = value.shape[-1]
+    first = gather_slots(value[:half], "x")
+    second = gather_slots(value[half:], "y")
+    first = gather_slots(first, "y")
+    second = gather_slots(second, "x")
+    return jnp.stack([first, jnp.swapaxes(second, 0, 1)]).reshape(-1, width)
+
+
+def scatter_tokens(partial, batch):
+    width = partial.shape[-1]
+    grid = partial.reshape(2, lax.axis_size("y"), lax.axis_size("x"), batch // 2, -1, width)
+    first = sum_slots(jnp.swapaxes(grid[0], 0, 1), "x")
+    second = sum_slots(grid[1], "y")
+    first = sum_slots(first, "y")
+    second = sum_slots(second, "x")
+    return jnp.concatenate([first, second], axis=0)
+
+
+def pick_kernel(start_ref, *refs):
+    count = len(refs) // 2
+    for source, target in zip(refs[:count], refs[count:]):
+        target[...] = source[...]
+
+
+def column_pieces(weight, groups):
+    spread, ycount = lax.axis_size("x"), lax.axis_size("y")
+    rows = weight.shape[0]
+    count = groups * depth
+    part = weight.shape[1] // (count * spread * ycount)
+    starts = [
+        (lax.axis_index("x") + d) % spread * ycount + lax.axis_index("y") for d in range(spread)
+    ]
+    if part % 128 == 0:
+
+        def source(d):
+            return pl.BlockSpec(
+                (rows, part), lambda i, start, d=d: (0, i * spread * ycount + start[d])
+            )
+
+        return pl.pallas_call(
+            pick_kernel,
+            out_shape=[jax.ShapeDtypeStruct((rows, count * part), weight.dtype)] * spread,
+            grid_spec=pltpu.PrefetchScalarGridSpec(
+                num_scalar_prefetch=1,
+                grid=(count,),
+                in_specs=[source(d) for d in range(spread)],
+                out_specs=[pl.BlockSpec((rows, part), lambda i, start: (0, i))] * spread,
+            ),
+            cost_estimate=pl.CostEstimate(
+                flops=0, transcendentals=0, bytes_accessed=4 * rows * count * part * spread
+            ),
+        )(jnp.stack(starts).astype(jnp.int32), *[weight] * spread)
+    return [
+        jnp.concatenate(
+            [
+                lax.dynamic_slice_in_dim(weight, (k * spread * ycount + start) * part, part, 1)
+                for k in range(count)
+            ],
+            axis=1,
+        )
+        for start in starts
+    ]
+
+
+def column_block(pieces):
+    spread, ccount = lax.axis_size("x"), lax.axis_size("c")
+    share = spread // ccount
+    place, core = lax.axis_index("x"), lax.axis_index("c")
+    got = [pieces[0]]
+    for d in range(1, spread):
+        pairs = [
+            (i // share * spread + i, i // share * spread + (i + d) % spread) for i in range(spread)
+        ]
+        got.append(lax.ppermute(pieces[d], ("c", "x"), pairs))
+    got = jnp.stack(got)
+    return jnp.concatenate(
+        [
+            lax.dynamic_index_in_dim(got, (place - core * share - j) % spread, 0, False)
+            for j in range(share)
+        ]
+    )
+
+
+def row_block(weight):
+    ycount, ccount = lax.axis_size("y"), lax.axis_size("c")
+    part = weight.shape[0] // (ycount * ccount)
+    pair = lax.axis_index("y") * ccount + lax.axis_index("c")
+    return lax.dynamic_slice_in_dim(weight, pair * part, part, 0)
+
+
+def core_halves(value):
+    ccount = lax.axis_size("c")
+    width = value.shape[1] // ccount
+    core = lax.axis_index("c")
+    return [
+        lax.dynamic_slice_in_dim(value, (core + d) % ccount * width, width, 1)
+        for d in range(ccount)
+    ]
+
+
+def gather_halves(value):
+    return gather_tokens(value.reshape(2, value.shape[0] // 2, -1))
+
+
+def gather_out(weight):
+    ycount = lax.axis_size("y")
+    part = weight.shape[0] // ycount
+    rows = lax.dynamic_slice_in_dim(weight, lax.axis_index("y") * part, part, 0)
+    block = core_halves(rows)[0]
+    held = in_order(gather_slots(block, "z"), "z").reshape(depth * part, -1)
+    mine = gather_halves(held)
+    return [mine] + [turned(mine, "c", -d) for d in range(1, lax.axis_size("c"))]
+
+
+def out_owner(terms):
+    total = terms[0].astype(wide)
+    for d in range(1, len(terms)):
+        total = total + turned(terms[d], "c", d).astype(wide)
+    mine = scatter_tokens(total.astype(low), 2)
+    mine = mine.reshape(depth, -1, mine.shape[-1]).astype(low)
+    place = lax.axis_index("z")
+    slots = jnp.stack(
+        [lax.dynamic_index_in_dim(mine, (place + d) % depth, 0, False) for d in range(depth)]
+    )
+    mine = sum_slots(slots, "z").astype(low)
+    whole = in_order(gather_slots(mine, "y"), "y")
+    whole = in_order(gather_slots(whole, "c"), "c")
+    ccount, ycount, rows, width = whole.shape
+    return jnp.transpose(whole, (1, 2, 0, 3)).reshape(ycount * rows, ccount * width).astype(wide)
+
+
+def gather_tile(block):
+    return lax.all_gather(block, ("z", "c"), axis=0, tiled=True)
+
+
+def scatter_tile(term):
+    return lax.psum_scatter(term, ("z", "c"), scatter_dimension=0, tiled=True)
+
+
+def column_owner(mine, groups):
+    spread, ycount, ccount = lax.axis_size("x"), lax.axis_size("y"), lax.axis_size("c")
+    share = spread // ccount
+    place, core, yplace = lax.axis_index("x"), lax.axis_index("c"), lax.axis_index("y")
+    rows = mine.shape[0] // share
+    width = mine.shape[1]
+    parts = mine.reshape(share, rows, width)
+    got = []
+    for d in range(spread):
+        send = lax.dynamic_index_in_dim(
+            parts, jnp.clip((place + d) % spread - core * share, 0, share - 1), 0, False
+        )
+        if d > 0:
+            pairs = [
+                ((i + d) % spread // share * spread + i, i // share * spread + (i + d) % spread)
+                for i in range(spread)
+            ]
+            send = lax.ppermute(send, ("c", "x"), pairs)
+        got.append(send)
+    got = jnp.stack(got)
+    held = jnp.stack(
+        [
+            lax.dynamic_index_in_dim(got, (place - core * share - j) % spread, 0, False)
+            for j in range(share)
+        ]
+    )
+    flat = gather_slots(gather_slots(held, "y"), "c").reshape(-1, rows, width)
+    part = width // (groups * depth)
+    ranks = []
+    for i in range(spread):
+        for k in range(ycount):
+            slot = (i // share - core) % ccount * ycount + (k - yplace) % ycount
+            ranks.append(lax.dynamic_index_in_dim(flat, slot * share + i % share, 0, False))
+    pieces = []
+    for at in range(groups * depth):
+        pieces += [r[:, at * part : (at + 1) * part] for r in ranks]
+    return jnp.concatenate(pieces, axis=1).astype(wide)
+
+
 def in_order(slots, axis):
     length = lax.axis_size(axis)
     place = lax.axis_index(axis)
@@ -53,131 +257,31 @@
     )
 
 
-def gather_tokens(value):
-    half = value.shape[0] // 2
-    width = value.shape[-1]
-    first = gather_slots(gather_slots(value[:half], "x"), "y")
-    second = gather_slots(gather_slots(value[half:], "y"), "x")
-    own = jnp.stack([first, jnp.swapaxes(second, 0, 1)])
-    own = own.reshape(-1, width)
-    length = lax.axis_size("c")
-    return [own] + [turned(own, "c", -d) for d in range(1, length)]
-
-
-def scatter_tokens(near, far, batch):
-    width = near.shape[-1]
-    total = near
-    for d, part in enumerate(far):
-        total = total + turned(part, "c", d + 1).astype(wide)
-    grid = total.reshape(2, lax.axis_size("y"), lax.axis_size("x"), batch // 2, -1, width)
-    first = sum_slots(sum_slots(jnp.swapaxes(grid[0], 0, 1), "x"), "y")
-    second = sum_slots(sum_slots(grid[1], "y"), "x")
-    return jnp.concatenate([first, second], axis=0)
-
-
-def segments(weight, groups, offset):
-    rows = weight.shape[0]
-    spread = lax.axis_size("x")
-    pairs = lax.axis_size("y") * lax.axis_size("c")
-    pair = lax.axis_index("y") * lax.axis_size("c") + lax.axis_index("c")
-    part = weight.shape[1] // (groups * depth * spread * pairs)
-    place = (lax.axis_index("x") + offset) % spread
-    picked = []
-    for g in range(groups):
-        for k in range(depth):
-            start = (((g * depth + k) * spread + place) * pairs + pair) * part
-            picked.append(lax.dynamic_slice_in_dim(weight, start, part, 1))
-    return jnp.concatenate(picked, axis=1)
-
-
-def column_tile(weight, groups):
-    spread = lax.axis_size("x")
-    place = lax.axis_index("x")
-    got = jnp.stack(
-        [segments(weight, groups, 0)]
-        + [turned(segments(weight, groups, d), "x", d) for d in range(1, spread)]
-    )
-    ordered = jnp.stack(
-        [lax.dynamic_index_in_dim(got, (place - j) % spread, 0, False) for j in range(spread)]
-    )
-    return lax.all_gather(ordered.reshape(-1, got.shape[-1]), "z", axis=0, tiled=True)
-
-
-def row_tile(weight):
-    pairs = lax.axis_size("y") * lax.axis_size("c")
-    pair = lax.axis_index("y") * lax.axis_size("c") + lax.axis_index("c")
-    part = weight.shape[0] // pairs
-    return lax.all_gather(
-        lax.dynamic_slice_in_dim(weight, pair * part, part, 0), "z", axis=0, tiled=True
-    )
-
-
-def column_owner(term, groups):
-    spread, ycount, ccount = lax.axis_size("x"), lax.axis_size("y"), lax.axis_size("c")
-    place = lax.axis_index("x")
-    mine = lax.psum_scatter(term, "z", scatter_dimension=0, tiled=True)
-    rows = mine.shape[0] // spread
-    parts = mine.reshape(spread, rows, -1)
-    slots = jnp.stack(
-        [lax.dynamic_index_in_dim(parts, place, 0, False)]
-        + [
-            turned(lax.dynamic_index_in_dim(parts, (place - d) % spread, 0, False), "x", -d)
-            for d in range(1, spread)
-        ]
-    )
-    whole = gather_slots(gather_slots(slots, "y"), "c")
-    part = mine.shape[1] // (groups * depth)
-    pieces = []
-    cplace, yplace = lax.axis_index("c"), lax.axis_index("y")
-    ranks = {}
-    flat = whole.reshape(-1, rows, mine.shape[1])
-    for j in range(spread):
-        for yy in range(ycount):
-            for cc in range(ccount):
-                slot = ((cc - cplace) % ccount * ycount + (yy - yplace) % ycount) * spread + (
-                    j - place
-                ) % spread
-                ranks[j, yy, cc] = lax.dynamic_index_in_dim(flat, slot, 0, False)
-    for g in range(groups):
-        for k in range(depth):
-            for j in range(spread):
-                for yy in range(ycount):
-                    for cc in range(ccount):
-                        at = (g * depth + k) * part
-                        pieces.append(ranks[j, yy, cc][:, at : at + part])
-    return jnp.concatenate(pieces, axis=1).astype(wide)
-
-
-def row_owner(term):
-    mine = lax.psum_scatter(term, "z", scatter_dimension=0, tiled=True)
+def row_owner(mine):
     whole = in_order(gather_slots(mine, "y"), "y")
     whole = in_order(gather_slots(whole, "c"), "c")
-    return jnp.swapaxes(whole, 0, 1).reshape(-1, term.shape[1]).astype(wide)
+    return jnp.swapaxes(whole, 0, 1).reshape(-1, mine.shape[1]).astype(wide)
 
 
 def rank_rows(values, axis):
-    spread, pairs = lax.axis_size("x"), lax.axis_size("y") * lax.axis_size("c")
-    pair = lax.axis_index("y") * lax.axis_size("c") + lax.axis_index("c")
-    part = values.shape[axis] // (depth * spread * pairs)
+    spread, ycount = lax.axis_size("x"), lax.axis_size("y")
+    part = values.shape[axis] // (depth * spread * ycount)
+    place = lax.axis_index("x") * ycount + lax.axis_index("y")
     return jnp.concatenate(
         [
-            lax.dynamic_slice_in_dim(
-                values, ((k * spread + lax.axis_index("x")) * pairs + pair) * part, part, axis
-            )
+            lax.dynamic_slice_in_dim(values, (k * spread * ycount + place) * part, part, axis)
             for k in range(depth)
         ],
         axis=axis,
     )
 
 
-def all_channels(values):
-    rows = values.shape[0]
-    whole = in_order(gather_slots(values, "x"), "x")
-    whole = in_order(gather_slots(whole, "y"), "y")
-    whole = in_order(gather_slots(whole, "c"), "c")
-    spread, ycount, ccount = lax.axis_size("x"), lax.axis_size("y"), lax.axis_size("c")
-    whole = whole.reshape(ccount, ycount, spread, rows, depth, -1)
-    return jnp.transpose(whole, (3, 4, 2, 1, 0, 5)).reshape(rows, -1)
+def all_channels(slots):
+    whole = in_order(slots, "y")
+    whole = in_order(jnp.swapaxes(whole, 0, 1), "x")
+    spread, ycount, rows = whole.shape[:3]
+    whole = whole.reshape(spread, ycount, rows, depth, -1)
+    return jnp.transpose(whole, (2, 3, 0, 1, 4)).reshape(rows, -1)
 
 
 def fill(source, target, place):
@@ -484,167 +588,192 @@
     down_weight,
     cotangent,
 ):
-    spread = lax.axis_size("x")
+    spread, ycount = lax.axis_size("x"), lax.axis_size("y")
     batch, local, width = tokens.shape
     place = lax.axis_index("z") * spread + lax.axis_index("x")
     position = place * local + jnp.arange(local)
     mask = (position[None, :] < lengths[:, None]).astype(wide)[..., None]
     block = spread * local
 
-    w_in = column_tile(in_weight, 3)
-    w_out = row_tile(out_weight)
-    w_gate = column_tile(gate_weight, 1)
-    w_up = column_tile(up_weight, 1)
-    w_down = row_tile(down_weight)
-
+    in_pieces = column_pieces(in_weight, 3)
+    out_weight, tokens = after((out_weight, tokens), in_pieces)
+    in_block = column_block(in_pieces)
     hidden = tokens.astype(wide)
     scale_one = rms_scale(hidden)
     normed = (hidden * scale_one * norm_gain).astype(low)
     normed_all = gather_tokens(normed)
+    gate_weight, down_weight, up_weight = after(
+        (gate_weight, down_weight, up_weight), normed, in_block
+    )
+    gate_block = column_block(column_pieces(gate_weight, 1))
+    up_block = column_block(column_pieces(up_weight, 1))
+    down_piece = after(row_block(down_weight), gate_block)
+    up_block = after(up_block, down_piece)
+    w_in = gather_tile(in_block)
+    w_gate = gather_tile(gate_block)
+    w_down = gather_tile(down_piece)
+    w_up = gather_tile(up_block)
+    w_out = gather_out(out_weight)
+    cotangent = after(cotangent, normed_all, gate_block, up_block)
     grad_out = cotangent.astype(wide) * mask
     grad_feed_all = gather_tokens(grad_out.astype(low))
 
-    channels = w_out.shape[0]
-    ycount = lax.axis_size("y")
+    channels = w_in.shape[1] // 3
     grid = (2 * ycount, spread, batch // 2, local)
     taps = jnp.concatenate(
         [rank_rows(conv_taps[:, g * width : (g + 1) * width], 1) for g in range(3)], axis=1
     )
     decay = rank_rows(filter_decay, 0).T
     residue = rank_rows(filter_residue, 0).T
-    mixed = [dot(v, w_in, low).reshape(grid + (3 * channels,)) for v in normed_all]
+    mixed = dot(normed_all, w_in, low).reshape(grid + (3 * channels,))
     opening = (lax.axis_index("x") + jnp.arange(spread)) % spread == 0
     opening = opening[None, :, None, None, None]
     closing = (lax.axis_index("x") + jnp.arange(spread)) % spread == spread - 1
     closing = closing[None, :, None, None, None]
 
-    tails = jnp.stack([jnp.roll(m[:, :, :, local - 2 :], 1, axis=1) for m in mixed])
-    from_z = passed(tails, "z", 1)
-    extended = []
-    for m, tail, behind in zip(mixed, tails, from_z):
-        extended.append(jnp.concatenate([jnp.where(opening, behind, tail), m], axis=3).astype(wide))
-    short = [
-        taps[0] * e[:, :, :, 2:] + taps[1] * e[:, :, :, 1:-1] + taps[2] * e[:, :, :, :-2]
-        for e in extended
-    ]
-    query = [s[..., :channels] for s in short]
-    keys = [s[..., channels : 2 * channels] for s in short]
-    values = [s[..., 2 * channels :] for s in short]
-    product = [(k * v).astype(low) for k, v in zip(keys, values)]
+    tail = jnp.roll(mixed[:, :, :, local - 2 :], 1, axis=1)
+    behind = passed(tail, "z", 1)
+    extended = jnp.concatenate([jnp.where(opening, behind, tail), mixed], axis=3).astype(wide)
+    short = (
+        taps[0] * extended[:, :, :, 2:]
+        + taps[1] * extended[:, :, :, 1:-1]
+        + taps[2] * extended[:, :, :, :-2]
+    )
+    query = short[..., :channels]
+    keys = short[..., channels : 2 * channels]
+    values = short[..., 2 * channels :]
+    product = (keys * values).astype(low)
 
     spot = lax.axis_index("x").astype(jnp.int32).reshape(1)
-    ends = [states_of(spot, p, decay) for p in product]
-    state_end = jnp.stack([e[0] for e in ends])
-    slope_end = jnp.stack([e[1] for e in ends])
+    state_end, slope_end = states_of(spot, product, decay)
     states = [passed(state_end, "z", k) for k in range(1, depth)]
     start = states[0]
     for k in range(1, depth - 1):
         start = start + jnp.exp(-decay * (k * block)) * states[k]
-    convolved = [forward_of(spot, p, decay, residue, s) for p, s in zip(product, start)]
-    gated = [(q * c.astype(wide)).astype(low).reshape(-1, channels) for q, c in zip(query, convolved)]
-    mixer = scatter_tokens(dot(gated[0], w_out), [dot(g, w_out, low) for g in gated[1:]], batch)
+    convolved = forward_of(spot, product, decay, residue, start)
+    gated = (query * convolved.astype(wide)).astype(low)
+    gated_slots = gated.reshape(2, ycount, spread, -1, channels)
+    got = swap_slots(
+        [
+            [gated_slots[:, k, i].reshape(-1, channels) for i in range(spread)]
+            for k in range(ycount)
+        ]
+    )
+    half = channels // 2
+    gated_own = jnp.concatenate(
+        [g[:, h * half : (h + 1) * half] for h in range(2) for line in got for g in line], axis=1
+    )
+    mixer = in_order(jnp.stack([dot(gated_own, w) for w in w_out]), "c")
+    mixer = jnp.concatenate([m for m in mixer], axis=1).reshape(batch, local, width)
     middle = hidden + mixer
 
     scale_two = rms_scale(middle)
     normed_two = (middle * scale_two * feed_gain).astype(low)
     normed_two_all = gather_tokens(normed_two)
-    active, grad_gate, grad_upper = [], [], []
-    for v, g in zip(normed_two_all, grad_feed_all):
-        gate = dot(v, w_gate)
-        upper = dot(v, w_up)
-        sigma = jax.nn.sigmoid(gate)
-        active.append((gate * sigma * upper).astype(low))
-        grad_active = dot_t(g, w_down)
-        grad_gate.append((grad_active * upper * sigma * (1.0 + gate * (1.0 - sigma))).astype(low))
-        grad_upper.append((grad_active * gate * sigma).astype(low))
-
-    def back_of(k, kind):
-        return (dot_t(grad_gate[k], w_gate) + dot_t(grad_upper[k], w_up)).astype(kind)
-
-    far = [back_of(k, low) for k in range(1, len(active))]
-    grad_normed_two = scatter_tokens(back_of(0, wide), far, batch)
-    feed = scatter_tokens(dot(active[0], w_down), [dot(a, w_down, low) for a in active[1:]], batch)
-    output = (mask * (middle + feed)).astype(low)
-
-    def joined(parts):
-        return jnp.concatenate(parts, axis=0)
-
-    normed_two_full = joined(normed_two_all)
-    grad_down = row_owner(dot_w(joined(active), joined(grad_feed_all)))
-    grad_gate_weight = column_owner(dot_w(normed_two_full, joined(grad_gate)), 1)
-    grad_up_weight = column_owner(dot_w(normed_two_full, joined(grad_upper)), 1)
+    gate = dot(normed_two_all, w_gate)
+    sigma = jax.nn.sigmoid(gate)
+    grad_active = dot_t(grad_feed_all, w_down)
+    grad_upper = (grad_active * gate * sigma).astype(low)
+    up_term = dot_w(normed_two_all, grad_upper)
+    up_mine = scatter_tile(up_term)
+    upper = dot(normed_two_all, after(w_up, up_term))
+    active = (gate * sigma * upper).astype(low)
+    grad_gate = (grad_active * upper * sigma * (1.0 + gate * (1.0 - sigma))).astype(low)
+    partial_two = (dot_t(grad_gate, w_gate) + dot_t(grad_upper, w_up)).astype(low)
+    grad_normed_two = scatter_tokens(partial_two, batch)
+    weigh_two, weigh_gate = after((normed_two_all, grad_gate), partial_two)
+    gate_mine = scatter_tile(dot_w(weigh_two, weigh_gate))
 
     grad_middle, grad_feed_gain = norm_back(middle, scale_two, feed_gain, grad_normed_two)
     grad_middle = grad_middle + grad_out
-    grad_mix_all = gather_tokens(grad_middle.astype(low))
-    grad_out_weight = row_owner(dot_w(joined(gated), joined(grad_mix_all)))
-
-    grad_gated = [dot_t(g, w_out).reshape(grid + (channels,)) for g in grad_mix_all]
-    grad_query = [g * c.astype(wide) for g, c in zip(grad_gated, convolved)]
-    grad_conv = [(g * q).astype(low) for g, q in zip(grad_gated, query)]
+    grad_mix = grad_middle.astype(low).reshape(-1, width)
+
+    mix_parts = core_halves(grad_mix)
+    grad_gated_own = sum(dot_t(m, w) for m, w in zip(mix_parts, w_out)).astype(low)
+    grad_slots = grad_gated_own.reshape(-1, 2, ycount, spread, half)
+    got = swap_slots(
+        [
+            [grad_slots[:, :, k, i].reshape(-1, channels) for i in range(spread)]
+            for k in range(ycount)
+        ]
+    )
+    grad_gated = jnp.stack([jnp.stack(line) for line in got])
+    grad_gated = grad_gated.reshape(ycount, spread, 2, batch // 2, local, channels)
+    grad_gated = jnp.moveaxis(grad_gated, 2, 0).reshape(grid + (channels,)).astype(wide)
+    grad_query = grad_gated * convolved.astype(wide)
+    grad_conv = (grad_gated * query).astype(low)
+
+    later_end = later_of(spot, grad_conv, decay)
+    laters = [passed(later_end, "z", -k) for k in range(1, depth)]
+    later = laters[0]
+    for k in range(1, depth - 1):
+        later = later + jnp.exp(-decay * (k * block)) * laters[k]
+    slope_end = after(slope_end, normed_two_all)
     slopes = [passed(slope_end, "z", k) for k in range(1, depth)]
     slope = slopes[0]
     for k in range(1, depth - 1):
         slope = slope + jnp.exp(-decay * (k * block)) * (slopes[k] + (k * block) * states[k])
-    later_end = jnp.stack([later_of(spot, g, decay) for g in grad_conv])
-    laters = [passed(later_end, "z", -k) for k in range(1, depth)]
-    later = laters[0]
-    for k in range(1, depth - 1):
-        later = later + jnp.exp(-decay * (k * block)) * laters[k]
-    backs = [
-        backward_of(spot, product[k], grad_conv[k], decay, residue, start[k], slope[k], later[k])
-        for k in range(len(product))
-    ]
-    grad_product = [b[0].astype(wide) for b in backs]
-    grad_poles = jnp.concatenate(
-        [sum(b[1] for b in backs[1:]) + backs[0][1], sum(b[2] for b in backs[1:]) + backs[0][2]],
-        axis=0,
-    )
-    grad_short = [
-        jnp.concatenate([q, p * v, p * k], axis=-1)
-        for q, p, v, k in zip(grad_query, grad_product, values, keys)
-    ]
-    heads = jnp.stack([jnp.roll(g[:, :, :, :2].astype(low), -1, axis=1) for g in grad_short])
-    from_next = passed(heads, "z", -1)
-    grad_mixed, grad_taps = [], []
-    for g, e, head, ahead in zip(grad_short, extended, heads, from_next):
-        whole = jnp.concatenate([g, jnp.where(closing, ahead, head).astype(wide)], axis=3)
-        grad_mixed.append(
-            (
-                taps[0] * whole[:, :, :, :-2] + taps[1] * whole[:, :, :, 1:-1] + taps[2] * whole[:, :, :, 2:]
-            )
-            .astype(low)
-            .reshape(-1, 3 * channels)
+
+    low_taps = [taps[:, g * channels : (g + 1) * channels] for g in range(3)]
+
+    def short_back(grad_short, weights):
+        head = jnp.roll(grad_short[:, :, :, :2].astype(low), -1, axis=1)
+        ahead = passed(head, "z", -1)
+        whole = jnp.concatenate([grad_short, jnp.where(closing, ahead, head).astype(wide)], axis=3)
+        result = (
+            weights[0] * whole[:, :, :, :-2]
+            + weights[1] * whole[:, :, :, 1:-1]
+            + weights[2] * whole[:, :, :, 2:]
         )
-        grad_taps.append(
-            jnp.stack(
-                [
-                    jnp.sum(g * e[:, :, :, 2:], axis=(0, 1, 2, 3)),
-                    jnp.sum(g * e[:, :, :, 1:-1], axis=(0, 1, 2, 3)),
-                    jnp.sum(g * e[:, :, :, :-2], axis=(0, 1, 2, 3)),
-                ]
-            )
-        )
-    grad_taps = sum(grad_taps[1:]) + grad_taps[0]
-    grad_in_weight = column_owner(dot_w(joined(normed_all), joined(grad_mixed)), 3)
-    grad_normed = scatter_tokens(
-        dot_t(grad_mixed[0], w_in), [dot_t(g, w_in, low) for g in grad_mixed[1:]], batch
-    )
+        return result.astype(low).reshape(-1, grad_short.shape[-1])
+
+    weigh_active, weigh_feed = after((active, grad_feed_all), grad_gated)
+    down_mine = scatter_tile(dot_w(weigh_active, weigh_feed))
+    grad_mixed_query = short_back(grad_query, low_taps[0])
+    query_mine = scatter_tile(dot_w(normed_all, grad_mixed_query))
+
+    grad_product, grad_residue, grad_decay = backward_of(
+        spot, product, grad_conv, decay, residue, start, slope, later
+    )
+    grad_product = grad_product.astype(wide)
+    grad_pair = jnp.concatenate([grad_product * values, grad_product * keys], axis=-1)
+    grad_mixed_pair = short_back(grad_pair, jnp.concatenate(low_taps[1:], axis=1))
+    pair_mine = scatter_tile(dot_w(normed_all, grad_mixed_pair))
+    grad_mixed = jnp.concatenate([grad_mixed_query, grad_mixed_pair], axis=1)
+    grad_normed = scatter_tokens(dot_t(grad_mixed, w_in, low), batch)
     grad_hidden, grad_norm_gain = norm_back(hidden, scale_one, norm_gain, grad_normed)
     grad_tokens = (grad_hidden + grad_middle).astype(low)
 
-    gains = jnp.stack([grad_norm_gain, grad_feed_gain])
-    for axis in ("x", "y", "c", "z"):
-        gains = sum_axis(gains, axis)
-    small = jnp.concatenate(
-        [grad_poles]
-        + [grad_taps[:, g * channels : (g + 1) * channels] for g in range(3)],
-        axis=0,
-    )
-    small = all_channels(sum_axis(small, "z"))
+    feed_active = after(active, grad_mixed_pair)
+    feed = scatter_tokens(dot(feed_active, w_down, low), batch)
+    output = (mask * (middle + feed)).astype(low)
+    up_mine = after(up_mine, grad_conv)
+    gate_mine = after(gate_mine, grad_product)
+    down_mine = after(down_mine, grad_mixed_pair)
+    gated_late, mix_late = after((gated_own, mix_parts), grad_gated)
+    grad_out_weight = out_owner([dot_w(gated_late, m) for m in mix_late])
+    grad_up_weight = column_owner(up_mine, 1)
+    grad_gate_weight = column_owner(gate_mine, 1)
+    grad_down = row_owner(down_mine)
+    grad_in_weight = jnp.concatenate(
+        [column_owner(query_mine, 1), column_owner(pair_mine, 2)], axis=1
+    )
+
+    query_late, pair_late, extended_late = after((grad_query, grad_pair, extended), grad_mixed_pair)
+    grad_taps = []
+    for g, part in enumerate((query_late, pair_late[..., :channels], pair_late[..., channels:])):
+        own = extended_late[..., g * channels : (g + 1) * channels]
+        grad_taps += [
+            jnp.sum(part * own[:, :, :, 2 - j : local + 2 - j], axis=(0, 1, 2, 3)) for j in range(3)
+        ]
+    gains = jnp.stack([grad_norm_gain, grad_feed_gain]).reshape(-1, channels)
+    small = jnp.concatenate([grad_residue, grad_decay, jnp.stack(grad_taps)], axis=0)
+    count = small.shape[0]
+    small = sum_axis(sum_axis(jnp.concatenate([small, gains], axis=0), "c"), "z")
+    small = gather_slots(gather_slots(small, "x"), "y")
+    gains = jnp.sum(small[:, :, count:], axis=(0, 1)).reshape(2, width)
+    small = all_channels(small[:, :, :count])
     poles = decay.shape[0]
-    grad_residue = small[:poles].T
-    grad_decay = small[poles : 2 * poles].T
     grad_conv_taps = jnp.concatenate(
         [small[2 * poles + 3 * g : 2 * poles + 3 * g + 3] for g in range(3)], axis=1
     )
@@ -654,8 +783,8 @@
         gains[0],
         grad_in_weight,
         grad_conv_taps,
-        grad_residue,
-        grad_decay,
+        small[:poles].T,
+        small[poles : 2 * poles].T,
         grad_out_weight,
         gains[1],
         grad_gate_weight,

time: 933 us -> 937 us (level)
  matrix products: 174 us -> 139 us
  waiting for transfers between devices: 370 us -> 341 us
  starting transfers between devices: 113 us -> 138 us
  other arithmetic: 87.3 us -> 109 us
  local copies, waits for them, and re-layouts: 125 us -> 142 us
    ppermute x0 -> x13, waiting for transfers between devices: none -> 73.3 us  [the longest x6 28.6 us: swap_slots(): line.append(lax.ppermute(slots[sy][sx], ('y', 'x'), pairs))]
    all_gather x5 -> x4, waiting for transfers between devices: 45.7 us -> 0.01 us  [gather_tile(): return lax.all_gather(block, ('z', 'c'), axis=0, tiled=True)]
    reduce_scatter x5, waiting for transfers between devices: 31.8 us -> 0.01 us  [scatter_tile(): return lax.psum_scatter(term, ('z', 'c'), scatter_dimension=0, tiled=True)]
    ppermute x0 -> x13, starting transfers between devices: none -> 26.7 us  [the longest x4 15.5 us: column_owner(): send = lax.ppermute(send, ('c', 'x'), pairs)]
    unnamed x287 -> x264, local copies, waits for them, and re-layouts: 46.7 us -> 66.5 us
    ppermute x68 -> x58, waiting for transfers between devices: 261 us -> 242 us  [turned(): lax.ppermute(value, axis, [(i, (i + by) % length) for i in range(length)])]
    dot_general x10 -> x6, matrix products: 67 us -> 48.4 us  [dot(): return jnp.dot(a, b, preferred_element_type=wide).astype(kind)]
    dot_general x10 -> x6, matrix products: 59 us -> 45.9 us  [dot_t(): lax.dot_general(a, b, (((1,), (1,)), ((), ())), preferred_element_type=wide)]
  transfers between devices with their start and end apart: 89 -> 92, of which waited for: 42 -> 42; matrix products, arithmetic and copies ran while one was open for 31% -> 32% of each run, Pallas kernels for 2% -> 4%
where the time goes in v2:
time: 937 us; the launch traced here: 928 us
  waiting for transfers between devices  341 us (36%)
  local copies, waits for them, and re-layouts  142 us (15%)
  matrix products  139 us (15%)
  starting transfers between devices  138 us (15%)
  other arithmetic  109 us (12%)
  Pallas kernels  41.2 us (4%)
  between operations  16.8 us (2%)
    ppermute x58, waiting for transfers between devices, turned(): lax.ppermute(value, axis, [(i, (i + by) % length) for i in range(length)])  242 us
    ppermute x58, starting transfers between devices, turned(): lax.ppermute(value, axis, [(i, (i + by) % length) for i in range(length)])  77.3 us
    unnamed x264, local copies, waits for them, and re-layouts  66.5 us
    dot_general x6, matrix products, dot(): return jnp.dot(a, b, preferred_element_type=wide).astype(kind)  48.4 us
    dot_general x6, matrix products, dot_t(): lax.dot_general(a, b, (((1,), (1,)), ((), ())), preferred_element_type=wide)  45.9 us
    dot_general x7, matrix products, dot_w(): lax.dot_general(a, b, (((0,), (0,)), ((), ())), preferred_element_type=wide)  44.8 us
    ppermute x12, starting transfers between devices, passed(): return lax.ppermute(value, axis, pairs)  33.9 us
    pallas_call x4, Pallas kernels, conv_call(): pl.pallas_call(kernel, out_shape=results, grid_spec=pltpu.PrefetchScalarG...  33.2 us
  transfers between devices with their start and end apart: 92, of which 42 were waited for; matrix products, arithmetic and copies ran while one was open for 32% of the time, Pallas kernels for 4%

profile of v2, /device:TPU:9, one launch (start us, length us, event | category | flops | bytes accessed | tf_op | source)
XLA Modules:
  0.0 927.7 jit_solution(17405970042188534419)
XLA Ops:
  7.8 8.0 shard_map.220
  17.3 11.7 %collective-permute-done.4 = bf16[256,1536]{1,0:T(8,128)(2,1)} collective-permute-done((bf16[256,1536]{1,0:T(8,128)(2,1)}, bf16[256,1536]{1,0:T(8,128)(2,1)}, u32[]{:S(2)}, u32[]{:S(2)}) %collective-permute-start.4) | collective-permute-done | bytes 786464 | tf_op jit(solution)/shard_map/ppermute | solution.py:147
  47.3 9.1 collective-permute-done.24
  83.1 11.5 %collective-permute-done.13 = bf16[128,1024]{1,0:T(8,128)(2,1)} collective-permute-done((bf16[128,1024]{1,0:T(8,128)(2,1)}, bf16[128,1024]{1,0:T(8,128)(2,1)}, u32[]{:S(2)}, u32[]{:S(2)}) %collective-permute-start.13) | collective-permute-done | bytes 262176 | tf_op jit(solution)/shard_map/ppermute | solution.py:22
  94.6 17.6 %collective-permute-done.14 = bf16[128,1024]{1,0:T(8,128)(2,1)} collective-permute-done((bf16[128,1024]{1,0:T(8,128)(2,1)}, bf16[128,1024]{1,0:T(8,128)(2,1)}, u32[]{:S(2)}, u32[]{:S(2)}) %collective-permute-start.14) | collective-permute-done | bytes 262176 | tf_op jit(solution)/shard_map/ppermute | solution.py:22
  130.2 21.1 %collective-permute-done.17 = bf16[1,256,1024]{2,1,0:T(8,128)(2,1)} collective-permute-done((bf16[1,256,1024]{2,1,0:T(8,128)(2,1)}, bf16[1,256,1024]{2,1,0:T(8,128)(2,1)}, u32[]{:S(2)}, u32[]{:S(2)}) %collective-permute-start.17) | collective-permute-done | bytes 524320 | tf_op jit(solution)/shard_map/ppermute | solution.py:22
  160.6 13.2 %collective-permute-done.16 = bf16[2,1,256,1024]{3,2,0,1:T(8,128)(2,1)S(1)} collective-permute-done((bf16[2,1,256,1024]{3,2,0,1:T(8,128)(2,1)S(1)}, bf16[2,1,256,1024]{3,2,0,1:T(8,128)(2,1)S(1)}, u32[]{:S(2)}, u32[]{:S(2)}) %collective-permute-start.16) | collective-permute-done | bytes 1048608 | tf_op jit(solution)/shard_map/ppermute | solution.py:22
  175.5 10.1 %fusion.13 = bf16[1024,1536]{1,0:T(8,128)(2,1)S(1)} fusion(bf16[1024,2048]{1,0:T(8,128)(2,1)} %bitcast.479, bf16[1,2048,1536]{2,1,0:T(8,128)(2,1)} %all-gather.11.cloned.1.call-done), kind=kOutput, calls=%fused_computation.39 | convolution fusion | flops 6444023808 | bytes 13631488 | tf_op jit(solution)/shard_map/dot_general | solution.py:565
  216.5 13.5 %collective-permute-done.7 = f32[4,16,512]{2,1,0:T(8,128)S(1)} collective-permute-done((f32[4,16,512]{2,1,0:T(8,128)S(1)}, f32[4,16,512]{2,1,0:T(8,128)S(1)}, u32[]{:S(2)}, u32[]{:S(2)}) %collective-permute-start.7) | collective-permute-done | bytes 131104 | tf_op jit(solution)/shard_map/ppermute | solution.py:28
  230.0 7.5 shard_map.222
  245.9 26.7 %collective-permute-done.10 = bf16[256,512]{1,0:T(8,128)(2,1)S(1)} collective-permute-done((bf16[256,512]{1,0:T(8,128)(2,1)S(1)}, bf16[256,512]{1,0:T(8,128)(2,1)S(1)}, u32[]{:S(2)}, u32[]{:S(2)}) %collective-permute-start.10) | collective-permute-done | bytes 262176 | tf_op jit(solution)/shard_map/ppermute | solution.py:67
  290.7 19.7 %collective-permute-done.29 = bf16[2,1,128,2048]{3,2,1,0:T(8,128)(2,1)S(1)} collective-permute-done((bf16[2,1,128,2048]{3,2,1,0:T(8,128)(2,1)S(1)}, bf16[2,1,128,2048]{3,2,1,0:T(8,128)(2,1)S(1)}, u32[]{:S(2)}, u32[]{:S(2)}) %collective-permute-start.29) | collective-permute-done | bytes 1048608 | tf_op jit(solution)/shard_map/ppermute | solution.py:22
  313.5 19.2 %collective-permute-done.23 = bf16[2,1,128,2048]{3,2,1,0:T(8,128)(2,1)S(1)} collective-permute-done((bf16[2,1,128,2048]{3,2,1,0:T(8,128)(2,1)S(1)}, bf16[2,1,128,2048]{3,2,1,0:T(8,128)(2,1)S(1)}, u32[]{:S(2)}, u32[]{:S(2)}) %collective-permute-start.23) | collective-permute-done | bytes 1048608 | tf_op jit(solution)/shard_map/ppermute | solution.py:22
  335.6 11.7 %fusion.8 = f32[1024,1408]{1,0:T(8,128)} fusion(bf16[1024,2048]{1,0:T(8,128)(2,1)} %bitcast.482, bf16[1,2048,1408]{2,1,0:T(8,128)(2,1)} %all-gather.13.cloned.1.call-done), kind=kOutput, calls=%fused_computation.16 | convolution fusion | flops 5905580032 | bytes 15728640 | tf_op jit(solution)/shard_map/dot_general | solution.py:565
  347.3 13.1 %multiply_convert_fusion.2 = (bf16[1024,1408]{1,0:T(8,128)(2,1)S(1)}, f32[1024,1408]{1,0:T(8,128)}) fusion(f32[1024,1408]{1,0:T(8,128)} %fusion.8, bf16[1024,2048]{1,0:T(8,128)(2,1)} %bitcast.477, bf16[1408,2048]{1,0:T(8,128)(2,1)} %all-gather.9.cloned.1.call-done), kind=kOutput, calls=%fused_computation.21 | convolution fusion | flops 5914230784 | bytes 24379392 | tf_op jit(solution)/shard_map/dot_general | solution.py:569
  362.0 8.6 convolution_convert_fusion.2
  370.6 15.0 %multiply_convert_fusion = (bf16[1024,1408]{1,0:T(8,128)(2,1)S(1)}, bf16[1024,1408]{1,0:T(8,128)(2,1)}) fusion(f32[1024,1408]{1,0:T(8,128)} %fusion.8, f32[1024,1408]{1,0:T(8,128)} %get-tuple-element.310, bf16[1024,2048]{1,0:T(8,128)(2,1)} %bitcast.483, bf16[2048,1408]{1,0:T(8,128)(2,1)} %all-gather.7.cloned.1.call-done), kind=kOutput, calls=%fused_computation.19 | convolution fusion | flops 5924323328 | bytes 27262976 | tf_op jit(solution)/shard_map/dot_general | solution.py:565
  387.2 8.9 fusion.6
  396.1 8.6 add_convert_fusion.1
  407.3 15.7 %collective-permute-done.30 = bf16[2,1,128,2048]{3,2,1,0:T(8,128)(2,1)S(1)} collective-permute-done((bf16[2,1,128,2048]{3,2,1,0:T(8,128)(2,1)S(1)}, bf16[2,1,128,2048]{3,2,1,0:T(8,128)(2,1)S(1)}, u32[]{:S(2)}, u32[]{:S(2)}) %collective-permute-start.30) | collective-permute-done | bytes 1048608 | tf_op jit(solution)/shard_map/ppermute | solution.py:22
  428.7 9.0 collective-permute-done.31
  507.1 17.2 %shard_map.224 = (bf16[4,2,1,128,512]{4,3,2,1,0:T(8,128)(2,1)S(1)}, f32[16,512]{1,0:T(8,128)S(1)}, f32[16,512]{1,0:T(8,128)S(1)}) custom-call(s32[1]{0:T(128)} %bitcast.21.place_ref, bf16[4,2,1,128,512]{4,3,2,1,0:T(8,128)(2,1)S(1)} %multiply_convert_fusion.5.signal_ref, bf16[4,2,1,128,512]{4,3,2,1,0:T(8,128)(2,1)S(1)} %get-tuple-element.153.signal_ref.grad_ref, ...), custom_call_target="tpu_custom_call" | custom-call | flops 100663296 | bytes 4653056 | tf_op jit(solution)/shard_map/pallas_call | solution.py:488
  527.8 8.7 collective-permute-start.43
  549.2 11.2 %convolution_convert_fusion.1 = bf16[2048,1408]{1,0:T(8,128)(2,1)} fusion(bf16[1024,2048]{1,0:T(8,128)(2,1)} %bitcast.484, bf16[1024,1408]{1,0:T(8,128)(2,1)} %copy-done.90), kind=kOutput, calls=%fused_computation.3 | convolution fusion | flops 5908463616 | bytes 12845056 | tf_op jit(solution)/shard_map/dot_general | solution.py:573
  565.1 11.0 %collective-permute-start.65 = (bf16[2048,1024]{1,0:T(8,128)(2,1)}, bf16[2048,1024]{1,0:T(8,128)(2,1)}, u32[]{:S(2)}, u32[]{:S(2)}) collective-permute-start(bf16[2048,1024]{1,0:T(8,128)(2,1)} %convolution_convert_fusion.3), channel_id=1, source_target_pairs={{0,8},{8,0},{1,9},{9,1},{2,10},{10,2},{3,11},{11,3},{4,12},{12,4},... | collective-permute-start | bytes 12582920 | tf_op jit(solution)/shard_map/ppermute | solution.py:22
  576.2 8.1 convolution_convert_fusion
  585.5 9.6 %fusion.16 = bf16[1024,2048]{1,0:T(8,128)(2,1)S(1)} fusion(bf16[1,2048,1536]{2,1,0:T(8,128)(2,1)} %all-gather.11.cloned.1.call-done, bf16[1024,1024]{1,0:T(8,128)(2,1)} %bitcast.502, bf16[1024,512]{1,0:T(8,128)(2,1)S(1)} %bitcast.511), kind=kOutput, calls=%fused_computation.40 | convolution fusion | flops 6450839552 | bytes 13631488 | tf_op jit(solution)/shard_map/dot_general | solution.py:569
  598.8 6.8 convolution_convert_fusion.4
  623.4 18.6 %collective-permute-done.44 = bf16[2,1,128,2048]{3,2,1,0:T(8,128)(2,1)} collective-permute-done((bf16[2,1,128,2048]{3,2,1,0:T(8,128)(2,1)S(1)}, bf16[2,1,128,2048]{3,2,1,0:T(8,128)(2,1)}, u32[]{:S(2)}, u32[]{:S(2)}) %collective-permute-start.44) | collective-permute-done | bytes 1048608 | tf_op jit(solution)/shard_map/ppermute | solution.py:22
  708.7 17.2 %collective-permute-done.59 = bf16[256,512]{1,0:T(8,128)(2,1)S(1)} collective-permute-done((bf16[256,512]{1,0:T(8,128)(2,1)}, bf16[256,512]{1,0:T(8,128)(2,1)S(1)}, u32[]{:S(2)}, u32[]{:S(2)}) %collective-permute-start.59) | collective-permute-done | bytes 262176 | tf_op jit(solution)/shard_map/ppermute | solution.py:230
  770.3 25.6 %collective-permute-done.71 = bf16[128,1024]{1,0:T(8,128)(2,1)S(1)} collective-permute-done((bf16[128,1024]{1,0:T(8,128)(2,1)S(1)}, bf16[128,1024]{1,0:T(8,128)(2,1)S(1)}, u32[]{:S(2)}, u32[]{:S(2)}) %collective-permute-start.71) | collective-permute-done | bytes 262176 | tf_op jit(solution)/shard_map/ppermute | solution.py:22
  874.8 7.5 collective-permute-done.81
  (661 shorter events, 489.8 us)
Async XLA Ops:
  7.2 168.3 %all-gather.11.cloned.1.call-start = ((), (), s32[]{:S(2)}) async-start(), calls=%async_computation.12 | async-start | bytes 7077888 | tf_op jit(solution)/shard_map/all_gather | solution.py:206
  31.3 304.2 %all-gather.13.cloned.1.call-start = ((), (), s32[]{:S(2)}) async-start(), calls=%async_computation.13 | async-start | bytes 6488064 | tf_op jit(solution)/shard_map/all_gather | solution.py:206
  58.7 288.6 %all-gather.9.cloned.1.call-start = ((), (), s32[]{:S(2)}) async-start(), calls=%async_computation.6 | async-start | bytes 6488064 | tf_op jit(solution)/shard_map/all_gather | solution.py:206
  59.7 310.9 %all-gather.7.cloned.1.call-start = ((), (), s32[]{:S(2)}) async-start(), calls=%async_computation.5 | async-start | bytes 6488064 | tf_op jit(solution)/shard_map/all_gather | solution.py:206
  61.7 33.0 %collective-permute-start.13 = (bf16[128,1024]{1,0:T(8,128)(2,1)}, bf16[128,1024]{1,0:T(8,128)(2,1)}, u32[]{:S(2)}, u32[]{:S(2)}) collective-permute-start(bf16[128,1024]{1,0:T(8,128)(2,1)} %dynamic_slice.306), channel_id=1, source_target_pairs={{0,4},{2,6},{4,0},{6,2},{1,5},{3,7},{5,1},{7,3},{8,12},{10,14},{12... | collective-permute-start | bytes 786440 | tf_op jit(solution)/shard_map/ppermute | solution.py:22
  64.1 48.1 %collective-permute-start.14 = (bf16[128,1024]{1,0:T(8,128)(2,1)}, bf16[128,1024]{1,0:T(8,128)(2,1)}, u32[]{:S(2)}, u32[]{:S(2)}) collective-permute-start(bf16[128,1024]{1,0:T(8,128)(2,1)} %dynamic_slice.306), channel_id=1, source_target_pairs={{0,2},{2,4},{4,6},{6,0},{1,3},{3,5},{5,7},{7,1},{8,10},{10,12},{12... | collective-permute-start | bytes 786440 | tf_op jit(solution)/shard_map/ppermute | solution.py:22
  68.5 55.4 %collective-permute-start.25 = (bf16[256,1408]{1,0:T(8,128)(2,1)}, bf16[256,1408]{1,0:T(8,128)(2,1)}, u32[]{:S(2)}, u32[]{:S(2)}) collective-permute-start(bf16[256,1408]{1,0:T(8,128)(2,1)} %concatenate.137), channel_id=1, source_target_pairs={{0,1},{9,8},{2,3},{11,10},{4,5},{13,12},{6,7},{15,14},{16,17},{25,... | collective-permute-start | bytes 2162696 | tf_op jit(solution)/shard_map/ppermute | solution.py:147
  70.0 44.4 %collective-permute-start = (bf16[1,128,2048]{2,1,0:T(8,128)(2,1)S(1)}, bf16[1,128,2048]{2,1,0:T(8,128)(2,1)S(1)}, u32[]{:S(2)}, u32[]{:S(2)}) collective-permute-start(bf16[1,128,2048]{2,1,0:T(8,128)(2,1)S(1)} %get-tuple-element.218), channel_id=1, source_target_pairs={{0,1},{1,0},{2,3},{3,2},{4,5},{5,4},{6,7},{7,6},{8,9},{9,8},{10,11... | collective-permute-start | bytes 1572872 | tf_op jit(solution)/shard_map/ppermute | solution.py:22
  81.9 37.0 %collective-permute-start.2 = (bf16[1,128,2048]{2,1,0:T(8,128)(2,1)S(1)}, bf16[1,128,2048]{2,1,0:T(8,128)(2,1)S(1)}, u32[]{:S(2)}, u32[]{:S(2)}) collective-permute-start(bf16[1,128,2048]{2,1,0:T(8,128)(2,1)S(1)} %get-tuple-element.217), channel_id=1, source_target_pairs={{0,16},{16,0},{1,17},{17,1},{2,18},{18,2},{3,19},{19,3},{4,20},{20... | collective-permute-start | bytes 1572872 | tf_op jit(solution)/shard_map/ppermute | solution.py:22
  117.4 37.7 %collective-permute-start.1 = (bf16[2,1,128,2048]{3,2,1,0:T(8,128)(2,1)}, bf16[2,1,128,2048]{3,2,1,0:T(8,128)(2,1)}, u32[]{:S(2)}, u32[]{:S(2)}) collective-permute-start(bf16[2,1,128,2048]{3,2,1,0:T(8,128)(2,1)} %get-tuple-element.214), channel_id=1, source_target_pairs={{0,16},{16,0},{1,17},{17,1},{2,18},{18,2},{3,19},{19,3},{4,20},{20... | collective-permute-start | bytes 3145736 | tf_op jit(solution)/shard_map/ppermute | solution.py:22
  120.0 36.6 %collective-permute-start.3 = (bf16[2,1,128,2048]{3,2,0,1:T(8,128)(2,1)}, bf16[2,1,128,2048]{3,2,0,1:T(8,128)(2,1)}, u32[]{:S(2)}, u32[]{:S(2)}) collective-permute-start(bf16[2,1,128,2048]{3,2,0,1:T(8,128)(2,1)} %get-tuple-element.220), channel_id=1, source_target_pairs={{0,1},{1,0},{2,3},{3,2},{4,5},{5,4},{6,7},{7,6},{8,9},{9,8},{10,11... | collective-permute-start | bytes 3145736 | tf_op jit(solution)/shard_map/ppermute | solution.py:22
  126.2 573.2 %reduce-scatter.6.cloned.1.call-start = ((), (), s32[]{:S(2)}) async-start(), calls=%async_computation.7 | async-start | bytes 2359296 | tf_op jit(solution)/shard_map/reduce_scatter | solution.py:210
  128.3 45.5 %collective-permute-start.16 = (bf16[2,1,256,1024]{3,2,0,1:T(8,128)(2,1)S(1)}, bf16[2,1,256,1024]{3,2,0,1:T(8,128)(2,1)S(1)}, u32[]{:S(2)}, u32[]{:S(2)}) collective-permute-start(bf16[2,1,256,1024]{3,2,0,1:T(8,128)(2,1)S(1)} %get-tuple-element.202), channel_id=1, source_target_pairs={{0,16},{16,0},{1,17},{17,1},{2,18},{18,2},{3,19},{19,3},{4,20},{20... | collective-permute-start | bytes 3145736 | tf_op jit(solution)/shard_map/ppermute | solution.py:22
  190.3 83.7 %collective-permute-start.19 = (bf16[2048,1024]{1,0:T(8,128)(2,1)S(1)}, bf16[2048,1024]{1,0:T(8,128)(2,1)}, u32[]{:S(2)}, u32[]{:S(2)}) collective-permute-start(bf16[2048,1024]{1,0:T(8,128)(2,1)S(1)} %bitcast.486), channel_id=1, source_target_pairs={{0,8},{8,0},{1,9},{9,1},{2,10},{10,2},{3,11},{11,3},{4,12},{12,4},... | collective-permute-start | bytes 12582920 | tf_op jit(solution)/shard_map/ppermute | solution.py:22
  214.8 67.2 %collective-permute-start.28 = (bf16[1,128,2048]{2,1,0:T(8,128)(2,1)}, bf16[1,128,2048]{2,1,0:T(8,128)(2,1)}, u32[]{:S(2)}, u32[]{:S(2)}) collective-permute-start(bf16[1,128,2048]{2,1,0:T(8,128)(2,1)} %get-tuple-element.189), channel_id=1, source_target_pairs={{0,16},{16,0},{1,17},{17,1},{2,18},{18,2},{3,19},{19,3},{4,20},{20... | collective-permute-start | bytes 1572872 | tf_op jit(solution)/shard_map/ppermute | solution.py:22
  241.6 48.9 %collective-permute-start.27 = (bf16[2,1,128,2048]{3,2,0,1:T(8,128)(2,1)S(1)}, bf16[2,1,128,2048]{3,2,0,1:T(8,128)(2,1)S(1)}, u32[]{:S(2)}, u32[]{:S(2)}) collective-permute-start(bf16[2,1,128,2048]{3,2,0,1:T(8,128)(2,1)S(1)} %get-tuple-element.186), channel_id=1, source_target_pairs={{0,16},{16,0},{1,17},{17,1},{2,18},{18,2},{3,19},{19,3},{4,20},{20... | collective-permute-start | bytes 3145736 | tf_op jit(solution)/shard_map/ppermute | solution.py:22
  290.1 42.7 %collective-permute-start.23 = (bf16[2,1,128,2048]{3,2,1,0:T(8,128)(2,1)S(1)}, bf16[2,1,128,2048]{3,2,1,0:T(8,128)(2,1)S(1)}, u32[]{:S(2)}, u32[]{:S(2)}) collective-permute-start(bf16[2,1,128,2048]{3,2,1,0:T(8,128)(2,1)S(1)} %get-tuple-element.200), channel_id=1, source_target_pairs={{0,1},{1,0},{2,3},{3,2},{4,5},{5,4},{6,7},{7,6},{8,9},{9,8},{10,11... | collective-permute-start | bytes 3145736 | tf_op jit(solution)/shard_map/ppermute | solution.py:22
  485.3 273.3 %reduce-scatter.8.cloned.1.call-start = ((), (), s32[]{:S(2)}) async-start(), calls=%async_computation.8 | async-start | bytes 4718592 | tf_op jit(solution)/shard_map/reduce_scatter | solution.py:210
  548.4 272.1 %reduce-scatter.12.cloned.1.call-start = ((), (), s32[]{:S(2)}) async-start(), calls=%async_computation.10 | async-start | bytes 6488064 | tf_op jit(solution)/shard_map/reduce_scatter | solution.py:210
  549.1 274.3 %reduce-scatter.10.cloned.1.call-start = ((), (), s32[]{:S(2)}) async-start(), calls=%async_computation.9 | async-start | bytes 6488064 | tf_op jit(solution)/shard_map/reduce_scatter | solution.py:210
  560.4 304.5 %reduce-scatter.14.cloned.1.call-start = ((), (), s32[]{:S(2)}) async-start(), calls=%async_computation.11 | async-start | bytes 6488064 | tf_op jit(solution)/shard_map/reduce_scatter | solution.py:210
  565.1 125.4 %collective-permute-start.65 = (bf16[2048,1024]{1,0:T(8,128)(2,1)}, bf16[2048,1024]{1,0:T(8,128)(2,1)}, u32[]{:S(2)}, u32[]{:S(2)}) collective-permute-start(bf16[2048,1024]{1,0:T(8,128)(2,1)} %convolution_convert_fusion.3), channel_id=1, source_target_pairs={{0,8},{8,0},{1,9},{9,1},{2,10},{10,2},{3,11},{11,3},{4,12},{12,4},... | collective-permute-start | bytes 12582920 | tf_op jit(solution)/shard_map/ppermute | solution.py:22
  606.2 35.8 %collective-permute-start.44 = (bf16[2,1,128,2048]{3,2,1,0:T(8,128)(2,1)S(1)}, bf16[2,1,128,2048]{3,2,1,0:T(8,128)(2,1)}, u32[]{:S(2)}, u32[]{:S(2)}) collective-permute-start(bf16[2,1,128,2048]{3,2,1,0:T(8,128)(2,1)S(1)} %slice_bitcast_fusion.10), channel_id=1, source_target_pairs={{0,1},{1,0},{2,3},{3,2},{4,5},{5,4},{6,7},{7,6},{8,9},{9,8},{10,11... | collective-permute-start | bytes 3145736 | tf_op jit(solution)/shard_map/ppermute | solution.py:22
  606.4 38.2 %collective-permute-start.46 = (bf16[2,1,128,2048]{3,2,1,0:T(8,128)(2,1)S(1)}, bf16[2,1,128,2048]{3,2,1,0:T(8,128)(2,1)}, u32[]{:S(2)}, u32[]{:S(2)}) collective-permute-start(bf16[2,1,128,2048]{3,2,1,0:T(8,128)(2,1)S(1)} %bitcast.514), channel_id=1, source_target_pairs={{0,16},{16,0},{1,17},{17,1},{2,18},{18,2},{3,19},{19,3},{4,20},{20... | collective-permute-start | bytes 3145736 | tf_op jit(solution)/shard_map/ppermute | solution.py:22
  620.0 33.3 %collective-permute-start.50 = (bf16[1,128,2048]{2,1,0:T(8,128)(2,1)S(1)}, bf16[1,128,2048]{2,1,0:T(8,128)(2,1)S(1)}, u32[]{:S(2)}, u32[]{:S(2)}) collective-permute-start(bf16[1,128,2048]{2,1,0:T(8,128)(2,1)S(1)} %fusion.72), channel_id=1, source_target_pairs={{0,16},{16,0},{1,17},{17,1},{2,18},{18,2},{3,19},{19,3},{4,20},{20... | collective-permute-start | bytes 1572872 | tf_op jit(solution)/shard_map/ppermute | solution.py:22
  622.7 30.7 %collective-permute-start.52 = (bf16[1,128,2048]{2,1,0:T(8,128)(2,1)S(1)}, bf16[1,128,2048]{2,1,0:T(8,128)(2,1)S(1)}, u32[]{:S(2)}, u32[]{:S(2)}) collective-permute-start(bf16[1,128,2048]{2,1,0:T(8,128)(2,1)S(1)} %fusion.73), channel_id=1, source_target_pairs={{0,1},{1,0},{2,3},{3,2},{4,5},{5,4},{6,7},{7,6},{8,9},{9,8},{10,11... | collective-permute-start | bytes 1572872 | tf_op jit(solution)/shard_map/ppermute | solution.py:22
  697.6 41.2 %collective-permute-start.66 = (bf16[2,1,256,1024]{3,2,1,0:T(8,128)(2,1)}, bf16[2,1,256,1024]{3,2,1,0:T(8,128)(2,1)}, u32[]{:S(2)}, u32[]{:S(2)}) collective-permute-start(bf16[2,1,256,1024]{3,2,1,0:T(8,128)(2,1)} %slice_bitcast_fusion.2), channel_id=1, source_target_pairs={{0,1},{1,0},{2,3},{3,2},{4,5},{5,4},{6,7},{7,6},{8,9},{9,8},{10,11... | collective-permute-start | bytes 3145736 | tf_op jit(solution)/shard_map/ppermute | solution.py:22
  707.5 34.3 %collective-permute-start.68 = (bf16[2,1,256,1024]{3,2,0,1:T(8,128)(2,1)}, bf16[2,1,256,1024]{3,2,0,1:T(8,128)(2,1)}, u32[]{:S(2)}, u32[]{:S(2)}) collective-permute-start(bf16[2,1,256,1024]{3,2,0,1:T(8,128)(2,1)} %bitcast.192), channel_id=1, source_target_pairs={{0,16},{16,0},{1,17},{17,1},{2,18},{18,2},{3,19},{19,3},{4,20},{20... | collective-permute-start | bytes 3145736 | tf_op jit(solution)/shard_map/ppermute | solution.py:22
  756.8 39.1 %collective-permute-start.71 = (bf16[128,1024]{1,0:T(8,128)(2,1)S(1)}, bf16[128,1024]{1,0:T(8,128)(2,1)S(1)}, u32[]{:S(2)}, u32[]{:S(2)}) collective-permute-start(bf16[128,1024]{1,0:T(8,128)(2,1)S(1)} %get-tuple-element.170), channel_id=1, source_target_pairs={{0,4},{2,6},{4,0},{6,2},{1,5},{3,7},{5,1},{7,3},{8,12},{10,14},{12... | collective-permute-start | bytes 786440 | tf_op jit(solution)/shard_map/ppermute | solution.py:22
  757.8 41.4 %collective-permute-start.72 = (bf16[128,1024]{1,0:T(8,128)(2,1)S(1)}, bf16[128,1024]{1,0:T(8,128)(2,1)}, u32[]{:S(2)}, u32[]{:S(2)}) collective-permute-start(bf16[128,1024]{1,0:T(8,128)(2,1)S(1)} %get-tuple-element.169), channel_id=1, source_target_pairs={{0,6},{2,0},{4,2},{6,4},{1,7},{3,1},{5,3},{7,5},{8,14},{10,8},{12,... | collective-permute-start | bytes 786440 | tf_op jit(solution)/shard_map/ppermute | solution.py:22
  758.6 42.2 %collective-permute-start.62 = (bf16[256,1024]{1,0:T(8,128)(2,1)}, bf16[256,1024]{1,0:T(8,128)(2,1)S(1)}, u32[]{:S(2)}, u32[]{:S(2)}) collective-permute-start(bf16[256,1024]{1,0:T(8,128)(2,1)} %reduce-scatter.8.cloned.1.call-done), channel_id=1, source_target_pairs={{8,1},{1,8},{10,3},{3,10},{12,5},{5,12},{14,7},{7,14},{24,17},{17,... | collective-permute-start | bytes 1572872 | tf_op jit(solution)/shard_map/ppermute | solution.py:230
  841.6 30.9 %collective-permute-start.76 = (bf16[1,256,1408]{2,1,0:T(8,128)(2,1)S(1)}, bf16[1,256,1408]{2,1,0:T(8,128)(2,1)}, u32[]{:S(2)}, u32[]{:S(2)}) collective-permute-start(bf16[1,256,1408]{2,1,0:T(8,128)(2,1)S(1)} %fusion.61), channel_id=1, source_target_pairs={{0,16},{16,0},{1,17},{17,1},{2,18},{18,2},{3,19},{19,3},{4,20},{20... | collective-permute-start | bytes 2162696 | tf_op jit(solution)/shard_map/ppermute | solution.py:22
  (156 other events, 2047.0 us)
Sparse Core Ops, SparseCore 0:
  31.4 84.4 all-gather.10
  118.1 62.2 all-gather.12
  182.6 70.0 all-gather.8
  254.1 62.1 all-gather.6
  485.4 48.0 reduce-scatter.5
  548.5 56.8 reduce-scatter.7
  608.3 63.0 reduce-scatter.11
  674.2 65.6 reduce-scatter.9
  742.8 85.9 reduce-scatter.13

commit v3 on v2

--- a/solution.py
+++ b/solution.py
@@ -1,3 +1,5 @@
+import functools
+
 import jax
 import jax.numpy as jnp
 from jax import lax
@@ -89,10 +91,23 @@
     return jnp.concatenate([first, second], axis=0)
 
 
-def pick_kernel(start_ref, *refs):
-    count = len(refs) // 2
-    for source, target in zip(refs[:count], refs[count:]):
-        target[...] = source[...]
+def pick_kernel(count, part, stride, start_ref, source, *refs):
+    targets, sems = refs[:-1], refs[-1]
+    copies = []
+    for d, target in enumerate(targets):
+        for k in range(count):
+            at = pl.multiple_of((k * stride + start_ref[d]) * part, part)
+            copies.append(
+                pltpu.make_async_copy(
+                    source.at[:, pl.ds(at, part)],
+                    target.at[:, k * part : (k + 1) * part],
+                    sems.at[d * count + k],
+                )
+            )
+    for copy in copies:
+        copy.start()
+    for copy in copies:
+        copy.wait()
 
 
 def column_pieces(weight, groups):
@@ -104,25 +119,19 @@
         (lax.axis_index("x") + d) % spread * ycount + lax.axis_index("y") for d in range(spread)
     ]
     if part % 128 == 0:
-
-        def source(d):
-            return pl.BlockSpec(
-                (rows, part), lambda i, start, d=d: (0, i * spread * ycount + start[d])
-            )
-
         return pl.pallas_call(
-            pick_kernel,
+            functools.partial(pick_kernel, count, part, spread * ycount),
             out_shape=[jax.ShapeDtypeStruct((rows, count * part), weight.dtype)] * spread,
             grid_spec=pltpu.PrefetchScalarGridSpec(
                 num_scalar_prefetch=1,
-                grid=(count,),
-                in_specs=[source(d) for d in range(spread)],
-                out_specs=[pl.BlockSpec((rows, part), lambda i, start: (0, i))] * spread,
+                in_specs=[pl.BlockSpec(memory_space=pl.ANY)],
+                out_specs=[pl.BlockSpec(memory_space=pl.ANY)] * spread,
+                scratch_shapes=[pltpu.SemaphoreType.DMA((count * spread,))],
             ),
             cost_estimate=pl.CostEstimate(
                 flops=0, transcendentals=0, bytes_accessed=4 * rows * count * part * spread
             ),
-        )(jnp.stack(starts).astype(jnp.int32), *[weight] * spread)
+        )(jnp.stack(starts).astype(jnp.int32), weight)
     return [
         jnp.concatenate(
             [
@@ -245,8 +254,8 @@
             ranks.append(lax.dynamic_index_in_dim(flat, slot * share + i % share, 0, False))
     pieces = []
     for at in range(groups * depth):
-        pieces += [r[:, at * part : (at + 1) * part] for r in ranks]
-    return jnp.concatenate(pieces, axis=1).astype(wide)
+        pieces += [r[:, at * part : (at + 1) * part].astype(wide) for r in ranks]
+    return jnp.concatenate(pieces, axis=1)
 
 
 def in_order(slots, axis):
@@ -596,25 +605,24 @@
     block = spread * local
 
     in_pieces = column_pieces(in_weight, 3)
-    out_weight, tokens = after((out_weight, tokens), in_pieces)
-    in_block = column_block(in_pieces)
-    hidden = tokens.astype(wide)
+    hidden = after(tokens, in_pieces).astype(wide)
     scale_one = rms_scale(hidden)
     normed = (hidden * scale_one * norm_gain).astype(low)
+    in_block = column_block(in_pieces)
+    w_in = gather_tile(in_block)
     normed_all = gather_tokens(normed)
-    gate_weight, down_weight, up_weight = after(
-        (gate_weight, down_weight, up_weight), normed, in_block
+    gate_weight, out_weight, up_weight, down_weight = after(
+        (gate_weight, out_weight, up_weight, down_weight), normed_all, in_block
     )
     gate_block = column_block(column_pieces(gate_weight, 1))
-    up_block = column_block(column_pieces(up_weight, 1))
+    w_gate = gather_tile(gate_block)
+    w_out = gather_out(after(out_weight, gate_block))
+    up_pieces = column_pieces(up_weight, 1)
     down_piece = after(row_block(down_weight), gate_block)
-    up_block = after(up_block, down_piece)
-    w_in = gather_tile(in_block)
-    w_gate = gather_tile(gate_block)
     w_down = gather_tile(down_piece)
+    up_block = after(column_block(after(up_pieces, w_out)), down_piece)
     w_up = gather_tile(up_block)
-    w_out = gather_out(out_weight)
-    cotangent = after(cotangent, normed_all, gate_block, up_block)
+    cotangent = after(cotangent, w_out)
     grad_out = cotangent.astype(wide) * mask
     grad_feed_all = gather_tokens(grad_out.astype(low))
 
@@ -682,7 +690,11 @@
     partial_two = (dot_t(grad_gate, w_gate) + dot_t(grad_upper, w_up)).astype(low)
     grad_normed_two = scatter_tokens(partial_two, batch)
     weigh_two, weigh_gate = after((normed_two_all, grad_gate), partial_two)
-    gate_mine = scatter_tile(dot_w(weigh_two, weigh_gate))
+    gate_term = dot_w(weigh_two, weigh_gate)
+    gate_mine = scatter_tile(gate_term)
+    weigh_active, weigh_feed = after((active, grad_feed_all), gate_term)
+    down_term = dot_w(weigh_active, weigh_feed)
+    down_mine = scatter_tile(down_term)
 
     grad_middle, grad_feed_gain = norm_back(middle, scale_two, feed_gain, grad_normed_two)
     grad_middle = grad_middle + grad_out
@@ -690,7 +702,7 @@
 
     mix_parts = core_halves(grad_mix)
     grad_gated_own = sum(dot_t(m, w) for m, w in zip(mix_parts, w_out)).astype(low)
-    grad_slots = grad_gated_own.reshape(-1, 2, ycount, spread, half)
+    grad_slots = after(grad_gated_own, up_mine, gate_term).reshape(-1, 2, ycount, spread, half)
     got = swap_slots(
         [
             [grad_slots[:, :, k, i].reshape(-1, channels) for i in range(spread)]
@@ -700,6 +712,7 @@
     grad_gated = jnp.stack([jnp.stack(line) for line in got])
     grad_gated = grad_gated.reshape(ycount, spread, 2, batch // 2, local, channels)
     grad_gated = jnp.moveaxis(grad_gated, 2, 0).reshape(grid + (channels,)).astype(wide)
+    grad_gated = after(grad_gated, down_term)
     grad_query = grad_gated * convolved.astype(wide)
     grad_conv = (grad_gated * query).astype(low)
 
@@ -727,10 +740,8 @@
         )
         return result.astype(low).reshape(-1, grad_short.shape[-1])
 
-    weigh_active, weigh_feed = after((active, grad_feed_all), grad_gated)
-    down_mine = scatter_tile(dot_w(weigh_active, weigh_feed))
     grad_mixed_query = short_back(grad_query, low_taps[0])
-    query_mine = scatter_tile(dot_w(normed_all, grad_mixed_query))
+    query_mine = scatter_tile(after(dot_w(normed_all, grad_mixed_query), down_term))
 
     grad_product, grad_residue, grad_decay = backward_of(
         spot, product, grad_conv, decay, residue, start, slope, later
@@ -738,18 +749,19 @@
     grad_product = grad_product.astype(wide)
     grad_pair = jnp.concatenate([grad_product * values, grad_product * keys], axis=-1)
     grad_mixed_pair = short_back(grad_pair, jnp.concatenate(low_taps[1:], axis=1))
+    grad_mixed_pair = after(grad_mixed_pair, gate_mine)
     pair_mine = scatter_tile(dot_w(normed_all, grad_mixed_pair))
     grad_mixed = jnp.concatenate([grad_mixed_query, grad_mixed_pair], axis=1)
     grad_normed = scatter_tokens(dot_t(grad_mixed, w_in, low), batch)
+    grad_normed = after(grad_normed, down_mine)
     grad_hidden, grad_norm_gain = norm_back(hidden, scale_one, norm_gain, grad_normed)
     grad_tokens = (grad_hidden + grad_middle).astype(low)
 
     feed_active = after(active, grad_mixed_pair)
     feed = scatter_tokens(dot(feed_active, w_down, low), batch)
+    feed = after(feed, query_mine)
     output = (mask * (middle + feed)).astype(low)
     up_mine = after(up_mine, grad_conv)
-    gate_mine = after(gate_mine, grad_product)
-    down_mine = after(down_mine, grad_mixed_pair)
     gated_late, mix_late = after((gated_own, mix_parts), grad_gated)
     grad_out_weight = out_owner([dot_w(gated_late, m) for m in mix_late])
     grad_up_weight = column_owner(up_mine, 1)

time: 937 us -> 963 us (1.028)
  Pallas kernels: 41.2 us -> 83 us
  waiting for transfers between devices: 341 us -> 324 us
  local copies, waits for them, and re-layouts: 142 us -> 130 us
    pallas_call x1, Pallas kernels: 7.98 us -> 49.8 us  [column_pieces(): pl.pallas_call(functools.partial(pick_kernel, count, part, spread * ycoun...]
    ppermute x4, waiting for transfers between devices: 23.8 us -> 6.2 us  [column_owner(): send = lax.ppermute(send, ('c', 'x'), pairs)]
    ppermute x6, waiting for transfers between devices: 28.6 us -> 11.3 us  [swap_slots(): line.append(lax.ppermute(slots[sy][sx], ('y', 'x'), pairs))]
    unnamed x264 -> x292, local copies, waits for them, and re-layouts: 66.5 us -> 54.5 us
  transfers between devices with their start and end apart: 92 -> 92, of which waited for: 42 -> 38; matrix products, arithmetic and copies ran while one was open for 32% -> 35% of each run, Pallas kernels for 4% -> 3%
where the time goes in v3:
time: 963 us; the launch traced here: 954 us
  waiting for transfers between devices  324 us (34%)
  matrix products  148 us (15%)
  starting transfers between devices  135 us (14%)
  local copies, waits for them, and re-layouts  130 us (13%)
  other arithmetic  117 us (12%)
  Pallas kernels  83 us (9%)
  between operations  17 us (2%)
    ppermute x58, waiting for transfers between devices, turned(): lax.ppermute(value, axis, [(i, (i + by) % length) for i in range(length)])  250 us
    ppermute x58, starting transfers between devices, turned(): lax.ppermute(value, axis, [(i, (i + by) % length) for i in range(length)])  69.4 us
    dot_general x6, matrix products, dot(): return jnp.dot(a, b, preferred_element_type=wide).astype(kind)  54.9 us
    unnamed x292, local copies, waits for them, and re-layouts  54.5 us
    pallas_call x1, Pallas kernels, column_pieces(): pl.pallas_call(functools.partial(pick_kernel, count, part, spread * ycoun...  49.8 us
    dot_general x6, matrix products, dot_t(): lax.dot_general(a, b, (((1,), (1,)), ((), ())), preferred_element_type=wide)  47.1 us
    dot_general x7, matrix products, dot_w(): lax.dot_general(a, b, (((0,), (0,)), ((), ())), preferred_element_type=wide)  45.7 us
    ppermute x12, starting transfers between devices, passed(): return lax.ppermute(value, axis, pairs)  37 us
  transfers between devices with their start and end apart: 92, of which 38 were waited for; matrix products, arithmetic and copies ran while one was open for 35% of the time, Pallas kernels for 3%

profile of v3, /device:TPU:9, one launch (start us, length us, event | category | flops | bytes accessed | tf_op | source)
XLA Modules:
  0.0 953.9 jit_solution(14149533485864686186)
XLA Ops:
  7.8 49.8 %shard_map.220 = (bf16[256,1536]{1,0:T(8,128)(2,1)}, bf16[256,1536]{1,0:T(8,128)(2,1)}) custom-call(s32[2]{0:T(128)} %pad_add_fusion.start_ref, bf16[256,6144]{1,0:T(8,128)(2,1)} %source.1), custom_call_target="tpu_custom_call" | custom-call | bytes 3145728 | tf_op jit(solution)/shard_map/pallas_call | solution.py:122
  59.0 11.7 %collective-permute-done.4 = bf16[256,1536]{1,0:T(8,128)(2,1)} collective-permute-done((bf16[256,1536]{1,0:T(8,128)(2,1)}, bf16[256,1536]{1,0:T(8,128)(2,1)}, u32[]{:S(2)}, u32[]{:S(2)}) %collective-permute-start.4) | collective-permute-done | bytes 786464 | tf_op jit(solution)/shard_map/ppermute | solution.py:156
  78.3 10.9 %collective-permute-done = bf16[1,128,2048]{2,1,0:T(8,128)(2,1)S(1)} collective-permute-done((bf16[1,128,2048]{2,1,0:T(8,128)(2,1)S(1)}, bf16[1,128,2048]{2,1,0:T(8,128)(2,1)S(1)}, u32[]{:S(2)}, u32[]{:S(2)}) %collective-permute-start) | collective-permute-done | bytes 524320 | tf_op jit(solution)/shard_map/ppermute | solution.py:24
  93.4 20.1 %collective-permute-done.1 = bf16[2,1,128,2048]{3,2,1,0:T(8,128)(2,1)} collective-permute-done((bf16[2,1,128,2048]{3,2,1,0:T(8,128)(2,1)}, bf16[2,1,128,2048]{3,2,1,0:T(8,128)(2,1)}, u32[]{:S(2)}, u32[]{:S(2)}) %collective-permute-start.1) | collective-permute-done | bytes 1048608 | tf_op jit(solution)/shard_map/ppermute | solution.py:24
  130.7 8.8 collective-permute-done.12
  149.5 22.2 %collective-permute-done.14 = bf16[128,1024]{1,0:T(8,128)(2,1)} collective-permute-done((bf16[128,1024]{1,0:T(8,128)(2,1)}, bf16[128,1024]{1,0:T(8,128)(2,1)}, u32[]{:S(2)}, u32[]{:S(2)}) %collective-permute-start.14) | collective-permute-done | bytes 262176 | tf_op jit(solution)/shard_map/ppermute | solution.py:24
  171.7 19.9 %collective-permute-done.15 = bf16[128,1024]{1,0:T(8,128)(2,1)} collective-permute-done((bf16[128,1024]{1,0:T(8,128)(2,1)}, bf16[128,1024]{1,0:T(8,128)(2,1)}, u32[]{:S(2)}, u32[]{:S(2)}) %collective-permute-start.15) | collective-permute-done | bytes 262176 | tf_op jit(solution)/shard_map/ppermute | solution.py:24
  203.5 20.7 %collective-permute-done.17 = bf16[2,1,256,1024]{3,2,0,1:T(8,128)(2,1)S(1)} collective-permute-done((bf16[2,1,256,1024]{3,2,0,1:T(8,128)(2,1)S(1)}, bf16[2,1,256,1024]{3,2,0,1:T(8,128)(2,1)S(1)}, u32[]{:S(2)}, u32[]{:S(2)}) %collective-permute-start.17) | collective-permute-done | bytes 1048608 | tf_op jit(solution)/shard_map/ppermute | solution.py:24
  240.2 10.3 %fusion.13 = bf16[1024,1536]{1,0:T(8,128)(2,1)S(1)} fusion(bf16[1024,2048]{1,0:T(8,128)(2,1)} %bitcast.477, bf16[1,2048,1536]{2,1,0:T(8,128)(2,1)} %all-gather.11.cloned.1.call-done), kind=kOutput, calls=%fused_computation.39 | convolution fusion | flops 6444023808 | bytes 13631488 | tf_op jit(solution)/shard_map/dot_general | solution.py:574
  279.8 10.1 %collective-permute-done.6 = f32[4,16,512]{2,1,0:T(8,128)S(1)} collective-permute-done((f32[4,16,512]{2,1,0:T(8,128)S(1)}, f32[4,16,512]{2,1,0:T(8,128)S(1)}, u32[]{:S(2)}, u32[]{:S(2)}) %collective-permute-start.6) | collective-permute-done | bytes 131104 | tf_op jit(solution)/shard_map/ppermute | solution.py:30
  289.9 11.3 %collective-permute-done.7 = f32[4,16,512]{2,1,0:T(8,128)S(1)} collective-permute-done((f32[4,16,512]{2,1,0:T(8,128)S(1)}, f32[4,16,512]{2,1,0:T(8,128)S(1)}, u32[]{:S(2)}, u32[]{:S(2)}) %collective-permute-start.7) | collective-permute-done | bytes 131104 | tf_op jit(solution)/shard_map/ppermute | solution.py:30
  317.9 8.6 collective-permute-done.10
  338.7 8.9 collective-permute-done.21
  350.5 19.5 %collective-permute-done.29 = bf16[2,1,128,2048]{3,2,1,0:T(8,128)(2,1)S(1)} collective-permute-done((bf16[2,1,128,2048]{3,2,1,0:T(8,128)(2,1)S(1)}, bf16[2,1,128,2048]{3,2,1,0:T(8,128)(2,1)S(1)}, u32[]{:S(2)}, u32[]{:S(2)}) %collective-permute-start.29) | collective-permute-done | bytes 1048608 | tf_op jit(solution)/shard_map/ppermute | solution.py:24
  373.1 19.3 %collective-permute-done.24 = bf16[2,1,128,2048]{3,2,1,0:T(8,128)(2,1)S(1)} collective-permute-done((bf16[2,1,128,2048]{3,2,1,0:T(8,128)(2,1)S(1)}, bf16[2,1,128,2048]{3,2,1,0:T(8,128)(2,1)S(1)}, u32[]{:S(2)}, u32[]{:S(2)}) %collective-permute-start.24) | collective-permute-done | bytes 1048608 | tf_op jit(solution)/shard_map/ppermute | solution.py:24
  395.4 11.9 %fusion.8 = f32[1024,1408]{1,0:T(8,128)} fusion(bf16[1024,2048]{1,0:T(8,128)(2,1)} %bitcast.482, bf16[1,2048,1408]{2,1,0:T(8,128)(2,1)} %all-gather.13.cloned.1.call-done), kind=kOutput, calls=%fused_computation.16 | convolution fusion | flops 5905580032 | bytes 15728640 | tf_op jit(solution)/shard_map/dot_general | solution.py:574
  407.3 13.0 %multiply_convert_fusion.2 = (bf16[1024,1408]{1,0:T(8,128)(2,1)S(1)}, f32[1024,1408]{1,0:T(8,128)}) fusion(f32[1024,1408]{1,0:T(8,128)} %fusion.8, bf16[1024,2048]{1,0:T(8,128)(2,1)} %bitcast.480, bf16[1408,2048]{1,0:T(8,128)(2,1)} %all-gather.9.cloned.1.call-done), kind=kOutput, calls=%fused_computation.21 | convolution fusion | flops 5914230784 | bytes 24379392 | tf_op jit(solution)/shard_map/dot_general | solution.py:578
  421.9 8.6 convolution_convert_fusion.2
  430.6 15.7 %multiply_convert_fusion = (bf16[1024,1408]{1,0:T(8,128)(2,1)S(1)}, bf16[1024,1408]{1,0:T(8,128)(2,1)}) fusion(f32[1024,1408]{1,0:T(8,128)} %fusion.8, f32[1024,1408]{1,0:T(8,128)} %get-tuple-element.324, bf16[1024,2048]{1,0:T(8,128)(2,1)} %bitcast.483, bf16[2048,1408]{1,0:T(8,128)(2,1)} %all-gather.7.cloned.1.call-done), kind=kOutput, calls=%fused_computation.19 | convolution fusion | flops 5924323328 | bytes 27262976 | tf_op jit(solution)/shard_map/dot_general | solution.py:574
  447.9 8.9 fusion.6
  469.5 19.4 %collective-permute-done.30 = bf16[2,1,128,2048]{3,2,1,0:T(8,128)(2,1)} collective-permute-done((bf16[2,1,128,2048]{3,2,1,0:T(8,128)(2,1)}, bf16[2,1,128,2048]{3,2,1,0:T(8,128)(2,1)}, u32[]{:S(2)}, u32[]{:S(2)}) %collective-permute-start.30) | collective-permute-done | bytes 1048608 | tf_op jit(solution)/shard_map/ppermute | solution.py:24
  497.4 8.8 convolution_convert_fusion.1
  526.7 10.4 %convolution_convert_fusion = bf16[1408,2048]{1,0:T(8,128)(2,1)} fusion(bf16[1024,1408]{1,0:T(8,128)(2,1)} %get-tuple-element.75, bf16[1024,2048]{1,0:T(8,128)(2,1)} %bitcast.481), kind=kOutput, calls=%fused_computation.2 | convolution fusion | flops 5908463616 | bytes 12845056 | tf_op jit(solution)/shard_map/dot_general | solution.py:582
  588.9 17.2 %shard_map.224 = (bf16[4,2,1,128,512]{4,3,2,1,0:T(8,128)(2,1)S(1)}, f32[16,512]{1,0:T(8,128)S(1)}, f32[16,512]{1,0:T(8,128)S(1)}) custom-call(s32[1]{0:T(128)} %bitcast.21.place_ref, bf16[4,2,1,128,512]{4,3,2,1,0:T(8,128)(2,1)S(1)} %copy-done.3, bf16[4,2,1,128,512]{4,3,2,1,0:T(8,128)(2,1)S(1)} %get-tuple-element.167.signal_ref.grad_ref, ...), custom_call_target="tpu_custom_call" | custom-call | flops 100663296 | bytes 4653056 | tf_op jit(solution)/shard_map/pallas_call | solution.py:497
  610.0 8.7 collective-permute-start.43
  670.1 9.7 %fusion.16 = bf16[1024,2048]{1,0:T(8,128)(2,1)S(1)} fusion(bf16[1,2048,1536]{2,1,0:T(8,128)(2,1)} %all-gather.11.cloned.1.call-done, bf16[1024,1024]{1,0:T(8,128)(2,1)} %bitcast.498, bf16[1024,512]{1,0:T(8,128)(2,1)} %bitcast.511), kind=kOutput, calls=%fused_computation.40 | convolution fusion | flops 6450839552 | bytes 13631488 | tf_op jit(solution)/shard_map/dot_general | solution.py:578
  691.3 9.8 %convolution_convert_fusion.4 = bf16[1024,2048]{1,0:T(8,128)(2,1)S(1)} fusion(bf16[1024,1408]{1,0:T(8,128)(2,1)} %get-tuple-element.75, bf16[1408,2048]{1,0:T(8,128)(2,1)} %all-gather.9.cloned.1.call-done), kind=kOutput, calls=%fused_computation.42 | convolution fusion | flops 5907677184 | bytes 12845056 | tf_op jit(solution)/shard_map/dot_general | solution.py:574
  701.1 9.3 multiply_reduce_fusion.1
  742.1 12.1 %collective-permute-done.81 = bf16[176,2048]{1,0:T(8,128)(2,1)S(1)} collective-permute-done((bf16[176,2048]{1,0:T(8,128)(2,1)}, bf16[176,2048]{1,0:T(8,128)(2,1)S(1)}, u32[]{:S(2)}, u32[]{:S(2)}) %collective-permute-start.81) | collective-permute-done | bytes 720928 | tf_op jit(solution)/shard_map/ppermute | solution.py:24
  763.7 18.9 %collective-permute-done.71 = bf16[128,1024]{1,0:T(8,128)(2,1)S(1)} collective-permute-done((bf16[128,1024]{1,0:T(8,128)(2,1)S(1)}, bf16[128,1024]{1,0:T(8,128)(2,1)S(1)}, u32[]{:S(2)}, u32[]{:S(2)}) %collective-permute-start.71) | collective-permute-done | bytes 262176 | tf_op jit(solution)/shard_map/ppermute | solution.py:24
  782.6 12.0 %collective-permute-done.72 = bf16[128,1024]{1,0:T(8,128)(2,1)S(1)} collective-permute-done((bf16[128,1024]{1,0:T(8,128)(2,1)S(1)}, bf16[128,1024]{1,0:T(8,128)(2,1)S(1)}, u32[]{:S(2)}, u32[]{:S(2)}) %collective-permute-start.72) | collective-permute-done | bytes 262176 | tf_op jit(solution)/shard_map/ppermute | solution.py:24
  810.2 15.7 %collective-permute-done.73 = bf16[128,1024]{1,0:T(8,128)(2,1)S(1)} collective-permute-done((bf16[128,1024]{1,0:T(8,128)(2,1)S(1)}, bf16[128,1024]{1,0:T(8,128)(2,1)S(1)}, u32[]{:S(2)}, u32[]{:S(2)}) %collective-permute-start.73) | collective-permute-done | bytes 262176 | tf_op jit(solution)/shard_map/ppermute | solution.py:24
  (690 shorter events, 474.4 us)
Async XLA Ops:
  7.2 233.0 %all-gather.11.cloned.1.call-start = ((), (), s32[]{:S(2)}) async-start(), calls=%async_computation.12 | async-start | bytes 7077888 | tf_op jit(solution)/shard_map/all_gather | solution.py:215
  73.0 322.4 %all-gather.13.cloned.1.call-start = ((), (), s32[]{:S(2)}) async-start(), calls=%async_computation.13 | async-start | bytes 6488064 | tf_op jit(solution)/shard_map/all_gather | solution.py:215
  141.7 265.6 %all-gather.9.cloned.1.call-start = ((), (), s32[]{:S(2)}) async-start(), calls=%async_computation.6 | async-start | bytes 6488064 | tf_op jit(solution)/shard_map/all_gather | solution.py:215
  143.8 28.0 %collective-permute-start.14 = (bf16[128,1024]{1,0:T(8,128)(2,1)}, bf16[128,1024]{1,0:T(8,128)(2,1)}, u32[]{:S(2)}, u32[]{:S(2)}) collective-permute-start(bf16[128,1024]{1,0:T(8,128)(2,1)} %dynamic_slice.315), channel_id=1, source_target_pairs={{0,4},{2,6},{4,0},{6,2},{1,5},{3,7},{5,1},{7,3},{8,12},{10,14},{12... | collective-permute-start | bytes 786440 | tf_op jit(solution)/shard_map/ppermute | solution.py:24
  146.1 45.5 %collective-permute-start.15 = (bf16[128,1024]{1,0:T(8,128)(2,1)}, bf16[128,1024]{1,0:T(8,128)(2,1)}, u32[]{:S(2)}, u32[]{:S(2)}) collective-permute-start(bf16[128,1024]{1,0:T(8,128)(2,1)} %dynamic_slice.315), channel_id=1, source_target_pairs={{0,2},{2,4},{4,6},{6,0},{1,3},{3,5},{5,7},{7,1},{8,10},{10,12},{12... | collective-permute-start | bytes 786440 | tf_op jit(solution)/shard_map/ppermute | solution.py:24
  233.8 196.8 %all-gather.7.cloned.1.call-start = ((), (), s32[]{:S(2)}) async-start(), calls=%async_computation.5 | async-start | bytes 6488064 | tf_op jit(solution)/shard_map/all_gather | solution.py:215
  259.2 77.4 %collective-permute-start.28 = (bf16[1,128,2048]{2,1,0:T(8,128)(2,1)}, bf16[1,128,2048]{2,1,0:T(8,128)(2,1)}, u32[]{:S(2)}, u32[]{:S(2)}) collective-permute-start(bf16[1,128,2048]{2,1,0:T(8,128)(2,1)} %get-tuple-element.203), channel_id=1, source_target_pairs={{0,16},{16,0},{1,17},{17,1},{2,18},{18,2},{3,19},{19,3},{4,20},{20... | collective-permute-start | bytes 1572872 | tf_op jit(solution)/shard_map/ppermute | solution.py:24
  259.6 52.4 %collective-permute-start.25 = (bf16[256,1408]{1,0:T(8,128)(2,1)S(1)}, bf16[256,1408]{1,0:T(8,128)(2,1)S(1)}, u32[]{:S(2)}, u32[]{:S(2)}) collective-permute-start(bf16[256,1408]{1,0:T(8,128)(2,1)S(1)} %copy-done.82), channel_id=1, source_target_pairs={{0,1},{9,8},{2,3},{11,10},{4,5},{13,12},{6,7},{15,14},{16,17},{25,... | collective-permute-start | bytes 2162696 | tf_op jit(solution)/shard_map/ppermute | solution.py:156
  289.9 59.2 %collective-permute-start.27 = (bf16[2,1,128,2048]{3,2,0,1:T(8,128)(2,1)}, bf16[2,1,128,2048]{3,2,0,1:T(8,128)(2,1)}, u32[]{:S(2)}, u32[]{:S(2)}) collective-permute-start(bf16[2,1,128,2048]{3,2,0,1:T(8,128)(2,1)} %get-tuple-element.200), channel_id=1, source_target_pairs={{0,16},{16,0},{1,17},{17,1},{2,18},{18,2},{3,19},{19,3},{4,20},{20... | collective-permute-start | bytes 3145736 | tf_op jit(solution)/shard_map/ppermute | solution.py:24
  313.3 204.7 %reduce-scatter.6.cloned.1.call-start = ((), (), s32[]{:S(2)}) async-start(), calls=%async_computation.7 | async-start | bytes 6488064 | tf_op jit(solution)/shard_map/reduce_scatter | solution.py:219
  337.8 32.2 %collective-permute-start.29 = (bf16[2,1,128,2048]{3,2,1,0:T(8,128)(2,1)S(1)}, bf16[2,1,128,2048]{3,2,1,0:T(8,128)(2,1)S(1)}, u32[]{:S(2)}, u32[]{:S(2)}) collective-permute-start(bf16[2,1,128,2048]{3,2,1,0:T(8,128)(2,1)S(1)} %get-tuple-element.206), channel_id=1, source_target_pairs={{0,1},{1,0},{2,3},{3,2},{4,5},{5,4},{6,7},{7,6},{8,9},{9,8},{10,11... | collective-permute-start | bytes 3145736 | tf_op jit(solution)/shard_map/ppermute | solution.py:24
  348.4 44.0 %collective-permute-start.24 = (bf16[2,1,128,2048]{3,2,1,0:T(8,128)(2,1)S(1)}, bf16[2,1,128,2048]{3,2,1,0:T(8,128)(2,1)S(1)}, u32[]{:S(2)}, u32[]{:S(2)}) collective-permute-start(bf16[2,1,128,2048]{3,2,1,0:T(8,128)(2,1)S(1)} %get-tuple-element.214), channel_id=1, source_target_pairs={{0,1},{1,0},{2,3},{3,2},{4,5},{5,4},{6,7},{7,6},{8,9},{9,8},{10,11... | collective-permute-start | bytes 3145736 | tf_op jit(solution)/shard_map/ppermute | solution.py:24
  430.5 218.3 %reduce-scatter.10.cloned.1.call-start = ((), (), s32[]{:S(2)}) async-start(), calls=%async_computation.9 | async-start | bytes 2359296 | tf_op jit(solution)/shard_map/reduce_scatter | solution.py:219
  551.7 118.4 %reduce-scatter.8.cloned.1.call-start = ((), (), s32[]{:S(2)}) async-start(), calls=%async_computation.8 | async-start | bytes 6488064 | tf_op jit(solution)/shard_map/reduce_scatter | solution.py:219
  552.5 185.4 %reduce-scatter.12.cloned.1.call-start = ((), (), s32[]{:S(2)}) async-start(), calls=%async_computation.10 | async-start | bytes 6488064 | tf_op jit(solution)/shard_map/reduce_scatter | solution.py:219
  553.2 328.6 %reduce-scatter.14.cloned.1.call-start = ((), (), s32[]{:S(2)}) async-start(), calls=%async_computation.11 | async-start | bytes 4718592 | tf_op jit(solution)/shard_map/reduce_scatter | solution.py:219
  583.0 59.9 %collective-permute-start.65 = (bf16[2048,1024]{1,0:T(8,128)(2,1)}, bf16[2048,1024]{1,0:T(8,128)(2,1)}, u32[]{:S(2)}, u32[]{:S(2)}) collective-permute-start(bf16[2048,1024]{1,0:T(8,128)(2,1)} %convolution_convert_fusion.3), channel_id=1, source_target_pairs={{0,8},{8,0},{1,9},{9,1},{2,10},{10,2},{3,11},{11,3},{4,12},{12,4},... | collective-permute-start | bytes 12582920 | tf_op jit(solution)/shard_map/ppermute | solution.py:24
  653.3 60.6 %collective-permute-start.66 = (bf16[2,1,256,1024]{3,2,1,0:T(8,128)(2,1)}, bf16[2,1,256,1024]{3,2,1,0:T(8,128)(2,1)}, u32[]{:S(2)}, u32[]{:S(2)}) collective-permute-start(bf16[2,1,256,1024]{3,2,1,0:T(8,128)(2,1)} %slice_bitcast_fusion.2), channel_id=1, source_target_pairs={{0,1},{1,0},{2,3},{3,2},{4,5},{5,4},{6,7},{7,6},{8,9},{9,8},{10,11... | collective-permute-start | bytes 3145736 | tf_op jit(solution)/shard_map/ppermute | solution.py:24
  663.7 55.1 %collective-permute-start.68 = (bf16[2,1,256,1024]{3,2,0,1:T(8,128)(2,1)}, bf16[2,1,256,1024]{3,2,0,1:T(8,128)(2,1)}, u32[]{:S(2)}, u32[]{:S(2)}) collective-permute-start(bf16[2,1,256,1024]{3,2,0,1:T(8,128)(2,1)} %bitcast.192), channel_id=1, source_target_pairs={{0,16},{16,0},{1,17},{17,1},{2,18},{18,2},{3,19},{19,3},{4,20},{20... | collective-permute-start | bytes 3145736 | tf_op jit(solution)/shard_map/ppermute | solution.py:24
  666.3 59.0 %collective-permute-start.61 = (bf16[2,1,256,512]{3,2,1,0:T(8,128)(2,1)S(1)}, bf16[2,1,256,512]{3,2,1,0:T(8,128)(2,1)}, u32[]{:S(2)}, u32[]{:S(2)}) collective-permute-start(bf16[2,1,256,512]{3,2,1,0:T(8,128)(2,1)S(1)} %get-tuple-element.272), channel_id=1, source_target_pairs={{0,8},{8,0},{1,9},{9,1},{2,10},{10,2},{3,11},{11,3},{4,12},{12,4},... | collective-permute-start | bytes 1572872 | tf_op jit(solution)/shard_map/ppermute | solution.py:24
  681.2 114.9 %collective-permute-start.49 = (bf16[2,1,128,2048]{3,2,1,0:T(8,128)(2,1)}, bf16[2,1,128,2048]{3,2,1,0:T(8,128)(2,1)}, u32[]{:S(2)}, u32[]{:S(2)}) collective-permute-start(bf16[2,1,128,2048]{3,2,1,0:T(8,128)(2,1)} %slice_bitcast_fusion.6), channel_id=1, source_target_pairs={{0,1},{1,0},{2,3},{3,2},{4,5},{5,4},{6,7},{7,6},{8,9},{9,8},{10,11... | collective-permute-start | bytes 3145736 | tf_op jit(solution)/shard_map/ppermute | solution.py:24
  683.9 115.9 %collective-permute-start.51 = (bf16[2,1,128,2048]{3,2,1,0:T(8,128)(2,1)}, bf16[2,1,128,2048]{3,2,1,0:T(8,128)(2,1)}, u32[]{:S(2)}, u32[]{:S(2)}) collective-permute-start(bf16[2,1,128,2048]{3,2,1,0:T(8,128)(2,1)} %bitcast.141), channel_id=1, source_target_pairs={{0,16},{16,0},{1,17},{17,1},{2,18},{18,2},{3,19},{19,3},{4,20},{20... | collective-permute-start | bytes 3145736 | tf_op jit(solution)/shard_map/ppermute | solution.py:24
  713.9 42.8 %collective-permute-start.75 = (bf16[256,1408]{1,0:T(8,128)(2,1)}, bf16[256,1408]{1,0:T(8,128)(2,1)}, u32[]{:S(2)}, u32[]{:S(2)}) collective-permute-start(bf16[256,1408]{1,0:T(8,128)(2,1)} %reduce-scatter.8.cloned.1.call-done), channel_id=1, source_target_pairs={{8,1},{1,8},{10,3},{3,10},{12,5},{5,12},{14,7},{7,14},{24,17},{17,... | collective-permute-start | bytes 2162696 | tf_op jit(solution)/shard_map/ppermute | solution.py:239
  754.2 28.4 %collective-permute-start.71 = (bf16[128,1024]{1,0:T(8,128)(2,1)S(1)}, bf16[128,1024]{1,0:T(8,128)(2,1)S(1)}, u32[]{:S(2)}, u32[]{:S(2)}) collective-permute-start(bf16[128,1024]{1,0:T(8,128)(2,1)S(1)} %get-tuple-element.184), channel_id=1, source_target_pairs={{0,4},{2,6},{4,0},{6,2},{1,5},{3,7},{5,1},{7,3},{8,12},{10,14},{12... | collective-permute-start | bytes 786440 | tf_op jit(solution)/shard_map/ppermute | solution.py:24
  756.8 37.8 %collective-permute-start.72 = (bf16[128,1024]{1,0:T(8,128)(2,1)S(1)}, bf16[128,1024]{1,0:T(8,128)(2,1)S(1)}, u32[]{:S(2)}, u32[]{:S(2)}) collective-permute-start(bf16[128,1024]{1,0:T(8,128)(2,1)S(1)} %get-tuple-element.183), channel_id=1, source_target_pairs={{0,6},{2,0},{4,2},{6,4},{1,7},{3,1},{5,3},{7,5},{8,14},{10,8},{12,... | collective-permute-start | bytes 786440 | tf_op jit(solution)/shard_map/ppermute | solution.py:24
  761.7 36.3 %collective-permute-start.44 = (bf16[2,1,128,2048]{3,2,1,0:T(8,128)(2,1)S(1)}, bf16[2,1,128,2048]{3,2,1,0:T(8,128)(2,1)S(1)}, u32[]{:S(2)}, u32[]{:S(2)}) collective-permute-start(bf16[2,1,128,2048]{3,2,1,0:T(8,128)(2,1)S(1)} %copy-done.70), channel_id=1, source_target_pairs={{0,1},{1,0},{2,3},{3,2},{4,5},{5,4},{6,7},{7,6},{8,9},{9,8},{10,11... | collective-permute-start | bytes 3145736 | tf_op jit(solution)/shard_map/ppermute | solution.py:24
  794.6 95.3 %collective-permute-start.82 = (bf16[2,176,2048]{2,1,0:T(8,128)(2,1)}, bf16[2,176,2048]{2,1,0:T(8,128)(2,1)}, u32[]{:S(2)}, u32[]{:S(2)}) collective-permute-start(bf16[2,176,2048]{2,1,0:T(8,128)(2,1)} %get-tuple-element.172), channel_id=1, source_target_pairs={{0,8},{8,0},{1,9},{9,1},{2,10},{10,2},{3,11},{11,3},{4,12},{12,4},... | collective-permute-start | bytes 4325384 | tf_op jit(solution)/shard_map/ppermute | solution.py:24
  796.1 31.2 %collective-permute-start.76 = (bf16[1,256,1408]{2,1,0:T(8,128)(2,1)S(1)}, bf16[1,256,1408]{2,1,0:T(8,128)(2,1)S(1)}, u32[]{:S(2)}, u32[]{:S(2)}) collective-permute-start(bf16[1,256,1408]{2,1,0:T(8,128)(2,1)S(1)} %fusion.59), channel_id=1, source_target_pairs={{0,16},{16,0},{1,17},{17,1},{2,18},{18,2},{3,19},{19,3},{4,20},{20... | collective-permute-start | bytes 2162696 | tf_op jit(solution)/shard_map/ppermute | solution.py:24
  799.8 37.4 %collective-permute-start.50 = (bf16[1,128,2048]{2,1,0:T(8,128)(2,1)S(1)}, bf16[1,128,2048]{2,1,0:T(8,128)(2,1)S(1)}, u32[]{:S(2)}, u32[]{:S(2)}) collective-permute-start(bf16[1,128,2048]{2,1,0:T(8,128)(2,1)S(1)} %fusion.70), channel_id=1, source_target_pairs={{0,16},{16,0},{1,17},{17,1},{2,18},{18,2},{3,19},{19,3},{4,20},{20... | collective-permute-start | bytes 1572872 | tf_op jit(solution)/shard_map/ppermute | solution.py:24
  805.0 38.6 %collective-permute-start.52 = (bf16[1,128,2048]{2,1,0:T(8,128)(2,1)S(1)}, bf16[1,128,2048]{2,1,0:T(8,128)(2,1)S(1)}, u32[]{:S(2)}, u32[]{:S(2)}) collective-permute-start(bf16[1,128,2048]{2,1,0:T(8,128)(2,1)S(1)} %fusion.71), channel_id=1, source_target_pairs={{0,1},{1,0},{2,3},{3,2},{4,5},{5,4},{6,7},{7,6},{8,9},{9,8},{10,11... | collective-permute-start | bytes 1572872 | tf_op jit(solution)/shard_map/ppermute | solution.py:24
  837.2 36.6 %collective-permute-start.74 = (bf16[2,128,1024]{2,1,0:T(8,128)(2,1)}, bf16[2,128,1024]{2,1,0:T(8,128)(2,1)}, u32[]{:S(2)}, u32[]{:S(2)}) collective-permute-start(bf16[2,128,1024]{2,1,0:T(8,128)(2,1)} %get-tuple-element.267), channel_id=1, source_target_pairs={{0,8},{8,0},{1,9},{9,1},{2,10},{10,2},{3,11},{11,3},{4,12},{12,4},... | collective-permute-start | bytes 1572872 | tf_op jit(solution)/shard_map/ppermute | solution.py:24
  857.4 40.7 %collective-permute-start.77 = (bf16[2,1,256,1408]{3,2,1,0:T(8,128)(2,1)}, bf16[2,1,256,1408]{3,2,1,0:T(8,128)(2,1)}, u32[]{:S(2)}, u32[]{:S(2)}) collective-permute-start(bf16[2,1,256,1408]{3,2,1,0:T(8,128)(2,1)} %get-tuple-element.179), channel_id=1, source_target_pairs={{0,8},{8,0},{1,9},{9,1},{2,10},{10,2},{3,11},{11,3},{4,12},{12,4},... | collective-permute-start | bytes 4325384 | tf_op jit(solution)/shard_map/ppermute | solution.py:24
  (170 other events, 2529.1 us)
Sparse Core Ops, SparseCore 0:
  73.1 65.2 all-gather.10
  141.9 73.8 all-gather.12
  233.9 68.9 all-gather.8
  313.4 59.9 all-gather.6
  430.7 65.9 reduce-scatter.5
  551.8 53.2 reduce-scatter.9
  608.0 62.0 reduce-scatter.7
  672.9 62.9 reduce-scatter.11
  738.8 71.5 reduce-scatter.13

commit v4 on v3

--- a/solution.py
+++ b/solution.py
@@ -15,10 +15,6 @@
 cores = 2
 
 
-def after(value, *earlier):
-    return lax.optimization_barrier((value, earlier))[0]
-
-
 def turned(value, axis, by):
     length = lax.axis_size(axis)
     return lax.ppermute(value, axis, [(i, (i + by) % length) for i in range(length)])
@@ -28,27 +24,6 @@
     length = lax.axis_size(axis)
     pairs = [(i, i + by) for i in range(length) if 0 <= i + by < length]
     return lax.ppermute(value, axis, pairs)
-
-
-def gather_slots(value, axis):
-    length = lax.axis_size(axis)
-    return jnp.stack([value] + [turned(value, axis, -d) for d in range(1, length)])
-
-
-def sum_slots(partial, axis):
-    length = lax.axis_size(axis)
-    total = partial[0].astype(wide)
-    for d in range(1, length):
-        total = total + turned(partial[d].astype(low), axis, d).astype(wide)
-    return total
-
-
-def sum_axis(value, axis):
-    length = lax.axis_size(axis)
-    total = value
-    for d in range(1, length):
-        total = total + turned(value, axis, d)
-    return total
 
 
 def swap_slots(slots):
@@ -71,24 +46,83 @@
     return result
 
 
-def gather_tokens(value):
-    half = value.shape[0] // 2
-    width = value.shape[-1]
-    first = gather_slots(value[:half], "x")
-    second = gather_slots(value[half:], "y")
-    first = gather_slots(first, "y")
-    second = gather_slots(second, "x")
-    return jnp.stack([first, jnp.swapaxes(second, 0, 1)]).reshape(-1, width)
-
-
-def scatter_tokens(partial, batch):
-    width = partial.shape[-1]
-    grid = partial.reshape(2, lax.axis_size("y"), lax.axis_size("x"), batch // 2, -1, width)
-    first = sum_slots(jnp.swapaxes(grid[0], 0, 1), "x")
-    second = sum_slots(grid[1], "y")
-    first = sum_slots(first, "y")
-    second = sum_slots(second, "x")
-    return jnp.concatenate([first, second], axis=0)
+class Line:
+    def __init__(self):
+        self.last = ()
+
+    def run(self, work, *values):
+        values = lax.optimization_barrier((values, self.last))[0]
+        result = work(*values)
+        self.last = jax.tree.leaves(result)
+        return result
+
+
+def moved(value, axis, sign):
+    return [turned(value, axis, sign * d) for d in range(1, lax.axis_size(axis))]
+
+
+class Gather:
+    def __init__(self, first, second):
+        self.held = (first, second)
+        self.got = (moved(first, "x", -1), moved(second, "y", -1))
+
+    def turn(self, line):
+        self.held = line.run(
+            lambda held, got: tuple(jnp.stack([h] + g) for h, g in zip(held, got)), self.held, self.got
+        )
+        self.got = (moved(self.held[0], "y", -1), moved(self.held[1], "x", -1))
+
+    def end(self, line):
+        def work(held, got):
+            first = jnp.stack([held[0]] + got[0])
+            second = jnp.swapaxes(jnp.stack([held[1]] + got[1]), 0, 1)
+            return jnp.stack([first, second]).reshape(-1, first.shape[-1])
+
+        return line.run(work, self.held, self.got)
+
+
+def split_sum(partial):
+    grid = partial.reshape(2, lax.axis_size("y"), lax.axis_size("x"), -1, partial.shape[-1])
+    first = [grid[0][:, d].astype(low) for d in range(grid.shape[2])]
+    second = [grid[1][d].astype(low) for d in range(grid.shape[1])]
+    return first, second
+
+
+def add_up(parts, got):
+    total = parts[0].astype(wide)
+    for g in got:
+        total = total + g.astype(wide)
+    return total
+
+
+class Scatter:
+    def __init__(self, parts):
+        self.parts = parts
+        self.send("x", "y")
+
+    def send(self, *axes):
+        self.got = [
+            [turned(p, axis, d + 1) for d, p in enumerate(part[1:])]
+            for part, axis in zip(self.parts, axes)
+        ]
+
+    def turn(self, line):
+        def work(parts, got):
+            result = []
+            for part, g in zip(parts, got):
+                total = add_up(part, g).astype(low)
+                result.append([total[d] for d in range(total.shape[0])])
+            return result
+
+        self.parts = line.run(work, self.parts, self.got)
+        self.send("y", "x")
+
+    def rest(self):
+        return self.parts, self.got
+
+    @staticmethod
+    def sum(parts, got):
+        return jnp.stack([add_up(part, g) for part, g in zip(parts, got)])
 
 
 def pick_kernel(count, part, stride, start_ref, source, *refs):
@@ -125,7 +159,7 @@
             grid_spec=pltpu.PrefetchScalarGridSpec(
                 num_scalar_prefetch=1,
                 in_specs=[pl.BlockSpec(memory_space=pl.ANY)],
-                out_specs=[pl.BlockSpec(memory_space=pl.ANY)] * spread,
+                out_specs=[pl.BlockSpec(memory_space=pltpu.VMEM)] * spread,
                 scratch_shapes=[pltpu.SemaphoreType.DMA((count * spread,))],
             ),
             cost_estimate=pl.CostEstimate(
@@ -144,16 +178,22 @@
     ]
 
 
-def column_block(pieces):
+def column_moves(pieces):
     spread, ccount = lax.axis_size("x"), lax.axis_size("c")
     share = spread // ccount
-    place, core = lax.axis_index("x"), lax.axis_index("c")
     got = [pieces[0]]
     for d in range(1, spread):
         pairs = [
             (i // share * spread + i, i // share * spread + (i + d) % spread) for i in range(spread)
         ]
         got.append(lax.ppermute(pieces[d], ("c", "x"), pairs))
+    return got
+
+
+def column_block(got):
+    spread, ccount = lax.axis_size("x"), lax.axis_size("c")
+    share = spread // ccount
+    place, core = lax.axis_index("x"), lax.axis_index("c")
     got = jnp.stack(got)
     return jnp.concatenate(
         [
@@ -180,35 +220,23 @@
     ]
 
 
-def gather_halves(value):
-    return gather_tokens(value.reshape(2, value.shape[0] // 2, -1))
-
-
-def gather_out(weight):
-    ycount = lax.axis_size("y")
-    part = weight.shape[0] // ycount
+def out_block(weight):
+    part = weight.shape[0] // lax.axis_size("y")
     rows = lax.dynamic_slice_in_dim(weight, lax.axis_index("y") * part, part, 0)
-    block = core_halves(rows)[0]
-    held = in_order(gather_slots(block, "z"), "z").reshape(depth * part, -1)
-    mine = gather_halves(held)
-    return [mine] + [turned(mine, "c", -d) for d in range(1, lax.axis_size("c"))]
-
-
-def out_owner(terms):
-    total = terms[0].astype(wide)
-    for d in range(1, len(terms)):
-        total = total + turned(terms[d], "c", d).astype(wide)
-    mine = scatter_tokens(total.astype(low), 2)
+    return core_halves(rows)[0]
+
+
+def by_z(slots):
+    held = in_order(jnp.stack(slots), "z")
+    return held.reshape(2, -1, held.shape[-1])
+
+
+def z_slots(mine):
     mine = mine.reshape(depth, -1, mine.shape[-1]).astype(low)
     place = lax.axis_index("z")
-    slots = jnp.stack(
-        [lax.dynamic_index_in_dim(mine, (place + d) % depth, 0, False) for d in range(depth)]
-    )
-    mine = sum_slots(slots, "z").astype(low)
-    whole = in_order(gather_slots(mine, "y"), "y")
-    whole = in_order(gather_slots(whole, "c"), "c")
-    ccount, ycount, rows, width = whole.shape
-    return jnp.transpose(whole, (1, 2, 0, 3)).reshape(ycount * rows, ccount * width).astype(wide)
+    return [
+        lax.dynamic_index_in_dim(mine, (place + d) % depth, 0, False) for d in range(depth)
+    ]
 
 
 def gather_tile(block):
@@ -219,41 +247,62 @@
     return lax.psum_scatter(term, ("z", "c"), scatter_dimension=0, tiled=True)
 
 
-def column_owner(mine, groups):
-    spread, ycount, ccount = lax.axis_size("x"), lax.axis_size("y"), lax.axis_size("c")
+def owner_parts(mine):
+    spread, ccount = lax.axis_size("x"), lax.axis_size("c")
     share = spread // ccount
-    place, core, yplace = lax.axis_index("x"), lax.axis_index("c"), lax.axis_index("y")
-    rows = mine.shape[0] // share
-    width = mine.shape[1]
-    parts = mine.reshape(share, rows, width)
-    got = []
-    for d in range(spread):
-        send = lax.dynamic_index_in_dim(
+    place, core = lax.axis_index("x"), lax.axis_index("c")
+    parts = mine.reshape(share, -1, mine.shape[-1])
+    return [
+        lax.dynamic_index_in_dim(
             parts, jnp.clip((place + d) % spread - core * share, 0, share - 1), 0, False
         )
-        if d > 0:
-            pairs = [
-                ((i + d) % spread // share * spread + i, i // share * spread + (i + d) % spread)
-                for i in range(spread)
-            ]
-            send = lax.ppermute(send, ("c", "x"), pairs)
-        got.append(send)
+        for d in range(spread)
+    ]
+
+
+def owner_moves(parts):
+    spread, ccount = lax.axis_size("x"), lax.axis_size("c")
+    share = spread // ccount
+    got = [parts[0]]
+    for d in range(1, spread):
+        pairs = [
+            ((i + d) % spread // share * spread + i, i // share * spread + (i + d) % spread)
+            for i in range(spread)
+        ]
+        got.append(lax.ppermute(parts[d], ("c", "x"), pairs))
+    return got
+
+
+def owner_held(got):
+    spread, ccount = lax.axis_size("x"), lax.axis_size("c")
+    share = spread // ccount
+    place, core = lax.axis_index("x"), lax.axis_index("c")
     got = jnp.stack(got)
-    held = jnp.stack(
+    return jnp.stack(
         [
             lax.dynamic_index_in_dim(got, (place - core * share - j) % spread, 0, False)
             for j in range(share)
         ]
     )
-    flat = gather_slots(gather_slots(held, "y"), "c").reshape(-1, rows, width)
-    part = width // (groups * depth)
+
+
+def owner_ranks(slots):
+    spread, ccount, ycount = lax.axis_size("x"), lax.axis_size("c"), lax.axis_size("y")
+    share = spread // ccount
+    core, yplace = lax.axis_index("c"), lax.axis_index("y")
+    flat = slots.reshape((-1,) + slots.shape[3:])
     ranks = []
     for i in range(spread):
         for k in range(ycount):
             slot = (i // share - core) % ccount * ycount + (k - yplace) % ycount
             ranks.append(lax.dynamic_index_in_dim(flat, slot * share + i % share, 0, False))
+    return ranks
+
+
+def owner_whole(ranks, count):
+    part = ranks[0].shape[1] // count
     pieces = []
-    for at in range(groups * depth):
+    for at in range(count):
         pieces += [r[:, at * part : (at + 1) * part].astype(wide) for r in ranks]
     return jnp.concatenate(pieces, axis=1)
 
@@ -264,12 +313,6 @@
     return jnp.stack(
         [lax.dynamic_index_in_dim(slots, (j - place) % length, 0, False) for j in range(length)]
     )
-
-
-def row_owner(mine):
-    whole = in_order(gather_slots(mine, "y"), "y")
-    whole = in_order(gather_slots(whole, "c"), "c")
-    return jnp.swapaxes(whole, 0, 1).reshape(-1, mine.shape[1]).astype(wide)
 
 
 def rank_rows(values, axis):
@@ -604,134 +647,211 @@
     mask = (position[None, :] < lengths[:, None]).astype(wide)[..., None]
     block = spread * local
 
-    in_pieces = column_pieces(in_weight, 3)
-    hidden = after(tokens, in_pieces).astype(wide)
-    scale_one = rms_scale(hidden)
-    normed = (hidden * scale_one * norm_gain).astype(low)
-    in_block = column_block(in_pieces)
-    w_in = gather_tile(in_block)
-    normed_all = gather_tokens(normed)
-    gate_weight, out_weight, up_weight, down_weight = after(
-        (gate_weight, out_weight, up_weight, down_weight), normed_all, in_block
-    )
-    gate_block = column_block(column_pieces(gate_weight, 1))
-    w_gate = gather_tile(gate_block)
-    w_out = gather_out(after(out_weight, gate_block))
-    up_pieces = column_pieces(up_weight, 1)
-    down_piece = after(row_block(down_weight), gate_block)
-    w_down = gather_tile(down_piece)
-    up_block = after(column_block(after(up_pieces, w_out)), down_piece)
-    w_up = gather_tile(up_block)
-    cotangent = after(cotangent, w_out)
-    grad_out = cotangent.astype(wide) * mask
-    grad_feed_all = gather_tokens(grad_out.astype(low))
+    count = 3 * depth
+    line = Line()
+    run = line.run
+
+    def stacked(value, got):
+        return jnp.stack([value] + got)
+
+    block_out = run(out_block, out_weight)
+    out_got = moved(block_out, "z", -1)
+    in_got = column_moves(run(lambda w: column_pieces(w, 3), in_weight))
+
+    def norm_one(values, gain):
+        values = values.astype(wide)
+        scale = rms_scale(values)
+        normed = (values * scale * gain).astype(low)
+        return normed[: batch // 2], normed[batch // 2 :], scale
+
+    first, second, scale_one = run(norm_one, tokens, norm_gain)
+    normed_move = Gather(first, second)
+    w_in = gather_tile(run(column_block, in_got))
+    normed_move.turn(line)
+    w_down = gather_tile(run(row_block, down_weight))
+    held = run(lambda own, got: by_z([own] + got), block_out, out_got)
+    out_move = Gather(held[:1], held[1:])
+    gate_got = column_moves(run(lambda w: column_pieces(w, 1), gate_weight))
+    normed_all = normed_move.end(line)
+    out_move.turn(line)
+    w_gate = gather_tile(run(column_block, gate_got))
+    up_got = column_moves(run(lambda w: column_pieces(w, 1), up_weight))
 
     channels = w_in.shape[1] // 3
+    half = channels // 2
     grid = (2 * ycount, spread, batch // 2, local)
-    taps = jnp.concatenate(
-        [rank_rows(conv_taps[:, g * width : (g + 1) * width], 1) for g in range(3)], axis=1
-    )
-    decay = rank_rows(filter_decay, 0).T
-    residue = rank_rows(filter_residue, 0).T
-    mixed = dot(normed_all, w_in, low).reshape(grid + (3 * channels,))
+
+    def rank_values(all_taps, all_decay, all_residue):
+        return (
+            jnp.concatenate(
+                [rank_rows(all_taps[:, g * width : (g + 1) * width], 1) for g in range(3)], axis=1
+            ),
+            rank_rows(all_decay, 0).T,
+            rank_rows(all_residue, 0).T,
+        )
+
+    taps, decay, residue = run(rank_values, conv_taps, filter_decay, filter_residue)
     opening = (lax.axis_index("x") + jnp.arange(spread)) % spread == 0
     opening = opening[None, :, None, None, None]
     closing = (lax.axis_index("x") + jnp.arange(spread)) % spread == spread - 1
     closing = closing[None, :, None, None, None]
 
-    tail = jnp.roll(mixed[:, :, :, local - 2 :], 1, axis=1)
+    def project(v, w):
+        value = dot(v, w, low).reshape(grid + (3 * channels,))
+        return value, jnp.roll(value[:, :, :, local - 2 :], 1, axis=1)
+
+    mixed, tail = run(project, normed_all, w_in)
     behind = passed(tail, "z", 1)
-    extended = jnp.concatenate([jnp.where(opening, behind, tail), mixed], axis=3).astype(wide)
-    short = (
-        taps[0] * extended[:, :, :, 2:]
-        + taps[1] * extended[:, :, :, 1:-1]
-        + taps[2] * extended[:, :, :, :-2]
-    )
-    query = short[..., :channels]
-    keys = short[..., channels : 2 * channels]
-    values = short[..., 2 * channels :]
-    product = (keys * values).astype(low)
+
+    def feed_grad(values):
+        values = (values.astype(wide) * mask).astype(low)
+        return values[: batch // 2], values[batch // 2 :]
+
+    feed_move = Gather(*run(feed_grad, cotangent))
+    w_up = gather_tile(run(column_block, up_got))
+    out_own = out_move.end(line)
+    w_out = [out_own] + moved(out_own, "c", -1)
+
+    def extend(value, ends, before, g):
+        at = slice(g * channels, (g + 1) * channels)
+        return jnp.concatenate(
+            [jnp.where(opening, before[..., at], ends[..., at]), value[..., at]], axis=3
+        ).astype(wide)
+
+    def short_of(value, ends, before, weights, g):
+        longer = extend(value, ends, before, g)
+        own = weights[:, g * channels : (g + 1) * channels]
+        return own[0] * longer[:, :, :, 2:] + own[1] * longer[:, :, :, 1:-1] + own[2] * longer[:, :, :, :-2]
 
     spot = lax.axis_index("x").astype(jnp.int32).reshape(1)
-    state_end, slope_end = states_of(spot, product, decay)
+
+    def multiply(value, ends, before, weights, rates):
+        keys, values = (short_of(value, ends, before, weights, g) for g in (1, 2))
+        product = (keys * values).astype(low)
+        return (product,) + tuple(states_of(spot, product, rates))
+
+    product, state_end, slope_end = run(multiply, mixed, tail, behind, taps, decay)
     states = [passed(state_end, "z", k) for k in range(1, depth)]
-    start = states[0]
-    for k in range(1, depth - 1):
-        start = start + jnp.exp(-decay * (k * block)) * states[k]
-    convolved = forward_of(spot, product, decay, residue, start)
-    gated = (query * convolved.astype(wide)).astype(low)
-    gated_slots = gated.reshape(2, ycount, spread, -1, channels)
-    got = swap_slots(
-        [
-            [gated_slots[:, k, i].reshape(-1, channels) for i in range(spread)]
-            for k in range(ycount)
-        ]
-    )
-    half = channels // 2
-    gated_own = jnp.concatenate(
-        [g[:, h * half : (h + 1) * half] for h in range(2) for line in got for g in line], axis=1
-    )
-    mixer = in_order(jnp.stack([dot(gated_own, w) for w in w_out]), "c")
-    mixer = jnp.concatenate([m for m in mixer], axis=1).reshape(batch, local, width)
-    middle = hidden + mixer
-
-    scale_two = rms_scale(middle)
-    normed_two = (middle * scale_two * feed_gain).astype(low)
-    normed_two_all = gather_tokens(normed_two)
-    gate = dot(normed_two_all, w_gate)
-    sigma = jax.nn.sigmoid(gate)
-    grad_active = dot_t(grad_feed_all, w_down)
-    grad_upper = (grad_active * gate * sigma).astype(low)
-    up_term = dot_w(normed_two_all, grad_upper)
+    feed_move.turn(line)
+
+    def combine(parts, rates):
+        total = parts[0]
+        for k in range(1, depth - 1):
+            total = total + jnp.exp(-rates * (k * block)) * parts[k]
+        return total
+
+    def convolve(parts, value, ends, before, weights, signal, rates, amounts):
+        start = combine(parts, rates)
+        result = forward_of(spot, signal, rates, amounts, start)
+        query = short_of(value, ends, before, weights, 0)
+        gated = (query * result.astype(wide)).astype(low)
+        slots = gated.reshape(2, ycount, spread, -1, channels)
+        return (
+            start,
+            result,
+            [[slots[:, k, i].reshape(-1, channels) for i in range(spread)] for k in range(ycount)],
+        )
+
+    start, convolved, gated = run(
+        convolve, states, mixed, tail, behind, taps, product, decay, residue
+    )
+    gated_got = swap_slots(gated)
+    grad_feed_all = feed_move.end(line)
+
+    def mix(got, weights, values, gain):
+        own = jnp.concatenate(
+            [g[:, h * half : (h + 1) * half] for h in range(2) for row in got for g in row], axis=1
+        )
+        mixer = in_order(jnp.stack([dot(own, w) for w in weights]), "c")
+        mixer = jnp.concatenate([m for m in mixer], axis=1).reshape(batch, local, width)
+        middle = values.astype(wide) + mixer
+        scale = rms_scale(middle)
+        normed = (middle * scale * gain).astype(low)
+        return own, middle, scale, normed[: batch // 2], normed[batch // 2 :]
+
+    gated_own, middle, scale_two, first, second = run(mix, gated_got, w_out, tokens, feed_gain)
+
+    two_move = Gather(first, second)
+    grad_active = run(dot_t, grad_feed_all, w_down)
+    two_move.turn(line)
+    slopes = [passed(slope_end, "z", k) for k in range(1, depth)]
+    normed_two_all = two_move.end(line)
+
+    def open_gate(v, w, back):
+        value = dot(v, w)
+        return value, (back * value * jax.nn.sigmoid(value)).astype(low)
+
+    gate, grad_upper = run(open_gate, normed_two_all, w_gate, grad_active)
+    up_term = run(dot_w, normed_two_all, grad_upper)
     up_mine = scatter_tile(up_term)
-    upper = dot(normed_two_all, after(w_up, up_term))
-    active = (gate * sigma * upper).astype(low)
-    grad_gate = (grad_active * upper * sigma * (1.0 + gate * (1.0 - sigma))).astype(low)
-    partial_two = (dot_t(grad_gate, w_gate) + dot_t(grad_upper, w_up)).astype(low)
-    grad_normed_two = scatter_tokens(partial_two, batch)
-    weigh_two, weigh_gate = after((normed_two_all, grad_gate), partial_two)
-    gate_term = dot_w(weigh_two, weigh_gate)
-    gate_mine = scatter_tile(gate_term)
-    weigh_active, weigh_feed = after((active, grad_feed_all), gate_term)
-    down_term = dot_w(weigh_active, weigh_feed)
-    down_mine = scatter_tile(down_term)
-
-    grad_middle, grad_feed_gain = norm_back(middle, scale_two, feed_gain, grad_normed_two)
-    grad_middle = grad_middle + grad_out
-    grad_mix = grad_middle.astype(low).reshape(-1, width)
-
-    mix_parts = core_halves(grad_mix)
-    grad_gated_own = sum(dot_t(m, w) for m, w in zip(mix_parts, w_out)).astype(low)
-    grad_slots = after(grad_gated_own, up_mine, gate_term).reshape(-1, 2, ycount, spread, half)
-    got = swap_slots(
-        [
-            [grad_slots[:, :, k, i].reshape(-1, channels) for i in range(spread)]
-            for k in range(ycount)
-        ]
-    )
-    grad_gated = jnp.stack([jnp.stack(line) for line in got])
-    grad_gated = grad_gated.reshape(ycount, spread, 2, batch // 2, local, channels)
-    grad_gated = jnp.moveaxis(grad_gated, 2, 0).reshape(grid + (channels,)).astype(wide)
-    grad_gated = after(grad_gated, down_term)
-    grad_query = grad_gated * convolved.astype(wide)
-    grad_conv = (grad_gated * query).astype(low)
-
-    later_end = later_of(spot, grad_conv, decay)
+
+    def activate(v, w, value, back):
+        upper = dot(v, w)
+        sigma = jax.nn.sigmoid(value)
+        return (
+            (value * sigma * upper).astype(low),
+            (back * upper * sigma * (1.0 + value * (1.0 - sigma))).astype(low),
+        )
+
+    active, grad_gate = run(activate, normed_two_all, w_up, gate, grad_active)
+    two_back = Scatter(
+        run(
+            lambda a, b, wa, wb: split_sum((dot_t(a, wa) + dot_t(b, wb)).astype(low)),
+            grad_gate,
+            grad_upper,
+            w_gate,
+            w_up,
+        )
+    )
+    gate_mine = scatter_tile(run(dot_w, normed_two_all, grad_gate))
+    down_mine = scatter_tile(run(dot_w, active, grad_feed_all))
+    two_back.turn(line)
+
+    def middle_back(rest, values, scale, gain, back, weights):
+        grad_normed = Scatter.sum(*rest).reshape(batch, local, width)
+        result, grad_gain = norm_back(values, scale, gain, grad_normed)
+        result = result + back.astype(wide) * mask
+        parts = core_halves(result.astype(low).reshape(-1, width))
+        own = sum(dot_t(m, w) for m, w in zip(parts, weights)).astype(low)
+        slots = own.reshape(-1, 2, ycount, spread, half)
+        return (
+            result,
+            grad_gain,
+            parts,
+            [
+                [slots[:, :, k, i].reshape(-1, channels) for i in range(spread)]
+                for k in range(ycount)
+            ],
+        )
+
+    grad_middle, grad_feed_gain, mix_parts, grad_slots = run(
+        middle_back, two_back.rest(), middle, scale_two, feed_gain, cotangent, w_out
+    )
+    grad_got = swap_slots(grad_slots)
+    out_terms = run(lambda g, parts: [dot_w(g, m) for m in parts], gated_own, mix_parts)
+    out_terms_got = [turned(t, "c", d + 1) for d, t in enumerate(out_terms[1:])]
+
+    def conv_grads(got, result, value, ends, before, weights, rates):
+        grad = jnp.stack([jnp.stack(row) for row in got])
+        grad = grad.reshape(ycount, spread, 2, batch // 2, local, channels)
+        grad = jnp.moveaxis(grad, 2, 0).reshape(grid + (channels,)).astype(wide)
+        grad_query = (grad * result.astype(wide)).astype(wide)
+        grad_conv = (grad * short_of(value, ends, before, weights, 0)).astype(low)
+        return (
+            grad_query,
+            jnp.roll(grad_query[:, :, :, :2].astype(low), -1, axis=1),
+            grad_conv,
+            later_of(spot, grad_conv, rates),
+        )
+
+    grad_query, query_head, grad_conv, later_end = run(
+        conv_grads, grad_got, convolved, mixed, tail, behind, taps, decay
+    )
     laters = [passed(later_end, "z", -k) for k in range(1, depth)]
-    later = laters[0]
-    for k in range(1, depth - 1):
-        later = later + jnp.exp(-decay * (k * block)) * laters[k]
-    slope_end = after(slope_end, normed_two_all)
-    slopes = [passed(slope_end, "z", k) for k in range(1, depth)]
-    slope = slopes[0]
-    for k in range(1, depth - 1):
-        slope = slope + jnp.exp(-decay * (k * block)) * (slopes[k] + (k * block) * states[k])
-
-    low_taps = [taps[:, g * channels : (g + 1) * channels] for g in range(3)]
-
-    def short_back(grad_short, weights):
-        head = jnp.roll(grad_short[:, :, :, :2].astype(low), -1, axis=1)
-        ahead = passed(head, "z", -1)
+    query_ahead = passed(query_head, "z", -1)
+    feed_back = Scatter(run(lambda a, w: split_sum(dot(a, w, low)), active, w_down))
+
+    def short_back(grad_short, head, ahead, weights):
         whole = jnp.concatenate([grad_short, jnp.where(closing, ahead, head).astype(wide)], axis=3)
         result = (
             weights[0] * whole[:, :, :, :-2]
@@ -740,65 +860,189 @@
         )
         return result.astype(low).reshape(-1, grad_short.shape[-1])
 
-    grad_mixed_query = short_back(grad_query, low_taps[0])
-    query_mine = scatter_tile(after(dot_w(normed_all, grad_mixed_query), down_term))
-
-    grad_product, grad_residue, grad_decay = backward_of(
-        spot, product, grad_conv, decay, residue, start, slope, later
-    )
-    grad_product = grad_product.astype(wide)
-    grad_pair = jnp.concatenate([grad_product * values, grad_product * keys], axis=-1)
-    grad_mixed_pair = short_back(grad_pair, jnp.concatenate(low_taps[1:], axis=1))
-    grad_mixed_pair = after(grad_mixed_pair, gate_mine)
-    pair_mine = scatter_tile(dot_w(normed_all, grad_mixed_pair))
-    grad_mixed = jnp.concatenate([grad_mixed_query, grad_mixed_pair], axis=1)
-    grad_normed = scatter_tokens(dot_t(grad_mixed, w_in, low), batch)
-    grad_normed = after(grad_normed, down_mine)
-    grad_hidden, grad_norm_gain = norm_back(hidden, scale_one, norm_gain, grad_normed)
-    grad_tokens = (grad_hidden + grad_middle).astype(low)
-
-    feed_active = after(active, grad_mixed_pair)
-    feed = scatter_tokens(dot(feed_active, w_down, low), batch)
-    feed = after(feed, query_mine)
-    output = (mask * (middle + feed)).astype(low)
-    up_mine = after(up_mine, grad_conv)
-    gated_late, mix_late = after((gated_own, mix_parts), grad_gated)
-    grad_out_weight = out_owner([dot_w(gated_late, m) for m in mix_late])
-    grad_up_weight = column_owner(up_mine, 1)
-    grad_gate_weight = column_owner(gate_mine, 1)
-    grad_down = row_owner(down_mine)
-    grad_in_weight = jnp.concatenate(
-        [column_owner(query_mine, 1), column_owner(pair_mine, 2)], axis=1
-    )
-
-    query_late, pair_late, extended_late = after((grad_query, grad_pair, extended), grad_mixed_pair)
-    grad_taps = []
-    for g, part in enumerate((query_late, pair_late[..., :channels], pair_late[..., channels:])):
-        own = extended_late[..., g * channels : (g + 1) * channels]
-        grad_taps += [
-            jnp.sum(part * own[:, :, :, 2 - j : local + 2 - j], axis=(0, 1, 2, 3)) for j in range(3)
-        ]
-    gains = jnp.stack([grad_norm_gain, grad_feed_gain]).reshape(-1, channels)
-    small = jnp.concatenate([grad_residue, grad_decay, jnp.stack(grad_taps)], axis=0)
-    count = small.shape[0]
-    small = sum_axis(sum_axis(jnp.concatenate([small, gains], axis=0), "c"), "z")
-    small = gather_slots(gather_slots(small, "x"), "y")
-    gains = jnp.sum(small[:, :, count:], axis=(0, 1)).reshape(2, width)
-    small = all_channels(small[:, :, :count])
+    def query_back(grad, head, ahead, weights, v):
+        result = short_back(grad, head, ahead, weights[:, :channels])
+        return result, dot_w(v, result)
+
+    grad_mixed_query, query_term = run(
+        query_back, grad_query, query_head, query_ahead, taps, normed_all
+    )
+    query_mine = scatter_tile(query_term)
+
+    def conv_back(signal, grad, rates, amounts, begin, parts, ended, ends_later, value, ends, before, weights):
+        slope = parts[0]
+        for k in range(1, depth - 1):
+            slope = slope + jnp.exp(-rates * (k * block)) * (parts[k] + (k * block) * ended[k])
+        later = combine(ends_later, rates)
+        grad_product, grad_residue, grad_decay = backward_of(
+            spot, signal, grad, rates, amounts, begin, slope, later
+        )
+        grad_product = grad_product.astype(wide)
+        keys, values = (short_of(value, ends, before, weights, g) for g in (1, 2))
+        pair = jnp.concatenate([grad_product * values, grad_product * keys], axis=-1)
+        return pair, jnp.roll(pair[:, :, :, :2].astype(low), -1, axis=1), grad_residue, grad_decay
+
+    grad_pair, pair_head, grad_residue, grad_decay = run(
+        conv_back,
+        product,
+        grad_conv,
+        decay,
+        residue,
+        start,
+        slopes,
+        states,
+        laters,
+        mixed,
+        tail,
+        behind,
+        taps,
+    )
+    pair_ahead = passed(pair_head, "z", -1)
+    feed_back.turn(line)
+
+    def pair_back(grad, head, ahead, weights, v):
+        result = short_back(grad, head, ahead, weights[:, channels:])
+        return result, dot_w(v, result)
+
+    grad_mixed_pair, pair_term = run(
+        pair_back, grad_pair, pair_head, pair_ahead, taps, normed_all
+    )
+    pair_mine = scatter_tile(pair_term)
+    one_back = Scatter(
+        run(
+            lambda a, b, w: split_sum(dot_t(jnp.concatenate([a, b], axis=1), w, low)),
+            grad_mixed_query,
+            grad_mixed_pair,
+            w_in,
+        )
+    )
+
+    out_back_parts = run(
+        lambda own, got: split_sum(add_up([own], got)), out_terms[0], out_terms_got
+    )
+    parts = run(lambda a, b: owner_parts(jnp.concatenate([a, b], axis=1)), up_mine, gate_mine)
+    both_got = owner_moves(parts)
+    output = run(
+        lambda rest, values: (
+            mask * (values + Scatter.sum(*rest).reshape(batch, local, width))
+        ).astype(low),
+        feed_back.rest(),
+        middle,
+    )
+    one_back.turn(line)
+    out_back = Scatter(out_back_parts)
+
+    def tap_sums(query, pair, value, ends, before):
+        sums = []
+        for g, part in enumerate((query, pair[..., :channels], pair[..., channels:])):
+            own = extend(value, ends, before, g)
+            sums += [
+                jnp.sum(part * own[:, :, :, 2 - j : local + 2 - j], axis=(0, 1, 2, 3))
+                for j in range(3)
+            ]
+        return jnp.stack(sums)
+
+    grad_taps = run(tap_sums, grad_query, grad_pair, mixed, tail, behind)
+    both_held = run(owner_held, both_got)
+    both_got = moved(both_held, "y", -1)
+
+    def tokens_back(rest, values, scale, gain, back, small):
+        values = values.astype(wide)
+        grad_normed = Scatter.sum(*rest).reshape(batch, local, width)
+        result, grad_gain = norm_back(values, scale, gain, grad_normed)
+        gains = jnp.stack([grad_gain, small[0]]).reshape(-1, channels)
+        return (result + back).astype(low), jnp.concatenate(list(small[1:]) + [gains], axis=0)
+
+    grad_tokens, small = run(
+        tokens_back,
+        one_back.rest(),
+        tokens,
+        scale_one,
+        norm_gain,
+        grad_middle,
+        (grad_feed_gain, grad_residue, grad_decay, grad_taps),
+    )
+    small_got = moved(small, "c", 1)
+    out_back.turn(line)
+    both_held = run(stacked, both_held, both_got)
+    both_got = moved(both_held, "c", -1)
+    small = run(lambda v, got: v + sum(got), small, small_got)
+    small_got = moved(small, "z", 1)
+    down_got = moved(run(lambda v: v + 0, down_mine), "y", -1)
+    out_slots = run(
+        lambda rest: z_slots(Scatter.sum(*rest).reshape(channels, -1)), out_back.rest()
+    )
+    out_got = [turned(p, "z", d + 1) for d, p in enumerate(out_slots[1:])]
+    small = run(lambda v, got: v + sum(got), small, small_got)
+    small_got = moved(small, "x", -1)
+
+    def both_whole(own, got):
+        ranks = owner_ranks(jnp.stack([own] + got))
+        middle_at = ranks[0].shape[1] // 2
+        return (
+            owner_whole([r[:, :middle_at] for r in ranks], depth),
+            owner_whole([r[:, middle_at:] for r in ranks], depth),
+        )
+
+    grad_up_weight, grad_gate_weight = run(both_whole, both_held, both_got)
+    down_held = run(stacked, down_mine, down_got)
+    down_got = moved(down_held, "c", -1)
+    out_held = run(lambda own, got: add_up([own], got).astype(low), out_slots[0], out_got)
+    out_got = moved(out_held, "y", -1)
+    small = run(stacked, small, small_got)
+    small_got = moved(small, "y", -1)
+
+    def down_whole(own, got):
+        whole = in_order(jnp.swapaxes(in_order(jnp.stack([own] + got), "c"), 0, 1), "y")
+        return whole.reshape(-1, width).astype(wide)
+
+    grad_down = run(down_whole, down_held, down_got)
+    out_held = run(stacked, out_held, out_got)
+    out_got = moved(out_held, "c", -1)
     poles = decay.shape[0]
-    grad_conv_taps = jnp.concatenate(
-        [small[2 * poles + 3 * g : 2 * poles + 3 * g + 3] for g in range(3)], axis=1
+
+    def small_whole(own, got):
+        slots = jnp.stack([own] + got)
+        rows = 2 * poles + 9
+        gains = jnp.sum(slots[:, :, rows:], axis=(0, 1)).reshape(2, width)
+        whole = all_channels(slots[:, :, :rows])
+        grad_conv_taps = jnp.concatenate(
+            [whole[2 * poles + 3 * g : 2 * poles + 3 * g + 3] for g in range(3)], axis=1
+        )
+        return gains[0], gains[1], grad_conv_taps, whole[:poles].T, whole[poles : 2 * poles].T
+
+    grad_norm_gain, feed_gain_sum, grad_conv_taps, residue_sum, decay_sum = run(
+        small_whole, small, small_got
+    )
+    parts = run(
+        lambda a, b: owner_parts(jnp.concatenate([a, b], axis=1)), query_mine, pair_mine
+    )
+    in_got = owner_moves(parts)
+
+    def out_whole(own, got):
+        whole = in_order(jnp.stack([own] + got), "c")
+        whole = in_order(jnp.swapaxes(whole, 0, 1), "y")
+        ys, cs, rows, columns = whole.shape
+        return jnp.swapaxes(whole, 1, 2).reshape(ys * rows, cs * columns).astype(wide)
+
+    grad_out_weight = run(out_whole, out_held, out_got)
+    in_held = run(owner_held, in_got)
+    in_held = run(stacked, in_held, moved(in_held, "y", -1))
+    grad_in_weight = run(
+        lambda own, got: owner_whole(owner_ranks(jnp.stack([own] + got)), count),
+        in_held,
+        moved(in_held, "c", -1),
     )
     return (
         output,
         grad_tokens,
-        gains[0],
+        grad_norm_gain,
         grad_in_weight,
         grad_conv_taps,
-        small[:poles].T,
-        small[poles : 2 * poles].T,
+        residue_sum,
+        decay_sum,
         grad_out_weight,
-        gains[1],
+        feed_gain_sum,
         grad_gate_weight,
         grad_up_weight,
         grad_down,

time: 963 us -> 806 us (0.84)
  waiting for transfers between devices: 324 us -> 256 us
  Pallas kernels: 83 us -> 36.7 us
  starting transfers between devices: 135 us -> 108 us
  local copies, waits for them, and re-layouts: 130 us -> 114 us
    ppermute x58 -> x54, waiting for transfers between devices: 250 us -> 199 us  [turned(): lax.ppermute(value, axis, [(i, (i + by) % length) for i in range(length)])]
    pallas_call x1, Pallas kernels: 49.8 us -> 3.46 us  [column_pieces(): pl.pallas_call(functools.partial(pick_kernel, count, part, spread * ycoun...]
    unnamed x292 -> x247, local copies, waits for them, and re-layouts: 54.5 us -> 33.8 us
    convert_element_type x12 -> x29, other arithmetic: 8.44 us -> 27.7 us  [the longest x8 10.3 us: work(): total = add_up(part, g).astype(low)]
    ppermute x58 -> x54, starting transfers between devices: 69.4 us -> 54.9 us  [turned(): lax.ppermute(value, axis, [(i, (i + by) % length) for i in range(length)])]
    add x20 -> x5, other arithmetic: 21.4 us -> 8.7 us  [the longest x1 4.34 us: add_up(): total = total + g.astype(wide)]
    another operation x45 -> x47, other arithmetic: 42.5 us -> 53.2 us  [the longest x12 14 us: work(): return jnp.stack([first, second]).reshape(-1, first.shape[-1])]
    ppermute x12, waiting for transfers between devices: 30.8 us -> 20.3 us  [passed(): return lax.ppermute(value, axis, pairs)]
  transfers between devices with their start and end apart: 92 -> 86, of which waited for: 38 -> 30; matrix products, arithmetic and copies ran while one was open for 35% -> 44% of each run, Pallas kernels for 3% -> 4%
where the time goes in v4:
time: 806 us; the launch traced here: 797 us
  waiting for transfers between devices  256 us (32%)
  matrix products  146 us (18%)
  other arithmetic  120 us (15%)
  local copies, waits for them, and re-layouts  114 us (14%)
  starting transfers between devices  108 us (13%)
  Pallas kernels  36.7 us (5%)
  between operations  16.7 us (2%)
    ppermute x54, waiting for transfers between devices, turned(): lax.ppermute(value, axis, [(i, (i + by) % length) for i in range(length)])  199 us
    dot_general x6, matrix products, dot(): return jnp.dot(a, b, preferred_element_type=wide).astype(kind)  55.1 us
    ppermute x54, starting transfers between devices, turned(): lax.ppermute(value, axis, [(i, (i + by) % length) for i in range(length)])  54.9 us
    dot_general x6, matrix products, dot_t(): lax.dot_general(a, b, (((1,), (1,)), ((), ())), preferred_element_type=wide)  46.1 us
    dot_general x7, matrix products, dot_w(): lax.dot_general(a, b, (((0,), (0,)), ((), ())), preferred_element_type=wide)  44.5 us
    unnamed x247, local copies, waits for them, and re-layouts  33.8 us
    pallas_call x4, Pallas kernels, conv_call(): pl.pallas_call(kernel, out_shape=results, grid_spec=pltpu.PrefetchScalarG...  33.2 us
    ppermute x12, starting transfers between devices, passed(): return lax.ppermute(value, axis, pairs)  27.7 us
  transfers between devices with their start and end apart: 86, of which 30 were waited for; matrix products, arithmetic and copies ran while one was open for 44% of the time, Pallas kernels for 4%

profile of v4, /device:TPU:9, one launch (start us, length us, event | category | flops | bytes accessed | tf_op | source)
XLA Modules:
  0.0 797.2 jit_solution(1104937410911794418)
XLA Ops:
  19.2 7.1 collective-permute-done.2
  30.1 10.9 %collective-permute-done = bf16[1,128,2048]{2,1,0:T(8,128)(2,1)} collective-permute-done((bf16[1,128,2048]{2,1,0:T(8,128)(2,1)S(1)}, bf16[1,128,2048]{2,1,0:T(8,128)(2,1)}, u32[]{:S(2)}, u32[]{:S(2)}) %collective-permute-start) | collective-permute-done | bytes 524320 | tf_op jit(solution)/shard_map/ppermute | solution.py:20
  61.7 9.6 %collective-permute-done.6 = bf16[128,1024]{1,0:T(8,128)(2,1)S(1)} collective-permute-done((bf16[128,1024]{1,0:T(8,128)(2,1)}, bf16[128,1024]{1,0:T(8,128)(2,1)S(1)}, u32[]{:S(2)}, u32[]{:S(2)}) %collective-permute-start.6) | collective-permute-done | bytes 262176 | tf_op jit(solution)/shard_map/ppermute | solution.py:20
  72.6 10.7 %collective-permute-done.7 = bf16[128,1024]{1,0:T(8,128)(2,1)S(1)} collective-permute-done((bf16[128,1024]{1,0:T(8,128)(2,1)}, bf16[128,1024]{1,0:T(8,128)(2,1)S(1)}, u32[]{:S(2)}, u32[]{:S(2)}) %collective-permute-start.7) | collective-permute-done | bytes 262176 | tf_op jit(solution)/shard_map/ppermute | solution.py:20
  83.3 19.7 %collective-permute-done.8 = bf16[128,1024]{1,0:T(8,128)(2,1)S(1)} collective-permute-done((bf16[128,1024]{1,0:T(8,128)(2,1)}, bf16[128,1024]{1,0:T(8,128)(2,1)S(1)}, u32[]{:S(2)}, u32[]{:S(2)}) %collective-permute-start.8) | collective-permute-done | bytes 262176 | tf_op jit(solution)/shard_map/ppermute | solution.py:20
  109.6 6.1 collective-permute-done.10
  129.2 25.3 %collective-permute-done.13 = bf16[2,1,256,1024]{3,2,0,1:T(8,128)(2,1)} collective-permute-done((bf16[2,1,256,1024]{3,2,0,1:T(8,128)(2,1)S(1)}, bf16[2,1,256,1024]{3,2,0,1:T(8,128)(2,1)}, u32[]{:S(2)}, u32[]{:S(2)}) %collective-permute-start.13) | collective-permute-done | bytes 1048608 | tf_op jit(solution)/shard_map/ppermute | solution.py:20
  160.4 10.1 %convolution_convert_fusion.4 = bf16[1024,1536]{1,0:T(8,128)(2,1)S(1)} fusion(bf16[1024,2048]{1,0:T(8,128)(2,1)} %bitcast.408, bf16[2048,1536]{1,0:T(8,128)(2,1)} %bitcast.537), kind=kOutput, calls=%fused_computation.26 | convolution fusion | flops 6444023808 | bytes 13631488 | tf_op jit(solution)/shard_map/dot_general | solution.py:617
  203.0 16.8 %collective-permute-done.16 = f32[4,16,512]{2,1,0:T(8,128)S(1)} collective-permute-done((f32[4,16,512]{2,1,0:T(8,128)S(1)}, f32[4,16,512]{2,1,0:T(8,128)S(1)}, u32[]{:S(2)}, u32[]{:S(2)}) %collective-permute-start.16) | collective-permute-done | bytes 131104 | tf_op jit(solution)/shard_map/ppermute | solution.py:26
  222.3 7.5 shard_map.222
  233.9 15.8 %collective-permute-done.24 = bf16[2,1,128,2048]{3,2,0,1:T(8,128)(2,1)S(1)} collective-permute-done((bf16[2,1,128,2048]{3,2,0,1:T(8,128)(2,1)S(1)}, bf16[2,1,128,2048]{3,2,0,1:T(8,128)(2,1)S(1)}, u32[]{:S(2)}, u32[]{:S(2)}) %collective-permute-start.24) | collective-permute-done | bytes 1048608 | tf_op jit(solution)/shard_map/ppermute | solution.py:20
  267.3 11.8 %fusion.125 = f32[1024,1408]{1,0:T(8,128)} fusion(bf16[1024,2048]{1,0:T(8,128)(2,1)} %bitcast.411, bf16[1408,2048]{1,0:T(8,128)(2,1)} %all-gather.8.cloned.1.call-done), kind=kOutput, calls=%fused_computation.492 | convolution fusion | flops 5905580032 | bytes 15728640 | tf_op jit(solution)/shard_map/dot_general | solution.py:621
  283.8 20.9 %collective-permute-done.29 = bf16[2,1,128,2048]{3,2,0,1:T(8,128)(2,1)S(1)} collective-permute-done((bf16[2,1,128,2048]{3,2,0,1:T(8,128)(2,1)S(1)}, bf16[2,1,128,2048]{3,2,0,1:T(8,128)(2,1)S(1)}, u32[]{:S(2)}, u32[]{:S(2)}) %collective-permute-start.29) | collective-permute-done | bytes 1048608 | tf_op jit(solution)/shard_map/ppermute | solution.py:20
  309.2 13.7 %multiply_convert_fusion.2 = (bf16[1024,1408]{1,0:T(8,128)(2,1)S(1)}, f32[1024,1408]{1,0:T(8,128)}) fusion(f32[1024,1408]{1,0:T(8,128)} %fusion.125, bf16[1024,2048]{1,0:T(8,128)(2,1)} %bitcast.413, bf16[2048,1408]{1,0:T(8,128)(2,1)} %bitcast.539), kind=kOutput, calls=%fused_computation.9 | convolution fusion | flops 5914230784 | bytes 24379392 | tf_op jit(solution)/shard_map/dot_general | solution.py:617
  324.4 8.7 %convolution_convert_fusion.2 = bf16[2048,1408]{1,0:T(8,128)(2,1)} fusion(bf16[1024,2048]{1,0:T(8,128)(2,1)S(1)} %bitcast.415, bf16[1024,1408]{1,0:T(8,128)(2,1)S(1)} %get-tuple-element.345), kind=kOutput, calls=%fused_computation.4 | convolution fusion | flops 5908463616 | bytes 12845056 | tf_op jit(solution)/shard_map/dot_general | solution.py:625
  333.2 15.0 %multiply_convert_fusion = (bf16[1024,1408]{1,0:T(8,128)(2,1)S(1)}, bf16[1024,1408]{1,0:T(8,128)(2,1)}) fusion(f32[1024,1408]{1,0:T(8,128)} %get-tuple-element.339, f32[1024,1408]{1,0:T(8,128)} %fusion.125, bf16[1024,2048]{1,0:T(8,128)(2,1)} %bitcast.414, bf16[2048,1408]{1,0:T(8,128)(2,1)} %bitcast.541), kind=kOutput, calls=%fused_computation.6 | convolution fusion | flops 5924323328 | bytes 27262976 | tf_op jit(solution)/shard_map/dot_general | solution.py:617
  349.8 8.9 %fusion.126 = f32[1024,2048]{1,0:T(8,128)S(1)} fusion(bf16[1024,1408]{1,0:T(8,128)(2,1)S(1)} %get-tuple-element.348, bf16[2048,1408]{1,0:T(8,128)(2,1)} %bitcast.540), kind=kOutput, calls=%fused_computation.493 | convolution fusion | flops 5905580032 | bytes 17039360 | tf_op jit(solution)/shard_map/dot_general | solution.py:621
  358.8 8.4 %add_convert_fusion = bf16[1024,2048]{1,0:T(8,128)(2,1)S(1)} fusion(f32[1024,2048]{1,0:T(8,128)S(1)} %fusion.126, bf16[1024,1408]{1,0:T(8,128)(2,1)} %copy-done.84, bf16[2048,1408]{1,0:T(8,128)(2,1)S(1)} %bitcast.542), kind=kOutput, calls=%fused_computation.1 | convolution fusion | flops 5909774336 | bytes 21233664 | tf_op jit(solution)/shard_map/dot_general | solution.py:621
  372.1 8.7 %convolution_convert_fusion.1 = bf16[2048,1408]{1,0:T(8,128)(2,1)} fusion(bf16[1024,2048]{1,0:T(8,128)(2,1)S(1)} %bitcast.416, bf16[1024,1408]{1,0:T(8,128)(2,1)S(1)} %copy-done.83), kind=kOutput, calls=%fused_computation.3 | convolution fusion | flops 5908463616 | bytes 12845056 | tf_op jit(solution)/shard_map/dot_general | solution.py:625
  382.3 10.7 %convolution_convert_fusion = bf16[1408,2048]{1,0:T(8,128)(2,1)} fusion(bf16[1024,1408]{1,0:T(8,128)(2,1)} %get-tuple-element.378, bf16[1024,2048]{1,0:T(8,128)(2,1)} %bitcast.412), kind=kOutput, calls=%fused_computation.2 | convolution fusion | flops 5908463616 | bytes 12845056 | tf_op jit(solution)/shard_map/dot_general | solution.py:625
  393.1 10.5 %collective-permute-done.30 = bf16[2,128,2048]{2,1,0:T(8,128)(2,1)S(1)} collective-permute-done((bf16[2,128,2048]{2,1,0:T(8,128)(2,1)}, bf16[2,128,2048]{2,1,0:T(8,128)(2,1)S(1)}, u32[]{:S(2)}, u32[]{:S(2)}) %collective-permute-start.30) | collective-permute-done | bytes 1048608 | tf_op jit(solution)/shard_map/ppermute | solution.py:20
  466.1 6.2 collective-permute-start.45
  477.5 8.7 %convolution_convert_fusion.5 = bf16[1024,2048]{1,0:T(8,128)(2,1)S(1)} fusion(bf16[1024,1408]{1,0:T(8,128)(2,1)S(1)} %copy-done.81, bf16[1408,2048]{1,0:T(8,128)(2,1)} %all-gather.8.cloned.1.call-done), kind=kOutput, calls=%fused_computation.27 | convolution fusion | flops 5907677184 | bytes 12845056 | tf_op jit(solution)/shard_map/dot_general | solution.py:617
  496.6 7.0 collective-permute-start.48
  509.3 17.2 %shard_map.224 = (bf16[4,2,1,128,512]{4,3,2,1,0:T(8,128)(2,1)S(1)}, f32[16,512]{1,0:T(8,128)S(1)}, f32[16,512]{1,0:T(8,128)S(1)}) custom-call(s32[1]{0:T(128)} %bitcast.place_ref, bf16[4,2,1,128,512]{4,3,2,1,0:T(8,128)(2,1)S(1)} %copy-done.3, bf16[4,2,1,128,512]{4,3,2,1,0:T(8,128)(2,1)S(1)} %get-tuple-element.386.signal_ref.grad_ref, ...), custom_call_target="tpu_custom_call" | custom-call | flops 100663296 | bytes 4653056 | tf_op jit(solution)/shard_map/pallas_call | solution.py:540
  538.5 6.2 convolution_convert_fusion.8
  544.7 9.1 %convolution_convert_fusion.3 = bf16[1024,2048]{1,0:T(8,128)(2,1)S(1)} fusion(bf16[2048,1536]{1,0:T(8,128)(2,1)} %bitcast.538, bf16[1024,1024]{1,0:T(8,128)(2,1)S(1)} %bitcast.437, bf16[1024,512]{1,0:T(8,128)(2,1)} %bitcast.459), kind=kOutput, calls=%fused_computation.25 | convolution fusion | flops 6450839552 | bytes 13631488 | tf_op jit(solution)/shard_map/dot_general | solution.py:621
  576.1 12.2 %collective-permute-start.54 = (bf16[256,2816]{1,0:T(8,128)(2,1)}, bf16[256,2816]{1,0:T(8,128)(2,1)}, u32[]{:S(2)}, u32[]{:S(2)}) collective-permute-start(bf16[256,2816]{1,0:T(8,128)(2,1)} %constant_dynamic-update-slice_fusion.20), channel_id=1, source_target_pairs={{8,1},{1,8},{10,3},{3,10},{12,5},{5,12},{14,7},{7,14},{24,17},{17,... | collective-permute-start | bytes 4325384 | tf_op jit(solution)/shard_map/ppermute | solution.py:272
  603.4 21.2 %collective-permute-done.54 = bf16[256,2816]{1,0:T(8,128)(2,1)} collective-permute-done((bf16[256,2816]{1,0:T(8,128)(2,1)}, bf16[256,2816]{1,0:T(8,128)(2,1)}, u32[]{:S(2)}, u32[]{:S(2)}) %collective-permute-start.54) | collective-permute-done | bytes 1441824 | tf_op jit(solution)/shard_map/ppermute | solution.py:272
  639.7 8.2 %collective-permute-done.56 = bf16[1,256,2816]{2,1,0:T(8,128)(2,1)} collective-permute-done((bf16[1,256,2816]{2,1,0:T(8,128)(2,1)}, bf16[1,256,2816]{2,1,0:T(8,128)(2,1)}, u32[]{:S(2)}, u32[]{:S(2)}) %collective-permute-start.56) | collective-permute-done | bytes 1441824 | tf_op jit(solution)/shard_map/ppermute | solution.py:20
  717.9 15.1 %collective-permute-done.66 = bf16[128,1024]{1,0:T(8,128)(2,1)} collective-permute-done((bf16[128,1024]{1,0:T(8,128)(2,1)}, bf16[128,1024]{1,0:T(8,128)(2,1)}, u32[]{:S(2)}, u32[]{:S(2)}) %collective-permute-start.66) | collective-permute-done | bytes 262176 | tf_op jit(solution)/shard_map/ppermute | solution.py:20
  768.8 12.6 %collective-permute-done.75 = bf16[1,256,1536]{2,1,0:T(8,128)(2,1)S(1)} collective-permute-done((bf16[1,256,1536]{2,1,0:T(8,128)(2,1)S(1)}, bf16[1,256,1536]{2,1,0:T(8,128)(2,1)S(1)}, u32[]{:S(2)}, u32[]{:S(2)}) %collective-permute-start.75) | collective-permute-done | bytes 786464 | tf_op jit(solution)/shard_map/ppermute | solution.py:20
  (638 shorter events, 399.9 us)
Async XLA Ops:
  7.2 153.2 %all-gather.10.cloned.1.call-start = ((), (), s32[]{:S(2)}) async-start(), calls=%async_computation.11 | async-start | bytes 7077888 | tf_op jit(solution)/shard_map/all_gather | solution.py:243
  28.7 238.6 %all-gather.8.cloned.1.call-start = ((), (), s32[]{:S(2)}) async-start(), calls=%async_computation.5 | async-start | bytes 6488064 | tf_op jit(solution)/shard_map/all_gather | solution.py:243
  46.8 262.4 %all-gather.14.cloned.1.call-start = ((), (), s32[]{:S(2)}) async-start(), calls=%async_computation.13 | async-start | bytes 6488064 | tf_op jit(solution)/shard_map/all_gather | solution.py:243
  46.8 56.7 %collective-permute-start.4 = (bf16[2,1,128,2048]{3,2,0,1:T(8,128)(2,1)}, bf16[2,1,128,2048]{3,2,0,1:T(8,128)(2,1)}, u32[]{:S(2)}, u32[]{:S(2)}) collective-permute-start(bf16[2,1,128,2048]{3,2,0,1:T(8,128)(2,1)} %pad_maximum_fusion.16), channel_id=1, source_target_pairs={{0,1},{1,0},{2,3},{3,2},{4,5},{5,4},{6,7},{7,6},{8,9},{9,8},{10,11... | collective-permute-start | bytes 3145736 | tf_op jit(solution)/shard_map/ppermute | solution.py:20
  48.2 55.3 %collective-permute-start.3 = (bf16[2,1,128,2048]{3,2,0,1:T(8,128)(2,1)}, bf16[2,1,128,2048]{3,2,0,1:T(8,128)(2,1)}, u32[]{:S(2)}, u32[]{:S(2)}) collective-permute-start(bf16[2,1,128,2048]{3,2,0,1:T(8,128)(2,1)} %get-tuple-element.660), channel_id=1, source_target_pairs={{0,16},{16,0},{1,17},{17,1},{2,18},{18,2},{3,19},{19,3},{4,20},{20... | collective-permute-start | bytes 3145736 | tf_op jit(solution)/shard_map/ppermute | solution.py:20
  49.6 33.7 %collective-permute-start.7 = (bf16[128,1024]{1,0:T(8,128)(2,1)}, bf16[128,1024]{1,0:T(8,128)(2,1)S(1)}, u32[]{:S(2)}, u32[]{:S(2)}) collective-permute-start(bf16[128,1024]{1,0:T(8,128)(2,1)} %dynamic_slice.238), channel_id=1, source_target_pairs={{0,4},{2,6},{4,0},{6,2},{1,5},{3,7},{5,1},{7,3},{8,12},{10,14},{12... | collective-permute-start | bytes 786440 | tf_op jit(solution)/shard_map/ppermute | solution.py:20
  51.9 51.1 %collective-permute-start.8 = (bf16[128,1024]{1,0:T(8,128)(2,1)}, bf16[128,1024]{1,0:T(8,128)(2,1)S(1)}, u32[]{:S(2)}, u32[]{:S(2)}) collective-permute-start(bf16[128,1024]{1,0:T(8,128)(2,1)} %dynamic_slice.238), channel_id=1, source_target_pairs={{0,2},{2,4},{4,6},{6,0},{1,3},{3,5},{5,7},{7,1},{8,10},{10,12},{12... | collective-permute-start | bytes 786440 | tf_op jit(solution)/shard_map/ppermute | solution.py:20
  71.3 44.6 %collective-permute-start.5 = (bf16[256,1408]{1,0:T(8,128)(2,1)}, bf16[256,1408]{1,0:T(8,128)(2,1)S(1)}, u32[]{:S(2)}, u32[]{:S(2)}) collective-permute-start(bf16[256,1408]{1,0:T(8,128)(2,1)} %concatenate.192), channel_id=1, source_target_pairs={{0,1},{9,8},{2,3},{11,10},{4,5},{13,12},{6,7},{15,14},{16,17},{25,... | collective-permute-start | bytes 2162696 | tf_op jit(solution)/shard_map/ppermute | solution.py:189
  117.2 216.0 %all-gather.12.cloned.1.call-start = ((), (), s32[]{:S(2)}) async-start(), calls=%async_computation.12 | async-start | bytes 6488064 | tf_op jit(solution)/shard_map/all_gather | solution.py:243
  119.3 62.0 %collective-permute-start.14 = (bf16[256,1408]{1,0:T(8,128)(2,1)}, bf16[256,1408]{1,0:T(8,128)(2,1)}, u32[]{:S(2)}, u32[]{:S(2)}) collective-permute-start(bf16[256,1408]{1,0:T(8,128)(2,1)} %concatenate.194), channel_id=1, source_target_pairs={{0,1},{9,8},{2,3},{11,10},{4,5},{13,12},{6,7},{15,14},{16,17},{25,... | collective-permute-start | bytes 2162696 | tf_op jit(solution)/shard_map/ppermute | solution.py:189
  123.1 31.3 %collective-permute-start.13 = (bf16[2,1,256,1024]{3,2,0,1:T(8,128)(2,1)S(1)}, bf16[2,1,256,1024]{3,2,0,1:T(8,128)(2,1)}, u32[]{:S(2)}, u32[]{:S(2)}) collective-permute-start(bf16[2,1,256,1024]{3,2,0,1:T(8,128)(2,1)S(1)} %pad_maximum_fusion.19), channel_id=1, source_target_pairs={{0,1},{1,0},{2,3},{3,2},{4,5},{5,4},{6,7},{7,6},{8,9},{9,8},{10,11... | collective-permute-start | bytes 3145736 | tf_op jit(solution)/shard_map/ppermute | solution.py:20
  159.7 92.7 %collective-permute-start.23 = (bf16[2048,1024]{1,0:T(8,128)(2,1)}, bf16[2048,1024]{1,0:T(8,128)(2,1)}, u32[]{:S(2)}, u32[]{:S(2)}) collective-permute-start(bf16[2048,1024]{1,0:T(8,128)(2,1)} %bitcast.47), channel_id=1, source_target_pairs={{0,8},{8,0},{1,9},{9,1},{2,10},{10,2},{3,11},{11,3},{4,12},{12,4},... | collective-permute-start | bytes 12582920 | tf_op jit(solution)/shard_map/ppermute | solution.py:20
  183.6 388.4 %reduce-scatter.6.cloned.1.call-start = ((), (), s32[]{:S(2)}) async-start(), calls=%async_computation.6 | async-start | bytes 6488064 | tf_op jit(solution)/shard_map/reduce_scatter | solution.py:247
  198.3 33.6 %collective-permute-start.25 = (bf16[2,1,128,2048]{3,2,0,1:T(8,128)(2,1)S(1)}, bf16[2,1,128,2048]{3,2,0,1:T(8,128)(2,1)S(1)}, u32[]{:S(2)}, u32[]{:S(2)}) collective-permute-start(bf16[2,1,128,2048]{3,2,0,1:T(8,128)(2,1)S(1)} %pad_maximum_fusion.21), channel_id=1, source_target_pairs={{0,1},{1,0},{2,3},{3,2},{4,5},{5,4},{6,7},{7,6},{8,9},{9,8},{10,11... | collective-permute-start | bytes 3145736 | tf_op jit(solution)/shard_map/ppermute | solution.py:20
  333.1 238.9 %reduce-scatter.8.cloned.1.call-start = ((), (), s32[]{:S(2)}) async-start(), calls=%async_computation.7 | async-start | bytes 6488064 | tf_op jit(solution)/shard_map/reduce_scatter | solution.py:247
  380.8 281.3 %reduce-scatter.10.cloned.1.call-start = ((), (), s32[]{:S(2)}) async-start(), calls=%async_computation.8 | async-start | bytes 6488064 | tf_op jit(solution)/shard_map/reduce_scatter | solution.py:247
  393.0 359.6 %reduce-scatter.12.cloned.1.call-start = ((), (), s32[]{:S(2)}) async-start(), calls=%async_computation.9 | async-start | bytes 2359296 | tf_op jit(solution)/shard_map/reduce_scatter | solution.py:247
  410.3 81.3 %collective-permute-start.39 = (f32[4,16,512]{2,1,0:T(8,128)S(1)}, f32[4,16,512]{2,1,0:T(8,128)}, u32[]{:S(2)}, u32[]{:S(2)}) collective-permute-start(f32[4,16,512]{2,1,0:T(8,128)S(1)} %get-tuple-element.297), channel_id=1, source_target_pairs={{0,2},{2,4},{4,6},{1,3},{3,5},{5,7},{8,10},{10,12},{12,14},{9,11},... | collective-permute-start | bytes 393224 | tf_op jit(solution)/shard_map/ppermute | solution.py:26
  412.2 84.4 %collective-permute-start.40 = (f32[4,16,512]{2,1,0:T(8,128)S(1)}, f32[4,16,512]{2,1,0:T(8,128)}, u32[]{:S(2)}, u32[]{:S(2)}) collective-permute-start(f32[4,16,512]{2,1,0:T(8,128)S(1)} %get-tuple-element.297), channel_id=1, source_target_pairs={{0,4},{2,6},{1,5},{3,7},{8,12},{10,14},{9,13},{11,15},{16,20},{18,... | collective-permute-start | bytes 393224 | tf_op jit(solution)/shard_map/ppermute | solution.py:26
  456.5 47.2 %collective-permute-start.41 = (f32[4,16,512]{2,1,0:T(8,128)S(1)}, f32[4,16,512]{2,1,0:T(8,128)}, u32[]{:S(2)}, u32[]{:S(2)}) collective-permute-start(f32[4,16,512]{2,1,0:T(8,128)S(1)} %get-tuple-element.297), channel_id=1, source_target_pairs={{0,6},{1,7},{8,14},{9,15},{16,22},{17,23},{24,30},{25,31}} | collective-permute-start | bytes 393224 | tf_op jit(solution)/shard_map/ppermute | solution.py:26
  496.6 256.1 %reduce-scatter.14.cloned.1.call-start = ((), (), s32[]{:S(2)}) async-start(), calls=%async_computation.10 | async-start | bytes 4718592 | tf_op jit(solution)/shard_map/reduce_scatter | solution.py:247
  496.6 61.9 %collective-permute-start.48 = (bf16[2048,1024]{1,0:T(8,128)(2,1)}, bf16[2048,1024]{1,0:T(8,128)(2,1)}, u32[]{:S(2)}, u32[]{:S(2)}) collective-permute-start(bf16[2048,1024]{1,0:T(8,128)(2,1)} %convolution_convert_fusion.6), channel_id=1, source_target_pairs={{0,8},{8,0},{1,9},{9,1},{2,10},{10,2},{3,11},{11,3},{4,12},{12,4},... | collective-permute-start | bytes 12582920 | tf_op jit(solution)/shard_map/ppermute | solution.py:20
  534.3 41.8 %collective-permute-start.47 = (bf16[128,2048]{1,0:T(8,128)(2,1)}, bf16[128,2048]{1,0:T(8,128)(2,1)}, u32[]{:S(2)}, u32[]{:S(2)}) collective-permute-start(bf16[128,2048]{1,0:T(8,128)(2,1)} %get-tuple-element.626), channel_id=1, source_target_pairs={{0,1},{1,0},{2,3},{3,2},{4,5},{5,4},{6,7},{7,6},{8,9},{9,8},{10,11... | collective-permute-start | bytes 1572872 | tf_op jit(solution)/shard_map/ppermute | solution.py:20
  536.1 40.0 %collective-permute-start.46 = (bf16[128,2048]{1,0:T(8,128)(2,1)}, bf16[128,2048]{1,0:T(8,128)(2,1)}, u32[]{:S(2)}, u32[]{:S(2)}) collective-permute-start(bf16[128,2048]{1,0:T(8,128)(2,1)} %get-tuple-element.628), channel_id=1, source_target_pairs={{0,16},{16,0},{1,17},{17,1},{2,18},{18,2},{3,19},{19,3},{4,20},{20... | collective-permute-start | bytes 1572872 | tf_op jit(solution)/shard_map/ppermute | solution.py:20
  555.6 36.3 %collective-permute-start.50 = (bf16[2,128,2048]{2,1,0:T(8,128)(2,1)}, bf16[2,128,2048]{2,1,0:T(8,128)(2,1)}, u32[]{:S(2)}, u32[]{:S(2)}) collective-permute-start(bf16[2,128,2048]{2,1,0:T(8,128)(2,1)} %get-tuple-element.565), channel_id=1, source_target_pairs={{0,1},{1,0},{2,3},{3,2},{4,5},{5,4},{6,7},{7,6},{8,9},{9,8},{10,11... | collective-permute-start | bytes 3145736 | tf_op jit(solution)/shard_map/ppermute | solution.py:20
  558.1 33.7 %collective-permute-start.51 = (bf16[2,128,2048]{2,1,0:T(8,128)(2,1)}, bf16[2,128,2048]{2,1,0:T(8,128)(2,1)}, u32[]{:S(2)}, u32[]{:S(2)}) collective-permute-start(bf16[2,128,2048]{2,1,0:T(8,128)(2,1)} %bitcast.158), channel_id=1, source_target_pairs={{0,16},{16,0},{1,17},{17,1},{2,18},{18,2},{3,19},{19,3},{4,20},{20... | collective-permute-start | bytes 3145736 | tf_op jit(solution)/shard_map/ppermute | solution.py:20
  570.6 63.5 %collective-permute-start.58 = (bf16[2,256,1024]{2,1,0:T(8,128)(2,1)}, bf16[2,256,1024]{2,1,0:T(8,128)(2,1)}, u32[]{:S(2)}, u32[]{:S(2)}) collective-permute-start(bf16[2,256,1024]{2,1,0:T(8,128)(2,1)} %bitcast.163), channel_id=1, source_target_pairs={{0,16},{16,0},{1,17},{17,1},{2,18},{18,2},{3,19},{19,3},{4,20},{20... | collective-permute-start | bytes 3145736 | tf_op jit(solution)/shard_map/ppermute | solution.py:20
  576.0 58.1 %collective-permute-start.57 = (bf16[2,256,1024]{2,1,0:T(8,128)(2,1)}, bf16[2,256,1024]{2,1,0:T(8,128)(2,1)}, u32[]{:S(2)}, u32[]{:S(2)}) collective-permute-start(bf16[2,256,1024]{2,1,0:T(8,128)(2,1)} %get-tuple-element.563), channel_id=1, source_target_pairs={{0,1},{1,0},{2,3},{3,2},{4,5},{5,4},{6,7},{7,6},{8,9},{9,8},{10,11... | collective-permute-start | bytes 3145736 | tf_op jit(solution)/shard_map/ppermute | solution.py:20
  576.1 48.6 %collective-permute-start.54 = (bf16[256,2816]{1,0:T(8,128)(2,1)}, bf16[256,2816]{1,0:T(8,128)(2,1)}, u32[]{:S(2)}, u32[]{:S(2)}) collective-permute-start(bf16[256,2816]{1,0:T(8,128)(2,1)} %constant_dynamic-update-slice_fusion.20), channel_id=1, source_target_pairs={{8,1},{1,8},{10,3},{3,10},{12,5},{5,12},{14,7},{7,14},{24,17},{17,... | collective-permute-start | bytes 4325384 | tf_op jit(solution)/shard_map/ppermute | solution.py:272
  597.3 31.9 %collective-permute-start.53 = (bf16[128,2048]{1,0:T(8,128)(2,1)}, bf16[128,2048]{1,0:T(8,128)(2,1)}, u32[]{:S(2)}, u32[]{:S(2)}) collective-permute-start(bf16[128,2048]{1,0:T(8,128)(2,1)} %get-tuple-element.622), channel_id=1, source_target_pairs={{0,1},{1,0},{2,3},{3,2},{4,5},{5,4},{6,7},{7,6},{8,9},{9,8},{10,11... | collective-permute-start | bytes 1572872 | tf_op jit(solution)/shard_map/ppermute | solution.py:20
  597.3 31.9 %collective-permute-start.52 = (bf16[128,2048]{1,0:T(8,128)(2,1)}, bf16[128,2048]{1,0:T(8,128)(2,1)}, u32[]{:S(2)}, u32[]{:S(2)}) collective-permute-start(bf16[128,2048]{1,0:T(8,128)(2,1)} %get-tuple-element.624), channel_id=1, source_target_pairs={{0,16},{16,0},{1,17},{17,1},{2,18},{18,2},{3,19},{19,3},{4,20},{20... | collective-permute-start | bytes 1572872 | tf_op jit(solution)/shard_map/ppermute | solution.py:20
  666.3 41.7 %collective-permute-start.68 = (bf16[176,2048]{1,0:T(8,128)(2,1)}, bf16[176,2048]{1,0:T(8,128)(2,1)}, u32[]{:S(2)}, u32[]{:S(2)}) collective-permute-start(bf16[176,2048]{1,0:T(8,128)(2,1)} %reduce-scatter.10.cloned.1.call-done), channel_id=1, source_target_pairs={{0,16},{16,0},{1,17},{17,1},{2,18},{18,2},{3,19},{19,3},{4,20},{20... | collective-permute-start | bytes 2162696 | tf_op jit(solution)/shard_map/ppermute | solution.py:20
  (139 other events, 1850.5 us)
Sparse Core Ops, SparseCore 0:
  28.8 84.3 all-gather.9
  115.4 62.2 all-gather.7
  179.9 66.9 all-gather.13
  248.9 62.1 all-gather.11
  333.2 65.9 reduce-scatter.5
  401.9 72.4 reduce-scatter.7
  477.3 75.0 reduce-scatter.9
  554.7 29.0 reduce-scatter.11
  654.4 70.8 reduce-scatter.13

commit v5 on v4

--- a/solution.py
+++ b/solution.py
@@ -47,14 +47,17 @@
 
 
 class Line:
-    def __init__(self):
-        self.last = ()
+    def __init__(self, token):
+        self.token = token
 
     def run(self, work, *values):
-        values = lax.optimization_barrier((values, self.last))[0]
-        result = work(*values)
-        self.last = jax.tree.leaves(result)
+        values, token = lax.optimization_barrier((values, self.token))
+        result, self.token = lax.optimization_barrier((work(*values), token))
         return result
+
+    def finish(self, work, *values):
+        values, token = lax.optimization_barrier((values, self.token))
+        return work(token, *values)
 
 
 def moved(value, axis, sign):
@@ -286,10 +289,10 @@
     )
 
 
-def owner_ranks(slots):
+def owner_ranks(slots, core):
     spread, ccount, ycount = lax.axis_size("x"), lax.axis_size("c"), lax.axis_size("y")
     share = spread // ccount
-    core, yplace = lax.axis_index("c"), lax.axis_index("y")
+    yplace = lax.axis_index("y")
     flat = slots.reshape((-1,) + slots.shape[3:])
     ranks = []
     for i in range(spread):
@@ -366,30 +369,27 @@
     return ref[seq, pl.ds(at, tile, stride=0), :]
 
 
-def states_kernel(place_ref, signal_ref, decay_ref, state_ref, slope_ref, held):
+def states_kernel(place_ref, signal_ref, decay_ref, state_ref, held):
     fill(signal_ref, held, place_ref[0])
     seqs, length, lanes = held.shape
     keep = [jnp.exp(-d) for d in halves(decay_ref)]
     count = len(keep)
-    zero = jnp.zeros((tile, lanes), wide)
 
     def step(i, carry):
-        state, slope = [list(v) for v in carry]
+        state = list(carry)
         for k in range(tile):
             for n in range(seqs):
                 new = row_of(held, n, i * tile + k)
                 for h in range(count):
                     at = n * count + h
-                    slope[at] = keep[h] * (slope[at] + state[at])
                     state[at] = keep[h] * state[at] + new
-        return tuple(state), tuple(slope)
-
-    start = tuple(zero for _ in range(seqs * count))
-    state, slope = lax.fori_loop(0, length // tile, step, (start, start))
+        return tuple(state)
+
+    zero = jnp.zeros((tile, lanes), wide)
+    state = lax.fori_loop(0, length // tile, step, tuple(zero for _ in range(seqs * count)))
     for n in range(seqs):
         for h in range(count):
             state_ref[n, h * tile : (h + 1) * tile, :] = state[n * count + h]
-            slope_ref[n, h * tile : (h + 1) * tile, :] = slope[n * count + h]
 
 
 def forward_kernel(place_ref, signal_ref, decay_ref, residue_ref, start_ref, out_ref, held, terms, made):
@@ -456,7 +456,6 @@
     decay_ref,
     residue_ref,
     start_ref,
-    slope_ref,
     end_ref,
     out_ref,
     residue_grad_ref,
@@ -465,6 +464,7 @@
     grads,
     terms,
     made,
+    later,
 ):
     fill(signal_ref, held, place_ref[0])
     fill(grad_ref, grads, place_ref[0])
@@ -472,60 +472,66 @@
     keep = [jnp.exp(-d) for d in halves(decay_ref)]
     weigh = halves(residue_ref)
     count = len(keep)
+    group = later.shape[0]
     zero = jnp.zeros((tile, lanes), wide)
-
-    def ahead(i, carry):
-        state, slope, first, second = [list(v) for v in carry]
-        for k in range(tile):
-            for n in range(seqs):
-                new = row_of(held, n, i * tile + k)
-                back = row_of(grads, n, i * tile + k)
-                for h in range(count):
-                    at = n * count + h
-                    slope[at] = keep[h] * (slope[at] + state[at])
-                    state[at] = keep[h] * state[at] + new
-                    first[at] = first[at] + back * state[at]
-                    second[at] = second[at] + back * slope[at]
-        return tuple(state), tuple(slope), tuple(first), tuple(second)
-
-    def load(ref):
-        return tuple(
-            ref[n, h * tile : (h + 1) * tile, :] for n in range(seqs) for h in range(count)
-        )
-
-    none = tuple(zero for _ in range(seqs * count))
-    _, _, first, second = lax.fori_loop(
-        0, length // tile, ahead, (load(start_ref), load(slope_ref), none, none)
-    )
+    none = tuple(zero for _ in range(group * count))
+    sum_first = [zero] * count
+    sum_second = [zero] * count
+    for base_seq in range(0, seqs, group):
+
+        def load(ref):
+            return tuple(
+                ref[base_seq + n, h * tile : (h + 1) * tile, :]
+                for n in range(group)
+                for h in range(count)
+            )
+
+        def back_step(i, carry):
+            state, first = [list(v) for v in carry]
+            base = length - tile - i * tile
+            for k in range(tile - 1, -1, -1):
+                for n in range(group):
+                    back = row_of(grads, base_seq + n, base + k)
+                    new = row_of(held, base_seq + n, base + k)
+                    total = None
+                    for h in range(count):
+                        at = n * count + h
+                        state[at] = keep[h] * state[at] + back
+                        first[at] = first[at] + new * state[at]
+                        later[n, pl.ds(((base + k) * count + h) * tile, tile), :] = state[at]
+                        term = weigh[h] * state[at]
+                        total = term if total is None else total + term
+                    terms[n, k * tile : (k + 1) * tile, :] = total
+            for n in range(group):
+                result = terms[n, pl.ds(0, tile, stride=tile), :]
+                for p in range(1, tile):
+                    result = result + terms[n, pl.ds(p, tile, stride=tile), :]
+                made[base_seq + n, pl.ds(base, tile), :] = result
+            return tuple(state), tuple(first)
+
+        _, first = lax.fori_loop(0, length // tile, back_step, (load(end_ref), none))
+
+        def ahead(i, carry):
+            state, second = [list(v) for v in carry]
+            for k in range(tile):
+                for n in range(group):
+                    new = row_of(held, base_seq + n, i * tile + k)
+                    for h in range(count):
+                        at = n * count + h
+                        state[at] = keep[h] * state[at] + new
+                        other = later[n, pl.ds(((i * tile + k) * count + h) * tile, tile), :]
+                        second[at] = second[at] + state[at] * other
+            return tuple(state), tuple(second)
+
+        _, second = lax.fori_loop(0, length // tile, ahead, (load(start_ref), none))
+        for n in range(group):
+            for h in range(count):
+                at = n * count + h
+                sum_first[h] = sum_first[h] + first[at]
+                sum_second[h] = sum_second[h] + (second[at] - first[at])
     for h in range(count):
-        sum_first, sum_second = first[h], second[h]
-        for n in range(1, seqs):
-            sum_first = sum_first + first[n * count + h]
-            sum_second = sum_second + second[n * count + h]
-        residue_grad_ref[h * tile : (h + 1) * tile, :] = sum_first
-        decay_grad_ref[h * tile : (h + 1) * tile, :] = -weigh[h] * sum_second
-
-    def back_step(i, carry):
-        state = list(carry)
-        base = length - tile - i * tile
-        for k in range(tile - 1, -1, -1):
-            for n in range(seqs):
-                new = row_of(grads, n, base + k)
-                total = None
-                for h in range(count):
-                    at = n * count + h
-                    state[at] = keep[h] * state[at] + new
-                    term = weigh[h] * state[at]
-                    total = term if total is None else total + term
-                terms[n, k * tile : (k + 1) * tile, :] = total
-        for n in range(seqs):
-            result = terms[n, pl.ds(0, tile, stride=tile), :]
-            for p in range(1, tile):
-                result = result + terms[n, pl.ds(p, tile, stride=tile), :]
-            made[n, pl.ds(base, tile), :] = result
-        return tuple(state)
-
-    lax.fori_loop(0, length // tile, back_step, load(end_ref))
+        residue_grad_ref[h * tile : (h + 1) * tile, :] = sum_first[h]
+        decay_grad_ref[h * tile : (h + 1) * tile, :] = -weigh[h] * sum_second[h]
     empty(made, out_ref, place_ref[0])
 
 
@@ -548,7 +554,7 @@
             scratch_shapes=[pltpu.VMEM(s + (lanes,), wide) for s in scratch],
         ),
         compiler_params=pltpu.CompilerParams(
-            dimension_semantics=("arbitrary",), vmem_limit_bytes=48 << 20
+            dimension_semantics=("arbitrary",), vmem_limit_bytes=56 << 20
         ),
         cost_estimate=pl.CostEstimate(
             flops=flops, transcendentals=0, bytes_accessed=sum(a.size * 4 for a in arrays)
@@ -564,9 +570,7 @@
 def states_of(place, signal, decay):
     seqs, length, channels, work = sizes(signal, decay.shape[0])
     shape = jax.ShapeDtypeStruct((seqs, decay.shape[0], channels), wide)
-    return conv_call(
-        states_kernel, place, [signal, decay], [shape, shape], [(seqs, length)], 4 * work
-    )
+    return conv_call(states_kernel, place, [signal, decay], [shape], [(seqs, length)], 2 * work)[0]
 
 
 def forward_of(place, signal, decay, residue, start):
@@ -587,15 +591,23 @@
     return conv_call(later_kernel, place, [signal, decay], [shape], [(seqs, length)], 2 * work)[0]
 
 
-def backward_of(place, signal, grad, decay, residue, start, slope, end):
-    seqs, length, channels, work = sizes(signal, decay.shape[0])
+def backward_of(place, signal, grad, decay, residue, start, end):
+    poles = decay.shape[0]
+    seqs, length, channels, work = sizes(signal, poles)
     shape = jax.ShapeDtypeStruct(decay.shape, wide)
+    group = min(seqs, 4)
     return conv_call(
         backward_kernel,
         place,
-        [signal, grad, decay, residue, start, slope, end],
+        [signal, grad, decay, residue, start, end],
         [jax.ShapeDtypeStruct(signal.shape, low), shape, shape],
-        [(seqs, length), (seqs, length), (seqs, tile * tile), (seqs, length)],
+        [
+            (seqs, length),
+            (seqs, length),
+            (group, tile * tile),
+            (seqs, length),
+            (group, length * poles),
+        ],
         12 * work,
     )
 
@@ -648,7 +660,7 @@
     block = spread * local
 
     count = 3 * depth
-    line = Line()
+    line = Line(lax.axis_index("c"))
     run = line.run
 
     def stacked(value, got):
@@ -667,9 +679,9 @@
     first, second, scale_one = run(norm_one, tokens, norm_gain)
     normed_move = Gather(first, second)
     w_in = gather_tile(run(column_block, in_got))
+    held = run(lambda own, got: by_z([own] + got), block_out, out_got)
     normed_move.turn(line)
     w_down = gather_tile(run(row_block, down_weight))
-    held = run(lambda own, got: by_z([own] + got), block_out, out_got)
     out_move = Gather(held[:1], held[1:])
     gate_got = column_moves(run(lambda w: column_pieces(w, 1), gate_weight))
     normed_all = normed_move.end(line)
@@ -728,9 +740,9 @@
     def multiply(value, ends, before, weights, rates):
         keys, values = (short_of(value, ends, before, weights, g) for g in (1, 2))
         product = (keys * values).astype(low)
-        return (product,) + tuple(states_of(spot, product, rates))
-
-    product, state_end, slope_end = run(multiply, mixed, tail, behind, taps, decay)
+        return product, states_of(spot, product, rates)
+
+    product, state_end = run(multiply, mixed, tail, behind, taps, decay)
     states = [passed(state_end, "z", k) for k in range(1, depth)]
     feed_move.turn(line)
 
@@ -774,7 +786,6 @@
     two_move = Gather(first, second)
     grad_active = run(dot_t, grad_feed_all, w_down)
     two_move.turn(line)
-    slopes = [passed(slope_end, "z", k) for k in range(1, depth)]
     normed_two_all = two_move.end(line)
 
     def open_gate(v, w, back):
@@ -813,16 +824,16 @@
         result = result + back.astype(wide) * mask
         parts = core_halves(result.astype(low).reshape(-1, width))
         own = sum(dot_t(m, w) for m, w in zip(parts, weights)).astype(low)
-        slots = own.reshape(-1, 2, ycount, spread, half)
-        return (
-            result,
-            grad_gain,
-            parts,
-            [
-                [slots[:, :, k, i].reshape(-1, channels) for i in range(spread)]
-                for k in range(ycount)
-            ],
-        )
+        ranks = ycount * spread
+
+        def slot(at):
+            pieces = [
+                own[:, (h * ranks + at) * half : (h * ranks + at + 1) * half] for h in range(2)
+            ]
+            return jnp.concatenate(pieces, axis=1)
+
+        slots = [[slot(k * spread + i) for i in range(spread)] for k in range(ycount)]
+        return result, grad_gain, parts, slots
 
     grad_middle, grad_feed_gain, mix_parts, grad_slots = run(
         middle_back, two_back.rest(), middle, scale_two, feed_gain, cotangent, w_out
@@ -864,18 +875,19 @@
         result = short_back(grad, head, ahead, weights[:, :channels])
         return result, dot_w(v, result)
 
+    up_parts_got = owner_moves(run(owner_parts, up_mine))
     grad_mixed_query, query_term = run(
         query_back, grad_query, query_head, query_ahead, taps, normed_all
     )
     query_mine = scatter_tile(query_term)
 
-    def conv_back(signal, grad, rates, amounts, begin, parts, ended, ends_later, value, ends, before, weights):
-        slope = parts[0]
-        for k in range(1, depth - 1):
-            slope = slope + jnp.exp(-rates * (k * block)) * (parts[k] + (k * block) * ended[k])
+    up_held = run(owner_held, up_parts_got)
+    up_got = moved(up_held, "y", -1)
+
+    def conv_back(signal, grad, rates, amounts, begin, ends_later, value, ends, before, weights):
         later = combine(ends_later, rates)
         grad_product, grad_residue, grad_decay = backward_of(
-            spot, signal, grad, rates, amounts, begin, slope, later
+            spot, signal, grad, rates, amounts, begin, later
         )
         grad_product = grad_product.astype(wide)
         keys, values = (short_of(value, ends, before, weights, g) for g in (1, 2))
@@ -889,8 +901,6 @@
         decay,
         residue,
         start,
-        slopes,
-        states,
         laters,
         mixed,
         tail,
@@ -899,6 +909,8 @@
     )
     pair_ahead = passed(pair_head, "z", -1)
     feed_back.turn(line)
+    up_held = run(stacked, up_held, up_got)
+    up_got = moved(up_held, "c", -1)
 
     def pair_back(grad, head, ahead, weights, v):
         result = short_back(grad, head, ahead, weights[:, channels:])
@@ -917,11 +929,6 @@
         )
     )
 
-    out_back_parts = run(
-        lambda own, got: split_sum(add_up([own], got)), out_terms[0], out_terms_got
-    )
-    parts = run(lambda a, b: owner_parts(jnp.concatenate([a, b], axis=1)), up_mine, gate_mine)
-    both_got = owner_moves(parts)
     output = run(
         lambda rest, values: (
             mask * (values + Scatter.sum(*rest).reshape(batch, local, width))
@@ -929,7 +936,16 @@
         feed_back.rest(),
         middle,
     )
+    out_back_parts = run(
+        lambda own, got: split_sum(add_up([own], got)), out_terms[0], out_terms_got
+    )
+
+    def column_whole(own, got):
+        return owner_whole(owner_ranks(jnp.stack([own] + got), lax.axis_index("c")), depth)
+
+    grad_up_weight = run(column_whole, up_held, up_got)
     one_back.turn(line)
+    gate_got = owner_moves(run(owner_parts, gate_mine))
     out_back = Scatter(out_back_parts)
 
     def tap_sums(query, pair, value, ends, before):
@@ -943,8 +959,6 @@
         return jnp.stack(sums)
 
     grad_taps = run(tap_sums, grad_query, grad_pair, mixed, tail, behind)
-    both_held = run(owner_held, both_got)
-    both_got = moved(both_held, "y", -1)
 
     def tokens_back(rest, values, scale, gain, back, small):
         values = values.astype(wide)
@@ -963,42 +977,38 @@
         (grad_feed_gain, grad_residue, grad_decay, grad_taps),
     )
     small_got = moved(small, "c", 1)
+    gate_held = run(owner_held, gate_got)
+    gate_got = moved(gate_held, "y", -1)
     out_back.turn(line)
-    both_held = run(stacked, both_held, both_got)
-    both_got = moved(both_held, "c", -1)
     small = run(lambda v, got: v + sum(got), small, small_got)
     small_got = moved(small, "z", 1)
-    down_got = moved(run(lambda v: v + 0, down_mine), "y", -1)
+    gate_held = run(stacked, gate_held, gate_got)
+    gate_got = moved(gate_held, "c", -1)
     out_slots = run(
         lambda rest: z_slots(Scatter.sum(*rest).reshape(channels, -1)), out_back.rest()
     )
     out_got = [turned(p, "z", d + 1) for d, p in enumerate(out_slots[1:])]
     small = run(lambda v, got: v + sum(got), small, small_got)
     small_got = moved(small, "x", -1)
-
-    def both_whole(own, got):
-        ranks = owner_ranks(jnp.stack([own] + got))
-        middle_at = ranks[0].shape[1] // 2
-        return (
-            owner_whole([r[:, :middle_at] for r in ranks], depth),
-            owner_whole([r[:, middle_at:] for r in ranks], depth),
-        )
-
-    grad_up_weight, grad_gate_weight = run(both_whole, both_held, both_got)
-    down_held = run(stacked, down_mine, down_got)
-    down_got = moved(down_held, "c", -1)
+    down_held = run(lambda v: v.reshape(1, -1, width), down_mine)
+    down_got = moved(down_held, "y", -1)
+    parts = run(
+        lambda a, b: owner_parts(jnp.concatenate([a, b], axis=1)), query_mine, pair_mine
+    )
+    in_got = owner_moves(parts)
+    grad_gate_weight = run(column_whole, gate_held, gate_got)
     out_held = run(lambda own, got: add_up([own], got).astype(low), out_slots[0], out_got)
     out_got = moved(out_held, "y", -1)
+    in_held = run(owner_held, in_got)
+    in_got = moved(in_held, "y", -1)
     small = run(stacked, small, small_got)
     small_got = moved(small, "y", -1)
-
-    def down_whole(own, got):
-        whole = in_order(jnp.swapaxes(in_order(jnp.stack([own] + got), "c"), 0, 1), "y")
-        return whole.reshape(-1, width).astype(wide)
-
-    grad_down = run(down_whole, down_held, down_got)
+    down_held = run(lambda own, got: jnp.concatenate([own] + got), down_held, down_got)
+    down_got = moved(down_held, "c", -1)
     out_held = run(stacked, out_held, out_got)
     out_got = moved(out_held, "c", -1)
+    in_held = run(stacked, in_held, in_got)
+    in_got = moved(in_held, "c", -1)
     poles = decay.shape[0]
 
     def small_whole(own, got):
@@ -1014,10 +1024,12 @@
     grad_norm_gain, feed_gain_sum, grad_conv_taps, residue_sum, decay_sum = run(
         small_whole, small, small_got
     )
-    parts = run(
-        lambda a, b: owner_parts(jnp.concatenate([a, b], axis=1)), query_mine, pair_mine
-    )
-    in_got = owner_moves(parts)
+
+    def down_whole(own, got):
+        whole = in_order(jnp.swapaxes(in_order(jnp.stack([own] + got), "c"), 0, 1), "y")
+        return whole.reshape(-1, width).astype(wide)
+
+    grad_down = run(down_whole, down_held, down_got)
 
     def out_whole(own, got):
         whole = in_order(jnp.stack([own] + got), "c")
@@ -1026,12 +1038,10 @@
         return jnp.swapaxes(whole, 1, 2).reshape(ys * rows, cs * columns).astype(wide)
 
     grad_out_weight = run(out_whole, out_held, out_got)
-    in_held = run(owner_held, in_got)
-    in_held = run(stacked, in_held, moved(in_held, "y", -1))
-    grad_in_weight = run(
-        lambda own, got: owner_whole(owner_ranks(jnp.stack([own] + got)), count),
+    grad_in_weight = line.finish(
+        lambda core, own, got: owner_whole(owner_ranks(jnp.stack([own] + got), core), count),
         in_held,
-        moved(in_held, "c", -1),
+        in_got,
     )
     return (
         output,

time: 806 us -> 801 us (level)
  local copies, waits for them, and re-layouts: 114 us -> 92.7 us
  other arithmetic: 120 us -> 141 us
  waiting for transfers between devices: 256 us -> 239 us
  matrix products: 146 us -> 159 us
    ppermute x2 -> x3, waiting for transfers between devices: 26.6 us -> 1.55 us  [owner_moves(): got.append(lax.ppermute(parts[d], ('c', 'x'), pairs))]
    ppermute x3, waiting for transfers between devices: 7.15 us -> 21.3 us  [column_moves(): got.append(lax.ppermute(pieces[d], ('c', 'x'), pairs))]
    ppermute x54 -> x56, waiting for transfers between devices: 199 us -> 186 us  [turned(): lax.ppermute(value, axis, [(i, (i + by) % length) for i in range(length)])]
    unnamed x247 -> x203, local copies, waits for them, and re-layouts: 33.8 us -> 22.1 us
    dot_general x6, matrix products: 55.1 us -> 66 us  [dot(): return jnp.dot(a, b, preferred_element_type=wide).astype(kind)]
    ppermute x12 -> x9, starting transfers between devices: 27.7 us -> 21.3 us  [passed(): return lax.ppermute(value, axis, pairs)]
    ppermute x54 -> x56, starting transfers between devices: 54.9 us -> 59.9 us  [turned(): lax.ppermute(value, axis, [(i, (i + by) % length) for i in range(length)])]
    ppermute x12 -> x9, waiting for transfers between devices: 20.3 us -> 22.3 us  [passed(): return lax.ppermute(value, axis, pairs)]
  transfers between devices with their start and end apart: 86 -> 86, of which waited for: 30 -> 37; matrix products, arithmetic and copies ran while one was open for 44% -> 46% of each run, Pallas kernels for 4% -> 4%
where the time goes in v5:
time: 801 us; the launch traced here: 789 us
  waiting for transfers between devices  239 us (30%)
  matrix products  159 us (20%)
  other arithmetic  141 us (18%)
  starting transfers between devices  102 us (13%)
  local copies, waits for them, and re-layouts  92.7 us (12%)
  Pallas kernels  38.7 us (5%)
  between operations  16.5 us (2%)
    ppermute x56, waiting for transfers between devices, turned(): lax.ppermute(value, axis, [(i, (i + by) % length) for i in range(length)])  186 us
    dot_general x6, matrix products, dot(): return jnp.dot(a, b, preferred_element_type=wide).astype(kind)  66 us
    ppermute x56, starting transfers between devices, turned(): lax.ppermute(value, axis, [(i, (i + by) % length) for i in range(length)])  59.9 us
    dot_general x7, matrix products, dot_w(): lax.dot_general(a, b, (((0,), (0,)), ((), ())), preferred_element_type=wide)  47.1 us
    dot_general x6, matrix products, dot_t(): lax.dot_general(a, b, (((1,), (1,)), ((), ())), preferred_element_type=wide)  46.3 us
    pallas_call x4, Pallas kernels, conv_call(): pl.pallas_call(kernel, out_shape=results, grid_spec=pltpu.PrefetchScalarG...  35.3 us
    ppermute x9, waiting for transfers between devices, passed(): return lax.ppermute(value, axis, pairs)  22.3 us
    unnamed x203, local copies, waits for them, and re-layouts  22.1 us
  transfers between devices with their start and end apart: 86, of which 37 were waited for; matrix products, arithmetic and copies ran while one was open for 46% of the time, Pallas kernels for 4%

profile of v5, /device:TPU:9, one launch (start us, length us, event | category | flops | bytes accessed | tf_op | source)
XLA Modules:
  0.0 789.4 jit_solution(16716976756320296295)
XLA Ops:
  19.1 7.2 collective-permute-done.5
  36.1 20.1 %collective-permute-done.3 = bf16[128,1024]{1,0:T(8,128)(2,1)} collective-permute-done((bf16[128,1024]{1,0:T(8,128)(2,1)}, bf16[128,1024]{1,0:T(8,128)(2,1)}, u32[]{:S(2)}, u32[]{:S(2)}) %collective-permute-start.3) | collective-permute-done | bytes 262176 | tf_op jit(solution)/shard_map/ppermute | solution.py:20
  56.1 19.2 %collective-permute-done.4 = bf16[128,1024]{1,0:T(8,128)(2,1)} collective-permute-done((bf16[128,1024]{1,0:T(8,128)(2,1)}, bf16[128,1024]{1,0:T(8,128)(2,1)}, u32[]{:S(2)}, u32[]{:S(2)}) %collective-permute-start.4) | collective-permute-done | bytes 262176 | tf_op jit(solution)/shard_map/ppermute | solution.py:20
  93.3 7.2 collective-permute-done.6
  113.9 14.1 %collective-permute-done.8 = bf16[256,1408]{1,0:T(8,128)(2,1)S(1)} collective-permute-done((bf16[256,1408]{1,0:T(8,128)(2,1)}, bf16[256,1408]{1,0:T(8,128)(2,1)S(1)}, u32[]{:S(2)}, u32[]{:S(2)}) %collective-permute-start.8) | collective-permute-done | bytes 720928 | tf_op jit(solution)/shard_map/ppermute | solution.py:192
  140.6 10.0 %convolution_convert_fusion.4 = bf16[1024,1536]{1,0:T(8,128)(2,1)S(1)} fusion(bf16[1024,2048]{1,0:T(8,128)(2,1)} %bitcast.424, bf16[2048,1536]{1,0:T(8,128)(2,1)} %all-gather.5.cloned.1.call-done), kind=kOutput, calls=%fused_computation.25 | convolution fusion | flops 6444023808 | bytes 13631488 | tf_op jit(solution)/shard_map/dot_general | solution.py:629
  158.9 11.9 %collective-permute-done.13 = bf16[2,1,256,1024]{3,2,0,1:T(8,128)(2,1)} collective-permute-done((bf16[2,1,256,1024]{3,2,0,1:T(8,128)(2,1)S(1)}, bf16[2,1,256,1024]{3,2,0,1:T(8,128)(2,1)}, u32[]{:S(2)}, u32[]{:S(2)}) %collective-permute-start.13) | collective-permute-done | bytes 1048608 | tf_op jit(solution)/shard_map/ppermute | solution.py:20
  170.8 7.8 collective-permute-start.11
  207.4 16.9 %collective-permute-done.16 = f32[4,16,512]{2,1,0:T(8,128)S(1)} collective-permute-done((f32[4,16,512]{2,1,0:T(8,128)}, f32[4,16,512]{2,1,0:T(8,128)S(1)}, u32[]{:S(2)}, u32[]{:S(2)}) %collective-permute-start.16) | collective-permute-done | bytes 131104 | tf_op jit(solution)/shard_map/ppermute | solution.py:26
  228.1 8.8 %shard_map.222 = bf16[4,2,1,128,512]{4,3,2,1,0:T(8,128)(2,1)} custom-call(s32[1]{0:T(128)} %bitcast.58.place_ref, bf16[4,2,1,128,512]{4,3,2,1,0:T(8,128)(2,1)} %fusion.51.signal_ref, f32[16,512]{1,0:T(8,128)} %maximum_bitcast_fusion.9.decay_ref, f32[16,512]{1,0:T(8,128)} %maximum_bitcast_fusion.10.residue_ref, f32[4,16,512]{2,1,0:T(8,128)} %multiply_add_fusion.2.start_ref), custom_call_target="tpu_custom_call" | custom-call | flops 33554432 | bytes 2293760 | tf_op jit(solution)/shard_map/pallas_call | solution.py:546
  240.6 8.0 %collective-permute-done.24 = bf16[2,1,128,2048]{3,2,0,1:T(8,128)(2,1)S(1)} collective-permute-done((bf16[2,1,128,2048]{3,2,0,1:T(8,128)(2,1)S(1)}, bf16[2,1,128,2048]{3,2,0,1:T(8,128)(2,1)S(1)}, u32[]{:S(2)}, u32[]{:S(2)}) %collective-permute-start.24) | collective-permute-done | bytes 1048608 | tf_op jit(solution)/shard_map/ppermute | solution.py:20
  272.8 11.9 %fusion.129 = f32[1024,1408]{1,0:T(8,128)} fusion(bf16[1024,2048]{1,0:T(8,128)(2,1)} %bitcast.427, bf16[1408,2048]{1,0:T(8,128)(2,1)} %all-gather.7.cloned.1.call-done), kind=kOutput, calls=%fused_computation.501 | convolution fusion | flops 5905580032 | bytes 15728640 | tf_op jit(solution)/shard_map/dot_general | solution.py:633
  286.2 21.8 %collective-permute-done.28 = bf16[2,1,128,2048]{3,2,0,1:T(8,128)(2,1)S(1)} collective-permute-done((bf16[2,1,128,2048]{3,2,0,1:T(8,128)(2,1)S(1)}, bf16[2,1,128,2048]{3,2,0,1:T(8,128)(2,1)S(1)}, u32[]{:S(2)}, u32[]{:S(2)}) %collective-permute-start.28) | collective-permute-done | bytes 1048608 | tf_op jit(solution)/shard_map/ppermute | solution.py:20
  311.1 24.7 %multiply_convert_fusion.2 = (bf16[1024,1408]{1,0:T(8,128)(2,1)S(1)}, f32[1024,1408]{1,0:T(8,128)}) fusion(f32[1024,1408]{1,0:T(8,128)} %fusion.129, bf16[1024,2048]{1,0:T(8,128)(2,1)} %bitcast.429, bf16[2048,1408]{1,0:T(8,128)(2,1)} %all-gather.11.cloned.1.call-done), kind=kOutput, calls=%fused_computation.8 | convolution fusion | flops 5914230784 | bytes 24379392 | tf_op jit(solution)/shard_map/dot_general | solution.py:629
  337.4 8.7 %convolution_convert_fusion.2 = bf16[2048,1408]{1,0:T(8,128)(2,1)} fusion(bf16[1024,2048]{1,0:T(8,128)(2,1)S(1)} %bitcast.431, bf16[1024,1408]{1,0:T(8,128)(2,1)S(1)} %get-tuple-element.732), kind=kOutput, calls=%fused_computation.4 | convolution fusion | flops 5908463616 | bytes 12845056 | tf_op jit(solution)/shard_map/dot_general | solution.py:637
  346.2 15.0 %multiply_convert_fusion = (bf16[1024,1408]{1,0:T(8,128)(2,1)S(1)}, bf16[1024,1408]{1,0:T(8,128)(2,1)}) fusion(f32[1024,1408]{1,0:T(8,128)} %get-tuple-element.722, f32[1024,1408]{1,0:T(8,128)} %fusion.129, bf16[1024,2048]{1,0:T(8,128)(2,1)} %bitcast.430, bf16[2048,1408]{1,0:T(8,128)(2,1)} %all-gather.9.cloned.1.call-done), kind=kOutput, calls=%fused_computation.5 | convolution fusion | flops 5924323328 | bytes 27262976 | tf_op jit(solution)/shard_map/dot_general | solution.py:629
  362.8 8.9 %fusion.130 = f32[1024,2048]{1,0:T(8,128)S(1)} fusion(bf16[1024,1408]{1,0:T(8,128)(2,1)S(1)} %get-tuple-element.741, bf16[2048,1408]{1,0:T(8,128)(2,1)} %all-gather.11.cloned.1.call-done), kind=kOutput, calls=%fused_computation.502 | convolution fusion | flops 5905580032 | bytes 17039360 | tf_op jit(solution)/shard_map/dot_general | solution.py:633
  371.7 8.4 %add_convert_fusion = bf16[1024,2048]{1,0:T(8,128)(2,1)S(1)} fusion(f32[1024,2048]{1,0:T(8,128)S(1)} %fusion.130, bf16[1024,1408]{1,0:T(8,128)(2,1)} %copy-done.66, bf16[2048,1408]{1,0:T(8,128)(2,1)S(1)} %copy-done.62), kind=kOutput, calls=%fused_computation.1 | convolution fusion | flops 5909774336 | bytes 21233664 | tf_op jit(solution)/shard_map/dot_general | solution.py:633
  385.1 8.7 %convolution_convert_fusion.1 = bf16[2048,1408]{1,0:T(8,128)(2,1)} fusion(bf16[1024,2048]{1,0:T(8,128)(2,1)S(1)} %bitcast.432, bf16[1024,1408]{1,0:T(8,128)(2,1)S(1)} %copy-done.65), kind=kOutput, calls=%fused_computation.3 | convolution fusion | flops 5908463616 | bytes 12845056 | tf_op jit(solution)/shard_map/dot_general | solution.py:637
  396.0 10.9 %convolution_convert_fusion = bf16[1408,2048]{1,0:T(8,128)(2,1)} fusion(bf16[1024,1408]{1,0:T(8,128)(2,1)} %get-tuple-element.797, bf16[1024,2048]{1,0:T(8,128)(2,1)} %bitcast.428), kind=kOutput, calls=%fused_computation.2 | convolution fusion | flops 5908463616 | bytes 12845056 | tf_op jit(solution)/shard_map/dot_general | solution.py:637
  407.0 9.1 %collective-permute-done.30 = bf16[2,128,2048]{2,1,0:T(8,128)(2,1)} collective-permute-done((bf16[2,128,2048]{2,1,0:T(8,128)(2,1)}, bf16[2,128,2048]{2,1,0:T(8,128)(2,1)}, u32[]{:S(2)}, u32[]{:S(2)}) %collective-permute-start.30) | collective-permute-done | bytes 1048608 | tf_op jit(solution)/shard_map/ppermute | solution.py:20
  423.7 7.9 collective-permute-done.32
  454.6 6.3 collective-permute-start.51
  475.2 8.7 %convolution_convert_fusion.5 = bf16[1024,2048]{1,0:T(8,128)(2,1)S(1)} fusion(bf16[1024,1408]{1,0:T(8,128)(2,1)S(1)} %copy-done.63, bf16[1408,2048]{1,0:T(8,128)(2,1)} %all-gather.7.cloned.1.call-done), kind=kOutput, calls=%fused_computation.26 | convolution fusion | flops 5907677184 | bytes 12845056 | tf_op jit(solution)/shard_map/dot_general | solution.py:629
  498.7 6.0 convolution_convert_fusion.9
  511.6 16.8 %shard_map.224 = (bf16[4,2,1,128,512]{4,3,2,1,0:T(8,128)(2,1)}, f32[16,512]{1,0:T(8,128)}, f32[16,512]{1,0:T(8,128)}) custom-call(s32[1]{0:T(128)} %bitcast.58.place_ref, bf16[4,2,1,128,512]{4,3,2,1,0:T(8,128)(2,1)} %fusion.51.signal_ref, bf16[4,2,1,128,512]{4,3,2,1,0:T(8,128)(2,1)} %get-tuple-element.828.signal_ref.grad_ref, ...), custom_call_target="tpu_custom_call" | custom-call | flops 100663296 | bytes 4521984 | tf_op jit(solution)/shard_map/pallas_call | solution.py:546
  543.6 5.9 collective-permute-done.47
  553.9 6.3 convolution_convert_fusion.8
  560.2 10.0 %convolution_convert_fusion.3 = bf16[1024,2048]{1,0:T(8,128)(2,1)S(1)} fusion(bf16[2048,1536]{1,0:T(8,128)(2,1)} %all-gather.5.cloned.1.call-done, bf16[1024,1024]{1,0:T(8,128)(2,1)} %bitcast.458, bf16[1024,512]{1,0:T(8,128)(2,1)} %bitcast.472), kind=kOutput, calls=%fused_computation.24 | convolution fusion | flops 6450839552 | bytes 13631488 | tf_op jit(solution)/shard_map/dot_general | solution.py:633
  631.0 18.1 %collective-permute-done.52 = bf16[128,2048]{1,0:T(8,128)(2,1)} collective-permute-done((bf16[128,2048]{1,0:T(8,128)(2,1)}, bf16[128,2048]{1,0:T(8,128)(2,1)}, u32[]{:S(2)}, u32[]{:S(2)}) %collective-permute-start.52) | collective-permute-done | bytes 524320 | tf_op jit(solution)/shard_map/ppermute | solution.py:20
  675.1 8.2 %collective-permute-done.63 = bf16[1,256,1408]{2,1,0:T(8,128)(2,1)S(1)} collective-permute-done((bf16[1,256,1408]{2,1,0:T(8,128)(2,1)S(1)}, bf16[1,256,1408]{2,1,0:T(8,128)(2,1)S(1)}, u32[]{:S(2)}, u32[]{:S(2)}) %collective-permute-start.63) | collective-permute-done | bytes 720928 | tf_op jit(solution)/shard_map/ppermute | solution.py:20
  733.1 17.5 %collective-permute-done.72 = bf16[128,1024]{1,0:T(8,128)(2,1)S(1)} collective-permute-done((bf16[128,1024]{1,0:T(8,128)(2,1)S(1)}, bf16[128,1024]{1,0:T(8,128)(2,1)S(1)}, u32[]{:S(2)}, u32[]{:S(2)}) %collective-permute-start.72) | collective-permute-done | bytes 262176 | tf_op jit(solution)/shard_map/ppermute | solution.py:20
  (600 shorter events, 401.8 us)
Async XLA Ops:
  7.2 133.4 %all-gather.5.cloned.1.call-start = ((), (), s32[]{:S(2)}) async-start(), calls=%async_computation.5 | async-start | bytes 7077888 | tf_op jit(solution)/shard_map/all_gather | solution.py:246
  28.7 242.1 %all-gather.7.cloned.1.call-start = ((), (), s32[]{:S(2)}) async-start(), calls=%async_computation.6 | async-start | bytes 6488064 | tf_op jit(solution)/shard_map/all_gather | solution.py:246
  28.8 27.3 %collective-permute-start.3 = (bf16[128,1024]{1,0:T(8,128)(2,1)}, bf16[128,1024]{1,0:T(8,128)(2,1)}, u32[]{:S(2)}, u32[]{:S(2)}) collective-permute-start(bf16[128,1024]{1,0:T(8,128)(2,1)} %dynamic_slice.254), channel_id=1, source_target_pairs={{0,4},{2,6},{4,0},{6,2},{1,5},{3,7},{5,1},{7,3},{8,12},{10,14},{12... | collective-permute-start | bytes 786440 | tf_op jit(solution)/shard_map/ppermute | solution.py:20
  31.3 44.1 %collective-permute-start.4 = (bf16[128,1024]{1,0:T(8,128)(2,1)}, bf16[128,1024]{1,0:T(8,128)(2,1)}, u32[]{:S(2)}, u32[]{:S(2)}) collective-permute-start(bf16[128,1024]{1,0:T(8,128)(2,1)} %dynamic_slice.254), channel_id=1, source_target_pairs={{0,2},{2,4},{4,6},{6,0},{1,3},{3,5},{5,7},{7,1},{8,10},{10,12},{12... | collective-permute-start | bytes 786440 | tf_op jit(solution)/shard_map/ppermute | solution.py:20
  33.5 44.4 %collective-permute-start = (bf16[1,128,2048]{2,1,0:T(8,128)(2,1)S(1)}, bf16[1,128,2048]{2,1,0:T(8,128)(2,1)}, u32[]{:S(2)}, u32[]{:S(2)}) collective-permute-start(bf16[1,128,2048]{2,1,0:T(8,128)(2,1)S(1)} %get-tuple-element.564), channel_id=1, source_target_pairs={{0,1},{1,0},{2,3},{3,2},{4,5},{5,4},{6,7},{7,6},{8,9},{9,8},{10,11... | collective-permute-start | bytes 1572872 | tf_op jit(solution)/shard_map/ppermute | solution.py:20
  33.5 44.4 %collective-permute-start.1 = (bf16[1,128,2048]{2,1,0:T(8,128)(2,1)}, bf16[1,128,2048]{2,1,0:T(8,128)(2,1)}, u32[]{:S(2)}, u32[]{:S(2)}) collective-permute-start(bf16[1,128,2048]{2,1,0:T(8,128)(2,1)} %get-tuple-element.566), channel_id=1, source_target_pairs={{0,16},{16,0},{1,17},{17,1},{2,18},{18,2},{3,19},{19,3},{4,20},{20... | collective-permute-start | bytes 1572872 | tf_op jit(solution)/shard_map/ppermute | solution.py:20
  83.1 228.0 %all-gather.11.cloned.1.call-start = ((), (), s32[]{:S(2)}) async-start(), calls=%async_computation.8 | async-start | bytes 6488064 | tf_op jit(solution)/shard_map/all_gather | solution.py:246
  92.0 36.0 %collective-permute-start.8 = (bf16[256,1408]{1,0:T(8,128)(2,1)}, bf16[256,1408]{1,0:T(8,128)(2,1)S(1)}, u32[]{:S(2)}, u32[]{:S(2)}) collective-permute-start(bf16[256,1408]{1,0:T(8,128)(2,1)} %concatenate.202), channel_id=1, source_target_pairs={{0,1},{9,8},{2,3},{11,10},{4,5},{13,12},{6,7},{15,14},{16,17},{25,... | collective-permute-start | bytes 2162696 | tf_op jit(solution)/shard_map/ppermute | solution.py:192
  129.2 217.0 %all-gather.9.cloned.1.call-start = ((), (), s32[]{:S(2)}) async-start(), calls=%async_computation.7 | async-start | bytes 6488064 | tf_op jit(solution)/shard_map/all_gather | solution.py:246
  137.7 33.1 %collective-permute-start.13 = (bf16[2,1,256,1024]{3,2,0,1:T(8,128)(2,1)S(1)}, bf16[2,1,256,1024]{3,2,0,1:T(8,128)(2,1)}, u32[]{:S(2)}, u32[]{:S(2)}) collective-permute-start(bf16[2,1,256,1024]{3,2,0,1:T(8,128)(2,1)S(1)} %pad_maximum_fusion.22), channel_id=1, source_target_pairs={{0,1},{1,0},{2,3},{3,2},{4,5},{5,4},{6,7},{7,6},{8,9},{9,8},{10,11... | collective-permute-start | bytes 3145736 | tf_op jit(solution)/shard_map/ppermute | solution.py:20
  184.9 76.0 %collective-permute-start.23 = (bf16[2048,1024]{1,0:T(8,128)(2,1)}, bf16[2048,1024]{1,0:T(8,128)(2,1)}, u32[]{:S(2)}, u32[]{:S(2)}) collective-permute-start(bf16[2048,1024]{1,0:T(8,128)(2,1)} %bitcast.51), channel_id=1, source_target_pairs={{0,8},{8,0},{1,9},{9,1},{2,10},{10,2},{3,11},{11,3},{4,12},{12,4},... | collective-permute-start | bytes 12582920 | tf_op jit(solution)/shard_map/ppermute | solution.py:20
  187.1 301.9 %reduce-scatter.6.cloned.1.call-start = ((), (), s32[]{:S(2)}) async-start(), calls=%async_computation.9 | async-start | bytes 6488064 | tf_op jit(solution)/shard_map/reduce_scatter | solution.py:250
  199.0 25.3 %collective-permute-start.16 = (f32[4,16,512]{2,1,0:T(8,128)}, f32[4,16,512]{2,1,0:T(8,128)S(1)}, u32[]{:S(2)}, u32[]{:S(2)}) collective-permute-start(f32[4,16,512]{2,1,0:T(8,128)} %shard_map.221), channel_id=1, source_target_pairs={{0,4},{2,6},{1,5},{3,7},{8,12},{10,14},{9,13},{11,15},{16,20},{18,... | collective-permute-start | bytes 393224 | tf_op jit(solution)/shard_map/ppermute | solution.py:26
  224.3 24.3 %collective-permute-start.24 = (bf16[2,1,128,2048]{3,2,0,1:T(8,128)(2,1)S(1)}, bf16[2,1,128,2048]{3,2,0,1:T(8,128)(2,1)S(1)}, u32[]{:S(2)}, u32[]{:S(2)}) collective-permute-start(bf16[2,1,128,2048]{3,2,0,1:T(8,128)(2,1)S(1)} %bitcast.445), channel_id=1, source_target_pairs={{0,16},{16,0},{1,17},{17,1},{2,18},{18,2},{3,19},{19,3},{4,20},{20... | collective-permute-start | bytes 3145736 | tf_op jit(solution)/shard_map/ppermute | solution.py:20
  346.1 276.2 %reduce-scatter.8.cloned.1.call-start = ((), (), s32[]{:S(2)}) async-start(), calls=%async_computation.10 | async-start | bytes 6488064 | tf_op jit(solution)/shard_map/reduce_scatter | solution.py:250
  393.8 303.5 %reduce-scatter.14.cloned.1.call-start = ((), (), s32[]{:S(2)}) async-start(), calls=%async_computation.13 | async-start | bytes 6488064 | tf_op jit(solution)/shard_map/reduce_scatter | solution.py:250
  406.9 294.0 %reduce-scatter.10.cloned.1.call-start = ((), (), s32[]{:S(2)}) async-start(), calls=%async_computation.11 | async-start | bytes 2359296 | tf_op jit(solution)/shard_map/reduce_scatter | solution.py:250
  454.6 122.3 %collective-permute-start.51 = (bf16[2048,1024]{1,0:T(8,128)(2,1)}, bf16[2048,1024]{1,0:T(8,128)(2,1)}, u32[]{:S(2)}, u32[]{:S(2)}) collective-permute-start(bf16[2048,1024]{1,0:T(8,128)(2,1)} %convolution_convert_fusion.6), channel_id=1, source_target_pairs={{0,8},{8,0},{1,9},{9,1},{2,10},{10,2},{3,11},{11,3},{4,12},{12,4},... | collective-permute-start | bytes 12582920 | tf_op jit(solution)/shard_map/ppermute | solution.py:20
  471.1 35.9 %collective-permute-start.39 = (f32[4,16,512]{2,1,0:T(8,128)}, f32[4,16,512]{2,1,0:T(8,128)S(1)}, u32[]{:S(2)}, u32[]{:S(2)}) collective-permute-start(f32[4,16,512]{2,1,0:T(8,128)} %shard_map.223), channel_id=1, source_target_pairs={{2,0},{4,2},{6,4},{3,1},{5,3},{7,5},{10,8},{12,10},{14,12},{11,9},... | collective-permute-start | bytes 393224 | tf_op jit(solution)/shard_map/ppermute | solution.py:26
  473.0 35.2 %collective-permute-start.40 = (f32[4,16,512]{2,1,0:T(8,128)}, f32[4,16,512]{2,1,0:T(8,128)S(1)}, u32[]{:S(2)}, u32[]{:S(2)}) collective-permute-start(f32[4,16,512]{2,1,0:T(8,128)} %shard_map.223), channel_id=1, source_target_pairs={{4,0},{6,2},{5,1},{7,3},{12,8},{14,10},{13,9},{15,11},{20,16},{22,... | collective-permute-start | bytes 393224 | tf_op jit(solution)/shard_map/ppermute | solution.py:26
  474.3 34.0 %collective-permute-start.41 = (f32[4,16,512]{2,1,0:T(8,128)}, f32[4,16,512]{2,1,0:T(8,128)S(1)}, u32[]{:S(2)}, u32[]{:S(2)}) collective-permute-start(f32[4,16,512]{2,1,0:T(8,128)} %shard_map.223), channel_id=1, source_target_pairs={{6,0},{7,1},{14,8},{15,9},{22,16},{23,17},{30,24},{31,25}} | collective-permute-start | bytes 393224 | tf_op jit(solution)/shard_map/ppermute | solution.py:26
  504.7 196.2 %reduce-scatter.12.cloned.1.call-start = ((), (), s32[]{:S(2)}) async-start(), calls=%async_computation.12 | async-start | bytes 4718592 | tf_op jit(solution)/shard_map/reduce_scatter | solution.py:250
  504.8 27.2 %collective-permute-start.37 = (bf16[2,128,2048]{2,1,0:T(8,128)(2,1)}, bf16[2,128,2048]{2,1,0:T(8,128)(2,1)}, u32[]{:S(2)}, u32[]{:S(2)}) collective-permute-start(bf16[2,128,2048]{2,1,0:T(8,128)(2,1)} %get-tuple-element.801), channel_id=1, source_target_pairs={{0,1},{1,0},{2,3},{3,2},{4,5},{5,4},{6,7},{7,6},{8,9},{9,8},{10,11... | collective-permute-start | bytes 3145736 | tf_op jit(solution)/shard_map/ppermute | solution.py:20
  507.1 25.3 %collective-permute-start.38 = (bf16[2,128,2048]{2,1,0:T(8,128)(2,1)}, bf16[2,128,2048]{2,1,0:T(8,128)(2,1)}, u32[]{:S(2)}, u32[]{:S(2)}) collective-permute-start(bf16[2,128,2048]{2,1,0:T(8,128)(2,1)} %bitcast.474), channel_id=1, source_target_pairs={{0,16},{16,0},{1,17},{17,1},{2,18},{18,2},{3,19},{19,3},{4,20},{20... | collective-permute-start | bytes 3145736 | tf_op jit(solution)/shard_map/ppermute | solution.py:20
  542.5 30.9 %collective-permute-start.44 = (bf16[128,2048]{1,0:T(8,128)(2,1)}, bf16[128,2048]{1,0:T(8,128)(2,1)}, u32[]{:S(2)}, u32[]{:S(2)}) collective-permute-start(bf16[128,2048]{1,0:T(8,128)(2,1)} %get-tuple-element.850), channel_id=1, source_target_pairs={{0,16},{16,0},{1,17},{17,1},{2,18},{18,2},{3,19},{19,3},{4,20},{20... | collective-permute-start | bytes 1572872 | tf_op jit(solution)/shard_map/ppermute | solution.py:20
  542.8 30.5 %collective-permute-start.45 = (bf16[128,2048]{1,0:T(8,128)(2,1)}, bf16[128,2048]{1,0:T(8,128)(2,1)}, u32[]{:S(2)}, u32[]{:S(2)}) collective-permute-start(bf16[128,2048]{1,0:T(8,128)(2,1)} %get-tuple-element.852), channel_id=1, source_target_pairs={{0,1},{1,0},{2,3},{3,2},{4,5},{5,4},{6,7},{7,6},{8,9},{9,8},{10,11... | collective-permute-start | bytes 1572872 | tf_op jit(solution)/shard_map/ppermute | solution.py:20
  593.2 71.6 %collective-permute-start.55 = (bf16[2,256,1024]{2,1,0:T(8,128)(2,1)}, bf16[2,256,1024]{2,1,0:T(8,128)(2,1)}, u32[]{:S(2)}, u32[]{:S(2)}) collective-permute-start(bf16[2,256,1024]{2,1,0:T(8,128)(2,1)} %get-tuple-element.941), channel_id=1, source_target_pairs={{0,1},{1,0},{2,3},{3,2},{4,5},{5,4},{6,7},{7,6},{8,9},{9,8},{10,11... | collective-permute-start | bytes 3145736 | tf_op jit(solution)/shard_map/ppermute | solution.py:20
  593.9 71.0 %collective-permute-start.56 = (bf16[2,256,1024]{2,1,0:T(8,128)(2,1)}, bf16[2,256,1024]{2,1,0:T(8,128)(2,1)}, u32[]{:S(2)}, u32[]{:S(2)}) collective-permute-start(bf16[2,256,1024]{2,1,0:T(8,128)(2,1)} %bitcast.169), channel_id=1, source_target_pairs={{0,16},{16,0},{1,17},{17,1},{2,18},{18,2},{3,19},{19,3},{4,20},{20... | collective-permute-start | bytes 3145736 | tf_op jit(solution)/shard_map/ppermute | solution.py:20
  620.5 28.6 %collective-permute-start.52 = (bf16[128,2048]{1,0:T(8,128)(2,1)}, bf16[128,2048]{1,0:T(8,128)(2,1)}, u32[]{:S(2)}, u32[]{:S(2)}) collective-permute-start(bf16[128,2048]{1,0:T(8,128)(2,1)} %get-tuple-element.904), channel_id=1, source_target_pairs={{0,16},{16,0},{1,17},{17,1},{2,18},{18,2},{3,19},{19,3},{4,20},{20... | collective-permute-start | bytes 1572872 | tf_op jit(solution)/shard_map/ppermute | solution.py:20
  621.7 27.4 %collective-permute-start.53 = (bf16[128,2048]{1,0:T(8,128)(2,1)}, bf16[128,2048]{1,0:T(8,128)(2,1)}, u32[]{:S(2)}, u32[]{:S(2)}) collective-permute-start(bf16[128,2048]{1,0:T(8,128)(2,1)} %get-tuple-element.906), channel_id=1, source_target_pairs={{0,1},{1,0},{2,3},{3,2},{4,5},{5,4},{6,7},{7,6},{8,9},{9,8},{10,11... | collective-permute-start | bytes 1572872 | tf_op jit(solution)/shard_map/ppermute | solution.py:20
  700.1 31.5 %collective-permute-start.73 = (bf16[1,176,2048]{2,1,0:T(8,128)(2,1)}, bf16[1,176,2048]{2,1,0:T(8,128)(2,1)}, u32[]{:S(2)}, u32[]{:S(2)}) collective-permute-start(bf16[1,176,2048]{2,1,0:T(8,128)(2,1)} %bitcast.491), channel_id=1, source_target_pairs={{0,16},{16,0},{1,17},{17,1},{2,18},{18,2},{3,19},{19,3},{4,20},{20... | collective-permute-start | bytes 2162696 | tf_op jit(solution)/shard_map/ppermute | solution.py:20
  726.5 27.1 %collective-permute-start.71 = (bf16[1,256,1536]{2,1,0:T(8,128)(2,1)S(1)}, bf16[1,256,1536]{2,1,0:T(8,128)(2,1)}, u32[]{:S(2)}, u32[]{:S(2)}) collective-permute-start(bf16[1,256,1536]{2,1,0:T(8,128)(2,1)S(1)} %fusion.65), channel_id=1, source_target_pairs={{0,16},{16,0},{1,17},{17,1},{2,18},{18,2},{3,19},{19,3},{4,20},{20... | collective-permute-start | bytes 2359304 | tf_op jit(solution)/shard_map/ppermute | solution.py:20
  (121 other events, 1688.1 us)
Sparse Core Ops, SparseCore 0:
  28.8 76.3 all-gather.4
  107.4 61.0 all-gather.6
  170.8 68.2 all-gather.10
  240.5 62.1 all-gather.8
  346.2 67.3 reduce-scatter.5
  416.4 65.4 reduce-scatter.7
  484.7 69.7 reduce-scatter.13
  556.8 29.9 reduce-scatter.9
  594.4 49.3 reduce-scatter.11

commit v6 on v5

--- a/solution.py
+++ b/solution.py
@@ -234,14 +234,6 @@
     return held.reshape(2, -1, held.shape[-1])
 
 
-def z_slots(mine):
-    mine = mine.reshape(depth, -1, mine.shape[-1]).astype(low)
-    place = lax.axis_index("z")
-    return [
-        lax.dynamic_index_in_dim(mine, (place + d) % depth, 0, False) for d in range(depth)
-    ]
-
-
 def gather_tile(block):
     return lax.all_gather(block, ("z", "c"), axis=0, tiled=True)
 
@@ -289,25 +281,47 @@
     )
 
 
-def owner_ranks(slots, core):
+def assemble_kernel(count, width, order_ref, *refs):
+    sources, target = refs[:-1], refs[-1]
+    part = width // count
+    ranks = order_ref.shape[0] // 2
+    for r in range(ranks):
+        core, slot = order_ref[2 * r], order_ref[2 * r + 1]
+        value = sources[0][slot]
+        for c in range(1, len(sources)):
+            value = jnp.where(core == c, sources[c][slot], value)
+        value = value.astype(wide)
+        for at in range(count):
+            start = (at * ranks + r) * part
+            target[:, start : start + part] = value[:, at * part : (at + 1) * part]
+
+
+def owner_whole(core, sources, count):
     spread, ccount, ycount = lax.axis_size("x"), lax.axis_size("c"), lax.axis_size("y")
     share = spread // ccount
     yplace = lax.axis_index("y")
-    flat = slots.reshape((-1,) + slots.shape[3:])
-    ranks = []
+    order = []
     for i in range(spread):
         for k in range(ycount):
-            slot = (i // share - core) % ccount * ycount + (k - yplace) % ycount
-            ranks.append(lax.dynamic_index_in_dim(flat, slot * share + i % share, 0, False))
-    return ranks
-
-
-def owner_whole(ranks, count):
-    part = ranks[0].shape[1] // count
-    pieces = []
-    for at in range(count):
-        pieces += [r[:, at * part : (at + 1) * part].astype(wide) for r in ranks]
-    return jnp.concatenate(pieces, axis=1)
+            order += [(i // share - core) % ccount, (k - yplace) % ycount * share + i % share]
+    sources = [v.reshape((-1,) + v.shape[2:]) for v in sources]
+    held, rows, width = sources[0].shape
+    block = min(rows, 64)
+    return pl.pallas_call(
+        functools.partial(assemble_kernel, count, width),
+        out_shape=jax.ShapeDtypeStruct((rows, width * spread * ycount), wide),
+        grid_spec=pltpu.PrefetchScalarGridSpec(
+            num_scalar_prefetch=1,
+            grid=(rows // block,),
+            in_specs=[pl.BlockSpec((held, block, width), lambda i, order: (0, i, 0))]
+            * len(sources),
+            out_specs=pl.BlockSpec((block, width * spread * ycount), lambda i, order: (i, 0)),
+        ),
+        compiler_params=pltpu.CompilerParams(vmem_limit_bytes=56 << 20),
+        cost_estimate=pl.CostEstimate(
+            flops=0, transcendentals=0, bytes_accessed=6 * rows * width * spread * ycount
+        ),
+    )(jnp.stack(order).astype(jnp.int32), *sources)
 
 
 def in_order(slots, axis):
@@ -660,34 +674,40 @@
     block = spread * local
 
     count = 3 * depth
+    extra = 8
     line = Line(lax.axis_index("c"))
     run = line.run
 
     def stacked(value, got):
         return jnp.stack([value] + got)
 
+    in_got = column_moves(run(lambda w: column_pieces(w, 3), in_weight))
     block_out = run(out_block, out_weight)
     out_got = moved(block_out, "z", -1)
-    in_got = column_moves(run(lambda w: column_pieces(w, 3), in_weight))
+    last = [(i * spread + spread - 1, (i + 1) * spread) for i in range(depth - 1)]
 
     def norm_one(values, gain):
         values = values.astype(wide)
         scale = rms_scale(values)
         normed = (values * scale * gain).astype(low)
-        return normed[: batch // 2], normed[batch // 2 :], scale
-
-    first, second, scale_one = run(norm_one, tokens, norm_gain)
-    normed_move = Gather(first, second)
+        return normed, normed[:, local - 2 :], scale
+
+    normed, ending, scale_one = run(norm_one, tokens, norm_gain)
+    before = lax.ppermute(ending, ("z", "x"), last)
     w_in = gather_tile(run(column_block, in_got))
+
+    def lengthen(values, rows):
+        rest = jnp.zeros((batch, extra - 2, width), values.dtype)
+        values = jnp.concatenate([values, rows, rest], axis=1)
+        return values[: batch // 2], values[batch // 2 :]
+
+    normed_move = Gather(*run(lengthen, normed, before))
     held = run(lambda own, got: by_z([own] + got), block_out, out_got)
     normed_move.turn(line)
     w_down = gather_tile(run(row_block, down_weight))
-    out_move = Gather(held[:1], held[1:])
     gate_got = column_moves(run(lambda w: column_pieces(w, 1), gate_weight))
     normed_all = normed_move.end(line)
-    out_move.turn(line)
-    w_gate = gather_tile(run(column_block, gate_got))
-    up_got = column_moves(run(lambda w: column_pieces(w, 1), up_weight))
+    out_move = Gather(held[:1], held[1:])
 
     channels = w_in.shape[1] // 3
     half = channels // 2
@@ -709,42 +729,42 @@
     closing = closing[None, :, None, None, None]
 
     def project(v, w):
-        value = dot(v, w, low).reshape(grid + (3 * channels,))
-        return value, jnp.roll(value[:, :, :, local - 2 :], 1, axis=1)
-
-    mixed, tail = run(project, normed_all, w_in)
-    behind = passed(tail, "z", 1)
+        return dot(v, w, low).reshape(grid[:3] + (local + extra, 3 * channels))
+
+    mixed = run(project, normed_all, w_in)
+    out_move.turn(line)
+    w_gate = gather_tile(run(column_block, gate_got))
+    up_got = column_moves(run(lambda w: column_pieces(w, 1), up_weight))
+
+    def extend(value, g):
+        own = value[..., g * channels : (g + 1) * channels]
+        earlier = jnp.roll(own[:, :, :, local - 2 : local], 1, axis=1)
+        earlier = jnp.where(opening, own[:, :, :, local : local + 2], earlier)
+        return jnp.concatenate([earlier, own[:, :, :, :local]], axis=3).astype(wide)
+
+    def short_of(value, weights, g):
+        longer = extend(value, g)
+        own = weights[:, g * channels : (g + 1) * channels]
+        return own[0] * longer[:, :, :, 2:] + own[1] * longer[:, :, :, 1:-1] + own[2] * longer[:, :, :, :-2]
+
+    spot = lax.axis_index("x").astype(jnp.int32).reshape(1)
+
+    def multiply(value, weights, rates):
+        keys, values = (short_of(value, weights, g) for g in (1, 2))
+        product = (keys * values).astype(low)
+        return product, states_of(spot, product, rates)
+
+    product, state_end = run(multiply, mixed, taps, decay)
+    states = [passed(state_end, "z", k) for k in range(1, depth)]
+    w_up = gather_tile(run(column_block, up_got))
+    out_own = out_move.end(line)
+    w_out = [out_own] + moved(out_own, "c", -1)
 
     def feed_grad(values):
         values = (values.astype(wide) * mask).astype(low)
         return values[: batch // 2], values[batch // 2 :]
 
     feed_move = Gather(*run(feed_grad, cotangent))
-    w_up = gather_tile(run(column_block, up_got))
-    out_own = out_move.end(line)
-    w_out = [out_own] + moved(out_own, "c", -1)
-
-    def extend(value, ends, before, g):
-        at = slice(g * channels, (g + 1) * channels)
-        return jnp.concatenate(
-            [jnp.where(opening, before[..., at], ends[..., at]), value[..., at]], axis=3
-        ).astype(wide)
-
-    def short_of(value, ends, before, weights, g):
-        longer = extend(value, ends, before, g)
-        own = weights[:, g * channels : (g + 1) * channels]
-        return own[0] * longer[:, :, :, 2:] + own[1] * longer[:, :, :, 1:-1] + own[2] * longer[:, :, :, :-2]
-
-    spot = lax.axis_index("x").astype(jnp.int32).reshape(1)
-
-    def multiply(value, ends, before, weights, rates):
-        keys, values = (short_of(value, ends, before, weights, g) for g in (1, 2))
-        product = (keys * values).astype(low)
-        return product, states_of(spot, product, rates)
-
-    product, state_end = run(multiply, mixed, tail, behind, taps, decay)
-    states = [passed(state_end, "z", k) for k in range(1, depth)]
-    feed_move.turn(line)
 
     def combine(parts, rates):
         total = parts[0]
@@ -752,23 +772,24 @@
             total = total + jnp.exp(-rates * (k * block)) * parts[k]
         return total
 
-    def convolve(parts, value, ends, before, weights, signal, rates, amounts):
+    def convolve(parts, value, weights, signal, rates, amounts):
         start = combine(parts, rates)
         result = forward_of(spot, signal, rates, amounts, start)
-        query = short_of(value, ends, before, weights, 0)
+        query = short_of(value, weights, 0)
         gated = (query * result.astype(wide)).astype(low)
         slots = gated.reshape(2, ycount, spread, -1, channels)
         return (
             start,
             result,
+            gated.reshape(-1, channels),
             [[slots[:, k, i].reshape(-1, channels) for i in range(spread)] for k in range(ycount)],
         )
 
-    start, convolved, gated = run(
-        convolve, states, mixed, tail, behind, taps, product, decay, residue
+    start, convolved, gated_all, gated = run(
+        convolve, states, mixed, taps, product, decay, residue
     )
     gated_got = swap_slots(gated)
-    grad_feed_all = feed_move.end(line)
+    feed_move.turn(line)
 
     def mix(got, weights, values, gain):
         own = jnp.concatenate(
@@ -779,11 +800,12 @@
         middle = values.astype(wide) + mixer
         scale = rms_scale(middle)
         normed = (middle * scale * gain).astype(low)
-        return own, middle, scale, normed[: batch // 2], normed[batch // 2 :]
-
-    gated_own, middle, scale_two, first, second = run(mix, gated_got, w_out, tokens, feed_gain)
+        return middle, scale, normed[: batch // 2], normed[batch // 2 :]
+
+    middle, scale_two, first, second = run(mix, gated_got, w_out, tokens, feed_gain)
 
     two_move = Gather(first, second)
+    grad_feed_all = feed_move.end(line)
     grad_active = run(dot_t, grad_feed_all, w_down)
     two_move.turn(line)
     normed_two_all = two_move.end(line)
@@ -833,93 +855,73 @@
             return jnp.concatenate(pieces, axis=1)
 
         slots = [[slot(k * spread + i) for i in range(spread)] for k in range(ycount)]
-        return result, grad_gain, parts, slots
-
-    grad_middle, grad_feed_gain, mix_parts, grad_slots = run(
+        rounded = result.astype(low)
+        return result, grad_gain, rounded[: batch // 2], rounded[batch // 2 :], slots
+
+    grad_middle, grad_feed_gain, first, second, grad_slots = run(
         middle_back, two_back.rest(), middle, scale_two, feed_gain, cotangent, w_out
     )
     grad_got = swap_slots(grad_slots)
-    out_terms = run(lambda g, parts: [dot_w(g, m) for m in parts], gated_own, mix_parts)
-    out_terms_got = [turned(t, "c", d + 1) for d, t in enumerate(out_terms[1:])]
-
-    def conv_grads(got, result, value, ends, before, weights, rates):
+    mix_move = Gather(first, second)
+
+    def conv_grads(got, result, value, weights, rates):
         grad = jnp.stack([jnp.stack(row) for row in got])
         grad = grad.reshape(ycount, spread, 2, batch // 2, local, channels)
         grad = jnp.moveaxis(grad, 2, 0).reshape(grid + (channels,)).astype(wide)
-        grad_query = (grad * result.astype(wide)).astype(wide)
-        grad_conv = (grad * short_of(value, ends, before, weights, 0)).astype(low)
-        return (
-            grad_query,
-            jnp.roll(grad_query[:, :, :, :2].astype(low), -1, axis=1),
-            grad_conv,
-            later_of(spot, grad_conv, rates),
-        )
-
-    grad_query, query_head, grad_conv, later_end = run(
-        conv_grads, grad_got, convolved, mixed, tail, behind, taps, decay
-    )
+        grad_query = grad * result.astype(wide)
+        grad_conv = (grad * short_of(value, weights, 0)).astype(low)
+        return grad_query, grad_conv, later_of(spot, grad_conv, rates)
+
+    grad_query, grad_conv, later_end = run(conv_grads, grad_got, convolved, mixed, taps, decay)
     laters = [passed(later_end, "z", -k) for k in range(1, depth)]
-    query_ahead = passed(query_head, "z", -1)
-    feed_back = Scatter(run(lambda a, w: split_sum(dot(a, w, low)), active, w_down))
-
-    def short_back(grad_short, head, ahead, weights):
-        whole = jnp.concatenate([grad_short, jnp.where(closing, ahead, head).astype(wide)], axis=3)
+    mix_move.turn(line)
+
+    def short_back(grad, weights):
+        head = jnp.roll(grad[:, :, :, :2], -1, axis=1)
+        whole = jnp.concatenate([grad, jnp.where(closing, 0.0, head)], axis=3)
         result = (
             weights[0] * whole[:, :, :, :-2]
             + weights[1] * whole[:, :, :, 1:-1]
             + weights[2] * whole[:, :, :, 2:]
         )
-        return result.astype(low).reshape(-1, grad_short.shape[-1])
-
-    def query_back(grad, head, ahead, weights, v):
-        result = short_back(grad, head, ahead, weights[:, :channels])
+        one, two = grad[:, :, :, :1], grad[:, :, :, 1:2]
+        earlier = jnp.concatenate([weights[2] * one, weights[1] * one + weights[2] * two], axis=3)
+        rest = jnp.zeros(grad.shape[:3] + (extra - 2, grad.shape[-1]), wide)
+        result = jnp.concatenate([result, jnp.where(opening, earlier, 0.0), rest], axis=3)
+        return result.astype(low).reshape(-1, grad.shape[-1])
+
+    def query_back(grad, weights, v):
+        result = short_back(grad, weights[:, :channels])
         return result, dot_w(v, result)
 
+    grad_mixed_query, query_term = run(query_back, grad_query, taps, normed_all)
+    query_mine = scatter_tile(query_term)
     up_parts_got = owner_moves(run(owner_parts, up_mine))
-    grad_mixed_query, query_term = run(
-        query_back, grad_query, query_head, query_ahead, taps, normed_all
-    )
-    query_mine = scatter_tile(query_term)
-
-    up_held = run(owner_held, up_parts_got)
-    up_got = moved(up_held, "y", -1)
-
-    def conv_back(signal, grad, rates, amounts, begin, ends_later, value, ends, before, weights):
+
+    def conv_back(signal, grad, rates, amounts, begin, ends_later, value, weights):
         later = combine(ends_later, rates)
         grad_product, grad_residue, grad_decay = backward_of(
             spot, signal, grad, rates, amounts, begin, later
         )
         grad_product = grad_product.astype(wide)
-        keys, values = (short_of(value, ends, before, weights, g) for g in (1, 2))
+        keys, values = (short_of(value, weights, g) for g in (1, 2))
         pair = jnp.concatenate([grad_product * values, grad_product * keys], axis=-1)
-        return pair, jnp.roll(pair[:, :, :, :2].astype(low), -1, axis=1), grad_residue, grad_decay
-
-    grad_pair, pair_head, grad_residue, grad_decay = run(
-        conv_back,
-        product,
-        grad_conv,
-        decay,
-        residue,
-        start,
-        laters,
-        mixed,
-        tail,
-        behind,
-        taps,
-    )
-    pair_ahead = passed(pair_head, "z", -1)
-    feed_back.turn(line)
-    up_held = run(stacked, up_held, up_got)
-    up_got = moved(up_held, "c", -1)
-
-    def pair_back(grad, head, ahead, weights, v):
-        result = short_back(grad, head, ahead, weights[:, channels:])
+        return pair, grad_residue, grad_decay
+
+    grad_pair, grad_residue, grad_decay = run(
+        conv_back, product, grad_conv, decay, residue, start, laters, mixed, taps
+    )
+
+    def pair_back(grad, weights, v):
+        result = short_back(grad, weights[:, channels:])
         return result, dot_w(v, result)
 
-    grad_mixed_pair, pair_term = run(
-        pair_back, grad_pair, pair_head, pair_ahead, taps, normed_all
-    )
+    grad_mixed_pair, pair_term = run(pair_back, grad_pair, taps, normed_all)
     pair_mine = scatter_tile(pair_term)
+    up_held = run(owner_held, up_parts_got)
+    up_got = moved(up_held, "y", -1)
+    grad_mix_all = mix_move.end(line)
+    out_mine = scatter_tile(run(dot_w, gated_all, grad_mix_all))
     one_back = Scatter(
         run(
             lambda a, b, w: split_sum(dot_t(jnp.concatenate([a, b], axis=1), w, low)),
@@ -929,6 +931,64 @@
         )
     )
 
+    feed_parts = run(lambda a, w: split_sum(dot(a, w, low)), active, w_down)
+    up_held = run(stacked, up_held, up_got)
+    up_got = moved(up_held, "c", -1)
+    one_back.turn(line)
+    feed_back = Scatter(feed_parts)
+    gate_got = owner_moves(run(owner_parts, gate_mine))
+
+    def tap_sums(query, pair, value):
+        sums = []
+        for g, part in enumerate((query, pair[..., :channels], pair[..., channels:])):
+            own = extend(value, g)
+            sums += [
+                jnp.sum(part * own[:, :, :, 2 - j : local + 2 - j], axis=(0, 1, 2, 3))
+                for j in range(3)
+            ]
+        return jnp.stack(sums)
+
+    grad_taps = run(tap_sums, grad_query, grad_pair, mixed)
+
+    def normed_sum(rest):
+        value = Scatter.sum(*rest).reshape(batch, local + extra, width)
+        return value[:, :local], value[:, local : local + 2].astype(low)
+
+    grad_normed, grad_before = run(normed_sum, one_back.rest())
+    grad_after = lax.ppermute(grad_before, ("z", "x"), [(j, i) for i, j in last])
+
+    def column_whole(own, got):
+        return owner_whole(lax.axis_index("c"), [own] + got, depth)
+
+    grad_up_weight = run(column_whole, up_held, up_got)
+    gate_held = run(owner_held, gate_got)
+    gate_got = moved(gate_held, "y", -1)
+    feed_back.turn(line)
+
+    def tokens_back(grad, extension, values, scale, gain, back, small):
+        values = values.astype(wide)
+        grad = jnp.concatenate(
+            [grad[:, : local - 2], grad[:, local - 2 :] + extension.astype(wide)], axis=1
+        )
+        result, grad_gain = norm_back(values, scale, gain, grad)
+        gains = jnp.stack([grad_gain, small[0]]).reshape(-1, channels)
+        return (result + back).astype(low), jnp.concatenate(list(small[1:]) + [gains], axis=0)
+
+    grad_tokens, small = run(
+        tokens_back,
+        grad_normed,
+        grad_after,
+        tokens,
+        scale_one,
+        norm_gain,
+        grad_middle,
+        (grad_feed_gain, grad_residue, grad_decay, grad_taps),
+    )
+    small_got = moved(small, "c", 1)
+    gate_held = run(stacked, gate_held, gate_got)
+    gate_got = moved(gate_held, "c", -1)
+    small = run(lambda v, got: v + sum(got), small, small_got)
+    small_got = moved(small, "z", 1)
     output = run(
         lambda rest, values: (
             mask * (values + Scatter.sum(*rest).reshape(batch, local, width))
@@ -936,77 +996,31 @@
         feed_back.rest(),
         middle,
     )
-    out_back_parts = run(
-        lambda own, got: split_sum(add_up([own], got)), out_terms[0], out_terms_got
-    )
-
-    def column_whole(own, got):
-        return owner_whole(owner_ranks(jnp.stack([own] + got), lax.axis_index("c")), depth)
-
-    grad_up_weight = run(column_whole, up_held, up_got)
-    one_back.turn(line)
-    gate_got = owner_moves(run(owner_parts, gate_mine))
-    out_back = Scatter(out_back_parts)
-
-    def tap_sums(query, pair, value, ends, before):
-        sums = []
-        for g, part in enumerate((query, pair[..., :channels], pair[..., channels:])):
-            own = extend(value, ends, before, g)
-            sums += [
-                jnp.sum(part * own[:, :, :, 2 - j : local + 2 - j], axis=(0, 1, 2, 3))
-                for j in range(3)
-            ]
-        return jnp.stack(sums)
-
-    grad_taps = run(tap_sums, grad_query, grad_pair, mixed, tail, behind)
-
-    def tokens_back(rest, values, scale, gain, back, small):
-        values = values.astype(wide)
-        grad_normed = Scatter.sum(*rest).reshape(batch, local, width)
-        result, grad_gain = norm_back(values, scale, gain, grad_normed)
-        gains = jnp.stack([grad_gain, small[0]]).reshape(-1, channels)
-        return (result + back).astype(low), jnp.concatenate(list(small[1:]) + [gains], axis=0)
-
-    grad_tokens, small = run(
-        tokens_back,
-        one_back.rest(),
-        tokens,
-        scale_one,
-        norm_gain,
-        grad_middle,
-        (grad_feed_gain, grad_residue, grad_decay, grad_taps),
-    )
-    small_got = moved(small, "c", 1)
-    gate_held = run(owner_held, gate_got)
-    gate_got = moved(gate_held, "y", -1)
-    out_back.turn(line)
-    small = run(lambda v, got: v + sum(got), small, small_got)
-    small_got = moved(small, "z", 1)
-    gate_held = run(stacked, gate_held, gate_got)
-    gate_got = moved(gate_held, "c", -1)
-    out_slots = run(
-        lambda rest: z_slots(Scatter.sum(*rest).reshape(channels, -1)), out_back.rest()
-    )
-    out_got = [turned(p, "z", d + 1) for d, p in enumerate(out_slots[1:])]
+    down_rows = down_mine.shape[0]
+    rows_held = run(lambda a, b: jnp.concatenate([a, b])[None], down_mine, out_mine)
+    rows_got = moved(rows_held, "y", -1)
+    grad_gate_weight = run(column_whole, gate_held, gate_got)
     small = run(lambda v, got: v + sum(got), small, small_got)
     small_got = moved(small, "x", -1)
-    down_held = run(lambda v: v.reshape(1, -1, width), down_mine)
-    down_got = moved(down_held, "y", -1)
     parts = run(
         lambda a, b: owner_parts(jnp.concatenate([a, b], axis=1)), query_mine, pair_mine
     )
     in_got = owner_moves(parts)
-    grad_gate_weight = run(column_whole, gate_held, gate_got)
-    out_held = run(lambda own, got: add_up([own], got).astype(low), out_slots[0], out_got)
-    out_got = moved(out_held, "y", -1)
+    rows_held = run(lambda own, got: jnp.concatenate([own] + got), rows_held, rows_got)
+    rows_got = moved(rows_held, "c", -1)
+    small = run(stacked, small, small_got)
+    small_got = moved(small, "y", -1)
     in_held = run(owner_held, in_got)
     in_got = moved(in_held, "y", -1)
-    small = run(stacked, small, small_got)
-    small_got = moved(small, "y", -1)
-    down_held = run(lambda own, got: jnp.concatenate([own] + got), down_held, down_got)
-    down_got = moved(down_held, "c", -1)
-    out_held = run(stacked, out_held, out_got)
-    out_got = moved(out_held, "c", -1)
+
+    def rows_whole(own, got):
+        whole = in_order(jnp.swapaxes(in_order(jnp.stack([own] + got), "c"), 0, 1), "y")
+        return (
+            whole[:, :, :down_rows].reshape(-1, width).astype(wide),
+            whole[:, :, down_rows:].reshape(-1, width).astype(wide),
+        )
+
+    grad_down, grad_out_weight = run(rows_whole, rows_held, rows_got)
     in_held = run(stacked, in_held, in_got)
     in_got = moved(in_held, "c", -1)
     poles = decay.shape[0]
@@ -1024,24 +1038,8 @@
     grad_norm_gain, feed_gain_sum, grad_conv_taps, residue_sum, decay_sum = run(
         small_whole, small, small_got
     )
-
-    def down_whole(own, got):
-        whole = in_order(jnp.swapaxes(in_order(jnp.stack([own] + got), "c"), 0, 1), "y")
-        return whole.reshape(-1, width).astype(wide)
-
-    grad_down = run(down_whole, down_held, down_got)
-
-    def out_whole(own, got):
-        whole = in_order(jnp.stack([own] + got), "c")
-        whole = in_order(jnp.swapaxes(whole, 0, 1), "y")
-        ys, cs, rows, columns = whole.shape
-        return jnp.swapaxes(whole, 1, 2).reshape(ys * rows, cs * columns).astype(wide)
-
-    grad_out_weight = run(out_whole, out_held, out_got)
     grad_in_weight = line.finish(
-        lambda core, own, got: owner_whole(owner_ranks(jnp.stack([own] + got), core), count),
-        in_held,
-        in_got,
+        lambda core, own, got: owner_whole(core, [own] + got, count), in_held, in_got
     )
     return (
         output,

time: 801 us -> 786 us (0.981)
  other arithmetic: 141 us -> 116 us
  local copies, waits for them, and re-layouts: 92.7 us -> 70.1 us
  Pallas kernels: 38.7 us -> 57.1 us
  waiting for transfers between devices: 239 us -> 256 us
    ppermute x56 -> x50, waiting for transfers between devices: 186 us -> 216 us  [turned(): lax.ppermute(value, axis, [(i, (i + by) % length) for i in range(length)])]
    pallas_call x0 -> x3, Pallas kernels: none -> 18 us  [owner_whole(): pl.pallas_call(functools.partial(assemble_kernel, count, width), out_shap...]
    ppermute x3, waiting for transfers between devices: 21.3 us -> 5.27 us  [column_moves(): got.append(lax.ppermute(pieces[d], ('c', 'x'), pairs))]
    another operation x8 -> x6, other arithmetic: 17 us -> 5.5 us  [the longest x1 2.94 us: rows_whole(): jnp.stack([own] + got)]
    concatenate x3 -> x1, local copies, waits for them, and re-layouts: 10.4 us -> 0.08 us  [lengthen(): values = jnp.concatenate([values, rows, rest], axis=1)]
    ppermute x9 -> x6, starting transfers between devices: 21.3 us -> 11.8 us  [passed(): return lax.ppermute(value, axis, pairs)]
    ppermute x56 -> x50, starting transfers between devices: 59.9 us -> 54.1 us  [turned(): lax.ppermute(value, axis, [(i, (i + by) % length) for i in range(length)])]
    slice x18 -> x16, local copies, waits for them, and re-layouts: 17.8 us -> 13.7 us  [the longest x5 8.29 us: extend(): return jnp.concatenate([earlier, own[:, :, :, :local]], axis=3).astype(wide)]
  transfers between devices with their start and end apart: 86 -> 80, of which waited for: 37 -> 30; matrix products, arithmetic and copies ran while one was open for 46% -> 42% of each run, Pallas kernels for 4% -> 6%
where the time goes in v6:
time: 786 us; the launch traced here: 771 us
  waiting for transfers between devices  256 us (33%)
  matrix products  158 us (20%)
  other arithmetic  116 us (15%)
  starting transfers between devices  97 us (12%)
  local copies, waits for them, and re-layouts  70.1 us (9%)
  Pallas kernels  57.1 us (7%)
  between operations  16.6 us (2%)
    ppermute x50, waiting for transfers between devices, turned(): lax.ppermute(value, axis, [(i, (i + by) % length) for i in range(length)])  216 us
    dot_general x6, matrix products, dot(): return jnp.dot(a, b, preferred_element_type=wide).astype(kind)  65.6 us
    ppermute x50, starting transfers between devices, turned(): lax.ppermute(value, axis, [(i, (i + by) % length) for i in range(length)])  54.1 us
    dot_general x6, matrix products, dot_t(): lax.dot_general(a, b, (((1,), (1,)), ((), ())), preferred_element_type=wide)  46.8 us
    dot_general x6, matrix products, dot_w(): lax.dot_general(a, b, (((0,), (0,)), ((), ())), preferred_element_type=wide)  45.9 us
    pallas_call x4, Pallas kernels, conv_call(): pl.pallas_call(kernel, out_shape=results, grid_spec=pltpu.PrefetchScalarG...  35.5 us
    ppermute x6, waiting for transfers between devices, passed(): return lax.ppermute(value, axis, pairs)  21.3 us
    unnamed x139, local copies, waits for them, and re-layouts  19.6 us
  transfers between devices with their start and end apart: 80, of which 30 were waited for; matrix products, arithmetic and copies ran while one was open for 42% of the time, Pallas kernels for 6%

profile of v6, /device:TPU:9, one launch (start us, length us, event | category | flops | bytes accessed | tf_op | source)
XLA Modules:
  0.0 771.2 jit_solution(210716524240026803)
XLA Ops:
  37.6 17.8 %collective-permute-done.5 = bf16[128,1024]{1,0:T(8,128)(2,1)} collective-permute-done((bf16[128,1024]{1,0:T(8,128)(2,1)}, bf16[128,1024]{1,0:T(8,128)(2,1)}, u32[]{:S(2)}, u32[]{:S(2)}) %collective-permute-start.5) | collective-permute-done | bytes 262176 | tf_op jit(solution)/shard_map/ppermute | solution.py:20
  55.4 19.5 %collective-permute-done.6 = bf16[128,1024]{1,0:T(8,128)(2,1)} collective-permute-done((bf16[128,1024]{1,0:T(8,128)(2,1)}, bf16[128,1024]{1,0:T(8,128)(2,1)}, u32[]{:S(2)}, u32[]{:S(2)}) %collective-permute-start.6) | collective-permute-done | bytes 262176 | tf_op jit(solution)/shard_map/ppermute | solution.py:20
  84.1 7.4 collective-permute-start.8
  102.4 12.0 %collective-permute-done.8 = bf16[2,1,136,2048]{3,2,0,1:T(8,128)(2,1)S(1)} collective-permute-done((bf16[2,1,136,2048]{3,2,0,1:T(8,128)(2,1)}, bf16[2,1,136,2048]{3,2,0,1:T(8,128)(2,1)S(1)}, u32[]{:S(2)}, u32[]{:S(2)}) %collective-permute-start.8) | collective-permute-done | bytes 1114144 | tf_op jit(solution)/shard_map/ppermute | solution.py:20
  123.1 11.8 %convolution_convert_fusion.3 = bf16[1088,1536]{1,0:T(8,128)(2,1)} fusion(bf16[1088,2048]{1,0:T(8,128)(2,1)} %bitcast.386, bf16[2048,1536]{1,0:T(8,128)(2,1)} %all-gather.5.cloned.1.call-done), kind=kOutput, calls=%fused_computation.4 | convolution fusion | flops 6846775296 | bytes 14090240 | tf_op jit(solution)/shard_map/dot_general | solution.py:643
  166.9 14.9 %collective-permute-done.16 = bf16[2,1,256,1024]{3,2,0,1:T(8,128)(2,1)} collective-permute-done((bf16[2,1,256,1024]{3,2,0,1:T(8,128)(2,1)}, bf16[2,1,256,1024]{3,2,0,1:T(8,128)(2,1)}, u32[]{:S(2)}, u32[]{:S(2)}) %collective-permute-start.16) | collective-permute-done | bytes 1048608 | tf_op jit(solution)/shard_map/ppermute | solution.py:20
  197.2 6.9 collective-permute-done.12
  204.1 14.4 %collective-permute-done.13 = f32[4,16,512]{2,1,0:T(8,128)S(1)} collective-permute-done((f32[4,16,512]{2,1,0:T(8,128)S(1)}, f32[4,16,512]{2,1,0:T(8,128)S(1)}, u32[]{:S(2)}, u32[]{:S(2)}) %collective-permute-start.13) | collective-permute-done | bytes 131104 | tf_op jit(solution)/shard_map/ppermute | solution.py:26
  223.8 8.9 %shard_map.222 = bf16[4,2,1,128,512]{4,3,2,1,0:T(8,128)(2,1)} custom-call(s32[1]{0:T(128)} %bitcast.44.place_ref, bf16[4,2,1,128,512]{4,3,2,1,0:T(8,128)(2,1)} %fusion.53.signal_ref, f32[16,512]{1,0:T(8,128)} %maximum_bitcast_fusion.12.decay_ref, f32[16,512]{1,0:T(8,128)} %maximum_bitcast_fusion.13.residue_ref, f32[4,16,512]{2,1,0:T(8,128)} %multiply_add_fusion.2.start_ref), custom_call_target="tpu_custom_call" | custom-call | flops 33554432 | bytes 2293760 | tf_op jit(solution)/shard_map/pallas_call | solution.py:560
  255.2 14.3 %collective-permute-done.26 = bf16[2,1,128,2048]{3,2,0,1:T(8,128)(2,1)S(1)} collective-permute-done((bf16[2,1,128,2048]{3,2,0,1:T(8,128)(2,1)S(1)}, bf16[2,1,128,2048]{3,2,0,1:T(8,128)(2,1)S(1)}, u32[]{:S(2)}, u32[]{:S(2)}) %collective-permute-start.26) | collective-permute-done | bytes 1048608 | tf_op jit(solution)/shard_map/ppermute | solution.py:20
  274.2 11.9 %fusion.122 = f32[1024,1408]{1,0:T(8,128)} fusion(bf16[1024,2048]{1,0:T(8,128)(2,1)} %bitcast.397, bf16[1408,2048]{1,0:T(8,128)(2,1)} %all-gather.7.cloned.1.call-done), kind=kOutput, calls=%fused_computation.419 | convolution fusion | flops 5905580032 | bytes 15728640 | tf_op jit(solution)/shard_map/dot_general | solution.py:647
  287.8 19.8 %collective-permute-done.28 = bf16[2,1,128,2048]{3,2,0,1:T(8,128)(2,1)S(1)} collective-permute-done((bf16[2,1,128,2048]{3,2,0,1:T(8,128)(2,1)S(1)}, bf16[2,1,128,2048]{3,2,0,1:T(8,128)(2,1)S(1)}, u32[]{:S(2)}, u32[]{:S(2)}) %collective-permute-start.28) | collective-permute-done | bytes 1048608 | tf_op jit(solution)/shard_map/ppermute | solution.py:20
  312.1 24.7 %multiply_convert_fusion.2 = (bf16[1024,1408]{1,0:T(8,128)(2,1)S(1)}, f32[1024,1408]{1,0:T(8,128)}) fusion(f32[1024,1408]{1,0:T(8,128)} %fusion.122, bf16[1024,2048]{1,0:T(8,128)(2,1)} %bitcast.399, bf16[2048,1408]{1,0:T(8,128)(2,1)} %all-gather.11.cloned.1.call-done), kind=kOutput, calls=%fused_computation.9 | convolution fusion | flops 5914230784 | bytes 24379392 | tf_op jit(solution)/shard_map/dot_general | solution.py:643
  338.3 8.7 %convolution_convert_fusion.2 = bf16[2048,1408]{1,0:T(8,128)(2,1)} fusion(bf16[1024,2048]{1,0:T(8,128)(2,1)S(1)} %bitcast.401, bf16[1024,1408]{1,0:T(8,128)(2,1)S(1)} %get-tuple-element.698), kind=kOutput, calls=%fused_computation.3 | convolution fusion | flops 5908463616 | bytes 12845056 | tf_op jit(solution)/shard_map/dot_general | solution.py:651
  347.1 15.1 %multiply_convert_fusion = (bf16[1024,1408]{1,0:T(8,128)(2,1)S(1)}, bf16[1024,1408]{1,0:T(8,128)(2,1)}) fusion(f32[1024,1408]{1,0:T(8,128)} %get-tuple-element.688, f32[1024,1408]{1,0:T(8,128)} %fusion.122, bf16[1024,2048]{1,0:T(8,128)(2,1)} %bitcast.400, bf16[2048,1408]{1,0:T(8,128)(2,1)} %all-gather.9.cloned.1.call-done), kind=kOutput, calls=%fused_computation.6 | convolution fusion | flops 5924323328 | bytes 27262976 | tf_op jit(solution)/shard_map/dot_general | solution.py:643
  363.8 8.9 %fusion.123 = f32[1024,2048]{1,0:T(8,128)S(1)} fusion(bf16[1024,1408]{1,0:T(8,128)(2,1)S(1)} %get-tuple-element.707, bf16[2048,1408]{1,0:T(8,128)(2,1)} %all-gather.11.cloned.1.call-done), kind=kOutput, calls=%fused_computation.420 | convolution fusion | flops 5905580032 | bytes 17039360 | tf_op jit(solution)/shard_map/dot_general | solution.py:647
  372.7 8.4 %add_convert_fusion = bf16[1024,2048]{1,0:T(8,128)(2,1)S(1)} fusion(f32[1024,2048]{1,0:T(8,128)S(1)} %fusion.123, bf16[1024,1408]{1,0:T(8,128)(2,1)} %copy-done.54, bf16[2048,1408]{1,0:T(8,128)(2,1)S(1)} %copy-done.50), kind=kOutput, calls=%fused_computation | convolution fusion | flops 5909774336 | bytes 21233664 | tf_op jit(solution)/shard_map/dot_general | solution.py:647
  386.1 8.7 %convolution_convert_fusion.1 = bf16[2048,1408]{1,0:T(8,128)(2,1)} fusion(bf16[1024,2048]{1,0:T(8,128)(2,1)S(1)} %bitcast.402, bf16[1024,1408]{1,0:T(8,128)(2,1)S(1)} %copy-done.53), kind=kOutput, calls=%fused_computation.2 | convolution fusion | flops 5908463616 | bytes 12845056 | tf_op jit(solution)/shard_map/dot_general | solution.py:651
  395.3 10.9 %convolution_convert_fusion = bf16[1408,2048]{1,0:T(8,128)(2,1)} fusion(bf16[1024,1408]{1,0:T(8,128)(2,1)} %get-tuple-element.822, bf16[1024,2048]{1,0:T(8,128)(2,1)} %bitcast.398), kind=kOutput, calls=%fused_computation.1 | convolution fusion | flops 5908463616 | bytes 12845056 | tf_op jit(solution)/shard_map/dot_general | solution.py:651
  406.1 9.3 %collective-permute-done.30 = bf16[2,128,2048]{2,1,0:T(8,128)(2,1)} collective-permute-done((bf16[2,128,2048]{2,1,0:T(8,128)(2,1)}, bf16[2,128,2048]{2,1,0:T(8,128)(2,1)}, u32[]{:S(2)}, u32[]{:S(2)}) %collective-permute-start.30) | collective-permute-done | bytes 1048608 | tf_op jit(solution)/shard_map/ppermute | solution.py:20
  422.5 6.9 collective-permute-done.32
  485.3 16.8 %shard_map.224 = (bf16[4,2,1,128,512]{4,3,2,1,0:T(8,128)(2,1)}, f32[16,512]{1,0:T(8,128)}, f32[16,512]{1,0:T(8,128)}) custom-call(s32[1]{0:T(128)} %bitcast.44.place_ref, bf16[4,2,1,128,512]{4,3,2,1,0:T(8,128)(2,1)} %fusion.53.signal_ref, bf16[4,2,1,128,512]{4,3,2,1,0:T(8,128)(2,1)} %get-tuple-element.776.signal_ref.grad_ref, ...), custom_call_target="tpu_custom_call" | custom-call | flops 100663296 | bytes 4521984 | tf_op jit(solution)/shard_map/pallas_call | solution.py:560
  509.9 14.8 %collective-permute-start.44 = (bf16[256,1408]{1,0:T(8,128)(2,1)S(1)}, bf16[256,1408]{1,0:T(8,128)(2,1)}, u32[]{:S(2)}, u32[]{:S(2)}) collective-permute-start(bf16[256,1408]{1,0:T(8,128)(2,1)S(1)} %copy-done.37), channel_id=1, source_target_pairs={{8,1},{1,8},{10,3},{3,10},{12,5},{5,12},{14,7},{7,14},{24,17},{17,... | collective-permute-start | bytes 2162696 | tf_op jit(solution)/shard_map/ppermute | solution.py:267
  528.8 7.3 convolution_convert_fusion.6
  547.7 10.5 %convolution_convert_fusion.4 = bf16[1088,2048]{1,0:T(8,128)(2,1)S(1)} fusion(bf16[2048,1536]{1,0:T(8,128)(2,1)} %all-gather.5.cloned.1.call-done, bf16[1088,1024]{1,0:T(8,128)(2,1)} %bitcast.427, bf16[1088,512]{1,0:T(8,128)(2,1)} %bitcast.440), kind=kOutput, calls=%fused_computation.5 | convolution fusion | flops 6854017024 | bytes 14090240 | tf_op jit(solution)/shard_map/dot_general | solution.py:647
  578.4 8.2 %collective-permute-done.47 = bf16[2,136,2048]{2,1,0:T(8,128)(2,1)S(1)} collective-permute-done((bf16[2,136,2048]{2,1,0:T(8,128)(2,1)S(1)}, bf16[2,136,2048]{2,1,0:T(8,128)(2,1)S(1)}, u32[]{:S(2)}, u32[]{:S(2)}) %collective-permute-start.47) | collective-permute-done | bytes 1114144 | tf_op jit(solution)/shard_map/ppermute | solution.py:20
  586.6 14.5 %collective-permute-done.48 = bf16[2,136,2048]{2,1,0:T(8,128)(2,1)S(1)} collective-permute-done((bf16[2,136,2048]{2,1,0:T(8,128)(2,1)S(1)}, bf16[2,136,2048]{2,1,0:T(8,128)(2,1)S(1)}, u32[]{:S(2)}, u32[]{:S(2)}) %collective-permute-start.48) | collective-permute-done | bytes 1114144 | tf_op jit(solution)/shard_map/ppermute | solution.py:20
  614.8 20.2 %collective-permute-done.52 = bf16[136,2048]{1,0:T(8,128)(2,1)} collective-permute-done((bf16[136,2048]{1,0:T(8,128)(2,1)}, bf16[136,2048]{1,0:T(8,128)(2,1)}, u32[]{:S(2)}, u32[]{:S(2)}) %collective-permute-start.52) | collective-permute-done | bytes 557088 | tf_op jit(solution)/shard_map/ppermute | solution.py:20
  660.4 10.4 %collective-permute-done.58 = bf16[1,256,1408]{2,1,0:T(8,128)(2,1)} collective-permute-done((bf16[1,256,1408]{2,1,0:T(8,128)(2,1)S(1)}, bf16[1,256,1408]{2,1,0:T(8,128)(2,1)}, u32[]{:S(2)}, u32[]{:S(2)}) %collective-permute-start.58) | collective-permute-done | bytes 720928 | tf_op jit(solution)/shard_map/ppermute | solution.py:20
  673.2 8.8 %collective-permute-done.54 = bf16[128,2048]{1,0:T(8,128)(2,1)} collective-permute-done((bf16[128,2048]{1,0:T(8,128)(2,1)}, bf16[128,2048]{1,0:T(8,128)(2,1)}, u32[]{:S(2)}, u32[]{:S(2)}) %collective-permute-start.54) | collective-permute-done | bytes 524320 | tf_op jit(solution)/shard_map/ppermute | solution.py:20
  716.5 11.2 %collective-permute-done.63 = f32[49,512]{1,0:T(8,128)S(1)} collective-permute-done((f32[49,512]{1,0:T(8,128)S(1)}, f32[49,512]{1,0:T(8,128)S(1)}, u32[]{:S(2)}, u32[]{:S(2)}) %collective-permute-start.63) | collective-permute-done | bytes 100384 | tf_op jit(solution)/shard_map/ppermute | solution.py:20
  739.8 9.4 %collective-permute-done.67 = bf16[1,256,1536]{2,1,0:T(8,128)(2,1)S(1)} collective-permute-done((bf16[1,256,1536]{2,1,0:T(8,128)(2,1)S(1)}, bf16[1,256,1536]{2,1,0:T(8,128)(2,1)S(1)}, u32[]{:S(2)}, u32[]{:S(2)}) %collective-permute-start.67) | collective-permute-done | bytes 786464 | tf_op jit(solution)/shard_map/ppermute | solution.py:20
  (513 shorter events, 361.6 us)
Async XLA Ops:
  7.2 115.9 %all-gather.5.cloned.1.call-start = ((), (), s32[]{:S(2)}) async-start(), calls=%async_computation.6 | async-start | bytes 7077888 | tf_op jit(solution)/shard_map/all_gather | solution.py:238
  26.8 245.5 %all-gather.7.cloned.1.call-start = ((), (), s32[]{:S(2)}) async-start(), calls=%async_computation.7 | async-start | bytes 6488064 | tf_op jit(solution)/shard_map/all_gather | solution.py:238
  28.2 27.1 %collective-permute-start.5 = (bf16[128,1024]{1,0:T(8,128)(2,1)}, bf16[128,1024]{1,0:T(8,128)(2,1)}, u32[]{:S(2)}, u32[]{:S(2)}) collective-permute-start(bf16[128,1024]{1,0:T(8,128)(2,1)} %dynamic_slice.191), channel_id=1, source_target_pairs={{0,4},{2,6},{4,0},{6,2},{1,5},{3,7},{5,1},{7,3},{8,12},{10,14},{12... | collective-permute-start | bytes 786440 | tf_op jit(solution)/shard_map/ppermute | solution.py:20
  30.7 44.1 %collective-permute-start.6 = (bf16[128,1024]{1,0:T(8,128)(2,1)}, bf16[128,1024]{1,0:T(8,128)(2,1)}, u32[]{:S(2)}, u32[]{:S(2)}) collective-permute-start(bf16[128,1024]{1,0:T(8,128)(2,1)} %dynamic_slice.191), channel_id=1, source_target_pairs={{0,2},{2,4},{4,6},{6,0},{1,3},{3,5},{5,7},{7,1},{8,10},{10,12},{12... | collective-permute-start | bytes 786440 | tf_op jit(solution)/shard_map/ppermute | solution.py:20
  35.5 41.9 %collective-permute-start.2 = (bf16[1,136,2048]{2,1,0:T(8,128)(2,1)S(1)}, bf16[1,136,2048]{2,1,0:T(8,128)(2,1)}, u32[]{:S(2)}, u32[]{:S(2)}) collective-permute-start(bf16[1,136,2048]{2,1,0:T(8,128)(2,1)S(1)} %get-tuple-element.535), channel_id=1, source_target_pairs={{0,1},{1,0},{2,3},{3,2},{4,5},{5,4},{6,7},{7,6},{8,9},{9,8},{10,11... | collective-permute-start | bytes 1671176 | tf_op jit(solution)/shard_map/ppermute | solution.py:20
  36.4 41.0 %collective-permute-start.3 = (bf16[1,136,2048]{2,1,0:T(8,128)(2,1)}, bf16[1,136,2048]{2,1,0:T(8,128)(2,1)}, u32[]{:S(2)}, u32[]{:S(2)}) collective-permute-start(bf16[1,136,2048]{2,1,0:T(8,128)(2,1)} %get-tuple-element.537), channel_id=1, source_target_pairs={{0,16},{16,0},{1,17},{17,1},{2,18},{18,2},{3,19},{19,3},{4,20},{20... | collective-permute-start | bytes 1671176 | tf_op jit(solution)/shard_map/ppermute | solution.py:20
  82.8 229.3 %all-gather.11.cloned.1.call-start = ((), (), s32[]{:S(2)}) async-start(), calls=%async_computation.9 | async-start | bytes 6488064 | tf_op jit(solution)/shard_map/all_gather | solution.py:238
  84.1 30.3 %collective-permute-start.8 = (bf16[2,1,136,2048]{3,2,0,1:T(8,128)(2,1)}, bf16[2,1,136,2048]{3,2,0,1:T(8,128)(2,1)S(1)}, u32[]{:S(2)}, u32[]{:S(2)}) collective-permute-start(bf16[2,1,136,2048]{3,2,0,1:T(8,128)(2,1)} %pad_maximum_fusion.15), channel_id=1, source_target_pairs={{0,1},{1,0},{2,3},{3,2},{4,5},{5,4},{6,7},{7,6},{8,9},{9,8},{10,11... | collective-permute-start | bytes 3342344 | tf_op jit(solution)/shard_map/ppermute | solution.py:20
  92.8 42.0 %collective-permute-start.10 = (bf16[1,256,1024]{2,1,0:T(8,128)(2,1)S(1)}, bf16[1,256,1024]{2,1,0:T(8,128)(2,1)}, u32[]{:S(2)}, u32[]{:S(2)}) collective-permute-start(bf16[1,256,1024]{2,1,0:T(8,128)(2,1)S(1)} %get-tuple-element.572), channel_id=1, source_target_pairs={{0,1},{1,0},{2,3},{3,2},{4,5},{5,4},{6,7},{7,6},{8,9},{9,8},{10,11... | collective-permute-start | bytes 1572872 | tf_op jit(solution)/shard_map/ppermute | solution.py:20
  92.9 42.0 %collective-permute-start.11 = (bf16[1,256,1024]{2,1,0:T(8,128)(2,1)S(1)}, bf16[1,256,1024]{2,1,0:T(8,128)(2,1)}, u32[]{:S(2)}, u32[]{:S(2)}) collective-permute-start(bf16[1,256,1024]{2,1,0:T(8,128)(2,1)S(1)} %get-tuple-element.574), channel_id=1, source_target_pairs={{0,16},{16,0},{1,17},{17,1},{2,18},{18,2},{3,19},{19,3},{4,20},{20... | collective-permute-start | bytes 1572872 | tf_op jit(solution)/shard_map/ppermute | solution.py:20
  101.1 38.1 %collective-permute-start.9 = (bf16[256,1408]{1,0:T(8,128)(2,1)}, bf16[256,1408]{1,0:T(8,128)(2,1)}, u32[]{:S(2)}, u32[]{:S(2)}) collective-permute-start(bf16[256,1408]{1,0:T(8,128)(2,1)} %concatenate.268), channel_id=1, source_target_pairs={{0,1},{9,8},{2,3},{11,10},{4,5},{13,12},{6,7},{15,14},{16,17},{25,... | collective-permute-start | bytes 2162696 | tf_op jit(solution)/shard_map/ppermute | solution.py:192
  141.5 205.6 %all-gather.9.cloned.1.call-start = ((), (), s32[]{:S(2)}) async-start(), calls=%async_computation.8 | async-start | bytes 6488064 | tf_op jit(solution)/shard_map/all_gather | solution.py:238
  148.7 33.2 %collective-permute-start.16 = (bf16[2,1,256,1024]{3,2,0,1:T(8,128)(2,1)}, bf16[2,1,256,1024]{3,2,0,1:T(8,128)(2,1)}, u32[]{:S(2)}, u32[]{:S(2)}) collective-permute-start(bf16[2,1,256,1024]{3,2,0,1:T(8,128)(2,1)} %pad_maximum_fusion.20), channel_id=1, source_target_pairs={{0,1},{1,0},{2,3},{3,2},{4,5},{5,4},{6,7},{7,6},{8,9},{9,8},{10,11... | collective-permute-start | bytes 3145736 | tf_op jit(solution)/shard_map/ppermute | solution.py:20
  187.8 57.9 %collective-permute-start.21 = (bf16[2048,1024]{1,0:T(8,128)(2,1)}, bf16[2048,1024]{1,0:T(8,128)(2,1)}, u32[]{:S(2)}, u32[]{:S(2)}) collective-permute-start(bf16[2048,1024]{1,0:T(8,128)(2,1)} %bitcast.58), channel_id=1, source_target_pairs={{0,8},{8,0},{1,9},{9,1},{2,10},{10,2},{3,11},{11,3},{4,12},{12,4},... | collective-permute-start | bytes 12582920 | tf_op jit(solution)/shard_map/ppermute | solution.py:20
  195.6 288.1 %reduce-scatter.7.cloned.1.call-start = ((), (), s32[]{:S(2)}) async-start(), calls=%async_computation.10 | async-start | bytes 6488064 | tf_op jit(solution)/shard_map/reduce_scatter | solution.py:242
  238.7 30.8 %collective-permute-start.26 = (bf16[2,1,128,2048]{3,2,0,1:T(8,128)(2,1)S(1)}, bf16[2,1,128,2048]{3,2,0,1:T(8,128)(2,1)S(1)}, u32[]{:S(2)}, u32[]{:S(2)}) collective-permute-start(bf16[2,1,128,2048]{3,2,0,1:T(8,128)(2,1)S(1)} %bitcast.413), channel_id=1, source_target_pairs={{0,16},{16,0},{1,17},{17,1},{2,18},{18,2},{3,19},{19,3},{4,20},{20... | collective-permute-start | bytes 3145736 | tf_op jit(solution)/shard_map/ppermute | solution.py:20
  241.1 28.5 %collective-permute-start.27 = (bf16[2,1,128,2048]{3,2,0,1:T(8,128)(2,1)S(1)}, bf16[2,1,128,2048]{3,2,0,1:T(8,128)(2,1)S(1)}, u32[]{:S(2)}, u32[]{:S(2)}) collective-permute-start(bf16[2,1,128,2048]{3,2,0,1:T(8,128)(2,1)S(1)} %pad_maximum_fusion.22), channel_id=1, source_target_pairs={{0,1},{1,0},{2,3},{3,2},{4,5},{5,4},{6,7},{7,6},{8,9},{9,8},{10,11... | collective-permute-start | bytes 3145736 | tf_op jit(solution)/shard_map/ppermute | solution.py:20
  347.0 256.7 %reduce-scatter.9.cloned.1.call-start = ((), (), s32[]{:S(2)}) async-start(), calls=%async_computation.11 | async-start | bytes 6488064 | tf_op jit(solution)/shard_map/reduce_scatter | solution.py:242
  394.8 292.6 %reduce-scatter.11.cloned.1.call-start = ((), (), s32[]{:S(2)}) async-start(), calls=%async_computation.12 | async-start | bytes 6488064 | tf_op jit(solution)/shard_map/reduce_scatter | solution.py:242
  447.9 239.5 %reduce-scatter.13.cloned.1.call-start = ((), (), s32[]{:S(2)}) async-start(), calls=%async_computation.13 | async-start | bytes 2359296 | tf_op jit(solution)/shard_map/reduce_scatter | solution.py:242
  482.6 54.9 %collective-permute-start.42 = (bf16[2,1,128,2048]{3,2,0,1:T(8,128)(2,1)}, bf16[2,1,128,2048]{3,2,0,1:T(8,128)(2,1)}, u32[]{:S(2)}, u32[]{:S(2)}) collective-permute-start(bf16[2,1,128,2048]{3,2,0,1:T(8,128)(2,1)} %pad_maximum_fusion.25), channel_id=1, source_target_pairs={{0,16},{16,0},{1,17},{17,1},{2,18},{18,2},{3,19},{19,3},{4,20},{20... | collective-permute-start | bytes 3145736 | tf_op jit(solution)/shard_map/ppermute | solution.py:20
  483.5 54.0 %collective-permute-start.43 = (bf16[2,1,128,2048]{3,2,0,1:T(8,128)(2,1)}, bf16[2,1,128,2048]{3,2,0,1:T(8,128)(2,1)}, u32[]{:S(2)}, u32[]{:S(2)}) collective-permute-start(bf16[2,1,128,2048]{3,2,0,1:T(8,128)(2,1)} %bitcast.409), channel_id=1, source_target_pairs={{0,1},{1,0},{2,3},{3,2},{4,5},{5,4},{6,7},{7,6},{8,9},{9,8},{10,11... | collective-permute-start | bytes 3145736 | tf_op jit(solution)/shard_map/ppermute | solution.py:20
  546.3 159.8 %reduce-scatter.15.cloned.1.call-start = ((), (), s32[]{:S(2)}) async-start(), calls=%async_computation.14 | async-start | bytes 2359296 | tf_op jit(solution)/shard_map/reduce_scatter | solution.py:242
  547.0 159.1 %reduce-scatter.17.cloned.1.call-start = ((), (), s32[]{:S(2)}) async-start(), calls=%async_computation.15 | async-start | bytes 4718592 | tf_op jit(solution)/shard_map/reduce_scatter | solution.py:242
  559.9 26.7 %collective-permute-start.47 = (bf16[2,136,2048]{2,1,0:T(8,128)(2,1)S(1)}, bf16[2,136,2048]{2,1,0:T(8,128)(2,1)S(1)}, u32[]{:S(2)}, u32[]{:S(2)}) collective-permute-start(bf16[2,136,2048]{2,1,0:T(8,128)(2,1)S(1)} %get-tuple-element.831), channel_id=1, source_target_pairs={{0,1},{1,0},{2,3},{3,2},{4,5},{5,4},{6,7},{7,6},{8,9},{9,8},{10,11... | collective-permute-start | bytes 3342344 | tf_op jit(solution)/shard_map/ppermute | solution.py:20
  559.9 41.2 %collective-permute-start.48 = (bf16[2,136,2048]{2,1,0:T(8,128)(2,1)S(1)}, bf16[2,136,2048]{2,1,0:T(8,128)(2,1)S(1)}, u32[]{:S(2)}, u32[]{:S(2)}) collective-permute-start(bf16[2,136,2048]{2,1,0:T(8,128)(2,1)S(1)} %bitcast.443), channel_id=1, source_target_pairs={{0,16},{16,0},{1,17},{17,1},{2,18},{18,2},{3,19},{19,3},{4,20},{20... | collective-permute-start | bytes 3342344 | tf_op jit(solution)/shard_map/ppermute | solution.py:20
  572.0 76.5 %collective-permute-start.45 = (bf16[2,128,2048]{2,1,0:T(8,128)(2,1)}, bf16[2,128,2048]{2,1,0:T(8,128)(2,1)}, u32[]{:S(2)}, u32[]{:S(2)}) collective-permute-start(bf16[2,128,2048]{2,1,0:T(8,128)(2,1)} %get-tuple-element.826), channel_id=1, source_target_pairs={{0,1},{1,0},{2,3},{3,2},{4,5},{5,4},{6,7},{7,6},{8,9},{9,8},{10,11... | collective-permute-start | bytes 3145736 | tf_op jit(solution)/shard_map/ppermute | solution.py:20
  572.0 76.5 %collective-permute-start.46 = (bf16[2,128,2048]{2,1,0:T(8,128)(2,1)}, bf16[2,128,2048]{2,1,0:T(8,128)(2,1)}, u32[]{:S(2)}, u32[]{:S(2)}) collective-permute-start(bf16[2,128,2048]{2,1,0:T(8,128)(2,1)} %bitcast.171), channel_id=1, source_target_pairs={{0,16},{16,0},{1,17},{17,1},{2,18},{18,2},{3,19},{19,3},{4,20},{20... | collective-permute-start | bytes 3145736 | tf_op jit(solution)/shard_map/ppermute | solution.py:20
  578.4 62.4 %collective-permute-start.51 = (bf16[2,1,256,1408]{3,2,0,1:T(8,128)(2,1)}, bf16[2,1,256,1408]{3,2,0,1:T(8,128)(2,1)}, u32[]{:S(2)}, u32[]{:S(2)}) collective-permute-start(bf16[2,1,256,1408]{3,2,0,1:T(8,128)(2,1)} %pad_maximum_fusion.12), channel_id=1, source_target_pairs={{0,8},{8,0},{1,9},{9,1},{2,10},{10,2},{3,11},{11,3},{4,12},{12,4},... | collective-permute-start | bytes 4325384 | tf_op jit(solution)/shard_map/ppermute | solution.py:20
  606.7 28.3 %collective-permute-start.52 = (bf16[136,2048]{1,0:T(8,128)(2,1)}, bf16[136,2048]{1,0:T(8,128)(2,1)}, u32[]{:S(2)}, u32[]{:S(2)}) collective-permute-start(bf16[136,2048]{1,0:T(8,128)(2,1)} %get-tuple-element.852), channel_id=1, source_target_pairs={{0,16},{16,0},{1,17},{17,1},{2,18},{18,2},{3,19},{19,3},{4,20},{20... | collective-permute-start | bytes 1671176 | tf_op jit(solution)/shard_map/ppermute | solution.py:20
  607.8 29.2 %collective-permute-start.53 = (bf16[136,2048]{1,0:T(8,128)(2,1)}, bf16[136,2048]{1,0:T(8,128)(2,1)}, u32[]{:S(2)}, u32[]{:S(2)}) collective-permute-start(bf16[136,2048]{1,0:T(8,128)(2,1)} %get-tuple-element.854), channel_id=1, source_target_pairs={{0,1},{1,0},{2,3},{3,2},{4,5},{5,4},{6,7},{7,6},{8,9},{9,8},{10,11... | collective-permute-start | bytes 1671176 | tf_op jit(solution)/shard_map/ppermute | solution.py:20
  654.8 27.3 %collective-permute-start.54 = (bf16[128,2048]{1,0:T(8,128)(2,1)}, bf16[128,2048]{1,0:T(8,128)(2,1)}, u32[]{:S(2)}, u32[]{:S(2)}) collective-permute-start(bf16[128,2048]{1,0:T(8,128)(2,1)} %get-tuple-element.881), channel_id=1, source_target_pairs={{0,16},{16,0},{1,17},{17,1},{2,18},{18,2},{3,19},{19,3},{4,20},{20... | collective-permute-start | bytes 1572872 | tf_op jit(solution)/shard_map/ppermute | solution.py:20
  (107 other events, 1122.8 us)
Sparse Core Ops, SparseCore 0:
  26.9 77.6 all-gather.4
  106.3 61.5 all-gather.6
  170.0 66.9 all-gather.10
  238.5 62.1 all-gather.8
  347.1 69.9 reduce-scatter.6
  419.8 73.5 reduce-scatter.8
  496.3 62.1 reduce-scatter.10
  560.8 30.7 reduce-scatter.12
  593.9 34.5 reduce-scatter.14
  631.2 52.5 reduce-scatter.16

commit v7 on v6

--- a/solution.py
+++ b/solution.py
@@ -705,9 +705,9 @@
     held = run(lambda own, got: by_z([own] + got), block_out, out_got)
     normed_move.turn(line)
     w_down = gather_tile(run(row_block, down_weight))
+    out_move = Gather(held[:1], held[1:])
     gate_got = column_moves(run(lambda w: column_pieces(w, 1), gate_weight))
     normed_all = normed_move.end(line)
-    out_move = Gather(held[:1], held[1:])
 
     channels = w_in.shape[1] // 3
     half = channels // 2
@@ -731,10 +731,8 @@
     def project(v, w):
         return dot(v, w, low).reshape(grid[:3] + (local + extra, 3 * channels))
 
+    out_move.turn(line)
     mixed = run(project, normed_all, w_in)
-    out_move.turn(line)
-    w_gate = gather_tile(run(column_block, gate_got))
-    up_got = column_moves(run(lambda w: column_pieces(w, 1), up_weight))
 
     def extend(value, g):
         own = value[..., g * channels : (g + 1) * channels]
@@ -756,15 +754,17 @@
 
     product, state_end = run(multiply, mixed, taps, decay)
     states = [passed(state_end, "z", k) for k in range(1, depth)]
-    w_up = gather_tile(run(column_block, up_got))
-    out_own = out_move.end(line)
-    w_out = [out_own] + moved(out_own, "c", -1)
+    w_gate = gather_tile(run(column_block, gate_got))
 
     def feed_grad(values):
         values = (values.astype(wide) * mask).astype(low)
         return values[: batch // 2], values[batch // 2 :]
 
     feed_move = Gather(*run(feed_grad, cotangent))
+    up_pieces = run(lambda w: column_pieces(w, 1), up_weight)
+    out_own = out_move.end(line)
+    w_out = [out_own] + moved(out_own, "c", -1)
+    feed_move.turn(line)
 
     def combine(parts, rates):
         total = parts[0]
@@ -789,7 +789,10 @@
         convolve, states, mixed, taps, product, decay, residue
     )
     gated_got = swap_slots(gated)
-    feed_move.turn(line)
+    up_got = column_moves(up_pieces)
+    grad_feed_all = feed_move.end(line)
+    w_up = gather_tile(run(column_block, up_got))
+    grad_active = run(dot_t, grad_feed_all, w_down)
 
     def mix(got, weights, values, gain):
         own = jnp.concatenate(
@@ -805,8 +808,6 @@
     middle, scale_two, first, second = run(mix, gated_got, w_out, tokens, feed_gain)
 
     two_move = Gather(first, second)
-    grad_feed_all = feed_move.end(line)
-    grad_active = run(dot_t, grad_feed_all, w_down)
     two_move.turn(line)
     normed_two_all = two_move.end(line)
 
@@ -837,8 +838,8 @@
         )
     )
     gate_mine = scatter_tile(run(dot_w, normed_two_all, grad_gate))
-    down_mine = scatter_tile(run(dot_w, active, grad_feed_all))
     two_back.turn(line)
+    feed_parts = run(lambda a, w: split_sum(dot(a, w, low)), active, w_down)
 
     def middle_back(rest, values, scale, gain, back, weights):
         grad_normed = Scatter.sum(*rest).reshape(batch, local, width)
@@ -862,6 +863,7 @@
         middle_back, two_back.rest(), middle, scale_two, feed_gain, cotangent, w_out
     )
     grad_got = swap_slots(grad_slots)
+    down_mine = scatter_tile(run(dot_w, active, grad_feed_all))
     mix_move = Gather(first, second)
 
     def conv_grads(got, result, value, weights, rates):
@@ -890,12 +892,7 @@
         result = jnp.concatenate([result, jnp.where(opening, earlier, 0.0), rest], axis=3)
         return result.astype(low).reshape(-1, grad.shape[-1])
 
-    def query_back(grad, weights, v):
-        result = short_back(grad, weights[:, :channels])
-        return result, dot_w(v, result)
-
-    grad_mixed_query, query_term = run(query_back, grad_query, taps, normed_all)
-    query_mine = scatter_tile(query_term)
+    feed_back = Scatter(feed_parts)
     up_parts_got = owner_moves(run(owner_parts, up_mine))
 
     def conv_back(signal, grad, rates, amounts, begin, ends_later, value, weights):
@@ -912,30 +909,36 @@
         conv_back, product, grad_conv, decay, residue, start, laters, mixed, taps
     )
 
-    def pair_back(grad, weights, v):
-        result = short_back(grad, weights[:, channels:])
+    grad_mix_all = mix_move.end(line)
+    feed_back.turn(line)
+
+    def in_back(query, pair, weights, v):
+        result = jnp.concatenate(
+            [
+                short_back(query, weights[:, :channels]),
+                short_back(pair, weights[:, channels:]),
+            ],
+            axis=1,
+        )
         return result, dot_w(v, result)
 
-    grad_mixed_pair, pair_term = run(pair_back, grad_pair, taps, normed_all)
-    pair_mine = scatter_tile(pair_term)
+    grad_mixed, in_term = run(in_back, grad_query, grad_pair, taps, normed_all)
+    in_mine = scatter_tile(in_term)
+    one_back = Scatter(run(lambda a, w: split_sum(dot_t(a, w, low)), grad_mixed, w_in))
+    out_mine = scatter_tile(run(dot_w, gated_all, grad_mix_all))
     up_held = run(owner_held, up_parts_got)
     up_got = moved(up_held, "y", -1)
-    grad_mix_all = mix_move.end(line)
-    out_mine = scatter_tile(run(dot_w, gated_all, grad_mix_all))
-    one_back = Scatter(
-        run(
-            lambda a, b, w: split_sum(dot_t(jnp.concatenate([a, b], axis=1), w, low)),
-            grad_mixed_query,
-            grad_mixed_pair,
-            w_in,
-        )
-    )
-
-    feed_parts = run(lambda a, w: split_sum(dot(a, w, low)), active, w_down)
+
+    output = run(
+        lambda rest, values: (
+            mask * (values + Scatter.sum(*rest).reshape(batch, local, width))
+        ).astype(low),
+        feed_back.rest(),
+        middle,
+    )
     up_held = run(stacked, up_held, up_got)
     up_got = moved(up_held, "c", -1)
     one_back.turn(line)
-    feed_back = Scatter(feed_parts)
     gate_got = owner_moves(run(owner_parts, gate_mine))
 
     def tap_sums(query, pair, value):
@@ -960,10 +963,11 @@
     def column_whole(own, got):
         return owner_whole(lax.axis_index("c"), [own] + got, depth)
 
-    grad_up_weight = run(column_whole, up_held, up_got)
     gate_held = run(owner_held, gate_got)
     gate_got = moved(gate_held, "y", -1)
-    feed_back.turn(line)
+    grad_up_weight = run(column_whole, up_held, up_got)
+    down_held = run(lambda v: v[None], down_mine)
+    down_got = moved(down_held, "y", -1)
 
     def tokens_back(grad, extension, values, scale, gain, back, small):
         values = values.astype(wide)
@@ -989,40 +993,22 @@
     gate_got = moved(gate_held, "c", -1)
     small = run(lambda v, got: v + sum(got), small, small_got)
     small_got = moved(small, "z", 1)
-    output = run(
-        lambda rest, values: (
-            mask * (values + Scatter.sum(*rest).reshape(batch, local, width))
-        ).astype(low),
-        feed_back.rest(),
-        middle,
-    )
-    down_rows = down_mine.shape[0]
-    rows_held = run(lambda a, b: jnp.concatenate([a, b])[None], down_mine, out_mine)
-    rows_got = moved(rows_held, "y", -1)
+    down_held = run(lambda own, got: jnp.concatenate([own] + got), down_held, down_got)
+    down_got = moved(down_held, "c", -1)
     grad_gate_weight = run(column_whole, gate_held, gate_got)
     small = run(lambda v, got: v + sum(got), small, small_got)
     small_got = moved(small, "x", -1)
-    parts = run(
-        lambda a, b: owner_parts(jnp.concatenate([a, b], axis=1)), query_mine, pair_mine
-    )
-    in_got = owner_moves(parts)
-    rows_held = run(lambda own, got: jnp.concatenate([own] + got), rows_held, rows_got)
-    rows_got = moved(rows_held, "c", -1)
+    in_got = owner_moves(run(owner_parts, in_mine))
+
+    def rows_whole(own, got):
+        whole = in_order(jnp.swapaxes(in_order(jnp.stack([own] + got), "c"), 0, 1), "y")
+        return whole.reshape(-1, width).astype(wide)
+
+    grad_down = run(rows_whole, down_held, down_got)
     small = run(stacked, small, small_got)
     small_got = moved(small, "y", -1)
     in_held = run(owner_held, in_got)
     in_got = moved(in_held, "y", -1)
-
-    def rows_whole(own, got):
-        whole = in_order(jnp.swapaxes(in_order(jnp.stack([own] + got), "c"), 0, 1), "y")
-        return (
-            whole[:, :, :down_rows].reshape(-1, width).astype(wide),
-            whole[:, :, down_rows:].reshape(-1, width).astype(wide),
-        )
-
-    grad_down, grad_out_weight = run(rows_whole, rows_held, rows_got)
-    in_held = run(stacked, in_held, in_got)
-    in_got = moved(in_held, "c", -1)
     poles = decay.shape[0]
 
     def small_whole(own, got):
@@ -1038,9 +1024,26 @@
     grad_norm_gain, feed_gain_sum, grad_conv_taps, residue_sum, decay_sum = run(
         small_whole, small, small_got
     )
-    grad_in_weight = line.finish(
-        lambda core, own, got: owner_whole(core, [own] + got, count), in_held, in_got
-    )
+    in_held = run(stacked, in_held, in_got)
+    in_got = moved(in_held, "c", -1)
+    out_held = run(lambda v: v[None], out_mine)
+    out_got = moved(out_held, "y", -1)
+    out_held = run(lambda own, got: jnp.concatenate([own] + got), out_held, out_got)
+    out_got = moved(out_held, "c", -1)
+    grad_in_weight = run(
+        lambda own, got: owner_whole(lax.axis_index("c"), [own] + got, count), in_held, in_got
+    )
+
+    def out_whole(core, own, got):
+        ccount = lax.axis_size("c")
+        slots = jnp.stack([own] + got)
+        slots = jnp.stack(
+            [lax.dynamic_index_in_dim(slots, (j - core) % ccount, 0, False) for j in range(ccount)]
+        )
+        whole = in_order(jnp.swapaxes(slots, 0, 1), "y")
+        return whole.reshape(-1, width).astype(wide)
+
+    grad_out_weight = line.finish(out_whole, out_held, out_got)
     return (
         output,
         grad_tokens,

time: 786 us -> 741 us (0.943)
  waiting for transfers between devices: 256 us -> 200 us
  starting transfers between devices: 97 us -> 118 us
  matrix products: 158 us -> 143 us
  other arithmetic: 116 us -> 124 us
    ppermute x50 -> x52, waiting for transfers between devices: 216 us -> 176 us  [turned(): lax.ppermute(value, axis, [(i, (i + by) % length) for i in range(length)])]
    ppermute x6, starting transfers between devices: 11.8 us -> 25.4 us  [passed(): return lax.ppermute(value, axis, pairs)]
    dot_general x6, matrix products: 65.6 us -> 54.5 us  [dot(): return jnp.dot(a, b, preferred_element_type=wide).astype(kind)]
    ppermute x6, waiting for transfers between devices: 21.3 us -> 11.8 us  [passed(): return lax.ppermute(value, axis, pairs)]
    ppermute x6, waiting for transfers between devices: 11.6 us -> 2.56 us  [swap_slots(): line.append(lax.ppermute(slots[sy][sx], ('y', 'x'), pairs))]
    ppermute x50 -> x52, starting transfers between devices: 54.1 us -> 59.9 us  [turned(): lax.ppermute(value, axis, [(i, (i + by) % length) for i in range(length)])]
    dot_general x6 -> x5, matrix products: 45.9 us -> 41.8 us  [dot_w(): lax.dot_general(a, b, (((0,), (0,)), ((), ())), preferred_element_type=wide)]
    unnamed x139 -> x155, local copies, waits for them, and re-layouts: 19.6 us -> 18.9 us
  transfers between devices with their start and end apart: 80 -> 81, of which waited for: 30 -> 32; matrix products, arithmetic and copies ran while one was open for 42% -> 44% of each run, Pallas kernels for 6% -> 7%
where the time goes in v7:
time: 741 us; the launch traced here: 733 us
  waiting for transfers between devices  200 us (27%)
  matrix products  143 us (19%)
  other arithmetic  124 us (17%)
  starting transfers between devices  118 us (16%)
  local copies, waits for them, and re-layouts  74.4 us (10%)
  Pallas kernels  56.8 us (8%)
  between operations  16.3 us (2%)
    ppermute x52, waiting for transfers between devices, turned(): lax.ppermute(value, axis, [(i, (i + by) % length) for i in range(length)])  176 us
    ppermute x52, starting transfers between devices, turned(): lax.ppermute(value, axis, [(i, (i + by) % length) for i in range(length)])  59.9 us
    dot_general x6, matrix products, dot(): return jnp.dot(a, b, preferred_element_type=wide).astype(kind)  54.5 us
    dot_general x6, matrix products, dot_t(): lax.dot_general(a, b, (((1,), (1,)), ((), ())), preferred_element_type=wide)  46.6 us
    dot_general x5, matrix products, dot_w(): lax.dot_general(a, b, (((0,), (0,)), ((), ())), preferred_element_type=wide)  41.8 us
    pallas_call x4, Pallas kernels, conv_call(): pl.pallas_call(kernel, out_shape=results, grid_spec=pltpu.PrefetchScalarG...  35.4 us
    ppermute x6, starting transfers between devices, passed(): return lax.ppermute(value, axis, pairs)  25.4 us
    unnamed x155, local copies, waits for them, and re-layouts  18.9 us
  transfers between devices with their start and end apart: 81, of which 32 were waited for; matrix products, arithmetic and copies ran while one was open for 44% of the time, Pallas kernels for 7%

profile of v7, /device:TPU:9, one launch (start us, length us, event | category | flops | bytes accessed | tf_op | source)
XLA Modules:
  0.0 733.3 jit_solution(15651278936739691979)
XLA Ops:
  37.6 17.8 %collective-permute-done.5 = bf16[128,1024]{1,0:T(8,128)(2,1)} collective-permute-done((bf16[128,1024]{1,0:T(8,128)(2,1)}, bf16[128,1024]{1,0:T(8,128)(2,1)}, u32[]{:S(2)}, u32[]{:S(2)}) %collective-permute-start.5) | collective-permute-done | bytes 262176 | tf_op jit(solution)/shard_map/ppermute | solution.py:20
  55.4 19.5 %collective-permute-done.6 = bf16[128,1024]{1,0:T(8,128)(2,1)} collective-permute-done((bf16[128,1024]{1,0:T(8,128)(2,1)}, bf16[128,1024]{1,0:T(8,128)(2,1)}, u32[]{:S(2)}, u32[]{:S(2)}) %collective-permute-start.6) | collective-permute-done | bytes 262176 | tf_op jit(solution)/shard_map/ppermute | solution.py:20
  84.2 7.4 %collective-permute-start.8 = (bf16[2,1,136,2048]{3,2,0,1:T(8,128)(2,1)}, bf16[2,1,136,2048]{3,2,0,1:T(8,128)(2,1)S(1)}, u32[]{:S(2)}, u32[]{:S(2)}) collective-permute-start(bf16[2,1,136,2048]{3,2,0,1:T(8,128)(2,1)} %pad_maximum_fusion.17), channel_id=1, source_target_pairs={{0,1},{1,0},{2,3},{3,2},{4,5},{5,4},{6,7},{7,6},{8,9},{9,8},{10,11... | collective-permute-start | bytes 3342344 | tf_op jit(solution)/shard_map/ppermute | solution.py:20
  103.2 11.3 %collective-permute-done.8 = bf16[2,1,136,2048]{3,2,0,1:T(8,128)(2,1)S(1)} collective-permute-done((bf16[2,1,136,2048]{3,2,0,1:T(8,128)(2,1)}, bf16[2,1,136,2048]{3,2,0,1:T(8,128)(2,1)S(1)}, u32[]{:S(2)}, u32[]{:S(2)}) %collective-permute-start.8) | collective-permute-done | bytes 1114144 | tf_op jit(solution)/shard_map/ppermute | solution.py:20
  129.9 10.6 %convolution_convert_fusion.4 = bf16[1088,1536]{1,0:T(8,128)(2,1)S(1)} fusion(bf16[1088,2048]{1,0:T(8,128)(2,1)} %bitcast.393, bf16[2048,1536]{1,0:T(8,128)(2,1)} %all-gather.5.cloned.1.call-done), kind=kOutput, calls=%fused_computation.5 | convolution fusion | flops 6846775296 | bytes 14090240 | tf_op jit(solution)/shard_map/dot_general | solution.py:643
  185.7 8.6 %collective-permute-start.22 = (bf16[2048,1024]{1,0:T(8,128)(2,1)}, bf16[2048,1024]{1,0:T(8,128)(2,1)}, u32[]{:S(2)}, u32[]{:S(2)}) collective-permute-start(bf16[2048,1024]{1,0:T(8,128)(2,1)} %bitcast.55), channel_id=1, source_target_pairs={{0,8},{8,0},{1,9},{9,1},{2,10},{10,2},{3,11},{11,3},{4,12},{12,4},... | collective-permute-start | bytes 12582920 | tf_op jit(solution)/shard_map/ppermute | solution.py:20
  201.0 8.8 %shard_map.222 = bf16[4,2,1,128,512]{4,3,2,1,0:T(8,128)(2,1)} custom-call(s32[1]{0:T(128)} %bitcast.41.place_ref, bf16[4,2,1,128,512]{4,3,2,1,0:T(8,128)(2,1)} %fusion.49.signal_ref, f32[16,512]{1,0:T(8,128)} %maximum_bitcast_fusion.11.decay_ref, f32[16,512]{1,0:T(8,128)} %maximum_bitcast_fusion.12.residue_ref, f32[4,16,512]{2,1,0:T(8,128)} %multiply_add_fusion.2.start_ref), custom_call_target="tpu_custom_call" | custom-call | flops 33554432 | bytes 2293760 | tf_op jit(solution)/shard_map/pallas_call | solution.py:560
  226.4 11.8 %fusion.123 = f32[1024,1408]{1,0:T(8,128)} fusion(bf16[1024,2048]{1,0:T(8,128)(2,1)} %bitcast.403, bf16[1408,2048]{1,0:T(8,128)(2,1)} %all-gather.7.cloned.1.call-done), kind=kOutput, calls=%fused_computation.426 | convolution fusion | flops 5905580032 | bytes 15728640 | tf_op jit(solution)/shard_map/dot_general | solution.py:647
  253.0 6.8 collective-permute-done.26
  262.7 16.7 %collective-permute-done.28 = bf16[2,1,128,2048]{3,2,0,1:T(8,128)(2,1)S(1)} collective-permute-done((bf16[2,1,128,2048]{3,2,0,1:T(8,128)(2,1)S(1)}, bf16[2,1,128,2048]{3,2,0,1:T(8,128)(2,1)S(1)}, u32[]{:S(2)}, u32[]{:S(2)}) %collective-permute-start.28) | collective-permute-done | bytes 1048608 | tf_op jit(solution)/shard_map/ppermute | solution.py:20
  284.0 13.2 %multiply_convert_fusion.2 = (bf16[1024,1408]{1,0:T(8,128)(2,1)S(1)}, f32[1024,1408]{1,0:T(8,128)}) fusion(f32[1024,1408]{1,0:T(8,128)} %fusion.123, bf16[1024,2048]{1,0:T(8,128)(2,1)} %bitcast.406, bf16[2048,1408]{1,0:T(8,128)(2,1)} %all-gather.11.cloned.1.call-done), kind=kOutput, calls=%fused_computation.10 | convolution fusion | flops 5914230784 | bytes 24379392 | tf_op jit(solution)/shard_map/dot_general | solution.py:643
  298.8 8.7 %convolution_convert_fusion.3 = bf16[2048,1408]{1,0:T(8,128)(2,1)} fusion(bf16[1024,2048]{1,0:T(8,128)(2,1)S(1)} %bitcast.408, bf16[1024,1408]{1,0:T(8,128)(2,1)S(1)} %get-tuple-element.702), kind=kOutput, calls=%fused_computation.4 | convolution fusion | flops 5908463616 | bytes 12845056 | tf_op jit(solution)/shard_map/dot_general | solution.py:651
  308.3 15.0 %multiply_convert_fusion = (bf16[1024,1408]{1,0:T(8,128)(2,1)S(1)}, bf16[1024,1408]{1,0:T(8,128)(2,1)}) fusion(f32[1024,1408]{1,0:T(8,128)} %get-tuple-element.692, f32[1024,1408]{1,0:T(8,128)} %fusion.123, bf16[1024,2048]{1,0:T(8,128)(2,1)} %bitcast.407, bf16[2048,1408]{1,0:T(8,128)(2,1)} %all-gather.9.cloned.1.call-done), kind=kOutput, calls=%fused_computation.7 | convolution fusion | flops 5924323328 | bytes 27262976 | tf_op jit(solution)/shard_map/dot_general | solution.py:643
  324.9 8.9 %fusion.124 = f32[1024,2048]{1,0:T(8,128)S(1)} fusion(bf16[1024,1408]{1,0:T(8,128)(2,1)S(1)} %get-tuple-element.711, bf16[2048,1408]{1,0:T(8,128)(2,1)} %all-gather.11.cloned.1.call-done), kind=kOutput, calls=%fused_computation.427 | convolution fusion | flops 5905580032 | bytes 17039360 | tf_op jit(solution)/shard_map/dot_general | solution.py:647
  333.8 8.4 %add_convert_fusion = bf16[1024,2048]{1,0:T(8,128)(2,1)S(1)} fusion(f32[1024,2048]{1,0:T(8,128)S(1)} %fusion.124, bf16[1024,1408]{1,0:T(8,128)(2,1)} %copy-done.64, bf16[2048,1408]{1,0:T(8,128)(2,1)S(1)} %copy-done.60), kind=kOutput, calls=%fused_computation | convolution fusion | flops 5909774336 | bytes 21233664 | tf_op jit(solution)/shard_map/dot_general | solution.py:647
  347.8 8.7 %convolution_convert_fusion.2 = bf16[2048,1408]{1,0:T(8,128)(2,1)} fusion(bf16[1024,2048]{1,0:T(8,128)(2,1)S(1)} %bitcast.409, bf16[1024,1408]{1,0:T(8,128)(2,1)S(1)} %copy-done.63), kind=kOutput, calls=%fused_computation.3 | convolution fusion | flops 5908463616 | bytes 12845056 | tf_op jit(solution)/shard_map/dot_general | solution.py:651
  365.0 8.8 %convolution_convert_fusion.6 = bf16[1024,2048]{1,0:T(8,128)(2,1)S(1)} fusion(bf16[1024,1408]{1,0:T(8,128)(2,1)S(1)} %copy-done.61, bf16[1408,2048]{1,0:T(8,128)(2,1)} %all-gather.7.cloned.1.call-done), kind=kOutput, calls=%fused_computation.26 | convolution fusion | flops 5907677184 | bytes 12845056 | tf_op jit(solution)/shard_map/dot_general | solution.py:643
  399.0 8.1 %convolution_convert_fusion.1 = bf16[1408,2048]{1,0:T(8,128)(2,1)} fusion(bf16[1024,1408]{1,0:T(8,128)(2,1)S(1)} %copy-done.61, bf16[1024,2048]{1,0:T(8,128)(2,1)S(1)} %bitcast.404), kind=kOutput, calls=%fused_computation.2 | convolution fusion | flops 5908463616 | bytes 12845056 | tf_op jit(solution)/shard_map/dot_general | solution.py:651
  423.0 14.3 %collective-permute-start.43 = (f32[4,16,512]{2,1,0:T(8,128)}, f32[4,16,512]{2,1,0:T(8,128)S(1)}, u32[]{:S(2)}, u32[]{:S(2)}) collective-permute-start(f32[4,16,512]{2,1,0:T(8,128)} %shard_map.223), channel_id=1, source_target_pairs={{2,0},{4,2},{6,4},{3,1},{5,3},{7,5},{10,8},{12,10},{14,12},{11,9},... | collective-permute-start | bytes 393224 | tf_op jit(solution)/shard_map/ppermute | solution.py:26
  447.2 7.9 %collective-permute-done.44 = f32[4,16,512]{2,1,0:T(8,128)S(1)} collective-permute-done((f32[4,16,512]{2,1,0:T(8,128)}, f32[4,16,512]{2,1,0:T(8,128)S(1)}, u32[]{:S(2)}, u32[]{:S(2)}) %collective-permute-start.44) | collective-permute-done | bytes 131104 | tf_op jit(solution)/shard_map/ppermute | solution.py:26
  462.3 16.8 %shard_map.224 = (bf16[4,2,1,128,512]{4,3,2,1,0:T(8,128)(2,1)}, f32[16,512]{1,0:T(8,128)}, f32[16,512]{1,0:T(8,128)}) custom-call(s32[1]{0:T(128)} %bitcast.41.place_ref, bf16[4,2,1,128,512]{4,3,2,1,0:T(8,128)(2,1)} %fusion.49.signal_ref, bf16[4,2,1,128,512]{4,3,2,1,0:T(8,128)(2,1)} %get-tuple-element.783.signal_ref.grad_ref, ...), custom_call_target="tpu_custom_call" | custom-call | flops 100663296 | bytes 4521984 | tf_op jit(solution)/shard_map/pallas_call | solution.py:560
  501.2 10.5 %convolution_convert_fusion = bf16[2048,1536]{1,0:T(8,128)(2,1)} fusion(bf16[1088,2048]{1,0:T(8,128)(2,1)S(1)} %bitcast.396, bf16[1088,1024]{1,0:T(8,128)(2,1)S(1)} %bitcast.384, bf16[1088,512]{1,0:T(8,128)(2,1)S(1)} %bitcast.392), kind=kOutput, calls=%fused_computation.1 | convolution fusion | flops 6854934528 | bytes 14090240 | tf_op jit(solution)/shard_map/dot_general | solution.py:651
  511.7 10.5 %convolution_convert_fusion.5 = bf16[1088,2048]{1,0:T(8,128)(2,1)S(1)} fusion(bf16[1088,1536]{1,0:T(8,128)(2,1)} %pad_maximum_fusion.7, bf16[2048,1536]{1,0:T(8,128)(2,1)} %all-gather.5.cloned.1.call-done), kind=kOutput, calls=%fused_computation.6 | convolution fusion | flops 6847332352 | bytes 14090240 | tf_op jit(solution)/shard_map/dot_general | solution.py:647
  523.9 6.1 collective-permute-start.48
  536.2 5.9 convolution_convert_fusion.7
  555.6 32.8 %collective-permute-done.51 = bf16[1,256,1408]{2,1,0:T(8,128)(2,1)S(1)} collective-permute-done((bf16[1,256,1408]{2,1,0:T(8,128)(2,1)S(1)}, bf16[1,256,1408]{2,1,0:T(8,128)(2,1)S(1)}, u32[]{:S(2)}, u32[]{:S(2)}) %collective-permute-start.51) | collective-permute-done | bytes 720928 | tf_op jit(solution)/shard_map/ppermute | solution.py:20
  611.5 6.7 collective-permute-start.54
  619.0 6.2 shard_map.225
  641.0 9.7 %collective-permute-done.63 = bf16[1,176,2048]{2,1,0:T(8,128)(2,1)S(1)} collective-permute-done((bf16[1,176,2048]{2,1,0:T(8,128)(2,1)}, bf16[1,176,2048]{2,1,0:T(8,128)(2,1)S(1)}, u32[]{:S(2)}, u32[]{:S(2)}) %collective-permute-start.63) | collective-permute-done | bytes 720928 | tf_op jit(solution)/shard_map/ppermute | solution.py:20
  663.4 7.6 %collective-permute-done.61 = f32[49,512]{1,0:T(8,128)S(1)} collective-permute-done((f32[49,512]{1,0:T(8,128)S(1)}, f32[49,512]{1,0:T(8,128)S(1)}, u32[]{:S(2)}, u32[]{:S(2)}) %collective-permute-start.61) | collective-permute-done | bytes 100384 | tf_op jit(solution)/shard_map/ppermute | solution.py:20
  691.3 13.8 %collective-permute-done.68 = bf16[1,256,1536]{2,1,0:T(8,128)(2,1)S(1)} collective-permute-done((bf16[1,256,1536]{2,1,0:T(8,128)(2,1)S(1)}, bf16[1,256,1536]{2,1,0:T(8,128)(2,1)S(1)}, u32[]{:S(2)}, u32[]{:S(2)}) %collective-permute-start.68) | collective-permute-done | bytes 786464 | tf_op jit(solution)/shard_map/ppermute | solution.py:20
  707.4 7.7 %collective-permute-done.70 = bf16[1,64,2048]{2,1,0:T(8,128)(2,1)S(1)} collective-permute-done((bf16[1,64,2048]{2,1,0:T(8,128)(2,1)}, bf16[1,64,2048]{2,1,0:T(8,128)(2,1)S(1)}, u32[]{:S(2)}, u32[]{:S(2)}) %collective-permute-start.70) | collective-permute-done | bytes 262176 | tf_op jit(solution)/shard_map/ppermute | solution.py:20
  (529 shorter events, 361.5 us)
Async XLA Ops:
  7.2 122.7 %all-gather.5.cloned.1.call-start = ((), (), s32[]{:S(2)}) async-start(), calls=%async_computation.5 | async-start | bytes 7077888 | tf_op jit(solution)/shard_map/all_gather | solution.py:238
  26.8 199.5 %all-gather.7.cloned.1.call-start = ((), (), s32[]{:S(2)}) async-start(), calls=%async_computation.6 | async-start | bytes 6488064 | tf_op jit(solution)/shard_map/all_gather | solution.py:238
  28.3 27.1 %collective-permute-start.5 = (bf16[128,1024]{1,0:T(8,128)(2,1)}, bf16[128,1024]{1,0:T(8,128)(2,1)}, u32[]{:S(2)}, u32[]{:S(2)}) collective-permute-start(bf16[128,1024]{1,0:T(8,128)(2,1)} %dynamic_slice.204), channel_id=1, source_target_pairs={{0,4},{2,6},{4,0},{6,2},{1,5},{3,7},{5,1},{7,3},{8,12},{10,14},{12... | collective-permute-start | bytes 786440 | tf_op jit(solution)/shard_map/ppermute | solution.py:20
  30.7 44.1 %collective-permute-start.6 = (bf16[128,1024]{1,0:T(8,128)(2,1)}, bf16[128,1024]{1,0:T(8,128)(2,1)}, u32[]{:S(2)}, u32[]{:S(2)}) collective-permute-start(bf16[128,1024]{1,0:T(8,128)(2,1)} %dynamic_slice.204), channel_id=1, source_target_pairs={{0,2},{2,4},{4,6},{6,0},{1,3},{3,5},{5,7},{7,1},{8,10},{10,12},{12... | collective-permute-start | bytes 786440 | tf_op jit(solution)/shard_map/ppermute | solution.py:20
  35.5 41.9 %collective-permute-start.2 = (bf16[1,136,2048]{2,1,0:T(8,128)(2,1)S(1)}, bf16[1,136,2048]{2,1,0:T(8,128)(2,1)}, u32[]{:S(2)}, u32[]{:S(2)}) collective-permute-start(bf16[1,136,2048]{2,1,0:T(8,128)(2,1)S(1)} %get-tuple-element.539), channel_id=1, source_target_pairs={{0,1},{1,0},{2,3},{3,2},{4,5},{5,4},{6,7},{7,6},{8,9},{9,8},{10,11... | collective-permute-start | bytes 1671176 | tf_op jit(solution)/shard_map/ppermute | solution.py:20
  36.4 41.0 %collective-permute-start.3 = (bf16[1,136,2048]{2,1,0:T(8,128)(2,1)}, bf16[1,136,2048]{2,1,0:T(8,128)(2,1)}, u32[]{:S(2)}, u32[]{:S(2)}) collective-permute-start(bf16[1,136,2048]{2,1,0:T(8,128)(2,1)} %get-tuple-element.541), channel_id=1, source_target_pairs={{0,16},{16,0},{1,17},{17,1},{2,18},{18,2},{3,19},{19,3},{4,20},{20... | collective-permute-start | bytes 1671176 | tf_op jit(solution)/shard_map/ppermute | solution.py:20
  82.8 201.2 %all-gather.11.cloned.1.call-start = ((), (), s32[]{:S(2)}) async-start(), calls=%async_computation.8 | async-start | bytes 6488064 | tf_op jit(solution)/shard_map/all_gather | solution.py:238
  84.2 30.3 %collective-permute-start.8 = (bf16[2,1,136,2048]{3,2,0,1:T(8,128)(2,1)}, bf16[2,1,136,2048]{3,2,0,1:T(8,128)(2,1)S(1)}, u32[]{:S(2)}, u32[]{:S(2)}) collective-permute-start(bf16[2,1,136,2048]{3,2,0,1:T(8,128)(2,1)} %pad_maximum_fusion.17), channel_id=1, source_target_pairs={{0,1},{1,0},{2,3},{3,2},{4,5},{5,4},{6,7},{7,6},{8,9},{9,8},{10,11... | collective-permute-start | bytes 3342344 | tf_op jit(solution)/shard_map/ppermute | solution.py:20
  93.4 29.8 %collective-permute-start.10 = (bf16[1,256,1024]{2,1,0:T(8,128)(2,1)S(1)}, bf16[1,256,1024]{2,1,0:T(8,128)(2,1)}, u32[]{:S(2)}, u32[]{:S(2)}) collective-permute-start(bf16[1,256,1024]{2,1,0:T(8,128)(2,1)S(1)} %get-tuple-element.569), channel_id=1, source_target_pairs={{0,16},{16,0},{1,17},{17,1},{2,18},{18,2},{3,19},{19,3},{4,20},{20... | collective-permute-start | bytes 1572872 | tf_op jit(solution)/shard_map/ppermute | solution.py:20
  93.7 32.0 %collective-permute-start.9 = (bf16[1,256,1024]{2,1,0:T(8,128)(2,1)S(1)}, bf16[1,256,1024]{2,1,0:T(8,128)(2,1)}, u32[]{:S(2)}, u32[]{:S(2)}) collective-permute-start(bf16[1,256,1024]{2,1,0:T(8,128)(2,1)S(1)} %get-tuple-element.567), channel_id=1, source_target_pairs={{0,1},{1,0},{2,3},{3,2},{4,5},{5,4},{6,7},{7,6},{8,9},{9,8},{10,11... | collective-permute-start | bytes 1572872 | tf_op jit(solution)/shard_map/ppermute | solution.py:20
  101.7 48.6 %collective-permute-start.14 = (bf16[256,1408]{1,0:T(8,128)(2,1)}, bf16[256,1408]{1,0:T(8,128)(2,1)}, u32[]{:S(2)}, u32[]{:S(2)}) collective-permute-start(bf16[256,1408]{1,0:T(8,128)(2,1)} %concatenate.265), channel_id=1, source_target_pairs={{0,1},{9,8},{2,3},{11,10},{4,5},{13,12},{6,7},{15,14},{16,17},{25,... | collective-permute-start | bytes 2162696 | tf_op jit(solution)/shard_map/ppermute | solution.py:192
  152.7 155.6 %all-gather.9.cloned.1.call-start = ((), (), s32[]{:S(2)}) async-start(), calls=%async_computation.7 | async-start | bytes 6488064 | tf_op jit(solution)/shard_map/all_gather | solution.py:238
  154.2 40.4 %collective-permute-start.11 = (f32[4,16,512]{2,1,0:T(8,128)S(1)}, f32[4,16,512]{2,1,0:T(8,128)}, u32[]{:S(2)}, u32[]{:S(2)}) collective-permute-start(f32[4,16,512]{2,1,0:T(8,128)S(1)} %copy-done.46), channel_id=1, source_target_pairs={{0,2},{2,4},{4,6},{1,3},{3,5},{5,7},{8,10},{10,12},{12,14},{9,11},... | collective-permute-start | bytes 393224 | tf_op jit(solution)/shard_map/ppermute | solution.py:26
  159.2 35.3 %collective-permute-start.12 = (f32[4,16,512]{2,1,0:T(8,128)S(1)}, f32[4,16,512]{2,1,0:T(8,128)}, u32[]{:S(2)}, u32[]{:S(2)}) collective-permute-start(f32[4,16,512]{2,1,0:T(8,128)S(1)} %copy-done.46), channel_id=1, source_target_pairs={{0,4},{2,6},{1,5},{3,7},{8,12},{10,14},{9,13},{11,15},{16,20},{18,... | collective-permute-start | bytes 393224 | tf_op jit(solution)/shard_map/ppermute | solution.py:26
  161.2 33.4 %collective-permute-start.13 = (f32[4,16,512]{2,1,0:T(8,128)S(1)}, f32[4,16,512]{2,1,0:T(8,128)}, u32[]{:S(2)}, u32[]{:S(2)}) collective-permute-start(f32[4,16,512]{2,1,0:T(8,128)S(1)} %copy-done.46), channel_id=1, source_target_pairs={{0,6},{1,7},{8,14},{9,15},{16,22},{17,23},{24,30},{25,31}} | collective-permute-start | bytes 393224 | tf_op jit(solution)/shard_map/ppermute | solution.py:26
  184.2 39.9 %collective-permute-start.25 = (bf16[256,1408]{1,0:T(8,128)(2,1)}, bf16[256,1408]{1,0:T(8,128)(2,1)}, u32[]{:S(2)}, u32[]{:S(2)}) collective-permute-start(bf16[256,1408]{1,0:T(8,128)(2,1)} %concatenate.274), channel_id=1, source_target_pairs={{0,1},{9,8},{2,3},{11,10},{4,5},{13,12},{6,7},{15,14},{16,17},{25,... | collective-permute-start | bytes 2162696 | tf_op jit(solution)/shard_map/ppermute | solution.py:192
  185.7 53.0 %collective-permute-start.22 = (bf16[2048,1024]{1,0:T(8,128)(2,1)}, bf16[2048,1024]{1,0:T(8,128)(2,1)}, u32[]{:S(2)}, u32[]{:S(2)}) collective-permute-start(bf16[2048,1024]{1,0:T(8,128)(2,1)} %bitcast.55), channel_id=1, source_target_pairs={{0,8},{8,0},{1,9},{9,1},{2,10},{10,2},{3,11},{11,3},{4,12},{12,4},... | collective-permute-start | bytes 12582920 | tf_op jit(solution)/shard_map/ppermute | solution.py:20
  212.8 25.9 %collective-permute-start.19 = (bf16[256,512]{1,0:T(8,128)(2,1)}, bf16[256,512]{1,0:T(8,128)(2,1)S(1)}, u32[]{:S(2)}, u32[]{:S(2)}) collective-permute-start(bf16[256,512]{1,0:T(8,128)(2,1)} %bitcast.67), channel_id=1, source_target_pairs={{0,1},{1,0},{16,17},{17,16},{2,3},{3,2},{18,19},{19,18},{4,5},{5,4... | collective-permute-start | bytes 786440 | tf_op jit(solution)/shard_map/ppermute | solution.py:44
  238.2 204.1 %reduce-scatter.6.cloned.1.call-start = ((), (), s32[]{:S(2)}) async-start(), calls=%async_computation.9 | async-start | bytes 6488064 | tf_op jit(solution)/shard_map/reduce_scatter | solution.py:242
  307.5 286.4 %reduce-scatter.8.cloned.1.call-start = ((), (), s32[]{:S(2)}) async-start(), calls=%async_computation.10 | async-start | bytes 6488064 | tf_op jit(solution)/shard_map/reduce_scatter | solution.py:242
  356.5 268.7 %reduce-scatter.10.cloned.1.call-start = ((), (), s32[]{:S(2)}) async-start(), calls=%async_computation.11 | async-start | bytes 6488064 | tf_op jit(solution)/shard_map/reduce_scatter | solution.py:242
  378.7 110.8 %collective-permute-start.32 = (bf16[2,128,2048]{2,1,0:T(8,128)(2,1)}, bf16[2,128,2048]{2,1,0:T(8,128)(2,1)}, u32[]{:S(2)}, u32[]{:S(2)}) collective-permute-start(bf16[2,128,2048]{2,1,0:T(8,128)(2,1)} %get-tuple-element.724), channel_id=1, source_target_pairs={{0,1},{1,0},{2,3},{3,2},{4,5},{5,4},{6,7},{7,6},{8,9},{9,8},{10,11... | collective-permute-start | bytes 3145736 | tf_op jit(solution)/shard_map/ppermute | solution.py:20
  379.8 109.7 %collective-permute-start.33 = (bf16[2,128,2048]{2,1,0:T(8,128)(2,1)}, bf16[2,128,2048]{2,1,0:T(8,128)(2,1)}, u32[]{:S(2)}, u32[]{:S(2)}) collective-permute-start(bf16[2,128,2048]{2,1,0:T(8,128)(2,1)} %bitcast.117), channel_id=1, source_target_pairs={{0,16},{16,0},{1,17},{17,1},{2,18},{18,2},{3,19},{19,3},{4,20},{20... | collective-permute-start | bytes 3145736 | tf_op jit(solution)/shard_map/ppermute | solution.py:20
  407.1 264.0 %reduce-scatter.12.cloned.1.call-start = ((), (), s32[]{:S(2)}) async-start(), calls=%async_computation.12 | async-start | bytes 7077888 | tf_op jit(solution)/shard_map/reduce_scatter | solution.py:242
  407.2 30.2 %collective-permute-start.36 = (bf16[1,128,2048]{2,1,0:T(8,128)(2,1)S(1)}, bf16[1,128,2048]{2,1,0:T(8,128)(2,1)S(1)}, u32[]{:S(2)}, u32[]{:S(2)}) collective-permute-start(bf16[1,128,2048]{2,1,0:T(8,128)(2,1)S(1)} %get-tuple-element.767), channel_id=1, source_target_pairs={{0,1},{1,0},{2,3},{3,2},{4,5},{5,4},{6,7},{7,6},{8,9},{9,8},{10,11... | collective-permute-start | bytes 1572872 | tf_op jit(solution)/shard_map/ppermute | solution.py:20
  408.0 30.7 %collective-permute-start.37 = (bf16[1,128,2048]{2,1,0:T(8,128)(2,1)S(1)}, bf16[1,128,2048]{2,1,0:T(8,128)(2,1)S(1)}, u32[]{:S(2)}, u32[]{:S(2)}) collective-permute-start(bf16[1,128,2048]{2,1,0:T(8,128)(2,1)S(1)} %get-tuple-element.769), channel_id=1, source_target_pairs={{0,16},{16,0},{1,17},{17,1},{2,18},{18,2},{3,19},{19,3},{4,20},{20... | collective-permute-start | bytes 1572872 | tf_op jit(solution)/shard_map/ppermute | solution.py:20
  446.1 36.2 %collective-permute-start.41 = (bf16[2,1,128,2048]{3,2,0,1:T(8,128)(2,1)}, bf16[2,1,128,2048]{3,2,0,1:T(8,128)(2,1)}, u32[]{:S(2)}, u32[]{:S(2)}) collective-permute-start(bf16[2,1,128,2048]{3,2,0,1:T(8,128)(2,1)} %pad_maximum_fusion.26), channel_id=1, source_target_pairs={{0,16},{16,0},{1,17},{17,1},{2,18},{18,2},{3,19},{19,3},{4,20},{20... | collective-permute-start | bytes 3145736 | tf_op jit(solution)/shard_map/ppermute | solution.py:20
  455.0 27.3 %collective-permute-start.42 = (bf16[2,1,128,2048]{3,2,0,1:T(8,128)(2,1)}, bf16[2,1,128,2048]{3,2,0,1:T(8,128)(2,1)}, u32[]{:S(2)}, u32[]{:S(2)}) collective-permute-start(bf16[2,1,128,2048]{3,2,0,1:T(8,128)(2,1)} %bitcast.416), channel_id=1, source_target_pairs={{0,1},{1,0},{2,3},{3,2},{4,5},{5,4},{6,7},{7,6},{8,9},{9,8},{10,11... | collective-permute-start | bytes 3145736 | tf_op jit(solution)/shard_map/ppermute | solution.py:20
  531.6 175.7 %reduce-scatter.14.cloned.1.call-start = ((), (), s32[]{:S(2)}) async-start(), calls=%async_computation.13 | async-start | bytes 2359296 | tf_op jit(solution)/shard_map/reduce_scatter | solution.py:242
  542.1 47.6 %collective-permute-start.49 = (bf16[2,136,2048]{2,1,0:T(8,128)(2,1)}, bf16[2,136,2048]{2,1,0:T(8,128)(2,1)S(1)}, u32[]{:S(2)}, u32[]{:S(2)}) collective-permute-start(bf16[2,136,2048]{2,1,0:T(8,128)(2,1)} %get-tuple-element.846), channel_id=1, source_target_pairs={{0,1},{1,0},{2,3},{3,2},{4,5},{5,4},{6,7},{7,6},{8,9},{9,8},{10,11... | collective-permute-start | bytes 3342344 | tf_op jit(solution)/shard_map/ppermute | solution.py:20
  543.5 46.1 %collective-permute-start.50 = (bf16[2,136,2048]{2,1,0:T(8,128)(2,1)}, bf16[2,136,2048]{2,1,0:T(8,128)(2,1)S(1)}, u32[]{:S(2)}, u32[]{:S(2)}) collective-permute-start(bf16[2,136,2048]{2,1,0:T(8,128)(2,1)} %bitcast.446), channel_id=1, source_target_pairs={{0,16},{16,0},{1,17},{17,1},{2,18},{18,2},{3,19},{19,3},{4,20},{20... | collective-permute-start | bytes 3342344 | tf_op jit(solution)/shard_map/ppermute | solution.py:20
  550.5 37.9 %collective-permute-start.51 = (bf16[1,256,1408]{2,1,0:T(8,128)(2,1)S(1)}, bf16[1,256,1408]{2,1,0:T(8,128)(2,1)S(1)}, u32[]{:S(2)}, u32[]{:S(2)}) collective-permute-start(bf16[1,256,1408]{2,1,0:T(8,128)(2,1)S(1)} %fusion.67), channel_id=1, source_target_pairs={{0,16},{16,0},{1,17},{17,1},{2,18},{18,2},{3,19},{19,3},{4,20},{20... | collective-permute-start | bytes 2162696 | tf_op jit(solution)/shard_map/ppermute | solution.py:20
  (116 other events, 1309.2 us)
Sparse Core Ops, SparseCore 0:
  27.0 77.6 all-gather.4
  106.3 66.0 all-gather.6
  174.6 59.2 all-gather.10
  238.3 69.9 all-gather.8
  311.0 74.4 reduce-scatter.5
  388.2 74.7 reduce-scatter.7
  465.3 62.1 reduce-scatter.9
  531.7 69.7 reduce-scatter.11
  655.9 33.4 reduce-scatter.13

commit v8 on v7

--- a/solution.py
+++ b/solution.py
@@ -702,12 +702,12 @@
         return values[: batch // 2], values[batch // 2 :]
 
     normed_move = Gather(*run(lengthen, normed, before))
-    held = run(lambda own, got: by_z([own] + got), block_out, out_got)
     normed_move.turn(line)
     w_down = gather_tile(run(row_block, down_weight))
+    gate_got = column_moves(run(lambda w: column_pieces(w, 1), gate_weight))
+    held = run(lambda own, got: by_z([own] + got), block_out, out_got)
+    normed_all = normed_move.end(line)
     out_move = Gather(held[:1], held[1:])
-    gate_got = column_moves(run(lambda w: column_pieces(w, 1), gate_weight))
-    normed_all = normed_move.end(line)
 
     channels = w_in.shape[1] // 3
     half = channels // 2
@@ -731,7 +731,6 @@
     def project(v, w):
         return dot(v, w, low).reshape(grid[:3] + (local + extra, 3 * channels))
 
-    out_move.turn(line)
     mixed = run(project, normed_all, w_in)
 
     def extend(value, g):
@@ -755,13 +754,14 @@
     product, state_end = run(multiply, mixed, taps, decay)
     states = [passed(state_end, "z", k) for k in range(1, depth)]
     w_gate = gather_tile(run(column_block, gate_got))
+    out_move.turn(line)
 
     def feed_grad(values):
         values = (values.astype(wide) * mask).astype(low)
         return values[: batch // 2], values[batch // 2 :]
 
     feed_move = Gather(*run(feed_grad, cotangent))
-    up_pieces = run(lambda w: column_pieces(w, 1), up_weight)
+    up_got = column_moves(run(lambda w: column_pieces(w, 1), up_weight))
     out_own = out_move.end(line)
     w_out = [out_own] + moved(out_own, "c", -1)
     feed_move.turn(line)
@@ -789,10 +789,8 @@
         convolve, states, mixed, taps, product, decay, residue
     )
     gated_got = swap_slots(gated)
-    up_got = column_moves(up_pieces)
+    w_up = gather_tile(run(column_block, up_got))
     grad_feed_all = feed_move.end(line)
-    w_up = gather_tile(run(column_block, up_got))
-    grad_active = run(dot_t, grad_feed_all, w_down)
 
     def mix(got, weights, values, gain):
         own = jnp.concatenate(
@@ -808,6 +806,7 @@
     middle, scale_two, first, second = run(mix, gated_got, w_out, tokens, feed_gain)
 
     two_move = Gather(first, second)
+    grad_active = run(dot_t, grad_feed_all, w_down)
     two_move.turn(line)
     normed_two_all = two_move.end(line)
 
@@ -909,6 +908,8 @@
         conv_back, product, grad_conv, decay, residue, start, laters, mixed, taps
     )
 
+    up_held = run(owner_held, up_parts_got)
+    up_got = moved(up_held, "y", -1)
     grad_mix_all = mix_move.end(line)
     feed_back.turn(line)
 
@@ -924,10 +925,13 @@
 
     grad_mixed, in_term = run(in_back, grad_query, grad_pair, taps, normed_all)
     in_mine = scatter_tile(in_term)
+    gate_got = owner_moves(run(owner_parts, gate_mine))
     one_back = Scatter(run(lambda a, w: split_sum(dot_t(a, w, low)), grad_mixed, w_in))
+    up_held = run(stacked, up_held, up_got)
+    up_got = moved(up_held, "c", -1)
     out_mine = scatter_tile(run(dot_w, gated_all, grad_mix_all))
-    up_held = run(owner_held, up_parts_got)
-    up_got = moved(up_held, "y", -1)
+    gate_held = run(owner_held, gate_got)
+    gate_got = moved(gate_held, "y", -1)
 
     output = run(
         lambda rest, values: (
@@ -936,10 +940,6 @@
         feed_back.rest(),
         middle,
     )
-    up_held = run(stacked, up_held, up_got)
-    up_got = moved(up_held, "c", -1)
-    one_back.turn(line)
-    gate_got = owner_moves(run(owner_parts, gate_mine))
 
     def tap_sums(query, pair, value):
         sums = []
@@ -957,17 +957,18 @@
         value = Scatter.sum(*rest).reshape(batch, local + extra, width)
         return value[:, :local], value[:, local : local + 2].astype(low)
 
+    def column_whole(own, got):
+        return owner_whole(lax.axis_index("c"), [own] + got, depth)
+
+    grad_up_weight = run(column_whole, up_held, up_got)
+    one_back.turn(line)
+    down_held = run(lambda v: v[None], down_mine)
+    down_got = moved(down_held, "y", -1)
+    gate_held = run(stacked, gate_held, gate_got)
+    gate_got = moved(gate_held, "c", -1)
     grad_normed, grad_before = run(normed_sum, one_back.rest())
     grad_after = lax.ppermute(grad_before, ("z", "x"), [(j, i) for i, j in last])
-
-    def column_whole(own, got):
-        return owner_whole(lax.axis_index("c"), [own] + got, depth)
-
-    gate_held = run(owner_held, gate_got)
-    gate_got = moved(gate_held, "y", -1)
-    grad_up_weight = run(column_whole, up_held, up_got)
-    down_held = run(lambda v: v[None], down_mine)
-    down_got = moved(down_held, "y", -1)
+    grad_gate_weight = run(column_whole, gate_held, gate_got)
 
     def tokens_back(grad, extension, values, scale, gain, back, small):
         values = values.astype(wide)
@@ -989,15 +990,10 @@
         (grad_feed_gain, grad_residue, grad_decay, grad_taps),
     )
     small_got = moved(small, "c", 1)
-    gate_held = run(stacked, gate_held, gate_got)
-    gate_got = moved(gate_held, "c", -1)
+    down_held = run(lambda own, got: jnp.concatenate([own] + got), down_held, down_got)
+    down_got = moved(down_held, "c", -1)
     small = run(lambda v, got: v + sum(got), small, small_got)
     small_got = moved(small, "z", 1)
-    down_held = run(lambda own, got: jnp.concatenate([own] + got), down_held, down_got)
-    down_got = moved(down_held, "c", -1)
-    grad_gate_weight = run(column_whole, gate_held, gate_got)
-    small = run(lambda v, got: v + sum(got), small, small_got)
-    small_got = moved(small, "x", -1)
     in_got = owner_moves(run(owner_parts, in_mine))
 
     def rows_whole(own, got):
@@ -1005,10 +1001,16 @@
         return whole.reshape(-1, width).astype(wide)
 
     grad_down = run(rows_whole, down_held, down_got)
+    in_held = run(owner_held, in_got)
+    in_got = moved(in_held, "y", -1)
+    small = run(lambda v, got: v + sum(got), small, small_got)
+    small_got = moved(small, "x", -1)
     small = run(stacked, small, small_got)
     small_got = moved(small, "y", -1)
-    in_held = run(owner_held, in_got)
-    in_got = moved(in_held, "y", -1)
+    out_held = run(lambda v: v[None], out_mine)
+    out_got = moved(out_held, "y", -1)
+    in_held = run(stacked, in_held, in_got)
+    in_got = moved(in_held, "c", -1)
     poles = decay.shape[0]
 
     def small_whole(own, got):
@@ -1024,10 +1026,6 @@
     grad_norm_gain, feed_gain_sum, grad_conv_taps, residue_sum, decay_sum = run(
         small_whole, small, small_got
     )
-    in_held = run(stacked, in_held, in_got)
-    in_got = moved(in_held, "c", -1)
-    out_held = run(lambda v: v[None], out_mine)
-    out_got = moved(out_held, "y", -1)
     out_held = run(lambda own, got: jnp.concatenate([own] + got), out_held, out_got)
     out_got = moved(out_held, "c", -1)
     grad_in_weight = run(

time: 741 us -> 725 us (0.978)
  starting transfers between devices: 118 us -> 104 us
    ppermute x52, starting transfers between devices: 59.9 us -> 44.2 us  [turned(): lax.ppermute(value, axis, [(i, (i + by) % length) for i in range(length)])]
    ppermute x52, waiting for transfers between devices: 176 us -> 161 us  [turned(): lax.ppermute(value, axis, [(i, (i + by) % length) for i in range(length)])]
    ppermute x3, waiting for transfers between devices: 3.72 us -> 15.9 us  [owner_moves(): got.append(lax.ppermute(parts[d], ('c', 'x'), pairs))]
    ppermute x6, waiting for transfers between devices: 2.56 us -> 13.5 us  [swap_slots(): line.append(lax.ppermute(slots[sy][sx], ('y', 'x'), pairs))]
    ppermute x3, starting transfers between devices: 13.4 us -> 21.3 us  [owner_moves(): got.append(lax.ppermute(parts[d], ('c', 'x'), pairs))]
    ppermute x6, starting transfers between devices: 25.4 us -> 17.6 us  [passed(): return lax.ppermute(value, axis, pairs)]
    unnamed x155 -> x171, local copies, waits for them, and re-layouts: 18.9 us -> 23.8 us
  transfers between devices with their start and end apart: 81 -> 81, of which waited for: 32 -> 34; matrix products, arithmetic and copies ran while one was open for 44% -> 42% of each run, Pallas kernels for 7% -> 7%
where the time goes in v8:
time: 725 us; the launch traced here: 713 us
  waiting for transfers between devices  207 us (29%)
  matrix products  141 us (19%)
  other arithmetic  119 us (16%)
  starting transfers between devices  104 us (14%)
  local copies, waits for them, and re-layouts  68 us (9%)
  Pallas kernels  57 us (8%)
  between operations  16.4 us (2%)
    ppermute x52, waiting for transfers between devices, turned(): lax.ppermute(value, axis, [(i, (i + by) % length) for i in range(length)])  161 us
    dot_general x6, matrix products, dot(): return jnp.dot(a, b, preferred_element_type=wide).astype(kind)  55 us
    dot_general x6, matrix products, dot_t(): lax.dot_general(a, b, (((1,), (1,)), ((), ())), preferred_element_type=wide)  46.8 us
    ppermute x52, starting transfers between devices, turned(): lax.ppermute(value, axis, [(i, (i + by) % length) for i in range(length)])  44.2 us
    dot_general x5, matrix products, dot_w(): lax.dot_general(a, b, (((0,), (0,)), ((), ())), preferred_element_type=wide)  39.6 us
    pallas_call x4, Pallas kernels, conv_call(): pl.pallas_call(kernel, out_shape=results, grid_spec=pltpu.PrefetchScalarG...  35.4 us
    unnamed x171, local copies, waits for them, and re-layouts  23.8 us
    ppermute x3, starting transfers between devices, owner_moves(): got.append(lax.ppermute(parts[d], ('c', 'x'), pairs))  21.3 us
  transfers between devices with their start and end apart: 81, of which 34 were waited for; matrix products, arithmetic and copies ran while one was open for 42% of the time, Pallas kernels for 7%

profile of v8, /device:TPU:9, one launch (start us, length us, event | category | flops | bytes accessed | tf_op | source)
XLA Modules:
  0.0 712.7 jit_solution(17329327391072925596)
XLA Ops:
  36.0 11.0 %collective-permute-done.2 = bf16[1,136,2048]{2,1,0:T(8,128)(2,1)} collective-permute-done((bf16[1,136,2048]{2,1,0:T(8,128)(2,1)S(1)}, bf16[1,136,2048]{2,1,0:T(8,128)(2,1)}, u32[]{:S(2)}, u32[]{:S(2)}) %collective-permute-start.2) | collective-permute-done | bytes 557088 | tf_op jit(solution)/shard_map/ppermute | solution.py:20
  65.3 12.7 %collective-permute-done.6 = bf16[128,1024]{1,0:T(8,128)(2,1)S(1)} collective-permute-done((bf16[128,1024]{1,0:T(8,128)(2,1)S(1)}, bf16[128,1024]{1,0:T(8,128)(2,1)S(1)}, u32[]{:S(2)}, u32[]{:S(2)}) %collective-permute-start.6) | collective-permute-done | bytes 262176 | tf_op jit(solution)/shard_map/ppermute | solution.py:20
  78.0 10.4 %collective-permute-done.7 = bf16[128,1024]{1,0:T(8,128)(2,1)} collective-permute-done((bf16[128,1024]{1,0:T(8,128)(2,1)S(1)}, bf16[128,1024]{1,0:T(8,128)(2,1)}, u32[]{:S(2)}, u32[]{:S(2)}) %collective-permute-start.7) | collective-permute-done | bytes 262176 | tf_op jit(solution)/shard_map/ppermute | solution.py:20
  88.4 17.9 %collective-permute-done.8 = bf16[128,1024]{1,0:T(8,128)(2,1)} collective-permute-done((bf16[128,1024]{1,0:T(8,128)(2,1)S(1)}, bf16[128,1024]{1,0:T(8,128)(2,1)}, u32[]{:S(2)}, u32[]{:S(2)}) %collective-permute-start.8) | collective-permute-done | bytes 262176 | tf_op jit(solution)/shard_map/ppermute | solution.py:20
  118.8 10.5 %convolution_convert_fusion.4 = bf16[1088,1536]{1,0:T(8,128)(2,1)S(1)} fusion(bf16[1088,2048]{1,0:T(8,128)(2,1)} %bitcast.393, bf16[2048,1536]{1,0:T(8,128)(2,1)} %all-gather.5.cloned.1.call-done), kind=kOutput, calls=%fused_computation.5 | convolution fusion | flops 6846775296 | bytes 14090240 | tf_op jit(solution)/shard_map/dot_general | solution.py:643
  143.9 9.1 %collective-permute-done.12 = bf16[1,256,1024]{2,1,0:T(8,128)(2,1)S(1)} collective-permute-done((bf16[1,256,1024]{2,1,0:T(8,128)(2,1)S(1)}, bf16[1,256,1024]{2,1,0:T(8,128)(2,1)S(1)}, u32[]{:S(2)}, u32[]{:S(2)}) %collective-permute-start.12) | collective-permute-done | bytes 524320 | tf_op jit(solution)/shard_map/ppermute | solution.py:20
  162.8 15.1 %collective-permute-done.17 = bf16[2,1,256,1024]{3,2,0,1:T(8,128)(2,1)} collective-permute-done((bf16[2,1,256,1024]{3,2,0,1:T(8,128)(2,1)}, bf16[2,1,256,1024]{3,2,0,1:T(8,128)(2,1)}, u32[]{:S(2)}, u32[]{:S(2)}) %collective-permute-start.17) | collective-permute-done | bytes 1048608 | tf_op jit(solution)/shard_map/ppermute | solution.py:20
  191.3 10.0 %collective-permute-done.15 = bf16[1,128,2048]{2,1,0:T(8,128)(2,1)S(1)} collective-permute-done((bf16[1,128,2048]{2,1,0:T(8,128)(2,1)S(1)}, bf16[1,128,2048]{2,1,0:T(8,128)(2,1)S(1)}, u32[]{:S(2)}, u32[]{:S(2)}) %collective-permute-start.15) | collective-permute-done | bytes 524320 | tf_op jit(solution)/shard_map/ppermute | solution.py:20
  220.6 8.8 %shard_map.222 = bf16[4,2,1,128,512]{4,3,2,1,0:T(8,128)(2,1)} custom-call(s32[1]{0:T(128)} %bitcast.36.place_ref, bf16[4,2,1,128,512]{4,3,2,1,0:T(8,128)(2,1)} %fusion.49.signal_ref, f32[16,512]{1,0:T(8,128)} %maximum_bitcast_fusion.11.decay_ref, f32[16,512]{1,0:T(8,128)} %maximum_bitcast_fusion.12.residue_ref, f32[4,16,512]{2,1,0:T(8,128)} %multiply_add_fusion.2.start_ref), custom_call_target="tpu_custom_call" | custom-call | flops 33554432 | bytes 2293760 | tf_op jit(solution)/shard_map/pallas_call | solution.py:560
  263.8 12.1 %fusion.123 = f32[1024,1408]{1,0:T(8,128)} fusion(bf16[1024,2048]{1,0:T(8,128)(2,1)} %bitcast.403, bf16[1408,2048]{1,0:T(8,128)(2,1)} %all-gather.7.cloned.1.call-done), kind=kOutput, calls=%fused_computation.426 | convolution fusion | flops 5905580032 | bytes 15728640 | tf_op jit(solution)/shard_map/dot_general | solution.py:647
  277.8 20.6 %collective-permute-done.28 = bf16[2,1,128,2048]{3,2,0,1:T(8,128)(2,1)S(1)} collective-permute-done((bf16[2,1,128,2048]{3,2,0,1:T(8,128)(2,1)S(1)}, bf16[2,1,128,2048]{3,2,0,1:T(8,128)(2,1)S(1)}, u32[]{:S(2)}, u32[]{:S(2)}) %collective-permute-start.28) | collective-permute-done | bytes 1048608 | tf_op jit(solution)/shard_map/ppermute | solution.py:20
  302.6 13.2 %multiply_convert_fusion.2 = (bf16[1024,1408]{1,0:T(8,128)(2,1)S(1)}, f32[1024,1408]{1,0:T(8,128)}) fusion(f32[1024,1408]{1,0:T(8,128)} %fusion.123, bf16[1024,2048]{1,0:T(8,128)(2,1)} %bitcast.406, bf16[2048,1408]{1,0:T(8,128)(2,1)} %all-gather.11.cloned.1.call-done), kind=kOutput, calls=%fused_computation.10 | convolution fusion | flops 5914230784 | bytes 24379392 | tf_op jit(solution)/shard_map/dot_general | solution.py:643
  317.4 8.7 %convolution_convert_fusion.3 = bf16[2048,1408]{1,0:T(8,128)(2,1)} fusion(bf16[1024,2048]{1,0:T(8,128)(2,1)S(1)} %bitcast.408, bf16[1024,1408]{1,0:T(8,128)(2,1)S(1)} %get-tuple-element.702), kind=kOutput, calls=%fused_computation.4 | convolution fusion | flops 5908463616 | bytes 12845056 | tf_op jit(solution)/shard_map/dot_general | solution.py:651
  326.1 15.2 %multiply_convert_fusion = (bf16[1024,1408]{1,0:T(8,128)(2,1)S(1)}, bf16[1024,1408]{1,0:T(8,128)(2,1)}) fusion(f32[1024,1408]{1,0:T(8,128)} %get-tuple-element.692, f32[1024,1408]{1,0:T(8,128)} %fusion.123, bf16[1024,2048]{1,0:T(8,128)(2,1)} %bitcast.407, bf16[2048,1408]{1,0:T(8,128)(2,1)} %all-gather.9.cloned.1.call-done), kind=kOutput, calls=%fused_computation.7 | convolution fusion | flops 5924323328 | bytes 27262976 | tf_op jit(solution)/shard_map/dot_general | solution.py:643
  342.9 8.9 %fusion.124 = f32[1024,2048]{1,0:T(8,128)S(1)} fusion(bf16[1024,1408]{1,0:T(8,128)(2,1)S(1)} %get-tuple-element.711, bf16[2048,1408]{1,0:T(8,128)(2,1)} %all-gather.11.cloned.1.call-done), kind=kOutput, calls=%fused_computation.427 | convolution fusion | flops 5905580032 | bytes 17039360 | tf_op jit(solution)/shard_map/dot_general | solution.py:647
  351.9 8.4 %add_convert_fusion = bf16[1024,2048]{1,0:T(8,128)(2,1)S(1)} fusion(f32[1024,2048]{1,0:T(8,128)S(1)} %fusion.124, bf16[1024,1408]{1,0:T(8,128)(2,1)} %copy-done.72, bf16[2048,1408]{1,0:T(8,128)(2,1)S(1)} %copy-done.68), kind=kOutput, calls=%fused_computation | convolution fusion | flops 5909774336 | bytes 21233664 | tf_op jit(solution)/shard_map/dot_general | solution.py:647
  365.2 8.7 %convolution_convert_fusion.2 = bf16[2048,1408]{1,0:T(8,128)(2,1)} fusion(bf16[1024,2048]{1,0:T(8,128)(2,1)S(1)} %bitcast.409, bf16[1024,1408]{1,0:T(8,128)(2,1)S(1)} %copy-done.71), kind=kOutput, calls=%fused_computation.3 | convolution fusion | flops 5908463616 | bytes 12845056 | tf_op jit(solution)/shard_map/dot_general | solution.py:651
  374.0 10.7 %collective-permute-done.30 = bf16[2,128,2048]{2,1,0:T(8,128)(2,1)} collective-permute-done((bf16[2,128,2048]{2,1,0:T(8,128)(2,1)}, bf16[2,128,2048]{2,1,0:T(8,128)(2,1)}, u32[]{:S(2)}, u32[]{:S(2)}) %collective-permute-start.30) | collective-permute-done | bytes 1048608 | tf_op jit(solution)/shard_map/ppermute | solution.py:20
  389.7 9.1 %convolution_convert_fusion.6 = bf16[1024,2048]{1,0:T(8,128)(2,1)S(1)} fusion(bf16[1024,1408]{1,0:T(8,128)(2,1)S(1)} %copy-done.69, bf16[1408,2048]{1,0:T(8,128)(2,1)} %all-gather.7.cloned.1.call-done), kind=kOutput, calls=%fused_computation.26 | convolution fusion | flops 5907677184 | bytes 12845056 | tf_op jit(solution)/shard_map/dot_general | solution.py:643
  424.8 8.1 %convolution_convert_fusion.1 = bf16[1408,2048]{1,0:T(8,128)(2,1)} fusion(bf16[1024,1408]{1,0:T(8,128)(2,1)S(1)} %copy-done.69, bf16[1024,2048]{1,0:T(8,128)(2,1)S(1)} %bitcast.404), kind=kOutput, calls=%fused_computation.2 | convolution fusion | flops 5908463616 | bytes 12845056 | tf_op jit(solution)/shard_map/dot_general | solution.py:651
  454.6 7.9 %collective-permute-start.44 = (f32[4,16,512]{2,1,0:T(8,128)}, f32[4,16,512]{2,1,0:T(8,128)S(1)}, u32[]{:S(2)}, u32[]{:S(2)}) collective-permute-start(f32[4,16,512]{2,1,0:T(8,128)} %shard_map.223), channel_id=1, source_target_pairs={{2,0},{4,2},{6,4},{3,1},{5,3},{7,5},{10,8},{12,10},{14,12},{11,9},... | collective-permute-start | bytes 393224 | tf_op jit(solution)/shard_map/ppermute | solution.py:26
  470.9 16.3 %collective-permute-start.43 = (bf16[256,1408]{1,0:T(8,128)(2,1)}, bf16[256,1408]{1,0:T(8,128)(2,1)S(1)}, u32[]{:S(2)}, u32[]{:S(2)}) collective-permute-start(bf16[256,1408]{1,0:T(8,128)(2,1)} %reduce-scatter.6.cloned.1.call-done), channel_id=1, source_target_pairs={{8,1},{1,8},{10,3},{3,10},{12,5},{5,12},{14,7},{7,14},{24,17},{17,... | collective-permute-start | bytes 2162696 | tf_op jit(solution)/shard_map/ppermute | solution.py:267
  492.8 16.8 %shard_map.224 = (bf16[4,2,1,128,512]{4,3,2,1,0:T(8,128)(2,1)}, f32[16,512]{1,0:T(8,128)}, f32[16,512]{1,0:T(8,128)}) custom-call(s32[1]{0:T(128)} %bitcast.36.place_ref, bf16[4,2,1,128,512]{4,3,2,1,0:T(8,128)(2,1)} %fusion.49.signal_ref, bf16[4,2,1,128,512]{4,3,2,1,0:T(8,128)(2,1)} %get-tuple-element.785.signal_ref.grad_ref, ...), custom_call_target="tpu_custom_call" | custom-call | flops 100663296 | bytes 4521984 | tf_op jit(solution)/shard_map/pallas_call | solution.py:560
  532.3 10.5 %convolution_convert_fusion = bf16[2048,1536]{1,0:T(8,128)(2,1)} fusion(bf16[1088,2048]{1,0:T(8,128)(2,1)S(1)} %bitcast.396, bf16[1088,1024]{1,0:T(8,128)(2,1)S(1)} %bitcast.383, bf16[1088,512]{1,0:T(8,128)(2,1)S(1)} %bitcast.392), kind=kOutput, calls=%fused_computation.1 | convolution fusion | flops 6854934528 | bytes 14090240 | tf_op jit(solution)/shard_map/dot_general | solution.py:651
  545.2 10.3 %convolution_convert_fusion.5 = bf16[1088,2048]{1,0:T(8,128)(2,1)S(1)} fusion(bf16[1088,1536]{1,0:T(8,128)(2,1)} %pad_maximum_fusion.7, bf16[2048,1536]{1,0:T(8,128)(2,1)} %all-gather.5.cloned.1.call-done), kind=kOutput, calls=%fused_computation.6 | convolution fusion | flops 6847332352 | bytes 14090240 | tf_op jit(solution)/shard_map/dot_general | solution.py:647
  569.2 10.4 %collective-permute-done.49 = bf16[256,1408]{1,0:T(8,128)(2,1)} collective-permute-done((bf16[256,1408]{1,0:T(8,128)(2,1)}, bf16[256,1408]{1,0:T(8,128)(2,1)}, u32[]{:S(2)}, u32[]{:S(2)}) %collective-permute-start.49) | collective-permute-done | bytes 720928 | tf_op jit(solution)/shard_map/ppermute | solution.py:267
  594.6 5.9 shard_map.225
  615.4 7.3 %collective-permute-done.54 = bf16[136,2048]{1,0:T(8,128)(2,1)S(1)} collective-permute-done((bf16[136,2048]{1,0:T(8,128)(2,1)}, bf16[136,2048]{1,0:T(8,128)(2,1)S(1)}, u32[]{:S(2)}, u32[]{:S(2)}) %collective-permute-start.54) | collective-permute-done | bytes 557088 | tf_op jit(solution)/shard_map/ppermute | solution.py:20
  626.2 7.6 %collective-permute-start.57 = (bf16[2,2,2048]{2,1,0:T(2,128)(2,1)S(1)}, bf16[2,2,2048]{2,1,0:T(2,128)(2,1)S(1)}, u32[]{:S(2)}, u32[]{:S(2)}) collective-permute-start(bf16[2,2,2048]{2,1,0:T(2,128)(2,1)S(1)} %fusion.86), channel_id=1, source_target_pairs={{2,1},{4,3},{6,5},{10,9},{12,11},{14,13},{18,17},{20,19},{22,21},{... | collective-permute-start | bytes 49160 | tf_op jit(solution)/shard_map/ppermute | solution.py:970
  634.5 6.2 shard_map.226
  664.3 5.4 collective-permute-done.64
  696.7 5.9 shard_map.227
  (545 shorter events, 356.5 us)
Async XLA Ops:
  7.2 111.6 %all-gather.5.cloned.1.call-start = ((), (), s32[]{:S(2)}) async-start(), calls=%async_computation.5 | async-start | bytes 7077888 | tf_op jit(solution)/shard_map/all_gather | solution.py:238
  26.8 233.8 %all-gather.7.cloned.1.call-start = ((), (), s32[]{:S(2)}) async-start(), calls=%async_computation.6 | async-start | bytes 6488064 | tf_op jit(solution)/shard_map/all_gather | solution.py:238
  52.6 250.0 %all-gather.11.cloned.1.call-start = ((), (), s32[]{:S(2)}) async-start(), calls=%async_computation.8 | async-start | bytes 6488064 | tf_op jit(solution)/shard_map/all_gather | solution.py:238
  52.7 57.3 %collective-permute-start.4 = (bf16[2,1,136,2048]{3,2,0,1:T(8,128)(2,1)}, bf16[2,1,136,2048]{3,2,0,1:T(8,128)(2,1)S(1)}, u32[]{:S(2)}, u32[]{:S(2)}) collective-permute-start(bf16[2,1,136,2048]{3,2,0,1:T(8,128)(2,1)} %bitcast.398), channel_id=1, source_target_pairs={{0,16},{16,0},{1,17},{17,1},{2,18},{18,2},{3,19},{19,3},{4,20},{20... | collective-permute-start | bytes 3342344 | tf_op jit(solution)/shard_map/ppermute | solution.py:20
  54.0 56.0 %collective-permute-start.5 = (bf16[2,1,136,2048]{3,2,0,1:T(8,128)(2,1)}, bf16[2,1,136,2048]{3,2,0,1:T(8,128)(2,1)}, u32[]{:S(2)}, u32[]{:S(2)}) collective-permute-start(bf16[2,1,136,2048]{3,2,0,1:T(8,128)(2,1)} %pad_maximum_fusion.17), channel_id=1, source_target_pairs={{0,1},{1,0},{2,3},{3,2},{4,5},{5,4},{6,7},{7,6},{8,9},{9,8},{10,11... | collective-permute-start | bytes 3342344 | tf_op jit(solution)/shard_map/ppermute | solution.py:20
  55.2 22.8 %collective-permute-start.6 = (bf16[128,1024]{1,0:T(8,128)(2,1)S(1)}, bf16[128,1024]{1,0:T(8,128)(2,1)S(1)}, u32[]{:S(2)}, u32[]{:S(2)}) collective-permute-start(bf16[128,1024]{1,0:T(8,128)(2,1)S(1)} %copy-done.43), channel_id=1, source_target_pairs={{0,6},{2,0},{4,2},{6,4},{1,7},{3,1},{5,3},{7,5},{8,14},{10,8},{12,... | collective-permute-start | bytes 786440 | tf_op jit(solution)/shard_map/ppermute | solution.py:20
  55.2 33.2 %collective-permute-start.7 = (bf16[128,1024]{1,0:T(8,128)(2,1)S(1)}, bf16[128,1024]{1,0:T(8,128)(2,1)}, u32[]{:S(2)}, u32[]{:S(2)}) collective-permute-start(bf16[128,1024]{1,0:T(8,128)(2,1)S(1)} %copy-done.43), channel_id=1, source_target_pairs={{0,4},{2,6},{4,0},{6,2},{1,5},{3,7},{5,1},{7,3},{8,12},{10,14},{12... | collective-permute-start | bytes 786440 | tf_op jit(solution)/shard_map/ppermute | solution.py:20
  57.6 48.6 %collective-permute-start.8 = (bf16[128,1024]{1,0:T(8,128)(2,1)S(1)}, bf16[128,1024]{1,0:T(8,128)(2,1)}, u32[]{:S(2)}, u32[]{:S(2)}) collective-permute-start(bf16[128,1024]{1,0:T(8,128)(2,1)S(1)} %copy-done.43), channel_id=1, source_target_pairs={{0,2},{2,4},{4,6},{6,0},{1,3},{3,5},{5,7},{7,1},{8,10},{10,12},{12... | collective-permute-start | bytes 786440 | tf_op jit(solution)/shard_map/ppermute | solution.py:20
  108.6 30.4 %collective-permute-start.14 = (bf16[256,1408]{1,0:T(8,128)(2,1)}, bf16[256,1408]{1,0:T(8,128)(2,1)}, u32[]{:S(2)}, u32[]{:S(2)}) collective-permute-start(bf16[256,1408]{1,0:T(8,128)(2,1)} %concatenate.265), channel_id=1, source_target_pairs={{0,1},{9,8},{2,3},{11,10},{4,5},{13,12},{6,7},{15,14},{16,17},{25,... | collective-permute-start | bytes 2162696 | tf_op jit(solution)/shard_map/ppermute | solution.py:192
  141.3 184.8 %all-gather.9.cloned.1.call-start = ((), (), s32[]{:S(2)}) async-start(), calls=%async_computation.7 | async-start | bytes 6488064 | tf_op jit(solution)/shard_map/all_gather | solution.py:238
  156.1 21.9 %collective-permute-start.17 = (bf16[2,1,256,1024]{3,2,0,1:T(8,128)(2,1)}, bf16[2,1,256,1024]{3,2,0,1:T(8,128)(2,1)}, u32[]{:S(2)}, u32[]{:S(2)}) collective-permute-start(bf16[2,1,256,1024]{3,2,0,1:T(8,128)(2,1)} %bitcast.45), channel_id=1, source_target_pairs={{0,16},{16,0},{1,17},{17,1},{2,18},{18,2},{3,19},{19,3},{4,20},{20... | collective-permute-start | bytes 3145736 | tf_op jit(solution)/shard_map/ppermute | solution.py:20
  183.7 67.3 %collective-permute-start.22 = (bf16[2048,1024]{1,0:T(8,128)(2,1)}, bf16[2048,1024]{1,0:T(8,128)(2,1)}, u32[]{:S(2)}, u32[]{:S(2)}) collective-permute-start(bf16[2048,1024]{1,0:T(8,128)(2,1)} %bitcast.55), channel_id=1, source_target_pairs={{0,8},{8,0},{1,9},{9,1},{2,10},{10,2},{3,11},{11,3},{4,12},{12,4},... | collective-permute-start | bytes 12582920 | tf_op jit(solution)/shard_map/ppermute | solution.py:20
  206.3 26.9 %collective-permute-start.25 = (bf16[256,1408]{1,0:T(8,128)(2,1)}, bf16[256,1408]{1,0:T(8,128)(2,1)S(1)}, u32[]{:S(2)}, u32[]{:S(2)}) collective-permute-start(bf16[256,1408]{1,0:T(8,128)(2,1)} %concatenate.274), channel_id=1, source_target_pairs={{0,1},{9,8},{2,3},{11,10},{4,5},{13,12},{6,7},{15,14},{16,17},{25,... | collective-permute-start | bytes 2162696 | tf_op jit(solution)/shard_map/ppermute | solution.py:192
  214.6 22.4 %collective-permute-start.23 = (bf16[2,1,128,2048]{3,2,0,1:T(8,128)(2,1)}, bf16[2,1,128,2048]{3,2,0,1:T(8,128)(2,1)}, u32[]{:S(2)}, u32[]{:S(2)}) collective-permute-start(bf16[2,1,128,2048]{3,2,0,1:T(8,128)(2,1)} %bitcast.70), channel_id=1, source_target_pairs={{0,16},{16,0},{1,17},{17,1},{2,18},{18,2},{3,19},{19,3},{4,20},{20... | collective-permute-start | bytes 3145736 | tf_op jit(solution)/shard_map/ppermute | solution.py:20
  216.2 24.4 %collective-permute-start.24 = (bf16[2,1,128,2048]{3,2,0,1:T(8,128)(2,1)}, bf16[2,1,128,2048]{3,2,0,1:T(8,128)(2,1)}, u32[]{:S(2)}, u32[]{:S(2)}) collective-permute-start(bf16[2,1,128,2048]{3,2,0,1:T(8,128)(2,1)} %pad_maximum_fusion.23), channel_id=1, source_target_pairs={{0,1},{1,0},{2,3},{3,2},{4,5},{5,4},{6,7},{7,6},{8,9},{9,8},{10,11... | collective-permute-start | bytes 3145736 | tf_op jit(solution)/shard_map/ppermute | solution.py:20
  235.4 232.1 %reduce-scatter.6.cloned.1.call-start = ((), (), s32[]{:S(2)}) async-start(), calls=%async_computation.9 | async-start | bytes 6488064 | tf_op jit(solution)/shard_map/reduce_scatter | solution.py:242
  276.2 22.3 %collective-permute-start.28 = (bf16[2,1,128,2048]{3,2,0,1:T(8,128)(2,1)S(1)}, bf16[2,1,128,2048]{3,2,0,1:T(8,128)(2,1)S(1)}, u32[]{:S(2)}, u32[]{:S(2)}) collective-permute-start(bf16[2,1,128,2048]{3,2,0,1:T(8,128)(2,1)S(1)} %pad_maximum_fusion.24), channel_id=1, source_target_pairs={{0,16},{16,0},{1,17},{17,1},{2,18},{18,2},{3,19},{19,3},{4,20},{20... | collective-permute-start | bytes 3145736 | tf_op jit(solution)/shard_map/ppermute | solution.py:20
  326.0 219.1 %reduce-scatter.8.cloned.1.call-start = ((), (), s32[]{:S(2)}) async-start(), calls=%async_computation.10 | async-start | bytes 6488064 | tf_op jit(solution)/shard_map/reduce_scatter | solution.py:242
  373.9 232.0 %reduce-scatter.10.cloned.1.call-start = ((), (), s32[]{:S(2)}) async-start(), calls=%async_computation.11 | async-start | bytes 6488064 | tf_op jit(solution)/shard_map/reduce_scatter | solution.py:242
  403.2 117.4 %collective-permute-start.32 = (bf16[2,128,2048]{2,1,0:T(8,128)(2,1)}, bf16[2,128,2048]{2,1,0:T(8,128)(2,1)}, u32[]{:S(2)}, u32[]{:S(2)}) collective-permute-start(bf16[2,128,2048]{2,1,0:T(8,128)(2,1)} %get-tuple-element.724), channel_id=1, source_target_pairs={{0,1},{1,0},{2,3},{3,2},{4,5},{5,4},{6,7},{7,6},{8,9},{9,8},{10,11... | collective-permute-start | bytes 3145736 | tf_op jit(solution)/shard_map/ppermute | solution.py:20
  404.4 116.2 %collective-permute-start.33 = (bf16[2,128,2048]{2,1,0:T(8,128)(2,1)}, bf16[2,128,2048]{2,1,0:T(8,128)(2,1)}, u32[]{:S(2)}, u32[]{:S(2)}) collective-permute-start(bf16[2,128,2048]{2,1,0:T(8,128)(2,1)} %bitcast.117), channel_id=1, source_target_pairs={{0,16},{16,0},{1,17},{17,1},{2,18},{18,2},{3,19},{19,3},{4,20},{20... | collective-permute-start | bytes 3145736 | tf_op jit(solution)/shard_map/ppermute | solution.py:20
  432.9 222.9 %reduce-scatter.12.cloned.1.call-start = ((), (), s32[]{:S(2)}) async-start(), calls=%async_computation.12 | async-start | bytes 7077888 | tf_op jit(solution)/shard_map/reduce_scatter | solution.py:242
  437.1 25.5 %collective-permute-start.36 = (bf16[1,128,2048]{2,1,0:T(8,128)(2,1)S(1)}, bf16[1,128,2048]{2,1,0:T(8,128)(2,1)S(1)}, u32[]{:S(2)}, u32[]{:S(2)}) collective-permute-start(bf16[1,128,2048]{2,1,0:T(8,128)(2,1)S(1)} %get-tuple-element.767), channel_id=1, source_target_pairs={{0,1},{1,0},{2,3},{3,2},{4,5},{5,4},{6,7},{7,6},{8,9},{9,8},{10,11... | collective-permute-start | bytes 1572872 | tf_op jit(solution)/shard_map/ppermute | solution.py:20
  437.1 27.0 %collective-permute-start.37 = (bf16[1,128,2048]{2,1,0:T(8,128)(2,1)S(1)}, bf16[1,128,2048]{2,1,0:T(8,128)(2,1)S(1)}, u32[]{:S(2)}, u32[]{:S(2)}) collective-permute-start(bf16[1,128,2048]{2,1,0:T(8,128)(2,1)S(1)} %get-tuple-element.769), channel_id=1, source_target_pairs={{0,16},{16,0},{1,17},{17,1},{2,18},{18,2},{3,19},{19,3},{4,20},{20... | collective-permute-start | bytes 1572872 | tf_op jit(solution)/shard_map/ppermute | solution.py:20
  467.5 46.3 %collective-permute-start.41 = (bf16[2,1,128,2048]{3,2,0,1:T(8,128)(2,1)}, bf16[2,1,128,2048]{3,2,0,1:T(8,128)(2,1)}, u32[]{:S(2)}, u32[]{:S(2)}) collective-permute-start(bf16[2,1,128,2048]{3,2,0,1:T(8,128)(2,1)} %pad_maximum_fusion.26), channel_id=1, source_target_pairs={{0,16},{16,0},{1,17},{17,1},{2,18},{18,2},{3,19},{19,3},{4,20},{20... | collective-permute-start | bytes 3145736 | tf_op jit(solution)/shard_map/ppermute | solution.py:20
  469.5 44.2 %collective-permute-start.42 = (bf16[2,1,128,2048]{3,2,0,1:T(8,128)(2,1)}, bf16[2,1,128,2048]{3,2,0,1:T(8,128)(2,1)}, u32[]{:S(2)}, u32[]{:S(2)}) collective-permute-start(bf16[2,1,128,2048]{3,2,0,1:T(8,128)(2,1)} %bitcast.415), channel_id=1, source_target_pairs={{0,1},{1,0},{2,3},{3,2},{4,5},{5,4},{6,7},{7,6},{8,9},{9,8},{10,11... | collective-permute-start | bytes 3145736 | tf_op jit(solution)/shard_map/ppermute | solution.py:20
  470.9 41.8 %collective-permute-start.43 = (bf16[256,1408]{1,0:T(8,128)(2,1)}, bf16[256,1408]{1,0:T(8,128)(2,1)S(1)}, u32[]{:S(2)}, u32[]{:S(2)}) collective-permute-start(bf16[256,1408]{1,0:T(8,128)(2,1)} %reduce-scatter.6.cloned.1.call-done), channel_id=1, source_target_pairs={{8,1},{1,8},{10,3},{3,10},{12,5},{5,12},{14,7},{7,14},{24,17},{17,... | collective-permute-start | bytes 2162696 | tf_op jit(solution)/shard_map/ppermute | solution.py:267
  542.8 140.1 %reduce-scatter.14.cloned.1.call-start = ((), (), s32[]{:S(2)}) async-start(), calls=%async_computation.13 | async-start | bytes 2359296 | tf_op jit(solution)/shard_map/reduce_scatter | solution.py:242
  544.8 37.2 %collective-permute-start.47 = (bf16[128,2048]{1,0:T(8,128)(2,1)}, bf16[128,2048]{1,0:T(8,128)(2,1)}, u32[]{:S(2)}, u32[]{:S(2)}) collective-permute-start(bf16[128,2048]{1,0:T(8,128)(2,1)} %get-tuple-element.815), channel_id=1, source_target_pairs={{0,16},{16,0},{1,17},{17,1},{2,18},{18,2},{3,19},{19,3},{4,20},{20... | collective-permute-start | bytes 1572872 | tf_op jit(solution)/shard_map/ppermute | solution.py:20
  545.1 36.8 %collective-permute-start.48 = (bf16[128,2048]{1,0:T(8,128)(2,1)}, bf16[128,2048]{1,0:T(8,128)(2,1)}, u32[]{:S(2)}, u32[]{:S(2)}) collective-permute-start(bf16[128,2048]{1,0:T(8,128)(2,1)} %get-tuple-element.817), channel_id=1, source_target_pairs={{0,1},{1,0},{2,3},{3,2},{4,5},{5,4},{6,7},{7,6},{8,9},{9,8},{10,11... | collective-permute-start | bytes 1572872 | tf_op jit(solution)/shard_map/ppermute | solution.py:20
  561.9 38.6 %collective-permute-start.51 = (bf16[2,136,2048]{2,1,0:T(8,128)(2,1)}, bf16[2,136,2048]{2,1,0:T(8,128)(2,1)}, u32[]{:S(2)}, u32[]{:S(2)}) collective-permute-start(bf16[2,136,2048]{2,1,0:T(8,128)(2,1)} %get-tuple-element.861), channel_id=1, source_target_pairs={{0,1},{1,0},{2,3},{3,2},{4,5},{5,4},{6,7},{7,6},{8,9},{9,8},{10,11... | collective-permute-start | bytes 3342344 | tf_op jit(solution)/shard_map/ppermute | solution.py:20
  562.0 38.5 %collective-permute-start.52 = (bf16[2,136,2048]{2,1,0:T(8,128)(2,1)}, bf16[2,136,2048]{2,1,0:T(8,128)(2,1)}, u32[]{:S(2)}, u32[]{:S(2)}) collective-permute-start(bf16[2,136,2048]{2,1,0:T(8,128)(2,1)} %bitcast.175), channel_id=1, source_target_pairs={{0,16},{16,0},{1,17},{17,1},{2,18},{18,2},{3,19},{19,3},{4,20},{20... | collective-permute-start | bytes 3342344 | tf_op jit(solution)/shard_map/ppermute | solution.py:20
  (124 other events, 1261.8 us)
Sparse Core Ops, SparseCore 0:
  26.9 84.4 all-gather.4
  113.0 62.1 all-gather.6
  177.5 66.9 all-gather.10
  245.9 62.1 all-gather.8
  326.2 67.4 reduce-scatter.5
  396.4 63.3 reduce-scatter.7
  462.1 69.6 reduce-scatter.9
  542.9 69.1 reduce-scatter.11
  634.0 28.6 reduce-scatter.13

commit v9 on v8

--- a/solution.py
+++ b/solution.py
@@ -682,8 +682,6 @@
         return jnp.stack([value] + got)
 
     in_got = column_moves(run(lambda w: column_pieces(w, 3), in_weight))
-    block_out = run(out_block, out_weight)
-    out_got = moved(block_out, "z", -1)
     last = [(i * spread + spread - 1, (i + 1) * spread) for i in range(depth - 1)]
 
     def norm_one(values, gain):
@@ -705,9 +703,16 @@
     normed_move.turn(line)
     w_down = gather_tile(run(row_block, down_weight))
     gate_got = column_moves(run(lambda w: column_pieces(w, 1), gate_weight))
-    held = run(lambda own, got: by_z([own] + got), block_out, out_got)
+
+    def feed_grad(values):
+        values = (values.astype(wide) * mask).astype(low)
+        return values[: batch // 2], values[batch // 2 :]
+
+    feed_move = Gather(*run(feed_grad, cotangent))
     normed_all = normed_move.end(line)
-    out_move = Gather(held[:1], held[1:])
+    feed_move.turn(line)
+    block_out = run(out_block, out_weight)
+    out_got = moved(block_out, "z", -1)
 
     channels = w_in.shape[1] // 3
     half = channels // 2
@@ -754,17 +759,11 @@
     product, state_end = run(multiply, mixed, taps, decay)
     states = [passed(state_end, "z", k) for k in range(1, depth)]
     w_gate = gather_tile(run(column_block, gate_got))
+    grad_feed_all = feed_move.end(line)
+    held = run(lambda own, got: by_z([own] + got), block_out, out_got)
+    out_move = Gather(held[:1], held[1:])
+    up_got = column_moves(run(lambda w: column_pieces(w, 1), up_weight))
     out_move.turn(line)
-
-    def feed_grad(values):
-        values = (values.astype(wide) * mask).astype(low)
-        return values[: batch // 2], values[batch // 2 :]
-
-    feed_move = Gather(*run(feed_grad, cotangent))
-    up_got = column_moves(run(lambda w: column_pieces(w, 1), up_weight))
-    out_own = out_move.end(line)
-    w_out = [out_own] + moved(out_own, "c", -1)
-    feed_move.turn(line)
 
     def combine(parts, rates):
         total = parts[0]
@@ -790,7 +789,8 @@
     )
     gated_got = swap_slots(gated)
     w_up = gather_tile(run(column_block, up_got))
-    grad_feed_all = feed_move.end(line)
+    out_own = out_move.end(line)
+    w_out = [out_own] + moved(out_own, "c", -1)
 
     def mix(got, weights, values, gain):
         own = jnp.concatenate(
@@ -910,8 +910,6 @@
 
     up_held = run(owner_held, up_parts_got)
     up_got = moved(up_held, "y", -1)
-    grad_mix_all = mix_move.end(line)
-    feed_back.turn(line)
 
     def in_back(query, pair, weights, v):
         result = jnp.concatenate(
@@ -925,21 +923,13 @@
 
     grad_mixed, in_term = run(in_back, grad_query, grad_pair, taps, normed_all)
     in_mine = scatter_tile(in_term)
+    one_back = Scatter(run(lambda a, w: split_sum(dot_t(a, w, low)), grad_mixed, w_in))
+    grad_mix_all = mix_move.end(line)
+    out_mine = scatter_tile(run(dot_w, gated_all, grad_mix_all))
     gate_got = owner_moves(run(owner_parts, gate_mine))
-    one_back = Scatter(run(lambda a, w: split_sum(dot_t(a, w, low)), grad_mixed, w_in))
+    feed_back.turn(line)
     up_held = run(stacked, up_held, up_got)
     up_got = moved(up_held, "c", -1)
-    out_mine = scatter_tile(run(dot_w, gated_all, grad_mix_all))
-    gate_held = run(owner_held, gate_got)
-    gate_got = moved(gate_held, "y", -1)
-
-    output = run(
-        lambda rest, values: (
-            mask * (values + Scatter.sum(*rest).reshape(batch, local, width))
-        ).astype(low),
-        feed_back.rest(),
-        middle,
-    )
 
     def tap_sums(query, pair, value):
         sums = []
@@ -952,6 +942,8 @@
         return jnp.stack(sums)
 
     grad_taps = run(tap_sums, grad_query, grad_pair, mixed)
+    gate_held = run(owner_held, gate_got)
+    gate_got = moved(gate_held, "y", -1)
 
     def normed_sum(rest):
         value = Scatter.sum(*rest).reshape(batch, local + extra, width)
@@ -962,6 +954,13 @@
 
     grad_up_weight = run(column_whole, up_held, up_got)
     one_back.turn(line)
+    output = run(
+        lambda rest, values: (
+            mask * (values + Scatter.sum(*rest).reshape(batch, local, width))
+        ).astype(low),
+        feed_back.rest(),
+        middle,
+    )
     down_held = run(lambda v: v[None], down_mine)
     down_got = moved(down_held, "y", -1)
     gate_held = run(stacked, gate_held, gate_got)
@@ -1003,12 +1002,12 @@
     grad_down = run(rows_whole, down_held, down_got)
     in_held = run(owner_held, in_got)
     in_got = moved(in_held, "y", -1)
+    out_held = run(lambda v: v[None], out_mine)
+    out_got = moved(out_held, "y", -1)
     small = run(lambda v, got: v + sum(got), small, small_got)
     small_got = moved(small, "x", -1)
     small = run(stacked, small, small_got)
     small_got = moved(small, "y", -1)
-    out_held = run(lambda v: v[None], out_mine)
-    out_got = moved(out_held, "y", -1)
     in_held = run(stacked, in_held, in_got)
     in_got = moved(in_held, "c", -1)
     poles = decay.shape[0]

time: 725 us -> 726 us (level)
  waiting for transfers between devices: 207 us -> 216 us
    ppermute x52, waiting for transfers between devices: 161 us -> 177 us  [turned(): lax.ppermute(value, axis, [(i, (i + by) % length) for i in range(length)])]
    ppermute x3, waiting for transfers between devices: 15.9 us -> 7.29 us  [owner_moves(): got.append(lax.ppermute(parts[d], ('c', 'x'), pairs))]
    unnamed x171 -> x159, local copies, waits for them, and re-layouts: 23.8 us -> 22.8 us
  transfers between devices with their start and end apart: 81 -> 81, of which waited for: 34 -> 35; matrix products, arithmetic and copies ran while one was open for 42% -> 42% of each run, Pallas kernels for 7% -> 7%
where the time goes in v9:
time: 726 us; the launch traced here: 712 us
  waiting for transfers between devices  216 us (30%)
  matrix products  141 us (19%)
  other arithmetic  119 us (16%)
  starting transfers between devices  97 us (13%)
  local copies, waits for them, and re-layouts  65 us (9%)
  Pallas kernels  56.8 us (8%)
  between operations  16.5 us (2%)
    ppermute x52, waiting for transfers between devices, turned(): lax.ppermute(value, axis, [(i, (i + by) % length) for i in range(length)])  177 us
    dot_general x6, matrix products, dot(): return jnp.dot(a, b, preferred_element_type=wide).astype(kind)  55 us
    dot_general x6, matrix products, dot_t(): lax.dot_general(a, b, (((1,), (1,)), ((), ())), preferred_element_type=wide)  46.8 us
    ppermute x52, starting transfers between devices, turned(): lax.ppermute(value, axis, [(i, (i + by) % length) for i in range(length)])  46.3 us
    dot_general x5, matrix products, dot_w(): lax.dot_general(a, b, (((0,), (0,)), ((), ())), preferred_element_type=wide)  39.6 us
    pallas_call x4, Pallas kernels, conv_call(): pl.pallas_call(kernel, out_shape=results, grid_spec=pltpu.PrefetchScalarG...  35.3 us
    unnamed x159, local copies, waits for them, and re-layouts  22.8 us
    another operation x15, other arithmetic, work(): return jnp.stack([first, second]).reshape(-1, first.shape[-1])  21.6 us
  transfers between devices with their start and end apart: 81, of which 35 were waited for; matrix products, arithmetic and copies ran while one was open for 42% of the time, Pallas kernels for 7%

profile of v9, /device:TPU:9, one launch (start us, length us, event | category | flops | bytes accessed | tf_op | source)
XLA Modules:
  0.0 712.5 jit_solution(7888005413689068975)
XLA Ops:
  17.4 7.1 collective-permute-done.1
  36.0 11.0 %collective-permute-done.2 = bf16[1,136,2048]{2,1,0:T(8,128)(2,1)} collective-permute-done((bf16[1,136,2048]{2,1,0:T(8,128)(2,1)S(1)}, bf16[1,136,2048]{2,1,0:T(8,128)(2,1)}, u32[]{:S(2)}, u32[]{:S(2)}) %collective-permute-start.2) | collective-permute-done | bytes 557088 | tf_op jit(solution)/shard_map/ppermute | solution.py:20
  62.9 13.9 %collective-permute-done.4 = bf16[2,1,136,2048]{3,2,0,1:T(8,128)(2,1)} collective-permute-done((bf16[2,1,136,2048]{3,2,0,1:T(8,128)(2,1)}, bf16[2,1,136,2048]{3,2,0,1:T(8,128)(2,1)}, u32[]{:S(2)}, u32[]{:S(2)}) %collective-permute-start.4) | collective-permute-done | bytes 1114144 | tf_op jit(solution)/shard_map/ppermute | solution.py:20
  95.7 10.5 %convolution_convert_fusion.4 = bf16[1088,1536]{1,0:T(8,128)(2,1)S(1)} fusion(bf16[1088,2048]{1,0:T(8,128)(2,1)} %bitcast.392, bf16[2048,1536]{1,0:T(8,128)(2,1)} %all-gather.5.cloned.1.call-done), kind=kOutput, calls=%fused_computation.5 | convolution fusion | flops 6846775296 | bytes 14090240 | tf_op jit(solution)/shard_map/dot_general | solution.py:643
  129.3 7.0 collective-permute-done.11
  136.3 13.6 %collective-permute-done.12 = bf16[128,1024]{1,0:T(8,128)(2,1)S(1)} collective-permute-done((bf16[128,1024]{1,0:T(8,128)(2,1)S(1)}, bf16[128,1024]{1,0:T(8,128)(2,1)S(1)}, u32[]{:S(2)}, u32[]{:S(2)}) %collective-permute-start.12) | collective-permute-done | bytes 262176 | tf_op jit(solution)/shard_map/ppermute | solution.py:20
  149.9 17.9 %collective-permute-done.13 = bf16[128,1024]{1,0:T(8,128)(2,1)S(1)} collective-permute-done((bf16[128,1024]{1,0:T(8,128)(2,1)S(1)}, bf16[128,1024]{1,0:T(8,128)(2,1)S(1)}, u32[]{:S(2)}, u32[]{:S(2)}) %collective-permute-start.13) | collective-permute-done | bytes 262176 | tf_op jit(solution)/shard_map/ppermute | solution.py:20
  192.4 8.8 %shard_map.222 = bf16[4,2,1,128,512]{4,3,2,1,0:T(8,128)(2,1)} custom-call(s32[1]{0:T(128)} %bitcast.36.place_ref, bf16[4,2,1,128,512]{4,3,2,1,0:T(8,128)(2,1)} %fusion.49.signal_ref, f32[16,512]{1,0:T(8,128)} %maximum_bitcast_fusion.11.decay_ref, f32[16,512]{1,0:T(8,128)} %maximum_bitcast_fusion.12.residue_ref, f32[4,16,512]{2,1,0:T(8,128)} %multiply_add_fusion.2.start_ref), custom_call_target="tpu_custom_call" | custom-call | flops 33554432 | bytes 2293760 | tf_op jit(solution)/shard_map/pallas_call | solution.py:560
  206.2 7.7 %collective-permute-done.23 = bf16[2,1,256,1024]{3,2,0,1:T(8,128)(2,1)} collective-permute-done((bf16[2,1,256,1024]{3,2,0,1:T(8,128)(2,1)}, bf16[2,1,256,1024]{3,2,0,1:T(8,128)(2,1)}, u32[]{:S(2)}, u32[]{:S(2)}) %collective-permute-start.23) | collective-permute-done | bytes 1048608 | tf_op jit(solution)/shard_map/ppermute | solution.py:20
  234.0 6.3 collective-permute-done.20
  251.5 12.1 %fusion.123 = f32[1024,1408]{1,0:T(8,128)} fusion(bf16[1024,2048]{1,0:T(8,128)(2,1)} %bitcast.402, bf16[1408,2048]{1,0:T(8,128)(2,1)} %all-gather.7.cloned.1.call-done), kind=kOutput, calls=%fused_computation.426 | convolution fusion | flops 5905580032 | bytes 15728640 | tf_op jit(solution)/shard_map/dot_general | solution.py:647
  265.2 22.0 %collective-permute-done.28 = bf16[2,1,128,2048]{3,2,0,1:T(8,128)(2,1)S(1)} collective-permute-done((bf16[2,1,128,2048]{3,2,0,1:T(8,128)(2,1)S(1)}, bf16[2,1,128,2048]{3,2,0,1:T(8,128)(2,1)S(1)}, u32[]{:S(2)}, u32[]{:S(2)}) %collective-permute-start.28) | collective-permute-done | bytes 1048608 | tf_op jit(solution)/shard_map/ppermute | solution.py:20
  290.3 13.2 %multiply_convert_fusion.2 = (bf16[1024,1408]{1,0:T(8,128)(2,1)S(1)}, f32[1024,1408]{1,0:T(8,128)}) fusion(f32[1024,1408]{1,0:T(8,128)} %fusion.123, bf16[1024,2048]{1,0:T(8,128)(2,1)} %bitcast.404, bf16[2048,1408]{1,0:T(8,128)(2,1)} %all-gather.11.cloned.1.call-done), kind=kOutput, calls=%fused_computation.10 | convolution fusion | flops 5914230784 | bytes 24379392 | tf_op jit(solution)/shard_map/dot_general | solution.py:643
  305.0 8.7 %convolution_convert_fusion.3 = bf16[2048,1408]{1,0:T(8,128)(2,1)} fusion(bf16[1024,2048]{1,0:T(8,128)(2,1)S(1)} %bitcast.406, bf16[1024,1408]{1,0:T(8,128)(2,1)S(1)} %get-tuple-element.702), kind=kOutput, calls=%fused_computation.4 | convolution fusion | flops 5908463616 | bytes 12845056 | tf_op jit(solution)/shard_map/dot_general | solution.py:651
  313.8 15.2 %multiply_convert_fusion = (bf16[1024,1408]{1,0:T(8,128)(2,1)S(1)}, bf16[1024,1408]{1,0:T(8,128)(2,1)}) fusion(f32[1024,1408]{1,0:T(8,128)} %get-tuple-element.692, f32[1024,1408]{1,0:T(8,128)} %fusion.123, bf16[1024,2048]{1,0:T(8,128)(2,1)} %bitcast.405, bf16[2048,1408]{1,0:T(8,128)(2,1)} %all-gather.9.cloned.1.call-done), kind=kOutput, calls=%fused_computation.7 | convolution fusion | flops 5924323328 | bytes 27262976 | tf_op jit(solution)/shard_map/dot_general | solution.py:643
  330.6 8.9 %fusion.124 = f32[1024,2048]{1,0:T(8,128)S(1)} fusion(bf16[1024,1408]{1,0:T(8,128)(2,1)S(1)} %get-tuple-element.711, bf16[2048,1408]{1,0:T(8,128)(2,1)} %all-gather.11.cloned.1.call-done), kind=kOutput, calls=%fused_computation.427 | convolution fusion | flops 5905580032 | bytes 17039360 | tf_op jit(solution)/shard_map/dot_general | solution.py:647
  339.5 8.4 %add_convert_fusion = bf16[1024,2048]{1,0:T(8,128)(2,1)S(1)} fusion(f32[1024,2048]{1,0:T(8,128)S(1)} %fusion.124, bf16[1024,1408]{1,0:T(8,128)(2,1)} %copy-done.66, bf16[2048,1408]{1,0:T(8,128)(2,1)S(1)} %copy-done.62), kind=kOutput, calls=%fused_computation | convolution fusion | flops 5909774336 | bytes 21233664 | tf_op jit(solution)/shard_map/dot_general | solution.py:647
  352.9 8.7 %convolution_convert_fusion.2 = bf16[2048,1408]{1,0:T(8,128)(2,1)} fusion(bf16[1024,2048]{1,0:T(8,128)(2,1)S(1)} %bitcast.407, bf16[1024,1408]{1,0:T(8,128)(2,1)S(1)} %copy-done.65), kind=kOutput, calls=%fused_computation.3 | convolution fusion | flops 5908463616 | bytes 12845056 | tf_op jit(solution)/shard_map/dot_general | solution.py:651
  362.4 10.4 %collective-permute-done.30 = bf16[2,128,2048]{2,1,0:T(8,128)(2,1)} collective-permute-done((bf16[2,128,2048]{2,1,0:T(8,128)(2,1)}, bf16[2,128,2048]{2,1,0:T(8,128)(2,1)}, u32[]{:S(2)}, u32[]{:S(2)}) %collective-permute-start.30) | collective-permute-done | bytes 1048608 | tf_op jit(solution)/shard_map/ppermute | solution.py:20
  377.2 9.2 %convolution_convert_fusion.6 = bf16[1024,2048]{1,0:T(8,128)(2,1)S(1)} fusion(bf16[1024,1408]{1,0:T(8,128)(2,1)S(1)} %copy-done.63, bf16[1408,2048]{1,0:T(8,128)(2,1)} %all-gather.7.cloned.1.call-done), kind=kOutput, calls=%fused_computation.26 | convolution fusion | flops 5907677184 | bytes 12845056 | tf_op jit(solution)/shard_map/dot_general | solution.py:643
  412.8 8.1 %convolution_convert_fusion.1 = bf16[1408,2048]{1,0:T(8,128)(2,1)} fusion(bf16[1024,1408]{1,0:T(8,128)(2,1)S(1)} %copy-done.63, bf16[1024,2048]{1,0:T(8,128)(2,1)S(1)} %bitcast.403), kind=kOutput, calls=%fused_computation.2 | convolution fusion | flops 5908463616 | bytes 12845056 | tf_op jit(solution)/shard_map/dot_general | solution.py:651
  455.9 16.6 %collective-permute-start.46 = (bf16[256,1408]{1,0:T(8,128)(2,1)}, bf16[256,1408]{1,0:T(8,128)(2,1)S(1)}, u32[]{:S(2)}, u32[]{:S(2)}) collective-permute-start(bf16[256,1408]{1,0:T(8,128)(2,1)} %reduce-scatter.8.cloned.1.call-done), channel_id=1, source_target_pairs={{8,1},{1,8},{10,3},{3,10},{12,5},{5,12},{14,7},{7,14},{24,17},{17,... | collective-permute-start | bytes 2162696 | tf_op jit(solution)/shard_map/ppermute | solution.py:267
  474.2 16.8 %shard_map.224 = (bf16[4,2,1,128,512]{4,3,2,1,0:T(8,128)(2,1)}, f32[16,512]{1,0:T(8,128)}, f32[16,512]{1,0:T(8,128)}) custom-call(s32[1]{0:T(128)} %bitcast.36.place_ref, bf16[4,2,1,128,512]{4,3,2,1,0:T(8,128)(2,1)} %fusion.49.signal_ref, bf16[4,2,1,128,512]{4,3,2,1,0:T(8,128)(2,1)} %get-tuple-element.786.signal_ref.grad_ref, ...), custom_call_target="tpu_custom_call" | custom-call | flops 100663296 | bytes 4521984 | tf_op jit(solution)/shard_map/pallas_call | solution.py:560
  507.5 10.4 %convolution_convert_fusion = bf16[2048,1536]{1,0:T(8,128)(2,1)} fusion(bf16[1088,2048]{1,0:T(8,128)(2,1)S(1)} %bitcast.395, bf16[1088,1024]{1,0:T(8,128)(2,1)S(1)} %bitcast.384, bf16[1088,512]{1,0:T(8,128)(2,1)S(1)} %bitcast.391), kind=kOutput, calls=%fused_computation.1 | convolution fusion | flops 6854934528 | bytes 14090240 | tf_op jit(solution)/shard_map/dot_general | solution.py:651
  517.9 10.3 %convolution_convert_fusion.5 = bf16[1088,2048]{1,0:T(8,128)(2,1)S(1)} fusion(bf16[1088,1536]{1,0:T(8,128)(2,1)} %pad_maximum_fusion.7, bf16[2048,1536]{1,0:T(8,128)(2,1)} %all-gather.5.cloned.1.call-done), kind=kOutput, calls=%fused_computation.6 | convolution fusion | flops 6847332352 | bytes 14090240 | tf_op jit(solution)/shard_map/dot_general | solution.py:647
  554.9 7.5 %collective-permute-done.51 = bf16[1,256,1408]{2,1,0:T(8,128)(2,1)S(1)} collective-permute-done((bf16[1,256,1408]{2,1,0:T(8,128)(2,1)S(1)}, bf16[1,256,1408]{2,1,0:T(8,128)(2,1)S(1)}, u32[]{:S(2)}, u32[]{:S(2)}) %collective-permute-start.51) | collective-permute-done | bytes 720928 | tf_op jit(solution)/shard_map/ppermute | solution.py:20
  574.3 5.9 shard_map.225
  580.2 11.0 %collective-permute-done.49 = bf16[2,136,2048]{2,1,0:T(8,128)(2,1)} collective-permute-done((bf16[2,136,2048]{2,1,0:T(8,128)(2,1)}, bf16[2,136,2048]{2,1,0:T(8,128)(2,1)}, u32[]{:S(2)}, u32[]{:S(2)}) %collective-permute-start.49) | collective-permute-done | bytes 1114144 | tf_op jit(solution)/shard_map/ppermute | solution.py:20
  602.5 10.5 %collective-permute-done.56 = bf16[1,256,1408]{2,1,0:T(8,128)(2,1)} collective-permute-done((bf16[1,256,1408]{2,1,0:T(8,128)(2,1)S(1)}, bf16[1,256,1408]{2,1,0:T(8,128)(2,1)}, u32[]{:S(2)}, u32[]{:S(2)}) %collective-permute-start.56) | collective-permute-done | bytes 720928 | tf_op jit(solution)/shard_map/ppermute | solution.py:20
  615.5 8.5 %collective-permute-done.54 = bf16[136,2048]{1,0:T(8,128)(2,1)} collective-permute-done((bf16[136,2048]{1,0:T(8,128)(2,1)}, bf16[136,2048]{1,0:T(8,128)(2,1)}, u32[]{:S(2)}, u32[]{:S(2)}) %collective-permute-start.54) | collective-permute-done | bytes 557088 | tf_op jit(solution)/shard_map/ppermute | solution.py:20
  631.7 6.2 shard_map.226
  684.5 6.6 collective-permute-done.67
  (534 shorter events, 356.9 us)
Async XLA Ops:
  7.2 88.5 %all-gather.5.cloned.1.call-start = ((), (), s32[]{:S(2)}) async-start(), calls=%async_computation.5 | async-start | bytes 7077888 | tf_op jit(solution)/shard_map/all_gather | solution.py:238
  26.8 222.9 %all-gather.7.cloned.1.call-start = ((), (), s32[]{:S(2)}) async-start(), calls=%async_computation.6 | async-start | bytes 6488064 | tf_op jit(solution)/shard_map/all_gather | solution.py:238
  52.6 237.7 %all-gather.11.cloned.1.call-start = ((), (), s32[]{:S(2)}) async-start(), calls=%async_computation.8 | async-start | bytes 6488064 | tf_op jit(solution)/shard_map/all_gather | solution.py:238
  53.4 23.5 %collective-permute-start.4 = (bf16[2,1,136,2048]{3,2,0,1:T(8,128)(2,1)}, bf16[2,1,136,2048]{3,2,0,1:T(8,128)(2,1)}, u32[]{:S(2)}, u32[]{:S(2)}) collective-permute-start(bf16[2,1,136,2048]{3,2,0,1:T(8,128)(2,1)} %bitcast.397), channel_id=1, source_target_pairs={{0,16},{16,0},{1,17},{17,1},{2,18},{18,2},{3,19},{19,3},{4,20},{20... | collective-permute-start | bytes 3342344 | tf_op jit(solution)/shard_map/ppermute | solution.py:20
  61.2 27.9 %collective-permute-start.6 = (bf16[1,128,2048]{2,1,0:T(8,128)(2,1)S(1)}, bf16[1,128,2048]{2,1,0:T(8,128)(2,1)S(1)}, u32[]{:S(2)}, u32[]{:S(2)}) collective-permute-start(bf16[1,128,2048]{2,1,0:T(8,128)(2,1)S(1)} %get-tuple-element.556), channel_id=1, source_target_pairs={{0,1},{1,0},{2,3},{3,2},{4,5},{5,4},{6,7},{7,6},{8,9},{9,8},{10,11... | collective-permute-start | bytes 1572872 | tf_op jit(solution)/shard_map/ppermute | solution.py:20
  61.4 27.6 %collective-permute-start.7 = (bf16[1,128,2048]{2,1,0:T(8,128)(2,1)S(1)}, bf16[1,128,2048]{2,1,0:T(8,128)(2,1)S(1)}, u32[]{:S(2)}, u32[]{:S(2)}) collective-permute-start(bf16[1,128,2048]{2,1,0:T(8,128)(2,1)S(1)} %get-tuple-element.558), channel_id=1, source_target_pairs={{0,16},{16,0},{1,17},{17,1},{2,18},{18,2},{3,19},{19,3},{4,20},{20... | collective-permute-start | bytes 1572872 | tf_op jit(solution)/shard_map/ppermute | solution.py:20
  61.7 54.2 %collective-permute-start.16 = (bf16[256,1408]{1,0:T(8,128)(2,1)}, bf16[256,1408]{1,0:T(8,128)(2,1)}, u32[]{:S(2)}, u32[]{:S(2)}) collective-permute-start(bf16[256,1408]{1,0:T(8,128)(2,1)} %concatenate.265), channel_id=1, source_target_pairs={{0,1},{9,8},{2,3},{11,10},{4,5},{13,12},{6,7},{15,14},{16,17},{25,... | collective-permute-start | bytes 2162696 | tf_op jit(solution)/shard_map/ppermute | solution.py:192
  94.7 28.6 %collective-permute-start.14 = (bf16[2,1,128,2048]{3,2,0,1:T(8,128)(2,1)}, bf16[2,1,128,2048]{3,2,0,1:T(8,128)(2,1)}, u32[]{:S(2)}, u32[]{:S(2)}) collective-permute-start(bf16[2,1,128,2048]{3,2,0,1:T(8,128)(2,1)} %bitcast.37), channel_id=1, source_target_pairs={{0,16},{16,0},{1,17},{17,1},{2,18},{18,2},{3,19},{19,3},{4,20},{20... | collective-permute-start | bytes 3145736 | tf_op jit(solution)/shard_map/ppermute | solution.py:20
  94.8 28.4 %collective-permute-start.15 = (bf16[2,1,128,2048]{3,2,0,1:T(8,128)(2,1)}, bf16[2,1,128,2048]{3,2,0,1:T(8,128)(2,1)}, u32[]{:S(2)}, u32[]{:S(2)}) collective-permute-start(bf16[2,1,128,2048]{3,2,0,1:T(8,128)(2,1)} %pad_maximum_fusion.19), channel_id=1, source_target_pairs={{0,1},{1,0},{2,3},{3,2},{4,5},{5,4},{6,7},{7,6},{8,9},{9,8},{10,11... | collective-permute-start | bytes 3145736 | tf_op jit(solution)/shard_map/ppermute | solution.py:20
  118.2 195.6 %all-gather.9.cloned.1.call-start = ((), (), s32[]{:S(2)}) async-start(), calls=%async_computation.7 | async-start | bytes 6488064 | tf_op jit(solution)/shard_map/all_gather | solution.py:238
  118.6 31.4 %collective-permute-start.12 = (bf16[128,1024]{1,0:T(8,128)(2,1)S(1)}, bf16[128,1024]{1,0:T(8,128)(2,1)S(1)}, u32[]{:S(2)}, u32[]{:S(2)}) collective-permute-start(bf16[128,1024]{1,0:T(8,128)(2,1)S(1)} %dynamic_slice.214), channel_id=1, source_target_pairs={{0,4},{2,6},{4,0},{6,2},{1,5},{3,7},{5,1},{7,3},{8,12},{10,14},{12... | collective-permute-start | bytes 786440 | tf_op jit(solution)/shard_map/ppermute | solution.py:20
  121.2 46.7 %collective-permute-start.13 = (bf16[128,1024]{1,0:T(8,128)(2,1)S(1)}, bf16[128,1024]{1,0:T(8,128)(2,1)S(1)}, u32[]{:S(2)}, u32[]{:S(2)}) collective-permute-start(bf16[128,1024]{1,0:T(8,128)(2,1)S(1)} %dynamic_slice.214), channel_id=1, source_target_pairs={{0,2},{2,4},{4,6},{6,0},{1,3},{3,5},{5,7},{7,1},{8,10},{10,12},{12... | collective-permute-start | bytes 786440 | tf_op jit(solution)/shard_map/ppermute | solution.py:20
  180.7 24.3 %collective-permute-start.24 = (bf16[256,1408]{1,0:T(8,128)(2,1)}, bf16[256,1408]{1,0:T(8,128)(2,1)S(1)}, u32[]{:S(2)}, u32[]{:S(2)}) collective-permute-start(bf16[256,1408]{1,0:T(8,128)(2,1)} %concatenate.274), channel_id=1, source_target_pairs={{0,1},{9,8},{2,3},{11,10},{4,5},{13,12},{6,7},{15,14},{16,17},{25,... | collective-permute-start | bytes 2162696 | tf_op jit(solution)/shard_map/ppermute | solution.py:192
  185.5 28.3 %collective-permute-start.23 = (bf16[2,1,256,1024]{3,2,0,1:T(8,128)(2,1)}, bf16[2,1,256,1024]{3,2,0,1:T(8,128)(2,1)}, u32[]{:S(2)}, u32[]{:S(2)}) collective-permute-start(bf16[2,1,256,1024]{3,2,0,1:T(8,128)(2,1)} %pad_maximum_fusion.23), channel_id=1, source_target_pairs={{0,1},{1,0},{2,3},{3,2},{4,5},{5,4},{6,7},{7,6},{8,9},{9,8},{10,11... | collective-permute-start | bytes 3145736 | tf_op jit(solution)/shard_map/ppermute | solution.py:20
  228.3 224.2 %reduce-scatter.8.cloned.1.call-start = ((), (), s32[]{:S(2)}) async-start(), calls=%async_computation.10 | async-start | bytes 6488064 | tf_op jit(solution)/shard_map/reduce_scatter | solution.py:242
  263.9 23.3 %collective-permute-start.28 = (bf16[2,1,128,2048]{3,2,0,1:T(8,128)(2,1)S(1)}, bf16[2,1,128,2048]{3,2,0,1:T(8,128)(2,1)S(1)}, u32[]{:S(2)}, u32[]{:S(2)}) collective-permute-start(bf16[2,1,128,2048]{3,2,0,1:T(8,128)(2,1)S(1)} %pad_maximum_fusion.24), channel_id=1, source_target_pairs={{0,16},{16,0},{1,17},{17,1},{2,18},{18,2},{3,19},{19,3},{4,20},{20... | collective-permute-start | bytes 3145736 | tf_op jit(solution)/shard_map/ppermute | solution.py:20
  313.7 230.4 %reduce-scatter.6.cloned.1.call-start = ((), (), s32[]{:S(2)}) async-start(), calls=%async_computation.9 | async-start | bytes 6488064 | tf_op jit(solution)/shard_map/reduce_scatter | solution.py:242
  361.6 240.9 %reduce-scatter.10.cloned.1.call-start = ((), (), s32[]{:S(2)}) async-start(), calls=%async_computation.11 | async-start | bytes 6488064 | tf_op jit(solution)/shard_map/reduce_scatter | solution.py:242
  391.9 152.2 %collective-permute-start.32 = (bf16[2,128,2048]{2,1,0:T(8,128)(2,1)}, bf16[2,128,2048]{2,1,0:T(8,128)(2,1)}, u32[]{:S(2)}, u32[]{:S(2)}) collective-permute-start(bf16[2,128,2048]{2,1,0:T(8,128)(2,1)} %get-tuple-element.724), channel_id=1, source_target_pairs={{0,1},{1,0},{2,3},{3,2},{4,5},{5,4},{6,7},{7,6},{8,9},{9,8},{10,11... | collective-permute-start | bytes 3145736 | tf_op jit(solution)/shard_map/ppermute | solution.py:20
  392.2 151.9 %collective-permute-start.33 = (bf16[2,128,2048]{2,1,0:T(8,128)(2,1)}, bf16[2,128,2048]{2,1,0:T(8,128)(2,1)}, u32[]{:S(2)}, u32[]{:S(2)}) collective-permute-start(bf16[2,128,2048]{2,1,0:T(8,128)(2,1)} %bitcast.117), channel_id=1, source_target_pairs={{0,16},{16,0},{1,17},{17,1},{2,18},{18,2},{3,19},{19,3},{4,20},{20... | collective-permute-start | bytes 3145736 | tf_op jit(solution)/shard_map/ppermute | solution.py:20
  420.9 231.9 %reduce-scatter.14.cloned.1.call-start = ((), (), s32[]{:S(2)}) async-start(), calls=%async_computation.13 | async-start | bytes 7077888 | tf_op jit(solution)/shard_map/reduce_scatter | solution.py:242
  452.6 82.9 %collective-permute-start.41 = (bf16[2,1,128,2048]{3,2,0,1:T(8,128)(2,1)}, bf16[2,1,128,2048]{3,2,0,1:T(8,128)(2,1)}, u32[]{:S(2)}, u32[]{:S(2)}) collective-permute-start(bf16[2,1,128,2048]{3,2,0,1:T(8,128)(2,1)} %pad_maximum_fusion.26), channel_id=1, source_target_pairs={{0,16},{16,0},{1,17},{17,1},{2,18},{18,2},{3,19},{19,3},{4,20},{20... | collective-permute-start | bytes 3145736 | tf_op jit(solution)/shard_map/ppermute | solution.py:20
  454.7 80.8 %collective-permute-start.42 = (bf16[2,1,128,2048]{3,2,0,1:T(8,128)(2,1)}, bf16[2,1,128,2048]{3,2,0,1:T(8,128)(2,1)}, u32[]{:S(2)}, u32[]{:S(2)}) collective-permute-start(bf16[2,1,128,2048]{3,2,0,1:T(8,128)(2,1)} %bitcast.414), channel_id=1, source_target_pairs={{0,1},{1,0},{2,3},{3,2},{4,5},{5,4},{6,7},{7,6},{8,9},{9,8},{10,11... | collective-permute-start | bytes 3145736 | tf_op jit(solution)/shard_map/ppermute | solution.py:20
  455.9 42.2 %collective-permute-start.46 = (bf16[256,1408]{1,0:T(8,128)(2,1)}, bf16[256,1408]{1,0:T(8,128)(2,1)S(1)}, u32[]{:S(2)}, u32[]{:S(2)}) collective-permute-start(bf16[256,1408]{1,0:T(8,128)(2,1)} %reduce-scatter.8.cloned.1.call-done), channel_id=1, source_target_pairs={{8,1},{1,8},{10,3},{3,10},{12,5},{5,12},{14,7},{7,14},{24,17},{17,... | collective-permute-start | bytes 2162696 | tf_op jit(solution)/shard_map/ppermute | solution.py:267
  530.3 141.1 %reduce-scatter.12.cloned.1.call-start = ((), (), s32[]{:S(2)}) async-start(), calls=%async_computation.12 | async-start | bytes 2359296 | tf_op jit(solution)/shard_map/reduce_scatter | solution.py:242
  553.3 37.9 %collective-permute-start.49 = (bf16[2,136,2048]{2,1,0:T(8,128)(2,1)}, bf16[2,136,2048]{2,1,0:T(8,128)(2,1)}, u32[]{:S(2)}, u32[]{:S(2)}) collective-permute-start(bf16[2,136,2048]{2,1,0:T(8,128)(2,1)} %get-tuple-element.842), channel_id=1, source_target_pairs={{0,1},{1,0},{2,3},{3,2},{4,5},{5,4},{6,7},{7,6},{8,9},{9,8},{10,11... | collective-permute-start | bytes 3342344 | tf_op jit(solution)/shard_map/ppermute | solution.py:20
  553.4 37.8 %collective-permute-start.50 = (bf16[2,136,2048]{2,1,0:T(8,128)(2,1)}, bf16[2,136,2048]{2,1,0:T(8,128)(2,1)}, u32[]{:S(2)}, u32[]{:S(2)}) collective-permute-start(bf16[2,136,2048]{2,1,0:T(8,128)(2,1)} %bitcast.162), channel_id=1, source_target_pairs={{0,16},{16,0},{1,17},{17,1},{2,18},{18,2},{3,19},{19,3},{4,20},{20... | collective-permute-start | bytes 3342344 | tf_op jit(solution)/shard_map/ppermute | solution.py:20
  554.3 43.2 %collective-permute-start.47 = (bf16[128,2048]{1,0:T(8,128)(2,1)}, bf16[128,2048]{1,0:T(8,128)(2,1)}, u32[]{:S(2)}, u32[]{:S(2)}) collective-permute-start(bf16[128,2048]{1,0:T(8,128)(2,1)} %get-tuple-element.838), channel_id=1, source_target_pairs={{0,16},{16,0},{1,17},{17,1},{2,18},{18,2},{3,19},{19,3},{4,20},{20... | collective-permute-start | bytes 1572872 | tf_op jit(solution)/shard_map/ppermute | solution.py:20
  572.1 25.5 %collective-permute-start.48 = (bf16[128,2048]{1,0:T(8,128)(2,1)}, bf16[128,2048]{1,0:T(8,128)(2,1)S(1)}, u32[]{:S(2)}, u32[]{:S(2)}) collective-permute-start(bf16[128,2048]{1,0:T(8,128)(2,1)} %get-tuple-element.840), channel_id=1, source_target_pairs={{0,1},{1,0},{2,3},{3,2},{4,5},{5,4},{6,7},{7,6},{8,9},{9,8},{10,11... | collective-permute-start | bytes 1572872 | tf_op jit(solution)/shard_map/ppermute | solution.py:20
  573.5 39.5 %collective-permute-start.56 = (bf16[1,256,1408]{2,1,0:T(8,128)(2,1)S(1)}, bf16[1,256,1408]{2,1,0:T(8,128)(2,1)}, u32[]{:S(2)}, u32[]{:S(2)}) collective-permute-start(bf16[1,256,1408]{2,1,0:T(8,128)(2,1)S(1)} %fusion.66), channel_id=1, source_target_pairs={{0,16},{16,0},{1,17},{17,1},{2,18},{18,2},{3,19},{19,3},{4,20},{20... | collective-permute-start | bytes 2162696 | tf_op jit(solution)/shard_map/ppermute | solution.py:20
  597.5 26.4 %collective-permute-start.54 = (bf16[136,2048]{1,0:T(8,128)(2,1)}, bf16[136,2048]{1,0:T(8,128)(2,1)}, u32[]{:S(2)}, u32[]{:S(2)}) collective-permute-start(bf16[136,2048]{1,0:T(8,128)(2,1)} %get-tuple-element.881), channel_id=1, source_target_pairs={{0,16},{16,0},{1,17},{17,1},{2,18},{18,2},{3,19},{19,3},{4,20},{20... | collective-permute-start | bytes 1671176 | tf_op jit(solution)/shard_map/ppermute | solution.py:20
  598.2 25.8 %collective-permute-start.55 = (bf16[136,2048]{1,0:T(8,128)(2,1)}, bf16[136,2048]{1,0:T(8,128)(2,1)}, u32[]{:S(2)}, u32[]{:S(2)}) collective-permute-start(bf16[136,2048]{1,0:T(8,128)(2,1)} %get-tuple-element.883), channel_id=1, source_target_pairs={{0,1},{1,0},{2,3},{3,2},{4,5},{5,4},{6,7},{7,6},{8,9},{9,8},{10,11... | collective-permute-start | bytes 1671176 | tf_op jit(solution)/shard_map/ppermute | solution.py:20
  (119 other events, 1270.4 us)
Sparse Core Ops, SparseCore 0:
  26.9 65.2 all-gather.4
  94.5 78.2 all-gather.6
  175.0 63.6 all-gather.10
  240.2 59.0 all-gather.8
  313.8 64.4 reduce-scatter.7
  381.0 63.1 reduce-scatter.5
  446.5 70.3 reduce-scatter.9
  530.4 69.6 reduce-scatter.13
  630.9 29.3 reduce-scatter.11

commit v10 on v9

--- a/solution.py
+++ b/solution.py
@@ -229,11 +229,6 @@
     return core_halves(rows)[0]
 
 
-def by_z(slots):
-    held = in_order(jnp.stack(slots), "z")
-    return held.reshape(2, -1, held.shape[-1])
-
-
 def gather_tile(block):
     return lax.all_gather(block, ("z", "c"), axis=0, tiled=True)
 
@@ -681,6 +676,7 @@
     def stacked(value, got):
         return jnp.stack([value] + got)
 
+    w_out = lax.all_gather(run(out_block, out_weight), "z", axis=0, tiled=True)
     in_got = column_moves(run(lambda w: column_pieces(w, 3), in_weight))
     last = [(i * spread + spread - 1, (i + 1) * spread) for i in range(depth - 1)]
 
@@ -692,7 +688,6 @@
 
     normed, ending, scale_one = run(norm_one, tokens, norm_gain)
     before = lax.ppermute(ending, ("z", "x"), last)
-    w_in = gather_tile(run(column_block, in_got))
 
     def lengthen(values, rows):
         rest = jnp.zeros((batch, extra - 2, width), values.dtype)
@@ -700,9 +695,11 @@
         return values[: batch // 2], values[batch // 2 :]
 
     normed_move = Gather(*run(lengthen, normed, before))
+    gate_got = column_moves(run(lambda w: column_pieces(w, 1), gate_weight))
+    in_block, w_out = run(lambda got, w: (column_block(got), w), in_got, w_out)
+    w_in = gather_tile(in_block)
     normed_move.turn(line)
     w_down = gather_tile(run(row_block, down_weight))
-    gate_got = column_moves(run(lambda w: column_pieces(w, 1), gate_weight))
 
     def feed_grad(values):
         values = (values.astype(wide) * mask).astype(low)
@@ -711,8 +708,6 @@
     feed_move = Gather(*run(feed_grad, cotangent))
     normed_all = normed_move.end(line)
     feed_move.turn(line)
-    block_out = run(out_block, out_weight)
-    out_got = moved(block_out, "z", -1)
 
     channels = w_in.shape[1] // 3
     half = channels // 2
@@ -759,9 +754,8 @@
     product, state_end = run(multiply, mixed, taps, decay)
     states = [passed(state_end, "z", k) for k in range(1, depth)]
     w_gate = gather_tile(run(column_block, gate_got))
+    out_move = Gather(*run(lambda w: (w[None, : w.shape[0] // 2], w[None, w.shape[0] // 2 :]), w_out))
     grad_feed_all = feed_move.end(line)
-    held = run(lambda own, got: by_z([own] + got), block_out, out_got)
-    out_move = Gather(held[:1], held[1:])
     up_got = column_moves(run(lambda w: column_pieces(w, 1), up_weight))
     out_move.turn(line)
 
@@ -838,7 +832,12 @@
     )
     gate_mine = scatter_tile(run(dot_w, normed_two_all, grad_gate))
     two_back.turn(line)
-    feed_parts = run(lambda a, w: split_sum(dot(a, w, low)), active, w_down)
+
+    def feed_slots(a, w):
+        value = dot(a, w, low).reshape(2, ycount, spread, -1, width)
+        return [[value[:, k, i] for i in range(spread)] for k in range(ycount)]
+
+    feed_parts = run(feed_slots, active, w_down)
 
     def middle_back(rest, values, scale, gain, back, weights):
         grad_normed = Scatter.sum(*rest).reshape(batch, local, width)
@@ -856,14 +855,14 @@
 
         slots = [[slot(k * spread + i) for i in range(spread)] for k in range(ycount)]
         rounded = result.astype(low)
-        return result, grad_gain, rounded[: batch // 2], rounded[batch // 2 :], slots
-
-    grad_middle, grad_feed_gain, first, second, grad_slots = run(
+        return result, grad_gain, rounded.reshape(2, -1, width), slots
+
+    grad_middle, grad_feed_gain, grad_mix, grad_slots = run(
         middle_back, two_back.rest(), middle, scale_two, feed_gain, cotangent, w_out
     )
     grad_got = swap_slots(grad_slots)
     down_mine = scatter_tile(run(dot_w, active, grad_feed_all))
-    mix_move = Gather(first, second)
+    mix_got = swap_slots([[grad_mix] * spread] * ycount)
 
     def conv_grads(got, result, value, weights, rates):
         grad = jnp.stack([jnp.stack(row) for row in got])
@@ -875,7 +874,6 @@
 
     grad_query, grad_conv, later_end = run(conv_grads, grad_got, convolved, mixed, taps, decay)
     laters = [passed(later_end, "z", -k) for k in range(1, depth)]
-    mix_move.turn(line)
 
     def short_back(grad, weights):
         head = jnp.roll(grad[:, :, :, :2], -1, axis=1)
@@ -891,7 +889,7 @@
         result = jnp.concatenate([result, jnp.where(opening, earlier, 0.0), rest], axis=3)
         return result.astype(low).reshape(-1, grad.shape[-1])
 
-    feed_back = Scatter(feed_parts)
+    feed_got = swap_slots(feed_parts)
     up_parts_got = owner_moves(run(owner_parts, up_mine))
 
     def conv_back(signal, grad, rates, amounts, begin, ends_later, value, weights):
@@ -924,10 +922,19 @@
     grad_mixed, in_term = run(in_back, grad_query, grad_pair, taps, normed_all)
     in_mine = scatter_tile(in_term)
     one_back = Scatter(run(lambda a, w: split_sum(dot_t(a, w, low)), grad_mixed, w_in))
-    grad_mix_all = mix_move.end(line)
+    grad_mix_all = run(
+        lambda got: jnp.concatenate([g[h] for h in range(2) for row in got for g in row]), mix_got
+    )
     out_mine = scatter_tile(run(dot_w, gated_all, grad_mix_all))
     gate_got = owner_moves(run(owner_parts, gate_mine))
-    feed_back.turn(line)
+    output = run(
+        lambda got, values: (
+            mask
+            * (values + add_up(got[0][:1], got[0][1:] + sum(got[1:], [])).reshape(batch, local, width))
+        ).astype(low),
+        feed_got,
+        middle,
+    )
     up_held = run(stacked, up_held, up_got)
     up_got = moved(up_held, "c", -1)
 
@@ -954,17 +961,11 @@
 
     grad_up_weight = run(column_whole, up_held, up_got)
     one_back.turn(line)
-    output = run(
-        lambda rest, values: (
-            mask * (values + Scatter.sum(*rest).reshape(batch, local, width))
-        ).astype(low),
-        feed_back.rest(),
-        middle,
-    )
     down_held = run(lambda v: v[None], down_mine)
     down_got = moved(down_held, "y", -1)
     gate_held = run(stacked, gate_held, gate_got)
     gate_got = moved(gate_held, "c", -1)
+    in_got = owner_moves(run(owner_parts, in_mine))
     grad_normed, grad_before = run(normed_sum, one_back.rest())
     grad_after = lax.ppermute(grad_before, ("z", "x"), [(j, i) for i, j in last])
     grad_gate_weight = run(column_whole, gate_held, gate_got)
@@ -989,19 +990,18 @@
         (grad_feed_gain, grad_residue, grad_decay, grad_taps),
     )
     small_got = moved(small, "c", 1)
+    in_held = run(owner_held, in_got)
+    in_got = moved(in_held, "y", -1)
     down_held = run(lambda own, got: jnp.concatenate([own] + got), down_held, down_got)
     down_got = moved(down_held, "c", -1)
     small = run(lambda v, got: v + sum(got), small, small_got)
     small_got = moved(small, "z", 1)
-    in_got = owner_moves(run(owner_parts, in_mine))
 
     def rows_whole(own, got):
         whole = in_order(jnp.swapaxes(in_order(jnp.stack([own] + got), "c"), 0, 1), "y")
         return whole.reshape(-1, width).astype(wide)
 
     grad_down = run(rows_whole, down_held, down_got)
-    in_held = run(owner_held, in_got)
-    in_got = moved(in_held, "y", -1)
     out_held = run(lambda v: v[None], out_mine)
     out_got = moved(out_held, "y", -1)
     small = run(lambda v, got: v + sum(got), small, small_got)

time: 726 us -> 722 us (level)
  waiting for transfers between devices: 216 us -> 225 us
  starting transfers between devices: 97 us -> 88.4 us
  other arithmetic: 119 us -> 111 us
    ppermute x52 -> x41, waiting for transfers between devices: 177 us -> 164 us  [turned(): lax.ppermute(value, axis, [(i, (i + by) % length) for i in range(length)])]
    ppermute x3, waiting for transfers between devices: 7.29 us -> 18.5 us  [owner_moves(): got.append(lax.ppermute(parts[d], ('c', 'x'), pairs))]
    ppermute x6 -> x12, waiting for transfers between devices: 20 us -> 29.9 us  [swap_slots(): line.append(lax.ppermute(slots[sy][sx], ('y', 'x'), pairs))]
    ppermute x52 -> x41, starting transfers between devices: 46.3 us -> 36.5 us  [turned(): lax.ppermute(value, axis, [(i, (i + by) % length) for i in range(length)])]
    unnamed x159 -> x164, local copies, waits for them, and re-layouts: 22.8 us -> 29.5 us
    another operation x15 -> x12, other arithmetic: 21.6 us -> 16.2 us  [work(): return jnp.stack([first, second]).reshape(-1, first.shape[-1])]
  transfers between devices with their start and end apart: 81 -> 77, of which waited for: 35 -> 37; matrix products, arithmetic and copies ran while one was open for 42% -> 42% of each run, Pallas kernels for 7% -> 8%
where the time goes in v10:
time: 722 us; the launch traced here: 710 us
  waiting for transfers between devices  225 us (31%)
  matrix products  141 us (20%)
  other arithmetic  111 us (15%)
  starting transfers between devices  88.4 us (12%)
  local copies, waits for them, and re-layouts  70.1 us (10%)
  Pallas kernels  57.2 us (8%)
  between operations  16.5 us (2%)
    ppermute x41, waiting for transfers between devices, turned(): lax.ppermute(value, axis, [(i, (i + by) % length) for i in range(length)])  164 us
    dot_general x6, matrix products, dot(): return jnp.dot(a, b, preferred_element_type=wide).astype(kind)  55 us
    dot_general x6, matrix products, dot_t(): lax.dot_general(a, b, (((1,), (1,)), ((), ())), preferred_element_type=wide)  46.9 us
    dot_general x5, matrix products, dot_w(): lax.dot_general(a, b, (((0,), (0,)), ((), ())), preferred_element_type=wide)  39.6 us
    ppermute x41, starting transfers between devices, turned(): lax.ppermute(value, axis, [(i, (i + by) % length) for i in range(length)])  36.5 us
    pallas_call x4, Pallas kernels, conv_call(): pl.pallas_call(kernel, out_shape=results, grid_spec=pltpu.PrefetchScalarG...  35.5 us
    ppermute x12, waiting for transfers between devices, swap_slots(): line.append(lax.ppermute(slots[sy][sx], ('y', 'x'), pairs))  29.9 us
    unnamed x164, local copies, waits for them, and re-layouts  29.5 us
  transfers between devices with their start and end apart: 77, of which 37 were waited for; matrix products, arithmetic and copies ran while one was open for 42% of the time, Pallas kernels for 8%

profile of v10, /device:TPU:9, one launch (start us, length us, event | category | flops | bytes accessed | tf_op | source)
XLA Modules:
  0.0 709.6 jit_solution(10565974289812867920)
XLA Ops:
  43.9 10.9 %collective-permute-done.1 = bf16[1,136,2048]{2,1,0:T(8,128)(2,1)} collective-permute-done((bf16[1,136,2048]{2,1,0:T(8,128)(2,1)S(1)}, bf16[1,136,2048]{2,1,0:T(8,128)(2,1)}, u32[]{:S(2)}, u32[]{:S(2)}) %collective-permute-start.1) | collective-permute-done | bytes 557088 | tf_op jit(solution)/shard_map/ppermute | solution.py:20
  69.9 16.0 %collective-permute-done.4 = bf16[2,1,136,2048]{3,2,0,1:T(8,128)(2,1)S(1)} collective-permute-done((bf16[2,1,136,2048]{3,2,0,1:T(8,128)(2,1)}, bf16[2,1,136,2048]{3,2,0,1:T(8,128)(2,1)S(1)}, u32[]{:S(2)}, u32[]{:S(2)}) %collective-permute-start.4) | collective-permute-done | bytes 1114144 | tf_op jit(solution)/shard_map/ppermute | solution.py:20
  92.4 15.8 %collective-permute-done.6 = bf16[1,128,2048]{2,1,0:T(8,128)(2,1)S(1)} collective-permute-done((bf16[1,128,2048]{2,1,0:T(8,128)(2,1)S(1)}, bf16[1,128,2048]{2,1,0:T(8,128)(2,1)S(1)}, u32[]{:S(2)}, u32[]{:S(2)}) %collective-permute-start.6) | collective-permute-done | bytes 524320 | tf_op jit(solution)/shard_map/ppermute | solution.py:20
  112.7 10.9 %convolution_convert_fusion.4 = bf16[1088,1536]{1,0:T(8,128)(2,1)S(1)} fusion(bf16[1088,2048]{1,0:T(8,128)(2,1)} %bitcast.380, bf16[2048,1536]{1,0:T(8,128)(2,1)} %all-gather.8.cloned.1.call-done), kind=kOutput, calls=%fused_computation.5 | convolution fusion | flops 6846775296 | bytes 14090240 | tf_op jit(solution)/shard_map/dot_general | solution.py:638
  144.6 14.1 %collective-permute-done.14 = bf16[2,1,128,2048]{3,2,0,1:T(8,128)(2,1)S(1)} collective-permute-done((bf16[2,1,128,2048]{3,2,0,1:T(8,128)(2,1)S(1)}, bf16[2,1,128,2048]{3,2,0,1:T(8,128)(2,1)S(1)}, u32[]{:S(2)}, u32[]{:S(2)}) %collective-permute-start.14) | collective-permute-done | bytes 1048608 | tf_op jit(solution)/shard_map/ppermute | solution.py:20
  188.6 8.9 %shard_map.222 = bf16[4,2,1,128,512]{4,3,2,1,0:T(8,128)(2,1)} custom-call(s32[1]{0:T(128)} %bitcast.36.place_ref, bf16[4,2,1,128,512]{4,3,2,1,0:T(8,128)(2,1)} %fusion.49.signal_ref, f32[16,512]{1,0:T(8,128)} %maximum_bitcast_fusion.9.decay_ref, f32[16,512]{1,0:T(8,128)} %maximum_bitcast_fusion.10.residue_ref, f32[4,16,512]{2,1,0:T(8,128)} %multiply_add_fusion.2.start_ref), custom_call_target="tpu_custom_call" | custom-call | flops 33554432 | bytes 2293760 | tf_op jit(solution)/shard_map/pallas_call | solution.py:555
  203.4 5.8 collective-permute-done.20
  223.9 5.4 collective-permute-done.17
  241.4 11.9 %fusion.118 = f32[1024,1408]{1,0:T(8,128)} fusion(bf16[1024,2048]{1,0:T(8,128)(2,1)} %bitcast.390, bf16[1408,2048]{1,0:T(8,128)(2,1)} %all-gather.10.cloned.1.call-done), kind=kOutput, calls=%fused_computation.414 | convolution fusion | flops 5905580032 | bytes 15728640 | tf_op jit(solution)/shard_map/dot_general | solution.py:642
  255.2 22.1 %collective-permute-done.25 = bf16[2,1,128,2048]{3,2,0,1:T(8,128)(2,1)S(1)} collective-permute-done((bf16[2,1,128,2048]{3,2,0,1:T(8,128)(2,1)S(1)}, bf16[2,1,128,2048]{3,2,0,1:T(8,128)(2,1)S(1)}, u32[]{:S(2)}, u32[]{:S(2)}) %collective-permute-start.25) | collective-permute-done | bytes 1048608 | tf_op jit(solution)/shard_map/ppermute | solution.py:20
  281.3 13.2 %multiply_convert_fusion.2 = (bf16[1024,1408]{1,0:T(8,128)(2,1)S(1)}, f32[1024,1408]{1,0:T(8,128)}) fusion(f32[1024,1408]{1,0:T(8,128)} %fusion.118, bf16[1024,2048]{1,0:T(8,128)(2,1)} %bitcast.392, bf16[2048,1408]{1,0:T(8,128)(2,1)} %all-gather.14.cloned.1.call-done), kind=kOutput, calls=%fused_computation.10 | convolution fusion | flops 5914230784 | bytes 24379392 | tf_op jit(solution)/shard_map/dot_general | solution.py:638
  296.1 8.7 %convolution_convert_fusion.3 = bf16[2048,1408]{1,0:T(8,128)(2,1)} fusion(bf16[1024,2048]{1,0:T(8,128)(2,1)S(1)} %bitcast.394, bf16[1024,1408]{1,0:T(8,128)(2,1)S(1)} %get-tuple-element.683), kind=kOutput, calls=%fused_computation.4 | convolution fusion | flops 5908463616 | bytes 12845056 | tf_op jit(solution)/shard_map/dot_general | solution.py:646
  304.8 15.3 %multiply_convert_fusion = (bf16[1024,1408]{1,0:T(8,128)(2,1)S(1)}, bf16[1024,1408]{1,0:T(8,128)(2,1)}) fusion(f32[1024,1408]{1,0:T(8,128)} %get-tuple-element.673, f32[1024,1408]{1,0:T(8,128)} %fusion.118, bf16[1024,2048]{1,0:T(8,128)(2,1)} %bitcast.393, bf16[2048,1408]{1,0:T(8,128)(2,1)} %all-gather.12.cloned.1.call-done), kind=kOutput, calls=%fused_computation.7 | convolution fusion | flops 5924323328 | bytes 27262976 | tf_op jit(solution)/shard_map/dot_general | solution.py:638
  321.7 8.9 %fusion.119 = f32[1024,2048]{1,0:T(8,128)S(1)} fusion(bf16[1024,1408]{1,0:T(8,128)(2,1)S(1)} %get-tuple-element.692, bf16[2048,1408]{1,0:T(8,128)(2,1)} %all-gather.14.cloned.1.call-done), kind=kOutput, calls=%fused_computation.415 | convolution fusion | flops 5905580032 | bytes 17039360 | tf_op jit(solution)/shard_map/dot_general | solution.py:642
  330.6 8.4 %add_convert_fusion = bf16[1024,2048]{1,0:T(8,128)(2,1)S(1)} fusion(f32[1024,2048]{1,0:T(8,128)S(1)} %fusion.119, bf16[1024,1408]{1,0:T(8,128)(2,1)} %copy-done.65, bf16[2048,1408]{1,0:T(8,128)(2,1)S(1)} %copy-done.61), kind=kOutput, calls=%fused_computation | convolution fusion | flops 5909774336 | bytes 21233664 | tf_op jit(solution)/shard_map/dot_general | solution.py:642
  344.1 8.7 %convolution_convert_fusion.2 = bf16[2048,1408]{1,0:T(8,128)(2,1)} fusion(bf16[1024,2048]{1,0:T(8,128)(2,1)S(1)} %bitcast.395, bf16[1024,1408]{1,0:T(8,128)(2,1)S(1)} %copy-done.64), kind=kOutput, calls=%fused_computation.3 | convolution fusion | flops 5908463616 | bytes 12845056 | tf_op jit(solution)/shard_map/dot_general | solution.py:646
  354.1 21.7 %collective-permute-done.27 = bf16[2,128,2048]{2,1,0:T(8,128)(2,1)} collective-permute-done((bf16[2,128,2048]{2,1,0:T(8,128)(2,1)}, bf16[2,128,2048]{2,1,0:T(8,128)(2,1)}, u32[]{:S(2)}, u32[]{:S(2)}) %collective-permute-start.27) | collective-permute-done | bytes 1048608 | tf_op jit(solution)/shard_map/ppermute | solution.py:20
  381.2 8.7 %convolution_convert_fusion.6 = bf16[1024,2048]{1,0:T(8,128)(2,1)S(1)} fusion(bf16[1024,1408]{1,0:T(8,128)(2,1)S(1)} %copy-done.62, bf16[1408,2048]{1,0:T(8,128)(2,1)} %all-gather.10.cloned.1.call-done), kind=kOutput, calls=%fused_computation.25 | convolution fusion | flops 5907677184 | bytes 12845056 | tf_op jit(solution)/shard_map/dot_general | solution.py:638
  405.9 8.1 %convolution_convert_fusion.1 = bf16[1408,2048]{1,0:T(8,128)(2,1)} fusion(bf16[1024,1408]{1,0:T(8,128)(2,1)S(1)} %copy-done.62, bf16[1024,2048]{1,0:T(8,128)(2,1)S(1)} %bitcast.391), kind=kOutput, calls=%fused_computation.2 | convolution fusion | flops 5908463616 | bytes 12845056 | tf_op jit(solution)/shard_map/dot_general | solution.py:646
  444.8 13.6 %collective-permute-start.43 = (bf16[256,1408]{1,0:T(8,128)(2,1)}, bf16[256,1408]{1,0:T(8,128)(2,1)S(1)}, u32[]{:S(2)}, u32[]{:S(2)}) collective-permute-start(bf16[256,1408]{1,0:T(8,128)(2,1)} %reduce-scatter.8.cloned.1.call-done), channel_id=1, source_target_pairs={{8,1},{1,8},{10,3},{3,10},{12,5},{5,12},{14,7},{7,14},{24,17},{17,... | collective-permute-start | bytes 2162696 | tf_op jit(solution)/shard_map/ppermute | solution.py:262
  459.1 16.8 %shard_map.224 = (bf16[4,2,1,128,512]{4,3,2,1,0:T(8,128)(2,1)}, f32[16,512]{1,0:T(8,128)}, f32[16,512]{1,0:T(8,128)}) custom-call(s32[1]{0:T(128)} %bitcast.36.place_ref, bf16[4,2,1,128,512]{4,3,2,1,0:T(8,128)(2,1)} %fusion.49.signal_ref, bf16[4,2,1,128,512]{4,3,2,1,0:T(8,128)(2,1)} %get-tuple-element.758.signal_ref.grad_ref, ...), custom_call_target="tpu_custom_call" | custom-call | flops 100663296 | bytes 4521984 | tf_op jit(solution)/shard_map/pallas_call | solution.py:555
  483.0 13.1 %collective-permute-done.43 = bf16[256,1408]{1,0:T(8,128)(2,1)S(1)} collective-permute-done((bf16[256,1408]{1,0:T(8,128)(2,1)}, bf16[256,1408]{1,0:T(8,128)(2,1)S(1)}, u32[]{:S(2)}, u32[]{:S(2)}) %collective-permute-start.43) | collective-permute-done | bytes 720928 | tf_op jit(solution)/shard_map/ppermute | solution.py:262
  502.7 10.5 %convolution_convert_fusion = bf16[2048,1536]{1,0:T(8,128)(2,1)} fusion(bf16[1088,2048]{1,0:T(8,128)(2,1)S(1)} %bitcast.383, bf16[1088,1024]{1,0:T(8,128)(2,1)S(1)} %bitcast.372, bf16[1088,512]{1,0:T(8,128)(2,1)S(1)} %bitcast.379), kind=kOutput, calls=%fused_computation.1 | convolution fusion | flops 6854934528 | bytes 14090240 | tf_op jit(solution)/shard_map/dot_general | solution.py:646
  513.5 10.3 %convolution_convert_fusion.5 = bf16[1088,2048]{1,0:T(8,128)(2,1)S(1)} fusion(bf16[1088,1536]{1,0:T(8,128)(2,1)} %pad_maximum_fusion.6, bf16[2048,1536]{1,0:T(8,128)(2,1)} %all-gather.8.cloned.1.call-done), kind=kOutput, calls=%fused_computation.6 | convolution fusion | flops 6847332352 | bytes 14090240 | tf_op jit(solution)/shard_map/dot_general | solution.py:642
  542.3 10.1 %collective-permute-done.31 = bf16[2,128,2048]{2,1,0:T(8,128)(2,1)} collective-permute-done((bf16[2,128,2048]{2,1,0:T(8,128)(2,1)}, bf16[2,128,2048]{2,1,0:T(8,128)(2,1)}, u32[]{:S(2)}, u32[]{:S(2)}) %collective-permute-start.31) | collective-permute-done | bytes 1048608 | tf_op jit(solution)/shard_map/ppermute | solution.py:44
  562.1 6.8 collective-permute-done.46
  580.8 5.9 shard_map.225
  586.7 7.0 collective-permute-done.44
  601.0 7.3 %collective-permute-done.51 = bf16[1,256,1408]{2,1,0:T(8,128)(2,1)} collective-permute-done((bf16[1,256,1408]{2,1,0:T(8,128)(2,1)}, bf16[1,256,1408]{2,1,0:T(8,128)(2,1)}, u32[]{:S(2)}, u32[]{:S(2)}) %collective-permute-start.51) | collective-permute-done | bytes 720928 | tf_op jit(solution)/shard_map/ppermute | solution.py:20
  611.2 8.8 %collective-permute-done.49 = bf16[136,2048]{1,0:T(8,128)(2,1)S(1)} collective-permute-done((bf16[136,2048]{1,0:T(8,128)(2,1)S(1)}, bf16[136,2048]{1,0:T(8,128)(2,1)S(1)}, u32[]{:S(2)}, u32[]{:S(2)}) %collective-permute-start.49) | collective-permute-done | bytes 557088 | tf_op jit(solution)/shard_map/ppermute | solution.py:20
  627.0 6.3 shard_map.226
  693.3 5.9 shard_map.227
  (514 shorter events, 347.1 us)
Async XLA Ops:
  7.2 31.8 %all-gather.6.cloned.1.call-start = ((), (), s32[]{:S(2)}) async-start(), calls=%async_computation.5 | async-start | bytes 1310720 | tf_op jit(solution)/shard_map/all_gather | solution.py:679
  9.3 103.4 %all-gather.8.cloned.1.call-start = ((), (), s32[]{:S(2)}) async-start(), calls=%async_computation.6 | async-start | bytes 7077888 | tf_op jit(solution)/shard_map/all_gather | solution.py:233
  41.3 198.4 %all-gather.10.cloned.1.call-start = ((), (), s32[]{:S(2)}) async-start(), calls=%async_computation.7 | async-start | bytes 6488064 | tf_op jit(solution)/shard_map/all_gather | solution.py:233
  61.4 219.9 %all-gather.14.cloned.1.call-start = ((), (), s32[]{:S(2)}) async-start(), calls=%async_computation.9 | async-start | bytes 6488064 | tf_op jit(solution)/shard_map/all_gather | solution.py:233
  61.5 24.4 %collective-permute-start.4 = (bf16[2,1,136,2048]{3,2,0,1:T(8,128)(2,1)}, bf16[2,1,136,2048]{3,2,0,1:T(8,128)(2,1)S(1)}, u32[]{:S(2)}, u32[]{:S(2)}) collective-permute-start(bf16[2,1,136,2048]{3,2,0,1:T(8,128)(2,1)} %bitcast.386), channel_id=1, source_target_pairs={{0,16},{16,0},{1,17},{17,1},{2,18},{18,2},{3,19},{19,3},{4,20},{20... | collective-permute-start | bytes 3342344 | tf_op jit(solution)/shard_map/ppermute | solution.py:20
  62.8 24.1 %collective-permute-start.5 = (bf16[2,1,136,2048]{3,2,0,1:T(8,128)(2,1)}, bf16[2,1,136,2048]{3,2,0,1:T(8,128)(2,1)}, u32[]{:S(2)}, u32[]{:S(2)}) collective-permute-start(bf16[2,1,136,2048]{3,2,0,1:T(8,128)(2,1)} %pad_maximum_fusion.16), channel_id=1, source_target_pairs={{0,1},{1,0},{2,3},{3,2},{4,5},{5,4},{6,7},{7,6},{8,9},{9,8},{10,11... | collective-permute-start | bytes 3342344 | tf_op jit(solution)/shard_map/ppermute | solution.py:20
  63.6 69.7 %collective-permute-start.11 = (bf16[256,1408]{1,0:T(8,128)(2,1)}, bf16[256,1408]{1,0:T(8,128)(2,1)}, u32[]{:S(2)}, u32[]{:S(2)}) collective-permute-start(bf16[256,1408]{1,0:T(8,128)(2,1)} %concatenate.268), channel_id=1, source_target_pairs={{0,1},{9,8},{2,3},{11,10},{4,5},{13,12},{6,7},{15,14},{16,17},{25,... | collective-permute-start | bytes 2162696 | tf_op jit(solution)/shard_map/ppermute | solution.py:192
  66.7 41.5 %collective-permute-start.6 = (bf16[1,128,2048]{2,1,0:T(8,128)(2,1)S(1)}, bf16[1,128,2048]{2,1,0:T(8,128)(2,1)S(1)}, u32[]{:S(2)}, u32[]{:S(2)}) collective-permute-start(bf16[1,128,2048]{2,1,0:T(8,128)(2,1)S(1)} %get-tuple-element.542), channel_id=1, source_target_pairs={{0,1},{1,0},{2,3},{3,2},{4,5},{5,4},{6,7},{7,6},{8,9},{9,8},{10,11... | collective-permute-start | bytes 1572872 | tf_op jit(solution)/shard_map/ppermute | solution.py:20
  69.7 38.6 %collective-permute-start.7 = (bf16[1,128,2048]{2,1,0:T(8,128)(2,1)S(1)}, bf16[1,128,2048]{2,1,0:T(8,128)(2,1)S(1)}, u32[]{:S(2)}, u32[]{:S(2)}) collective-permute-start(bf16[1,128,2048]{2,1,0:T(8,128)(2,1)S(1)} %get-tuple-element.544), channel_id=1, source_target_pairs={{0,16},{16,0},{1,17},{17,1},{2,18},{18,2},{3,19},{19,3},{4,20},{20... | collective-permute-start | bytes 1572872 | tf_op jit(solution)/shard_map/ppermute | solution.py:20
  135.6 169.2 %all-gather.12.cloned.1.call-start = ((), (), s32[]{:S(2)}) async-start(), calls=%async_computation.8 | async-start | bytes 6488064 | tf_op jit(solution)/shard_map/all_gather | solution.py:233
  135.8 24.9 %collective-permute-start.15 = (bf16[2,1,128,2048]{3,2,0,1:T(8,128)(2,1)S(1)}, bf16[2,1,128,2048]{3,2,0,1:T(8,128)(2,1)S(1)}, u32[]{:S(2)}, u32[]{:S(2)}) collective-permute-start(bf16[2,1,128,2048]{3,2,0,1:T(8,128)(2,1)S(1)} %copy-done.25), channel_id=1, source_target_pairs={{0,1},{1,0},{2,3},{3,2},{4,5},{5,4},{6,7},{7,6},{8,9},{9,8},{10,11... | collective-permute-start | bytes 3145736 | tf_op jit(solution)/shard_map/ppermute | solution.py:20
  135.9 43.9 %collective-permute-start.10 = (f32[4,16,512]{2,1,0:T(8,128)S(1)}, f32[4,16,512]{2,1,0:T(8,128)}, u32[]{:S(2)}, u32[]{:S(2)}) collective-permute-start(f32[4,16,512]{2,1,0:T(8,128)S(1)} %copy-done.45), channel_id=1, source_target_pairs={{0,6},{1,7},{8,14},{9,15},{16,22},{17,23},{24,30},{25,31}} | collective-permute-start | bytes 393224 | tf_op jit(solution)/shard_map/ppermute | solution.py:26
  137.2 42.6 %collective-permute-start.8 = (f32[4,16,512]{2,1,0:T(8,128)S(1)}, f32[4,16,512]{2,1,0:T(8,128)}, u32[]{:S(2)}, u32[]{:S(2)}) collective-permute-start(f32[4,16,512]{2,1,0:T(8,128)S(1)} %copy-done.45), channel_id=1, source_target_pairs={{0,2},{2,4},{4,6},{1,3},{3,5},{5,7},{8,10},{10,12},{12,14},{9,11},... | collective-permute-start | bytes 393224 | tf_op jit(solution)/shard_map/ppermute | solution.py:26
  140.3 39.6 %collective-permute-start.9 = (f32[4,16,512]{2,1,0:T(8,128)S(1)}, f32[4,16,512]{2,1,0:T(8,128)}, u32[]{:S(2)}, u32[]{:S(2)}) collective-permute-start(f32[4,16,512]{2,1,0:T(8,128)S(1)} %copy-done.45), channel_id=1, source_target_pairs={{0,4},{2,6},{1,5},{3,7},{8,12},{10,14},{9,13},{11,15},{16,20},{18,... | collective-permute-start | bytes 393224 | tf_op jit(solution)/shard_map/ppermute | solution.py:26
  174.3 27.0 %collective-permute-start.21 = (bf16[256,1408]{1,0:T(8,128)(2,1)}, bf16[256,1408]{1,0:T(8,128)(2,1)S(1)}, u32[]{:S(2)}, u32[]{:S(2)}) collective-permute-start(bf16[256,1408]{1,0:T(8,128)(2,1)} %concatenate.277), channel_id=1, source_target_pairs={{0,1},{9,8},{2,3},{11,10},{4,5},{13,12},{6,7},{15,14},{16,17},{25,... | collective-permute-start | bytes 2162696 | tf_op jit(solution)/shard_map/ppermute | solution.py:192
  181.5 27.7 %collective-permute-start.20 = (bf16[2,1,256,1024]{3,2,0,1:T(8,128)(2,1)}, bf16[2,1,256,1024]{3,2,0,1:T(8,128)(2,1)}, u32[]{:S(2)}, u32[]{:S(2)}) collective-permute-start(bf16[2,1,256,1024]{3,2,0,1:T(8,128)(2,1)} %pad_maximum_fusion.20), channel_id=1, source_target_pairs={{0,1},{1,0},{2,3},{3,2},{4,5},{5,4},{6,7},{7,6},{8,9},{9,8},{10,11... | collective-permute-start | bytes 3145736 | tf_op jit(solution)/shard_map/ppermute | solution.py:20
  218.5 223.5 %reduce-scatter.8.cloned.1.call-start = ((), (), s32[]{:S(2)}) async-start(), calls=%async_computation.11 | async-start | bytes 6488064 | tf_op jit(solution)/shard_map/reduce_scatter | solution.py:237
  304.7 237.6 %reduce-scatter.6.cloned.1.call-start = ((), (), s32[]{:S(2)}) async-start(), calls=%async_computation.10 | async-start | bytes 6488064 | tf_op jit(solution)/shard_map/reduce_scatter | solution.py:237
  352.7 248.2 %reduce-scatter.12.cloned.1.call-start = ((), (), s32[]{:S(2)}) async-start(), calls=%async_computation.13 | async-start | bytes 6488064 | tf_op jit(solution)/shard_map/reduce_scatter | solution.py:237
  413.9 197.3 %reduce-scatter.10.cloned.1.call-start = ((), (), s32[]{:S(2)}) async-start(), calls=%async_computation.12 | async-start | bytes 7077888 | tf_op jit(solution)/shard_map/reduce_scatter | solution.py:237
  440.5 101.8 %collective-permute-start.29 = (bf16[2,128,2048]{2,1,0:T(8,128)(2,1)}, bf16[2,128,2048]{2,1,0:T(8,128)(2,1)}, u32[]{:S(2)}, u32[]{:S(2)}) collective-permute-start(bf16[2,128,2048]{2,1,0:T(8,128)(2,1)} %get-tuple-element.705), channel_id=1, source_target_pairs={{0,1},{1,0},{16,17},{17,16},{2,3},{3,2},{18,19},{19,18},{4,5},{5,4... | collective-permute-start | bytes 3145736 | tf_op jit(solution)/shard_map/ppermute | solution.py:44
  441.0 101.3 %collective-permute-start.30 = (bf16[2,128,2048]{2,1,0:T(8,128)(2,1)}, bf16[2,128,2048]{2,1,0:T(8,128)(2,1)}, u32[]{:S(2)}, u32[]{:S(2)}) collective-permute-start(bf16[2,128,2048]{2,1,0:T(8,128)(2,1)} %get-tuple-element.706), channel_id=1, source_target_pairs={{0,16},{1,17},{16,0},{17,1},{2,18},{3,19},{18,2},{19,3},{4,20},{5,... | collective-permute-start | bytes 3145736 | tf_op jit(solution)/shard_map/ppermute | solution.py:44
  442.0 85.1 %collective-permute-start.34 = (bf16[2,128,2048]{2,1,0:T(8,128)(2,1)}, bf16[2,128,2048]{2,1,0:T(8,128)(2,1)}, u32[]{:S(2)}, u32[]{:S(2)}) collective-permute-start(bf16[2,128,2048]{2,1,0:T(8,128)(2,1)} %get-tuple-element.790), channel_id=1, source_target_pairs={{0,1},{1,0},{16,17},{17,16},{2,3},{3,2},{18,19},{19,18},{4,5},{5,4... | collective-permute-start | bytes 3145736 | tf_op jit(solution)/shard_map/ppermute | solution.py:44
  444.6 84.9 %collective-permute-start.35 = (bf16[2,128,2048]{2,1,0:T(8,128)(2,1)}, bf16[2,128,2048]{2,1,0:T(8,128)(2,1)}, u32[]{:S(2)}, u32[]{:S(2)}) collective-permute-start(bf16[2,128,2048]{2,1,0:T(8,128)(2,1)} %get-tuple-element.790), channel_id=1, source_target_pairs={{0,16},{1,17},{16,0},{17,1},{2,18},{3,19},{18,2},{19,3},{4,20},{5,... | collective-permute-start | bytes 3145736 | tf_op jit(solution)/shard_map/ppermute | solution.py:44
  444.8 51.4 %collective-permute-start.43 = (bf16[256,1408]{1,0:T(8,128)(2,1)}, bf16[256,1408]{1,0:T(8,128)(2,1)S(1)}, u32[]{:S(2)}, u32[]{:S(2)}) collective-permute-start(bf16[256,1408]{1,0:T(8,128)(2,1)} %reduce-scatter.8.cloned.1.call-done), channel_id=1, source_target_pairs={{8,1},{1,8},{10,3},{3,10},{12,5},{5,12},{14,7},{7,14},{24,17},{17,... | collective-permute-start | bytes 2162696 | tf_op jit(solution)/shard_map/ppermute | solution.py:262
  496.2 33.3 %collective-permute-start.36 = (bf16[2,128,2048]{2,1,0:T(8,128)(2,1)}, bf16[2,128,2048]{2,1,0:T(8,128)(2,1)}, u32[]{:S(2)}, u32[]{:S(2)}) collective-permute-start(bf16[2,128,2048]{2,1,0:T(8,128)(2,1)} %get-tuple-element.790), channel_id=1, source_target_pairs={{0,17},{1,16},{16,1},{17,0},{2,19},{3,18},{18,3},{19,2},{4,21},{5,... | collective-permute-start | bytes 3145736 | tf_op jit(solution)/shard_map/ppermute | solution.py:44
  513.2 152.7 %reduce-scatter.14.cloned.1.call-start = ((), (), s32[]{:S(2)}) async-start(), calls=%async_computation.14 | async-start | bytes 2359296 | tf_op jit(solution)/shard_map/reduce_scatter | solution.py:237
  527.1 25.3 %collective-permute-start.31 = (bf16[2,128,2048]{2,1,0:T(8,128)(2,1)}, bf16[2,128,2048]{2,1,0:T(8,128)(2,1)}, u32[]{:S(2)}, u32[]{:S(2)}) collective-permute-start(bf16[2,128,2048]{2,1,0:T(8,128)(2,1)} %get-tuple-element.707), channel_id=1, source_target_pairs={{0,17},{1,16},{16,1},{17,0},{2,19},{3,18},{18,3},{19,2},{4,21},{5,... | collective-permute-start | bytes 3145736 | tf_op jit(solution)/shard_map/ppermute | solution.py:44
  538.3 30.7 %collective-permute-start.46 = (bf16[1,256,1408]{2,1,0:T(8,128)(2,1)S(1)}, bf16[1,256,1408]{2,1,0:T(8,128)(2,1)}, u32[]{:S(2)}, u32[]{:S(2)}) collective-permute-start(bf16[1,256,1408]{2,1,0:T(8,128)(2,1)S(1)} %fusion.65), channel_id=1, source_target_pairs={{0,16},{16,0},{1,17},{17,1},{2,18},{18,2},{3,19},{19,3},{4,20},{20... | collective-permute-start | bytes 2162696 | tf_op jit(solution)/shard_map/ppermute | solution.py:20
  561.3 32.4 %collective-permute-start.44 = (bf16[2,136,2048]{2,1,0:T(8,128)(2,1)}, bf16[2,136,2048]{2,1,0:T(8,128)(2,1)}, u32[]{:S(2)}, u32[]{:S(2)}) collective-permute-start(bf16[2,136,2048]{2,1,0:T(8,128)(2,1)} %get-tuple-element.812), channel_id=1, source_target_pairs={{0,1},{1,0},{2,3},{3,2},{4,5},{5,4},{6,7},{7,6},{8,9},{9,8},{10,11... | collective-permute-start | bytes 3342344 | tf_op jit(solution)/shard_map/ppermute | solution.py:20
  561.4 32.3 %collective-permute-start.45 = (bf16[2,136,2048]{2,1,0:T(8,128)(2,1)}, bf16[2,136,2048]{2,1,0:T(8,128)(2,1)}, u32[]{:S(2)}, u32[]{:S(2)}) collective-permute-start(bf16[2,136,2048]{2,1,0:T(8,128)(2,1)} %bitcast.153), channel_id=1, source_target_pairs={{0,16},{16,0},{1,17},{17,1},{2,18},{18,2},{3,19},{19,3},{4,20},{20... | collective-permute-start | bytes 3342344 | tf_op jit(solution)/shard_map/ppermute | solution.py:20
  580.5 27.8 %collective-permute-start.51 = (bf16[1,256,1408]{2,1,0:T(8,128)(2,1)}, bf16[1,256,1408]{2,1,0:T(8,128)(2,1)}, u32[]{:S(2)}, u32[]{:S(2)}) collective-permute-start(bf16[1,256,1408]{2,1,0:T(8,128)(2,1)} %fusion.64), channel_id=1, source_target_pairs={{0,16},{16,0},{1,17},{17,1},{2,18},{18,2},{3,19},{19,3},{4,20},{20... | collective-permute-start | bytes 2162696 | tf_op jit(solution)/shard_map/ppermute | solution.py:20
  (113 other events, 1254.5 us)
Sparse Core Ops, SparseCore 0:
  10.2 28.8 all-gather.5
  41.5 63.0 all-gather.7
  106.8 67.1 all-gather.9
  176.0 62.2 all-gather.13
  239.8 59.0 all-gather.11
  304.9 64.9 reduce-scatter.7
  372.7 62.9 reduce-scatter.5
  438.0 69.1 reduce-scatter.11
  513.3 70.7 reduce-scatter.9
  626.9 31.4 reduce-scatter.13

commit v11 on v10

--- a/solution.py
+++ b/solution.py
@@ -706,6 +706,7 @@
         return values[: batch // 2], values[batch // 2 :]
 
     feed_move = Gather(*run(feed_grad, cotangent))
+    up_got = column_moves(run(lambda w: column_pieces(w, 1), up_weight))
     normed_all = normed_move.end(line)
     feed_move.turn(line)
 
@@ -753,10 +754,10 @@
 
     product, state_end = run(multiply, mixed, taps, decay)
     states = [passed(state_end, "z", k) for k in range(1, depth)]
-    w_gate = gather_tile(run(column_block, gate_got))
+    both_blocks = run(lambda a, b: jnp.stack([column_block(a), column_block(b)]), gate_got, up_got)
+    both = lax.all_gather(both_blocks, ("z", "c"), axis=1, tiled=True)
     out_move = Gather(*run(lambda w: (w[None, : w.shape[0] // 2], w[None, w.shape[0] // 2 :]), w_out))
     grad_feed_all = feed_move.end(line)
-    up_got = column_moves(run(lambda w: column_pieces(w, 1), up_weight))
     out_move.turn(line)
 
     def combine(parts, rates):
@@ -774,15 +775,13 @@
         return (
             start,
             result,
-            gated.reshape(-1, channels),
             [[slots[:, k, i].reshape(-1, channels) for i in range(spread)] for k in range(ycount)],
         )
 
-    start, convolved, gated_all, gated = run(
+    start, convolved, gated = run(
         convolve, states, mixed, taps, product, decay, residue
     )
     gated_got = swap_slots(gated)
-    w_up = gather_tile(run(column_block, up_got))
     out_own = out_move.end(line)
     w_out = [out_own] + moved(out_own, "c", -1)
 
@@ -805,29 +804,28 @@
     normed_two_all = two_move.end(line)
 
     def open_gate(v, w, back):
-        value = dot(v, w)
+        value = dot(v, w[0])
         return value, (back * value * jax.nn.sigmoid(value)).astype(low)
 
-    gate, grad_upper = run(open_gate, normed_two_all, w_gate, grad_active)
+    gate, grad_upper = run(open_gate, normed_two_all, both, grad_active)
     up_term = run(dot_w, normed_two_all, grad_upper)
     up_mine = scatter_tile(up_term)
 
     def activate(v, w, value, back):
-        upper = dot(v, w)
+        upper = dot(v, w[1])
         sigma = jax.nn.sigmoid(value)
         return (
             (value * sigma * upper).astype(low),
             (back * upper * sigma * (1.0 + value * (1.0 - sigma))).astype(low),
         )
 
-    active, grad_gate = run(activate, normed_two_all, w_up, gate, grad_active)
+    active, grad_gate = run(activate, normed_two_all, both, gate, grad_active)
     two_back = Scatter(
         run(
-            lambda a, b, wa, wb: split_sum((dot_t(a, wa) + dot_t(b, wb)).astype(low)),
+            lambda a, b, w: split_sum((dot_t(a, w[0]) + dot_t(b, w[1])).astype(low)),
             grad_gate,
             grad_upper,
-            w_gate,
-            w_up,
+            both,
         )
     )
     gate_mine = scatter_tile(run(dot_w, normed_two_all, grad_gate))
@@ -855,7 +853,7 @@
 
         slots = [[slot(k * spread + i) for i in range(spread)] for k in range(ycount)]
         rounded = result.astype(low)
-        return result, grad_gain, rounded.reshape(2, -1, width), slots
+        return result, grad_gain, rounded.reshape(-1, width), slots
 
     grad_middle, grad_feed_gain, grad_mix, grad_slots = run(
         middle_back, two_back.rest(), middle, scale_two, feed_gain, cotangent, w_out
@@ -922,19 +920,16 @@
     grad_mixed, in_term = run(in_back, grad_query, grad_pair, taps, normed_all)
     in_mine = scatter_tile(in_term)
     one_back = Scatter(run(lambda a, w: split_sum(dot_t(a, w, low)), grad_mixed, w_in))
-    grad_mix_all = run(
-        lambda got: jnp.concatenate([g[h] for h in range(2) for row in got for g in row]), mix_got
+    grad_mix_all, gated_all = run(
+        lambda got, own: (
+            jnp.concatenate([g for row in got for g in row]),
+            jnp.concatenate([g for row in own for g in row]),
+        ),
+        mix_got,
+        gated,
     )
     out_mine = scatter_tile(run(dot_w, gated_all, grad_mix_all))
     gate_got = owner_moves(run(owner_parts, gate_mine))
-    output = run(
-        lambda got, values: (
-            mask
-            * (values + add_up(got[0][:1], got[0][1:] + sum(got[1:], [])).reshape(batch, local, width))
-        ).astype(low),
-        feed_got,
-        middle,
-    )
     up_held = run(stacked, up_held, up_got)
     up_got = moved(up_held, "c", -1)
 
@@ -949,26 +944,34 @@
         return jnp.stack(sums)
 
     grad_taps = run(tap_sums, grad_query, grad_pair, mixed)
+    one_back.turn(line)
     gate_held = run(owner_held, gate_got)
     gate_got = moved(gate_held, "y", -1)
+
+    def column_whole(own, got):
+        return owner_whole(lax.axis_index("c"), [own] + got, depth)
+
+    grad_up_weight = run(column_whole, up_held, up_got)
+    output = run(
+        lambda got, values: (
+            mask
+            * (values + add_up(got[0][:1], got[0][1:] + sum(got[1:], [])).reshape(batch, local, width))
+        ).astype(low),
+        feed_got,
+        middle,
+    )
 
     def normed_sum(rest):
         value = Scatter.sum(*rest).reshape(batch, local + extra, width)
         return value[:, :local], value[:, local : local + 2].astype(low)
 
-    def column_whole(own, got):
-        return owner_whole(lax.axis_index("c"), [own] + got, depth)
-
-    grad_up_weight = run(column_whole, up_held, up_got)
-    one_back.turn(line)
+    grad_normed, grad_before = run(normed_sum, one_back.rest())
+    grad_after = lax.ppermute(grad_before, ("z", "x"), [(j, i) for i, j in last])
     down_held = run(lambda v: v[None], down_mine)
     down_got = moved(down_held, "y", -1)
     gate_held = run(stacked, gate_held, gate_got)
     gate_got = moved(gate_held, "c", -1)
     in_got = owner_moves(run(owner_parts, in_mine))
-    grad_normed, grad_before = run(normed_sum, one_back.rest())
-    grad_after = lax.ppermute(grad_before, ("z", "x"), [(j, i) for i, j in last])
-    grad_gate_weight = run(column_whole, gate_held, gate_got)
 
     def tokens_back(grad, extension, values, scale, gain, back, small):
         values = values.astype(wide)
@@ -990,6 +993,7 @@
         (grad_feed_gain, grad_residue, grad_decay, grad_taps),
     )
     small_got = moved(small, "c", 1)
+    grad_gate_weight = run(column_whole, gate_held, gate_got)
     in_held = run(owner_held, in_got)
     in_got = moved(in_held, "y", -1)
     down_held = run(lambda own, got: jnp.concatenate([own] + got), down_held, down_got)
@@ -1002,14 +1006,19 @@
         return whole.reshape(-1, width).astype(wide)
 
     grad_down = run(rows_whole, down_held, down_got)
+    small = run(lambda v, got: v + sum(got), small, small_got)
+    small_got = moved(small, "x", -1)
+    in_held = run(stacked, in_held, in_got)
+    in_got = moved(in_held, "c", -1)
     out_held = run(lambda v: v[None], out_mine)
     out_got = moved(out_held, "y", -1)
-    small = run(lambda v, got: v + sum(got), small, small_got)
-    small_got = moved(small, "x", -1)
     small = run(stacked, small, small_got)
     small_got = moved(small, "y", -1)
-    in_held = run(stacked, in_held, in_got)
-    in_got = moved(in_held, "c", -1)
+    grad_in_weight = run(
+        lambda own, got: owner_whole(lax.axis_index("c"), [own] + got, count), in_held, in_got
+    )
+    out_held = run(lambda own, got: jnp.concatenate([own] + got), out_held, out_got)
+    out_got = moved(out_held, "c", -1)
     poles = decay.shape[0]
 
     def small_whole(own, got):
@@ -1024,11 +1033,6 @@
 
     grad_norm_gain, feed_gain_sum, grad_conv_taps, residue_sum, decay_sum = run(
         small_whole, small, small_got
-    )
-    out_held = run(lambda own, got: jnp.concatenate([own] + got), out_held, out_got)
-    out_got = moved(out_held, "c", -1)
-    grad_in_weight = run(
-        lambda own, got: owner_whole(lax.axis_index("c"), [own] + got, count), in_held, in_got
     )
 
     def out_whole(core, own, got):

time: 722 us -> 796 us (1.10)
  waiting for transfers between devices: 225 us -> 306 us
    ppermute x12, waiting for transfers between devices: 29.9 us -> 95 us  [swap_slots(): line.append(lax.ppermute(slots[sy][sx], ('y', 'x'), pairs))]
    ppermute x3, waiting for transfers between devices: 18.5 us -> 2.09 us  [owner_moves(): got.append(lax.ppermute(parts[d], ('c', 'x'), pairs))]
    all_gather x0 -> x1, waiting for transfers between devices: none -> 14.5 us  [body(): both = lax.all_gather(both_blocks, ('z', 'c'), axis=1, tiled=True)]
    reduce_scatter x5, waiting for transfers between devices: 0.01 us -> 13.4 us  [scatter_tile(): return lax.psum_scatter(term, ('z', 'c'), scatter_dimension=0, tiled=True)]
    unnamed x164 -> x165, local copies, waits for them, and re-layouts: 29.5 us -> 21 us
  transfers between devices with their start and end apart: 77 -> 76, of which waited for: 37 -> 40; matrix products, arithmetic and copies ran while one was open for 42% -> 33% of each run, Pallas kernels for 8% -> 7%
where the time goes in v11:
time: 796 us; the launch traced here: 788 us
  waiting for transfers between devices  306 us (38%)
  matrix products  146 us (18%)
  other arithmetic  106 us (13%)
  starting transfers between devices  92.4 us (12%)
  local copies, waits for them, and re-layouts  63.6 us (8%)
  Pallas kernels  56.9 us (7%)
  between operations  16.3 us (2%)
    ppermute x41, waiting for transfers between devices, turned(): lax.ppermute(value, axis, [(i, (i + by) % length) for i in range(length)])  163 us
    ppermute x12, waiting for transfers between devices, swap_slots(): line.append(lax.ppermute(slots[sy][sx], ('y', 'x'), pairs))  95 us
    dot_general x6, matrix products, dot(): return jnp.dot(a, b, preferred_element_type=wide).astype(kind)  56.3 us
    dot_general x6, matrix products, dot_t(): lax.dot_general(a, b, (((1,), (1,)), ((), ())), preferred_element_type=wide)  50.7 us
    dot_general x5, matrix products, dot_w(): lax.dot_general(a, b, (((0,), (0,)), ((), ())), preferred_element_type=wide)  39.5 us
    ppermute x41, starting transfers between devices, turned(): lax.ppermute(value, axis, [(i, (i + by) % length) for i in range(length)])  39.1 us
    pallas_call x4, Pallas kernels, conv_call(): pl.pallas_call(kernel, out_shape=results, grid_spec=pltpu.PrefetchScalarG...  35.5 us
    unnamed x165, local copies, waits for them, and re-layouts  21 us
  transfers between devices with their start and end apart: 76, of which 40 were waited for; matrix products, arithmetic and copies ran while one was open for 33% of the time, Pallas kernels for 7%

profile of v11, /device:TPU:9, one launch (start us, length us, event | category | flops | bytes accessed | tf_op | source)
XLA Modules:
  0.0 787.7 jit_solution(1138943104180730097)
XLA Ops:
  43.9 10.9 %collective-permute-done.1 = bf16[1,136,2048]{2,1,0:T(8,128)(2,1)} collective-permute-done((bf16[1,136,2048]{2,1,0:T(8,128)(2,1)S(1)}, bf16[1,136,2048]{2,1,0:T(8,128)(2,1)}, u32[]{:S(2)}, u32[]{:S(2)}) %collective-permute-start.1) | collective-permute-done | bytes 557088 | tf_op jit(solution)/shard_map/ppermute | solution.py:20
  74.7 11.1 %collective-permute-done.4 = bf16[2,1,136,2048]{3,2,0,1:T(8,128)(2,1)S(1)} collective-permute-done((bf16[2,1,136,2048]{3,2,0,1:T(8,128)(2,1)}, bf16[2,1,136,2048]{3,2,0,1:T(8,128)(2,1)S(1)}, u32[]{:S(2)}, u32[]{:S(2)}) %collective-permute-start.4) | collective-permute-done | bytes 1114144 | tf_op jit(solution)/shard_map/ppermute | solution.py:20
  87.4 13.5 %collective-permute-done.5 = bf16[2,1,136,2048]{3,2,0,1:T(8,128)(2,1)} collective-permute-done((bf16[2,1,136,2048]{3,2,0,1:T(8,128)(2,1)}, bf16[2,1,136,2048]{3,2,0,1:T(8,128)(2,1)}, u32[]{:S(2)}, u32[]{:S(2)}) %collective-permute-start.5) | collective-permute-done | bytes 1114144 | tf_op jit(solution)/shard_map/ppermute | solution.py:20
  113.9 11.3 %convolution_convert_fusion.4 = bf16[1088,1536]{1,0:T(8,128)(2,1)S(1)} fusion(bf16[1088,2048]{1,0:T(8,128)(2,1)} %bitcast.375, bf16[2048,1536]{1,0:T(8,128)(2,1)} %all-gather.7.cloned.1.call-done), kind=kOutput, calls=%fused_computation.5 | convolution fusion | flops 6846775296 | bytes 14090240 | tf_op jit(solution)/shard_map/dot_general | solution.py:638
  148.6 15.7 %collective-permute-done.15 = bf16[2,1,128,2048]{3,2,0,1:T(8,128)(2,1)S(1)} collective-permute-done((bf16[2,1,128,2048]{3,2,0,1:T(8,128)(2,1)S(1)}, bf16[2,1,128,2048]{3,2,0,1:T(8,128)(2,1)S(1)}, u32[]{:S(2)}, u32[]{:S(2)}) %collective-permute-start.15) | collective-permute-done | bytes 1048608 | tf_op jit(solution)/shard_map/ppermute | solution.py:20
  169.6 6.3 collective-permute-done.13
  182.9 8.8 %shard_map.222 = bf16[4,2,1,128,512]{4,3,2,1,0:T(8,128)(2,1)} custom-call(s32[1]{0:T(128)} %bitcast.36.place_ref, bf16[4,2,1,128,512]{4,3,2,1,0:T(8,128)(2,1)} %fusion.63.signal_ref, f32[16,512]{1,0:T(8,128)} %maximum_bitcast_fusion.9.decay_ref, f32[16,512]{1,0:T(8,128)} %maximum_bitcast_fusion.10.residue_ref, f32[4,16,512]{2,1,0:T(8,128)} %multiply_add_fusion.2.start_ref), custom_call_target="tpu_custom_call" | custom-call | flops 33554432 | bytes 2293760 | tf_op jit(solution)/shard_map/pallas_call | solution.py:555
  214.4 6.4 collective-permute-done.18
  231.9 11.8 %fusion.130 = f32[1024,1408]{1,0:T(8,128)} fusion(bf16[1024,2048]{1,0:T(8,128)(2,1)} %bitcast.384, bf16[1408,2048]{1,0:T(8,128)(2,1)} %all-gather.9.cloned.1.call-done), kind=kOutput, calls=%fused_computation.419 | convolution fusion | flops 5905580032 | bytes 15728640 | tf_op jit(solution)/shard_map/dot_general | solution.py:642
  245.2 22.1 %collective-permute-done.25 = bf16[2,1,128,2048]{3,2,0,1:T(8,128)(2,1)S(1)} collective-permute-done((bf16[2,1,128,2048]{3,2,0,1:T(8,128)(2,1)S(1)}, bf16[2,1,128,2048]{3,2,0,1:T(8,128)(2,1)S(1)}, u32[]{:S(2)}, u32[]{:S(2)}) %collective-permute-start.25) | collective-permute-done | bytes 1048608 | tf_op jit(solution)/shard_map/ppermute | solution.py:20
  270.4 14.5 %all-gather.11.cloned.1.call-done = bf16[2,2048,1408]{2,1,0:T(8,128)(2,1)} async-done(((bf16[2,256,1408]{2,1,0:T(8,128)(2,1)}), bf16[2,2048,1408]{2,1,0:T(8,128)(2,1)}) %all-gather.11.cloned.1.call-update) | async-done | bytes 11534352 | tf_op jit(solution)/shard_map/all_gather | solution.py:758
  285.0 13.3 %multiply_convert_fusion.2 = (bf16[1024,1408]{1,0:T(8,128)(2,1)S(1)}, f32[1024,1408]{1,0:T(8,128)}) fusion(f32[1024,1408]{1,0:T(8,128)} %fusion.130, bf16[1024,2048]{1,0:T(8,128)(2,1)} %bitcast.386, bf16[2,2048,1408]{2,1,0:T(8,128)(2,1)} %all-gather.11.cloned.1.call-done), kind=kOutput, calls=%fused_computation.21 | convolution fusion | flops 5914230784 | bytes 24379392 | tf_op jit(solution)/shard_map/dot_general | solution.py:638
  299.8 8.5 %convolution_convert_fusion.3 = bf16[2048,1408]{1,0:T(8,128)(2,1)} fusion(bf16[1024,2048]{1,0:T(8,128)(2,1)S(1)} %bitcast.388, bf16[1024,1408]{1,0:T(8,128)(2,1)S(1)} %get-tuple-element.680), kind=kOutput, calls=%fused_computation.4 | convolution fusion | flops 5908463616 | bytes 12845056 | tf_op jit(solution)/shard_map/dot_general | solution.py:646
  308.5 15.7 %multiply_convert_fusion = (bf16[1024,1408]{1,0:T(8,128)(2,1)}, bf16[1024,1408]{1,0:T(8,128)(2,1)}) fusion(f32[1024,1408]{1,0:T(8,128)} %get-tuple-element.670, f32[1024,1408]{1,0:T(8,128)} %fusion.130, bf16[1024,2048]{1,0:T(8,128)(2,1)} %bitcast.387, bf16[2,2048,1408]{2,1,0:T(8,128)(2,1)} %all-gather.11.cloned.1.call-done), kind=kOutput, calls=%fused_computation.17 | convolution fusion | flops 5924323328 | bytes 27262976 | tf_op jit(solution)/shard_map/dot_general | solution.py:638
  324.2 10.9 %fusion = f32[1024,2048]{1,0:T(8,128)} fusion(bf16[1024,1408]{1,0:T(8,128)(2,1)S(1)} %copy-done.65, bf16[2,2048,1408]{2,1,0:T(8,128)(2,1)} %all-gather.11.cloned.1.call-done), kind=kOutput, calls=%fused_computation.7 | convolution fusion | flops 5905580032 | bytes 17039360 | tf_op jit(solution)/shard_map/dot_general | solution.py:642
  335.1 10.1 %add_convert_fusion = bf16[1024,2048]{1,0:T(8,128)(2,1)S(1)} fusion(f32[1024,2048]{1,0:T(8,128)} %fusion, bf16[1024,1408]{1,0:T(8,128)(2,1)} %get-tuple-element.688, bf16[2,2048,1408]{2,1,0:T(8,128)(2,1)S(1)} %bitcast.513), kind=kOutput, calls=%fused_computation | convolution fusion | flops 5909774336 | bytes 21233664 | tf_op jit(solution)/shard_map/dot_general | solution.py:642
  350.2 8.7 %convolution_convert_fusion.2 = bf16[2048,1408]{1,0:T(8,128)(2,1)} fusion(bf16[1024,2048]{1,0:T(8,128)(2,1)S(1)} %bitcast.389, bf16[1024,1408]{1,0:T(8,128)(2,1)S(1)} %copy-done.66), kind=kOutput, calls=%fused_computation.3 | convolution fusion | flops 5908463616 | bytes 12845056 | tf_op jit(solution)/shard_map/dot_general | solution.py:646
  361.6 22.1 %collective-permute-done.27 = bf16[2,128,2048]{2,1,0:T(8,128)(2,1)} collective-permute-done((bf16[2,128,2048]{2,1,0:T(8,128)(2,1)}, bf16[2,128,2048]{2,1,0:T(8,128)(2,1)}, u32[]{:S(2)}, u32[]{:S(2)}) %collective-permute-start.27) | collective-permute-done | bytes 1048608 | tf_op jit(solution)/shard_map/ppermute | solution.py:20
  390.3 9.1 %convolution_convert_fusion.6 = bf16[1024,2048]{1,0:T(8,128)(2,1)S(1)} fusion(bf16[1024,1408]{1,0:T(8,128)(2,1)S(1)} %copy-done.63, bf16[1408,2048]{1,0:T(8,128)(2,1)} %all-gather.9.cloned.1.call-done), kind=kOutput, calls=%fused_computation.38 | convolution fusion | flops 5907677184 | bytes 12845056 | tf_op jit(solution)/shard_map/dot_general | solution.py:638
  415.2 8.1 %convolution_convert_fusion.1 = bf16[1408,2048]{1,0:T(8,128)(2,1)} fusion(bf16[1024,1408]{1,0:T(8,128)(2,1)S(1)} %copy-done.63, bf16[1024,2048]{1,0:T(8,128)(2,1)S(1)} %bitcast.385), kind=kOutput, calls=%fused_computation.2 | convolution fusion | flops 5908463616 | bytes 12845056 | tf_op jit(solution)/shard_map/dot_general | solution.py:646
  462.1 9.3 %collective-permute-start.37 = (bf16[256,1408]{1,0:T(8,128)(2,1)}, bf16[256,1408]{1,0:T(8,128)(2,1)S(1)}, u32[]{:S(2)}, u32[]{:S(2)}) collective-permute-start(bf16[256,1408]{1,0:T(8,128)(2,1)} %reduce-scatter.6.cloned.1.call-done), channel_id=1, source_target_pairs={{8,1},{1,8},{10,3},{3,10},{12,5},{5,12},{14,7},{7,14},{24,17},{17,... | collective-permute-start | bytes 2162696 | tf_op jit(solution)/shard_map/ppermute | solution.py:262
  472.2 17.0 %shard_map.224 = (bf16[4,2,1,128,512]{4,3,2,1,0:T(8,128)(2,1)}, f32[16,512]{1,0:T(8,128)}, f32[16,512]{1,0:T(8,128)}) custom-call(s32[1]{0:T(128)} %bitcast.36.place_ref, bf16[4,2,1,128,512]{4,3,2,1,0:T(8,128)(2,1)} %fusion.63.signal_ref, bf16[4,2,1,128,512]{4,3,2,1,0:T(8,128)(2,1)} %get-tuple-element.752.signal_ref.grad_ref, ...), custom_call_target="tpu_custom_call" | custom-call | flops 100663296 | bytes 4521984 | tf_op jit(solution)/shard_map/pallas_call | solution.py:555
  505.7 10.5 %convolution_convert_fusion = bf16[2048,1536]{1,0:T(8,128)(2,1)} fusion(bf16[1088,2048]{1,0:T(8,128)(2,1)S(1)} %bitcast.378, bf16[1088,1024]{1,0:T(8,128)(2,1)S(1)} %bitcast.365, bf16[1088,512]{1,0:T(8,128)(2,1)S(1)} %bitcast.374), kind=kOutput, calls=%fused_computation.1 | convolution fusion | flops 6854934528 | bytes 14090240 | tf_op jit(solution)/shard_map/dot_general | solution.py:646
  520.1 10.5 %convolution_convert_fusion.5 = bf16[1088,2048]{1,0:T(8,128)(2,1)S(1)} fusion(bf16[1088,1536]{1,0:T(8,128)(2,1)} %pad_maximum_fusion.7, bf16[2048,1536]{1,0:T(8,128)(2,1)} %all-gather.7.cloned.1.call-done), kind=kOutput, calls=%fused_computation.6 | convolution fusion | flops 6847332352 | bytes 14090240 | tf_op jit(solution)/shard_map/dot_general | solution.py:642
  533.9 30.9 %collective-permute-done.42 = bf16[256,2048]{1,0:T(8,128)(2,1)S(1)} collective-permute-done((bf16[256,2048]{1,0:T(8,128)(2,1)}, bf16[256,2048]{1,0:T(8,128)(2,1)S(1)}, u32[]{:S(2)}, u32[]{:S(2)}) %collective-permute-start.42) | collective-permute-done | bytes 1048608 | tf_op jit(solution)/shard_map/ppermute | solution.py:44
  564.8 44.0 %collective-permute-done.43 = bf16[256,2048]{1,0:T(8,128)(2,1)S(1)} collective-permute-done((bf16[256,2048]{1,0:T(8,128)(2,1)}, bf16[256,2048]{1,0:T(8,128)(2,1)S(1)}, u32[]{:S(2)}, u32[]{:S(2)}) %collective-permute-start.43) | collective-permute-done | bytes 1048608 | tf_op jit(solution)/shard_map/ppermute | solution.py:44
  615.8 9.6 %collective-permute-done.41 = bf16[1,256,1408]{2,1,0:T(8,128)(2,1)} collective-permute-done((bf16[1,256,1408]{2,1,0:T(8,128)(2,1)S(1)}, bf16[1,256,1408]{2,1,0:T(8,128)(2,1)}, u32[]{:S(2)}, u32[]{:S(2)}) %collective-permute-start.41) | collective-permute-done | bytes 720928 | tf_op jit(solution)/shard_map/ppermute | solution.py:20
  672.9 13.7 %collective-permute-done.52 = bf16[1,256,1408]{2,1,0:T(8,128)(2,1)} collective-permute-done((bf16[1,256,1408]{2,1,0:T(8,128)(2,1)}, bf16[1,256,1408]{2,1,0:T(8,128)(2,1)}, u32[]{:S(2)}, u32[]{:S(2)}) %collective-permute-start.52) | collective-permute-done | bytes 720928 | tf_op jit(solution)/shard_map/ppermute | solution.py:20
  686.6 8.1 %collective-permute-start.51 = (bf16[2,2,2048]{2,1,0:T(2,128)(2,1)S(1)}, bf16[2,2,2048]{2,1,0:T(2,128)(2,1)S(1)}, u32[]{:S(2)}, u32[]{:S(2)}) collective-permute-start(bf16[2,2,2048]{2,1,0:T(2,128)(2,1)S(1)} %fusion.96), channel_id=1, source_target_pairs={{2,1},{4,3},{6,5},{10,9},{12,11},{14,13},{18,17},{20,19},{22,21},{... | collective-permute-start | bytes 49160 | tf_op jit(solution)/shard_map/ppermute | solution.py:969
  708.0 5.9 shard_map.226
  745.7 13.3 %reduce-scatter.14.cloned.1.call-done = bf16[64,2048]{1,0:T(8,128)(2,1)} async-done(((bf16[512,2048]{1,0:T(8,128)(2,1)}), bf16[64,2048]{1,0:T(8,128)(2,1)}) %reduce-scatter.14.cloned.1.call-update) | async-done | bytes 262160 | tf_op jit(solution)/shard_map/reduce_scatter | solution.py:237
  764.7 6.0 shard_map.227
  (515 shorter events, 353.7 us)
Async XLA Ops:
  7.2 31.8 %all-gather.5.cloned.1.call-start = ((), (), s32[]{:S(2)}) async-start(), calls=%async_computation.5 | async-start | bytes 1310720 | tf_op jit(solution)/shard_map/all_gather | solution.py:679
  9.3 104.7 %all-gather.7.cloned.1.call-start = ((), (), s32[]{:S(2)}) async-start(), calls=%async_computation.6 | async-start | bytes 7077888 | tf_op jit(solution)/shard_map/all_gather | solution.py:233
  41.3 188.8 %all-gather.9.cloned.1.call-start = ((), (), s32[]{:S(2)}) async-start(), calls=%async_computation.7 | async-start | bytes 6488064 | tf_op jit(solution)/shard_map/all_gather | solution.py:233
  61.4 223.5 %all-gather.11.cloned.1.call-start = ((), (), s32[]{:S(2)}) async-start(), calls=%async_computation.8 | async-start | bytes 12976128 | tf_op jit(solution)/shard_map/all_gather | solution.py:758
  62.1 72.9 %collective-permute-start.11 = (bf16[256,1408]{1,0:T(8,128)(2,1)}, bf16[256,1408]{1,0:T(8,128)(2,1)}, u32[]{:S(2)}, u32[]{:S(2)}) collective-permute-start(bf16[256,1408]{1,0:T(8,128)(2,1)} %concatenate.271), channel_id=1, source_target_pairs={{0,1},{9,8},{2,3},{11,10},{4,5},{13,12},{6,7},{15,14},{16,17},{25,... | collective-permute-start | bytes 2162696 | tf_op jit(solution)/shard_map/ppermute | solution.py:192
  64.7 36.2 %collective-permute-start.5 = (bf16[2,1,136,2048]{3,2,0,1:T(8,128)(2,1)}, bf16[2,1,136,2048]{3,2,0,1:T(8,128)(2,1)}, u32[]{:S(2)}, u32[]{:S(2)}) collective-permute-start(bf16[2,1,136,2048]{3,2,0,1:T(8,128)(2,1)} %pad_maximum_fusion.18), channel_id=1, source_target_pairs={{0,1},{1,0},{2,3},{3,2},{4,5},{5,4},{6,7},{7,6},{8,9},{9,8},{10,11... | collective-permute-start | bytes 3342344 | tf_op jit(solution)/shard_map/ppermute | solution.py:20
  74.2 35.3 %collective-permute-start.6 = (bf16[1,128,2048]{2,1,0:T(8,128)(2,1)S(1)}, bf16[1,128,2048]{2,1,0:T(8,128)(2,1)S(1)}, u32[]{:S(2)}, u32[]{:S(2)}) collective-permute-start(bf16[1,128,2048]{2,1,0:T(8,128)(2,1)S(1)} %get-tuple-element.545), channel_id=1, source_target_pairs={{0,1},{1,0},{2,3},{3,2},{4,5},{5,4},{6,7},{7,6},{8,9},{9,8},{10,11... | collective-permute-start | bytes 1572872 | tf_op jit(solution)/shard_map/ppermute | solution.py:20
  74.2 35.3 %collective-permute-start.7 = (bf16[1,128,2048]{2,1,0:T(8,128)(2,1)S(1)}, bf16[1,128,2048]{2,1,0:T(8,128)(2,1)S(1)}, u32[]{:S(2)}, u32[]{:S(2)}) collective-permute-start(bf16[1,128,2048]{2,1,0:T(8,128)(2,1)S(1)} %get-tuple-element.547), channel_id=1, source_target_pairs={{0,16},{16,0},{1,17},{17,1},{2,18},{18,2},{3,19},{19,3},{4,20},{20... | collective-permute-start | bytes 1572872 | tf_op jit(solution)/shard_map/ppermute | solution.py:20
  85.9 49.1 %collective-permute-start.12 = (bf16[256,1408]{1,0:T(8,128)(2,1)}, bf16[256,1408]{1,0:T(8,128)(2,1)}, u32[]{:S(2)}, u32[]{:S(2)}) collective-permute-start(bf16[256,1408]{1,0:T(8,128)(2,1)} %concatenate.273), channel_id=1, source_target_pairs={{0,1},{9,8},{2,3},{11,10},{4,5},{13,12},{6,7},{15,14},{16,17},{25,... | collective-permute-start | bytes 2162696 | tf_op jit(solution)/shard_map/ppermute | solution.py:192
  139.2 314.0 %reduce-scatter.6.cloned.1.call-start = ((), (), s32[]{:S(2)}) async-start(), calls=%async_computation.9 | async-start | bytes 6488064 | tf_op jit(solution)/shard_map/reduce_scatter | solution.py:237
  139.4 24.9 %collective-permute-start.15 = (bf16[2,1,128,2048]{3,2,0,1:T(8,128)(2,1)S(1)}, bf16[2,1,128,2048]{3,2,0,1:T(8,128)(2,1)S(1)}, u32[]{:S(2)}, u32[]{:S(2)}) collective-permute-start(bf16[2,1,128,2048]{3,2,0,1:T(8,128)(2,1)S(1)} %bitcast.396), channel_id=1, source_target_pairs={{0,16},{16,0},{1,17},{17,1},{2,18},{18,2},{3,19},{19,3},{4,20},{20... | collective-permute-start | bytes 3145736 | tf_op jit(solution)/shard_map/ppermute | solution.py:20
  140.6 23.7 %collective-permute-start.16 = (bf16[2,1,128,2048]{3,2,0,1:T(8,128)(2,1)S(1)}, bf16[2,1,128,2048]{3,2,0,1:T(8,128)(2,1)S(1)}, u32[]{:S(2)}, u32[]{:S(2)}) collective-permute-start(bf16[2,1,128,2048]{3,2,0,1:T(8,128)(2,1)S(1)} %copy-done.19), channel_id=1, source_target_pairs={{0,1},{1,0},{2,3},{3,2},{4,5},{5,4},{6,7},{7,6},{8,9},{9,8},{10,11... | collective-permute-start | bytes 3145736 | tf_op jit(solution)/shard_map/ppermute | solution.py:20
  140.6 35.5 %collective-permute-start.10 = (f32[4,16,512]{2,1,0:T(8,128)S(1)}, f32[4,16,512]{2,1,0:T(8,128)S(1)}, u32[]{:S(2)}, u32[]{:S(2)}) collective-permute-start(f32[4,16,512]{2,1,0:T(8,128)S(1)} %copy-done.47), channel_id=1, source_target_pairs={{0,6},{1,7},{8,14},{9,15},{16,22},{17,23},{24,30},{25,31}} | collective-permute-start | bytes 393224 | tf_op jit(solution)/shard_map/ppermute | solution.py:26
  141.3 34.9 %collective-permute-start.8 = (f32[4,16,512]{2,1,0:T(8,128)S(1)}, f32[4,16,512]{2,1,0:T(8,128)S(1)}, u32[]{:S(2)}, u32[]{:S(2)}) collective-permute-start(f32[4,16,512]{2,1,0:T(8,128)S(1)} %copy-done.47), channel_id=1, source_target_pairs={{0,2},{2,4},{4,6},{1,3},{3,5},{5,7},{8,10},{10,12},{12,14},{9,11},... | collective-permute-start | bytes 393224 | tf_op jit(solution)/shard_map/ppermute | solution.py:26
  144.5 31.6 %collective-permute-start.9 = (f32[4,16,512]{2,1,0:T(8,128)S(1)}, f32[4,16,512]{2,1,0:T(8,128)S(1)}, u32[]{:S(2)}, u32[]{:S(2)}) collective-permute-start(f32[4,16,512]{2,1,0:T(8,128)S(1)} %copy-done.47), channel_id=1, source_target_pairs={{0,4},{2,6},{1,5},{3,7},{8,12},{10,14},{9,13},{11,15},{16,20},{18,... | collective-permute-start | bytes 393224 | tf_op jit(solution)/shard_map/ppermute | solution.py:26
  243.8 23.5 %collective-permute-start.25 = (bf16[2,1,128,2048]{3,2,0,1:T(8,128)(2,1)S(1)}, bf16[2,1,128,2048]{3,2,0,1:T(8,128)(2,1)S(1)}, u32[]{:S(2)}, u32[]{:S(2)}) collective-permute-start(bf16[2,1,128,2048]{3,2,0,1:T(8,128)(2,1)S(1)} %pad_maximum_fusion.23), channel_id=1, source_target_pairs={{0,16},{16,0},{1,17},{17,1},{2,18},{18,2},{3,19},{19,3},{4,20},{20... | collective-permute-start | bytes 3145736 | tf_op jit(solution)/shard_map/ppermute | solution.py:20
  244.6 22.7 %collective-permute-start.26 = (bf16[2,1,128,2048]{3,2,0,1:T(8,128)(2,1)S(1)}, bf16[2,1,128,2048]{3,2,0,1:T(8,128)(2,1)S(1)}, u32[]{:S(2)}, u32[]{:S(2)}) collective-permute-start(bf16[2,1,128,2048]{3,2,0,1:T(8,128)(2,1)S(1)} %bitcast.400), channel_id=1, source_target_pairs={{0,1},{1,0},{2,3},{3,2},{4,5},{5,4},{6,7},{7,6},{8,9},{9,8},{10,11... | collective-permute-start | bytes 3145736 | tf_op jit(solution)/shard_map/ppermute | solution.py:20
  308.4 306.0 %reduce-scatter.8.cloned.1.call-start = ((), (), s32[]{:S(2)}) async-start(), calls=%async_computation.10 | async-start | bytes 6488064 | tf_op jit(solution)/shard_map/reduce_scatter | solution.py:237
  358.8 314.1 %reduce-scatter.12.cloned.1.call-start = ((), (), s32[]{:S(2)}) async-start(), calls=%async_computation.12 | async-start | bytes 6488064 | tf_op jit(solution)/shard_map/reduce_scatter | solution.py:237
  358.9 24.8 %collective-permute-start.27 = (bf16[2,128,2048]{2,1,0:T(8,128)(2,1)}, bf16[2,128,2048]{2,1,0:T(8,128)(2,1)}, u32[]{:S(2)}, u32[]{:S(2)}) collective-permute-start(bf16[2,128,2048]{2,1,0:T(8,128)(2,1)} %get-tuple-element.683), channel_id=1, source_target_pairs={{0,1},{1,0},{2,3},{3,2},{4,5},{5,4},{6,7},{7,6},{8,9},{9,8},{10,11... | collective-permute-start | bytes 3145736 | tf_op jit(solution)/shard_map/ppermute | solution.py:20
  360.4 24.4 %collective-permute-start.28 = (bf16[2,128,2048]{2,1,0:T(8,128)(2,1)}, bf16[2,128,2048]{2,1,0:T(8,128)(2,1)}, u32[]{:S(2)}, u32[]{:S(2)}) collective-permute-start(bf16[2,128,2048]{2,1,0:T(8,128)(2,1)} %bitcast.431), channel_id=1, source_target_pairs={{0,16},{16,0},{1,17},{17,1},{2,18},{18,2},{3,19},{19,3},{4,20},{20... | collective-permute-start | bytes 3145736 | tf_op jit(solution)/shard_map/ppermute | solution.py:20
  423.3 275.5 %reduce-scatter.10.cloned.1.call-start = ((), (), s32[]{:S(2)}) async-start(), calls=%async_computation.11 | async-start | bytes 7077888 | tf_op jit(solution)/shard_map/reduce_scatter | solution.py:237
  462.1 34.2 %collective-permute-start.37 = (bf16[256,1408]{1,0:T(8,128)(2,1)}, bf16[256,1408]{1,0:T(8,128)(2,1)S(1)}, u32[]{:S(2)}, u32[]{:S(2)}) collective-permute-start(bf16[256,1408]{1,0:T(8,128)(2,1)} %reduce-scatter.6.cloned.1.call-done), channel_id=1, source_target_pairs={{8,1},{1,8},{10,3},{3,10},{12,5},{5,12},{14,7},{7,14},{24,17},{17,... | collective-permute-start | bytes 2162696 | tf_op jit(solution)/shard_map/ppermute | solution.py:262
  516.2 242.9 %reduce-scatter.14.cloned.1.call-start = ((), (), s32[]{:S(2)}) async-start(), calls=%async_computation.13 | async-start | bytes 2359296 | tf_op jit(solution)/shard_map/reduce_scatter | solution.py:237
  516.8 148.2 %collective-permute-start.29 = (bf16[2,128,2048]{2,1,0:T(8,128)(2,1)}, bf16[2,128,2048]{2,1,0:T(8,128)(2,1)}, u32[]{:S(2)}, u32[]{:S(2)}) collective-permute-start(bf16[2,128,2048]{2,1,0:T(8,128)(2,1)} %get-tuple-element.701), channel_id=1, source_target_pairs={{0,1},{1,0},{16,17},{17,16},{2,3},{3,2},{18,19},{19,18},{4,5},{5,4... | collective-permute-start | bytes 3145736 | tf_op jit(solution)/shard_map/ppermute | solution.py:44
  516.9 149.7 %collective-permute-start.30 = (bf16[2,128,2048]{2,1,0:T(8,128)(2,1)}, bf16[2,128,2048]{2,1,0:T(8,128)(2,1)}, u32[]{:S(2)}, u32[]{:S(2)}) collective-permute-start(bf16[2,128,2048]{2,1,0:T(8,128)(2,1)} %get-tuple-element.702), channel_id=1, source_target_pairs={{0,16},{1,17},{16,0},{17,1},{2,18},{3,19},{18,2},{19,3},{4,20},{5,... | collective-permute-start | bytes 3145736 | tf_op jit(solution)/shard_map/ppermute | solution.py:44
  517.5 47.4 %collective-permute-start.42 = (bf16[256,2048]{1,0:T(8,128)(2,1)}, bf16[256,2048]{1,0:T(8,128)(2,1)S(1)}, u32[]{:S(2)}, u32[]{:S(2)}) collective-permute-start(bf16[256,2048]{1,0:T(8,128)(2,1)} %bitcast.405), channel_id=1, source_target_pairs={{0,1},{1,0},{16,17},{17,16},{2,3},{3,2},{18,19},{19,18},{4,5},{5,4... | collective-permute-start | bytes 3145736 | tf_op jit(solution)/shard_map/ppermute | solution.py:44
  518.9 89.9 %collective-permute-start.43 = (bf16[256,2048]{1,0:T(8,128)(2,1)}, bf16[256,2048]{1,0:T(8,128)(2,1)S(1)}, u32[]{:S(2)}, u32[]{:S(2)}) collective-permute-start(bf16[256,2048]{1,0:T(8,128)(2,1)} %bitcast.406), channel_id=1, source_target_pairs={{0,16},{1,17},{16,0},{17,1},{2,18},{3,19},{18,2},{19,3},{4,20},{5,... | collective-permute-start | bytes 3145736 | tf_op jit(solution)/shard_map/ppermute | solution.py:44
  519.8 89.1 %collective-permute-start.44 = (bf16[256,2048]{1,0:T(8,128)(2,1)}, bf16[256,2048]{1,0:T(8,128)(2,1)S(1)}, u32[]{:S(2)}, u32[]{:S(2)}) collective-permute-start(bf16[256,2048]{1,0:T(8,128)(2,1)} %bitcast.407), channel_id=1, source_target_pairs={{0,17},{1,16},{16,1},{17,0},{2,19},{3,18},{18,3},{19,2},{4,21},{5,... | collective-permute-start | bytes 3145736 | tf_op jit(solution)/shard_map/ppermute | solution.py:44
  564.8 101.7 %collective-permute-start.31 = (bf16[2,128,2048]{2,1,0:T(8,128)(2,1)}, bf16[2,128,2048]{2,1,0:T(8,128)(2,1)}, u32[]{:S(2)}, u32[]{:S(2)}) collective-permute-start(bf16[2,128,2048]{2,1,0:T(8,128)(2,1)} %get-tuple-element.703), channel_id=1, source_target_pairs={{0,17},{1,16},{16,1},{17,0},{2,19},{3,18},{18,3},{19,2},{4,21},{5,... | collective-permute-start | bytes 3145736 | tf_op jit(solution)/shard_map/ppermute | solution.py:44
  614.4 25.5 %collective-permute-start.47 = (bf16[2,136,2048]{2,1,0:T(8,128)(2,1)}, bf16[2,136,2048]{2,1,0:T(8,128)(2,1)}, u32[]{:S(2)}, u32[]{:S(2)}) collective-permute-start(bf16[2,136,2048]{2,1,0:T(8,128)(2,1)} %get-tuple-element.812), channel_id=1, source_target_pairs={{0,1},{1,0},{2,3},{3,2},{4,5},{5,4},{6,7},{7,6},{8,9},{9,8},{10,11... | collective-permute-start | bytes 3342344 | tf_op jit(solution)/shard_map/ppermute | solution.py:20
  625.4 24.3 %collective-permute-start.48 = (bf16[2,136,2048]{2,1,0:T(8,128)(2,1)}, bf16[2,136,2048]{2,1,0:T(8,128)(2,1)}, u32[]{:S(2)}, u32[]{:S(2)}) collective-permute-start(bf16[2,136,2048]{2,1,0:T(8,128)(2,1)} %bitcast.428), channel_id=1, source_target_pairs={{0,16},{16,0},{1,17},{17,1},{2,18},{18,2},{3,19},{19,3},{4,20},{20... | collective-permute-start | bytes 3342344 | tf_op jit(solution)/shard_map/ppermute | solution.py:20
  (116 other events, 1611.2 us)
Sparse Core Ops, SparseCore 0:
  10.2 28.8 all-gather.4
  41.5 63.0 all-gather.6
  106.8 67.1 all-gather.8
  176.0 108.9 all-gather.10
  308.5 64.4 reduce-scatter.5
  375.7 63.1 reduce-scatter.7
  441.2 74.4 reduce-scatter.11
  518.6 69.0 reduce-scatter.9
  718.8 40.1 reduce-scatter.13

commit v12 on v10

--- a/solution.py
+++ b/solution.py
@@ -706,6 +706,7 @@
         return values[: batch // 2], values[batch // 2 :]
 
     feed_move = Gather(*run(feed_grad, cotangent))
+    up_got = column_moves(run(lambda w: column_pieces(w, 1), up_weight))
     normed_all = normed_move.end(line)
     feed_move.turn(line)
 
@@ -756,7 +757,6 @@
     w_gate = gather_tile(run(column_block, gate_got))
     out_move = Gather(*run(lambda w: (w[None, : w.shape[0] // 2], w[None, w.shape[0] // 2 :]), w_out))
     grad_feed_all = feed_move.end(line)
-    up_got = column_moves(run(lambda w: column_pieces(w, 1), up_weight))
     out_move.turn(line)
 
     def combine(parts, rates):
@@ -855,14 +855,14 @@
 
         slots = [[slot(k * spread + i) for i in range(spread)] for k in range(ycount)]
         rounded = result.astype(low)
-        return result, grad_gain, rounded.reshape(2, -1, width), slots
-
-    grad_middle, grad_feed_gain, grad_mix, grad_slots = run(
+        return result, grad_gain, rounded[: batch // 2], rounded[batch // 2 :], slots
+
+    grad_middle, grad_feed_gain, first, second, grad_slots = run(
         middle_back, two_back.rest(), middle, scale_two, feed_gain, cotangent, w_out
     )
     grad_got = swap_slots(grad_slots)
     down_mine = scatter_tile(run(dot_w, active, grad_feed_all))
-    mix_got = swap_slots([[grad_mix] * spread] * ycount)
+    mix_move = Gather(first, second)
 
     def conv_grads(got, result, value, weights, rates):
         grad = jnp.stack([jnp.stack(row) for row in got])
@@ -874,6 +874,7 @@
 
     grad_query, grad_conv, later_end = run(conv_grads, grad_got, convolved, mixed, taps, decay)
     laters = [passed(later_end, "z", -k) for k in range(1, depth)]
+    mix_move.turn(line)
 
     def short_back(grad, weights):
         head = jnp.roll(grad[:, :, :, :2], -1, axis=1)
@@ -891,6 +892,7 @@
 
     feed_got = swap_slots(feed_parts)
     up_parts_got = owner_moves(run(owner_parts, up_mine))
+    gate_got = owner_moves(run(owner_parts, gate_mine))
 
     def conv_back(signal, grad, rates, amounts, begin, ends_later, value, weights):
         later = combine(ends_later, rates)
@@ -906,6 +908,7 @@
         conv_back, product, grad_conv, decay, residue, start, laters, mixed, taps
     )
 
+    mix_move.got = run(lambda got: got, mix_move.got)
     up_held = run(owner_held, up_parts_got)
     up_got = moved(up_held, "y", -1)
 
@@ -921,22 +924,15 @@
 
     grad_mixed, in_term = run(in_back, grad_query, grad_pair, taps, normed_all)
     in_mine = scatter_tile(in_term)
+    gate_held = run(owner_held, gate_got)
+    gate_got = moved(gate_held, "y", -1)
     one_back = Scatter(run(lambda a, w: split_sum(dot_t(a, w, low)), grad_mixed, w_in))
-    grad_mix_all = run(
-        lambda got: jnp.concatenate([g[h] for h in range(2) for row in got for g in row]), mix_got
-    )
+    grad_mix_all = mix_move.end(line)
     out_mine = scatter_tile(run(dot_w, gated_all, grad_mix_all))
-    gate_got = owner_moves(run(owner_parts, gate_mine))
-    output = run(
-        lambda got, values: (
-            mask
-            * (values + add_up(got[0][:1], got[0][1:] + sum(got[1:], [])).reshape(batch, local, width))
-        ).astype(low),
-        feed_got,
-        middle,
-    )
     up_held = run(stacked, up_held, up_got)
     up_got = moved(up_held, "c", -1)
+    gate_held = run(stacked, gate_held, gate_got)
+    gate_got = moved(gate_held, "c", -1)
 
     def tap_sums(query, pair, value):
         sums = []
@@ -949,12 +945,6 @@
         return jnp.stack(sums)
 
     grad_taps = run(tap_sums, grad_query, grad_pair, mixed)
-    gate_held = run(owner_held, gate_got)
-    gate_got = moved(gate_held, "y", -1)
-
-    def normed_sum(rest):
-        value = Scatter.sum(*rest).reshape(batch, local + extra, width)
-        return value[:, :local], value[:, local : local + 2].astype(low)
 
     def column_whole(own, got):
         return owner_whole(lax.axis_index("c"), [own] + got, depth)
@@ -963,12 +953,14 @@
     one_back.turn(line)
     down_held = run(lambda v: v[None], down_mine)
     down_got = moved(down_held, "y", -1)
-    gate_held = run(stacked, gate_held, gate_got)
-    gate_got = moved(gate_held, "c", -1)
-    in_got = owner_moves(run(owner_parts, in_mine))
+    grad_gate_weight = run(column_whole, gate_held, gate_got)
+    def normed_sum(rest):
+        value = Scatter.sum(*rest).reshape(batch, local + extra, width)
+        return value[:, :local], value[:, local : local + 2].astype(low)
+
     grad_normed, grad_before = run(normed_sum, one_back.rest())
     grad_after = lax.ppermute(grad_before, ("z", "x"), [(j, i) for i, j in last])
-    grad_gate_weight = run(column_whole, gate_held, gate_got)
+    in_got = owner_moves(run(owner_parts, in_mine))
 
     def tokens_back(grad, extension, values, scale, gain, back, small):
         values = values.astype(wide)
@@ -990,10 +982,18 @@
         (grad_feed_gain, grad_residue, grad_decay, grad_taps),
     )
     small_got = moved(small, "c", 1)
+    down_held = run(lambda own, got: jnp.concatenate([own] + got), down_held, down_got)
+    down_got = moved(down_held, "c", -1)
     in_held = run(owner_held, in_got)
     in_got = moved(in_held, "y", -1)
-    down_held = run(lambda own, got: jnp.concatenate([own] + got), down_held, down_got)
-    down_got = moved(down_held, "c", -1)
+    output = run(
+        lambda got, values: (
+            mask
+            * (values + add_up(got[0][:1], got[0][1:] + sum(got[1:], [])).reshape(batch, local, width))
+        ).astype(low),
+        feed_got,
+        middle,
+    )
     small = run(lambda v, got: v + sum(got), small, small_got)
     small_got = moved(small, "z", 1)
 
@@ -1002,14 +1002,19 @@
         return whole.reshape(-1, width).astype(wide)
 
     grad_down = run(rows_whole, down_held, down_got)
+    small = run(lambda v, got: v + sum(got), small, small_got)
+    small_got = moved(small, "x", -1)
+    in_held = run(stacked, in_held, in_got)
+    in_got = moved(in_held, "c", -1)
     out_held = run(lambda v: v[None], out_mine)
     out_got = moved(out_held, "y", -1)
-    small = run(lambda v, got: v + sum(got), small, small_got)
-    small_got = moved(small, "x", -1)
     small = run(stacked, small, small_got)
     small_got = moved(small, "y", -1)
-    in_held = run(stacked, in_held, in_got)
-    in_got = moved(in_held, "c", -1)
+    grad_in_weight = run(
+        lambda own, got: owner_whole(lax.axis_index("c"), [own] + got, count), in_held, in_got
+    )
+    out_held = run(lambda own, got: jnp.concatenate([own] + got), out_held, out_got)
+    out_got = moved(out_held, "c", -1)
     poles = decay.shape[0]
 
     def small_whole(own, got):
@@ -1024,11 +1029,6 @@
 
     grad_norm_gain, feed_gain_sum, grad_conv_taps, residue_sum, decay_sum = run(
         small_whole, small, small_got
-    )
-    out_held = run(lambda own, got: jnp.concatenate([own] + got), out_held, out_got)
-    out_got = moved(out_held, "c", -1)
-    grad_in_weight = run(
-        lambda own, got: owner_whole(lax.axis_index("c"), [own] + got, count), in_held, in_got
     )
 
     def out_whole(core, own, got):

time: 722 us -> 752 us (1.042)
  waiting for transfers between devices: 225 us -> 272 us
  starting transfers between devices: 88.4 us -> 74.2 us
  other arithmetic: 111 us -> 123 us
  local copies, waits for them, and re-layouts: 70.1 us -> 60.8 us
    ppermute x41 -> x45, waiting for transfers between devices: 164 us -> 202 us  [turned(): lax.ppermute(value, axis, [(i, (i + by) % length) for i in range(length)])]
    reduce_scatter x5, waiting for transfers between devices: 0.01 us -> 14.2 us  [scatter_tile(): return lax.psum_scatter(term, ('z', 'c'), scatter_dimension=0, tiled=True)]
    ppermute x12 -> x9, waiting for transfers between devices: 29.9 us -> 17.8 us  [swap_slots(): line.append(lax.ppermute(slots[sy][sx], ('y', 'x'), pairs))]
    unnamed x164 -> x145, local copies, waits for them, and re-layouts: 29.5 us -> 18.7 us
    ppermute x6, waiting for transfers between devices: 2.48 us -> 11.7 us  [passed(): return lax.ppermute(value, axis, pairs)]
    ppermute x3, starting transfers between devices: 21.4 us -> 13.6 us  [owner_moves(): got.append(lax.ppermute(parts[d], ('c', 'x'), pairs))]
    ppermute x41 -> x45, starting transfers between devices: 36.5 us -> 31.8 us  [turned(): lax.ppermute(value, axis, [(i, (i + by) % length) for i in range(length)])]
    another operation x12 -> x15, other arithmetic: 16.2 us -> 20.5 us  [work(): return jnp.stack([first, second]).reshape(-1, first.shape[-1])]
  transfers between devices with their start and end apart: 77 -> 78, of which waited for: 37 -> 36; matrix products, arithmetic and copies ran while one was open for 42% -> 40% of each run, Pallas kernels for 8% -> 8%
where the time goes in v12:
time: 752 us; the launch traced here: 745 us
  waiting for transfers between devices  272 us (36%)
  matrix products  142 us (19%)
  other arithmetic  123 us (16%)
  starting transfers between devices  74.2 us (10%)
  local copies, waits for them, and re-layouts  60.8 us (8%)
  Pallas kernels  56.8 us (8%)
  between operations  16.5 us (2%)
    ppermute x45, waiting for transfers between devices, turned(): lax.ppermute(value, axis, [(i, (i + by) % length) for i in range(length)])  202 us
    dot_general x6, matrix products, dot(): return jnp.dot(a, b, preferred_element_type=wide).astype(kind)  55.9 us
    dot_general x6, matrix products, dot_t(): lax.dot_general(a, b, (((1,), (1,)), ((), ())), preferred_element_type=wide)  46.6 us
    dot_general x5, matrix products, dot_w(): lax.dot_general(a, b, (((0,), (0,)), ((), ())), preferred_element_type=wide)  39.6 us
    pallas_call x4, Pallas kernels, conv_call(): pl.pallas_call(kernel, out_shape=results, grid_spec=pltpu.PrefetchScalarG...  35.5 us
    ppermute x45, starting transfers between devices, turned(): lax.ppermute(value, axis, [(i, (i + by) % length) for i in range(length)])  31.8 us
    another operation x15, other arithmetic, work(): return jnp.stack([first, second]).reshape(-1, first.shape[-1])  20.5 us
    unnamed x145, local copies, waits for them, and re-layouts  18.7 us
  transfers between devices with their start and end apart: 78, of which 36 were waited for; matrix products, arithmetic and copies ran while one was open for 40% of the time, Pallas kernels for 8%

profile of v12, /device:TPU:9, one launch (start us, length us, event | category | flops | bytes accessed | tf_op | source)
XLA Modules:
  0.0 745.1 jit_solution(13660726853539898188)
XLA Ops:
  43.9 10.9 %collective-permute-done.1 = bf16[1,136,2048]{2,1,0:T(8,128)(2,1)} collective-permute-done((bf16[1,136,2048]{2,1,0:T(8,128)(2,1)S(1)}, bf16[1,136,2048]{2,1,0:T(8,128)(2,1)}, u32[]{:S(2)}, u32[]{:S(2)}) %collective-permute-start.1) | collective-permute-done | bytes 557088 | tf_op jit(solution)/shard_map/ppermute | solution.py:20
  75.0 11.1 %collective-permute-done.4 = bf16[2,1,136,2048]{3,2,0,1:T(8,128)(2,1)S(1)} collective-permute-done((bf16[2,1,136,2048]{3,2,0,1:T(8,128)(2,1)}, bf16[2,1,136,2048]{3,2,0,1:T(8,128)(2,1)S(1)}, u32[]{:S(2)}, u32[]{:S(2)}) %collective-permute-start.4) | collective-permute-done | bytes 1114144 | tf_op jit(solution)/shard_map/ppermute | solution.py:20
  86.1 14.3 %collective-permute-done.5 = bf16[2,1,136,2048]{3,2,0,1:T(8,128)(2,1)} collective-permute-done((bf16[2,1,136,2048]{3,2,0,1:T(8,128)(2,1)}, bf16[2,1,136,2048]{3,2,0,1:T(8,128)(2,1)}, u32[]{:S(2)}, u32[]{:S(2)}) %collective-permute-start.5) | collective-permute-done | bytes 1114144 | tf_op jit(solution)/shard_map/ppermute | solution.py:20
  114.0 11.3 %convolution_convert_fusion.4 = bf16[1088,1536]{1,0:T(8,128)(2,1)S(1)} fusion(bf16[1088,2048]{1,0:T(8,128)(2,1)} %bitcast.384, bf16[2048,1536]{1,0:T(8,128)(2,1)} %all-gather.8.cloned.1.call-done), kind=kOutput, calls=%fused_computation.5 | convolution fusion | flops 6846775296 | bytes 14090240 | tf_op jit(solution)/shard_map/dot_general | solution.py:638
  145.0 16.9 %collective-permute-done.14 = bf16[2,1,128,2048]{3,2,0,1:T(8,128)(2,1)S(1)} collective-permute-done((bf16[2,1,128,2048]{3,2,0,1:T(8,128)(2,1)S(1)}, bf16[2,1,128,2048]{3,2,0,1:T(8,128)(2,1)S(1)}, u32[]{:S(2)}, u32[]{:S(2)}) %collective-permute-start.14) | collective-permute-done | bytes 1048608 | tf_op jit(solution)/shard_map/ppermute | solution.py:20
  167.4 15.1 %collective-permute-done.12 = bf16[1,256,1024]{2,1,0:T(8,128)(2,1)S(1)} collective-permute-done((bf16[1,256,1024]{2,1,0:T(8,128)(2,1)S(1)}, bf16[1,256,1024]{2,1,0:T(8,128)(2,1)S(1)}, u32[]{:S(2)}, u32[]{:S(2)}) %collective-permute-start.12) | collective-permute-done | bytes 524320 | tf_op jit(solution)/shard_map/ppermute | solution.py:20
  188.8 11.7 %collective-permute-done.9 = f32[4,16,512]{2,1,0:T(8,128)S(1)} collective-permute-done((f32[4,16,512]{2,1,0:T(8,128)S(1)}, f32[4,16,512]{2,1,0:T(8,128)S(1)}, u32[]{:S(2)}, u32[]{:S(2)}) %collective-permute-start.9) | collective-permute-done | bytes 131104 | tf_op jit(solution)/shard_map/ppermute | solution.py:26
  204.3 8.8 %shard_map.222 = bf16[4,2,1,128,512]{4,3,2,1,0:T(8,128)(2,1)} custom-call(s32[1]{0:T(128)} %bitcast.36.place_ref, bf16[4,2,1,128,512]{4,3,2,1,0:T(8,128)(2,1)} %fusion.49.signal_ref, f32[16,512]{1,0:T(8,128)} %maximum_bitcast_fusion.11.decay_ref, f32[16,512]{1,0:T(8,128)} %maximum_bitcast_fusion.12.residue_ref, f32[4,16,512]{2,1,0:T(8,128)} %multiply_add_fusion.2.start_ref), custom_call_target="tpu_custom_call" | custom-call | flops 33554432 | bytes 2293760 | tf_op jit(solution)/shard_map/pallas_call | solution.py:555
  218.1 7.8 %collective-permute-done.19 = bf16[2,1,256,1024]{3,2,0,1:T(8,128)(2,1)} collective-permute-done((bf16[2,1,256,1024]{3,2,0,1:T(8,128)(2,1)}, bf16[2,1,256,1024]{3,2,0,1:T(8,128)(2,1)}, u32[]{:S(2)}, u32[]{:S(2)}) %collective-permute-start.19) | collective-permute-done | bytes 1048608 | tf_op jit(solution)/shard_map/ppermute | solution.py:20
  240.1 7.1 collective-permute-done.18
  258.2 12.0 %fusion.119 = f32[1024,1408]{1,0:T(8,128)} fusion(bf16[1024,2048]{1,0:T(8,128)(2,1)} %bitcast.394, bf16[1408,2048]{1,0:T(8,128)(2,1)} %all-gather.10.cloned.1.call-done), kind=kOutput, calls=%fused_computation.412 | convolution fusion | flops 5905580032 | bytes 15728640 | tf_op jit(solution)/shard_map/dot_general | solution.py:642
  272.3 21.2 %collective-permute-done.25 = bf16[2,1,128,2048]{3,2,0,1:T(8,128)(2,1)S(1)} collective-permute-done((bf16[2,1,128,2048]{3,2,0,1:T(8,128)(2,1)S(1)}, bf16[2,1,128,2048]{3,2,0,1:T(8,128)(2,1)S(1)}, u32[]{:S(2)}, u32[]{:S(2)}) %collective-permute-start.25) | collective-permute-done | bytes 1048608 | tf_op jit(solution)/shard_map/ppermute | solution.py:20
  296.5 13.2 %multiply_convert_fusion.2 = (bf16[1024,1408]{1,0:T(8,128)(2,1)S(1)}, f32[1024,1408]{1,0:T(8,128)}) fusion(f32[1024,1408]{1,0:T(8,128)} %fusion.119, bf16[1024,2048]{1,0:T(8,128)(2,1)} %bitcast.396, bf16[2048,1408]{1,0:T(8,128)(2,1)} %all-gather.14.cloned.1.call-done), kind=kOutput, calls=%fused_computation.10 | convolution fusion | flops 5914230784 | bytes 24379392 | tf_op jit(solution)/shard_map/dot_general | solution.py:638
  311.3 8.7 %convolution_convert_fusion.3 = bf16[2048,1408]{1,0:T(8,128)(2,1)} fusion(bf16[1024,2048]{1,0:T(8,128)(2,1)S(1)} %bitcast.398, bf16[1024,1408]{1,0:T(8,128)(2,1)S(1)} %get-tuple-element.695), kind=kOutput, calls=%fused_computation.4 | convolution fusion | flops 5908463616 | bytes 12845056 | tf_op jit(solution)/shard_map/dot_general | solution.py:646
  320.0 15.3 %multiply_convert_fusion = (bf16[1024,1408]{1,0:T(8,128)(2,1)S(1)}, bf16[1024,1408]{1,0:T(8,128)(2,1)}) fusion(f32[1024,1408]{1,0:T(8,128)} %get-tuple-element.685, f32[1024,1408]{1,0:T(8,128)} %fusion.119, bf16[1024,2048]{1,0:T(8,128)(2,1)} %bitcast.397, bf16[2048,1408]{1,0:T(8,128)(2,1)} %all-gather.12.cloned.1.call-done), kind=kOutput, calls=%fused_computation.7 | convolution fusion | flops 5924323328 | bytes 27262976 | tf_op jit(solution)/shard_map/dot_general | solution.py:638
  336.9 8.9 %fusion.120 = f32[1024,2048]{1,0:T(8,128)S(1)} fusion(bf16[1024,1408]{1,0:T(8,128)(2,1)S(1)} %get-tuple-element.704, bf16[2048,1408]{1,0:T(8,128)(2,1)} %all-gather.14.cloned.1.call-done), kind=kOutput, calls=%fused_computation.413 | convolution fusion | flops 5905580032 | bytes 17039360 | tf_op jit(solution)/shard_map/dot_general | solution.py:642
  345.8 8.4 %add_convert_fusion = bf16[1024,2048]{1,0:T(8,128)(2,1)S(1)} fusion(f32[1024,2048]{1,0:T(8,128)S(1)} %fusion.120, bf16[1024,1408]{1,0:T(8,128)(2,1)} %copy-done.59, bf16[2048,1408]{1,0:T(8,128)(2,1)S(1)} %copy-done.55), kind=kOutput, calls=%fused_computation | convolution fusion | flops 5909774336 | bytes 21233664 | tf_op jit(solution)/shard_map/dot_general | solution.py:642
  359.9 8.7 %convolution_convert_fusion.2 = bf16[2048,1408]{1,0:T(8,128)(2,1)} fusion(bf16[1024,2048]{1,0:T(8,128)(2,1)S(1)} %bitcast.399, bf16[1024,1408]{1,0:T(8,128)(2,1)S(1)} %copy-done.58), kind=kOutput, calls=%fused_computation.3 | convolution fusion | flops 5908463616 | bytes 12845056 | tf_op jit(solution)/shard_map/dot_general | solution.py:646
  369.0 11.9 %collective-permute-done.27 = bf16[2,128,2048]{2,1,0:T(8,128)(2,1)} collective-permute-done((bf16[2,128,2048]{2,1,0:T(8,128)(2,1)}, bf16[2,128,2048]{2,1,0:T(8,128)(2,1)}, u32[]{:S(2)}, u32[]{:S(2)}) %collective-permute-start.27) | collective-permute-done | bytes 1048608 | tf_op jit(solution)/shard_map/ppermute | solution.py:20
  386.4 8.7 %convolution_convert_fusion.6 = bf16[1024,2048]{1,0:T(8,128)(2,1)S(1)} fusion(bf16[1024,1408]{1,0:T(8,128)(2,1)S(1)} %copy-done.56, bf16[1408,2048]{1,0:T(8,128)(2,1)} %all-gather.10.cloned.1.call-done), kind=kOutput, calls=%fused_computation.26 | convolution fusion | flops 5907677184 | bytes 12845056 | tf_op jit(solution)/shard_map/dot_general | solution.py:638
  410.5 8.0 %convolution_convert_fusion.1 = bf16[1408,2048]{1,0:T(8,128)(2,1)} fusion(bf16[1024,1408]{1,0:T(8,128)(2,1)S(1)} %copy-done.56, bf16[1024,2048]{1,0:T(8,128)(2,1)S(1)} %bitcast.395), kind=kOutput, calls=%fused_computation.2 | convolution fusion | flops 5908463616 | bytes 12845056 | tf_op jit(solution)/shard_map/dot_general | solution.py:646
  449.3 10.2 %reduce-scatter.6.cloned.1.call-done = bf16[256,1408]{1,0:T(8,128)(2,1)} async-done(((bf16[2048,1408]{1,0:T(8,128)(2,1)}), bf16[256,1408]{1,0:T(8,128)(2,1)}) %reduce-scatter.6.cloned.1.call-update) | async-done | bytes 720912 | tf_op jit(solution)/shard_map/reduce_scatter | solution.py:237
  459.5 6.1 collective-permute-start.42
  472.0 16.8 %shard_map.224 = (bf16[4,2,1,128,512]{4,3,2,1,0:T(8,128)(2,1)}, f32[16,512]{1,0:T(8,128)}, f32[16,512]{1,0:T(8,128)}) custom-call(s32[1]{0:T(128)} %bitcast.36.place_ref, bf16[4,2,1,128,512]{4,3,2,1,0:T(8,128)(2,1)} %fusion.49.signal_ref, bf16[4,2,1,128,512]{4,3,2,1,0:T(8,128)(2,1)} %get-tuple-element.779.signal_ref.grad_ref, ...), custom_call_target="tpu_custom_call" | custom-call | flops 100663296 | bytes 4521984 | tf_op jit(solution)/shard_map/pallas_call | solution.py:555
  501.4 10.5 %convolution_convert_fusion = bf16[2048,1536]{1,0:T(8,128)(2,1)} fusion(bf16[1088,2048]{1,0:T(8,128)(2,1)S(1)} %bitcast.387, bf16[1088,1024]{1,0:T(8,128)(2,1)S(1)} %bitcast.376, bf16[1088,512]{1,0:T(8,128)(2,1)S(1)} %bitcast.383), kind=kOutput, calls=%fused_computation.1 | convolution fusion | flops 6854934528 | bytes 14090240 | tf_op jit(solution)/shard_map/dot_general | solution.py:646
  515.9 9.2 %collective-permute-done.45 = bf16[256,1408]{1,0:T(8,128)(2,1)} collective-permute-done((bf16[256,1408]{1,0:T(8,128)(2,1)}, bf16[256,1408]{1,0:T(8,128)(2,1)}, u32[]{:S(2)}, u32[]{:S(2)}) %collective-permute-start.45) | collective-permute-done | bytes 720928 | tf_op jit(solution)/shard_map/ppermute | solution.py:262
  527.4 10.3 %convolution_convert_fusion.5 = bf16[1088,2048]{1,0:T(8,128)(2,1)S(1)} fusion(bf16[1088,1536]{1,0:T(8,128)(2,1)} %pad_maximum_fusion.7, bf16[2048,1536]{1,0:T(8,128)(2,1)} %all-gather.8.cloned.1.call-done), kind=kOutput, calls=%fused_computation.6 | convolution fusion | flops 6847332352 | bytes 14090240 | tf_op jit(solution)/shard_map/dot_general | solution.py:642
  592.4 7.0 collective-permute-done.51
  617.4 50.9 %collective-permute-done.55 = bf16[1,176,2048]{2,1,0:T(8,128)(2,1)} collective-permute-done((bf16[1,176,2048]{2,1,0:T(8,128)(2,1)}, bf16[1,176,2048]{2,1,0:T(8,128)(2,1)}, u32[]{:S(2)}, u32[]{:S(2)}) %collective-permute-start.55) | collective-permute-done | bytes 720928 | tf_op jit(solution)/shard_map/ppermute | solution.py:20
  676.2 7.5 %collective-permute-done.54 = bf16[256,1536]{1,0:T(8,128)(2,1)} collective-permute-done((bf16[256,1536]{1,0:T(8,128)(2,1)S(1)}, bf16[256,1536]{1,0:T(8,128)(2,1)}, u32[]{:S(2)}, u32[]{:S(2)}) %collective-permute-start.54) | collective-permute-done | bytes 786464 | tf_op jit(solution)/shard_map/ppermute | solution.py:262
  698.8 7.6 %collective-permute-done.59 = f32[49,512]{1,0:T(8,128)S(1)} collective-permute-done((f32[49,512]{1,0:T(8,128)S(1)}, f32[49,512]{1,0:T(8,128)S(1)}, u32[]{:S(2)}, u32[]{:S(2)}) %collective-permute-start.59) | collective-permute-done | bytes 100384 | tf_op jit(solution)/shard_map/ppermute | solution.py:20
  721.6 6.0 shard_map.227
  (503 shorter events, 346.4 us)
Async XLA Ops:
  7.2 31.8 %all-gather.6.cloned.1.call-start = ((), (), s32[]{:S(2)}) async-start(), calls=%async_computation.5 | async-start | bytes 1310720 | tf_op jit(solution)/shard_map/all_gather | solution.py:679
  9.3 104.7 %all-gather.8.cloned.1.call-start = ((), (), s32[]{:S(2)}) async-start(), calls=%async_computation.6 | async-start | bytes 7077888 | tf_op jit(solution)/shard_map/all_gather | solution.py:233
  41.3 215.7 %all-gather.10.cloned.1.call-start = ((), (), s32[]{:S(2)}) async-start(), calls=%async_computation.7 | async-start | bytes 6488064 | tf_op jit(solution)/shard_map/all_gather | solution.py:233
  61.4 235.1 %all-gather.14.cloned.1.call-start = ((), (), s32[]{:S(2)}) async-start(), calls=%async_computation.9 | async-start | bytes 6488064 | tf_op jit(solution)/shard_map/all_gather | solution.py:233
  62.2 72.8 %collective-permute-start.11 = (bf16[256,1408]{1,0:T(8,128)(2,1)}, bf16[256,1408]{1,0:T(8,128)(2,1)}, u32[]{:S(2)}, u32[]{:S(2)}) collective-permute-start(bf16[256,1408]{1,0:T(8,128)(2,1)} %concatenate.265), channel_id=1, source_target_pairs={{0,1},{9,8},{2,3},{11,10},{4,5},{13,12},{6,7},{15,14},{16,17},{25,... | collective-permute-start | bytes 2162696 | tf_op jit(solution)/shard_map/ppermute | solution.py:192
  65.0 35.4 %collective-permute-start.5 = (bf16[2,1,136,2048]{3,2,0,1:T(8,128)(2,1)}, bf16[2,1,136,2048]{3,2,0,1:T(8,128)(2,1)}, u32[]{:S(2)}, u32[]{:S(2)}) collective-permute-start(bf16[2,1,136,2048]{3,2,0,1:T(8,128)(2,1)} %pad_maximum_fusion.17), channel_id=1, source_target_pairs={{0,1},{1,0},{2,3},{3,2},{4,5},{5,4},{6,7},{7,6},{8,9},{9,8},{10,11... | collective-permute-start | bytes 3342344 | tf_op jit(solution)/shard_map/ppermute | solution.py:20
  74.6 35.0 %collective-permute-start.6 = (bf16[1,128,2048]{2,1,0:T(8,128)(2,1)S(1)}, bf16[1,128,2048]{2,1,0:T(8,128)(2,1)S(1)}, u32[]{:S(2)}, u32[]{:S(2)}) collective-permute-start(bf16[1,128,2048]{2,1,0:T(8,128)(2,1)S(1)} %get-tuple-element.557), channel_id=1, source_target_pairs={{0,1},{1,0},{2,3},{3,2},{4,5},{5,4},{6,7},{7,6},{8,9},{9,8},{10,11... | collective-permute-start | bytes 1572872 | tf_op jit(solution)/shard_map/ppermute | solution.py:20
  74.6 35.0 %collective-permute-start.7 = (bf16[1,128,2048]{2,1,0:T(8,128)(2,1)S(1)}, bf16[1,128,2048]{2,1,0:T(8,128)(2,1)S(1)}, u32[]{:S(2)}, u32[]{:S(2)}) collective-permute-start(bf16[1,128,2048]{2,1,0:T(8,128)(2,1)S(1)} %get-tuple-element.559), channel_id=1, source_target_pairs={{0,16},{16,0},{1,17},{17,1},{2,18},{18,2},{3,19},{19,3},{4,20},{20... | collective-permute-start | bytes 1572872 | tf_op jit(solution)/shard_map/ppermute | solution.py:20
  137.3 182.7 %all-gather.12.cloned.1.call-start = ((), (), s32[]{:S(2)}) async-start(), calls=%async_computation.8 | async-start | bytes 6488064 | tf_op jit(solution)/shard_map/all_gather | solution.py:233
  137.4 24.6 %collective-permute-start.14 = (bf16[2,1,128,2048]{3,2,0,1:T(8,128)(2,1)S(1)}, bf16[2,1,128,2048]{3,2,0,1:T(8,128)(2,1)S(1)}, u32[]{:S(2)}, u32[]{:S(2)}) collective-permute-start(bf16[2,1,128,2048]{3,2,0,1:T(8,128)(2,1)S(1)} %bitcast.407), channel_id=1, source_target_pairs={{0,16},{16,0},{1,17},{17,1},{2,18},{18,2},{3,19},{19,3},{4,20},{20... | collective-permute-start | bytes 3145736 | tf_op jit(solution)/shard_map/ppermute | solution.py:20
  138.7 78.3 %collective-permute-start.21 = (bf16[256,1408]{1,0:T(8,128)(2,1)}, bf16[256,1408]{1,0:T(8,128)(2,1)S(1)}, u32[]{:S(2)}, u32[]{:S(2)}) collective-permute-start(bf16[256,1408]{1,0:T(8,128)(2,1)} %concatenate.267), channel_id=1, source_target_pairs={{0,1},{9,8},{2,3},{11,10},{4,5},{13,12},{6,7},{15,14},{16,17},{25,... | collective-permute-start | bytes 2162696 | tf_op jit(solution)/shard_map/ppermute | solution.py:192
  140.0 48.8 %collective-permute-start.10 = (f32[4,16,512]{2,1,0:T(8,128)S(1)}, f32[4,16,512]{2,1,0:T(8,128)S(1)}, u32[]{:S(2)}, u32[]{:S(2)}) collective-permute-start(f32[4,16,512]{2,1,0:T(8,128)S(1)} %copy-done.39), channel_id=1, source_target_pairs={{0,6},{1,7},{8,14},{9,15},{16,22},{17,23},{24,30},{25,31}} | collective-permute-start | bytes 393224 | tf_op jit(solution)/shard_map/ppermute | solution.py:26
  140.6 48.2 %collective-permute-start.8 = (f32[4,16,512]{2,1,0:T(8,128)S(1)}, f32[4,16,512]{2,1,0:T(8,128)S(1)}, u32[]{:S(2)}, u32[]{:S(2)}) collective-permute-start(f32[4,16,512]{2,1,0:T(8,128)S(1)} %copy-done.39), channel_id=1, source_target_pairs={{0,2},{2,4},{4,6},{1,3},{3,5},{5,7},{8,10},{10,12},{12,14},{9,11},... | collective-permute-start | bytes 393224 | tf_op jit(solution)/shard_map/ppermute | solution.py:26
  162.0 24.7 %collective-permute-start.13 = (bf16[1,256,1024]{2,1,0:T(8,128)(2,1)S(1)}, bf16[1,256,1024]{2,1,0:T(8,128)(2,1)S(1)}, u32[]{:S(2)}, u32[]{:S(2)}) collective-permute-start(bf16[1,256,1024]{2,1,0:T(8,128)(2,1)S(1)} %get-tuple-element.605), channel_id=1, source_target_pairs={{0,16},{16,0},{1,17},{17,1},{2,18},{18,2},{3,19},{19,3},{4,20},{20... | collective-permute-start | bytes 1572872 | tf_op jit(solution)/shard_map/ppermute | solution.py:20
  200.5 25.4 %collective-permute-start.19 = (bf16[2,1,256,1024]{3,2,0,1:T(8,128)(2,1)}, bf16[2,1,256,1024]{3,2,0,1:T(8,128)(2,1)}, u32[]{:S(2)}, u32[]{:S(2)}) collective-permute-start(bf16[2,1,256,1024]{3,2,0,1:T(8,128)(2,1)} %bitcast.67), channel_id=1, source_target_pairs={{0,16},{16,0},{1,17},{17,1},{2,18},{18,2},{3,19},{19,3},{4,20},{20... | collective-permute-start | bytes 3145736 | tf_op jit(solution)/shard_map/ppermute | solution.py:20
  200.5 25.4 %collective-permute-start.20 = (bf16[2,1,256,1024]{3,2,0,1:T(8,128)(2,1)}, bf16[2,1,256,1024]{3,2,0,1:T(8,128)(2,1)}, u32[]{:S(2)}, u32[]{:S(2)}) collective-permute-start(bf16[2,1,256,1024]{3,2,0,1:T(8,128)(2,1)} %pad_maximum_fusion.21), channel_id=1, source_target_pairs={{0,1},{1,0},{2,3},{3,2},{4,5},{5,4},{6,7},{7,6},{8,9},{9,8},{10,11... | collective-permute-start | bytes 3145736 | tf_op jit(solution)/shard_map/ppermute | solution.py:20
  234.9 214.4 %reduce-scatter.8.cloned.1.call-start = ((), (), s32[]{:S(2)}) async-start(), calls=%async_computation.11 | async-start | bytes 6488064 | tf_op jit(solution)/shard_map/reduce_scatter | solution.py:237
  319.9 139.6 %reduce-scatter.6.cloned.1.call-start = ((), (), s32[]{:S(2)}) async-start(), calls=%async_computation.10 | async-start | bytes 6488064 | tf_op jit(solution)/shard_map/reduce_scatter | solution.py:237
  368.5 218.1 %reduce-scatter.12.cloned.1.call-start = ((), (), s32[]{:S(2)}) async-start(), calls=%async_computation.13 | async-start | bytes 6488064 | tf_op jit(solution)/shard_map/reduce_scatter | solution.py:237
  418.6 190.9 %reduce-scatter.10.cloned.1.call-start = ((), (), s32[]{:S(2)}) async-start(), calls=%async_computation.12 | async-start | bytes 7077888 | tf_op jit(solution)/shard_map/reduce_scatter | solution.py:237
  421.5 24.7 %collective-permute-start.40 = (bf16[1,128,2048]{2,1,0:T(8,128)(2,1)S(1)}, bf16[1,128,2048]{2,1,0:T(8,128)(2,1)S(1)}, u32[]{:S(2)}, u32[]{:S(2)}) collective-permute-start(bf16[1,128,2048]{2,1,0:T(8,128)(2,1)S(1)} %get-tuple-element.766), channel_id=1, source_target_pairs={{0,1},{1,0},{2,3},{3,2},{4,5},{5,4},{6,7},{7,6},{8,9},{9,8},{10,11... | collective-permute-start | bytes 1572872 | tf_op jit(solution)/shard_map/ppermute | solution.py:20
  448.3 43.7 %collective-permute-start.43 = (bf16[2,1,128,2048]{3,2,0,1:T(8,128)(2,1)}, bf16[2,1,128,2048]{3,2,0,1:T(8,128)(2,1)}, u32[]{:S(2)}, u32[]{:S(2)}) collective-permute-start(bf16[2,1,128,2048]{3,2,0,1:T(8,128)(2,1)} %pad_maximum_fusion.24), channel_id=1, source_target_pairs={{0,16},{16,0},{1,17},{17,1},{2,18},{18,2},{3,19},{19,3},{4,20},{20... | collective-permute-start | bytes 3145736 | tf_op jit(solution)/shard_map/ppermute | solution.py:20
  449.3 42.7 %collective-permute-start.44 = (bf16[2,1,128,2048]{3,2,0,1:T(8,128)(2,1)}, bf16[2,1,128,2048]{3,2,0,1:T(8,128)(2,1)}, u32[]{:S(2)}, u32[]{:S(2)}) collective-permute-start(bf16[2,1,128,2048]{3,2,0,1:T(8,128)(2,1)} %bitcast.144), channel_id=1, source_target_pairs={{0,1},{1,0},{2,3},{3,2},{4,5},{5,4},{6,7},{7,6},{8,9},{9,8},{10,11... | collective-permute-start | bytes 3145736 | tf_op jit(solution)/shard_map/ppermute | solution.py:20
  459.5 32.5 %collective-permute-start.42 = (bf16[256,1408]{1,0:T(8,128)(2,1)}, bf16[256,1408]{1,0:T(8,128)(2,1)S(1)}, u32[]{:S(2)}, u32[]{:S(2)}) collective-permute-start(bf16[256,1408]{1,0:T(8,128)(2,1)} %reduce-scatter.8.cloned.1.call-done), channel_id=1, source_target_pairs={{8,1},{1,8},{10,3},{3,10},{12,5},{5,12},{14,7},{7,14},{24,17},{17,... | collective-permute-start | bytes 2162696 | tf_op jit(solution)/shard_map/ppermute | solution.py:262
  511.8 204.0 %reduce-scatter.14.cloned.1.call-start = ((), (), s32[]{:S(2)}) async-start(), calls=%async_computation.14 | async-start | bytes 2359296 | tf_op jit(solution)/shard_map/reduce_scatter | solution.py:237
  514.7 36.5 %collective-permute-start.48 = (bf16[1,256,1408]{2,1,0:T(8,128)(2,1)S(1)}, bf16[1,256,1408]{2,1,0:T(8,128)(2,1)}, u32[]{:S(2)}, u32[]{:S(2)}) collective-permute-start(bf16[1,256,1408]{2,1,0:T(8,128)(2,1)S(1)} %fusion.65), channel_id=1, source_target_pairs={{0,16},{16,0},{1,17},{17,1},{2,18},{18,2},{3,19},{19,3},{4,20},{20... | collective-permute-start | bytes 2162696 | tf_op jit(solution)/shard_map/ppermute | solution.py:20
  550.6 25.7 %collective-permute-start.46 = (bf16[2,136,2048]{2,1,0:T(8,128)(2,1)}, bf16[2,136,2048]{2,1,0:T(8,128)(2,1)}, u32[]{:S(2)}, u32[]{:S(2)}) collective-permute-start(bf16[2,136,2048]{2,1,0:T(8,128)(2,1)} %get-tuple-element.821), channel_id=1, source_target_pairs={{0,1},{1,0},{2,3},{3,2},{4,5},{5,4},{6,7},{7,6},{8,9},{9,8},{10,11... | collective-permute-start | bytes 3342344 | tf_op jit(solution)/shard_map/ppermute | solution.py:20
  550.6 29.7 %collective-permute-start.47 = (bf16[2,136,2048]{2,1,0:T(8,128)(2,1)}, bf16[2,136,2048]{2,1,0:T(8,128)(2,1)}, u32[]{:S(2)}, u32[]{:S(2)}) collective-permute-start(bf16[2,136,2048]{2,1,0:T(8,128)(2,1)} %bitcast.430), channel_id=1, source_target_pairs={{0,16},{16,0},{1,17},{17,1},{2,18},{18,2},{3,19},{19,3},{4,20},{20... | collective-permute-start | bytes 3342344 | tf_op jit(solution)/shard_map/ppermute | solution.py:20
  606.5 78.6 %collective-permute-start.29 = (bf16[2,128,2048]{2,1,0:T(8,128)(2,1)}, bf16[2,128,2048]{2,1,0:T(8,128)(2,1)}, u32[]{:S(2)}, u32[]{:S(2)}) collective-permute-start(bf16[2,128,2048]{2,1,0:T(8,128)(2,1)} %get-tuple-element.717), channel_id=1, source_target_pairs={{0,1},{1,0},{16,17},{17,16},{2,3},{3,2},{18,19},{19,18},{4,5},{5,4... | collective-permute-start | bytes 3145736 | tf_op jit(solution)/shard_map/ppermute | solution.py:44
  606.6 78.6 %collective-permute-start.30 = (bf16[2,128,2048]{2,1,0:T(8,128)(2,1)}, bf16[2,128,2048]{2,1,0:T(8,128)(2,1)}, u32[]{:S(2)}, u32[]{:S(2)}) collective-permute-start(bf16[2,128,2048]{2,1,0:T(8,128)(2,1)} %get-tuple-element.718), channel_id=1, source_target_pairs={{0,16},{1,17},{16,0},{17,1},{2,18},{3,19},{18,2},{19,3},{4,20},{5,... | collective-permute-start | bytes 3145736 | tf_op jit(solution)/shard_map/ppermute | solution.py:44
  606.9 78.2 %collective-permute-start.31 = (bf16[2,128,2048]{2,1,0:T(8,128)(2,1)}, bf16[2,128,2048]{2,1,0:T(8,128)(2,1)}, u32[]{:S(2)}, u32[]{:S(2)}) collective-permute-start(bf16[2,128,2048]{2,1,0:T(8,128)(2,1)} %get-tuple-element.719), channel_id=1, source_target_pairs={{0,17},{1,16},{16,1},{17,0},{2,19},{3,18},{18,3},{19,2},{4,21},{5,... | collective-permute-start | bytes 3145736 | tf_op jit(solution)/shard_map/ppermute | solution.py:44
  609.2 59.1 %collective-permute-start.55 = (bf16[1,176,2048]{2,1,0:T(8,128)(2,1)}, bf16[1,176,2048]{2,1,0:T(8,128)(2,1)}, u32[]{:S(2)}, u32[]{:S(2)}) collective-permute-start(bf16[1,176,2048]{2,1,0:T(8,128)(2,1)} %bitcast.196), channel_id=1, source_target_pairs={{0,16},{16,0},{1,17},{17,1},{2,18},{18,2},{3,19},{19,3},{4,20},{20... | collective-permute-start | bytes 2162696 | tf_op jit(solution)/shard_map/ppermute | solution.py:20
  (108 other events, 1288.2 us)
Sparse Core Ops, SparseCore 0:
  10.2 28.8 all-gather.5
  41.5 63.0 all-gather.7
  106.8 64.2 all-gather.9
  173.2 66.0 all-gather.13
  240.7 60.1 all-gather.11
  320.0 66.8 reduce-scatter.7
  389.8 69.6 reduce-scatter.5
  461.8 65.7 reduce-scatter.11
  530.4 68.1 reduce-scatter.9
  676.4 39.4 reduce-scatter.13

commit v13 on v12

--- a/solution.py
+++ b/solution.py
@@ -700,15 +700,10 @@
     w_in = gather_tile(in_block)
     normed_move.turn(line)
     w_down = gather_tile(run(row_block, down_weight))
-
-    def feed_grad(values):
-        values = (values.astype(wide) * mask).astype(low)
-        return values[: batch // 2], values[batch // 2 :]
-
-    feed_move = Gather(*run(feed_grad, cotangent))
+    out_move = Gather(*run(lambda w: (w[None, : w.shape[0] // 2], w[None, w.shape[0] // 2 :]), w_out))
     up_got = column_moves(run(lambda w: column_pieces(w, 1), up_weight))
     normed_all = normed_move.end(line)
-    feed_move.turn(line)
+    out_move.turn(line)
 
     channels = w_in.shape[1] // 3
     half = channels // 2
@@ -755,9 +750,14 @@
     product, state_end = run(multiply, mixed, taps, decay)
     states = [passed(state_end, "z", k) for k in range(1, depth)]
     w_gate = gather_tile(run(column_block, gate_got))
-    out_move = Gather(*run(lambda w: (w[None, : w.shape[0] // 2], w[None, w.shape[0] // 2 :]), w_out))
-    grad_feed_all = feed_move.end(line)
-    out_move.turn(line)
+    out_own = out_move.end(line)
+    w_out = [out_own] + moved(out_own, "c", -1)
+
+    def feed_grad(values):
+        values = (values.astype(wide) * mask).astype(low)
+        return values[: batch // 2], values[batch // 2 :]
+
+    feed_move = Gather(*run(feed_grad, cotangent))
 
     def combine(parts, rates):
         total = parts[0]
@@ -783,8 +783,7 @@
     )
     gated_got = swap_slots(gated)
     w_up = gather_tile(run(column_block, up_got))
-    out_own = out_move.end(line)
-    w_out = [out_own] + moved(out_own, "c", -1)
+    feed_move.turn(line)
 
     def mix(got, weights, values, gain):
         own = jnp.concatenate(
@@ -800,8 +799,9 @@
     middle, scale_two, first, second = run(mix, gated_got, w_out, tokens, feed_gain)
 
     two_move = Gather(first, second)
+    two_move.turn(line)
+    grad_feed_all = feed_move.end(line)
     grad_active = run(dot_t, grad_feed_all, w_down)
-    two_move.turn(line)
     normed_two_all = two_move.end(line)
 
     def open_gate(v, w, back):
@@ -832,12 +832,7 @@
     )
     gate_mine = scatter_tile(run(dot_w, normed_two_all, grad_gate))
     two_back.turn(line)
-
-    def feed_slots(a, w):
-        value = dot(a, w, low).reshape(2, ycount, spread, -1, width)
-        return [[value[:, k, i] for i in range(spread)] for k in range(ycount)]
-
-    feed_parts = run(feed_slots, active, w_down)
+    feed_parts = run(lambda a, w: split_sum(dot(a, w, low)), active, w_down)
 
     def middle_back(rest, values, scale, gain, back, weights):
         grad_normed = Scatter.sum(*rest).reshape(batch, local, width)
@@ -890,7 +885,7 @@
         result = jnp.concatenate([result, jnp.where(opening, earlier, 0.0), rest], axis=3)
         return result.astype(low).reshape(-1, grad.shape[-1])
 
-    feed_got = swap_slots(feed_parts)
+    feed_back = Scatter(feed_parts)
     up_parts_got = owner_moves(run(owner_parts, up_mine))
     gate_got = owner_moves(run(owner_parts, gate_mine))
 
@@ -924,9 +919,11 @@
 
     grad_mixed, in_term = run(in_back, grad_query, grad_pair, taps, normed_all)
     in_mine = scatter_tile(in_term)
+    feed_back.turn(line)
     gate_held = run(owner_held, gate_got)
     gate_got = moved(gate_held, "y", -1)
     one_back = Scatter(run(lambda a, w: split_sum(dot_t(a, w, low)), grad_mixed, w_in))
+    feed_back.got = run(lambda got: got, feed_back.got)
     grad_mix_all = mix_move.end(line)
     out_mine = scatter_tile(run(dot_w, gated_all, grad_mix_all))
     up_held = run(stacked, up_held, up_got)
@@ -987,11 +984,10 @@
     in_held = run(owner_held, in_got)
     in_got = moved(in_held, "y", -1)
     output = run(
-        lambda got, values: (
-            mask
-            * (values + add_up(got[0][:1], got[0][1:] + sum(got[1:], [])).reshape(batch, local, width))
+        lambda rest, values: (
+            mask * (values + Scatter.sum(*rest).reshape(batch, local, width))
         ).astype(low),
-        feed_got,
+        feed_back.rest(),
         middle,
     )
     small = run(lambda v, got: v + sum(got), small, small_got)

time: 752 us -> 706 us (0.939)
  waiting for transfers between devices: 272 us -> 196 us
  starting transfers between devices: 74.2 us -> 92.4 us
  local copies, waits for them, and re-layouts: 60.8 us -> 71.7 us
    ppermute x45 -> x49, waiting for transfers between devices: 202 us -> 169 us  [turned(): lax.ppermute(value, axis, [(i, (i + by) % length) for i in range(length)])]
    ppermute x3, waiting for transfers between devices: 16.7 us -> 0.01 us  [owner_moves(): got.append(lax.ppermute(parts[d], ('c', 'x'), pairs))]
    reduce_scatter x5, waiting for transfers between devices: 14.2 us -> 0.01 us  [scatter_tile(): return lax.psum_scatter(term, ('z', 'c'), scatter_dimension=0, tiled=True)]
    ppermute x6, waiting for transfers between devices: 11.7 us -> 2.95 us  [passed(): return lax.ppermute(value, axis, pairs)]
    ppermute x1, starting transfers between devices: 1.66 us -> 9.68 us  [body(): lax.ppermute(grad_before, ('z', 'x'), [(j, i) for i, j in last])]
    ppermute x45 -> x49, starting transfers between devices: 31.8 us -> 39.7 us  [turned(): lax.ppermute(value, axis, [(i, (i + by) % length) for i in range(length)])]
    ppermute x9 -> x6, waiting for transfers between devices: 17.8 us -> 14 us  [swap_slots(): line.append(lax.ppermute(slots[sy][sx], ('y', 'x'), pairs))]
    unnamed x145 -> x175, local copies, waits for them, and re-layouts: 18.7 us -> 21.4 us
  transfers between devices with their start and end apart: 78 -> 79, of which waited for: 36 -> 37; matrix products, arithmetic and copies ran while one was open for 40% -> 44% of each run, Pallas kernels for 8% -> 8%
where the time goes in v13:
time: 706 us; the launch traced here: 697 us
  waiting for transfers between devices  196 us (28%)
  matrix products  141 us (20%)
  other arithmetic  122 us (17%)
  starting transfers between devices  92.4 us (13%)
  local copies, waits for them, and re-layouts  71.7 us (10%)
  Pallas kernels  56.8 us (8%)
  between operations  16.6 us (2%)
    ppermute x49, waiting for transfers between devices, turned(): lax.ppermute(value, axis, [(i, (i + by) % length) for i in range(length)])  169 us
    dot_general x6, matrix products, dot(): return jnp.dot(a, b, preferred_element_type=wide).astype(kind)  55.4 us
    dot_general x6, matrix products, dot_t(): lax.dot_general(a, b, (((1,), (1,)), ((), ())), preferred_element_type=wide)  46.2 us
    ppermute x49, starting transfers between devices, turned(): lax.ppermute(value, axis, [(i, (i + by) % length) for i in range(length)])  39.7 us
    dot_general x5, matrix products, dot_w(): lax.dot_general(a, b, (((0,), (0,)), ((), ())), preferred_element_type=wide)  39.7 us
    pallas_call x4, Pallas kernels, conv_call(): pl.pallas_call(kernel, out_shape=results, grid_spec=pltpu.PrefetchScalarG...  35.5 us
    unnamed x175, local copies, waits for them, and re-layouts  21.4 us
    ppermute x3, starting transfers between devices, owner_moves(): got.append(lax.ppermute(parts[d], ('c', 'x'), pairs))  19.2 us
  transfers between devices with their start and end apart: 79, of which 37 were waited for; matrix products, arithmetic and copies ran while one was open for 44% of the time, Pallas kernels for 8%

profile of v13, /device:TPU:9, one launch (start us, length us, event | category | flops | bytes accessed | tf_op | source)
XLA Modules:
  0.0 696.9 jit_solution(3857459491031583109)
XLA Ops:
  33.7 5.3 all-gather.6.cloned.1.call-done
  43.9 10.9 %collective-permute-done.1 = bf16[1,136,2048]{2,1,0:T(8,128)(2,1)} collective-permute-done((bf16[1,136,2048]{2,1,0:T(8,128)(2,1)S(1)}, bf16[1,136,2048]{2,1,0:T(8,128)(2,1)}, u32[]{:S(2)}, u32[]{:S(2)}) %collective-permute-start.1) | collective-permute-done | bytes 557088 | tf_op jit(solution)/shard_map/ppermute | solution.py:20
  77.4 8.5 %collective-permute-done.4 = bf16[2,1,136,2048]{3,2,0,1:T(8,128)(2,1)S(1)} collective-permute-done((bf16[2,1,136,2048]{3,2,0,1:T(8,128)(2,1)}, bf16[2,1,136,2048]{3,2,0,1:T(8,128)(2,1)S(1)}, u32[]{:S(2)}, u32[]{:S(2)}) %collective-permute-start.4) | collective-permute-done | bytes 1114144 | tf_op jit(solution)/shard_map/ppermute | solution.py:20
  92.6 15.6 %collective-permute-done.6 = bf16[1,256,1024]{2,1,0:T(8,128)(2,1)S(1)} collective-permute-done((bf16[1,256,1024]{2,1,0:T(8,128)(2,1)S(1)}, bf16[1,256,1024]{2,1,0:T(8,128)(2,1)S(1)}, u32[]{:S(2)}, u32[]{:S(2)}) %collective-permute-start.6) | collective-permute-done | bytes 524320 | tf_op jit(solution)/shard_map/ppermute | solution.py:20
  112.6 11.0 %convolution_convert_fusion.4 = bf16[1088,1536]{1,0:T(8,128)(2,1)S(1)} fusion(bf16[1088,2048]{1,0:T(8,128)(2,1)} %bitcast.392, bf16[2048,1536]{1,0:T(8,128)(2,1)} %all-gather.8.cloned.1.call-done), kind=kOutput, calls=%fused_computation.5 | convolution fusion | flops 6846775296 | bytes 14090240 | tf_op jit(solution)/shard_map/dot_general | solution.py:638
  136.0 22.9 %collective-permute-done.11 = bf16[2,1,256,1024]{3,2,0,1:T(8,128)(2,1)S(1)} collective-permute-done((bf16[2,1,256,1024]{3,2,0,1:T(8,128)(2,1)S(1)}, bf16[2,1,256,1024]{3,2,0,1:T(8,128)(2,1)S(1)}, u32[]{:S(2)}, u32[]{:S(2)}) %collective-permute-start.11) | collective-permute-done | bytes 1048608 | tf_op jit(solution)/shard_map/ppermute | solution.py:20
  182.8 8.8 %shard_map.222 = bf16[4,2,1,128,512]{4,3,2,1,0:T(8,128)(2,1)} custom-call(s32[1]{0:T(128)} %bitcast.38.place_ref, bf16[4,2,1,128,512]{4,3,2,1,0:T(8,128)(2,1)} %fusion.49.signal_ref, f32[16,512]{1,0:T(8,128)} %maximum_bitcast_fusion.11.decay_ref, f32[16,512]{1,0:T(8,128)} %maximum_bitcast_fusion.12.residue_ref, f32[4,16,512]{2,1,0:T(8,128)} %multiply_add_fusion.2.start_ref), custom_call_target="tpu_custom_call" | custom-call | flops 33554432 | bytes 2293760 | tf_op jit(solution)/shard_map/pallas_call | solution.py:555
  225.2 20.4 %collective-permute-done.21 = bf16[1,128,2048]{2,1,0:T(8,128)(2,1)S(1)} collective-permute-done((bf16[1,128,2048]{2,1,0:T(8,128)(2,1)S(1)}, bf16[1,128,2048]{2,1,0:T(8,128)(2,1)S(1)}, u32[]{:S(2)}, u32[]{:S(2)}) %collective-permute-start.21) | collective-permute-done | bytes 524320 | tf_op jit(solution)/shard_map/ppermute | solution.py:20
  254.2 12.3 %fusion.122 = f32[1024,1408]{1,0:T(8,128)} fusion(bf16[1024,2048]{1,0:T(8,128)(2,1)} %bitcast.402, bf16[1408,2048]{1,0:T(8,128)(2,1)} %all-gather.10.cloned.1.call-done), kind=kOutput, calls=%fused_computation.421 | convolution fusion | flops 5905580032 | bytes 15728640 | tf_op jit(solution)/shard_map/dot_general | solution.py:642
  266.5 10.9 %collective-permute-done.23 = bf16[2,1,128,2048]{3,2,0,1:T(8,128)(2,1)S(1)} collective-permute-done((bf16[2,1,128,2048]{3,2,0,1:T(8,128)(2,1)}, bf16[2,1,128,2048]{3,2,0,1:T(8,128)(2,1)S(1)}, u32[]{:S(2)}, u32[]{:S(2)}) %collective-permute-start.23) | collective-permute-done | bytes 1048608 | tf_op jit(solution)/shard_map/ppermute | solution.py:20
  282.7 13.2 %multiply_convert_fusion.2 = (bf16[1024,1408]{1,0:T(8,128)(2,1)S(1)}, f32[1024,1408]{1,0:T(8,128)}) fusion(f32[1024,1408]{1,0:T(8,128)} %fusion.122, bf16[1024,2048]{1,0:T(8,128)(2,1)} %bitcast.404, bf16[2048,1408]{1,0:T(8,128)(2,1)} %all-gather.14.cloned.1.call-done), kind=kOutput, calls=%fused_computation.10 | convolution fusion | flops 5914230784 | bytes 24379392 | tf_op jit(solution)/shard_map/dot_general | solution.py:638
  297.5 8.7 %convolution_convert_fusion.3 = bf16[2048,1408]{1,0:T(8,128)(2,1)} fusion(bf16[1024,2048]{1,0:T(8,128)(2,1)S(1)} %bitcast.406, bf16[1024,1408]{1,0:T(8,128)(2,1)S(1)} %get-tuple-element.708), kind=kOutput, calls=%fused_computation.4 | convolution fusion | flops 5908463616 | bytes 12845056 | tf_op jit(solution)/shard_map/dot_general | solution.py:646
  306.2 15.2 %multiply_convert_fusion = (bf16[1024,1408]{1,0:T(8,128)(2,1)S(1)}, bf16[1024,1408]{1,0:T(8,128)(2,1)}) fusion(f32[1024,1408]{1,0:T(8,128)} %get-tuple-element.698, f32[1024,1408]{1,0:T(8,128)} %fusion.122, bf16[1024,2048]{1,0:T(8,128)(2,1)} %bitcast.405, bf16[2048,1408]{1,0:T(8,128)(2,1)} %all-gather.12.cloned.1.call-done), kind=kOutput, calls=%fused_computation.7 | convolution fusion | flops 5924323328 | bytes 27262976 | tf_op jit(solution)/shard_map/dot_general | solution.py:638
  323.0 8.9 %fusion.123 = f32[1024,2048]{1,0:T(8,128)S(1)} fusion(bf16[1024,1408]{1,0:T(8,128)(2,1)S(1)} %get-tuple-element.717, bf16[2048,1408]{1,0:T(8,128)(2,1)} %all-gather.14.cloned.1.call-done), kind=kOutput, calls=%fused_computation.422 | convolution fusion | flops 5905580032 | bytes 17039360 | tf_op jit(solution)/shard_map/dot_general | solution.py:642
  332.0 8.4 %add_convert_fusion = bf16[1024,2048]{1,0:T(8,128)(2,1)S(1)} fusion(f32[1024,2048]{1,0:T(8,128)S(1)} %fusion.123, bf16[1024,1408]{1,0:T(8,128)(2,1)} %copy-done.74, bf16[2048,1408]{1,0:T(8,128)(2,1)S(1)} %copy-done.70), kind=kOutput, calls=%fused_computation | convolution fusion | flops 5909774336 | bytes 21233664 | tf_op jit(solution)/shard_map/dot_general | solution.py:642
  345.4 8.7 %convolution_convert_fusion.2 = bf16[2048,1408]{1,0:T(8,128)(2,1)} fusion(bf16[1024,2048]{1,0:T(8,128)(2,1)S(1)} %bitcast.407, bf16[1024,1408]{1,0:T(8,128)(2,1)S(1)} %copy-done.73), kind=kOutput, calls=%fused_computation.3 | convolution fusion | flops 5908463616 | bytes 12845056 | tf_op jit(solution)/shard_map/dot_general | solution.py:646
  354.9 11.8 %collective-permute-done.27 = bf16[2,128,2048]{2,1,0:T(8,128)(2,1)} collective-permute-done((bf16[2,128,2048]{2,1,0:T(8,128)(2,1)}, bf16[2,128,2048]{2,1,0:T(8,128)(2,1)}, u32[]{:S(2)}, u32[]{:S(2)}) %collective-permute-start.27) | collective-permute-done | bytes 1048608 | tf_op jit(solution)/shard_map/ppermute | solution.py:20
  371.0 9.1 %convolution_convert_fusion.6 = bf16[1024,2048]{1,0:T(8,128)(2,1)S(1)} fusion(bf16[1024,1408]{1,0:T(8,128)(2,1)S(1)} %copy-done.71, bf16[1408,2048]{1,0:T(8,128)(2,1)} %all-gather.10.cloned.1.call-done), kind=kOutput, calls=%fused_computation.26 | convolution fusion | flops 5907677184 | bytes 12845056 | tf_op jit(solution)/shard_map/dot_general | solution.py:638
  408.6 8.1 %convolution_convert_fusion.1 = bf16[1408,2048]{1,0:T(8,128)(2,1)} fusion(bf16[1024,1408]{1,0:T(8,128)(2,1)S(1)} %copy-done.71, bf16[1024,2048]{1,0:T(8,128)(2,1)S(1)} %bitcast.403), kind=kOutput, calls=%fused_computation.2 | convolution fusion | flops 5908463616 | bytes 12845056 | tf_op jit(solution)/shard_map/dot_general | solution.py:646
  448.6 14.8 %collective-permute-start.41 = (bf16[256,1408]{1,0:T(8,128)(2,1)}, bf16[256,1408]{1,0:T(8,128)(2,1)S(1)}, u32[]{:S(2)}, u32[]{:S(2)}) collective-permute-start(bf16[256,1408]{1,0:T(8,128)(2,1)} %reduce-scatter.8.cloned.1.call-done), channel_id=1, source_target_pairs={{8,1},{1,8},{10,3},{3,10},{12,5},{5,12},{14,7},{7,14},{24,17},{17,... | collective-permute-start | bytes 2162696 | tf_op jit(solution)/shard_map/ppermute | solution.py:262
  469.8 16.8 %shard_map.224 = (bf16[4,2,1,128,512]{4,3,2,1,0:T(8,128)(2,1)}, f32[16,512]{1,0:T(8,128)}, f32[16,512]{1,0:T(8,128)}) custom-call(s32[1]{0:T(128)} %bitcast.38.place_ref, bf16[4,2,1,128,512]{4,3,2,1,0:T(8,128)(2,1)} %fusion.49.signal_ref, bf16[4,2,1,128,512]{4,3,2,1,0:T(8,128)(2,1)} %get-tuple-element.792.signal_ref.grad_ref, ...), custom_call_target="tpu_custom_call" | custom-call | flops 100663296 | bytes 4521984 | tf_op jit(solution)/shard_map/pallas_call | solution.py:555
  498.5 10.5 %convolution_convert_fusion = bf16[2048,1536]{1,0:T(8,128)(2,1)} fusion(bf16[1088,2048]{1,0:T(8,128)(2,1)S(1)} %bitcast.395, bf16[1088,1024]{1,0:T(8,128)(2,1)S(1)} %bitcast.381, bf16[1088,512]{1,0:T(8,128)(2,1)S(1)} %bitcast.390), kind=kOutput, calls=%fused_computation.1 | convolution fusion | flops 6854934528 | bytes 14090240 | tf_op jit(solution)/shard_map/dot_general | solution.py:646
  525.1 9.5 %convolution_convert_fusion.5 = bf16[1088,2048]{1,0:T(8,128)(2,1)S(1)} fusion(bf16[1088,1536]{1,0:T(8,128)(2,1)S(1)} %copy-done.35, bf16[2048,1536]{1,0:T(8,128)(2,1)} %all-gather.8.cloned.1.call-done), kind=kOutput, calls=%fused_computation.6 | convolution fusion | flops 6847332352 | bytes 14090240 | tf_op jit(solution)/shard_map/dot_general | solution.py:642
  553.6 12.8 %collective-permute-done.51 = bf16[1,256,1408]{2,1,0:T(8,128)(2,1)} collective-permute-done((bf16[1,256,1408]{2,1,0:T(8,128)(2,1)}, bf16[1,256,1408]{2,1,0:T(8,128)(2,1)}, u32[]{:S(2)}, u32[]{:S(2)}) %collective-permute-start.51) | collective-permute-done | bytes 720928 | tf_op jit(solution)/shard_map/ppermute | solution.py:20
  575.6 5.9 shard_map.225
  581.5 6.9 collective-permute-done.48
  594.7 5.8 shard_map.226
  600.5 7.5 %collective-permute-done.52 = bf16[136,2048]{1,0:T(8,128)(2,1)} collective-permute-done((bf16[136,2048]{1,0:T(8,128)(2,1)}, bf16[136,2048]{1,0:T(8,128)(2,1)}, u32[]{:S(2)}, u32[]{:S(2)}) %collective-permute-start.52) | collective-permute-done | bytes 557088 | tf_op jit(solution)/shard_map/ppermute | solution.py:20
  612.6 9.7 %collective-permute-start.57 = (bf16[2,2,2048]{2,1,0:T(2,128)(2,1)S(1)}, bf16[2,2,2048]{2,1,0:T(2,128)(2,1)S(1)}, u32[]{:S(2)}, u32[]{:S(2)}) collective-permute-start(bf16[2,2,2048]{2,1,0:T(2,128)(2,1)S(1)} %fusion.86), channel_id=1, source_target_pairs={{2,1},{4,3},{6,5},{10,9},{12,11},{14,13},{18,17},{20,19},{22,21},{... | collective-permute-start | bytes 49160 | tf_op jit(solution)/shard_map/ppermute | solution.py:959
  632.7 7.0 collective-permute-done.56
  653.2 5.9 collective-permute-done.60
  673.6 6.0 shard_map.227
  (543 shorter events, 342.6 us)
Async XLA Ops:
  7.2 31.8 %all-gather.6.cloned.1.call-start = ((), (), s32[]{:S(2)}) async-start(), calls=%async_computation.5 | async-start | bytes 1310720 | tf_op jit(solution)/shard_map/all_gather | solution.py:679
  9.3 103.4 %all-gather.8.cloned.1.call-start = ((), (), s32[]{:S(2)}) async-start(), calls=%async_computation.6 | async-start | bytes 7077888 | tf_op jit(solution)/shard_map/all_gather | solution.py:233
  41.3 211.2 %all-gather.10.cloned.1.call-start = ((), (), s32[]{:S(2)}) async-start(), calls=%async_computation.7 | async-start | bytes 6488064 | tf_op jit(solution)/shard_map/all_gather | solution.py:233
  61.4 221.3 %all-gather.14.cloned.1.call-start = ((), (), s32[]{:S(2)}) async-start(), calls=%async_computation.9 | async-start | bytes 6488064 | tf_op jit(solution)/shard_map/all_gather | solution.py:233
  61.4 24.4 %collective-permute-start.4 = (bf16[2,1,136,2048]{3,2,0,1:T(8,128)(2,1)}, bf16[2,1,136,2048]{3,2,0,1:T(8,128)(2,1)S(1)}, u32[]{:S(2)}, u32[]{:S(2)}) collective-permute-start(bf16[2,1,136,2048]{3,2,0,1:T(8,128)(2,1)} %bitcast.398), channel_id=1, source_target_pairs={{0,16},{16,0},{1,17},{17,1},{2,18},{18,2},{3,19},{19,3},{4,20},{20... | collective-permute-start | bytes 3342344 | tf_op jit(solution)/shard_map/ppermute | solution.py:20
  63.5 69.9 %collective-permute-start.13 = (bf16[256,1408]{1,0:T(8,128)(2,1)}, bf16[256,1408]{1,0:T(8,128)(2,1)}, u32[]{:S(2)}, u32[]{:S(2)}) collective-permute-start(bf16[256,1408]{1,0:T(8,128)(2,1)} %concatenate.265), channel_id=1, source_target_pairs={{0,1},{9,8},{2,3},{11,10},{4,5},{13,12},{6,7},{15,14},{16,17},{25,... | collective-permute-start | bytes 2162696 | tf_op jit(solution)/shard_map/ppermute | solution.py:192
  74.2 33.9 %collective-permute-start.6 = (bf16[1,256,1024]{2,1,0:T(8,128)(2,1)S(1)}, bf16[1,256,1024]{2,1,0:T(8,128)(2,1)S(1)}, u32[]{:S(2)}, u32[]{:S(2)}) collective-permute-start(bf16[1,256,1024]{2,1,0:T(8,128)(2,1)S(1)} %get-tuple-element.571), channel_id=1, source_target_pairs={{0,1},{1,0},{2,3},{3,2},{4,5},{5,4},{6,7},{7,6},{8,9},{9,8},{10,11... | collective-permute-start | bytes 1572872 | tf_op jit(solution)/shard_map/ppermute | solution.py:20
  77.2 31.0 %collective-permute-start.7 = (bf16[1,256,1024]{2,1,0:T(8,128)(2,1)S(1)}, bf16[1,256,1024]{2,1,0:T(8,128)(2,1)S(1)}, u32[]{:S(2)}, u32[]{:S(2)}) collective-permute-start(bf16[1,256,1024]{2,1,0:T(8,128)(2,1)S(1)} %get-tuple-element.573), channel_id=1, source_target_pairs={{0,16},{16,0},{1,17},{17,1},{2,18},{18,2},{3,19},{19,3},{4,20},{20... | collective-permute-start | bytes 1572872 | tf_op jit(solution)/shard_map/ppermute | solution.py:20
  135.7 170.5 %all-gather.12.cloned.1.call-start = ((), (), s32[]{:S(2)}) async-start(), calls=%async_computation.8 | async-start | bytes 6488064 | tf_op jit(solution)/shard_map/all_gather | solution.py:233
  135.9 24.5 %collective-permute-start.12 = (bf16[2,1,256,1024]{3,2,0,1:T(8,128)(2,1)S(1)}, bf16[2,1,256,1024]{3,2,0,1:T(8,128)(2,1)S(1)}, u32[]{:S(2)}, u32[]{:S(2)}) collective-permute-start(bf16[2,1,256,1024]{3,2,0,1:T(8,128)(2,1)S(1)} %copy-done.29), channel_id=1, source_target_pairs={{0,1},{1,0},{2,3},{3,2},{4,5},{5,4},{6,7},{7,6},{8,9},{9,8},{10,11... | collective-permute-start | bytes 3145736 | tf_op jit(solution)/shard_map/ppermute | solution.py:20
  164.7 48.5 %collective-permute-start.17 = (bf16[2048,1024]{1,0:T(8,128)(2,1)}, bf16[2048,1024]{1,0:T(8,128)(2,1)}, u32[]{:S(2)}, u32[]{:S(2)}) collective-permute-start(bf16[2048,1024]{1,0:T(8,128)(2,1)} %bitcast.52), channel_id=1, source_target_pairs={{0,8},{8,0},{1,9},{9,1},{2,10},{10,2},{3,11},{11,3},{4,12},{12,4},... | collective-permute-start | bytes 12582920 | tf_op jit(solution)/shard_map/ppermute | solution.py:20
  165.1 30.5 %collective-permute-start.20 = (bf16[256,1408]{1,0:T(8,128)(2,1)}, bf16[256,1408]{1,0:T(8,128)(2,1)S(1)}, u32[]{:S(2)}, u32[]{:S(2)}) collective-permute-start(bf16[256,1408]{1,0:T(8,128)(2,1)} %concatenate.267), channel_id=1, source_target_pairs={{0,1},{9,8},{2,3},{11,10},{4,5},{13,12},{6,7},{15,14},{16,17},{25,... | collective-permute-start | bytes 2162696 | tf_op jit(solution)/shard_map/ppermute | solution.py:192
  175.6 25.9 %collective-permute-start.18 = (bf16[1,128,2048]{2,1,0:T(8,128)(2,1)S(1)}, bf16[1,128,2048]{2,1,0:T(8,128)(2,1)}, u32[]{:S(2)}, u32[]{:S(2)}) collective-permute-start(bf16[1,128,2048]{2,1,0:T(8,128)(2,1)S(1)} %get-tuple-element.637), channel_id=1, source_target_pairs={{0,1},{1,0},{2,3},{3,2},{4,5},{5,4},{6,7},{7,6},{8,9},{9,8},{10,11... | collective-permute-start | bytes 1572872 | tf_op jit(solution)/shard_map/ppermute | solution.py:20
  201.4 243.8 %reduce-scatter.8.cloned.1.call-start = ((), (), s32[]{:S(2)}) async-start(), calls=%async_computation.11 | async-start | bytes 6488064 | tf_op jit(solution)/shard_map/reduce_scatter | solution.py:237
  204.0 45.7 %collective-permute-start.25 = (bf16[2,1,128,2048]{3,2,0,1:T(8,128)(2,1)S(1)}, bf16[2,1,128,2048]{3,2,0,1:T(8,128)(2,1)S(1)}, u32[]{:S(2)}, u32[]{:S(2)}) collective-permute-start(bf16[2,1,128,2048]{3,2,0,1:T(8,128)(2,1)S(1)} %bitcast.420), channel_id=1, source_target_pairs={{0,16},{16,0},{1,17},{17,1},{2,18},{18,2},{3,19},{19,3},{4,20},{20... | collective-permute-start | bytes 3145736 | tf_op jit(solution)/shard_map/ppermute | solution.py:20
  206.3 43.5 %collective-permute-start.26 = (bf16[2,1,128,2048]{3,2,0,1:T(8,128)(2,1)S(1)}, bf16[2,1,128,2048]{3,2,0,1:T(8,128)(2,1)S(1)}, u32[]{:S(2)}, u32[]{:S(2)}) collective-permute-start(bf16[2,1,128,2048]{3,2,0,1:T(8,128)(2,1)S(1)} %pad_maximum_fusion.21), channel_id=1, source_target_pairs={{0,1},{1,0},{2,3},{3,2},{4,5},{5,4},{6,7},{7,6},{8,9},{9,8},{10,11... | collective-permute-start | bytes 3145736 | tf_op jit(solution)/shard_map/ppermute | solution.py:20
  252.6 24.9 %collective-permute-start.23 = (bf16[2,1,128,2048]{3,2,0,1:T(8,128)(2,1)}, bf16[2,1,128,2048]{3,2,0,1:T(8,128)(2,1)S(1)}, u32[]{:S(2)}, u32[]{:S(2)}) collective-permute-start(bf16[2,1,128,2048]{3,2,0,1:T(8,128)(2,1)} %pad_maximum_fusion.22), channel_id=1, source_target_pairs={{0,16},{16,0},{1,17},{17,1},{2,18},{18,2},{3,19},{19,3},{4,20},{20... | collective-permute-start | bytes 3145736 | tf_op jit(solution)/shard_map/ppermute | solution.py:20
  254.2 24.4 %collective-permute-start.24 = (bf16[2,1,128,2048]{3,2,0,1:T(8,128)(2,1)}, bf16[2,1,128,2048]{3,2,0,1:T(8,128)(2,1)S(1)}, u32[]{:S(2)}, u32[]{:S(2)}) collective-permute-start(bf16[2,1,128,2048]{3,2,0,1:T(8,128)(2,1)} %bitcast.422), channel_id=1, source_target_pairs={{0,1},{1,0},{2,3},{3,2},{4,5},{5,4},{6,7},{7,6},{8,9},{9,8},{10,11... | collective-permute-start | bytes 3145736 | tf_op jit(solution)/shard_map/ppermute | solution.py:20
  306.2 139.0 %reduce-scatter.6.cloned.1.call-start = ((), (), s32[]{:S(2)}) async-start(), calls=%async_computation.10 | async-start | bytes 6488064 | tf_op jit(solution)/shard_map/reduce_scatter | solution.py:237
  354.1 240.6 %reduce-scatter.12.cloned.1.call-start = ((), (), s32[]{:S(2)}) async-start(), calls=%async_computation.13 | async-start | bytes 6488064 | tf_op jit(solution)/shard_map/reduce_scatter | solution.py:237
  385.6 127.4 %collective-permute-start.29 = (bf16[2,128,2048]{2,1,0:T(8,128)(2,1)}, bf16[2,128,2048]{2,1,0:T(8,128)(2,1)}, u32[]{:S(2)}, u32[]{:S(2)}) collective-permute-start(bf16[2,128,2048]{2,1,0:T(8,128)(2,1)} %get-tuple-element.730), channel_id=1, source_target_pairs={{0,1},{1,0},{2,3},{3,2},{4,5},{5,4},{6,7},{7,6},{8,9},{9,8},{10,11... | collective-permute-start | bytes 3145736 | tf_op jit(solution)/shard_map/ppermute | solution.py:20
  386.0 127.0 %collective-permute-start.30 = (bf16[2,128,2048]{2,1,0:T(8,128)(2,1)}, bf16[2,128,2048]{2,1,0:T(8,128)(2,1)}, u32[]{:S(2)}, u32[]{:S(2)}) collective-permute-start(bf16[2,128,2048]{2,1,0:T(8,128)(2,1)} %bitcast.114), channel_id=1, source_target_pairs={{0,16},{16,0},{1,17},{17,1},{2,18},{18,2},{3,19},{19,3},{4,20},{20... | collective-permute-start | bytes 3145736 | tf_op jit(solution)/shard_map/ppermute | solution.py:20
  416.8 205.9 %reduce-scatter.10.cloned.1.call-start = ((), (), s32[]{:S(2)}) async-start(), calls=%async_computation.12 | async-start | bytes 7077888 | tf_op jit(solution)/shard_map/reduce_scatter | solution.py:237
  445.2 44.6 %collective-permute-start.42 = (bf16[2,1,128,2048]{3,2,0,1:T(8,128)(2,1)}, bf16[2,1,128,2048]{3,2,0,1:T(8,128)(2,1)}, u32[]{:S(2)}, u32[]{:S(2)}) collective-permute-start(bf16[2,1,128,2048]{3,2,0,1:T(8,128)(2,1)} %pad_maximum_fusion.24), channel_id=1, source_target_pairs={{0,16},{16,0},{1,17},{17,1},{2,18},{18,2},{3,19},{19,3},{4,20},{20... | collective-permute-start | bytes 3145736 | tf_op jit(solution)/shard_map/ppermute | solution.py:20
  448.6 41.2 %collective-permute-start.43 = (bf16[2,1,128,2048]{3,2,0,1:T(8,128)(2,1)}, bf16[2,1,128,2048]{3,2,0,1:T(8,128)(2,1)}, u32[]{:S(2)}, u32[]{:S(2)}) collective-permute-start(bf16[2,1,128,2048]{3,2,0,1:T(8,128)(2,1)} %bitcast.413), channel_id=1, source_target_pairs={{0,1},{1,0},{2,3},{3,2},{4,5},{5,4},{6,7},{7,6},{8,9},{9,8},{10,11... | collective-permute-start | bytes 3145736 | tf_op jit(solution)/shard_map/ppermute | solution.py:20
  448.6 43.6 %collective-permute-start.41 = (bf16[256,1408]{1,0:T(8,128)(2,1)}, bf16[256,1408]{1,0:T(8,128)(2,1)S(1)}, u32[]{:S(2)}, u32[]{:S(2)}) collective-permute-start(bf16[256,1408]{1,0:T(8,128)(2,1)} %reduce-scatter.8.cloned.1.call-done), channel_id=1, source_target_pairs={{8,1},{1,8},{10,3},{3,10},{12,5},{5,12},{14,7},{7,14},{24,17},{17,... | collective-permute-start | bytes 2162696 | tf_op jit(solution)/shard_map/ppermute | solution.py:262
  489.8 33.1 %collective-permute-start.46 = (bf16[256,1408]{1,0:T(8,128)(2,1)}, bf16[256,1408]{1,0:T(8,128)(2,1)}, u32[]{:S(2)}, u32[]{:S(2)}) collective-permute-start(bf16[256,1408]{1,0:T(8,128)(2,1)} %reduce-scatter.6.cloned.1.call-done), channel_id=1, source_target_pairs={{8,1},{1,8},{10,3},{3,10},{12,5},{5,12},{14,7},{7,14},{24,17},{17,... | collective-permute-start | bytes 2162696 | tf_op jit(solution)/shard_map/ppermute | solution.py:262
  518.3 149.3 %reduce-scatter.14.cloned.1.call-start = ((), (), s32[]{:S(2)}) async-start(), calls=%async_computation.14 | async-start | bytes 2359296 | tf_op jit(solution)/shard_map/reduce_scatter | solution.py:237
  522.8 28.2 %collective-permute-start.49 = (bf16[1,256,1408]{2,1,0:T(8,128)(2,1)S(1)}, bf16[1,256,1408]{2,1,0:T(8,128)(2,1)}, u32[]{:S(2)}, u32[]{:S(2)}) collective-permute-start(bf16[1,256,1408]{2,1,0:T(8,128)(2,1)S(1)} %fusion.67), channel_id=1, source_target_pairs={{0,16},{16,0},{1,17},{17,1},{2,18},{18,2},{3,19},{19,3},{4,20},{20... | collective-permute-start | bytes 2162696 | tf_op jit(solution)/shard_map/ppermute | solution.py:20
  538.1 28.4 %collective-permute-start.51 = (bf16[1,256,1408]{2,1,0:T(8,128)(2,1)}, bf16[1,256,1408]{2,1,0:T(8,128)(2,1)}, u32[]{:S(2)}, u32[]{:S(2)}) collective-permute-start(bf16[1,256,1408]{2,1,0:T(8,128)(2,1)} %fusion.66), channel_id=1, source_target_pairs={{0,16},{16,0},{1,17},{17,1},{2,18},{18,2},{3,19},{19,3},{4,20},{20... | collective-permute-start | bytes 2162696 | tf_op jit(solution)/shard_map/ppermute | solution.py:20
  539.4 42.1 %collective-permute-start.47 = (bf16[2,136,2048]{2,1,0:T(8,128)(2,1)}, bf16[2,136,2048]{2,1,0:T(8,128)(2,1)}, u32[]{:S(2)}, u32[]{:S(2)}) collective-permute-start(bf16[2,136,2048]{2,1,0:T(8,128)(2,1)} %get-tuple-element.847), channel_id=1, source_target_pairs={{0,1},{1,0},{2,3},{3,2},{4,5},{5,4},{6,7},{7,6},{8,9},{9,8},{10,11... | collective-permute-start | bytes 3342344 | tf_op jit(solution)/shard_map/ppermute | solution.py:20
  540.9 47.5 %collective-permute-start.48 = (bf16[2,136,2048]{2,1,0:T(8,128)(2,1)}, bf16[2,136,2048]{2,1,0:T(8,128)(2,1)}, u32[]{:S(2)}, u32[]{:S(2)}) collective-permute-start(bf16[2,136,2048]{2,1,0:T(8,128)(2,1)} %bitcast.165), channel_id=1, source_target_pairs={{0,16},{16,0},{1,17},{17,1},{2,18},{18,2},{3,19},{19,3},{4,20},{20... | collective-permute-start | bytes 3342344 | tf_op jit(solution)/shard_map/ppermute | solution.py:20
  (124 other events, 1269.9 us)
Sparse Core Ops, SparseCore 0:
  10.2 28.8 all-gather.5
  41.5 63.0 all-gather.7
  106.2 59.2 all-gather.9
  167.6 64.4 all-gather.13
  233.6 59.0 all-gather.11
  306.3 63.2 reduce-scatter.7
  372.5 63.1 reduce-scatter.5
  437.9 71.5 reduce-scatter.11
  518.4 72.0 reduce-scatter.9
  622.4 36.1 reduce-scatter.13

commit v14 on v13

--- a/solution.py
+++ b/solution.py
@@ -728,6 +728,7 @@
         return dot(v, w, low).reshape(grid[:3] + (local + extra, 3 * channels))
 
     mixed = run(project, normed_all, w_in)
+    out_move.got = run(lambda got: got, out_move.got)
 
     def extend(value, g):
         own = value[..., g * channels : (g + 1) * channels]
@@ -928,8 +929,6 @@
     out_mine = scatter_tile(run(dot_w, gated_all, grad_mix_all))
     up_held = run(stacked, up_held, up_got)
     up_got = moved(up_held, "c", -1)
-    gate_held = run(stacked, gate_held, gate_got)
-    gate_got = moved(gate_held, "c", -1)
 
     def tap_sums(query, pair, value):
         sums = []
@@ -947,17 +946,29 @@
         return owner_whole(lax.axis_index("c"), [own] + got, depth)
 
     grad_up_weight = run(column_whole, up_held, up_got)
+    gate_held = run(stacked, gate_held, gate_got)
+    gate_got = moved(gate_held, "c", -1)
     one_back.turn(line)
-    down_held = run(lambda v: v[None], down_mine)
-    down_got = moved(down_held, "y", -1)
     grad_gate_weight = run(column_whole, gate_held, gate_got)
+    in_got = owner_moves(run(owner_parts, in_mine))
+
     def normed_sum(rest):
         value = Scatter.sum(*rest).reshape(batch, local + extra, width)
         return value[:, :local], value[:, local : local + 2].astype(low)
 
     grad_normed, grad_before = run(normed_sum, one_back.rest())
     grad_after = lax.ppermute(grad_before, ("z", "x"), [(j, i) for i, j in last])
-    in_got = owner_moves(run(owner_parts, in_mine))
+    output = run(
+        lambda rest, values: (
+            mask * (values + Scatter.sum(*rest).reshape(batch, local, width))
+        ).astype(low),
+        feed_back.rest(),
+        middle,
+    )
+    in_held = run(owner_held, in_got)
+    in_got = moved(in_held, "y", -1)
+    down_held = run(lambda v: v[None], down_mine)
+    down_got = moved(down_held, "y", -1)
 
     def tokens_back(grad, extension, values, scale, gain, back, small):
         values = values.astype(wide)
@@ -979,36 +990,27 @@
         (grad_feed_gain, grad_residue, grad_decay, grad_taps),
     )
     small_got = moved(small, "c", 1)
+    small = run(lambda v, got: v + sum(got), small, small_got)
+    small_got = moved(small, "z", 1)
+    in_held = run(stacked, in_held, in_got)
+    in_got = moved(in_held, "c", -1)
+    small = run(lambda v, got: v + sum(got), small, small_got)
+    small_got = moved(small, "x", -1)
+    grad_in_weight = run(
+        lambda own, got: owner_whole(lax.axis_index("c"), [own] + got, count), in_held, in_got
+    )
     down_held = run(lambda own, got: jnp.concatenate([own] + got), down_held, down_got)
     down_got = moved(down_held, "c", -1)
-    in_held = run(owner_held, in_got)
-    in_got = moved(in_held, "y", -1)
-    output = run(
-        lambda rest, values: (
-            mask * (values + Scatter.sum(*rest).reshape(batch, local, width))
-        ).astype(low),
-        feed_back.rest(),
-        middle,
-    )
-    small = run(lambda v, got: v + sum(got), small, small_got)
-    small_got = moved(small, "z", 1)
-
-    def rows_whole(own, got):
-        whole = in_order(jnp.swapaxes(in_order(jnp.stack([own] + got), "c"), 0, 1), "y")
-        return whole.reshape(-1, width).astype(wide)
-
-    grad_down = run(rows_whole, down_held, down_got)
-    small = run(lambda v, got: v + sum(got), small, small_got)
-    small_got = moved(small, "x", -1)
-    in_held = run(stacked, in_held, in_got)
-    in_got = moved(in_held, "c", -1)
     out_held = run(lambda v: v[None], out_mine)
     out_got = moved(out_held, "y", -1)
     small = run(stacked, small, small_got)
     small_got = moved(small, "y", -1)
-    grad_in_weight = run(
-        lambda own, got: owner_whole(lax.axis_index("c"), [own] + got, count), in_held, in_got
-    )
+
+    def rows_whole(own, got):
+        whole = in_order(jnp.swapaxes(in_order(jnp.stack([own] + got), "c"), 0, 1), "y")
+        return whole.reshape(-1, width).astype(wide)
+
+    grad_down = run(rows_whole, down_held, down_got)
     out_held = run(lambda own, got: jnp.concatenate([own] + got), out_held, out_got)
     out_got = moved(out_held, "c", -1)
     poles = decay.shape[0]

time: 706 us -> 709 us (level)
  waiting for transfers between devices: 196 us -> 206 us
    ppermute x49, starting transfers between devices: 39.7 us -> 49.6 us  [turned(): lax.ppermute(value, axis, [(i, (i + by) % length) for i in range(length)])]
    ppermute x49, waiting for transfers between devices: 169 us -> 178 us  [turned(): lax.ppermute(value, axis, [(i, (i + by) % length) for i in range(length)])]
    ppermute x1, starting transfers between devices: 9.68 us -> 1.41 us  [body(): lax.ppermute(grad_before, ('z', 'x'), [(j, i) for i, j in last])]
    ppermute x6, waiting for transfers between devices: 14 us -> 5.9 us  [swap_slots(): line.append(lax.ppermute(slots[sy][sx], ('y', 'x'), pairs))]
    ppermute x3, waiting for transfers between devices: 0.01 us -> 7.12 us  [owner_moves(): got.append(lax.ppermute(parts[d], ('c', 'x'), pairs))]
    unnamed x175 -> x169, local copies, waits for them, and re-layouts: 21.4 us -> 20.9 us
  transfers between devices with their start and end apart: 79 -> 79, of which waited for: 37 -> 36; matrix products, arithmetic and copies ran while one was open for 44% -> 41% of each run, Pallas kernels for 8% -> 8%
where the time goes in v14:
time: 709 us; the launch traced here: 702 us
  waiting for transfers between devices  206 us (29%)
  matrix products  141 us (20%)
  other arithmetic  119 us (17%)
  starting transfers between devices  90.5 us (13%)
  local copies, waits for them, and re-layouts  72.6 us (10%)
  Pallas kernels  56.5 us (8%)
  between operations  16.7 us (2%)
    ppermute x49, waiting for transfers between devices, turned(): lax.ppermute(value, axis, [(i, (i + by) % length) for i in range(length)])  178 us
    dot_general x6, matrix products, dot(): return jnp.dot(a, b, preferred_element_type=wide).astype(kind)  55.3 us
    ppermute x49, starting transfers between devices, turned(): lax.ppermute(value, axis, [(i, (i + by) % length) for i in range(length)])  49.6 us
    dot_general x6, matrix products, dot_t(): lax.dot_general(a, b, (((1,), (1,)), ((), ())), preferred_element_type=wide)  46.2 us
    dot_general x5, matrix products, dot_w(): lax.dot_general(a, b, (((0,), (0,)), ((), ())), preferred_element_type=wide)  39.7 us
    pallas_call x4, Pallas kernels, conv_call(): pl.pallas_call(kernel, out_shape=results, grid_spec=pltpu.PrefetchScalarG...  35.3 us
    unnamed x169, local copies, waits for them, and re-layouts  20.9 us
    another operation x15, other arithmetic, work(): return jnp.stack([first, second]).reshape(-1, first.shape[-1])  17.9 us
  transfers between devices with their start and end apart: 79, of which 36 were waited for; matrix products, arithmetic and copies ran while one was open for 41% of the time, Pallas kernels for 8%

profile of v14, /device:TPU:9, one launch (start us, length us, event | category | flops | bytes accessed | tf_op | source)
XLA Modules:
  0.0 702.0 jit_solution(13966731239917947613)
XLA Ops:
  43.9 10.9 %collective-permute-done.1 = bf16[1,136,2048]{2,1,0:T(8,128)(2,1)} collective-permute-done((bf16[1,136,2048]{2,1,0:T(8,128)(2,1)S(1)}, bf16[1,136,2048]{2,1,0:T(8,128)(2,1)}, u32[]{:S(2)}, u32[]{:S(2)}) %collective-permute-start.1) | collective-permute-done | bytes 557088 | tf_op jit(solution)/shard_map/ppermute | solution.py:20
  77.4 8.4 %collective-permute-done.4 = bf16[2,1,136,2048]{3,2,0,1:T(8,128)(2,1)S(1)} collective-permute-done((bf16[2,1,136,2048]{3,2,0,1:T(8,128)(2,1)}, bf16[2,1,136,2048]{3,2,0,1:T(8,128)(2,1)S(1)}, u32[]{:S(2)}, u32[]{:S(2)}) %collective-permute-start.4) | collective-permute-done | bytes 1114144 | tf_op jit(solution)/shard_map/ppermute | solution.py:20
  92.6 15.6 %collective-permute-done.6 = bf16[1,256,1024]{2,1,0:T(8,128)(2,1)S(1)} collective-permute-done((bf16[1,256,1024]{2,1,0:T(8,128)(2,1)S(1)}, bf16[1,256,1024]{2,1,0:T(8,128)(2,1)S(1)}, u32[]{:S(2)}, u32[]{:S(2)}) %collective-permute-start.6) | collective-permute-done | bytes 524320 | tf_op jit(solution)/shard_map/ppermute | solution.py:20
  111.8 10.8 %convolution_convert_fusion.4 = bf16[1088,1536]{1,0:T(8,128)(2,1)S(1)} fusion(bf16[1088,2048]{1,0:T(8,128)(2,1)} %bitcast.391, bf16[2048,1536]{1,0:T(8,128)(2,1)} %all-gather.8.cloned.1.call-done), kind=kOutput, calls=%fused_computation.5 | convolution fusion | flops 6846775296 | bytes 14090240 | tf_op jit(solution)/shard_map/dot_general | solution.py:638
  122.6 13.3 %collective-permute-done.8 = bf16[2,1,256,1024]{3,2,0,1:T(8,128)(2,1)} collective-permute-done((bf16[2,1,256,1024]{3,2,0,1:T(8,128)(2,1)S(1)}, bf16[2,1,256,1024]{3,2,0,1:T(8,128)(2,1)}, u32[]{:S(2)}, u32[]{:S(2)}) %collective-permute-start.8) | collective-permute-done | bytes 1048608 | tf_op jit(solution)/shard_map/ppermute | solution.py:20
  165.1 7.1 %collective-permute-start.18 = (bf16[1,128,2048]{2,1,0:T(8,128)(2,1)S(1)}, bf16[1,128,2048]{2,1,0:T(8,128)(2,1)}, u32[]{:S(2)}, u32[]{:S(2)}) collective-permute-start(bf16[1,128,2048]{2,1,0:T(8,128)(2,1)S(1)} %get-tuple-element.643), channel_id=1, source_target_pairs={{0,1},{1,0},{2,3},{3,2},{4,5},{5,4},{6,7},{7,6},{8,9},{9,8},{10,11... | collective-permute-start | bytes 1572872 | tf_op jit(solution)/shard_map/ppermute | solution.py:20
  176.6 8.8 %shard_map.222 = bf16[4,2,1,128,512]{4,3,2,1,0:T(8,128)(2,1)} custom-call(s32[1]{0:T(128)} %bitcast.39.place_ref, bf16[4,2,1,128,512]{4,3,2,1,0:T(8,128)(2,1)} %fusion.49.signal_ref, f32[16,512]{1,0:T(8,128)} %maximum_bitcast_fusion.11.decay_ref, f32[16,512]{1,0:T(8,128)} %maximum_bitcast_fusion.12.residue_ref, f32[4,16,512]{2,1,0:T(8,128)} %multiply_add_fusion.2.start_ref), custom_call_target="tpu_custom_call" | custom-call | flops 33554432 | bytes 2293760 | tf_op jit(solution)/shard_map/pallas_call | solution.py:555
  216.9 20.9 %collective-permute-done.21 = bf16[1,128,2048]{2,1,0:T(8,128)(2,1)S(1)} collective-permute-done((bf16[1,128,2048]{2,1,0:T(8,128)(2,1)S(1)}, bf16[1,128,2048]{2,1,0:T(8,128)(2,1)S(1)}, u32[]{:S(2)}, u32[]{:S(2)}) %collective-permute-start.21) | collective-permute-done | bytes 524320 | tf_op jit(solution)/shard_map/ppermute | solution.py:20
  245.1 12.2 %fusion.122 = f32[1024,1408]{1,0:T(8,128)} fusion(bf16[1024,2048]{1,0:T(8,128)(2,1)} %bitcast.401, bf16[1408,2048]{1,0:T(8,128)(2,1)} %all-gather.10.cloned.1.call-done), kind=kOutput, calls=%fused_computation.421 | convolution fusion | flops 5905580032 | bytes 15728640 | tf_op jit(solution)/shard_map/dot_general | solution.py:642
  257.4 10.6 %collective-permute-done.23 = bf16[2,1,128,2048]{3,2,0,1:T(8,128)(2,1)S(1)} collective-permute-done((bf16[2,1,128,2048]{3,2,0,1:T(8,128)(2,1)}, bf16[2,1,128,2048]{3,2,0,1:T(8,128)(2,1)S(1)}, u32[]{:S(2)}, u32[]{:S(2)}) %collective-permute-start.23) | collective-permute-done | bytes 1048608 | tf_op jit(solution)/shard_map/ppermute | solution.py:20
  272.0 13.3 %multiply_convert_fusion.2 = (bf16[1024,1408]{1,0:T(8,128)(2,1)S(1)}, f32[1024,1408]{1,0:T(8,128)}) fusion(f32[1024,1408]{1,0:T(8,128)} %fusion.122, bf16[1024,2048]{1,0:T(8,128)(2,1)} %bitcast.403, bf16[2048,1408]{1,0:T(8,128)(2,1)} %all-gather.14.cloned.1.call-done), kind=kOutput, calls=%fused_computation.10 | convolution fusion | flops 5914230784 | bytes 24379392 | tf_op jit(solution)/shard_map/dot_general | solution.py:638
  286.9 8.7 %convolution_convert_fusion.3 = bf16[2048,1408]{1,0:T(8,128)(2,1)} fusion(bf16[1024,2048]{1,0:T(8,128)(2,1)S(1)} %bitcast.405, bf16[1024,1408]{1,0:T(8,128)(2,1)S(1)} %get-tuple-element.714), kind=kOutput, calls=%fused_computation.4 | convolution fusion | flops 5908463616 | bytes 12845056 | tf_op jit(solution)/shard_map/dot_general | solution.py:646
  295.6 15.2 %multiply_convert_fusion = (bf16[1024,1408]{1,0:T(8,128)(2,1)S(1)}, bf16[1024,1408]{1,0:T(8,128)(2,1)}) fusion(f32[1024,1408]{1,0:T(8,128)} %get-tuple-element.704, f32[1024,1408]{1,0:T(8,128)} %fusion.122, bf16[1024,2048]{1,0:T(8,128)(2,1)} %bitcast.404, bf16[2048,1408]{1,0:T(8,128)(2,1)} %all-gather.12.cloned.1.call-done), kind=kOutput, calls=%fused_computation.7 | convolution fusion | flops 5924323328 | bytes 27262976 | tf_op jit(solution)/shard_map/dot_general | solution.py:638
  312.4 8.9 %fusion.123 = f32[1024,2048]{1,0:T(8,128)S(1)} fusion(bf16[1024,1408]{1,0:T(8,128)(2,1)S(1)} %get-tuple-element.723, bf16[2048,1408]{1,0:T(8,128)(2,1)} %all-gather.14.cloned.1.call-done), kind=kOutput, calls=%fused_computation.422 | convolution fusion | flops 5905580032 | bytes 17039360 | tf_op jit(solution)/shard_map/dot_general | solution.py:642
  321.4 8.4 %add_convert_fusion = bf16[1024,2048]{1,0:T(8,128)(2,1)S(1)} fusion(f32[1024,2048]{1,0:T(8,128)S(1)} %fusion.123, bf16[1024,1408]{1,0:T(8,128)(2,1)} %copy-done.71, bf16[2048,1408]{1,0:T(8,128)(2,1)S(1)} %copy-done.67), kind=kOutput, calls=%fused_computation | convolution fusion | flops 5909774336 | bytes 21233664 | tf_op jit(solution)/shard_map/dot_general | solution.py:642
  335.1 8.7 %convolution_convert_fusion.2 = bf16[2048,1408]{1,0:T(8,128)(2,1)} fusion(bf16[1024,2048]{1,0:T(8,128)(2,1)S(1)} %bitcast.406, bf16[1024,1408]{1,0:T(8,128)(2,1)S(1)} %copy-done.70), kind=kOutput, calls=%fused_computation.3 | convolution fusion | flops 5908463616 | bytes 12845056 | tf_op jit(solution)/shard_map/dot_general | solution.py:646
  343.9 11.6 %collective-permute-done.27 = bf16[2,128,2048]{2,1,0:T(8,128)(2,1)} collective-permute-done((bf16[2,128,2048]{2,1,0:T(8,128)(2,1)}, bf16[2,128,2048]{2,1,0:T(8,128)(2,1)}, u32[]{:S(2)}, u32[]{:S(2)}) %collective-permute-start.27) | collective-permute-done | bytes 1048608 | tf_op jit(solution)/shard_map/ppermute | solution.py:20
  361.0 9.1 %convolution_convert_fusion.6 = bf16[1024,2048]{1,0:T(8,128)(2,1)S(1)} fusion(bf16[1024,1408]{1,0:T(8,128)(2,1)S(1)} %copy-done.68, bf16[1408,2048]{1,0:T(8,128)(2,1)} %all-gather.10.cloned.1.call-done), kind=kOutput, calls=%fused_computation.26 | convolution fusion | flops 5907677184 | bytes 12845056 | tf_op jit(solution)/shard_map/dot_general | solution.py:638
  374.7 6.1 collective-permute-done.31
  397.2 8.1 %convolution_convert_fusion.1 = bf16[1408,2048]{1,0:T(8,128)(2,1)} fusion(bf16[1024,1408]{1,0:T(8,128)(2,1)S(1)} %copy-done.68, bf16[1024,2048]{1,0:T(8,128)(2,1)S(1)} %bitcast.402), kind=kOutput, calls=%fused_computation.2 | convolution fusion | flops 5908463616 | bytes 12845056 | tf_op jit(solution)/shard_map/dot_general | solution.py:646
  429.0 11.3 %collective-permute-start.41 = (bf16[256,1408]{1,0:T(8,128)(2,1)}, bf16[256,1408]{1,0:T(8,128)(2,1)S(1)}, u32[]{:S(2)}, u32[]{:S(2)}) collective-permute-start(bf16[256,1408]{1,0:T(8,128)(2,1)} %reduce-scatter.8.cloned.1.call-done), channel_id=1, source_target_pairs={{8,1},{1,8},{10,3},{3,10},{12,5},{5,12},{14,7},{7,14},{24,17},{17,... | collective-permute-start | bytes 2162696 | tf_op jit(solution)/shard_map/ppermute | solution.py:262
  446.3 16.8 %shard_map.224 = (bf16[4,2,1,128,512]{4,3,2,1,0:T(8,128)(2,1)}, f32[16,512]{1,0:T(8,128)}, f32[16,512]{1,0:T(8,128)}) custom-call(s32[1]{0:T(128)} %bitcast.39.place_ref, bf16[4,2,1,128,512]{4,3,2,1,0:T(8,128)(2,1)} %fusion.49.signal_ref, bf16[4,2,1,128,512]{4,3,2,1,0:T(8,128)(2,1)} %get-tuple-element.798.signal_ref.grad_ref, ...), custom_call_target="tpu_custom_call" | custom-call | flops 100663296 | bytes 4521984 | tf_op jit(solution)/shard_map/pallas_call | solution.py:555
  475.6 10.4 %convolution_convert_fusion = bf16[2048,1536]{1,0:T(8,128)(2,1)} fusion(bf16[1088,2048]{1,0:T(8,128)(2,1)S(1)} %bitcast.394, bf16[1088,1024]{1,0:T(8,128)(2,1)S(1)} %bitcast.382, bf16[1088,512]{1,0:T(8,128)(2,1)S(1)} %bitcast.390), kind=kOutput, calls=%fused_computation.1 | convolution fusion | flops 6854934528 | bytes 14090240 | tf_op jit(solution)/shard_map/dot_general | solution.py:646
  490.5 21.2 %collective-permute-done.29 = bf16[2,128,2048]{2,1,0:T(8,128)(2,1)} collective-permute-done((bf16[2,128,2048]{2,1,0:T(8,128)(2,1)}, bf16[2,128,2048]{2,1,0:T(8,128)(2,1)}, u32[]{:S(2)}, u32[]{:S(2)}) %collective-permute-start.29) | collective-permute-done | bytes 1048608 | tf_op jit(solution)/shard_map/ppermute | solution.py:20
  520.3 9.5 %convolution_convert_fusion.5 = bf16[1088,2048]{1,0:T(8,128)(2,1)S(1)} fusion(bf16[1088,1536]{1,0:T(8,128)(2,1)S(1)} %copy-done.29, bf16[2048,1536]{1,0:T(8,128)(2,1)} %all-gather.8.cloned.1.call-done), kind=kOutput, calls=%fused_computation.6 | convolution fusion | flops 6847332352 | bytes 14090240 | tf_op jit(solution)/shard_map/dot_general | solution.py:642
  560.2 5.9 shard_map.225
  568.8 16.3 %collective-permute-done.48 = bf16[2,136,2048]{2,1,0:T(8,128)(2,1)} collective-permute-done((bf16[2,136,2048]{2,1,0:T(8,128)(2,1)}, bf16[2,136,2048]{2,1,0:T(8,128)(2,1)}, u32[]{:S(2)}, u32[]{:S(2)}) %collective-permute-start.48) | collective-permute-done | bytes 1114144 | tf_op jit(solution)/shard_map/ppermute | solution.py:20
  593.2 5.8 shard_map.226
  599.1 7.0 collective-permute-done.52
  617.6 7.1 %collective-permute-done.56 = bf16[256,1536]{1,0:T(8,128)(2,1)S(1)} collective-permute-done((bf16[256,1536]{1,0:T(8,128)(2,1)S(1)}, bf16[256,1536]{1,0:T(8,128)(2,1)S(1)}, u32[]{:S(2)}, u32[]{:S(2)}) %collective-permute-start.56) | collective-permute-done | bytes 786464 | tf_op jit(solution)/shard_map/ppermute | solution.py:262
  649.2 9.4 %collective-permute-done.59 = f32[49,512]{1,0:T(8,128)S(1)} collective-permute-done((f32[49,512]{1,0:T(8,128)S(1)}, f32[49,512]{1,0:T(8,128)S(1)}, u32[]{:S(2)}, u32[]{:S(2)}) %collective-permute-start.59) | collective-permute-done | bytes 100384 | tf_op jit(solution)/shard_map/ppermute | solution.py:20
  661.4 5.9 shard_map.227
  (537 shorter events, 341.9 us)
Async XLA Ops:
  7.2 31.8 %all-gather.6.cloned.1.call-start = ((), (), s32[]{:S(2)}) async-start(), calls=%async_computation.5 | async-start | bytes 1310720 | tf_op jit(solution)/shard_map/all_gather | solution.py:679
  9.3 102.5 %all-gather.8.cloned.1.call-start = ((), (), s32[]{:S(2)}) async-start(), calls=%async_computation.6 | async-start | bytes 7077888 | tf_op jit(solution)/shard_map/all_gather | solution.py:233
  41.3 203.1 %all-gather.10.cloned.1.call-start = ((), (), s32[]{:S(2)}) async-start(), calls=%async_computation.7 | async-start | bytes 6488064 | tf_op jit(solution)/shard_map/all_gather | solution.py:233
  61.4 210.6 %all-gather.14.cloned.1.call-start = ((), (), s32[]{:S(2)}) async-start(), calls=%async_computation.9 | async-start | bytes 6488064 | tf_op jit(solution)/shard_map/all_gather | solution.py:233
  61.5 24.4 %collective-permute-start.4 = (bf16[2,1,136,2048]{3,2,0,1:T(8,128)(2,1)}, bf16[2,1,136,2048]{3,2,0,1:T(8,128)(2,1)S(1)}, u32[]{:S(2)}, u32[]{:S(2)}) collective-permute-start(bf16[2,1,136,2048]{3,2,0,1:T(8,128)(2,1)} %bitcast.397), channel_id=1, source_target_pairs={{0,16},{16,0},{1,17},{17,1},{2,18},{18,2},{3,19},{19,3},{4,20},{20... | collective-permute-start | bytes 3342344 | tf_op jit(solution)/shard_map/ppermute | solution.py:20
  63.5 81.4 %collective-permute-start.13 = (bf16[256,1408]{1,0:T(8,128)(2,1)}, bf16[256,1408]{1,0:T(8,128)(2,1)}, u32[]{:S(2)}, u32[]{:S(2)}) collective-permute-start(bf16[256,1408]{1,0:T(8,128)(2,1)} %concatenate.265), channel_id=1, source_target_pairs={{0,1},{9,8},{2,3},{11,10},{4,5},{13,12},{6,7},{15,14},{16,17},{25,... | collective-permute-start | bytes 2162696 | tf_op jit(solution)/shard_map/ppermute | solution.py:192
  74.3 33.9 %collective-permute-start.6 = (bf16[1,256,1024]{2,1,0:T(8,128)(2,1)S(1)}, bf16[1,256,1024]{2,1,0:T(8,128)(2,1)S(1)}, u32[]{:S(2)}, u32[]{:S(2)}) collective-permute-start(bf16[1,256,1024]{2,1,0:T(8,128)(2,1)S(1)} %get-tuple-element.574), channel_id=1, source_target_pairs={{0,1},{1,0},{2,3},{3,2},{4,5},{5,4},{6,7},{7,6},{8,9},{9,8},{10,11... | collective-permute-start | bytes 1572872 | tf_op jit(solution)/shard_map/ppermute | solution.py:20
  77.2 31.0 %collective-permute-start.7 = (bf16[1,256,1024]{2,1,0:T(8,128)(2,1)S(1)}, bf16[1,256,1024]{2,1,0:T(8,128)(2,1)S(1)}, u32[]{:S(2)}, u32[]{:S(2)}) collective-permute-start(bf16[1,256,1024]{2,1,0:T(8,128)(2,1)S(1)} %get-tuple-element.576), channel_id=1, source_target_pairs={{0,16},{16,0},{1,17},{17,1},{2,18},{18,2},{3,19},{19,3},{4,20},{20... | collective-permute-start | bytes 1572872 | tf_op jit(solution)/shard_map/ppermute | solution.py:20
  111.5 24.4 %collective-permute-start.8 = (bf16[2,1,256,1024]{3,2,0,1:T(8,128)(2,1)S(1)}, bf16[2,1,256,1024]{3,2,0,1:T(8,128)(2,1)}, u32[]{:S(2)}, u32[]{:S(2)}) collective-permute-start(bf16[2,1,256,1024]{3,2,0,1:T(8,128)(2,1)S(1)} %bitcast.413), channel_id=1, source_target_pairs={{0,16},{16,0},{1,17},{17,1},{2,18},{18,2},{3,19},{19,3},{4,20},{20... | collective-permute-start | bytes 3145736 | tf_op jit(solution)/shard_map/ppermute | solution.py:20
  111.8 24.9 %collective-permute-start.9 = (bf16[2,1,256,1024]{3,2,0,1:T(8,128)(2,1)S(1)}, bf16[2,1,256,1024]{3,2,0,1:T(8,128)(2,1)}, u32[]{:S(2)}, u32[]{:S(2)}) collective-permute-start(bf16[2,1,256,1024]{3,2,0,1:T(8,128)(2,1)S(1)} %pad_maximum_fusion.19), channel_id=1, source_target_pairs={{0,1},{1,0},{2,3},{3,2},{4,5},{5,4},{6,7},{7,6},{8,9},{9,8},{10,11... | collective-permute-start | bytes 3145736 | tf_op jit(solution)/shard_map/ppermute | solution.py:20
  147.2 148.4 %all-gather.12.cloned.1.call-start = ((), (), s32[]{:S(2)}) async-start(), calls=%async_computation.8 | async-start | bytes 6488064 | tf_op jit(solution)/shard_map/all_gather | solution.py:233
  153.1 52.0 %collective-permute-start.17 = (bf16[2048,1024]{1,0:T(8,128)(2,1)}, bf16[2048,1024]{1,0:T(8,128)(2,1)}, u32[]{:S(2)}, u32[]{:S(2)}) collective-permute-start(bf16[2048,1024]{1,0:T(8,128)(2,1)} %bitcast.52), channel_id=1, source_target_pairs={{0,8},{8,0},{1,9},{9,1},{2,10},{10,2},{3,11},{11,3},{4,12},{12,4},... | collective-permute-start | bytes 12582920 | tf_op jit(solution)/shard_map/ppermute | solution.py:20
  153.2 36.2 %collective-permute-start.20 = (bf16[256,1408]{1,0:T(8,128)(2,1)}, bf16[256,1408]{1,0:T(8,128)(2,1)S(1)}, u32[]{:S(2)}, u32[]{:S(2)}) collective-permute-start(bf16[256,1408]{1,0:T(8,128)(2,1)} %concatenate.267), channel_id=1, source_target_pairs={{0,1},{9,8},{2,3},{11,10},{4,5},{13,12},{6,7},{15,14},{16,17},{25,... | collective-permute-start | bytes 2162696 | tf_op jit(solution)/shard_map/ppermute | solution.py:192
  165.1 28.0 %collective-permute-start.18 = (bf16[1,128,2048]{2,1,0:T(8,128)(2,1)S(1)}, bf16[1,128,2048]{2,1,0:T(8,128)(2,1)}, u32[]{:S(2)}, u32[]{:S(2)}) collective-permute-start(bf16[1,128,2048]{2,1,0:T(8,128)(2,1)S(1)} %get-tuple-element.643), channel_id=1, source_target_pairs={{0,1},{1,0},{2,3},{3,2},{4,5},{5,4},{6,7},{7,6},{8,9},{9,8},{10,11... | collective-permute-start | bytes 1572872 | tf_op jit(solution)/shard_map/ppermute | solution.py:20
  193.1 234.3 %reduce-scatter.8.cloned.1.call-start = ((), (), s32[]{:S(2)}) async-start(), calls=%async_computation.11 | async-start | bytes 6488064 | tf_op jit(solution)/shard_map/reduce_scatter | solution.py:237
  196.6 45.1 %collective-permute-start.25 = (bf16[2,1,128,2048]{3,2,0,1:T(8,128)(2,1)S(1)}, bf16[2,1,128,2048]{3,2,0,1:T(8,128)(2,1)S(1)}, u32[]{:S(2)}, u32[]{:S(2)}) collective-permute-start(bf16[2,1,128,2048]{3,2,0,1:T(8,128)(2,1)S(1)} %bitcast.416), channel_id=1, source_target_pairs={{0,16},{16,0},{1,17},{17,1},{2,18},{18,2},{3,19},{19,3},{4,20},{20... | collective-permute-start | bytes 3145736 | tf_op jit(solution)/shard_map/ppermute | solution.py:20
  198.5 43.2 %collective-permute-start.26 = (bf16[2,1,128,2048]{3,2,0,1:T(8,128)(2,1)S(1)}, bf16[2,1,128,2048]{3,2,0,1:T(8,128)(2,1)S(1)}, u32[]{:S(2)}, u32[]{:S(2)}) collective-permute-start(bf16[2,1,128,2048]{3,2,0,1:T(8,128)(2,1)S(1)} %pad_maximum_fusion.21), channel_id=1, source_target_pairs={{0,1},{1,0},{2,3},{3,2},{4,5},{5,4},{6,7},{7,6},{8,9},{9,8},{10,11... | collective-permute-start | bytes 3145736 | tf_op jit(solution)/shard_map/ppermute | solution.py:20
  295.6 133.5 %reduce-scatter.6.cloned.1.call-start = ((), (), s32[]{:S(2)}) async-start(), calls=%async_computation.10 | async-start | bytes 6488064 | tf_op jit(solution)/shard_map/reduce_scatter | solution.py:237
  343.8 255.2 %reduce-scatter.10.cloned.1.call-start = ((), (), s32[]{:S(2)}) async-start(), calls=%async_computation.12 | async-start | bytes 7077888 | tf_op jit(solution)/shard_map/reduce_scatter | solution.py:237
  425.1 41.1 %collective-permute-start.42 = (bf16[2,1,128,2048]{3,2,0,1:T(8,128)(2,1)}, bf16[2,1,128,2048]{3,2,0,1:T(8,128)(2,1)}, u32[]{:S(2)}, u32[]{:S(2)}) collective-permute-start(bf16[2,1,128,2048]{3,2,0,1:T(8,128)(2,1)} %pad_maximum_fusion.24), channel_id=1, source_target_pairs={{0,16},{16,0},{1,17},{17,1},{2,18},{18,2},{3,19},{19,3},{4,20},{20... | collective-permute-start | bytes 3145736 | tf_op jit(solution)/shard_map/ppermute | solution.py:20
  426.0 40.3 %collective-permute-start.43 = (bf16[2,1,128,2048]{3,2,0,1:T(8,128)(2,1)}, bf16[2,1,128,2048]{3,2,0,1:T(8,128)(2,1)}, u32[]{:S(2)}, u32[]{:S(2)}) collective-permute-start(bf16[2,1,128,2048]{3,2,0,1:T(8,128)(2,1)} %bitcast.144), channel_id=1, source_target_pairs={{0,1},{1,0},{2,3},{3,2},{4,5},{5,4},{6,7},{7,6},{8,9},{9,8},{10,11... | collective-permute-start | bytes 3145736 | tf_op jit(solution)/shard_map/ppermute | solution.py:20
  429.0 37.2 %collective-permute-start.41 = (bf16[256,1408]{1,0:T(8,128)(2,1)}, bf16[256,1408]{1,0:T(8,128)(2,1)S(1)}, u32[]{:S(2)}, u32[]{:S(2)}) collective-permute-start(bf16[256,1408]{1,0:T(8,128)(2,1)} %reduce-scatter.8.cloned.1.call-done), channel_id=1, source_target_pairs={{8,1},{1,8},{10,3},{3,10},{12,5},{5,12},{14,7},{7,14},{24,17},{17,... | collective-permute-start | bytes 2162696 | tf_op jit(solution)/shard_map/ppermute | solution.py:262
  486.1 138.9 %reduce-scatter.12.cloned.1.call-start = ((), (), s32[]{:S(2)}) async-start(), calls=%async_computation.13 | async-start | bytes 6488064 | tf_op jit(solution)/shard_map/reduce_scatter | solution.py:237
  486.1 25.6 %collective-permute-start.29 = (bf16[2,128,2048]{2,1,0:T(8,128)(2,1)}, bf16[2,128,2048]{2,1,0:T(8,128)(2,1)}, u32[]{:S(2)}, u32[]{:S(2)}) collective-permute-start(bf16[2,128,2048]{2,1,0:T(8,128)(2,1)} %get-tuple-element.736), channel_id=1, source_target_pairs={{0,1},{1,0},{2,3},{3,2},{4,5},{5,4},{6,7},{7,6},{8,9},{9,8},{10,11... | collective-permute-start | bytes 3145736 | tf_op jit(solution)/shard_map/ppermute | solution.py:20
  486.2 25.5 %collective-permute-start.30 = (bf16[2,128,2048]{2,1,0:T(8,128)(2,1)}, bf16[2,128,2048]{2,1,0:T(8,128)(2,1)}, u32[]{:S(2)}, u32[]{:S(2)}) collective-permute-start(bf16[2,128,2048]{2,1,0:T(8,128)(2,1)} %bitcast.444), channel_id=1, source_target_pairs={{0,16},{16,0},{1,17},{17,1},{2,18},{18,2},{3,19},{19,3},{4,20},{20... | collective-permute-start | bytes 3145736 | tf_op jit(solution)/shard_map/ppermute | solution.py:20
  488.1 181.1 %reduce-scatter.14.cloned.1.call-start = ((), (), s32[]{:S(2)}) async-start(), calls=%async_computation.14 | async-start | bytes 2359296 | tf_op jit(solution)/shard_map/reduce_scatter | solution.py:237
  488.1 31.0 %collective-permute-start.46 = (bf16[256,1408]{1,0:T(8,128)(2,1)}, bf16[256,1408]{1,0:T(8,128)(2,1)S(1)}, u32[]{:S(2)}, u32[]{:S(2)}) collective-permute-start(bf16[256,1408]{1,0:T(8,128)(2,1)} %reduce-scatter.6.cloned.1.call-done), channel_id=1, source_target_pairs={{8,1},{1,8},{10,3},{3,10},{12,5},{5,12},{14,7},{7,14},{24,17},{17,... | collective-permute-start | bytes 2162696 | tf_op jit(solution)/shard_map/ppermute | solution.py:262
  518.9 26.9 %collective-permute-start.50 = (bf16[1,256,1408]{2,1,0:T(8,128)(2,1)S(1)}, bf16[1,256,1408]{2,1,0:T(8,128)(2,1)}, u32[]{:S(2)}, u32[]{:S(2)}) collective-permute-start(bf16[1,256,1408]{2,1,0:T(8,128)(2,1)S(1)} %fusion.67), channel_id=1, source_target_pairs={{0,16},{16,0},{1,17},{17,1},{2,18},{18,2},{3,19},{19,3},{4,20},{20... | collective-permute-start | bytes 2162696 | tf_op jit(solution)/shard_map/ppermute | solution.py:20
  533.3 32.8 %collective-permute-start.49 = (bf16[1,256,1408]{2,1,0:T(8,128)(2,1)}, bf16[1,256,1408]{2,1,0:T(8,128)(2,1)}, u32[]{:S(2)}, u32[]{:S(2)}) collective-permute-start(bf16[1,256,1408]{2,1,0:T(8,128)(2,1)} %fusion.66), channel_id=1, source_target_pairs={{0,16},{16,0},{1,17},{17,1},{2,18},{18,2},{3,19},{19,3},{4,20},{20... | collective-permute-start | bytes 2162696 | tf_op jit(solution)/shard_map/ppermute | solution.py:20
  534.5 34.3 %collective-permute-start.47 = (bf16[2,136,2048]{2,1,0:T(8,128)(2,1)}, bf16[2,136,2048]{2,1,0:T(8,128)(2,1)}, u32[]{:S(2)}, u32[]{:S(2)}) collective-permute-start(bf16[2,136,2048]{2,1,0:T(8,128)(2,1)} %get-tuple-element.852), channel_id=1, source_target_pairs={{0,1},{1,0},{2,3},{3,2},{4,5},{5,4},{6,7},{7,6},{8,9},{9,8},{10,11... | collective-permute-start | bytes 3342344 | tf_op jit(solution)/shard_map/ppermute | solution.py:20
  535.4 49.7 %collective-permute-start.48 = (bf16[2,136,2048]{2,1,0:T(8,128)(2,1)}, bf16[2,136,2048]{2,1,0:T(8,128)(2,1)}, u32[]{:S(2)}, u32[]{:S(2)}) collective-permute-start(bf16[2,136,2048]{2,1,0:T(8,128)(2,1)} %bitcast.165), channel_id=1, source_target_pairs={{0,16},{16,0},{1,17},{17,1},{2,18},{18,2},{3,19},{19,3},{4,20},{20... | collective-permute-start | bytes 3342344 | tf_op jit(solution)/shard_map/ppermute | solution.py:20
  638.9 28.4 %collective-permute-start.63 = (bf16[1,176,2048]{2,1,0:T(8,128)(2,1)S(1)}, bf16[1,176,2048]{2,1,0:T(8,128)(2,1)S(1)}, u32[]{:S(2)}, u32[]{:S(2)}) collective-permute-start(bf16[1,176,2048]{2,1,0:T(8,128)(2,1)S(1)} %bitcast.461), channel_id=1, source_target_pairs={{0,16},{16,0},{1,17},{17,1},{2,18},{18,2},{3,19},{19,3},{4,20},{20... | collective-permute-start | bytes 2162696 | tf_op jit(solution)/shard_map/ppermute | solution.py:20
  (121 other events, 1306.4 us)
Sparse Core Ops, SparseCore 0:
  10.2 28.8 all-gather.5
  41.5 63.0 all-gather.7
  106.2 62.2 all-gather.9
  170.5 58.9 all-gather.13
  231.0 59.0 all-gather.11
  295.7 65.9 reduce-scatter.7
  364.5 64.5 reduce-scatter.5
  486.2 66.2 reduce-scatter.9
  554.8 62.9 reduce-scatter.11
  619.9 40.5 reduce-scatter.13

commit v15 on v14

--- a/solution.py
+++ b/solution.py
@@ -907,6 +907,8 @@
     mix_move.got = run(lambda got: got, mix_move.got)
     up_held = run(owner_held, up_parts_got)
     up_got = moved(up_held, "y", -1)
+    grad_mix_all = mix_move.end(line)
+    feed_back.got = run(lambda got: got, feed_back.got)
 
     def in_back(query, pair, weights, v):
         result = jnp.concatenate(
@@ -925,7 +927,6 @@
     gate_got = moved(gate_held, "y", -1)
     one_back = Scatter(run(lambda a, w: split_sum(dot_t(a, w, low)), grad_mixed, w_in))
     feed_back.got = run(lambda got: got, feed_back.got)
-    grad_mix_all = mix_move.end(line)
     out_mine = scatter_tile(run(dot_w, gated_all, grad_mix_all))
     up_held = run(stacked, up_held, up_got)
     up_got = moved(up_held, "c", -1)
@@ -949,6 +950,8 @@
     gate_held = run(stacked, gate_held, gate_got)
     gate_got = moved(gate_held, "c", -1)
     one_back.turn(line)
+    down_held = run(lambda v: v[None], down_mine)
+    down_got = moved(down_held, "y", -1)
     grad_gate_weight = run(column_whole, gate_held, gate_got)
     in_got = owner_moves(run(owner_parts, in_mine))
 
@@ -967,8 +970,6 @@
     )
     in_held = run(owner_held, in_got)
     in_got = moved(in_held, "y", -1)
-    down_held = run(lambda v: v[None], down_mine)
-    down_got = moved(down_held, "y", -1)
 
     def tokens_back(grad, extension, values, scale, gain, back, small):
         values = values.astype(wide)

time: 709 us -> 702 us (level)
  waiting for transfers between devices: 206 us -> 195 us
    ppermute x49, waiting for transfers between devices: 178 us -> 154 us  [turned(): lax.ppermute(value, axis, [(i, (i + by) % length) for i in range(length)])]
    ppermute x6, waiting for transfers between devices: 5.9 us -> 15.1 us  [swap_slots(): line.append(lax.ppermute(slots[sy][sx], ('y', 'x'), pairs))]
    unnamed x169 -> x167, local copies, waits for them, and re-layouts: 20.9 us -> 20.7 us
  transfers between devices with their start and end apart: 79 -> 79, of which waited for: 36 -> 38; matrix products, arithmetic and copies ran while one was open for 41% -> 44% of each run, Pallas kernels for 8% -> 8%
where the time goes in v15:
time: 702 us; the launch traced here: 694 us
  waiting for transfers between devices  195 us (28%)
  matrix products  141 us (20%)
  other arithmetic  117 us (17%)
  starting transfers between devices  94.7 us (13%)
  local copies, waits for them, and re-layouts  74.2 us (11%)
  Pallas kernels  56.4 us (8%)
  between operations  16.6 us (2%)
    ppermute x49, waiting for transfers between devices, turned(): lax.ppermute(value, axis, [(i, (i + by) % length) for i in range(length)])  154 us
    dot_general x6, matrix products, dot(): return jnp.dot(a, b, preferred_element_type=wide).astype(kind)  55.3 us
    dot_general x6, matrix products, dot_t(): lax.dot_general(a, b, (((1,), (1,)), ((), ())), preferred_element_type=wide)  45.7 us
    ppermute x49, starting transfers between devices, turned(): lax.ppermute(value, axis, [(i, (i + by) % length) for i in range(length)])  45.1 us
    dot_general x5, matrix products, dot_w(): lax.dot_general(a, b, (((0,), (0,)), ((), ())), preferred_element_type=wide)  39.7 us
    pallas_call x4, Pallas kernels, conv_call(): pl.pallas_call(kernel, out_shape=results, grid_spec=pltpu.PrefetchScalarG...  35.3 us
    ppermute x3, starting transfers between devices, owner_moves(): got.append(lax.ppermute(parts[d], ('c', 'x'), pairs))  23.2 us
    unnamed x167, local copies, waits for them, and re-layouts  20.7 us
  transfers between devices with their start and end apart: 79, of which 38 were waited for; matrix products, arithmetic and copies ran while one was open for 44% of the time, Pallas kernels for 8%

profile of v15, /device:TPU:9, one launch (start us, length us, event | category | flops | bytes accessed | tf_op | source)
XLA Modules:
  0.0 694.4 jit_solution(14412915723932094316)
XLA Ops:
  33.7 5.3 all-gather.6.cloned.1.call-done
  43.9 10.9 %collective-permute-done.1 = bf16[1,136,2048]{2,1,0:T(8,128)(2,1)} collective-permute-done((bf16[1,136,2048]{2,1,0:T(8,128)(2,1)S(1)}, bf16[1,136,2048]{2,1,0:T(8,128)(2,1)}, u32[]{:S(2)}, u32[]{:S(2)}) %collective-permute-start.1) | collective-permute-done | bytes 557088 | tf_op jit(solution)/shard_map/ppermute | solution.py:20
  77.5 8.3 %collective-permute-done.4 = bf16[2,1,136,2048]{3,2,0,1:T(8,128)(2,1)S(1)} collective-permute-done((bf16[2,1,136,2048]{3,2,0,1:T(8,128)(2,1)}, bf16[2,1,136,2048]{3,2,0,1:T(8,128)(2,1)S(1)}, u32[]{:S(2)}, u32[]{:S(2)}) %collective-permute-start.4) | collective-permute-done | bytes 1114144 | tf_op jit(solution)/shard_map/ppermute | solution.py:20
  92.6 15.6 %collective-permute-done.6 = bf16[1,256,1024]{2,1,0:T(8,128)(2,1)S(1)} collective-permute-done((bf16[1,256,1024]{2,1,0:T(8,128)(2,1)S(1)}, bf16[1,256,1024]{2,1,0:T(8,128)(2,1)S(1)}, u32[]{:S(2)}, u32[]{:S(2)}) %collective-permute-start.6) | collective-permute-done | bytes 524320 | tf_op jit(solution)/shard_map/ppermute | solution.py:20
  111.8 10.8 %convolution_convert_fusion.4 = bf16[1088,1536]{1,0:T(8,128)(2,1)S(1)} fusion(bf16[1088,2048]{1,0:T(8,128)(2,1)} %bitcast.391, bf16[2048,1536]{1,0:T(8,128)(2,1)} %all-gather.8.cloned.1.call-done), kind=kOutput, calls=%fused_computation.5 | convolution fusion | flops 6846775296 | bytes 14090240 | tf_op jit(solution)/shard_map/dot_general | solution.py:638
  122.6 13.3 %collective-permute-done.8 = bf16[2,1,256,1024]{3,2,0,1:T(8,128)(2,1)} collective-permute-done((bf16[2,1,256,1024]{3,2,0,1:T(8,128)(2,1)S(1)}, bf16[2,1,256,1024]{3,2,0,1:T(8,128)(2,1)}, u32[]{:S(2)}, u32[]{:S(2)}) %collective-permute-start.8) | collective-permute-done | bytes 1048608 | tf_op jit(solution)/shard_map/ppermute | solution.py:20
  168.1 5.1 collective-permute-done.11
  176.6 8.8 %shard_map.222 = bf16[4,2,1,128,512]{4,3,2,1,0:T(8,128)(2,1)} custom-call(s32[1]{0:T(128)} %bitcast.39.place_ref, bf16[4,2,1,128,512]{4,3,2,1,0:T(8,128)(2,1)} %fusion.49.signal_ref, f32[16,512]{1,0:T(8,128)} %maximum_bitcast_fusion.11.decay_ref, f32[16,512]{1,0:T(8,128)} %maximum_bitcast_fusion.12.residue_ref, f32[4,16,512]{2,1,0:T(8,128)} %multiply_add_fusion.2.start_ref), custom_call_target="tpu_custom_call" | custom-call | flops 33554432 | bytes 2293760 | tf_op jit(solution)/shard_map/pallas_call | solution.py:555
  216.9 21.0 %collective-permute-done.21 = bf16[1,128,2048]{2,1,0:T(8,128)(2,1)S(1)} collective-permute-done((bf16[1,128,2048]{2,1,0:T(8,128)(2,1)S(1)}, bf16[1,128,2048]{2,1,0:T(8,128)(2,1)S(1)}, u32[]{:S(2)}, u32[]{:S(2)}) %collective-permute-start.21) | collective-permute-done | bytes 524320 | tf_op jit(solution)/shard_map/ppermute | solution.py:20
  245.1 12.0 %fusion.122 = f32[1024,1408]{1,0:T(8,128)} fusion(bf16[1024,2048]{1,0:T(8,128)(2,1)} %bitcast.401, bf16[1408,2048]{1,0:T(8,128)(2,1)} %all-gather.10.cloned.1.call-done), kind=kOutput, calls=%fused_computation.421 | convolution fusion | flops 5905580032 | bytes 15728640 | tf_op jit(solution)/shard_map/dot_general | solution.py:642
  257.1 11.0 %collective-permute-done.23 = bf16[2,1,128,2048]{3,2,0,1:T(8,128)(2,1)S(1)} collective-permute-done((bf16[2,1,128,2048]{3,2,0,1:T(8,128)(2,1)}, bf16[2,1,128,2048]{3,2,0,1:T(8,128)(2,1)S(1)}, u32[]{:S(2)}, u32[]{:S(2)}) %collective-permute-start.23) | collective-permute-done | bytes 1048608 | tf_op jit(solution)/shard_map/ppermute | solution.py:20
  272.2 13.3 %multiply_convert_fusion.2 = (bf16[1024,1408]{1,0:T(8,128)(2,1)S(1)}, f32[1024,1408]{1,0:T(8,128)}) fusion(f32[1024,1408]{1,0:T(8,128)} %fusion.122, bf16[1024,2048]{1,0:T(8,128)(2,1)} %bitcast.404, bf16[2048,1408]{1,0:T(8,128)(2,1)} %all-gather.14.cloned.1.call-done), kind=kOutput, calls=%fused_computation.10 | convolution fusion | flops 5914230784 | bytes 24379392 | tf_op jit(solution)/shard_map/dot_general | solution.py:638
  287.0 8.7 %convolution_convert_fusion.3 = bf16[2048,1408]{1,0:T(8,128)(2,1)} fusion(bf16[1024,2048]{1,0:T(8,128)(2,1)S(1)} %bitcast.406, bf16[1024,1408]{1,0:T(8,128)(2,1)S(1)} %get-tuple-element.717), kind=kOutput, calls=%fused_computation.4 | convolution fusion | flops 5908463616 | bytes 12845056 | tf_op jit(solution)/shard_map/dot_general | solution.py:646
  295.7 15.2 %multiply_convert_fusion = (bf16[1024,1408]{1,0:T(8,128)(2,1)S(1)}, bf16[1024,1408]{1,0:T(8,128)(2,1)}) fusion(f32[1024,1408]{1,0:T(8,128)} %get-tuple-element.707, f32[1024,1408]{1,0:T(8,128)} %fusion.122, bf16[1024,2048]{1,0:T(8,128)(2,1)} %bitcast.405, bf16[2048,1408]{1,0:T(8,128)(2,1)} %all-gather.12.cloned.1.call-done), kind=kOutput, calls=%fused_computation.7 | convolution fusion | flops 5924323328 | bytes 27262976 | tf_op jit(solution)/shard_map/dot_general | solution.py:638
  312.6 8.9 %fusion.123 = f32[1024,2048]{1,0:T(8,128)S(1)} fusion(bf16[1024,1408]{1,0:T(8,128)(2,1)S(1)} %get-tuple-element.726, bf16[2048,1408]{1,0:T(8,128)(2,1)} %all-gather.14.cloned.1.call-done), kind=kOutput, calls=%fused_computation.422 | convolution fusion | flops 5905580032 | bytes 17039360 | tf_op jit(solution)/shard_map/dot_general | solution.py:642
  321.5 8.4 %add_convert_fusion = bf16[1024,2048]{1,0:T(8,128)(2,1)S(1)} fusion(f32[1024,2048]{1,0:T(8,128)S(1)} %fusion.123, bf16[1024,1408]{1,0:T(8,128)(2,1)} %copy-done.70, bf16[2048,1408]{1,0:T(8,128)(2,1)S(1)} %copy-done.66), kind=kOutput, calls=%fused_computation | convolution fusion | flops 5909774336 | bytes 21233664 | tf_op jit(solution)/shard_map/dot_general | solution.py:642
  335.2 8.7 %convolution_convert_fusion.2 = bf16[2048,1408]{1,0:T(8,128)(2,1)} fusion(bf16[1024,2048]{1,0:T(8,128)(2,1)S(1)} %bitcast.407, bf16[1024,1408]{1,0:T(8,128)(2,1)S(1)} %copy-done.69), kind=kOutput, calls=%fused_computation.3 | convolution fusion | flops 5908463616 | bytes 12845056 | tf_op jit(solution)/shard_map/dot_general | solution.py:646
  343.9 11.8 %collective-permute-done.27 = bf16[2,128,2048]{2,1,0:T(8,128)(2,1)} collective-permute-done((bf16[2,128,2048]{2,1,0:T(8,128)(2,1)}, bf16[2,128,2048]{2,1,0:T(8,128)(2,1)}, u32[]{:S(2)}, u32[]{:S(2)}) %collective-permute-start.27) | collective-permute-done | bytes 1048608 | tf_op jit(solution)/shard_map/ppermute | solution.py:20
  361.0 9.1 %convolution_convert_fusion.6 = bf16[1024,2048]{1,0:T(8,128)(2,1)S(1)} fusion(bf16[1024,1408]{1,0:T(8,128)(2,1)S(1)} %copy-done.67, bf16[1408,2048]{1,0:T(8,128)(2,1)} %all-gather.10.cloned.1.call-done), kind=kOutput, calls=%fused_computation.26 | convolution fusion | flops 5907677184 | bytes 12845056 | tf_op jit(solution)/shard_map/dot_general | solution.py:638
  397.3 8.1 %convolution_convert_fusion.1 = bf16[1408,2048]{1,0:T(8,128)(2,1)} fusion(bf16[1024,1408]{1,0:T(8,128)(2,1)S(1)} %copy-done.67, bf16[1024,2048]{1,0:T(8,128)(2,1)S(1)} %bitcast.402), kind=kOutput, calls=%fused_computation.2 | convolution fusion | flops 5908463616 | bytes 12845056 | tf_op jit(solution)/shard_map/dot_general | solution.py:646
  437.7 17.0 %collective-permute-start.43 = (bf16[256,1408]{1,0:T(8,128)(2,1)}, bf16[256,1408]{1,0:T(8,128)(2,1)S(1)}, u32[]{:S(2)}, u32[]{:S(2)}) collective-permute-start(bf16[256,1408]{1,0:T(8,128)(2,1)} %reduce-scatter.8.cloned.1.call-done), channel_id=1, source_target_pairs={{8,1},{1,8},{10,3},{3,10},{12,5},{5,12},{14,7},{7,14},{24,17},{17,... | collective-permute-start | bytes 2162696 | tf_op jit(solution)/shard_map/ppermute | solution.py:262
  461.1 16.8 %shard_map.224 = (bf16[4,2,1,128,512]{4,3,2,1,0:T(8,128)(2,1)}, f32[16,512]{1,0:T(8,128)}, f32[16,512]{1,0:T(8,128)}) custom-call(s32[1]{0:T(128)} %bitcast.39.place_ref, bf16[4,2,1,128,512]{4,3,2,1,0:T(8,128)(2,1)} %fusion.49.signal_ref, bf16[4,2,1,128,512]{4,3,2,1,0:T(8,128)(2,1)} %get-tuple-element.802.signal_ref.grad_ref, ...), custom_call_target="tpu_custom_call" | custom-call | flops 100663296 | bytes 4521984 | tf_op jit(solution)/shard_map/pallas_call | solution.py:555
  495.1 10.5 %convolution_convert_fusion = bf16[2048,1536]{1,0:T(8,128)(2,1)} fusion(bf16[1088,2048]{1,0:T(8,128)(2,1)S(1)} %bitcast.394, bf16[1088,1024]{1,0:T(8,128)(2,1)S(1)} %bitcast.382, bf16[1088,512]{1,0:T(8,128)(2,1)S(1)} %bitcast.390), kind=kOutput, calls=%fused_computation.1 | convolution fusion | flops 6854934528 | bytes 14090240 | tf_op jit(solution)/shard_map/dot_general | solution.py:646
  515.6 5.9 collective-permute-done.46
  522.6 9.3 %convolution_convert_fusion.5 = bf16[1088,2048]{1,0:T(8,128)(2,1)S(1)} fusion(bf16[1088,1536]{1,0:T(8,128)(2,1)S(1)} %copy-done.32, bf16[2048,1536]{1,0:T(8,128)(2,1)} %all-gather.8.cloned.1.call-done), kind=kOutput, calls=%fused_computation.6 | convolution fusion | flops 6847332352 | bytes 14090240 | tf_op jit(solution)/shard_map/dot_general | solution.py:642
  556.2 5.8 shard_map.225
  564.7 15.1 %collective-permute-done.48 = bf16[2,136,2048]{2,1,0:T(8,128)(2,1)} collective-permute-done((bf16[2,136,2048]{2,1,0:T(8,128)(2,1)}, bf16[2,136,2048]{2,1,0:T(8,128)(2,1)}, u32[]{:S(2)}, u32[]{:S(2)}) %collective-permute-start.48) | collective-permute-done | bytes 1114144 | tf_op jit(solution)/shard_map/ppermute | solution.py:20
  585.8 5.8 shard_map.226
  591.6 7.3 %collective-permute-done.52 = bf16[136,2048]{1,0:T(8,128)(2,1)} collective-permute-done((bf16[136,2048]{1,0:T(8,128)(2,1)}, bf16[136,2048]{1,0:T(8,128)(2,1)}, u32[]{:S(2)}, u32[]{:S(2)}) %collective-permute-start.52) | collective-permute-done | bytes 557088 | tf_op jit(solution)/shard_map/ppermute | solution.py:20
  626.2 7.3 %collective-permute-done.61 = bf16[1,256,1536]{2,1,0:T(8,128)(2,1)} collective-permute-done((bf16[1,256,1536]{2,1,0:T(8,128)(2,1)S(1)}, bf16[1,256,1536]{2,1,0:T(8,128)(2,1)}, u32[]{:S(2)}, u32[]{:S(2)}) %collective-permute-start.61) | collective-permute-done | bytes 786464 | tf_op jit(solution)/shard_map/ppermute | solution.py:20
  643.3 5.4 collective-permute-done.59
  651.9 5.9 shard_map.227
  (535 shorter events, 351.6 us)
Async XLA Ops:
  7.2 31.8 %all-gather.6.cloned.1.call-start = ((), (), s32[]{:S(2)}) async-start(), calls=%async_computation.5 | async-start | bytes 1310720 | tf_op jit(solution)/shard_map/all_gather | solution.py:679
  9.3 102.5 %all-gather.8.cloned.1.call-start = ((), (), s32[]{:S(2)}) async-start(), calls=%async_computation.6 | async-start | bytes 7077888 | tf_op jit(solution)/shard_map/all_gather | solution.py:233
  41.3 203.2 %all-gather.10.cloned.1.call-start = ((), (), s32[]{:S(2)}) async-start(), calls=%async_computation.7 | async-start | bytes 6488064 | tf_op jit(solution)/shard_map/all_gather | solution.py:233
  61.4 210.8 %all-gather.14.cloned.1.call-start = ((), (), s32[]{:S(2)}) async-start(), calls=%async_computation.9 | async-start | bytes 6488064 | tf_op jit(solution)/shard_map/all_gather | solution.py:233
  61.5 24.4 %collective-permute-start.4 = (bf16[2,1,136,2048]{3,2,0,1:T(8,128)(2,1)}, bf16[2,1,136,2048]{3,2,0,1:T(8,128)(2,1)S(1)}, u32[]{:S(2)}, u32[]{:S(2)}) collective-permute-start(bf16[2,1,136,2048]{3,2,0,1:T(8,128)(2,1)} %bitcast.397), channel_id=1, source_target_pairs={{0,16},{16,0},{1,17},{17,1},{2,18},{18,2},{3,19},{19,3},{4,20},{20... | collective-permute-start | bytes 3342344 | tf_op jit(solution)/shard_map/ppermute | solution.py:20
  62.7 23.9 %collective-permute-start.5 = (bf16[2,1,136,2048]{3,2,0,1:T(8,128)(2,1)}, bf16[2,1,136,2048]{3,2,0,1:T(8,128)(2,1)S(1)}, u32[]{:S(2)}, u32[]{:S(2)}) collective-permute-start(bf16[2,1,136,2048]{3,2,0,1:T(8,128)(2,1)} %pad_maximum_fusion.17), channel_id=1, source_target_pairs={{0,1},{1,0},{2,3},{3,2},{4,5},{5,4},{6,7},{7,6},{8,9},{9,8},{10,11... | collective-permute-start | bytes 3342344 | tf_op jit(solution)/shard_map/ppermute | solution.py:20
  63.5 81.3 %collective-permute-start.13 = (bf16[256,1408]{1,0:T(8,128)(2,1)}, bf16[256,1408]{1,0:T(8,128)(2,1)}, u32[]{:S(2)}, u32[]{:S(2)}) collective-permute-start(bf16[256,1408]{1,0:T(8,128)(2,1)} %concatenate.265), channel_id=1, source_target_pairs={{0,1},{9,8},{2,3},{11,10},{4,5},{13,12},{6,7},{15,14},{16,17},{25,... | collective-permute-start | bytes 2162696 | tf_op jit(solution)/shard_map/ppermute | solution.py:192
  74.4 33.8 %collective-permute-start.6 = (bf16[1,256,1024]{2,1,0:T(8,128)(2,1)S(1)}, bf16[1,256,1024]{2,1,0:T(8,128)(2,1)S(1)}, u32[]{:S(2)}, u32[]{:S(2)}) collective-permute-start(bf16[1,256,1024]{2,1,0:T(8,128)(2,1)S(1)} %get-tuple-element.577), channel_id=1, source_target_pairs={{0,1},{1,0},{2,3},{3,2},{4,5},{5,4},{6,7},{7,6},{8,9},{9,8},{10,11... | collective-permute-start | bytes 1572872 | tf_op jit(solution)/shard_map/ppermute | solution.py:20
  77.4 30.8 %collective-permute-start.7 = (bf16[1,256,1024]{2,1,0:T(8,128)(2,1)S(1)}, bf16[1,256,1024]{2,1,0:T(8,128)(2,1)S(1)}, u32[]{:S(2)}, u32[]{:S(2)}) collective-permute-start(bf16[1,256,1024]{2,1,0:T(8,128)(2,1)S(1)} %get-tuple-element.579), channel_id=1, source_target_pairs={{0,16},{16,0},{1,17},{17,1},{2,18},{18,2},{3,19},{19,3},{4,20},{20... | collective-permute-start | bytes 1572872 | tf_op jit(solution)/shard_map/ppermute | solution.py:20
  111.5 24.4 %collective-permute-start.8 = (bf16[2,1,256,1024]{3,2,0,1:T(8,128)(2,1)S(1)}, bf16[2,1,256,1024]{3,2,0,1:T(8,128)(2,1)}, u32[]{:S(2)}, u32[]{:S(2)}) collective-permute-start(bf16[2,1,256,1024]{3,2,0,1:T(8,128)(2,1)S(1)} %bitcast.413), channel_id=1, source_target_pairs={{0,16},{16,0},{1,17},{17,1},{2,18},{18,2},{3,19},{19,3},{4,20},{20... | collective-permute-start | bytes 3145736 | tf_op jit(solution)/shard_map/ppermute | solution.py:20
  111.8 24.9 %collective-permute-start.9 = (bf16[2,1,256,1024]{3,2,0,1:T(8,128)(2,1)S(1)}, bf16[2,1,256,1024]{3,2,0,1:T(8,128)(2,1)}, u32[]{:S(2)}, u32[]{:S(2)}) collective-permute-start(bf16[2,1,256,1024]{3,2,0,1:T(8,128)(2,1)S(1)} %pad_maximum_fusion.19), channel_id=1, source_target_pairs={{0,1},{1,0},{2,3},{3,2},{4,5},{5,4},{6,7},{7,6},{8,9},{9,8},{10,11... | collective-permute-start | bytes 3145736 | tf_op jit(solution)/shard_map/ppermute | solution.py:20
  147.2 148.5 %all-gather.12.cloned.1.call-start = ((), (), s32[]{:S(2)}) async-start(), calls=%async_computation.8 | async-start | bytes 6488064 | tf_op jit(solution)/shard_map/all_gather | solution.py:233
  153.1 52.1 %collective-permute-start.17 = (bf16[2048,1024]{1,0:T(8,128)(2,1)}, bf16[2048,1024]{1,0:T(8,128)(2,1)}, u32[]{:S(2)}, u32[]{:S(2)}) collective-permute-start(bf16[2048,1024]{1,0:T(8,128)(2,1)} %bitcast.52), channel_id=1, source_target_pairs={{0,8},{8,0},{1,9},{9,1},{2,10},{10,2},{3,11},{11,3},{4,12},{12,4},... | collective-permute-start | bytes 12582920 | tf_op jit(solution)/shard_map/ppermute | solution.py:20
  153.2 36.2 %collective-permute-start.20 = (bf16[256,1408]{1,0:T(8,128)(2,1)}, bf16[256,1408]{1,0:T(8,128)(2,1)S(1)}, u32[]{:S(2)}, u32[]{:S(2)}) collective-permute-start(bf16[256,1408]{1,0:T(8,128)(2,1)} %concatenate.267), channel_id=1, source_target_pairs={{0,1},{9,8},{2,3},{11,10},{4,5},{13,12},{6,7},{15,14},{16,17},{25,... | collective-permute-start | bytes 2162696 | tf_op jit(solution)/shard_map/ppermute | solution.py:192
  165.1 28.0 %collective-permute-start.18 = (bf16[1,128,2048]{2,1,0:T(8,128)(2,1)S(1)}, bf16[1,128,2048]{2,1,0:T(8,128)(2,1)}, u32[]{:S(2)}, u32[]{:S(2)}) collective-permute-start(bf16[1,128,2048]{2,1,0:T(8,128)(2,1)S(1)} %get-tuple-element.646), channel_id=1, source_target_pairs={{0,1},{1,0},{2,3},{3,2},{4,5},{5,4},{6,7},{7,6},{8,9},{9,8},{10,11... | collective-permute-start | bytes 1572872 | tf_op jit(solution)/shard_map/ppermute | solution.py:20
  193.1 241.2 %reduce-scatter.8.cloned.1.call-start = ((), (), s32[]{:S(2)}) async-start(), calls=%async_computation.11 | async-start | bytes 6488064 | tf_op jit(solution)/shard_map/reduce_scatter | solution.py:237
  196.6 45.1 %collective-permute-start.25 = (bf16[2,1,128,2048]{3,2,0,1:T(8,128)(2,1)S(1)}, bf16[2,1,128,2048]{3,2,0,1:T(8,128)(2,1)S(1)}, u32[]{:S(2)}, u32[]{:S(2)}) collective-permute-start(bf16[2,1,128,2048]{3,2,0,1:T(8,128)(2,1)S(1)} %bitcast.419), channel_id=1, source_target_pairs={{0,16},{16,0},{1,17},{17,1},{2,18},{18,2},{3,19},{19,3},{4,20},{20... | collective-permute-start | bytes 3145736 | tf_op jit(solution)/shard_map/ppermute | solution.py:20
  198.6 43.2 %collective-permute-start.26 = (bf16[2,1,128,2048]{3,2,0,1:T(8,128)(2,1)S(1)}, bf16[2,1,128,2048]{3,2,0,1:T(8,128)(2,1)S(1)}, u32[]{:S(2)}, u32[]{:S(2)}) collective-permute-start(bf16[2,1,128,2048]{3,2,0,1:T(8,128)(2,1)S(1)} %pad_maximum_fusion.21), channel_id=1, source_target_pairs={{0,1},{1,0},{2,3},{3,2},{4,5},{5,4},{6,7},{7,6},{8,9},{9,8},{10,11... | collective-permute-start | bytes 3145736 | tf_op jit(solution)/shard_map/ppermute | solution.py:20
  215.6 24.0 %collective-permute-start.22 = (bf16[1,128,2048]{2,1,0:T(8,128)(2,1)S(1)}, bf16[1,128,2048]{2,1,0:T(8,128)(2,1)S(1)}, u32[]{:S(2)}, u32[]{:S(2)}) collective-permute-start(bf16[1,128,2048]{2,1,0:T(8,128)(2,1)S(1)} %get-tuple-element.666), channel_id=1, source_target_pairs={{0,16},{16,0},{1,17},{17,1},{2,18},{18,2},{3,19},{19,3},{4,20},{20... | collective-permute-start | bytes 1572872 | tf_op jit(solution)/shard_map/ppermute | solution.py:20
  295.7 138.6 %reduce-scatter.6.cloned.1.call-start = ((), (), s32[]{:S(2)}) async-start(), calls=%async_computation.10 | async-start | bytes 6488064 | tf_op jit(solution)/shard_map/reduce_scatter | solution.py:237
  343.9 241.9 %reduce-scatter.12.cloned.1.call-start = ((), (), s32[]{:S(2)}) async-start(), calls=%async_computation.13 | async-start | bytes 6488064 | tf_op jit(solution)/shard_map/reduce_scatter | solution.py:237
  374.7 114.1 %collective-permute-start.29 = (bf16[2,128,2048]{2,1,0:T(8,128)(2,1)}, bf16[2,128,2048]{2,1,0:T(8,128)(2,1)}, u32[]{:S(2)}, u32[]{:S(2)}) collective-permute-start(bf16[2,128,2048]{2,1,0:T(8,128)(2,1)} %get-tuple-element.739), channel_id=1, source_target_pairs={{0,1},{1,0},{2,3},{3,2},{4,5},{5,4},{6,7},{7,6},{8,9},{9,8},{10,11... | collective-permute-start | bytes 3145736 | tf_op jit(solution)/shard_map/ppermute | solution.py:20
  375.9 112.9 %collective-permute-start.30 = (bf16[2,128,2048]{2,1,0:T(8,128)(2,1)}, bf16[2,128,2048]{2,1,0:T(8,128)(2,1)}, u32[]{:S(2)}, u32[]{:S(2)}) collective-permute-start(bf16[2,128,2048]{2,1,0:T(8,128)(2,1)} %bitcast.114), channel_id=1, source_target_pairs={{0,16},{16,0},{1,17},{17,1},{2,18},{18,2},{3,19},{19,3},{4,20},{20... | collective-permute-start | bytes 3145736 | tf_op jit(solution)/shard_map/ppermute | solution.py:20
  405.5 186.1 %reduce-scatter.10.cloned.1.call-start = ((), (), s32[]{:S(2)}) async-start(), calls=%async_computation.12 | async-start | bytes 7077888 | tf_op jit(solution)/shard_map/reduce_scatter | solution.py:237
  434.3 46.8 %collective-permute-start.38 = (bf16[2,1,128,2048]{3,2,0,1:T(8,128)(2,1)}, bf16[2,1,128,2048]{3,2,0,1:T(8,128)(2,1)}, u32[]{:S(2)}, u32[]{:S(2)}) collective-permute-start(bf16[2,1,128,2048]{3,2,0,1:T(8,128)(2,1)} %pad_maximum_fusion.24), channel_id=1, source_target_pairs={{0,16},{16,0},{1,17},{17,1},{2,18},{18,2},{3,19},{19,3},{4,20},{20... | collective-permute-start | bytes 3145736 | tf_op jit(solution)/shard_map/ppermute | solution.py:20
  436.6 44.5 %collective-permute-start.39 = (bf16[2,1,128,2048]{3,2,0,1:T(8,128)(2,1)}, bf16[2,1,128,2048]{3,2,0,1:T(8,128)(2,1)}, u32[]{:S(2)}, u32[]{:S(2)}) collective-permute-start(bf16[2,1,128,2048]{3,2,0,1:T(8,128)(2,1)} %bitcast.415), channel_id=1, source_target_pairs={{0,1},{1,0},{2,3},{3,2},{4,5},{5,4},{6,7},{7,6},{8,9},{9,8},{10,11... | collective-permute-start | bytes 3145736 | tf_op jit(solution)/shard_map/ppermute | solution.py:20
  437.7 43.3 %collective-permute-start.43 = (bf16[256,1408]{1,0:T(8,128)(2,1)}, bf16[256,1408]{1,0:T(8,128)(2,1)S(1)}, u32[]{:S(2)}, u32[]{:S(2)}) collective-permute-start(bf16[256,1408]{1,0:T(8,128)(2,1)} %reduce-scatter.8.cloned.1.call-done), channel_id=1, source_target_pairs={{8,1},{1,8},{10,3},{3,10},{12,5},{5,12},{14,7},{7,14},{24,17},{17,... | collective-permute-start | bytes 2162696 | tf_op jit(solution)/shard_map/ppermute | solution.py:262
  505.6 156.0 %reduce-scatter.14.cloned.1.call-start = ((), (), s32[]{:S(2)}) async-start(), calls=%async_computation.14 | async-start | bytes 2359296 | tf_op jit(solution)/shard_map/reduce_scatter | solution.py:237
  514.7 28.9 %collective-permute-start.50 = (bf16[1,256,1408]{2,1,0:T(8,128)(2,1)S(1)}, bf16[1,256,1408]{2,1,0:T(8,128)(2,1)}, u32[]{:S(2)}, u32[]{:S(2)}) collective-permute-start(bf16[1,256,1408]{2,1,0:T(8,128)(2,1)S(1)} %fusion.67), channel_id=1, source_target_pairs={{0,16},{16,0},{1,17},{17,1},{2,18},{18,2},{3,19},{19,3},{4,20},{20... | collective-permute-start | bytes 2162696 | tf_op jit(solution)/shard_map/ppermute | solution.py:20
  535.3 26.7 %collective-permute-start.49 = (bf16[1,256,1408]{2,1,0:T(8,128)(2,1)}, bf16[1,256,1408]{2,1,0:T(8,128)(2,1)}, u32[]{:S(2)}, u32[]{:S(2)}) collective-permute-start(bf16[1,256,1408]{2,1,0:T(8,128)(2,1)} %fusion.66), channel_id=1, source_target_pairs={{0,16},{16,0},{1,17},{17,1},{2,18},{18,2},{3,19},{19,3},{4,20},{20... | collective-permute-start | bytes 2162696 | tf_op jit(solution)/shard_map/ppermute | solution.py:20
  535.9 28.8 %collective-permute-start.47 = (bf16[2,136,2048]{2,1,0:T(8,128)(2,1)}, bf16[2,136,2048]{2,1,0:T(8,128)(2,1)}, u32[]{:S(2)}, u32[]{:S(2)}) collective-permute-start(bf16[2,136,2048]{2,1,0:T(8,128)(2,1)} %get-tuple-element.866), channel_id=1, source_target_pairs={{0,1},{1,0},{2,3},{3,2},{4,5},{5,4},{6,7},{7,6},{8,9},{9,8},{10,11... | collective-permute-start | bytes 3342344 | tf_op jit(solution)/shard_map/ppermute | solution.py:20
  535.9 43.9 %collective-permute-start.48 = (bf16[2,136,2048]{2,1,0:T(8,128)(2,1)}, bf16[2,136,2048]{2,1,0:T(8,128)(2,1)}, u32[]{:S(2)}, u32[]{:S(2)}) collective-permute-start(bf16[2,136,2048]{2,1,0:T(8,128)(2,1)} %bitcast.174), channel_id=1, source_target_pairs={{0,16},{16,0},{1,17},{17,1},{2,18},{18,2},{3,19},{19,3},{4,20},{20... | collective-permute-start | bytes 3342344 | tf_op jit(solution)/shard_map/ppermute | solution.py:20
  (120 other events, 1268.6 us)
Sparse Core Ops, SparseCore 0:
  10.2 28.8 all-gather.5
  41.5 63.0 all-gather.7
  106.2 62.1 all-gather.9
  170.5 58.9 all-gather.13
  230.9 59.0 all-gather.11
  295.8 65.7 reduce-scatter.7
  364.5 63.4 reduce-scatter.5
  430.3 68.9 reduce-scatter.11
  505.8 68.8 reduce-scatter.9
  585.9 34.2 reduce-scatter.13

commit v16 on v15

--- a/solution.py
+++ b/solution.py
@@ -946,7 +946,17 @@
     def column_whole(own, got):
         return owner_whole(lax.axis_index("c"), [own] + got, depth)
 
+    small = run(
+        lambda a, b, c, gain: jnp.concatenate([a, b, c, gain.reshape(-1, channels)], axis=0),
+        grad_residue,
+        grad_decay,
+        grad_taps,
+        grad_feed_gain,
+    )
+    small_got = moved(small, "c", 1)
     grad_up_weight = run(column_whole, up_held, up_got)
+    small = run(lambda v, got: v + sum(got), small, small_got)
+    small_got = moved(small, "z", 1)
     gate_held = run(stacked, gate_held, gate_got)
     gate_got = moved(gate_held, "c", -1)
     one_back.turn(line)
@@ -968,44 +978,51 @@
         feed_back.rest(),
         middle,
     )
+    small = run(lambda v, got: v + sum(got), small, small_got)
+    small_got = moved(small, "x", -1)
     in_held = run(owner_held, in_got)
     in_got = moved(in_held, "y", -1)
-
-    def tokens_back(grad, extension, values, scale, gain, back, small):
+    small = run(stacked, small, small_got)
+    small_got = moved(small, "y", -1)
+
+    def tokens_back(grad, extension, values, scale, gain, back):
         values = values.astype(wide)
         grad = jnp.concatenate(
             [grad[:, : local - 2], grad[:, local - 2 :] + extension.astype(wide)], axis=1
         )
         result, grad_gain = norm_back(values, scale, gain, grad)
-        gains = jnp.stack([grad_gain, small[0]]).reshape(-1, channels)
-        return (result + back).astype(low), jnp.concatenate(list(small[1:]) + [gains], axis=0)
-
-    grad_tokens, small = run(
-        tokens_back,
-        grad_normed,
-        grad_after,
-        tokens,
-        scale_one,
-        norm_gain,
-        grad_middle,
-        (grad_feed_gain, grad_residue, grad_decay, grad_taps),
-    )
-    small_got = moved(small, "c", 1)
-    small = run(lambda v, got: v + sum(got), small, small_got)
-    small_got = moved(small, "z", 1)
+        return (result + back).astype(low), grad_gain.reshape(-1, channels)
+
+    grad_tokens, gain_sum = run(
+        tokens_back, grad_normed, grad_after, tokens, scale_one, norm_gain, grad_middle
+    )
+    gain_got = moved(gain_sum, "c", 1)
+    poles = decay.shape[0]
+
+    def small_whole(own, got):
+        slots = jnp.stack([own] + got)
+        rows = 2 * poles + 9
+        gain = jnp.sum(slots[:, :, rows:], axis=(0, 1)).reshape(width)
+        whole = all_channels(slots[:, :, :rows])
+        grad_conv_taps = jnp.concatenate(
+            [whole[2 * poles + 3 * g : 2 * poles + 3 * g + 3] for g in range(3)], axis=1
+        )
+        return gain, grad_conv_taps, whole[:poles].T, whole[poles : 2 * poles].T
+
+    feed_gain_sum, grad_conv_taps, residue_sum, decay_sum = run(small_whole, small, small_got)
+    gain_sum = run(lambda v, got: v + sum(got), gain_sum, gain_got)
+    gain_got = moved(gain_sum, "z", 1)
     in_held = run(stacked, in_held, in_got)
     in_got = moved(in_held, "c", -1)
-    small = run(lambda v, got: v + sum(got), small, small_got)
-    small_got = moved(small, "x", -1)
-    grad_in_weight = run(
-        lambda own, got: owner_whole(lax.axis_index("c"), [own] + got, count), in_held, in_got
-    )
     down_held = run(lambda own, got: jnp.concatenate([own] + got), down_held, down_got)
     down_got = moved(down_held, "c", -1)
     out_held = run(lambda v: v[None], out_mine)
     out_got = moved(out_held, "y", -1)
-    small = run(stacked, small, small_got)
-    small_got = moved(small, "y", -1)
+    grad_in_weight = run(
+        lambda own, got: owner_whole(lax.axis_index("c"), [own] + got, count), in_held, in_got
+    )
+    gain_sum = run(lambda v, got: v + sum(got), gain_sum, gain_got)
+    gain_got = swap_slots([[gain_sum] * spread] * ycount)
 
     def rows_whole(own, got):
         whole = in_order(jnp.swapaxes(in_order(jnp.stack([own] + got), "c"), 0, 1), "y")
@@ -1014,21 +1031,7 @@
     grad_down = run(rows_whole, down_held, down_got)
     out_held = run(lambda own, got: jnp.concatenate([own] + got), out_held, out_got)
     out_got = moved(out_held, "c", -1)
-    poles = decay.shape[0]
-
-    def small_whole(own, got):
-        slots = jnp.stack([own] + got)
-        rows = 2 * poles + 9
-        gains = jnp.sum(slots[:, :, rows:], axis=(0, 1)).reshape(2, width)
-        whole = all_channels(slots[:, :, :rows])
-        grad_conv_taps = jnp.concatenate(
-            [whole[2 * poles + 3 * g : 2 * poles + 3 * g + 3] for g in range(3)], axis=1
-        )
-        return gains[0], gains[1], grad_conv_taps, whole[:poles].T, whole[poles : 2 * poles].T
-
-    grad_norm_gain, feed_gain_sum, grad_conv_taps, residue_sum, decay_sum = run(
-        small_whole, small, small_got
-    )
+    grad_norm_gain = run(lambda got: sum(sum(got, [])).reshape(width), gain_got)
 
     def out_whole(core, own, got):
         ccount = lax.axis_size("c")

time: 702 us -> 697 us (level)
  waiting for transfers between devices: 195 us -> 173 us
  starting transfers between devices: 94.7 us -> 108 us
    ppermute x49 -> x53, waiting for transfers between devices: 154 us -> 136 us  [turned(): lax.ppermute(value, axis, [(i, (i + by) % length) for i in range(length)])]
    ppermute x49 -> x53, starting transfers between devices: 45.1 us -> 52.8 us  [turned(): lax.ppermute(value, axis, [(i, (i + by) % length) for i in range(length)])]
    ppermute x6 -> x9, waiting for transfers between devices: 15.1 us -> 17.6 us  [swap_slots(): line.append(lax.ppermute(slots[sy][sx], ('y', 'x'), pairs))]
    unnamed x167 -> x166, local copies, waits for them, and re-layouts: 20.7 us -> 19.3 us
  transfers between devices with their start and end apart: 79 -> 86, of which waited for: 38 -> 33; matrix products, arithmetic and copies ran while one was open for 44% -> 45% of each run, Pallas kernels for 8% -> 8%
where the time goes in v16:
time: 697 us; the launch traced here: 687 us
  waiting for transfers between devices  173 us (25%)
  matrix products  141 us (20%)
  other arithmetic  118 us (17%)
  starting transfers between devices  108 us (15%)
  local copies, waits for them, and re-layouts  72.9 us (10%)
  Pallas kernels  56.3 us (8%)
  between operations  16.6 us (2%)
    ppermute x53, waiting for transfers between devices, turned(): lax.ppermute(value, axis, [(i, (i + by) % length) for i in range(length)])  136 us
    dot_general x6, matrix products, dot(): return jnp.dot(a, b, preferred_element_type=wide).astype(kind)  55.4 us
    ppermute x53, starting transfers between devices, turned(): lax.ppermute(value, axis, [(i, (i + by) % length) for i in range(length)])  52.8 us
    dot_general x6, matrix products, dot_t(): lax.dot_general(a, b, (((1,), (1,)), ((), ())), preferred_element_type=wide)  45.7 us
    dot_general x5, matrix products, dot_w(): lax.dot_general(a, b, (((0,), (0,)), ((), ())), preferred_element_type=wide)  39.7 us
    pallas_call x4, Pallas kernels, conv_call(): pl.pallas_call(kernel, out_shape=results, grid_spec=pltpu.PrefetchScalarG...  35.3 us
    ppermute x3, starting transfers between devices, owner_moves(): got.append(lax.ppermute(parts[d], ('c', 'x'), pairs))  24.6 us
    unnamed x166, local copies, waits for them, and re-layouts  19.3 us
  transfers between devices with their start and end apart: 86, of which 33 were waited for; matrix products, arithmetic and copies ran while one was open for 45% of the time, Pallas kernels for 8%

profile of v16, /device:TPU:9, one launch (start us, length us, event | category | flops | bytes accessed | tf_op | source)
XLA Modules:
  0.0 686.5 jit_solution(4868298838163807040)
XLA Ops:
  33.7 5.3 all-gather.6.cloned.1.call-done
  43.9 10.9 %collective-permute-done.1 = bf16[1,136,2048]{2,1,0:T(8,128)(2,1)} collective-permute-done((bf16[1,136,2048]{2,1,0:T(8,128)(2,1)S(1)}, bf16[1,136,2048]{2,1,0:T(8,128)(2,1)}, u32[]{:S(2)}, u32[]{:S(2)}) %collective-permute-start.1) | collective-permute-done | bytes 557088 | tf_op jit(solution)/shard_map/ppermute | solution.py:20
  77.5 8.3 %collective-permute-done.4 = bf16[2,1,136,2048]{3,2,0,1:T(8,128)(2,1)S(1)} collective-permute-done((bf16[2,1,136,2048]{3,2,0,1:T(8,128)(2,1)}, bf16[2,1,136,2048]{3,2,0,1:T(8,128)(2,1)S(1)}, u32[]{:S(2)}, u32[]{:S(2)}) %collective-permute-start.4) | collective-permute-done | bytes 1114144 | tf_op jit(solution)/shard_map/ppermute | solution.py:20
  92.6 15.6 %collective-permute-done.6 = bf16[1,256,1024]{2,1,0:T(8,128)(2,1)S(1)} collective-permute-done((bf16[1,256,1024]{2,1,0:T(8,128)(2,1)S(1)}, bf16[1,256,1024]{2,1,0:T(8,128)(2,1)S(1)}, u32[]{:S(2)}, u32[]{:S(2)}) %collective-permute-start.6) | collective-permute-done | bytes 524320 | tf_op jit(solution)/shard_map/ppermute | solution.py:20
  111.8 10.8 %convolution_convert_fusion.4 = bf16[1088,1536]{1,0:T(8,128)(2,1)S(1)} fusion(bf16[1088,2048]{1,0:T(8,128)(2,1)} %bitcast.387, bf16[2048,1536]{1,0:T(8,128)(2,1)} %all-gather.8.cloned.1.call-done), kind=kOutput, calls=%fused_computation.5 | convolution fusion | flops 6846775296 | bytes 14090240 | tf_op jit(solution)/shard_map/dot_general | solution.py:638
  122.6 13.3 %collective-permute-done.8 = bf16[2,1,256,1024]{3,2,0,1:T(8,128)(2,1)} collective-permute-done((bf16[2,1,256,1024]{3,2,0,1:T(8,128)(2,1)S(1)}, bf16[2,1,256,1024]{3,2,0,1:T(8,128)(2,1)}, u32[]{:S(2)}, u32[]{:S(2)}) %collective-permute-start.8) | collective-permute-done | bytes 1048608 | tf_op jit(solution)/shard_map/ppermute | solution.py:20
  165.1 7.1 %collective-permute-start.18 = (bf16[1,128,2048]{2,1,0:T(8,128)(2,1)S(1)}, bf16[1,128,2048]{2,1,0:T(8,128)(2,1)}, u32[]{:S(2)}, u32[]{:S(2)}) collective-permute-start(bf16[1,128,2048]{2,1,0:T(8,128)(2,1)S(1)} %get-tuple-element.667), channel_id=1, source_target_pairs={{0,1},{1,0},{2,3},{3,2},{4,5},{5,4},{6,7},{7,6},{8,9},{9,8},{10,11... | collective-permute-start | bytes 1572872 | tf_op jit(solution)/shard_map/ppermute | solution.py:20
  176.6 8.8 %shard_map.222 = bf16[4,2,1,128,512]{4,3,2,1,0:T(8,128)(2,1)} custom-call(s32[1]{0:T(128)} %bitcast.39.place_ref, bf16[4,2,1,128,512]{4,3,2,1,0:T(8,128)(2,1)} %fusion.49.signal_ref, f32[16,512]{1,0:T(8,128)} %maximum_bitcast_fusion.11.decay_ref, f32[16,512]{1,0:T(8,128)} %maximum_bitcast_fusion.12.residue_ref, f32[4,16,512]{2,1,0:T(8,128)} %multiply_add_fusion.2.start_ref), custom_call_target="tpu_custom_call" | custom-call | flops 33554432 | bytes 2293760 | tf_op jit(solution)/shard_map/pallas_call | solution.py:555
  216.9 20.9 %collective-permute-done.21 = bf16[1,128,2048]{2,1,0:T(8,128)(2,1)S(1)} collective-permute-done((bf16[1,128,2048]{2,1,0:T(8,128)(2,1)S(1)}, bf16[1,128,2048]{2,1,0:T(8,128)(2,1)S(1)}, u32[]{:S(2)}, u32[]{:S(2)}) %collective-permute-start.21) | collective-permute-done | bytes 524320 | tf_op jit(solution)/shard_map/ppermute | solution.py:20
  245.1 12.0 %fusion.122 = f32[1024,1408]{1,0:T(8,128)} fusion(bf16[1024,2048]{1,0:T(8,128)(2,1)} %bitcast.397, bf16[1408,2048]{1,0:T(8,128)(2,1)} %all-gather.10.cloned.1.call-done), kind=kOutput, calls=%fused_computation.420 | convolution fusion | flops 5905580032 | bytes 15728640 | tf_op jit(solution)/shard_map/dot_general | solution.py:642
  257.1 10.8 %collective-permute-done.23 = bf16[2,1,128,2048]{3,2,0,1:T(8,128)(2,1)S(1)} collective-permute-done((bf16[2,1,128,2048]{3,2,0,1:T(8,128)(2,1)}, bf16[2,1,128,2048]{3,2,0,1:T(8,128)(2,1)S(1)}, u32[]{:S(2)}, u32[]{:S(2)}) %collective-permute-start.23) | collective-permute-done | bytes 1048608 | tf_op jit(solution)/shard_map/ppermute | solution.py:20
  272.0 13.3 %multiply_convert_fusion.2 = (bf16[1024,1408]{1,0:T(8,128)(2,1)S(1)}, f32[1024,1408]{1,0:T(8,128)}) fusion(f32[1024,1408]{1,0:T(8,128)} %fusion.122, bf16[1024,2048]{1,0:T(8,128)(2,1)} %bitcast.400, bf16[2048,1408]{1,0:T(8,128)(2,1)} %all-gather.14.cloned.1.call-done), kind=kOutput, calls=%fused_computation.10 | convolution fusion | flops 5914230784 | bytes 24379392 | tf_op jit(solution)/shard_map/dot_general | solution.py:638
  286.9 8.7 %convolution_convert_fusion.3 = bf16[2048,1408]{1,0:T(8,128)(2,1)} fusion(bf16[1024,2048]{1,0:T(8,128)(2,1)S(1)} %bitcast.402, bf16[1024,1408]{1,0:T(8,128)(2,1)S(1)} %get-tuple-element.738), kind=kOutput, calls=%fused_computation.4 | convolution fusion | flops 5908463616 | bytes 12845056 | tf_op jit(solution)/shard_map/dot_general | solution.py:646
  295.6 15.3 %multiply_convert_fusion = (bf16[1024,1408]{1,0:T(8,128)(2,1)S(1)}, bf16[1024,1408]{1,0:T(8,128)(2,1)}) fusion(f32[1024,1408]{1,0:T(8,128)} %get-tuple-element.728, f32[1024,1408]{1,0:T(8,128)} %fusion.122, bf16[1024,2048]{1,0:T(8,128)(2,1)} %bitcast.401, bf16[2048,1408]{1,0:T(8,128)(2,1)} %all-gather.12.cloned.1.call-done), kind=kOutput, calls=%fused_computation.7 | convolution fusion | flops 5924323328 | bytes 27262976 | tf_op jit(solution)/shard_map/dot_general | solution.py:638
  312.5 8.9 %fusion.123 = f32[1024,2048]{1,0:T(8,128)S(1)} fusion(bf16[1024,1408]{1,0:T(8,128)(2,1)S(1)} %get-tuple-element.747, bf16[2048,1408]{1,0:T(8,128)(2,1)} %all-gather.14.cloned.1.call-done), kind=kOutput, calls=%fused_computation.421 | convolution fusion | flops 5905580032 | bytes 17039360 | tf_op jit(solution)/shard_map/dot_general | solution.py:642
  321.4 8.4 %add_convert_fusion = bf16[1024,2048]{1,0:T(8,128)(2,1)S(1)} fusion(f32[1024,2048]{1,0:T(8,128)S(1)} %fusion.123, bf16[1024,1408]{1,0:T(8,128)(2,1)} %copy-done.70, bf16[2048,1408]{1,0:T(8,128)(2,1)S(1)} %copy-done.66), kind=kOutput, calls=%fused_computation | convolution fusion | flops 5909774336 | bytes 21233664 | tf_op jit(solution)/shard_map/dot_general | solution.py:642
  335.2 8.7 %convolution_convert_fusion.2 = bf16[2048,1408]{1,0:T(8,128)(2,1)} fusion(bf16[1024,2048]{1,0:T(8,128)(2,1)S(1)} %bitcast.403, bf16[1024,1408]{1,0:T(8,128)(2,1)S(1)} %copy-done.69), kind=kOutput, calls=%fused_computation.3 | convolution fusion | flops 5908463616 | bytes 12845056 | tf_op jit(solution)/shard_map/dot_general | solution.py:646
  343.9 11.5 %collective-permute-done.27 = bf16[2,128,2048]{2,1,0:T(8,128)(2,1)} collective-permute-done((bf16[2,128,2048]{2,1,0:T(8,128)(2,1)}, bf16[2,128,2048]{2,1,0:T(8,128)(2,1)}, u32[]{:S(2)}, u32[]{:S(2)}) %collective-permute-start.27) | collective-permute-done | bytes 1048608 | tf_op jit(solution)/shard_map/ppermute | solution.py:20
  360.9 9.1 %convolution_convert_fusion.6 = bf16[1024,2048]{1,0:T(8,128)(2,1)S(1)} fusion(bf16[1024,1408]{1,0:T(8,128)(2,1)S(1)} %copy-done.67, bf16[1408,2048]{1,0:T(8,128)(2,1)} %all-gather.10.cloned.1.call-done), kind=kOutput, calls=%fused_computation.26 | convolution fusion | flops 5907677184 | bytes 12845056 | tf_op jit(solution)/shard_map/dot_general | solution.py:638
  397.2 8.1 %convolution_convert_fusion.1 = bf16[1408,2048]{1,0:T(8,128)(2,1)} fusion(bf16[1024,1408]{1,0:T(8,128)(2,1)S(1)} %copy-done.67, bf16[1024,2048]{1,0:T(8,128)(2,1)S(1)} %bitcast.398), kind=kOutput, calls=%fused_computation.2 | convolution fusion | flops 5908463616 | bytes 12845056 | tf_op jit(solution)/shard_map/dot_general | solution.py:646
  437.8 17.0 %collective-permute-start.43 = (bf16[256,1408]{1,0:T(8,128)(2,1)}, bf16[256,1408]{1,0:T(8,128)(2,1)S(1)}, u32[]{:S(2)}, u32[]{:S(2)}) collective-permute-start(bf16[256,1408]{1,0:T(8,128)(2,1)} %reduce-scatter.8.cloned.1.call-done), channel_id=1, source_target_pairs={{8,1},{1,8},{10,3},{3,10},{12,5},{5,12},{14,7},{7,14},{24,17},{17,... | collective-permute-start | bytes 2162696 | tf_op jit(solution)/shard_map/ppermute | solution.py:262
  461.1 16.8 %shard_map.224 = (bf16[4,2,1,128,512]{4,3,2,1,0:T(8,128)(2,1)}, f32[16,512]{1,0:T(8,128)}, f32[16,512]{1,0:T(8,128)}) custom-call(s32[1]{0:T(128)} %bitcast.39.place_ref, bf16[4,2,1,128,512]{4,3,2,1,0:T(8,128)(2,1)} %fusion.49.signal_ref, bf16[4,2,1,128,512]{4,3,2,1,0:T(8,128)(2,1)} %get-tuple-element.823.signal_ref.grad_ref, ...), custom_call_target="tpu_custom_call" | custom-call | flops 100663296 | bytes 4521984 | tf_op jit(solution)/shard_map/pallas_call | solution.py:555
  495.2 10.5 %convolution_convert_fusion = bf16[2048,1536]{1,0:T(8,128)(2,1)} fusion(bf16[1088,2048]{1,0:T(8,128)(2,1)S(1)} %bitcast.390, bf16[1088,1024]{1,0:T(8,128)(2,1)S(1)} %bitcast.379, bf16[1088,512]{1,0:T(8,128)(2,1)S(1)} %bitcast.386), kind=kOutput, calls=%fused_computation.1 | convolution fusion | flops 6854934528 | bytes 14090240 | tf_op jit(solution)/shard_map/dot_general | solution.py:646
  515.8 6.1 collective-permute-done.46
  522.2 9.3 %convolution_convert_fusion.5 = bf16[1088,2048]{1,0:T(8,128)(2,1)S(1)} fusion(bf16[1088,1536]{1,0:T(8,128)(2,1)S(1)} %copy-done.33, bf16[2048,1536]{1,0:T(8,128)(2,1)} %all-gather.8.cloned.1.call-done), kind=kOutput, calls=%fused_computation.6 | convolution fusion | flops 6847332352 | bytes 14090240 | tf_op jit(solution)/shard_map/dot_general | solution.py:642
  557.5 5.8 shard_map.225
  565.8 14.3 %collective-permute-done.48 = bf16[2,136,2048]{2,1,0:T(8,128)(2,1)} collective-permute-done((bf16[2,136,2048]{2,1,0:T(8,128)(2,1)}, bf16[2,136,2048]{2,1,0:T(8,128)(2,1)}, u32[]{:S(2)}, u32[]{:S(2)}) %collective-permute-start.48) | collective-permute-done | bytes 1114144 | tf_op jit(solution)/shard_map/ppermute | solution.py:20
  593.0 5.8 shard_map.226
  603.4 5.3 collective-permute-start.61
  613.4 5.8 collective-permute-start.56
  629.3 14.5 %collective-permute-done.67 = bf16[1,256,1536]{2,1,0:T(8,128)(2,1)S(1)} collective-permute-done((bf16[1,256,1536]{2,1,0:T(8,128)(2,1)S(1)}, bf16[1,256,1536]{2,1,0:T(8,128)(2,1)S(1)}, u32[]{:S(2)}, u32[]{:S(2)}) %collective-permute-start.67) | collective-permute-done | bytes 786464 | tf_op jit(solution)/shard_map/ppermute | solution.py:20
  656.2 5.9 shard_map.227
  (551 shorter events, 337.0 us)
Async XLA Ops:
  7.2 31.8 %all-gather.6.cloned.1.call-start = ((), (), s32[]{:S(2)}) async-start(), calls=%async_computation.5 | async-start | bytes 1310720 | tf_op jit(solution)/shard_map/all_gather | solution.py:679
  9.3 102.5 %all-gather.8.cloned.1.call-start = ((), (), s32[]{:S(2)}) async-start(), calls=%async_computation.6 | async-start | bytes 7077888 | tf_op jit(solution)/shard_map/all_gather | solution.py:233
  41.3 203.1 %all-gather.10.cloned.1.call-start = ((), (), s32[]{:S(2)}) async-start(), calls=%async_computation.7 | async-start | bytes 6488064 | tf_op jit(solution)/shard_map/all_gather | solution.py:233
  61.4 210.6 %all-gather.14.cloned.1.call-start = ((), (), s32[]{:S(2)}) async-start(), calls=%async_computation.9 | async-start | bytes 6488064 | tf_op jit(solution)/shard_map/all_gather | solution.py:233
  63.5 81.4 %collective-permute-start.13 = (bf16[256,1408]{1,0:T(8,128)(2,1)}, bf16[256,1408]{1,0:T(8,128)(2,1)}, u32[]{:S(2)}, u32[]{:S(2)}) collective-permute-start(bf16[256,1408]{1,0:T(8,128)(2,1)} %concatenate.265), channel_id=1, source_target_pairs={{0,1},{9,8},{2,3},{11,10},{4,5},{13,12},{6,7},{15,14},{16,17},{25,... | collective-permute-start | bytes 2162696 | tf_op jit(solution)/shard_map/ppermute | solution.py:192
  74.4 33.8 %collective-permute-start.6 = (bf16[1,256,1024]{2,1,0:T(8,128)(2,1)S(1)}, bf16[1,256,1024]{2,1,0:T(8,128)(2,1)S(1)}, u32[]{:S(2)}, u32[]{:S(2)}) collective-permute-start(bf16[1,256,1024]{2,1,0:T(8,128)(2,1)S(1)} %get-tuple-element.598), channel_id=1, source_target_pairs={{0,1},{1,0},{2,3},{3,2},{4,5},{5,4},{6,7},{7,6},{8,9},{9,8},{10,11... | collective-permute-start | bytes 1572872 | tf_op jit(solution)/shard_map/ppermute | solution.py:20
  77.3 30.8 %collective-permute-start.7 = (bf16[1,256,1024]{2,1,0:T(8,128)(2,1)S(1)}, bf16[1,256,1024]{2,1,0:T(8,128)(2,1)S(1)}, u32[]{:S(2)}, u32[]{:S(2)}) collective-permute-start(bf16[1,256,1024]{2,1,0:T(8,128)(2,1)S(1)} %get-tuple-element.600), channel_id=1, source_target_pairs={{0,16},{16,0},{1,17},{17,1},{2,18},{18,2},{3,19},{19,3},{4,20},{20... | collective-permute-start | bytes 1572872 | tf_op jit(solution)/shard_map/ppermute | solution.py:20
  111.5 24.4 %collective-permute-start.8 = (bf16[2,1,256,1024]{3,2,0,1:T(8,128)(2,1)S(1)}, bf16[2,1,256,1024]{3,2,0,1:T(8,128)(2,1)}, u32[]{:S(2)}, u32[]{:S(2)}) collective-permute-start(bf16[2,1,256,1024]{3,2,0,1:T(8,128)(2,1)S(1)} %bitcast.409), channel_id=1, source_target_pairs={{0,16},{16,0},{1,17},{17,1},{2,18},{18,2},{3,19},{19,3},{4,20},{20... | collective-permute-start | bytes 3145736 | tf_op jit(solution)/shard_map/ppermute | solution.py:20
  111.8 24.9 %collective-permute-start.9 = (bf16[2,1,256,1024]{3,2,0,1:T(8,128)(2,1)S(1)}, bf16[2,1,256,1024]{3,2,0,1:T(8,128)(2,1)}, u32[]{:S(2)}, u32[]{:S(2)}) collective-permute-start(bf16[2,1,256,1024]{3,2,0,1:T(8,128)(2,1)S(1)} %pad_maximum_fusion.19), channel_id=1, source_target_pairs={{0,1},{1,0},{2,3},{3,2},{4,5},{5,4},{6,7},{7,6},{8,9},{9,8},{10,11... | collective-permute-start | bytes 3145736 | tf_op jit(solution)/shard_map/ppermute | solution.py:20
  147.2 148.4 %all-gather.12.cloned.1.call-start = ((), (), s32[]{:S(2)}) async-start(), calls=%async_computation.8 | async-start | bytes 6488064 | tf_op jit(solution)/shard_map/all_gather | solution.py:233
  153.1 52.0 %collective-permute-start.17 = (bf16[2048,1024]{1,0:T(8,128)(2,1)}, bf16[2048,1024]{1,0:T(8,128)(2,1)}, u32[]{:S(2)}, u32[]{:S(2)}) collective-permute-start(bf16[2048,1024]{1,0:T(8,128)(2,1)} %bitcast.52), channel_id=1, source_target_pairs={{0,8},{8,0},{1,9},{9,1},{2,10},{10,2},{3,11},{11,3},{4,12},{12,4},... | collective-permute-start | bytes 12582920 | tf_op jit(solution)/shard_map/ppermute | solution.py:20
  153.2 36.2 %collective-permute-start.20 = (bf16[256,1408]{1,0:T(8,128)(2,1)}, bf16[256,1408]{1,0:T(8,128)(2,1)S(1)}, u32[]{:S(2)}, u32[]{:S(2)}) collective-permute-start(bf16[256,1408]{1,0:T(8,128)(2,1)} %concatenate.267), channel_id=1, source_target_pairs={{0,1},{9,8},{2,3},{11,10},{4,5},{13,12},{6,7},{15,14},{16,17},{25,... | collective-permute-start | bytes 2162696 | tf_op jit(solution)/shard_map/ppermute | solution.py:192
  165.1 28.0 %collective-permute-start.18 = (bf16[1,128,2048]{2,1,0:T(8,128)(2,1)S(1)}, bf16[1,128,2048]{2,1,0:T(8,128)(2,1)}, u32[]{:S(2)}, u32[]{:S(2)}) collective-permute-start(bf16[1,128,2048]{2,1,0:T(8,128)(2,1)S(1)} %get-tuple-element.667), channel_id=1, source_target_pairs={{0,1},{1,0},{2,3},{3,2},{4,5},{5,4},{6,7},{7,6},{8,9},{9,8},{10,11... | collective-permute-start | bytes 1572872 | tf_op jit(solution)/shard_map/ppermute | solution.py:20
  193.1 241.1 %reduce-scatter.8.cloned.1.call-start = ((), (), s32[]{:S(2)}) async-start(), calls=%async_computation.11 | async-start | bytes 6488064 | tf_op jit(solution)/shard_map/reduce_scatter | solution.py:237
  196.6 45.1 %collective-permute-start.25 = (bf16[2,1,128,2048]{3,2,0,1:T(8,128)(2,1)S(1)}, bf16[2,1,128,2048]{3,2,0,1:T(8,128)(2,1)S(1)}, u32[]{:S(2)}, u32[]{:S(2)}) collective-permute-start(bf16[2,1,128,2048]{3,2,0,1:T(8,128)(2,1)S(1)} %bitcast.415), channel_id=1, source_target_pairs={{0,16},{16,0},{1,17},{17,1},{2,18},{18,2},{3,19},{19,3},{4,20},{20... | collective-permute-start | bytes 3145736 | tf_op jit(solution)/shard_map/ppermute | solution.py:20
  198.5 43.2 %collective-permute-start.26 = (bf16[2,1,128,2048]{3,2,0,1:T(8,128)(2,1)S(1)}, bf16[2,1,128,2048]{3,2,0,1:T(8,128)(2,1)S(1)}, u32[]{:S(2)}, u32[]{:S(2)}) collective-permute-start(bf16[2,1,128,2048]{3,2,0,1:T(8,128)(2,1)S(1)} %pad_maximum_fusion.21), channel_id=1, source_target_pairs={{0,1},{1,0},{2,3},{3,2},{4,5},{5,4},{6,7},{7,6},{8,9},{9,8},{10,11... | collective-permute-start | bytes 3145736 | tf_op jit(solution)/shard_map/ppermute | solution.py:20
  295.6 138.6 %reduce-scatter.6.cloned.1.call-start = ((), (), s32[]{:S(2)}) async-start(), calls=%async_computation.10 | async-start | bytes 6488064 | tf_op jit(solution)/shard_map/reduce_scatter | solution.py:237
  343.9 248.9 %reduce-scatter.12.cloned.1.call-start = ((), (), s32[]{:S(2)}) async-start(), calls=%async_computation.13 | async-start | bytes 6488064 | tf_op jit(solution)/shard_map/reduce_scatter | solution.py:237
  374.7 114.2 %collective-permute-start.29 = (bf16[2,128,2048]{2,1,0:T(8,128)(2,1)}, bf16[2,128,2048]{2,1,0:T(8,128)(2,1)}, u32[]{:S(2)}, u32[]{:S(2)}) collective-permute-start(bf16[2,128,2048]{2,1,0:T(8,128)(2,1)} %get-tuple-element.760), channel_id=1, source_target_pairs={{0,1},{1,0},{2,3},{3,2},{4,5},{5,4},{6,7},{7,6},{8,9},{9,8},{10,11... | collective-permute-start | bytes 3145736 | tf_op jit(solution)/shard_map/ppermute | solution.py:20
  375.9 113.0 %collective-permute-start.30 = (bf16[2,128,2048]{2,1,0:T(8,128)(2,1)}, bf16[2,128,2048]{2,1,0:T(8,128)(2,1)}, u32[]{:S(2)}, u32[]{:S(2)}) collective-permute-start(bf16[2,128,2048]{2,1,0:T(8,128)(2,1)} %bitcast.114), channel_id=1, source_target_pairs={{0,16},{16,0},{1,17},{17,1},{2,18},{18,2},{3,19},{19,3},{4,20},{20... | collective-permute-start | bytes 3145736 | tf_op jit(solution)/shard_map/ppermute | solution.py:20
  405.4 193.4 %reduce-scatter.10.cloned.1.call-start = ((), (), s32[]{:S(2)}) async-start(), calls=%async_computation.12 | async-start | bytes 7077888 | tf_op jit(solution)/shard_map/reduce_scatter | solution.py:237
  434.2 46.9 %collective-permute-start.38 = (bf16[2,1,128,2048]{3,2,0,1:T(8,128)(2,1)}, bf16[2,1,128,2048]{3,2,0,1:T(8,128)(2,1)}, u32[]{:S(2)}, u32[]{:S(2)}) collective-permute-start(bf16[2,1,128,2048]{3,2,0,1:T(8,128)(2,1)} %pad_maximum_fusion.24), channel_id=1, source_target_pairs={{0,16},{16,0},{1,17},{17,1},{2,18},{18,2},{3,19},{19,3},{4,20},{20... | collective-permute-start | bytes 3145736 | tf_op jit(solution)/shard_map/ppermute | solution.py:20
  436.6 44.5 %collective-permute-start.39 = (bf16[2,1,128,2048]{3,2,0,1:T(8,128)(2,1)}, bf16[2,1,128,2048]{3,2,0,1:T(8,128)(2,1)}, u32[]{:S(2)}, u32[]{:S(2)}) collective-permute-start(bf16[2,1,128,2048]{3,2,0,1:T(8,128)(2,1)} %bitcast.411), channel_id=1, source_target_pairs={{0,1},{1,0},{2,3},{3,2},{4,5},{5,4},{6,7},{7,6},{8,9},{9,8},{10,11... | collective-permute-start | bytes 3145736 | tf_op jit(solution)/shard_map/ppermute | solution.py:20
  437.8 43.4 %collective-permute-start.43 = (bf16[256,1408]{1,0:T(8,128)(2,1)}, bf16[256,1408]{1,0:T(8,128)(2,1)S(1)}, u32[]{:S(2)}, u32[]{:S(2)}) collective-permute-start(bf16[256,1408]{1,0:T(8,128)(2,1)} %reduce-scatter.8.cloned.1.call-done), channel_id=1, source_target_pairs={{8,1},{1,8},{10,3},{3,10},{12,5},{5,12},{14,7},{7,14},{24,17},{17,... | collective-permute-start | bytes 2162696 | tf_op jit(solution)/shard_map/ppermute | solution.py:262
  505.7 150.0 %reduce-scatter.14.cloned.1.call-start = ((), (), s32[]{:S(2)}) async-start(), calls=%async_computation.14 | async-start | bytes 2359296 | tf_op jit(solution)/shard_map/reduce_scatter | solution.py:237
  515.0 28.9 %collective-permute-start.50 = (bf16[1,256,1408]{2,1,0:T(8,128)(2,1)}, bf16[1,256,1408]{2,1,0:T(8,128)(2,1)}, u32[]{:S(2)}, u32[]{:S(2)}) collective-permute-start(bf16[1,256,1408]{2,1,0:T(8,128)(2,1)} %fusion.67), channel_id=1, source_target_pairs={{0,16},{16,0},{1,17},{17,1},{2,18},{18,2},{3,19},{19,3},{4,20},{20... | collective-permute-start | bytes 2162696 | tf_op jit(solution)/shard_map/ppermute | solution.py:20
  535.0 28.3 %collective-permute-start.49 = (bf16[1,256,1408]{2,1,0:T(8,128)(2,1)S(1)}, bf16[1,256,1408]{2,1,0:T(8,128)(2,1)}, u32[]{:S(2)}, u32[]{:S(2)}) collective-permute-start(bf16[1,256,1408]{2,1,0:T(8,128)(2,1)S(1)} %fusion.66), channel_id=1, source_target_pairs={{0,16},{16,0},{1,17},{17,1},{2,18},{18,2},{3,19},{19,3},{4,20},{20... | collective-permute-start | bytes 2162696 | tf_op jit(solution)/shard_map/ppermute | solution.py:20
  535.5 30.3 %collective-permute-start.47 = (bf16[2,136,2048]{2,1,0:T(8,128)(2,1)}, bf16[2,136,2048]{2,1,0:T(8,128)(2,1)}, u32[]{:S(2)}, u32[]{:S(2)}) collective-permute-start(bf16[2,136,2048]{2,1,0:T(8,128)(2,1)} %get-tuple-element.887), channel_id=1, source_target_pairs={{0,1},{1,0},{2,3},{3,2},{4,5},{5,4},{6,7},{7,6},{8,9},{9,8},{10,11... | collective-permute-start | bytes 3342344 | tf_op jit(solution)/shard_map/ppermute | solution.py:20
  535.5 44.5 %collective-permute-start.48 = (bf16[2,136,2048]{2,1,0:T(8,128)(2,1)}, bf16[2,136,2048]{2,1,0:T(8,128)(2,1)}, u32[]{:S(2)}, u32[]{:S(2)}) collective-permute-start(bf16[2,136,2048]{2,1,0:T(8,128)(2,1)} %bitcast.174), channel_id=1, source_target_pairs={{0,16},{16,0},{1,17},{17,1},{2,18},{18,2},{3,19},{19,3},{4,20},{20... | collective-permute-start | bytes 3342344 | tf_op jit(solution)/shard_map/ppermute | solution.py:20
  586.0 26.3 %collective-permute-start.57 = (f32[45,512]{1,0:T(8,128)S(1)}, f32[45,512]{1,0:T(8,128)S(1)}, u32[]{:S(2)}, u32[]{:S(2)}) collective-permute-start(f32[45,512]{1,0:T(8,128)S(1)} %add.619), channel_id=1, source_target_pairs={{0,2},{2,4},{4,6},{6,0},{1,3},{3,5},{5,7},{7,1},{8,10},{10,12},{12... | collective-permute-start | bytes 276488 | tf_op jit(solution)/shard_map/ppermute | solution.py:20
  587.5 24.8 %collective-permute-start.58 = (f32[45,512]{1,0:T(8,128)S(1)}, f32[45,512]{1,0:T(8,128)S(1)}, u32[]{:S(2)}, u32[]{:S(2)}) collective-permute-start(f32[45,512]{1,0:T(8,128)S(1)} %add.619), channel_id=1, source_target_pairs={{0,4},{2,6},{4,0},{6,2},{1,5},{3,7},{5,1},{7,3},{8,12},{10,14},{12... | collective-permute-start | bytes 276488 | tf_op jit(solution)/shard_map/ppermute | solution.py:20
  599.2 47.6 %collective-permute-start.69 = (bf16[1,176,2048]{2,1,0:T(8,128)(2,1)}, bf16[1,176,2048]{2,1,0:T(8,128)(2,1)}, u32[]{:S(2)}, u32[]{:S(2)}) collective-permute-start(bf16[1,176,2048]{2,1,0:T(8,128)(2,1)} %bitcast.458), channel_id=1, source_target_pairs={{0,16},{16,0},{1,17},{17,1},{2,18},{18,2},{3,19},{19,3},{4,20},{20... | collective-permute-start | bytes 2162696 | tf_op jit(solution)/shard_map/ppermute | solution.py:20
  (127 other events, 1349.0 us)
Sparse Core Ops, SparseCore 0:
  10.2 28.8 all-gather.5
  41.5 63.0 all-gather.7
  106.2 62.2 all-gather.9
  170.6 58.9 all-gather.13
  231.1 59.0 all-gather.11
  295.7 65.9 reduce-scatter.7
  364.5 63.4 reduce-scatter.5
  430.3 68.9 reduce-scatter.11
  505.8 68.7 reduce-scatter.9
  586.2 37.7 reduce-scatter.13

commit v17 on v16

--- a/solution.py
+++ b/solution.py
@@ -960,10 +960,12 @@
     gate_held = run(stacked, gate_held, gate_got)
     gate_got = moved(gate_held, "c", -1)
     one_back.turn(line)
+    in_got = owner_moves(run(owner_parts, in_mine))
     down_held = run(lambda v: v[None], down_mine)
     down_got = moved(down_held, "y", -1)
     grad_gate_weight = run(column_whole, gate_held, gate_got)
-    in_got = owner_moves(run(owner_parts, in_mine))
+    in_held = run(owner_held, in_got)
+    in_got = moved(in_held, "y", -1)
 
     def normed_sum(rest):
         value = Scatter.sum(*rest).reshape(batch, local + extra, width)
@@ -980,8 +982,6 @@
     )
     small = run(lambda v, got: v + sum(got), small, small_got)
     small_got = moved(small, "x", -1)
-    in_held = run(owner_held, in_got)
-    in_got = moved(in_held, "y", -1)
     small = run(stacked, small, small_got)
     small_got = moved(small, "y", -1)
 
@@ -997,6 +997,8 @@
         tokens_back, grad_normed, grad_after, tokens, scale_one, norm_gain, grad_middle
     )
     gain_got = moved(gain_sum, "c", 1)
+    in_held = run(stacked, in_held, in_got)
+    in_got = moved(in_held, "c", -1)
     poles = decay.shape[0]
 
     def small_whole(own, got):
@@ -1012,8 +1014,6 @@
     feed_gain_sum, grad_conv_taps, residue_sum, decay_sum = run(small_whole, small, small_got)
     gain_sum = run(lambda v, got: v + sum(got), gain_sum, gain_got)
     gain_got = moved(gain_sum, "z", 1)
-    in_held = run(stacked, in_held, in_got)
-    in_got = moved(in_held, "c", -1)
     down_held = run(lambda own, got: jnp.concatenate([own] + got), down_held, down_got)
     down_got = moved(down_held, "c", -1)
     out_held = run(lambda v: v[None], out_mine)

time: 697 us -> 745 us (1.069)
  waiting for transfers between devices: 173 us -> 230 us
  starting transfers between devices: 108 us -> 94.4 us
  other arithmetic: 118 us -> 126 us
    reduce_scatter x5, waiting for transfers between devices: 0.01 us -> 51.9 us  [scatter_tile(): return lax.psum_scatter(term, ('z', 'c'), scatter_dimension=0, tiled=True)]
    ppermute x3, starting transfers between devices: 24.6 us -> 15.8 us  [owner_moves(): got.append(lax.ppermute(parts[d], ('c', 'x'), pairs))]
  transfers between devices with their start and end apart: 86 -> 86, of which waited for: 33 -> 33; matrix products, arithmetic and copies ran while one was open for 45% -> 41% of each run, Pallas kernels for 8% -> 8%
where the time goes in v17:
time: 745 us; the launch traced here: 734 us
  waiting for transfers between devices  230 us (31%)
  matrix products  141 us (19%)
  other arithmetic  126 us (17%)
  starting transfers between devices  94.4 us (13%)
  local copies, waits for them, and re-layouts  70 us (9%)
  Pallas kernels  56.5 us (8%)
  between operations  16.6 us (2%)
    ppermute x53, waiting for transfers between devices, turned(): lax.ppermute(value, axis, [(i, (i + by) % length) for i in range(length)])  141 us
    dot_general x6, matrix products, dot(): return jnp.dot(a, b, preferred_element_type=wide).astype(kind)  55.4 us
    reduce_scatter x5, waiting for transfers between devices, scatter_tile(): return lax.psum_scatter(term, ('z', 'c'), scatter_dimension=0, tiled=True)  51.9 us
    ppermute x53, starting transfers between devices, turned(): lax.ppermute(value, axis, [(i, (i + by) % length) for i in range(length)])  49.2 us
    dot_general x6, matrix products, dot_t(): lax.dot_general(a, b, (((1,), (1,)), ((), ())), preferred_element_type=wide)  45.8 us
    dot_general x5, matrix products, dot_w(): lax.dot_general(a, b, (((0,), (0,)), ((), ())), preferred_element_type=wide)  39.7 us
    pallas_call x4, Pallas kernels, conv_call(): pl.pallas_call(kernel, out_shape=results, grid_spec=pltpu.PrefetchScalarG...  35.3 us
    pallas_call x3, Pallas kernels, owner_whole(): pl.pallas_call(functools.partial(assemble_kernel, count, width), out_shap...  17.6 us
  transfers between devices with their start and end apart: 86, of which 33 were waited for; matrix products, arithmetic and copies ran while one was open for 41% of the time, Pallas kernels for 8%

profile of v17, /device:TPU:9, one launch (start us, length us, event | category | flops | bytes accessed | tf_op | source)
XLA Modules:
  0.0 734.4 jit_solution(17550498148742196950)
XLA Ops:
  33.7 5.3 all-gather.6.cloned.1.call-done
  43.9 10.9 %collective-permute-done.1 = bf16[1,136,2048]{2,1,0:T(8,128)(2,1)} collective-permute-done((bf16[1,136,2048]{2,1,0:T(8,128)(2,1)S(1)}, bf16[1,136,2048]{2,1,0:T(8,128)(2,1)}, u32[]{:S(2)}, u32[]{:S(2)}) %collective-permute-start.1) | collective-permute-done | bytes 557088 | tf_op jit(solution)/shard_map/ppermute | solution.py:20
  77.5 8.3 %collective-permute-done.4 = bf16[2,1,136,2048]{3,2,0,1:T(8,128)(2,1)S(1)} collective-permute-done((bf16[2,1,136,2048]{3,2,0,1:T(8,128)(2,1)}, bf16[2,1,136,2048]{3,2,0,1:T(8,128)(2,1)S(1)}, u32[]{:S(2)}, u32[]{:S(2)}) %collective-permute-start.4) | collective-permute-done | bytes 1114144 | tf_op jit(solution)/shard_map/ppermute | solution.py:20
  92.6 15.6 %collective-permute-done.6 = bf16[1,256,1024]{2,1,0:T(8,128)(2,1)S(1)} collective-permute-done((bf16[1,256,1024]{2,1,0:T(8,128)(2,1)S(1)}, bf16[1,256,1024]{2,1,0:T(8,128)(2,1)S(1)}, u32[]{:S(2)}, u32[]{:S(2)}) %collective-permute-start.6) | collective-permute-done | bytes 524320 | tf_op jit(solution)/shard_map/ppermute | solution.py:20
  111.8 10.8 %convolution_convert_fusion.4 = bf16[1088,1536]{1,0:T(8,128)(2,1)S(1)} fusion(bf16[1088,2048]{1,0:T(8,128)(2,1)} %bitcast.387, bf16[2048,1536]{1,0:T(8,128)(2,1)} %all-gather.8.cloned.1.call-done), kind=kOutput, calls=%fused_computation.5 | convolution fusion | flops 6846775296 | bytes 14090240 | tf_op jit(solution)/shard_map/dot_general | solution.py:638
  122.6 13.3 %collective-permute-done.8 = bf16[2,1,256,1024]{3,2,0,1:T(8,128)(2,1)} collective-permute-done((bf16[2,1,256,1024]{3,2,0,1:T(8,128)(2,1)S(1)}, bf16[2,1,256,1024]{3,2,0,1:T(8,128)(2,1)}, u32[]{:S(2)}, u32[]{:S(2)}) %collective-permute-start.8) | collective-permute-done | bytes 1048608 | tf_op jit(solution)/shard_map/ppermute | solution.py:20
  165.1 7.1 collective-permute-start.18
  176.6 8.8 %shard_map.222 = bf16[4,2,1,128,512]{4,3,2,1,0:T(8,128)(2,1)} custom-call(s32[1]{0:T(128)} %bitcast.39.place_ref, bf16[4,2,1,128,512]{4,3,2,1,0:T(8,128)(2,1)} %fusion.49.signal_ref, f32[16,512]{1,0:T(8,128)} %maximum_bitcast_fusion.11.decay_ref, f32[16,512]{1,0:T(8,128)} %maximum_bitcast_fusion.12.residue_ref, f32[4,16,512]{2,1,0:T(8,128)} %multiply_add_fusion.2.start_ref), custom_call_target="tpu_custom_call" | custom-call | flops 33554432 | bytes 2293760 | tf_op jit(solution)/shard_map/pallas_call | solution.py:555
  216.9 20.9 %collective-permute-done.21 = bf16[1,128,2048]{2,1,0:T(8,128)(2,1)S(1)} collective-permute-done((bf16[1,128,2048]{2,1,0:T(8,128)(2,1)S(1)}, bf16[1,128,2048]{2,1,0:T(8,128)(2,1)S(1)}, u32[]{:S(2)}, u32[]{:S(2)}) %collective-permute-start.21) | collective-permute-done | bytes 524320 | tf_op jit(solution)/shard_map/ppermute | solution.py:20
  245.1 12.0 %fusion.122 = f32[1024,1408]{1,0:T(8,128)} fusion(bf16[1024,2048]{1,0:T(8,128)(2,1)} %bitcast.397, bf16[1408,2048]{1,0:T(8,128)(2,1)} %all-gather.10.cloned.1.call-done), kind=kOutput, calls=%fused_computation.420 | convolution fusion | flops 5905580032 | bytes 15728640 | tf_op jit(solution)/shard_map/dot_general | solution.py:642
  257.1 10.8 %collective-permute-done.23 = bf16[2,1,128,2048]{3,2,0,1:T(8,128)(2,1)S(1)} collective-permute-done((bf16[2,1,128,2048]{3,2,0,1:T(8,128)(2,1)}, bf16[2,1,128,2048]{3,2,0,1:T(8,128)(2,1)S(1)}, u32[]{:S(2)}, u32[]{:S(2)}) %collective-permute-start.23) | collective-permute-done | bytes 1048608 | tf_op jit(solution)/shard_map/ppermute | solution.py:20
  272.0 13.3 %multiply_convert_fusion.2 = (bf16[1024,1408]{1,0:T(8,128)(2,1)S(1)}, f32[1024,1408]{1,0:T(8,128)}) fusion(f32[1024,1408]{1,0:T(8,128)} %fusion.122, bf16[1024,2048]{1,0:T(8,128)(2,1)} %bitcast.400, bf16[2048,1408]{1,0:T(8,128)(2,1)} %all-gather.14.cloned.1.call-done), kind=kOutput, calls=%fused_computation.10 | convolution fusion | flops 5914230784 | bytes 24379392 | tf_op jit(solution)/shard_map/dot_general | solution.py:638
  286.9 8.7 %convolution_convert_fusion.3 = bf16[2048,1408]{1,0:T(8,128)(2,1)} fusion(bf16[1024,2048]{1,0:T(8,128)(2,1)S(1)} %bitcast.402, bf16[1024,1408]{1,0:T(8,128)(2,1)S(1)} %get-tuple-element.738), kind=kOutput, calls=%fused_computation.4 | convolution fusion | flops 5908463616 | bytes 12845056 | tf_op jit(solution)/shard_map/dot_general | solution.py:646
  295.6 15.3 %multiply_convert_fusion = (bf16[1024,1408]{1,0:T(8,128)(2,1)S(1)}, bf16[1024,1408]{1,0:T(8,128)(2,1)}) fusion(f32[1024,1408]{1,0:T(8,128)} %get-tuple-element.728, f32[1024,1408]{1,0:T(8,128)} %fusion.122, bf16[1024,2048]{1,0:T(8,128)(2,1)} %bitcast.401, bf16[2048,1408]{1,0:T(8,128)(2,1)} %all-gather.12.cloned.1.call-done), kind=kOutput, calls=%fused_computation.7 | convolution fusion | flops 5924323328 | bytes 27262976 | tf_op jit(solution)/shard_map/dot_general | solution.py:638
  312.5 8.9 %fusion.123 = f32[1024,2048]{1,0:T(8,128)S(1)} fusion(bf16[1024,1408]{1,0:T(8,128)(2,1)S(1)} %get-tuple-element.747, bf16[2048,1408]{1,0:T(8,128)(2,1)} %all-gather.14.cloned.1.call-done), kind=kOutput, calls=%fused_computation.421 | convolution fusion | flops 5905580032 | bytes 17039360 | tf_op jit(solution)/shard_map/dot_general | solution.py:642
  321.4 8.4 %add_convert_fusion = bf16[1024,2048]{1,0:T(8,128)(2,1)S(1)} fusion(f32[1024,2048]{1,0:T(8,128)S(1)} %fusion.123, bf16[1024,1408]{1,0:T(8,128)(2,1)} %copy-done.70, bf16[2048,1408]{1,0:T(8,128)(2,1)S(1)} %copy-done.66), kind=kOutput, calls=%fused_computation | convolution fusion | flops 5909774336 | bytes 21233664 | tf_op jit(solution)/shard_map/dot_general | solution.py:642
  335.2 8.7 %convolution_convert_fusion.2 = bf16[2048,1408]{1,0:T(8,128)(2,1)} fusion(bf16[1024,2048]{1,0:T(8,128)(2,1)S(1)} %bitcast.403, bf16[1024,1408]{1,0:T(8,128)(2,1)S(1)} %copy-done.69), kind=kOutput, calls=%fused_computation.3 | convolution fusion | flops 5908463616 | bytes 12845056 | tf_op jit(solution)/shard_map/dot_general | solution.py:646
  343.9 11.6 %collective-permute-done.27 = bf16[2,128,2048]{2,1,0:T(8,128)(2,1)} collective-permute-done((bf16[2,128,2048]{2,1,0:T(8,128)(2,1)}, bf16[2,128,2048]{2,1,0:T(8,128)(2,1)}, u32[]{:S(2)}, u32[]{:S(2)}) %collective-permute-start.27) | collective-permute-done | bytes 1048608 | tf_op jit(solution)/shard_map/ppermute | solution.py:20
  360.9 9.1 %convolution_convert_fusion.6 = bf16[1024,2048]{1,0:T(8,128)(2,1)S(1)} fusion(bf16[1024,1408]{1,0:T(8,128)(2,1)S(1)} %copy-done.67, bf16[1408,2048]{1,0:T(8,128)(2,1)} %all-gather.10.cloned.1.call-done), kind=kOutput, calls=%fused_computation.26 | convolution fusion | flops 5907677184 | bytes 12845056 | tf_op jit(solution)/shard_map/dot_general | solution.py:638
  397.3 8.1 %convolution_convert_fusion.1 = bf16[1408,2048]{1,0:T(8,128)(2,1)} fusion(bf16[1024,1408]{1,0:T(8,128)(2,1)S(1)} %copy-done.67, bf16[1024,2048]{1,0:T(8,128)(2,1)S(1)} %bitcast.398), kind=kOutput, calls=%fused_computation.2 | convolution fusion | flops 5908463616 | bytes 12845056 | tf_op jit(solution)/shard_map/dot_general | solution.py:646
  410.0 5.0 collective-permute-done.37
  437.7 11.5 %collective-permute-start.43 = (bf16[256,1408]{1,0:T(8,128)(2,1)}, bf16[256,1408]{1,0:T(8,128)(2,1)S(1)}, u32[]{:S(2)}, u32[]{:S(2)}) collective-permute-start(bf16[256,1408]{1,0:T(8,128)(2,1)} %reduce-scatter.8.cloned.1.call-done), channel_id=1, source_target_pairs={{8,1},{1,8},{10,3},{3,10},{12,5},{5,12},{14,7},{7,14},{24,17},{17,... | collective-permute-start | bytes 2162696 | tf_op jit(solution)/shard_map/ppermute | solution.py:262
  455.2 16.8 %shard_map.224 = (bf16[4,2,1,128,512]{4,3,2,1,0:T(8,128)(2,1)}, f32[16,512]{1,0:T(8,128)}, f32[16,512]{1,0:T(8,128)}) custom-call(s32[1]{0:T(128)} %bitcast.39.place_ref, bf16[4,2,1,128,512]{4,3,2,1,0:T(8,128)(2,1)} %fusion.49.signal_ref, bf16[4,2,1,128,512]{4,3,2,1,0:T(8,128)(2,1)} %get-tuple-element.823.signal_ref.grad_ref, ...), custom_call_target="tpu_custom_call" | custom-call | flops 100663296 | bytes 4521984 | tf_op jit(solution)/shard_map/pallas_call | solution.py:555
  489.2 10.5 %convolution_convert_fusion = bf16[2048,1536]{1,0:T(8,128)(2,1)} fusion(bf16[1088,2048]{1,0:T(8,128)(2,1)S(1)} %bitcast.390, bf16[1088,1024]{1,0:T(8,128)(2,1)S(1)} %bitcast.379, bf16[1088,512]{1,0:T(8,128)(2,1)S(1)} %bitcast.386), kind=kOutput, calls=%fused_computation.1 | convolution fusion | flops 6854934528 | bytes 14090240 | tf_op jit(solution)/shard_map/dot_general | solution.py:646
  510.0 5.2 collective-permute-done.46
  515.6 9.4 %convolution_convert_fusion.5 = bf16[1088,2048]{1,0:T(8,128)(2,1)S(1)} fusion(bf16[1088,1536]{1,0:T(8,128)(2,1)S(1)} %copy-done.32, bf16[2048,1536]{1,0:T(8,128)(2,1)} %all-gather.8.cloned.1.call-done), kind=kOutput, calls=%fused_computation.6 | convolution fusion | flops 6847332352 | bytes 14090240 | tf_op jit(solution)/shard_map/dot_general | solution.py:642
  551.7 5.8 shard_map.225
  560.0 14.2 %collective-permute-done.48 = bf16[2,136,2048]{2,1,0:T(8,128)(2,1)} collective-permute-done((bf16[2,136,2048]{2,1,0:T(8,128)(2,1)}, bf16[2,136,2048]{2,1,0:T(8,128)(2,1)}, u32[]{:S(2)}, u32[]{:S(2)}) %collective-permute-start.48) | collective-permute-done | bytes 1114144 | tf_op jit(solution)/shard_map/ppermute | solution.py:20
  582.7 51.9 %reduce-scatter.12.cloned.1.call-done = bf16[176,2048]{1,0:T(8,128)(2,1)} async-done(((bf16[1408,2048]{1,0:T(8,128)(2,1)}), bf16[176,2048]{1,0:T(8,128)(2,1)}) %reduce-scatter.12.cloned.1.call-update) | async-done | bytes 720912 | tf_op jit(solution)/shard_map/reduce_scatter | solution.py:237
  635.4 5.9 shard_map.226
  668.5 17.7 %collective-permute-done.64 = bf16[1,256,1536]{2,1,0:T(8,128)(2,1)} collective-permute-done((bf16[1,256,1536]{2,1,0:T(8,128)(2,1)S(1)}, bf16[1,256,1536]{2,1,0:T(8,128)(2,1)}, u32[]{:S(2)}, u32[]{:S(2)}) %collective-permute-start.64) | collective-permute-done | bytes 786464 | tf_op jit(solution)/shard_map/ppermute | solution.py:20
  704.1 5.9 shard_map.227
  (551 shorter events, 342.1 us)
Async XLA Ops:
  7.2 31.8 %all-gather.6.cloned.1.call-start = ((), (), s32[]{:S(2)}) async-start(), calls=%async_computation.5 | async-start | bytes 1310720 | tf_op jit(solution)/shard_map/all_gather | solution.py:679
  9.3 102.5 %all-gather.8.cloned.1.call-start = ((), (), s32[]{:S(2)}) async-start(), calls=%async_computation.6 | async-start | bytes 7077888 | tf_op jit(solution)/shard_map/all_gather | solution.py:233
  41.3 203.1 %all-gather.10.cloned.1.call-start = ((), (), s32[]{:S(2)}) async-start(), calls=%async_computation.7 | async-start | bytes 6488064 | tf_op jit(solution)/shard_map/all_gather | solution.py:233
  61.4 210.6 %all-gather.14.cloned.1.call-start = ((), (), s32[]{:S(2)}) async-start(), calls=%async_computation.9 | async-start | bytes 6488064 | tf_op jit(solution)/shard_map/all_gather | solution.py:233
  63.5 81.4 %collective-permute-start.13 = (bf16[256,1408]{1,0:T(8,128)(2,1)}, bf16[256,1408]{1,0:T(8,128)(2,1)}, u32[]{:S(2)}, u32[]{:S(2)}) collective-permute-start(bf16[256,1408]{1,0:T(8,128)(2,1)} %concatenate.265), channel_id=1, source_target_pairs={{0,1},{9,8},{2,3},{11,10},{4,5},{13,12},{6,7},{15,14},{16,17},{25,... | collective-permute-start | bytes 2162696 | tf_op jit(solution)/shard_map/ppermute | solution.py:192
  74.4 33.8 %collective-permute-start.6 = (bf16[1,256,1024]{2,1,0:T(8,128)(2,1)S(1)}, bf16[1,256,1024]{2,1,0:T(8,128)(2,1)S(1)}, u32[]{:S(2)}, u32[]{:S(2)}) collective-permute-start(bf16[1,256,1024]{2,1,0:T(8,128)(2,1)S(1)} %get-tuple-element.598), channel_id=1, source_target_pairs={{0,1},{1,0},{2,3},{3,2},{4,5},{5,4},{6,7},{7,6},{8,9},{9,8},{10,11... | collective-permute-start | bytes 1572872 | tf_op jit(solution)/shard_map/ppermute | solution.py:20
  77.3 30.8 %collective-permute-start.7 = (bf16[1,256,1024]{2,1,0:T(8,128)(2,1)S(1)}, bf16[1,256,1024]{2,1,0:T(8,128)(2,1)S(1)}, u32[]{:S(2)}, u32[]{:S(2)}) collective-permute-start(bf16[1,256,1024]{2,1,0:T(8,128)(2,1)S(1)} %get-tuple-element.600), channel_id=1, source_target_pairs={{0,16},{16,0},{1,17},{17,1},{2,18},{18,2},{3,19},{19,3},{4,20},{20... | collective-permute-start | bytes 1572872 | tf_op jit(solution)/shard_map/ppermute | solution.py:20
  147.2 148.5 %all-gather.12.cloned.1.call-start = ((), (), s32[]{:S(2)}) async-start(), calls=%async_computation.8 | async-start | bytes 6488064 | tf_op jit(solution)/shard_map/all_gather | solution.py:233
  153.1 52.0 %collective-permute-start.17 = (bf16[2048,1024]{1,0:T(8,128)(2,1)}, bf16[2048,1024]{1,0:T(8,128)(2,1)}, u32[]{:S(2)}, u32[]{:S(2)}) collective-permute-start(bf16[2048,1024]{1,0:T(8,128)(2,1)} %bitcast.52), channel_id=1, source_target_pairs={{0,8},{8,0},{1,9},{9,1},{2,10},{10,2},{3,11},{11,3},{4,12},{12,4},... | collective-permute-start | bytes 12582920 | tf_op jit(solution)/shard_map/ppermute | solution.py:20
  153.2 36.2 %collective-permute-start.20 = (bf16[256,1408]{1,0:T(8,128)(2,1)}, bf16[256,1408]{1,0:T(8,128)(2,1)S(1)}, u32[]{:S(2)}, u32[]{:S(2)}) collective-permute-start(bf16[256,1408]{1,0:T(8,128)(2,1)} %concatenate.267), channel_id=1, source_target_pairs={{0,1},{9,8},{2,3},{11,10},{4,5},{13,12},{6,7},{15,14},{16,17},{25,... | collective-permute-start | bytes 2162696 | tf_op jit(solution)/shard_map/ppermute | solution.py:192
  193.1 241.0 %reduce-scatter.8.cloned.1.call-start = ((), (), s32[]{:S(2)}) async-start(), calls=%async_computation.11 | async-start | bytes 6488064 | tf_op jit(solution)/shard_map/reduce_scatter | solution.py:237
  196.6 45.1 %collective-permute-start.25 = (bf16[2,1,128,2048]{3,2,0,1:T(8,128)(2,1)S(1)}, bf16[2,1,128,2048]{3,2,0,1:T(8,128)(2,1)S(1)}, u32[]{:S(2)}, u32[]{:S(2)}) collective-permute-start(bf16[2,1,128,2048]{3,2,0,1:T(8,128)(2,1)S(1)} %bitcast.415), channel_id=1, source_target_pairs={{0,16},{16,0},{1,17},{17,1},{2,18},{18,2},{3,19},{19,3},{4,20},{20... | collective-permute-start | bytes 3145736 | tf_op jit(solution)/shard_map/ppermute | solution.py:20
  198.5 43.2 %collective-permute-start.26 = (bf16[2,1,128,2048]{3,2,0,1:T(8,128)(2,1)S(1)}, bf16[2,1,128,2048]{3,2,0,1:T(8,128)(2,1)S(1)}, u32[]{:S(2)}, u32[]{:S(2)}) collective-permute-start(bf16[2,1,128,2048]{3,2,0,1:T(8,128)(2,1)S(1)} %pad_maximum_fusion.21), channel_id=1, source_target_pairs={{0,1},{1,0},{2,3},{3,2},{4,5},{5,4},{6,7},{7,6},{8,9},{9,8},{10,11... | collective-permute-start | bytes 3145736 | tf_op jit(solution)/shard_map/ppermute | solution.py:20
  295.6 138.6 %reduce-scatter.6.cloned.1.call-start = ((), (), s32[]{:S(2)}) async-start(), calls=%async_computation.10 | async-start | bytes 6488064 | tf_op jit(solution)/shard_map/reduce_scatter | solution.py:237
  343.9 235.7 %reduce-scatter.10.cloned.1.call-start = ((), (), s32[]{:S(2)}) async-start(), calls=%async_computation.12 | async-start | bytes 7077888 | tf_op jit(solution)/shard_map/reduce_scatter | solution.py:237
  374.7 108.2 %collective-permute-start.29 = (bf16[2,128,2048]{2,1,0:T(8,128)(2,1)}, bf16[2,128,2048]{2,1,0:T(8,128)(2,1)}, u32[]{:S(2)}, u32[]{:S(2)}) collective-permute-start(bf16[2,128,2048]{2,1,0:T(8,128)(2,1)} %get-tuple-element.760), channel_id=1, source_target_pairs={{0,1},{1,0},{2,3},{3,2},{4,5},{5,4},{6,7},{7,6},{8,9},{9,8},{10,11... | collective-permute-start | bytes 3145736 | tf_op jit(solution)/shard_map/ppermute | solution.py:20
  375.9 107.0 %collective-permute-start.30 = (bf16[2,128,2048]{2,1,0:T(8,128)(2,1)}, bf16[2,128,2048]{2,1,0:T(8,128)(2,1)}, u32[]{:S(2)}, u32[]{:S(2)}) collective-permute-start(bf16[2,128,2048]{2,1,0:T(8,128)(2,1)} %bitcast.114), channel_id=1, source_target_pairs={{0,16},{16,0},{1,17},{17,1},{2,18},{18,2},{3,19},{19,3},{4,20},{20... | collective-permute-start | bytes 3145736 | tf_op jit(solution)/shard_map/ppermute | solution.py:20
  434.1 41.1 %collective-permute-start.38 = (bf16[2,1,128,2048]{3,2,0,1:T(8,128)(2,1)}, bf16[2,1,128,2048]{3,2,0,1:T(8,128)(2,1)}, u32[]{:S(2)}, u32[]{:S(2)}) collective-permute-start(bf16[2,1,128,2048]{3,2,0,1:T(8,128)(2,1)} %pad_maximum_fusion.24), channel_id=1, source_target_pairs={{0,16},{16,0},{1,17},{17,1},{2,18},{18,2},{3,19},{19,3},{4,20},{20... | collective-permute-start | bytes 3145736 | tf_op jit(solution)/shard_map/ppermute | solution.py:20
  436.6 38.6 %collective-permute-start.39 = (bf16[2,1,128,2048]{3,2,0,1:T(8,128)(2,1)}, bf16[2,1,128,2048]{3,2,0,1:T(8,128)(2,1)}, u32[]{:S(2)}, u32[]{:S(2)}) collective-permute-start(bf16[2,1,128,2048]{3,2,0,1:T(8,128)(2,1)} %bitcast.411), channel_id=1, source_target_pairs={{0,1},{1,0},{2,3},{3,2},{4,5},{5,4},{6,7},{7,6},{8,9},{9,8},{10,11... | collective-permute-start | bytes 3145736 | tf_op jit(solution)/shard_map/ppermute | solution.py:20
  437.7 37.5 %collective-permute-start.43 = (bf16[256,1408]{1,0:T(8,128)(2,1)}, bf16[256,1408]{1,0:T(8,128)(2,1)S(1)}, u32[]{:S(2)}, u32[]{:S(2)}) collective-permute-start(bf16[256,1408]{1,0:T(8,128)(2,1)} %reduce-scatter.8.cloned.1.call-done), channel_id=1, source_target_pairs={{8,1},{1,8},{10,3},{3,10},{12,5},{5,12},{14,7},{7,14},{24,17},{17,... | collective-permute-start | bytes 2162696 | tf_op jit(solution)/shard_map/ppermute | solution.py:262
  499.7 134.9 %reduce-scatter.12.cloned.1.call-start = ((), (), s32[]{:S(2)}) async-start(), calls=%async_computation.13 | async-start | bytes 6488064 | tf_op jit(solution)/shard_map/reduce_scatter | solution.py:237
  500.5 202.4 %reduce-scatter.14.cloned.1.call-start = ((), (), s32[]{:S(2)}) async-start(), calls=%async_computation.14 | async-start | bytes 2359296 | tf_op jit(solution)/shard_map/reduce_scatter | solution.py:237
  528.5 29.0 %collective-permute-start.49 = (bf16[1,256,1408]{2,1,0:T(8,128)(2,1)S(1)}, bf16[1,256,1408]{2,1,0:T(8,128)(2,1)}, u32[]{:S(2)}, u32[]{:S(2)}) collective-permute-start(bf16[1,256,1408]{2,1,0:T(8,128)(2,1)S(1)} %fusion.66), channel_id=1, source_target_pairs={{0,16},{16,0},{1,17},{17,1},{2,18},{18,2},{3,19},{19,3},{4,20},{20... | collective-permute-start | bytes 2162696 | tf_op jit(solution)/shard_map/ppermute | solution.py:20
  530.5 29.5 %collective-permute-start.47 = (bf16[2,136,2048]{2,1,0:T(8,128)(2,1)}, bf16[2,136,2048]{2,1,0:T(8,128)(2,1)}, u32[]{:S(2)}, u32[]{:S(2)}) collective-permute-start(bf16[2,136,2048]{2,1,0:T(8,128)(2,1)} %get-tuple-element.887), channel_id=1, source_target_pairs={{0,1},{1,0},{2,3},{3,2},{4,5},{5,4},{6,7},{7,6},{8,9},{9,8},{10,11... | collective-permute-start | bytes 3342344 | tf_op jit(solution)/shard_map/ppermute | solution.py:20
  530.5 43.7 %collective-permute-start.48 = (bf16[2,136,2048]{2,1,0:T(8,128)(2,1)}, bf16[2,136,2048]{2,1,0:T(8,128)(2,1)}, u32[]{:S(2)}, u32[]{:S(2)}) collective-permute-start(bf16[2,136,2048]{2,1,0:T(8,128)(2,1)} %bitcast.174), channel_id=1, source_target_pairs={{0,16},{16,0},{1,17},{17,1},{2,18},{18,2},{3,19},{19,3},{4,20},{20... | collective-permute-start | bytes 3342344 | tf_op jit(solution)/shard_map/ppermute | solution.py:20
  574.2 60.4 %collective-permute-start.56 = (bf16[2,1,256,1408]{3,2,0,1:T(8,128)(2,1)}, bf16[2,1,256,1408]{3,2,0,1:T(8,128)(2,1)}, u32[]{:S(2)}, u32[]{:S(2)}) collective-permute-start(bf16[2,1,256,1408]{3,2,0,1:T(8,128)(2,1)} %pad_maximum_fusion.14), channel_id=1, source_target_pairs={{0,8},{8,0},{1,9},{9,1},{2,10},{10,2},{3,11},{11,3},{4,12},{12,4},... | collective-permute-start | bytes 4325384 | tf_op jit(solution)/shard_map/ppermute | solution.py:20
  579.6 61.7 %collective-permute-start.55 = (bf16[256,1536]{1,0:T(8,128)(2,1)}, bf16[256,1536]{1,0:T(8,128)(2,1)S(1)}, u32[]{:S(2)}, u32[]{:S(2)}) collective-permute-start(bf16[256,1536]{1,0:T(8,128)(2,1)} %reduce-scatter.10.cloned.1.call-done), channel_id=1, source_target_pairs={{8,1},{1,8},{10,3},{3,10},{12,5},{5,12},{14,7},{7,14},{24,17},{17,... | collective-permute-start | bytes 2359304 | tf_op jit(solution)/shard_map/ppermute | solution.py:262
  581.6 63.0 %collective-permute-start.53 = (bf16[136,2048]{1,0:T(8,128)(2,1)}, bf16[136,2048]{1,0:T(8,128)(2,1)}, u32[]{:S(2)}, u32[]{:S(2)}) collective-permute-start(bf16[136,2048]{1,0:T(8,128)(2,1)} %get-tuple-element.938), channel_id=1, source_target_pairs={{0,16},{16,0},{1,17},{17,1},{2,18},{18,2},{3,19},{19,3},{4,20},{20... | collective-permute-start | bytes 1671176 | tf_op jit(solution)/shard_map/ppermute | solution.py:20
  582.7 61.8 %collective-permute-start.54 = (bf16[136,2048]{1,0:T(8,128)(2,1)}, bf16[136,2048]{1,0:T(8,128)(2,1)}, u32[]{:S(2)}, u32[]{:S(2)}) collective-permute-start(bf16[136,2048]{1,0:T(8,128)(2,1)} %get-tuple-element.940), channel_id=1, source_target_pairs={{0,1},{1,0},{2,3},{3,2},{4,5},{5,4},{6,7},{7,6},{8,9},{9,8},{10,11... | collective-permute-start | bytes 1671176 | tf_op jit(solution)/shard_map/ppermute | solution.py:20
  582.7 69.4 %collective-permute-start.58 = (f32[45,512]{1,0:T(8,128)S(1)}, f32[45,512]{1,0:T(8,128)}, u32[]{:S(2)}, u32[]{:S(2)}) collective-permute-start(f32[45,512]{1,0:T(8,128)S(1)} %add.619), channel_id=1, source_target_pairs={{0,2},{2,4},{4,6},{6,0},{1,3},{3,5},{5,7},{7,1},{8,10},{10,12},{12... | collective-permute-start | bytes 276488 | tf_op jit(solution)/shard_map/ppermute | solution.py:20
  653.3 43.6 %collective-permute-start.69 = (bf16[1,176,2048]{2,1,0:T(8,128)(2,1)}, bf16[1,176,2048]{2,1,0:T(8,128)(2,1)}, u32[]{:S(2)}, u32[]{:S(2)}) collective-permute-start(bf16[1,176,2048]{2,1,0:T(8,128)(2,1)} %bitcast.200), channel_id=1, source_target_pairs={{0,16},{16,0},{1,17},{17,1},{2,18},{18,2},{3,19},{19,3},{4,20},{20... | collective-permute-start | bytes 2162696 | tf_op jit(solution)/shard_map/ppermute | solution.py:20
  667.5 29.3 %collective-permute-start.62 = (f32[4,512]{1,0:T(4,128)S(1)}, f32[4,512]{1,0:T(4,128)S(1)}, u32[]{:S(2)}, u32[]{:S(2)}) collective-permute-start(f32[4,512]{1,0:T(4,128)S(1)} %reshape.783), channel_id=1, source_target_pairs={{0,8},{8,0},{1,9},{9,1},{2,10},{10,2},{3,11},{11,3},{4,12},{12,4},... | collective-permute-start | bytes 24584 | tf_op jit(solution)/shard_map/ppermute | solution.py:20
  (127 other events, 1417.3 us)
Sparse Core Ops, SparseCore 0:
  10.2 28.8 all-gather.5
  41.5 63.0 all-gather.7
  106.2 62.2 all-gather.9
  170.6 58.9 all-gather.13
  231.1 59.0 all-gather.11
  295.7 65.9 reduce-scatter.7
  364.5 63.4 reduce-scatter.5
  499.8 67.3 reduce-scatter.9
  569.6 65.0 reduce-scatter.11
  653.4 32.7 reduce-scatter.13

commit v18 on v17

--- a/solution.py
+++ b/solution.py
@@ -960,9 +960,9 @@
     gate_held = run(stacked, gate_held, gate_got)
     gate_got = moved(gate_held, "c", -1)
     one_back.turn(line)
-    in_got = owner_moves(run(owner_parts, in_mine))
     down_held = run(lambda v: v[None], down_mine)
     down_got = moved(down_held, "y", -1)
+    in_got = owner_moves(run(owner_parts, in_mine))
     grad_gate_weight = run(column_whole, gate_held, gate_got)
     in_held = run(owner_held, in_got)
     in_got = moved(in_held, "y", -1)

time: 745 us -> 710 us (0.953)
  waiting for transfers between devices: 230 us -> 178 us
  starting transfers between devices: 94.4 us -> 114 us
    reduce_scatter x5, waiting for transfers between devices: 51.9 us -> 0.01 us  [scatter_tile(): return lax.psum_scatter(term, ('z', 'c'), scatter_dimension=0, tiled=True)]
    ppermute x53, starting transfers between devices: 49.2 us -> 62 us  [turned(): lax.ppermute(value, axis, [(i, (i + by) % length) for i in range(length)])]
    unnamed x166 -> x164, local copies, waits for them, and re-layouts: 16.3 us -> 18.1 us
  transfers between devices with their start and end apart: 86 -> 86, of which waited for: 33 -> 31; matrix products, arithmetic and copies ran while one was open for 41% -> 44% of each run, Pallas kernels for 8% -> 8%
where the time goes in v18:
time: 710 us; the launch traced here: 699 us
  waiting for transfers between devices  178 us (25%)
  matrix products  141 us (20%)
  other arithmetic  121 us (17%)
  starting transfers between devices  114 us (16%)
  local copies, waits for them, and re-layouts  71.7 us (10%)
  Pallas kernels  56.4 us (8%)
  between operations  16.6 us (2%)
    ppermute x53, waiting for transfers between devices, turned(): lax.ppermute(value, axis, [(i, (i + by) % length) for i in range(length)])  138 us
    ppermute x53, starting transfers between devices, turned(): lax.ppermute(value, axis, [(i, (i + by) % length) for i in range(length)])  62 us
    dot_general x6, matrix products, dot(): return jnp.dot(a, b, preferred_element_type=wide).astype(kind)  55.4 us
    dot_general x6, matrix products, dot_t(): lax.dot_general(a, b, (((1,), (1,)), ((), ())), preferred_element_type=wide)  45.8 us
    dot_general x5, matrix products, dot_w(): lax.dot_general(a, b, (((0,), (0,)), ((), ())), preferred_element_type=wide)  39.7 us
    pallas_call x4, Pallas kernels, conv_call(): pl.pallas_call(kernel, out_shape=results, grid_spec=pltpu.PrefetchScalarG...  35.3 us
    ppermute x3, starting transfers between devices, owner_moves(): got.append(lax.ppermute(parts[d], ('c', 'x'), pairs))  21 us
    unnamed x164, local copies, waits for them, and re-layouts  18.1 us
  transfers between devices with their start and end apart: 86, of which 31 were waited for; matrix products, arithmetic and copies ran while one was open for 44% of the time, Pallas kernels for 8%

profile of v18, /device:TPU:9, one launch (start us, length us, event | category | flops | bytes accessed | tf_op | source)
XLA Modules:
  0.0 699.1 jit_solution(18391050136065591510)
XLA Ops:
  33.7 5.3 all-gather.6.cloned.1.call-done
  43.9 10.9 %collective-permute-done.1 = bf16[1,136,2048]{2,1,0:T(8,128)(2,1)} collective-permute-done((bf16[1,136,2048]{2,1,0:T(8,128)(2,1)S(1)}, bf16[1,136,2048]{2,1,0:T(8,128)(2,1)}, u32[]{:S(2)}, u32[]{:S(2)}) %collective-permute-start.1) | collective-permute-done | bytes 557088 | tf_op jit(solution)/shard_map/ppermute | solution.py:20
  77.5 8.4 %collective-permute-done.4 = bf16[2,1,136,2048]{3,2,0,1:T(8,128)(2,1)S(1)} collective-permute-done((bf16[2,1,136,2048]{3,2,0,1:T(8,128)(2,1)}, bf16[2,1,136,2048]{3,2,0,1:T(8,128)(2,1)S(1)}, u32[]{:S(2)}, u32[]{:S(2)}) %collective-permute-start.4) | collective-permute-done | bytes 1114144 | tf_op jit(solution)/shard_map/ppermute | solution.py:20
  92.6 15.6 %collective-permute-done.6 = bf16[1,256,1024]{2,1,0:T(8,128)(2,1)S(1)} collective-permute-done((bf16[1,256,1024]{2,1,0:T(8,128)(2,1)S(1)}, bf16[1,256,1024]{2,1,0:T(8,128)(2,1)S(1)}, u32[]{:S(2)}, u32[]{:S(2)}) %collective-permute-start.6) | collective-permute-done | bytes 524320 | tf_op jit(solution)/shard_map/ppermute | solution.py:20
  111.8 10.8 %convolution_convert_fusion.4 = bf16[1088,1536]{1,0:T(8,128)(2,1)S(1)} fusion(bf16[1088,2048]{1,0:T(8,128)(2,1)} %bitcast.387, bf16[2048,1536]{1,0:T(8,128)(2,1)} %all-gather.8.cloned.1.call-done), kind=kOutput, calls=%fused_computation.5 | convolution fusion | flops 6846775296 | bytes 14090240 | tf_op jit(solution)/shard_map/dot_general | solution.py:638
  122.6 13.3 %collective-permute-done.8 = bf16[2,1,256,1024]{3,2,0,1:T(8,128)(2,1)} collective-permute-done((bf16[2,1,256,1024]{3,2,0,1:T(8,128)(2,1)S(1)}, bf16[2,1,256,1024]{3,2,0,1:T(8,128)(2,1)}, u32[]{:S(2)}, u32[]{:S(2)}) %collective-permute-start.8) | collective-permute-done | bytes 1048608 | tf_op jit(solution)/shard_map/ppermute | solution.py:20
  165.1 7.1 %collective-permute-start.18 = (bf16[1,128,2048]{2,1,0:T(8,128)(2,1)S(1)}, bf16[1,128,2048]{2,1,0:T(8,128)(2,1)}, u32[]{:S(2)}, u32[]{:S(2)}) collective-permute-start(bf16[1,128,2048]{2,1,0:T(8,128)(2,1)S(1)} %get-tuple-element.667), channel_id=1, source_target_pairs={{0,1},{1,0},{2,3},{3,2},{4,5},{5,4},{6,7},{7,6},{8,9},{9,8},{10,11... | collective-permute-start | bytes 1572872 | tf_op jit(solution)/shard_map/ppermute | solution.py:20
  176.6 8.8 %shard_map.222 = bf16[4,2,1,128,512]{4,3,2,1,0:T(8,128)(2,1)} custom-call(s32[1]{0:T(128)} %bitcast.39.place_ref, bf16[4,2,1,128,512]{4,3,2,1,0:T(8,128)(2,1)} %fusion.49.signal_ref, f32[16,512]{1,0:T(8,128)} %maximum_bitcast_fusion.11.decay_ref, f32[16,512]{1,0:T(8,128)} %maximum_bitcast_fusion.12.residue_ref, f32[4,16,512]{2,1,0:T(8,128)} %multiply_add_fusion.2.start_ref), custom_call_target="tpu_custom_call" | custom-call | flops 33554432 | bytes 2293760 | tf_op jit(solution)/shard_map/pallas_call | solution.py:555
  216.9 20.9 %collective-permute-done.21 = bf16[1,128,2048]{2,1,0:T(8,128)(2,1)S(1)} collective-permute-done((bf16[1,128,2048]{2,1,0:T(8,128)(2,1)S(1)}, bf16[1,128,2048]{2,1,0:T(8,128)(2,1)S(1)}, u32[]{:S(2)}, u32[]{:S(2)}) %collective-permute-start.21) | collective-permute-done | bytes 524320 | tf_op jit(solution)/shard_map/ppermute | solution.py:20
  245.1 12.0 %fusion.122 = f32[1024,1408]{1,0:T(8,128)} fusion(bf16[1024,2048]{1,0:T(8,128)(2,1)} %bitcast.397, bf16[1408,2048]{1,0:T(8,128)(2,1)} %all-gather.10.cloned.1.call-done), kind=kOutput, calls=%fused_computation.420 | convolution fusion | flops 5905580032 | bytes 15728640 | tf_op jit(solution)/shard_map/dot_general | solution.py:642
  257.1 10.9 %collective-permute-done.23 = bf16[2,1,128,2048]{3,2,0,1:T(8,128)(2,1)S(1)} collective-permute-done((bf16[2,1,128,2048]{3,2,0,1:T(8,128)(2,1)}, bf16[2,1,128,2048]{3,2,0,1:T(8,128)(2,1)S(1)}, u32[]{:S(2)}, u32[]{:S(2)}) %collective-permute-start.23) | collective-permute-done | bytes 1048608 | tf_op jit(solution)/shard_map/ppermute | solution.py:20
  272.1 13.3 %multiply_convert_fusion.2 = (bf16[1024,1408]{1,0:T(8,128)(2,1)S(1)}, f32[1024,1408]{1,0:T(8,128)}) fusion(f32[1024,1408]{1,0:T(8,128)} %fusion.122, bf16[1024,2048]{1,0:T(8,128)(2,1)} %bitcast.400, bf16[2048,1408]{1,0:T(8,128)(2,1)} %all-gather.14.cloned.1.call-done), kind=kOutput, calls=%fused_computation.10 | convolution fusion | flops 5914230784 | bytes 24379392 | tf_op jit(solution)/shard_map/dot_general | solution.py:638
  287.0 8.7 %convolution_convert_fusion.3 = bf16[2048,1408]{1,0:T(8,128)(2,1)} fusion(bf16[1024,2048]{1,0:T(8,128)(2,1)S(1)} %bitcast.402, bf16[1024,1408]{1,0:T(8,128)(2,1)S(1)} %get-tuple-element.738), kind=kOutput, calls=%fused_computation.4 | convolution fusion | flops 5908463616 | bytes 12845056 | tf_op jit(solution)/shard_map/dot_general | solution.py:646
  295.7 15.2 %multiply_convert_fusion = (bf16[1024,1408]{1,0:T(8,128)(2,1)S(1)}, bf16[1024,1408]{1,0:T(8,128)(2,1)}) fusion(f32[1024,1408]{1,0:T(8,128)} %get-tuple-element.728, f32[1024,1408]{1,0:T(8,128)} %fusion.122, bf16[1024,2048]{1,0:T(8,128)(2,1)} %bitcast.401, bf16[2048,1408]{1,0:T(8,128)(2,1)} %all-gather.12.cloned.1.call-done), kind=kOutput, calls=%fused_computation.7 | convolution fusion | flops 5924323328 | bytes 27262976 | tf_op jit(solution)/shard_map/dot_general | solution.py:638
  312.6 8.9 %fusion.123 = f32[1024,2048]{1,0:T(8,128)S(1)} fusion(bf16[1024,1408]{1,0:T(8,128)(2,1)S(1)} %get-tuple-element.747, bf16[2048,1408]{1,0:T(8,128)(2,1)} %all-gather.14.cloned.1.call-done), kind=kOutput, calls=%fused_computation.421 | convolution fusion | flops 5905580032 | bytes 17039360 | tf_op jit(solution)/shard_map/dot_general | solution.py:642
  321.5 8.4 %add_convert_fusion = bf16[1024,2048]{1,0:T(8,128)(2,1)S(1)} fusion(f32[1024,2048]{1,0:T(8,128)S(1)} %fusion.123, bf16[1024,1408]{1,0:T(8,128)(2,1)} %copy-done.69, bf16[2048,1408]{1,0:T(8,128)(2,1)S(1)} %copy-done.65), kind=kOutput, calls=%fused_computation | convolution fusion | flops 5909774336 | bytes 21233664 | tf_op jit(solution)/shard_map/dot_general | solution.py:642
  335.1 8.7 %convolution_convert_fusion.2 = bf16[2048,1408]{1,0:T(8,128)(2,1)} fusion(bf16[1024,2048]{1,0:T(8,128)(2,1)S(1)} %bitcast.403, bf16[1024,1408]{1,0:T(8,128)(2,1)S(1)} %copy-done.68), kind=kOutput, calls=%fused_computation.3 | convolution fusion | flops 5908463616 | bytes 12845056 | tf_op jit(solution)/shard_map/dot_general | solution.py:646
  343.9 11.8 %collective-permute-done.27 = bf16[2,128,2048]{2,1,0:T(8,128)(2,1)} collective-permute-done((bf16[2,128,2048]{2,1,0:T(8,128)(2,1)}, bf16[2,128,2048]{2,1,0:T(8,128)(2,1)}, u32[]{:S(2)}, u32[]{:S(2)}) %collective-permute-start.27) | collective-permute-done | bytes 1048608 | tf_op jit(solution)/shard_map/ppermute | solution.py:20
  360.9 9.1 %convolution_convert_fusion.6 = bf16[1024,2048]{1,0:T(8,128)(2,1)S(1)} fusion(bf16[1024,1408]{1,0:T(8,128)(2,1)S(1)} %copy-done.66, bf16[1408,2048]{1,0:T(8,128)(2,1)} %all-gather.10.cloned.1.call-done), kind=kOutput, calls=%fused_computation.26 | convolution fusion | flops 5907677184 | bytes 12845056 | tf_op jit(solution)/shard_map/dot_general | solution.py:638
  397.2 8.1 %convolution_convert_fusion.1 = bf16[1408,2048]{1,0:T(8,128)(2,1)} fusion(bf16[1024,1408]{1,0:T(8,128)(2,1)S(1)} %copy-done.66, bf16[1024,2048]{1,0:T(8,128)(2,1)S(1)} %bitcast.398), kind=kOutput, calls=%fused_computation.2 | convolution fusion | flops 5908463616 | bytes 12845056 | tf_op jit(solution)/shard_map/dot_general | solution.py:646
  437.7 16.8 %collective-permute-start.43 = (bf16[256,1408]{1,0:T(8,128)(2,1)}, bf16[256,1408]{1,0:T(8,128)(2,1)S(1)}, u32[]{:S(2)}, u32[]{:S(2)}) collective-permute-start(bf16[256,1408]{1,0:T(8,128)(2,1)} %reduce-scatter.8.cloned.1.call-done), channel_id=1, source_target_pairs={{8,1},{1,8},{10,3},{3,10},{12,5},{5,12},{14,7},{7,14},{24,17},{17,... | collective-permute-start | bytes 2162696 | tf_op jit(solution)/shard_map/ppermute | solution.py:262
  460.9 16.8 %shard_map.224 = (bf16[4,2,1,128,512]{4,3,2,1,0:T(8,128)(2,1)}, f32[16,512]{1,0:T(8,128)}, f32[16,512]{1,0:T(8,128)}) custom-call(s32[1]{0:T(128)} %bitcast.39.place_ref, bf16[4,2,1,128,512]{4,3,2,1,0:T(8,128)(2,1)} %fusion.49.signal_ref, bf16[4,2,1,128,512]{4,3,2,1,0:T(8,128)(2,1)} %get-tuple-element.823.signal_ref.grad_ref, ...), custom_call_target="tpu_custom_call" | custom-call | flops 100663296 | bytes 4521984 | tf_op jit(solution)/shard_map/pallas_call | solution.py:555
  495.0 10.5 %convolution_convert_fusion = bf16[2048,1536]{1,0:T(8,128)(2,1)} fusion(bf16[1088,2048]{1,0:T(8,128)(2,1)S(1)} %bitcast.390, bf16[1088,1024]{1,0:T(8,128)(2,1)S(1)} %bitcast.379, bf16[1088,512]{1,0:T(8,128)(2,1)S(1)} %bitcast.386), kind=kOutput, calls=%fused_computation.1 | convolution fusion | flops 6854934528 | bytes 14090240 | tf_op jit(solution)/shard_map/dot_general | solution.py:646
  515.7 5.9 collective-permute-done.46
  521.9 9.3 %convolution_convert_fusion.5 = bf16[1088,2048]{1,0:T(8,128)(2,1)S(1)} fusion(bf16[1088,1536]{1,0:T(8,128)(2,1)S(1)} %copy-done.32, bf16[2048,1536]{1,0:T(8,128)(2,1)} %all-gather.8.cloned.1.call-done), kind=kOutput, calls=%fused_computation.6 | convolution fusion | flops 6847332352 | bytes 14090240 | tf_op jit(solution)/shard_map/dot_general | solution.py:642
  557.3 5.8 shard_map.225
  565.6 14.5 %collective-permute-done.48 = bf16[2,136,2048]{2,1,0:T(8,128)(2,1)} collective-permute-done((bf16[2,136,2048]{2,1,0:T(8,128)(2,1)}, bf16[2,136,2048]{2,1,0:T(8,128)(2,1)}, u32[]{:S(2)}, u32[]{:S(2)}) %collective-permute-start.48) | collective-permute-done | bytes 1114144 | tf_op jit(solution)/shard_map/ppermute | solution.py:20
  594.8 5.9 shard_map.226
  617.1 5.9 collective-permute-start.57
  636.2 14.3 %collective-permute-done.64 = bf16[1,256,1536]{2,1,0:T(8,128)(2,1)} collective-permute-done((bf16[1,256,1536]{2,1,0:T(8,128)(2,1)S(1)}, bf16[1,256,1536]{2,1,0:T(8,128)(2,1)}, u32[]{:S(2)}, u32[]{:S(2)}) %collective-permute-start.64) | collective-permute-done | bytes 786464 | tf_op jit(solution)/shard_map/ppermute | solution.py:20
  662.9 5.9 collective-permute-start.66
  669.5 5.9 shard_map.227
  (549 shorter events, 348.7 us)
Async XLA Ops:
  7.2 31.8 %all-gather.6.cloned.1.call-start = ((), (), s32[]{:S(2)}) async-start(), calls=%async_computation.5 | async-start | bytes 1310720 | tf_op jit(solution)/shard_map/all_gather | solution.py:679
  9.3 102.5 %all-gather.8.cloned.1.call-start = ((), (), s32[]{:S(2)}) async-start(), calls=%async_computation.6 | async-start | bytes 7077888 | tf_op jit(solution)/shard_map/all_gather | solution.py:233
  41.3 203.2 %all-gather.10.cloned.1.call-start = ((), (), s32[]{:S(2)}) async-start(), calls=%async_computation.7 | async-start | bytes 6488064 | tf_op jit(solution)/shard_map/all_gather | solution.py:233
  61.4 210.7 %all-gather.14.cloned.1.call-start = ((), (), s32[]{:S(2)}) async-start(), calls=%async_computation.9 | async-start | bytes 6488064 | tf_op jit(solution)/shard_map/all_gather | solution.py:233
  63.5 81.4 %collective-permute-start.13 = (bf16[256,1408]{1,0:T(8,128)(2,1)}, bf16[256,1408]{1,0:T(8,128)(2,1)}, u32[]{:S(2)}, u32[]{:S(2)}) collective-permute-start(bf16[256,1408]{1,0:T(8,128)(2,1)} %concatenate.265), channel_id=1, source_target_pairs={{0,1},{9,8},{2,3},{11,10},{4,5},{13,12},{6,7},{15,14},{16,17},{25,... | collective-permute-start | bytes 2162696 | tf_op jit(solution)/shard_map/ppermute | solution.py:192
  74.3 33.8 %collective-permute-start.6 = (bf16[1,256,1024]{2,1,0:T(8,128)(2,1)S(1)}, bf16[1,256,1024]{2,1,0:T(8,128)(2,1)S(1)}, u32[]{:S(2)}, u32[]{:S(2)}) collective-permute-start(bf16[1,256,1024]{2,1,0:T(8,128)(2,1)S(1)} %get-tuple-element.598), channel_id=1, source_target_pairs={{0,1},{1,0},{2,3},{3,2},{4,5},{5,4},{6,7},{7,6},{8,9},{9,8},{10,11... | collective-permute-start | bytes 1572872 | tf_op jit(solution)/shard_map/ppermute | solution.py:20
  77.3 30.9 %collective-permute-start.7 = (bf16[1,256,1024]{2,1,0:T(8,128)(2,1)S(1)}, bf16[1,256,1024]{2,1,0:T(8,128)(2,1)S(1)}, u32[]{:S(2)}, u32[]{:S(2)}) collective-permute-start(bf16[1,256,1024]{2,1,0:T(8,128)(2,1)S(1)} %get-tuple-element.600), channel_id=1, source_target_pairs={{0,16},{16,0},{1,17},{17,1},{2,18},{18,2},{3,19},{19,3},{4,20},{20... | collective-permute-start | bytes 1572872 | tf_op jit(solution)/shard_map/ppermute | solution.py:20
  147.2 148.5 %all-gather.12.cloned.1.call-start = ((), (), s32[]{:S(2)}) async-start(), calls=%async_computation.8 | async-start | bytes 6488064 | tf_op jit(solution)/shard_map/all_gather | solution.py:233
  153.1 52.1 %collective-permute-start.17 = (bf16[2048,1024]{1,0:T(8,128)(2,1)}, bf16[2048,1024]{1,0:T(8,128)(2,1)}, u32[]{:S(2)}, u32[]{:S(2)}) collective-permute-start(bf16[2048,1024]{1,0:T(8,128)(2,1)} %bitcast.52), channel_id=1, source_target_pairs={{0,8},{8,0},{1,9},{9,1},{2,10},{10,2},{3,11},{11,3},{4,12},{12,4},... | collective-permute-start | bytes 12582920 | tf_op jit(solution)/shard_map/ppermute | solution.py:20
  153.1 36.2 %collective-permute-start.20 = (bf16[256,1408]{1,0:T(8,128)(2,1)}, bf16[256,1408]{1,0:T(8,128)(2,1)S(1)}, u32[]{:S(2)}, u32[]{:S(2)}) collective-permute-start(bf16[256,1408]{1,0:T(8,128)(2,1)} %concatenate.267), channel_id=1, source_target_pairs={{0,1},{9,8},{2,3},{11,10},{4,5},{13,12},{6,7},{15,14},{16,17},{25,... | collective-permute-start | bytes 2162696 | tf_op jit(solution)/shard_map/ppermute | solution.py:192
  165.1 28.0 %collective-permute-start.18 = (bf16[1,128,2048]{2,1,0:T(8,128)(2,1)S(1)}, bf16[1,128,2048]{2,1,0:T(8,128)(2,1)}, u32[]{:S(2)}, u32[]{:S(2)}) collective-permute-start(bf16[1,128,2048]{2,1,0:T(8,128)(2,1)S(1)} %get-tuple-element.667), channel_id=1, source_target_pairs={{0,1},{1,0},{2,3},{3,2},{4,5},{5,4},{6,7},{7,6},{8,9},{9,8},{10,11... | collective-permute-start | bytes 1572872 | tf_op jit(solution)/shard_map/ppermute | solution.py:20
  193.1 241.0 %reduce-scatter.8.cloned.1.call-start = ((), (), s32[]{:S(2)}) async-start(), calls=%async_computation.11 | async-start | bytes 6488064 | tf_op jit(solution)/shard_map/reduce_scatter | solution.py:237
  196.6 45.1 %collective-permute-start.25 = (bf16[2,1,128,2048]{3,2,0,1:T(8,128)(2,1)S(1)}, bf16[2,1,128,2048]{3,2,0,1:T(8,128)(2,1)S(1)}, u32[]{:S(2)}, u32[]{:S(2)}) collective-permute-start(bf16[2,1,128,2048]{3,2,0,1:T(8,128)(2,1)S(1)} %bitcast.415), channel_id=1, source_target_pairs={{0,16},{16,0},{1,17},{17,1},{2,18},{18,2},{3,19},{19,3},{4,20},{20... | collective-permute-start | bytes 3145736 | tf_op jit(solution)/shard_map/ppermute | solution.py:20
  198.6 43.2 %collective-permute-start.26 = (bf16[2,1,128,2048]{3,2,0,1:T(8,128)(2,1)S(1)}, bf16[2,1,128,2048]{3,2,0,1:T(8,128)(2,1)S(1)}, u32[]{:S(2)}, u32[]{:S(2)}) collective-permute-start(bf16[2,1,128,2048]{3,2,0,1:T(8,128)(2,1)S(1)} %pad_maximum_fusion.21), channel_id=1, source_target_pairs={{0,1},{1,0},{2,3},{3,2},{4,5},{5,4},{6,7},{7,6},{8,9},{9,8},{10,11... | collective-permute-start | bytes 3145736 | tf_op jit(solution)/shard_map/ppermute | solution.py:20
  295.7 138.5 %reduce-scatter.6.cloned.1.call-start = ((), (), s32[]{:S(2)}) async-start(), calls=%async_computation.10 | async-start | bytes 6488064 | tf_op jit(solution)/shard_map/reduce_scatter | solution.py:237
  343.8 241.6 %reduce-scatter.12.cloned.1.call-start = ((), (), s32[]{:S(2)}) async-start(), calls=%async_computation.13 | async-start | bytes 6488064 | tf_op jit(solution)/shard_map/reduce_scatter | solution.py:237
  374.6 114.1 %collective-permute-start.29 = (bf16[2,128,2048]{2,1,0:T(8,128)(2,1)}, bf16[2,128,2048]{2,1,0:T(8,128)(2,1)}, u32[]{:S(2)}, u32[]{:S(2)}) collective-permute-start(bf16[2,128,2048]{2,1,0:T(8,128)(2,1)} %get-tuple-element.760), channel_id=1, source_target_pairs={{0,1},{1,0},{2,3},{3,2},{4,5},{5,4},{6,7},{7,6},{8,9},{9,8},{10,11... | collective-permute-start | bytes 3145736 | tf_op jit(solution)/shard_map/ppermute | solution.py:20
  375.8 112.9 %collective-permute-start.30 = (bf16[2,128,2048]{2,1,0:T(8,128)(2,1)}, bf16[2,128,2048]{2,1,0:T(8,128)(2,1)}, u32[]{:S(2)}, u32[]{:S(2)}) collective-permute-start(bf16[2,128,2048]{2,1,0:T(8,128)(2,1)} %bitcast.114), channel_id=1, source_target_pairs={{0,16},{16,0},{1,17},{17,1},{2,18},{18,2},{3,19},{19,3},{4,20},{20... | collective-permute-start | bytes 3145736 | tf_op jit(solution)/shard_map/ppermute | solution.py:20
  405.3 180.1 %reduce-scatter.10.cloned.1.call-start = ((), (), s32[]{:S(2)}) async-start(), calls=%async_computation.12 | async-start | bytes 7077888 | tf_op jit(solution)/shard_map/reduce_scatter | solution.py:237
  434.1 46.8 %collective-permute-start.38 = (bf16[2,1,128,2048]{3,2,0,1:T(8,128)(2,1)}, bf16[2,1,128,2048]{3,2,0,1:T(8,128)(2,1)}, u32[]{:S(2)}, u32[]{:S(2)}) collective-permute-start(bf16[2,1,128,2048]{3,2,0,1:T(8,128)(2,1)} %pad_maximum_fusion.24), channel_id=1, source_target_pairs={{0,16},{16,0},{1,17},{17,1},{2,18},{18,2},{3,19},{19,3},{4,20},{20... | collective-permute-start | bytes 3145736 | tf_op jit(solution)/shard_map/ppermute | solution.py:20
  436.3 44.6 %collective-permute-start.39 = (bf16[2,1,128,2048]{3,2,0,1:T(8,128)(2,1)}, bf16[2,1,128,2048]{3,2,0,1:T(8,128)(2,1)}, u32[]{:S(2)}, u32[]{:S(2)}) collective-permute-start(bf16[2,1,128,2048]{3,2,0,1:T(8,128)(2,1)} %bitcast.411), channel_id=1, source_target_pairs={{0,1},{1,0},{2,3},{3,2},{4,5},{5,4},{6,7},{7,6},{8,9},{9,8},{10,11... | collective-permute-start | bytes 3145736 | tf_op jit(solution)/shard_map/ppermute | solution.py:20
  437.7 43.2 %collective-permute-start.43 = (bf16[256,1408]{1,0:T(8,128)(2,1)}, bf16[256,1408]{1,0:T(8,128)(2,1)S(1)}, u32[]{:S(2)}, u32[]{:S(2)}) collective-permute-start(bf16[256,1408]{1,0:T(8,128)(2,1)} %reduce-scatter.8.cloned.1.call-done), channel_id=1, source_target_pairs={{8,1},{1,8},{10,3},{3,10},{12,5},{5,12},{14,7},{7,14},{24,17},{17,... | collective-permute-start | bytes 2162696 | tf_op jit(solution)/shard_map/ppermute | solution.py:262
  505.5 163.3 %reduce-scatter.14.cloned.1.call-start = ((), (), s32[]{:S(2)}) async-start(), calls=%async_computation.14 | async-start | bytes 2359296 | tf_op jit(solution)/shard_map/reduce_scatter | solution.py:237
  515.0 28.8 %collective-permute-start.50 = (bf16[1,256,1408]{2,1,0:T(8,128)(2,1)}, bf16[1,256,1408]{2,1,0:T(8,128)(2,1)}, u32[]{:S(2)}, u32[]{:S(2)}) collective-permute-start(bf16[1,256,1408]{2,1,0:T(8,128)(2,1)} %fusion.67), channel_id=1, source_target_pairs={{0,16},{16,0},{1,17},{17,1},{2,18},{18,2},{3,19},{19,3},{4,20},{20... | collective-permute-start | bytes 2162696 | tf_op jit(solution)/shard_map/ppermute | solution.py:20
  534.7 28.4 %collective-permute-start.49 = (bf16[1,256,1408]{2,1,0:T(8,128)(2,1)S(1)}, bf16[1,256,1408]{2,1,0:T(8,128)(2,1)}, u32[]{:S(2)}, u32[]{:S(2)}) collective-permute-start(bf16[1,256,1408]{2,1,0:T(8,128)(2,1)S(1)} %fusion.66), channel_id=1, source_target_pairs={{0,16},{16,0},{1,17},{17,1},{2,18},{18,2},{3,19},{19,3},{4,20},{20... | collective-permute-start | bytes 2162696 | tf_op jit(solution)/shard_map/ppermute | solution.py:20
  535.6 29.9 %collective-permute-start.47 = (bf16[2,136,2048]{2,1,0:T(8,128)(2,1)}, bf16[2,136,2048]{2,1,0:T(8,128)(2,1)}, u32[]{:S(2)}, u32[]{:S(2)}) collective-permute-start(bf16[2,136,2048]{2,1,0:T(8,128)(2,1)} %get-tuple-element.887), channel_id=1, source_target_pairs={{0,1},{1,0},{2,3},{3,2},{4,5},{5,4},{6,7},{7,6},{8,9},{9,8},{10,11... | collective-permute-start | bytes 3342344 | tf_op jit(solution)/shard_map/ppermute | solution.py:20
  535.6 44.5 %collective-permute-start.48 = (bf16[2,136,2048]{2,1,0:T(8,128)(2,1)}, bf16[2,136,2048]{2,1,0:T(8,128)(2,1)}, u32[]{:S(2)}, u32[]{:S(2)}) collective-permute-start(bf16[2,136,2048]{2,1,0:T(8,128)(2,1)} %bitcast.174), channel_id=1, source_target_pairs={{0,16},{16,0},{1,17},{17,1},{2,18},{18,2},{3,19},{19,3},{4,20},{20... | collective-permute-start | bytes 3342344 | tf_op jit(solution)/shard_map/ppermute | solution.py:20
  588.1 28.1 %collective-permute-start.58 = (f32[45,512]{1,0:T(8,128)S(1)}, f32[45,512]{1,0:T(8,128)S(1)}, u32[]{:S(2)}, u32[]{:S(2)}) collective-permute-start(f32[45,512]{1,0:T(8,128)S(1)} %add.619), channel_id=1, source_target_pairs={{0,2},{2,4},{4,6},{6,0},{1,3},{3,5},{5,7},{7,1},{8,10},{10,12},{12... | collective-permute-start | bytes 276488 | tf_op jit(solution)/shard_map/ppermute | solution.py:20
  589.7 26.4 %collective-permute-start.59 = (f32[45,512]{1,0:T(8,128)S(1)}, f32[45,512]{1,0:T(8,128)S(1)}, u32[]{:S(2)}, u32[]{:S(2)}) collective-permute-start(f32[45,512]{1,0:T(8,128)S(1)} %add.619), channel_id=1, source_target_pairs={{0,4},{2,6},{4,0},{6,2},{1,5},{3,7},{5,1},{7,3},{8,12},{10,14},{12... | collective-permute-start | bytes 276488 | tf_op jit(solution)/shard_map/ppermute | solution.py:20
  616.4 43.6 %collective-permute-start.69 = (bf16[1,176,2048]{2,1,0:T(8,128)(2,1)}, bf16[1,176,2048]{2,1,0:T(8,128)(2,1)}, u32[]{:S(2)}, u32[]{:S(2)}) collective-permute-start(bf16[1,176,2048]{2,1,0:T(8,128)(2,1)} %bitcast.200), channel_id=1, source_target_pairs={{0,16},{16,0},{1,17},{17,1},{2,18},{18,2},{3,19},{19,3},{4,20},{20... | collective-permute-start | bytes 2162696 | tf_op jit(solution)/shard_map/ppermute | solution.py:20
  622.9 27.6 %collective-permute-start.64 = (bf16[1,256,1536]{2,1,0:T(8,128)(2,1)S(1)}, bf16[1,256,1536]{2,1,0:T(8,128)(2,1)}, u32[]{:S(2)}, u32[]{:S(2)}) collective-permute-start(bf16[1,256,1536]{2,1,0:T(8,128)(2,1)S(1)} %fusion.63), channel_id=1, source_target_pairs={{0,16},{16,0},{1,17},{17,1},{2,18},{18,2},{3,19},{19,3},{4,20},{20... | collective-permute-start | bytes 2359304 | tf_op jit(solution)/shard_map/ppermute | solution.py:20
  631.8 28.1 %collective-permute-start.62 = (f32[4,512]{1,0:T(4,128)S(1)}, f32[4,512]{1,0:T(4,128)S(1)}, u32[]{:S(2)}, u32[]{:S(2)}) collective-permute-start(f32[4,512]{1,0:T(4,128)S(1)} %reshape.783), channel_id=1, source_target_pairs={{0,8},{8,0},{1,9},{9,1},{2,10},{10,2},{3,11},{11,3},{4,12},{12,4},... | collective-permute-start | bytes 24584 | tf_op jit(solution)/shard_map/ppermute | solution.py:20
  (126 other events, 1404.5 us)
Sparse Core Ops, SparseCore 0:
  10.2 28.8 all-gather.5
  41.5 63.0 all-gather.7
  106.2 62.2 all-gather.9
  170.6 58.9 all-gather.13
  231.1 59.0 all-gather.11
  295.8 65.8 reduce-scatter.7
  364.5 63.4 reduce-scatter.5
  430.3 68.9 reduce-scatter.11
  505.6 68.8 reduce-scatter.9
  616.5 33.6 reduce-scatter.13
